TPU v7x, 32 devices: a whole 2x2x4 slice. The times are simulated.
32 devices in a mesh: dp: 8 (over y, x, core), seq: 4 (over z).
Axes of the slice: x: 2, y: 2, z: 4, core: 2. Of those that a mesh axis runs over, the one named last changes fastest.
Arguments:
- inputs: float32 [8, 2048, 1472], P('dp', 'seq'), may hold values from -6 to 6
- layer3_rows: bfloat16 [12288, 1472], P(('dp', 'seq')), may hold values from -2 to 2
- layer4_rows: bfloat16 [12288, 1472], P(('dp', 'seq')), may hold values from -2 to 2
- norm_gains: float32 [4, 1472], replicated, may hold values from 0.25 to 1.75
- gate_weight: float32 [1472], replicated, may hold values from -0.15625 to 0.15625
- rel_bias: float32 [32, 6], replicated, may hold values from -4 to 4
- segment_ids: int32 [8, 2048], P('dp'), may hold values from 0 to 7, never falling along the last dimension, each value on 1 to 800 neighbouring positions
- cotangent: float32 [8, 2048, 1472], P('dp', 'seq'), may hold values from -24 to 24
Outputs:
- output: float32 [8, 2048, 1472], P('dp', 'seq')
- gate_mask: float32 [8, 2048], P('dp', 'seq')
- input_grad: float32 [8, 2048, 1472], P('dp', 'seq')
- layer3_grad: float32 [12288, 1472], P(('dp', 'seq'))
- layer4_grad: float32 [12288, 1472], P(('dp', 'seq'))
- norm_gains_grad: float32 [4, 1472], replicated
- gate_weight_grad: float32 [1472], replicated
- rel_bias_grad: float32 [32, 6], replicated
Inputs may be any that keep to these rules, and one draw needn't show every extreme that they name: `segment_ids`: segment numbers never fall along a sequence; a document holds at most 800 tokens, and some document holds exactly that many.
All inputs are finite; a program needn't handle non-finite values.
Results may differ from a plain program's by a relative error of at most 0.03.
Values may be sent and summed in bfloat16 or wider, within the bound.
No kernel may reach another device: no remote copies, remote signals or barrier semaphores. Data moves between devices by JAX's collectives and lax.ppermute only.
A program may use at most 512 MiB of HBM per device.

v0:
```python
import jax
import jax.numpy as jnp
from jax import lax
from jax.sharding import PartitionSpec as P

HEADS = 6
HEAD_DIM = 64
FF = 3584
BUCKETS = 32
INNER = 384


epsilon = 1e-06
gate_scale = -30.0
gate_offset = -3.5
masked_out = -1e30
limits = (12, 16, 23, 32, 46, 64, 91)


def bucket_of(relative):
    magnitude = jnp.abs(relative)
    beyond = jnp.zeros_like(magnitude)
    for bound_value in limits:
        beyond = beyond + (magnitude >= bound_value).astype(jnp.int32)
    inside = jnp.where(magnitude < 8, magnitude, 8 + beyond)
    return inside + 16 * (relative > 0).astype(jnp.int32)


def bucket_table(queries, first_pos, keys_count):
    relative = (
        jnp.arange(keys_count, dtype=jnp.int32)[None, :]
        - (first_pos + jnp.arange(queries, dtype=jnp.int32))[:, None]
    )
    return bucket_of(relative)


def rms_forward(stream, gain_row):
    inverse = lax.rsqrt(jnp.mean(stream * stream, axis=1, keepdims=True) + epsilon)
    return (stream * inverse * gain_row, inverse)


def stream_backward(stream, inverse, scaled):
    return inverse * scaled - stream * inverse**3 * jnp.mean(scaled * stream, axis=1, keepdims=True)


def rms_backward(stream, inverse, gain_row, grad_normed):
    grad_gain = jnp.sum(grad_normed * stream * inverse, axis=0)
    return (stream_backward(stream, inverse, gain_row * grad_normed), grad_gain)


def gelu_tanh(values):
    return 0.5 * values * (1.0 + jnp.tanh(0.7978845608028654 * (values + 0.044715 * values**3)))


def times_rows(left_side, weight):
    return lax.dot_general(
        left_side, weight, (((1,), (1,)), ((), ())), preferred_element_type=jnp.float32
    )


def times_plain(left_side, weight):
    return jnp.dot(left_side, weight, preferred_element_type=jnp.float32)


def outer_sum(left_side, right_side):
    return lax.dot_general(
        left_side, right_side, (((0,), (0,)), ((), ())), preferred_element_type=jnp.float32
    )


def fetch_rows(local_rows):
    return lax.all_gather(local_rows, ("dp", "seq"), axis=0, tiled=True)


def reduce_rows(grad_rows):
    return lax.psum_scatter(grad_rows, ("dp", "seq"), scatter_dimension=0, tiled=True)


def collect(key_part, value_part, gate_part):
    if gate_part is None:
        all_keys, all_values = (
            lax.all_gather(key_part, "seq", axis=1, tiled=True),
            lax.all_gather(value_part, "seq", axis=1, tiled=True),
        )
        return (all_keys, all_values, None)
    return (
        lax.all_gather(key_part, "seq", axis=1, tiled=True),
        lax.all_gather(value_part, "seq", axis=1, tiled=True),
        lax.all_gather(gate_part, "seq", axis=1, tiled=True),
    )


def head_slice(values, head_index):
    return lax.dynamic_slice_in_dim(values, head_index * HEAD_DIM, HEAD_DIM, 2)


def head_scores(queries, all_keys, all_gates, head_index, context):
    allowed, buckets, rel_bias, first_pos = context
    scores = jnp.einsum(
        "btd,bsd->bts",
        head_slice(queries, head_index),
        head_slice(all_keys, head_index),
        preferred_element_type=jnp.float32,
    )
    column = lax.dynamic_index_in_dim(rel_bias, head_index, 1, keepdims=False)
    scores = scores + jnp.take(column, buckets)[None]
    if all_gates is not None:
        scores = scores + all_gates.astype(jnp.float32)[:, None, :]
    return jnp.where(allowed, scores, masked_out)


def diagonal_buckets(pair_sum, first_pos):
    tokens_here, length_all = pair_sum.shape
    flipped = pair_sum[::-1]
    padded = jnp.pad(flipped, ((0, 0), (0, tokens_here)))
    sheared = padded.reshape(-1)[: tokens_here * (length_all + tokens_here - 1)].reshape(
        tokens_here, length_all + tokens_here - 1
    )
    diagonal_sums = jnp.sum(sheared, axis=0)
    relative = (
        jnp.arange(length_all + tokens_here - 1, dtype=jnp.int32) - (tokens_here - 1) - first_pos
    )
    one_hot = (
        bucket_of(relative)[:, None] == jnp.arange(BUCKETS, dtype=jnp.int32)[None, :]
    ).astype(jnp.float32)
    return jnp.dot(diagonal_sums, one_hot, precision=lax.Precision.HIGHEST)


def attend_forward(queries, all_keys, all_values, all_gates, context):

    def one_head(head_index):
        scores = head_scores(queries, all_keys, all_gates, head_index, context)
        row_peak = jnp.max(scores, axis=2, keepdims=True)
        exponent = jnp.exp(scores - row_peak)
        row_total = jnp.sum(exponent, axis=2, keepdims=True)
        weights_low = (exponent / row_total).astype(jnp.bfloat16)
        mixed_head = jnp.einsum(
            "bts,bsd->btd",
            weights_low,
            head_slice(all_values, head_index),
            preferred_element_type=jnp.float32,
        )
        return (mixed_head, (row_peak + jnp.log(row_total))[:, :, 0])

    mixed_heads, log_total = lax.map(one_head, jnp.arange(HEADS))
    seqs_here, tokens_here = (queries.shape[0], queries.shape[1])
    return (mixed_heads.transpose(1, 2, 0, 3).reshape(seqs_here * tokens_here, INNER), log_total)


def attend_backward(queries, all_keys, all_values, all_gates, log_total, grad_mixed, context):
    allowed, buckets, rel_bias, first_pos = context

    def one_head(head_index):
        scores = head_scores(queries, all_keys, all_gates, head_index, context)
        probs_full = jnp.exp(scores - log_total[head_index][:, :, None])
        grad_head = head_slice(grad_mixed, head_index)
        grad_probs = jnp.einsum(
            "btd,bsd->bts",
            grad_head,
            head_slice(all_values, head_index),
            preferred_element_type=jnp.float32,
        )
        grad_value = jnp.einsum(
            "bts,btd->bsd",
            probs_full.astype(jnp.bfloat16),
            grad_head,
            preferred_element_type=jnp.float32,
        )
        grad_scores = probs_full * (
            grad_probs - jnp.sum(probs_full * grad_probs, axis=2, keepdims=True)
        )
        scores_low = grad_scores.astype(jnp.bfloat16)
        grad_query = jnp.einsum(
            "bts,bsd->btd",
            scores_low,
            head_slice(all_keys, head_index),
            preferred_element_type=jnp.float32,
        )
        grad_key = jnp.einsum(
            "bts,btd->bsd",
            scores_low,
            head_slice(queries, head_index),
            preferred_element_type=jnp.float32,
        )
        pair_sum = jnp.sum(grad_scores, axis=0)
        grad_column = diagonal_buckets(pair_sum, first_pos)
        return (grad_query, grad_key, grad_value, grad_column, jnp.sum(grad_scores, axis=1))

    grad_query, grad_key, grad_value, grad_table, grad_gates = lax.map(one_head, jnp.arange(HEADS))
    seqs_here, tokens_here, length_all = (queries.shape[0], queries.shape[1], all_keys.shape[1])
    grad_query = grad_query.transpose(1, 2, 0, 3).reshape(seqs_here, tokens_here, INNER)
    grad_key = grad_key.transpose(1, 2, 0, 3).reshape(seqs_here, length_all, INNER)
    grad_value = grad_value.transpose(1, 2, 0, 3).reshape(seqs_here, length_all, INNER)
    return (grad_query, grad_key, grad_value, grad_table.T, jnp.sum(grad_gates, axis=0))


def layer_forward(stream, gathered, gain_one, gain_two, gate_low, context, shape_info):
    seqs_here, tokens_here = shape_info
    head_shape = (seqs_here, tokens_here, INNER)
    normed, inverse_one = rms_forward(stream, gain_one)
    normed_low = normed.astype(jnp.bfloat16)
    projected = times_rows(normed_low, gathered[: 3 * INNER]).astype(jnp.bfloat16)
    queries = projected[:, :INNER].reshape(head_shape)
    key_part = projected[:, INNER : 2 * INNER].reshape(head_shape)
    value_part = projected[:, 2 * INNER :].reshape(head_shape)
    all_keys, all_values, all_gates = collect(key_part, value_part, gate_low)
    mixed_heads, log_total = attend_forward(queries, all_keys, all_values, all_gates, context)
    attended = mixed_heads.astype(jnp.bfloat16)
    middle = stream + times_plain(attended, gathered[3 * INNER : 4 * INNER])
    normed_two, inverse_two = rms_forward(middle, gain_two)
    normed_two_low = normed_two.astype(jnp.bfloat16)
    up_both = times_rows(normed_two_low, gathered[4 * INNER : 4 * INNER + 2 * FF])
    up_gelu = up_both[:, :FF]
    up_linear = up_both[:, FF:]
    hidden = (gelu_tanh(up_gelu) * up_linear).astype(jnp.bfloat16)
    result = middle + times_plain(hidden, gathered[4 * INNER + 2 * FF :])
    kept = (
        stream,
        inverse_one,
        normed_low,
        queries,
        key_part,
        value_part,
        attended,
        log_total,
        middle,
        inverse_two,
        normed_two_low,
        up_gelu,
        up_linear,
        hidden,
    )
    return (result, kept)


def layer_backward(grad_out, kept, gathered, gain_one, gain_two, gate_low, context, shape_info):
    (
        stream,
        inverse_one,
        normed_low,
        queries,
        key_part,
        value_part,
        attended,
        log_total,
        middle,
        inverse_two,
        normed_two_low,
        up_gelu,
        up_linear,
        hidden,
    ) = kept
    seqs_here, tokens_here = shape_info
    rows_here = seqs_here * tokens_here
    w_down = gathered[4 * INNER + 2 * FF :]
    branch_low = grad_out.astype(jnp.bfloat16)
    grad_down = outer_sum(hidden, branch_low)
    grad_hidden = times_rows(branch_low, w_down)
    activated, gelu_pullback = jax.vjp(gelu_tanh, up_gelu)
    grad_gelu = gelu_pullback(grad_hidden * up_linear)[0]
    grad_ffn_low = jnp.concatenate([grad_gelu, grad_hidden * activated], axis=1).astype(
        jnp.bfloat16
    )
    grad_ffn = outer_sum(grad_ffn_low, normed_two_low)
    grad_normed_two = times_plain(grad_ffn_low, gathered[4 * INNER : 4 * INNER + 2 * FF])
    grad_middle, grad_gain_two = rms_backward(middle, inverse_two, gain_two, grad_normed_two)
    grad_middle = grad_out + grad_middle
    middle_low = grad_middle.astype(jnp.bfloat16)
    grad_attn_out = outer_sum(attended, middle_low)
    grad_mixed = (
        times_rows(middle_low, gathered[3 * INNER : 4 * INNER])
        .astype(jnp.bfloat16)
        .reshape(seqs_here, tokens_here, INNER)
    )
    all_keys, all_values, all_gates = collect(key_part, value_part, gate_low)
    grad_query, grad_key, grad_value, grad_table, grad_gates = attend_backward(
        queries, all_keys, all_values, all_gates, log_total, grad_mixed, context
    )
    if gate_low is None:
        grad_key, grad_value = (
            lax.psum_scatter(
                grad_key.astype(jnp.bfloat16), "seq", scatter_dimension=1, tiled=True
            ).astype(jnp.float32),
            lax.psum_scatter(
                grad_value.astype(jnp.bfloat16), "seq", scatter_dimension=1, tiled=True
            ).astype(jnp.float32),
        )
        grad_gate = None
    else:
        grad_key, grad_value, grad_gate = (
            lax.psum_scatter(
                grad_key.astype(jnp.bfloat16), "seq", scatter_dimension=1, tiled=True
            ).astype(jnp.float32),
            lax.psum_scatter(
                grad_value.astype(jnp.bfloat16), "seq", scatter_dimension=1, tiled=True
            ).astype(jnp.float32),
            lax.psum_scatter(
                grad_gates.astype(jnp.bfloat16), "seq", scatter_dimension=1, tiled=True
            ).astype(jnp.float32),
        )
        grad_gate = grad_gate.reshape(rows_here)
    grad_input_low = jnp.concatenate(
        [
            grad_query.reshape(rows_here, INNER),
            grad_key.reshape(rows_here, INNER),
            grad_value.reshape(rows_here, INNER),
        ],
        axis=1,
    ).astype(jnp.bfloat16)
    grad_input_rows = outer_sum(grad_input_low, normed_low)
    grad_normed = times_plain(grad_input_low, gathered[: 3 * INNER])
    grad_stream, grad_gain_one = rms_backward(stream, inverse_one, gain_one, grad_normed)
    grad_rows = jnp.concatenate([grad_input_rows, grad_attn_out, grad_ffn, grad_down], axis=0)
    return (
        grad_middle + grad_stream,
        grad_rows,
        grad_table,
        grad_gate,
        grad_gain_one,
        grad_gain_two,
    )


def per_device(
    inputs, layer3_rows, layer4_rows, norm_gains, gate_weight, rel_bias, segment_ids, cotangent
):
    seqs_here, tokens_here, width = inputs.shape
    length_all = segment_ids.shape[1]
    first_pos = lax.axis_index("seq") * tokens_here
    own_segments = lax.dynamic_slice_in_dim(segment_ids, first_pos, tokens_here, 1)
    allowed = own_segments[:, :, None] == segment_ids[:, None, :]
    buckets = bucket_table(tokens_here, first_pos, length_all)
    context = (allowed, buckets, rel_bias, first_pos)
    shape_info = (seqs_here, tokens_here)
    stream = inputs.reshape(seqs_here * tokens_here, width)
    gathered_three = fetch_rows(layer3_rows)
    after_three, kept_three = layer_forward(
        stream, gathered_three, norm_gains[0], norm_gains[1], None, context, shape_info
    )
    gate_inverse = lax.rsqrt(jnp.mean(after_three * after_three, axis=1, keepdims=True) + epsilon)
    gate_normed = after_three * gate_inverse
    gate_logit = jnp.sum(gate_normed * gate_weight, axis=1) + gate_offset
    sigmoid_value = 1.0 / (1.0 + jnp.exp(-gate_logit))
    gate_mask = gate_scale * sigmoid_value
    gate_low = gate_mask.astype(jnp.bfloat16).reshape(shape_info)
    gathered_four = fetch_rows(layer4_rows)
    after_four, kept_four = layer_forward(
        after_three, gathered_four, norm_gains[2], norm_gains[3], gate_low, context, shape_info
    )
    back_four = fetch_rows(layer4_rows)
    grad_three_out, rows_four, table_four, grad_gate, gain_four_one, gain_four_two = layer_backward(
        cotangent.reshape(seqs_here * tokens_here, width),
        kept_four,
        back_four,
        norm_gains[2],
        norm_gains[3],
        gate_low,
        context,
        shape_info,
    )
    local_four = reduce_rows(rows_four)
    grad_logit = grad_gate * gate_scale * sigmoid_value * (1.0 - sigmoid_value)
    grad_gate_weight = jnp.sum(grad_logit[:, None] * gate_normed, axis=0)
    gate_stream = stream_backward(after_three, gate_inverse, grad_logit[:, None] * gate_weight)
    grad_three_out = grad_three_out + gate_stream
    back_three = fetch_rows(layer3_rows)
    grad_input, rows_three, table_three, unused, gain_three_one, gain_three_two = layer_backward(
        grad_three_out,
        kept_three,
        back_three,
        norm_gains[0],
        norm_gains[1],
        None,
        context,
        shape_info,
    )
    local_three = reduce_rows(rows_three)
    gains_grad = jnp.stack([gain_three_one, gain_three_two, gain_four_one, gain_four_two])
    summed = lax.psum((gains_grad, grad_gate_weight, table_three + table_four), ("dp", "seq"))
    return (
        after_four.reshape(inputs.shape),
        gate_mask.reshape(shape_info),
        grad_input.reshape(inputs.shape),
        local_three,
        local_four,
        summed[0],
        summed[1],
        summed[2],
    )


def solution(mesh):
    placed = (
        P("dp", "seq", None),
        P(("dp", "seq"), None),
        P(("dp", "seq"), None),
        P(),
        P(),
        P(),
        P("dp", None),
        P("dp", "seq", None),
    )
    return jax.shard_map(
        per_device,
        mesh=mesh,
        in_specs=placed,
        out_specs=(
            P("dp", "seq", None),
            P("dp", "seq"),
            P("dp", "seq", None),
            P(("dp", "seq"), None),
            P(("dp", "seq"), None),
            P(),
            P(),
            P(),
        ),
        check_vma=False,
    )
```

profile of v0, /device:TPU:24, one launch (start us, length us, event | category | flops | bytes accessed | tf_op | source)
XLA Modules:
  0.0 3869.4 jit_solution(9402944301353929418)
XLA Ops:
  12.3 213.0 %all-gather.11.cloned.1.call-done = bf16[12288,1472]{0,1:T(8,128)(2,1)} async-done(((bf16[384,1472]{0,1:T(8,128)(2,1)}), bf16[12288,1472]{0,1:T(8,128)(2,1)}) %all-gather.11.cloned.1.call-update) | async-done | bytes 36175888 | tf_op jit(solution)/shard_map/all_gather | solution.py:72
  233.8 32.2 all-gather.15.cloned.1.call-done
  266.0 38.1 all-gather.17.cloned.1.call-done
  304.8 266.6 %while.66 = (s32[]{:T(128)}, bf16[6,1,512,64]{2,3,1,0:T(8,128)(2,1)S(1)}, f32[6,1,512]{2,1,0:T(1,128)}, s32[6]{0:T(128)S(1)}, bf16[1,512,384]{2,1,0:T(8,128)(2,1...) while((s32[]{:T(128)}, ...), condition=%wide.region_4.6_spmd.clone, body=%wide.region_1.5_spmd.clone.sunk | while | flops 379584000 | bytes 13944585 | solution.py:145
  310.4 35.4 fusion.349
  354.7 35.4 fusion.349
  399.0 35.5 fusion.349
  443.4 35.4 fusion.349
  487.7 35.4 fusion.349
  532.0 35.4 fusion.349
  576.0 20.0 fusion.176
  631.4 23.7 all-gather.19.cloned.1.call-done
  655.1 38.0 all-gather.21.cloned.1.call-done
  693.1 263.9 %while.67 = (s32[]{:T(128)}, bf16[6,1,512,64]{2,3,1,0:T(8,128)(2,1)S(1)}, f32[6,1,512]{2,1,0:T(1,128)S(1)}, s32[6]{0:T(128)S(1)}, bf16[1,512,384]{2,1,0:T(8,128)...) while((s32[]{:T(128)}, ...), condition=%wide.region_11.13_spmd.clone, body=%wide.region_8.12_spmd.clone.sunk | while | flops 380634624 | bytes 13965073 | solution.py:145
  698.7 35.5 fusion.356
  742.6 35.5 fusion.356
  786.5 35.5 fusion.356
  830.3 35.5 fusion.356
  874.2 35.5 fusion.356
  918.1 35.5 fusion.356
  961.0 19.9 fusion.172
  980.9 20.9 fusion.201
  1001.8 19.6 multiply_reduce_fusion.3
  1032.2 646.2 %while.68 = (s32[]{:T(128)}, bf16[6,1,512,64]{2,3,1,0:T(8,128)(2,1)S(1)}, bf16[6,1,2048,64]{2,3,1,0:T(8,128)(2,1)}, bf16[6,1,2048,64]{2,3,1,0:T(8,128)(2,1)}, f3...) while((s32[]{:T(128)}, ...), condition=%wide.region_18.20_spmd.clone, body=%wide.region_14.19_spmd.clone.sunk | while | flops 788877952 | bytes 118746504 | solution.py:189
  1041.0 37.5 multiply_reduce_fusion.15
  1082.6 32.7 rev.10
  1148.6 37.4 multiply_reduce_fusion.15
  1190.2 32.7 rev.10
  1256.3 37.5 multiply_reduce_fusion.15
  1297.9 32.7 rev.10
  1363.9 37.4 multiply_reduce_fusion.15
  1405.5 32.7 rev.10
  1471.6 37.5 multiply_reduce_fusion.15
  1513.2 32.7 rev.10
  1579.2 37.5 multiply_reduce_fusion.15
  1620.8 32.7 rev.10
  1681.3 18.2 reduce-scatter.22.cloned.1.call-done
  1702.2 34.8 reduce-scatter.12.cloned.1.call-done
  1737.0 37.2 reduce-scatter.10.cloned.1.call-done
  1781.6 19.1 fusion.193
  1800.7 19.4 multiply_reduce_fusion.5
  1829.1 659.0 %while.69 = (s32[]{:T(128)}, bf16[6,1,512,64]{2,3,1,0:T(8,128)(2,1)}, bf16[6,1,2048,64]{2,3,1,0:T(8,128)(2,1)S(1)}, bf16[6,1,2048,64]{2,3,1,0:T(8,128)(2,1)S(1)}...) while((s32[]{:T(128)}, ...), condition=%wide.region_29.31_spmd.clone, body=%wide.region_26.30_spmd.clone.sunk | while | flops 786780800 | bytes 118717688 | solution.py:189
  1839.7 37.7 multiply_reduce_fusion.16
  1883.1 32.7 rev.11
  1949.5 37.7 multiply_reduce_fusion.16
  1992.9 32.7 rev.11
  2059.3 37.7 multiply_reduce_fusion.16
  2102.7 32.7 rev.11
  2169.1 37.7 multiply_reduce_fusion.16
  2212.5 32.7 rev.11
  2278.9 37.7 multiply_reduce_fusion.16
  2322.3 32.7 rev.11
  2388.7 37.7 multiply_reduce_fusion.16
  2432.1 32.7 rev.11
  2489.9 21.8 fusion.203
  2514.0 12.2 fusion.275
  2531.3 46.4 %pad_maximum_fusion.1 = f32[12288,1472]{0,1:T(8,128)} fusion(f32[3584,1472]{0,1:T(8,128)} %fusion.275, f32[7168,1472]{0,1:T(8,128)} %fusion.203, f32[384,1472]{0,1:T(8,128)S(1)} %copy-done.22, f32[1152,1472]{0,1:T(8,128)} %fusion.249), kind=kLoop, calls=%fused_computation.210 | loop fusion | flops 54263808 | bytes 144703488 | tf_op jit(solution)/shard_map/concatenate | solution.py:313
  2582.0 15.6 fusion.242
  2597.6 28.8 fusion.202
  2633.3 58.0 %pad_maximum_fusion = f32[12288,1472]{0,1:T(8,128)} fusion(f32[3584,1472]{0,1:T(8,128)} %fusion.242, f32[7168,1472]{0,1:T(8,128)} %fusion.202, f32[384,1472]{0,1:T(8,128)} %fusion.239, f32[1152,1472]{0,1:T(8,128)} %fusion.248), kind=kLoop, calls=%fused_computation.209 | loop fusion | flops 54263808 | bytes 144703488 | tf_op jit(solution)/shard_map/concatenate | solution.py:313
  2692.0 12.3 fusion.210
  2711.2 43.8 %all-reduce.2 = (f32[4,1472]{1,0:T(4,128)}, f32[1472]{0:T(1024)}, f32[32,6]{0,1:T(8,128)}) all-reduce(f32[4,1472]{1,0:T(4,128)S(1)} %pad_maximum_fusion.14, f32[1472]{0:T(1024)S(1)} %copy-done.65, f32[32,6]{0,1:T(8,128)S(1)} %add_bitcast_fusion), channel_id=1, replica_groups=mesh['dp'=8,'seq'=4] {'dp','seq'}, use_global_device_ids=true, to_apply=%region_39.41 | all-reduce | flops 7552 | bytes 60416 | tf_op jit(solution)/shard_map/psum | solution.py:379
  2760.1 456.7 %reduce-scatter.20.cloned.1.call-done = f32[384,1472]{0,1:T(8,128)} async-done(((f32[12288,1472]{0,1:T(8,128)}), f32[384,1472]{0,1:T(8,128)}) %reduce-scatter.20.cloned.1.call-update) | async-done | bytes 2261008 | tf_op jit(solution)/shard_map/reduce_scatter | solution.py:76
  3216.8 645.7 %reduce-scatter.18.cloned.1.call-done = f32[384,1472]{0,1:T(8,128)} async-done(((f32[12288,1472]{0,1:T(8,128)}), f32[384,1472]{0,1:T(8,128)}) %reduce-scatter.18.cloned.1.call-update) | async-done | bytes 2261008 | tf_op jit(solution)/shard_map/reduce_scatter | solution.py:76
  (609 shorter events, 626.0 us)
Async XLA Ops:
  7.2 218.1 %copy-start.4 = (f32[1,512,1472]{1,2,0:T(8,128)S(1)}, f32[1,512,1472]{1,2,0:T(8,128)}, u32[]{:S(2)}) copy-start(f32[1,512,1472]{1,2,0:T(8,128)} %param.18) | copy-start | bytes 9043972
  7.2 218.1 %all-gather.11.cloned.1.call-start = ((), (), s32[]{:S(2)}) async-start(), calls=%async_computation.7 | async-start | bytes 37306368 | tf_op jit(solution)/shard_map/all_gather | solution.py:72
  7.9 258.1 %all-gather.15.cloned.1.call-start = ((), (), s32[]{:S(2)}) async-start(), calls=%async_computation.15 | async-start | bytes 1966080 | tf_op jit(solution)/shard_map/all_gather | solution.py:82
  9.5 220.1 %copy-start.40 = (f32[1472]{0:T(1024)}, f32[1472]{0:T(1024)S(1)}, u32[]{:S(2)}) copy-start(f32[1472]{0:T(1024)S(1)} %get-tuple-element.686) | copy-start | bytes 17668
  12.3 218.4 %copy-start.57 = (f32[512]{0:T(512)}, f32[512]{0:T(512)S(1)}, u32[]{:S(2)}) copy-start(f32[512]{0:T(512)S(1)} %get-tuple-element.955) | copy-start | bytes 6148
  230.7 73.4 %all-gather.17.cloned.1.call-start = ((), (), s32[]{:S(2)}) async-start(), calls=%async_computation.16 | async-start | bytes 1966080 | tf_op jit(solution)/shard_map/all_gather | solution.py:83
  231.4 381.6 %all-gather.13.cloned.1.call-start = ((), (), s32[]{:S(2)}) async-start(), calls=%async_computation.8 | async-start | bytes 37306368 | tf_op jit(solution)/shard_map/all_gather | solution.py:72
  232.0 423.0 %all-gather.19.cloned.1.call-start = ((), (), s32[]{:S(2)}) async-start(), calls=%async_computation.17 | async-start | bytes 1966080 | tf_op jit(solution)/shard_map/all_gather | solution.py:87
  304.8 266.6 %copy-start.5 = (f32[1,512,1472]{1,2,0:T(8,128)S(1)}, f32[1,512,1472]{1,2,0:T(8,128)}, u32[]{:S(2)}) copy-start(f32[1,512,1472]{1,2,0:T(8,128)} %param.18) | copy-start | bytes 9043972
  571.4 24.6 copy-start.27
  576.0 20.0 copy-start.67
  618.9 74.1 %all-gather.21.cloned.1.call-start = ((), (), s32[]{:S(2)}) async-start(), calls=%async_computation.18 | async-start | bytes 1966080 | tf_op jit(solution)/shard_map/all_gather | solution.py:88
  619.5 1080.0 %reduce-scatter.22.cloned.1.call-start = ((), (), s32[]{:S(2)}) async-start(), calls=%async_computation.19 | async-start | bytes 655360
  619.9 73.1 %copy-start.55 = (f32[512]{0:T(512)}, f32[512]{0:T(512)S(1)}, u32[]{:S(2)}) copy-start(f32[512]{0:T(512)S(1)} %multiply_reduce_fusion.10) | copy-start | bytes 6148
  693.1 263.9 %copy-start.8 = (f32[512,1472]{0,1:T(8,128)S(1)}, f32[512,1472]{0,1:T(8,128)}, u32[]{:S(2)}) copy-start(f32[512,1472]{0,1:T(8,128)} %copy-done.7) | copy-start | bytes 9043972
  957.0 23.9 copy-start.29
  961.0 60.4 %copy-start.70 = (f32[512]{0:T(512)}, f32[512]{0:T(512)S(1)}, u32[]{:S(2)}) copy-start(f32[512]{0:T(512)S(1)} %get-tuple-element.961) | copy-start | bytes 6148
  980.9 20.9 copy-start.19
  1041.0 37.5 copy-start.2
  1148.6 37.5 copy-start.2
  1256.3 37.5 copy-start.2
  1363.9 37.5 copy-start.2
  1471.6 37.5 copy-start.2
  1579.2 37.5 copy-start.2
  1678.5 101.5 %copy-start.33 = (bf16[6,1,512,64]{2,3,1,0:T(8,128)(2,1)}, bf16[6,1,512,64]{2,3,1,0:T(8,128)(2,1)S(1)}, u32[]{:S(2)}) copy-start(bf16[6,1,512,64]{2,3,1,0:T(8,128)(2,1)S(1)} %get-tuple-element.526) | copy-start | bytes 1179652
  1678.5 23.7 copy-start.56
  1678.5 95.6 %copy-start.9 = (f32[512,1472]{0,1:T(8,128)S(1)}, f32[512,1472]{0,1:T(8,128)}, u32[]{:S(2)}) copy-start(f32[512,1472]{0,1:T(8,128)} %copy-done.7) | copy-start | bytes 9043972
  1678.5 95.6 %copy-start.43 = (f32[1472]{0:T(1024)S(1)}, f32[1472]{0:T(1024)}, u32[]{:S(2)}) copy-start(f32[1472]{0:T(1024)} %get-tuple-element.687) | copy-start | bytes 17668
  1678.5 95.6 %copy-start.47 = (f32[1472]{0:T(1024)S(1)}, f32[1472]{0:T(1024)}, u32[]{:S(2)}) copy-start(f32[1472]{0:T(1024)} %param.22) | copy-start | bytes 17668
  1678.5 95.6 %copy-start.53 = (f32[512]{0:T(512)S(1)}, f32[512]{0:T(512)}, u32[]{:S(2)}) copy-start(f32[512]{0:T(512)} %copy-done.52) | copy-start | bytes 6148
  1679.8 57.2 %reduce-scatter.12.cloned.1.call-start = ((), (), s32[]{:S(2)}) async-start(), calls=%async_computation.10 | async-start | bytes 1966080 | tf_op jit(solution)/shard_map/reduce_scatter | solution.py:294
  1680.5 93.6 %reduce-scatter.10.cloned.1.call-start = ((), (), s32[]{:S(2)}) async-start(), calls=%async_computation.9 | async-start | bytes 1966080 | tf_op jit(solution)/shard_map/reduce_scatter | solution.py:291
  1681.3 945.2 %reduce-scatter.16.cloned.1.call-start = ((), (), s32[]{:S(2)}) async-start(), calls=%async_computation.12 | async-start | bytes 1966080 | tf_op jit(solution)/shard_map/reduce_scatter | solution.py:284
  1781.6 19.1 copy-start.20
  1781.6 19.1 copy-start.17
  1781.6 19.1 copy-start.49
  1781.6 19.1 copy-start.68
  1800.7 19.4 copy-start.71
  1839.7 37.7 copy-start.3
  1949.5 37.7 copy-start.3
  2059.3 37.7 copy-start.3
  2169.1 37.7 copy-start.3
  2278.9 37.7 copy-start.3
  2388.7 37.7 copy-start.3
  2488.1 23.5 copy-start.59
  2489.8 21.8 copy-start.13
  2489.8 21.8 copy-start.30
  2489.8 136.7 %reduce-scatter.14.cloned.1.call-start = ((), (), s32[]{:S(2)}) async-start(), calls=%async_computation.11 | async-start | bytes 1966080 | tf_op jit(solution)/shard_map/reduce_scatter | solution.py:281
  2514.0 12.3 copy-start.37
  2531.3 685.5 %reduce-scatter.20.cloned.1.call-start = ((), (), s32[]{:S(2)}) async-start(), calls=%async_computation.14 | async-start | bytes 74612736 | tf_op jit(solution)/shard_map/reduce_scatter | solution.py:76
  2577.8 1284.7 %reduce-scatter.18.cloned.1.call-start = ((), (), s32[]{:S(2)}) async-start(), calls=%async_computation.13 | async-start | bytes 74612736 | tf_op jit(solution)/shard_map/reduce_scatter | solution.py:76
  2582.0 15.6 copy-start.18
  2582.0 15.6 copy-start.50
  2582.0 15.6 copy-start.69
  2597.6 28.9 copy-start.6
  2597.6 28.9 copy-start.35
  2597.6 28.9 copy-start.41
  2597.6 28.9 copy-start.58
  2692.0 12.4 copy-start.62
  2692.0 12.4 copy-start.63
  2692.0 12.4 copy-start.60
  2692.0 13.1 copy-start.38
  2692.0 13.1 copy-start.39
  2705.1 49.9 %copy-start.66 = (f32[512]{0:T(512)S(1)}, f32[512]{0:T(512)}, u32[]{:S(2)}) copy-start(f32[512]{0:T(512)} %get-tuple-element.954) | copy-start | bytes 6148
  (42 other events, 213.5 us)
Sparse Core Ops, SparseCore 0:
  10.9 214.3 all-gather.10
  230.8 35.1 all-gather.14
  268.1 35.9 all-gather.16
  306.9 214.3 all-gather.12
  619.1 35.9 all-gather.18
  657.0 35.9 all-gather.20
  1679.9 19.5 reduce-scatter.21
  1702.4 34.5 reduce-scatter.11
  1739.9 34.2 reduce-scatter.9
  2489.9 34.2 reduce-scatter.15
  2531.4 34.2 reduce-scatter.13
  2577.9 638.8 reduce-scatter.19
  3224.9 637.4 reduce-scatter.17
where the time goes:
time: 3920 us; the launch traced here: 3870 us
  waiting for transfers between devices  1540 us (39%)
  matrix products  1280 us (33%)
  local copies, waits for them, and re-layouts  735 us (19%)
  other arithmetic  180 us (5%)
  loops' own time  63.7 us (2%)
  blocking collectives  54.6 us (1%)
    reduce_scatter x2, waiting for transfers between devices, reduce_rows(): lax.psum_scatter(grad_rows, ('dp', 'seq'), scatter_dimension=0, tiled=True)  1100 us
    dot_general x24, matrix products, head_scores(): jnp.einsum('btd,bsd->bts', head_slice(queries, head_index), head_slice(al...  877 us
    rev x12, local copies, waits for them, and re-layouts, diagonal_buckets(): flipped = pair_sum[::-1]  392 us
    all_gather x2, waiting for transfers between devices, fetch_rows(): return lax.all_gather(local_rows, ('dp', 'seq'), axis=0, tiled=True)  213 us
    reshape x24, local copies, waits for them, and re-layouts, diagonal_buckets(): padded.reshape(-1)[:tokens_here * (length_all + tokens_here - 1)]  176 us
    concatenate x2, other arithmetic, layer_backward(): jnp.concatenate([grad_input_rows, grad_attn_out, grad_ffn, grad_down], ax...  104 us
    dot_general x8, matrix products, outer_sum(): lax.dot_general(left_side, right_side, (((0,), (0,)), ((), ())), preferre...  94.8 us
    dot_general x8, matrix products, times_rows(): lax.dot_general(left_side, weight, (((1,), (1,)), ((), ())), preferred_el...  93.6 us
  transfers between devices with their start and end apart: 13, of which 10 were waited for; matrix products, arithmetic and copies ran while one was open for 14% of the time, Pallas kernels for 0%

commit v1 on v0

v1 whole, which is shorter than its diff:
```python
import functools

import jax
import jax.numpy as jnp
from jax import lax
from jax.experimental import pallas as pl
from jax.experimental.pallas import tpu as pltpu
from jax.sharding import PartitionSpec as P

HEADS = 6
PAIRS = 3
BLOCK = 128
WIDE = 2 * BLOCK
INNER = 384
BUCKETS = 32
OFFSETS = 5
masked_out = -1e30
limits = (12, 16, 23, 32, 46, 64, 91)
both_last = (((1,), (1,)), ((), ()))


def bucket_of(relative):
    magnitude = jnp.abs(relative)
    beyond = jnp.zeros_like(magnitude)
    for bound_value in limits:
        beyond = beyond + (magnitude >= bound_value).astype(jnp.int32)
    inside = jnp.where(magnitude < 8, magnitude, 8 + beyond)
    return inside + 16 * (relative > 0).astype(jnp.int32)


def near_buckets(offset):
    if offset < 0:
        return range(1, 16)
    if offset > 0:
        return range(17, 32)
    return range(0, 32)


def tile_buckets(offset, width):
    key_at = lax.broadcasted_iota(jnp.int32, (BLOCK, width), 0)
    query_at = lax.broadcasted_iota(jnp.int32, (BLOCK, width), 1) % BLOCK
    return bucket_of(offset * BLOCK + key_at - query_at)


def bias_body(table_ref, tiles_ref):
    head = pl.program_id(0)
    tiles_ref[0, 0] = jnp.full((BLOCK, BLOCK), table_ref[15, head], jnp.float32)
    tiles_ref[0, 4] = jnp.full((BLOCK, BLOCK), table_ref[31, head], jnp.float32)
    for offset in (-1, 0, 1):
        buckets = tile_buckets(offset, BLOCK)
        tile = jnp.zeros((BLOCK, BLOCK), jnp.float32)
        for bucket in near_buckets(offset):
            tile = jnp.where(buckets == bucket, table_ref[bucket, head], tile)
        tiles_ref[0, offset + 2] = tile


def bias_tiles(rel_bias):
    return pl.pallas_call(
        bias_body,
        grid=(HEADS,),
        in_specs=[pl.BlockSpec(memory_space=pltpu.SMEM)],
        out_specs=pl.BlockSpec((1, OFFSETS, BLOCK, BLOCK), lambda h: (h, 0, 0, 0)),
        out_shape=jax.ShapeDtypeStruct((HEADS, OFFSETS, BLOCK, BLOCK), jnp.float32),
        name="bias_tiles",
    )(rel_bias)


def lane_masks():
    lane = lax.broadcasted_iota(jnp.int32, (BLOCK, BLOCK), 1)
    low = jnp.where(lane < 64, 1.0, 0.0).astype(jnp.bfloat16)
    high = jnp.where(lane < 64, 0.0, 1.0).astype(jnp.bfloat16)
    return low, high


def stacked(block, masks):
    low, high = masks
    return jnp.concatenate([block * low, block * high], axis=0)


def pair_cols(pair):
    return slice(pair * BLOCK, (pair + 1) * BLOCK)


def value_cols(pair):
    return slice(INNER + pair * BLOCK, INNER + (pair + 1) * BLOCK)


def block_rows(block):
    return pl.ds(pl.multiple_of(block * BLOCK, BLOCK), BLOCK)


def fold(values):
    return values.reshape(BLOCK // 8, 8, WIDE)


def shift_tile(gated, rows, own_segment, segment_ref, shared_ref):
    same = segment_ref[rows, :] == own_segment
    inside = shared_ref[rows, 2 * INNER :].astype(jnp.float32) if gated else 0.0
    shift = jnp.where(same, inside, masked_out)
    return jnp.concatenate([shift, shift], axis=1)


def bias_pair(bias_ref, pair, offset):
    return jnp.concatenate([bias_ref[2 * pair, offset], bias_ref[2 * pair + 1, offset]], axis=1)


def pick_heads(wide):
    return jnp.concatenate([wide[:64, :BLOCK], wide[64:, BLOCK:]], axis=0)


def forward_body(gated, low_ref, high_ref, base_ref, *refs):
    query_ref, shared_ref, own_ref, segment_ref, bias_ref = refs[:5]
    mixed_ref, total_ref, turned_ref, score_ref = refs[5:]
    step = pl.program_id(0)
    key_blocks = shared_ref.shape[0] // BLOCK

    @pl.when(step == 0)
    def _():
        @pl.loop(0, key_blocks)
        def _(block):
            rows = block_rows(block)
            turned_ref[:, rows] = shared_ref[rows, INNER : 2 * INNER].T

    first, last = low_ref[step], high_ref[step]
    own_block = base_ref[0] + step
    own_segment = own_ref[0]
    masks = lane_masks()
    queries = [stacked(query_ref[:, pair_cols(pair)], masks) for pair in range(PAIRS)]

    def scores(block, peaks):
        rows = block_rows(block)
        shift = shift_tile(gated, rows, own_segment, segment_ref, shared_ref)
        offset = jnp.clip(block - own_block, -2, 2) + 2
        new_peaks = []
        for pair in range(PAIRS):
            score = lax.dot_general(
                shared_ref[rows, pair_cols(pair)],
                queries[pair],
                both_last,
                preferred_element_type=jnp.float32,
            )
            score = score + bias_pair(bias_ref, pair, offset) + shift
            score_ref[pair, block] = score
            new_peaks.append(jnp.maximum(peaks[pair], jnp.max(fold(score), axis=0)))
        return tuple(new_peaks)

    start = jnp.full((8, WIDE), -3e38, jnp.float32)
    peaks = lax.fori_loop(first, last, scores, (start,) * PAIRS)
    for pair in range(PAIRS):
        peak = jnp.max(peaks[pair], axis=0, keepdims=True)

        def mix(block, carry, pair=pair, peak=peak):
            total, mixed = carry
            weight = jnp.exp(score_ref[pair, block] - peak)
            total = total + jnp.sum(fold(weight), axis=0)
            mixed = mixed + jnp.dot(
                turned_ref[pair_cols(pair), block_rows(block)],
                weight.astype(jnp.bfloat16),
                preferred_element_type=jnp.float32,
            )
            return total, mixed

        zero = (jnp.zeros((8, WIDE), jnp.float32), jnp.zeros((BLOCK, WIDE), jnp.float32))
        total, mixed = lax.fori_loop(first, last, mix, zero)
        row_total = jnp.sum(total, axis=0, keepdims=True)
        mixed = pick_heads(mixed * (1.0 / row_total))
        mixed_ref[:, pair_cols(pair)] = mixed.T.astype(jnp.bfloat16)
        total_ref[0, pair : pair + 1, :] = peak + jnp.log(row_total)


def whole(shape):
    return pl.BlockSpec(shape, lambda i, *_: (0,) * len(shape), pipeline_mode=pl.Buffered(1))


def rows_spec(width):
    return pl.BlockSpec((BLOCK, width), lambda i, *_: (i, 0))


def attend_forward(queries, shared, context):
    lows, highs, base, own_rows, segment_wide, tiles = context
    tokens, (length, width) = queries.shape[0], shared.shape
    steps, key_blocks = tokens // BLOCK, length // BLOCK
    return pl.pallas_call(
        functools.partial(forward_body, width > 2 * INNER),
        grid_spec=pltpu.PrefetchScalarGridSpec(
            num_scalar_prefetch=3,
            grid=(steps,),
            in_specs=[
                rows_spec(INNER),
                whole((length, width)),
                pl.BlockSpec((1, 1, BLOCK), lambda i, *_: (i, 0, 0)),
                whole((length, BLOCK)),
                whole(tiles.shape),
            ],
            out_specs=[
                rows_spec(INNER),
                pl.BlockSpec((1, 8, WIDE), lambda i, *_: (i, 0, 0)),
            ],
            scratch_shapes=[
                pltpu.VMEM((INNER, length), jnp.bfloat16),
                pltpu.VMEM((PAIRS, key_blocks, BLOCK, WIDE), jnp.float32),
            ],
        ),
        out_shape=[
            jax.ShapeDtypeStruct((tokens, INNER), jnp.bfloat16),
            jax.ShapeDtypeStruct((steps, 8, WIDE), jnp.float32),
        ],
        compiler_params=pltpu.CompilerParams(vmem_limit_bytes=40 << 20),
        cost_estimate=pl.CostEstimate(
            flops=tokens * length * INNER * 4,
            bytes_accessed=8 << 20,
            transcendentals=tokens * length * 3,
        ),
        name="attend_forward",
    )(lows, highs, base, queries, shared, own_rows, segment_wide, tiles)


def backward_body(gated, low_ref, high_ref, base_ref, *refs):
    query_ref, grad_ref, shared_ref, own_ref, segment_ref, bias_ref, total_ref = refs[:7]
    grad_query_ref, grad_shared_ref, bucket_ref = refs[7:10]
    turned_ref, prob_ref, pull_ref, sum_ref, bias_sum_ref, turn_sum_ref = refs[10:]
    step = pl.program_id(0)
    key_blocks = shared_ref.shape[0] // BLOCK

    @pl.when(step == 0)
    def _():
        bias_sum_ref[...] = jnp.zeros_like(bias_sum_ref)

        @pl.loop(0, key_blocks)
        def _(block):
            rows = block_rows(block)
            turned_ref[:, rows] = shared_ref[rows, :INNER].T
            sum_ref[rows, :] = jnp.zeros((BLOCK, sum_ref.shape[1]), jnp.float32)

    first, last = low_ref[step], high_ref[step]
    own_block = base_ref[0] + step
    own_segment = own_ref[0]
    masks = lane_masks()
    queries = [stacked(query_ref[:, pair_cols(pair)], masks) for pair in range(PAIRS)]
    grads = [stacked(grad_ref[:, pair_cols(pair)], masks) for pair in range(PAIRS)]
    totals = [total_ref[0, pair : pair + 1, :] for pair in range(PAIRS)]

    def weights(block, deltas):
        rows = block_rows(block)
        shift = shift_tile(gated, rows, own_segment, segment_ref, shared_ref)
        offset = jnp.clip(block - own_block, -2, 2) + 2
        new_deltas = []
        for pair in range(PAIRS):
            cols = pair_cols(pair)
            score = lax.dot_general(
                shared_ref[rows, cols], queries[pair], both_last, preferred_element_type=jnp.float32
            )
            pull = lax.dot_general(
                shared_ref[rows, value_cols(pair)],
                grads[pair],
                both_last,
                preferred_element_type=jnp.float32,
            )
            prob = jnp.exp(score + bias_pair(bias_ref, pair, offset) + shift - totals[pair])
            prob_ref[pair, block] = prob
            pull_ref[pair, block] = pull
            sum_ref[rows, value_cols(pair)] += jnp.dot(
                prob.astype(jnp.bfloat16), grads[pair], preferred_element_type=jnp.float32
            )
            new_deltas.append(deltas[pair] + jnp.sum(fold(prob * pull), axis=0))
        return tuple(new_deltas)

    start = jnp.zeros((8, WIDE), jnp.float32)
    deltas = lax.fori_loop(first, last, weights, (start,) * PAIRS)
    deltas = [jnp.sum(delta, axis=0, keepdims=True) for delta in deltas]
    turn_sum_ref[...] = jnp.zeros_like(turn_sum_ref)

    @pl.loop(first, last)
    def _(block):
        rows = block_rows(block)
        offset = jnp.clip(block - own_block, -2, 2) + 2
        gate_part = jnp.zeros((BLOCK, BLOCK), jnp.float32)
        for pair in range(PAIRS):
            cols = pair_cols(pair)
            grad_score = prob_ref[pair, block] * (pull_ref[pair, block] - deltas[pair])
            bias_sum_ref[pair, offset] += grad_score
            if gated:
                gate_part = gate_part + (grad_score[:, :BLOCK] + grad_score[:, BLOCK:])
            score_low = grad_score.astype(jnp.bfloat16)
            sum_ref[rows, cols] += jnp.dot(
                score_low, queries[pair], preferred_element_type=jnp.float32
            )
            turn_sum_ref[pair] += jnp.dot(
                turned_ref[cols, rows], score_low, preferred_element_type=jnp.float32
            )
        if gated:
            sum_ref[rows, 2 * INNER :] += gate_part

    for pair in range(PAIRS):
        grad_query_ref[:, pair_cols(pair)] = pick_heads(turn_sum_ref[pair]).T.astype(jnp.bfloat16)

    @pl.when(step == pl.num_programs(0) - 1)
    def _():
        @pl.loop(0, key_blocks)
        def _(block):
            rows = block_rows(block)
            both = slice(0, 2 * INNER)
            grad_shared_ref[rows, both] = sum_ref[rows, both].astype(jnp.bfloat16)
            if gated:
                gate_total = jnp.sum(sum_ref[rows, 2 * INNER :], axis=1, keepdims=True)
                grad_shared_ref[rows, 2 * INNER :] = jnp.broadcast_to(
                    gate_total, (BLOCK, BLOCK)
                ).astype(jnp.bfloat16)

        tables = {offset: tile_buckets(offset, WIDE) for offset in (-1, 0, 1)}

        @pl.loop(0, PAIRS)
        def _(pair):
            for bucket in range(BUCKETS):
                part = jnp.zeros((8, WIDE), jnp.float32)
                for offset in (-1, 0, 1):
                    if bucket in near_buckets(offset):
                        chosen = jnp.where(
                            tables[offset] == bucket, bias_sum_ref[pair, offset + 2], 0.0
                        )
                        part = part + jnp.sum(fold(chosen), axis=0)
                if bucket == 15:
                    part = part + jnp.sum(fold(bias_sum_ref[pair, 0]), axis=0)
                if bucket == 31:
                    part = part + jnp.sum(fold(bias_sum_ref[pair, 4]), axis=0)
                bucket_ref[pair, bucket : bucket + 1, :] = jnp.sum(part, axis=0, keepdims=True)


def attend_backward(queries, grad_mixed, shared, log_total, context):
    lows, highs, base, own_rows, segment_wide, tiles = context
    tokens, (length, width) = queries.shape[0], shared.shape
    steps, key_blocks = tokens // BLOCK, length // BLOCK
    grad_query, grad_shared, bucket_sums = pl.pallas_call(
        functools.partial(backward_body, width > 2 * INNER),
        grid_spec=pltpu.PrefetchScalarGridSpec(
            num_scalar_prefetch=3,
            grid=(steps,),
            in_specs=[
                rows_spec(INNER),
                rows_spec(INNER),
                whole((length, width)),
                pl.BlockSpec((1, 1, BLOCK), lambda i, *_: (i, 0, 0)),
                whole((length, BLOCK)),
                whole(tiles.shape),
                pl.BlockSpec((1, 8, WIDE), lambda i, *_: (i, 0, 0)),
            ],
            out_specs=[
                rows_spec(INNER),
                whole((length, width)),
                whole((PAIRS, BUCKETS, WIDE)),
            ],
            scratch_shapes=[
                pltpu.VMEM((INNER, length), jnp.bfloat16),
                pltpu.VMEM((PAIRS, key_blocks, BLOCK, WIDE), jnp.float32),
                pltpu.VMEM((PAIRS, key_blocks, BLOCK, WIDE), jnp.float32),
                pltpu.VMEM((length, width), jnp.float32),
                pltpu.VMEM((PAIRS, OFFSETS, BLOCK, WIDE), jnp.float32),
                pltpu.VMEM((PAIRS, BLOCK, WIDE), jnp.float32),
            ],
        ),
        out_shape=[
            jax.ShapeDtypeStruct((tokens, INNER), jnp.bfloat16),
            jax.ShapeDtypeStruct((length, width), jnp.bfloat16),
            jax.ShapeDtypeStruct((PAIRS, BUCKETS, WIDE), jnp.float32),
        ],
        compiler_params=pltpu.CompilerParams(vmem_limit_bytes=48 << 20),
        cost_estimate=pl.CostEstimate(
            flops=tokens * length * INNER * 10,
            bytes_accessed=12 << 20,
            transcendentals=tokens * length * 3,
        ),
        name="attend_backward",
    )(lows, highs, base, queries, grad_mixed, shared, own_rows, segment_wide, tiles, log_total)
    table = jnp.sum(bucket_sums.reshape(PAIRS, BUCKETS, 2, BLOCK), axis=3)
    return grad_query, grad_shared, table.transpose(1, 0, 2).reshape(BUCKETS, HEADS)


def attention_context(segment_row, first_pos, tokens, rel_bias):
    length = segment_row.shape[0]
    steps = tokens // BLOCK
    own = lax.dynamic_slice_in_dim(segment_row, first_pos, tokens, 0).reshape(steps, 1, BLOCK)
    lows = jnp.sum(segment_row[None, :] < own[:, 0, :1], axis=1, dtype=jnp.int32) // BLOCK
    ends = jnp.sum(segment_row[None, :] <= own[:, 0, BLOCK - 1 :], axis=1, dtype=jnp.int32)
    highs = (ends + BLOCK - 1) // BLOCK
    base = (first_pos // BLOCK).astype(jnp.int32).reshape(1)
    segment_wide = jnp.broadcast_to(segment_row[:, None], (length, BLOCK))
    return lows, highs, base, own, segment_wide, bias_tiles(rel_bias)

HEAD_DIM = 64
FF = 3584
epsilon = 1e-06
gate_scale = -30.0
gate_offset = -3.5

def rms_forward(stream, gain_row):
    inverse = lax.rsqrt(jnp.mean(stream * stream, axis=1, keepdims=True) + epsilon)
    return (stream * inverse * gain_row, inverse)


def stream_backward(stream, inverse, scaled):
    return inverse * scaled - stream * inverse**3 * jnp.mean(scaled * stream, axis=1, keepdims=True)


def rms_backward(stream, inverse, gain_row, grad_normed):
    grad_gain = jnp.sum(grad_normed * stream * inverse, axis=0)
    return (stream_backward(stream, inverse, gain_row * grad_normed), grad_gain)


def gelu_tanh(values):
    return 0.5 * values * (1.0 + jnp.tanh(0.7978845608028654 * (values + 0.044715 * values**3)))


def times_rows(left_side, weight):
    return lax.dot_general(
        left_side, weight, (((1,), (1,)), ((), ())), preferred_element_type=jnp.float32
    )


def times_plain(left_side, weight):
    return jnp.dot(left_side, weight, preferred_element_type=jnp.float32)


def outer_sum(left_side, right_side):
    return lax.dot_general(
        left_side, right_side, (((0,), (0,)), ((), ())), preferred_element_type=jnp.float32
    )


def fetch_rows(local_rows):
    return lax.all_gather(local_rows, ("dp", "seq"), axis=0, tiled=True)


def reduce_rows(grad_rows):
    summed = lax.psum_scatter(grad_rows, ("dp", "seq"), scatter_dimension=0, tiled=True)
    return summed.astype(jnp.float32)


def share_keys(projected, gate_low):
    parts = [projected[:, INNER:]]
    if gate_low is not None:
        parts.append(jnp.broadcast_to(gate_low[:, None], (gate_low.shape[0], BLOCK)))
    return lax.all_gather(jnp.concatenate(parts, axis=1), "seq", axis=0, tiled=True)


def layer_forward(stream, gathered, gain_one, gain_two, gate_low, context):
    normed, inverse_one = rms_forward(stream, gain_one)
    normed_low = normed.astype(jnp.bfloat16)
    projected = times_rows(normed_low, gathered[: 3 * INNER]).astype(jnp.bfloat16)
    queries = projected[:, :INNER]
    shared = share_keys(projected, gate_low)
    attended, log_total = attend_forward(queries, shared, context)
    middle = stream + times_plain(attended, gathered[3 * INNER : 4 * INNER])
    normed_two, inverse_two = rms_forward(middle, gain_two)
    normed_two_low = normed_two.astype(jnp.bfloat16)
    up_both = times_rows(normed_two_low, gathered[4 * INNER : 4 * INNER + 2 * FF])
    up_gelu = up_both[:, :FF]
    up_linear = up_both[:, FF:]
    hidden = (gelu_tanh(up_gelu) * up_linear).astype(jnp.bfloat16)
    result = middle + times_plain(hidden, gathered[4 * INNER + 2 * FF :])
    kept = (
        stream,
        inverse_one,
        normed_low,
        queries,
        shared,
        attended,
        log_total,
        middle,
        inverse_two,
        normed_two_low,
        up_gelu,
        up_linear,
        hidden,
    )
    return (result, kept)


def layer_backward(grad_out, kept, gathered, gain_one, gain_two, context):
    (
        stream,
        inverse_one,
        normed_low,
        queries,
        shared,
        attended,
        log_total,
        middle,
        inverse_two,
        normed_two_low,
        up_gelu,
        up_linear,
        hidden,
    ) = kept
    w_down = gathered[4 * INNER + 2 * FF :]
    branch_low = grad_out.astype(jnp.bfloat16)
    grad_down = outer_sum(hidden, branch_low).astype(jnp.bfloat16)
    grad_hidden = times_rows(branch_low, w_down)
    activated, gelu_pullback = jax.vjp(gelu_tanh, up_gelu)
    grad_gelu = gelu_pullback(grad_hidden * up_linear)[0]
    grad_ffn_low = jnp.concatenate([grad_gelu, grad_hidden * activated], axis=1).astype(
        jnp.bfloat16
    )
    grad_ffn = outer_sum(grad_ffn_low, normed_two_low).astype(jnp.bfloat16)
    grad_normed_two = times_plain(grad_ffn_low, gathered[4 * INNER : 4 * INNER + 2 * FF])
    grad_middle, grad_gain_two = rms_backward(middle, inverse_two, gain_two, grad_normed_two)
    grad_middle = grad_out + grad_middle
    middle_low = grad_middle.astype(jnp.bfloat16)
    grad_attn_out = outer_sum(attended, middle_low).astype(jnp.bfloat16)
    grad_mixed = times_rows(middle_low, gathered[3 * INNER : 4 * INNER]).astype(jnp.bfloat16)
    grad_query, grad_shared, grad_table = attend_backward(
        queries, grad_mixed, shared, log_total, context
    )
    grad_own = lax.psum_scatter(grad_shared, "seq", scatter_dimension=0, tiled=True)
    grad_input_low = jnp.concatenate([grad_query, grad_own[:, : 2 * INNER]], axis=1)
    grad_gate = grad_own[:, 2 * INNER :].astype(jnp.float32)
    grad_input_rows = outer_sum(grad_input_low, normed_low).astype(jnp.bfloat16)
    grad_normed = times_plain(grad_input_low, gathered[: 3 * INNER])
    grad_stream, grad_gain_one = rms_backward(stream, inverse_one, gain_one, grad_normed)
    grad_rows = jnp.concatenate([grad_input_rows, grad_attn_out, grad_ffn, grad_down], axis=0)
    return (
        grad_middle + grad_stream,
        grad_rows,
        grad_table,
        grad_gate,
        grad_gain_one,
        grad_gain_two,
    )


def per_device(
    inputs, layer3_rows, layer4_rows, norm_gains, gate_weight, rel_bias, segment_ids, cotangent
):
    seqs_here, tokens_here, width = inputs.shape
    first_pos = lax.axis_index("seq") * tokens_here
    context = attention_context(segment_ids[0], first_pos, tokens_here, rel_bias)
    stream = inputs.reshape(tokens_here, width)
    gathered_three = fetch_rows(layer3_rows)
    after_three, kept_three = layer_forward(
        stream, gathered_three, norm_gains[0], norm_gains[1], None, context
    )
    gate_inverse = lax.rsqrt(jnp.mean(after_three * after_three, axis=1, keepdims=True) + epsilon)
    gate_normed = after_three * gate_inverse
    gate_logit = jnp.sum(gate_normed * gate_weight, axis=1) + gate_offset
    sigmoid_value = 1.0 / (1.0 + jnp.exp(-gate_logit))
    gate_mask = gate_scale * sigmoid_value
    gate_low = gate_mask.astype(jnp.bfloat16)
    gathered_four = fetch_rows(layer4_rows)
    after_four, kept_four = layer_forward(
        after_three, gathered_four, norm_gains[2], norm_gains[3], gate_low, context
    )
    grad_three_out, rows_four, table_four, grad_gate, gain_four_one, gain_four_two = layer_backward(
        cotangent.reshape(tokens_here, width),
        kept_four,
        gathered_four,
        norm_gains[2],
        norm_gains[3],
        context,
    )
    local_four = reduce_rows(rows_four)
    grad_logit = grad_gate[:, 0] * gate_scale * sigmoid_value * (1.0 - sigmoid_value)
    grad_gate_weight = jnp.sum(grad_logit[:, None] * gate_normed, axis=0)
    gate_stream = stream_backward(after_three, gate_inverse, grad_logit[:, None] * gate_weight)
    grad_three_out = grad_three_out + gate_stream
    grad_input, rows_three, table_three, unused, gain_three_one, gain_three_two = layer_backward(
        grad_three_out,
        kept_three,
        gathered_three,
        norm_gains[0],
        norm_gains[1],
        context,
    )
    local_three = reduce_rows(rows_three)
    gains_grad = jnp.stack([gain_three_one, gain_three_two, gain_four_one, gain_four_two])
    summed = lax.psum((gains_grad, grad_gate_weight, table_three + table_four), ("dp", "seq"))
    return (
        after_four.reshape(inputs.shape),
        gate_mask.reshape(seqs_here, tokens_here),
        grad_input.reshape(inputs.shape),
        local_three,
        local_four,
        summed[0],
        summed[1],
        summed[2],
    )


def solution(mesh):
    placed = (
        P("dp", "seq", None),
        P(("dp", "seq"), None),
        P(("dp", "seq"), None),
        P(),
        P(),
        P(),
        P("dp", None),
        P("dp", "seq", None),
    )
    return jax.shard_map(
        per_device,
        mesh=mesh,
        in_specs=placed,
        out_specs=(
            P("dp", "seq", None),
            P("dp", "seq"),
            P("dp", "seq", None),
            P(("dp", "seq"), None),
            P(("dp", "seq"), None),
            P(),
            P(),
            P(),
        ),
        check_vma=False,
    )
```

time: 3920 us -> 1710 us (0.44)
  matrix products: 1280 us -> 255 us
  local copies, waits for them, and re-layouts: 735 us -> 122 us
  waiting for transfers between devices: 1540 us -> 1080 us
  other arithmetic: 180 us -> 86.2 us
  Pallas kernels: 0 us -> 71.9 us
  loops' own time: 63.7 us -> 0 us
    reduce_scatter x6 -> x2, waiting for transfers between devices: 1170 us -> 78.2 us  [layer_backward(): lax.psum_scatter(grad_shared, 'seq', scatter_dimension=0, tiled=True)]
    dot_general x96 -> x0, matrix products: 1010 us -> none  [the longest x24 877 us: head_scores(): jnp.einsum('btd,bsd->bts', head_slice(queries, head_index), head_slice(al...]
    unnamed x14 -> x10, waiting for transfers between devices: 22.1 us -> 513 us
    rev x12 -> x0, local copies, waits for them, and re-layouts: 392 us -> none  [diagonal_buckets(): flipped = pair_sum[::-1]]
    reshape x24 -> x3, local copies, waits for them, and re-layouts: 176 us -> 0.11 us  [the longest x2 0.1 us: attend_backward(): table = jnp.sum(bucket_sums.reshape(PAIRS, BUCKETS, 2, BLOCK), axis=3)]
    all_gather x2, waiting for transfers between devices: 213 us -> 370 us  [fetch_rows(): return lax.all_gather(local_rows, ('dp', 'seq'), axis=0, tiled=True)]
    unnamed x140, local copies, waits for them, and re-layouts: 10.4 us -> 113 us
    pallas_call x0 -> x5, Pallas kernels: none -> 71.9 us  [the longest x2 43.2 us: attend_backward(): pl.pallas_call(functools.partial(backward_body, width > 2 * INNER), grid_...]
  transfers between devices with their start and end apart: 13 -> 8, of which waited for: 10 -> 7; matrix products, arithmetic and copies ran while one was open for 14% -> 18% of each run, Pallas kernels for 0% -> 1%
where the time goes in v1:
time: 1710 us; the launch traced here: 1700 us
  waiting for transfers between devices  1080 us (63%)
  matrix products  255 us (15%)
  local copies, waits for them, and re-layouts  122 us (7%)
  other arithmetic  86.2 us (5%)
  Pallas kernels  71.9 us (4%)
  blocking collectives  62.2 us (4%)
    unnamed x10, waiting for transfers between devices  513 us
    all_gather x2, waiting for transfers between devices, fetch_rows(): return lax.all_gather(local_rows, ('dp', 'seq'), axis=0, tiled=True)  370 us
    all_gather x2, waiting for transfers between devices, share_keys(): lax.all_gather(jnp.concatenate(parts, axis=1), 'seq', axis=0, tiled=True)  122 us
    unnamed x140, local copies, waits for them, and re-layouts  113 us
    dot_general x8, matrix products, times_rows(): lax.dot_general(left_side, weight, (((1,), (1,)), ((), ())), preferred_el...  95.8 us
    dot_general x8, matrix products, times_plain(): return jnp.dot(left_side, weight, preferred_element_type=jnp.float32)  84.5 us
    reduce_scatter x2, waiting for transfers between devices, layer_backward(): lax.psum_scatter(grad_shared, 'seq', scatter_dimension=0, tiled=True)  78.2 us
    dot_general x8, matrix products, outer_sum(): lax.dot_general(left_side, right_side, (((0,), (0,)), ((), ())), preferre...  74.6 us
  transfers between devices with their start and end apart: 8, of which 7 were waited for; matrix products, arithmetic and copies ran while one was open for 18% of the time, Pallas kernels for 1%

profile of v1, /device:TPU:24, one launch (start us, length us, event | category | flops | bytes accessed | tf_op | source)
XLA Modules:
  0.0 1696.4 jit_solution(1328636655289134001)
XLA Ops:
  8.0 1.6 slice_reduce_fusion
  9.5 2.1 fusion.44
  12.3 213.0 %all-gather.5.cloned.1.call-done = bf16[12288,1472]{0,1:T(8,128)(2,1)} async-done(((bf16[384,1472]{0,1:T(8,128)(2,1)}), bf16[12288,1472]{0,1:T(8,128)(2,1)}) %all-gather.5.cloned.1.call-update) | async-done | bytes 36175888 | tf_op jit(solution)/shard_map/all_gather | solution.py:430
  225.3 4.3 convolution_convert_fusion.7
  229.7 1.0 copy-done.33
  233.4 4.7 bias_tiles.1.refs_4_.refs_5_
  238.7 1.1 slice.117.refs_0_
  239.8 53.0 %all-gather.7.cloned.1.call-done.refs_1_.refs_2_ = bf16[2048,768]{1,0:T(8,128)(2,1)} async-done(((bf16[512,768]{1,0:T(8,128)(2,1)}), bf16[2048,768]{1,0:T(8,128)(2,1)}) %all-gather.7.cloned.1.call-update) | async-done | bytes 3145744 | tf_op jit(solution)/shard_map/all_gather | solution.py:442
  293.1 1.5 copy-done
  294.6 1.9 copy-done.3
  296.5 12.0 attend_forward.2
  308.6 4.0 multiply_reduce_fusion.10
  313.7 20.0 %fusion.6 = f32[512,7168]{1,0:T(8,128)} fusion(bf16[12288,1472]{0,1:T(8,128)(2,1)} %all-gather.5.cloned.1.call-done, f32[512,1472]{0,1:T(8,128)} %get-tuple-element.65, f32[1472]{0:T(1024)S(1)} %get-tuple-element.39, f32[512]{0:T(512)S(1)} %get-tuple-element.59), kind=kOutput, calls=%fused_computation.10 | convolution fusion | flops 10806788096 | bytes 38805248 | tf_op jit(solution)/shard_map/dot_general | solution.py:414
  333.7 6.6 multiply_convert_fusion.3
  340.4 10.5 multiply_reduce_fusion.9
  351.6 1.0 copy-done.23
  353.5 157.2 %all-gather.9.cloned.1.call-done = bf16[12288,1472]{0,1:T(8,128)(2,1)} async-done(((bf16[384,1472]{0,1:T(8,128)(2,1)}), bf16[12288,1472]{0,1:T(8,128)(2,1)}) %all-gather.9.cloned.1.call-update) | async-done | bytes 36175888 | tf_op jit(solution)/shard_map/all_gather | solution.py:430
  510.8 5.2 convolution_convert_fusion.6
  516.0 1.0 copy-done.34
  517.2 1.0 pad_maximum_fusion.9
  518.3 1.0 slice.125.refs_0_
  519.4 68.6 %all-gather.11.cloned.1.call-done.refs_1_.refs_2_ = bf16[2048,896]{1,0:T(8,128)(2,1)} async-done(((bf16[512,896]{1,0:T(8,128)(2,1)}), bf16[2048,896]{1,0:T(8,128)(2,1)}) %all-gather.11.cloned.1.call-update) | async-done | bytes 3670032 | tf_op jit(solution)/shard_map/all_gather | solution.py:442
  588.0 2.0 copy-done.2
  590.0 12.0 attend_forward.3
  602.1 4.0 multiply_reduce_fusion.7
  606.1 19.9 %fusion.2 = f32[512,7168]{1,0:T(8,128)} fusion(bf16[12288,1472]{0,1:T(8,128)(2,1)} %all-gather.9.cloned.1.call-done, f32[512,1472]{0,1:T(8,128)} %get-tuple-element.69, f32[1472]{0:T(1024)S(1)} %copy-done.50, f32[512]{0:T(512)S(1)} %get-tuple-element.63), kind=kOutput, calls=%fused_computation.6 | convolution fusion | flops 10806788096 | bytes 38805248 | tf_op jit(solution)/shard_map/dot_general | solution.py:414
  626.0 20.9 %fusion.31 = (bf16[512,3584]{1,0:T(8,128)(2,1)}, bf16[512,3584]{1,0:T(8,128)(2,1)}, bf16[512,3584]{1,0:T(8,128)(2,1)}) fusion(f32[512,7168]{1,0:T(8,128)} %fusion.2, bf16[12288,1472]{0,1:T(8,128)(2,1)} %all-gather.9.cloned.1.call-done, f32[1,512,1472]{1,2,0:T(8,128)} %param.15), kind=kOutput, calls=%fused_computation.43 | convolution fusion | flops 5449973760 | bytes 39256064 | tf_op jit(solution)/shard_map/dot_general | solution.py:414
  646.9 19.6 %multiply_reduce_fusion.1 = (f32[1472]{0:T(1024)}, f32[512]{0:T(512)S(1)}, f32[512,1472]{0,1:T(8,128)}) fusion(f32[512,1472]{0,1:T(8,128)} %get-tuple-element.69, f32[512]{0:T(512)S(1)} %get-tuple-element.63, f32[1472]{0:T(1024)S(1)} %copy-done.50, bf16[12288,1472]{0,1:T(8,128)(2,1)} %all-gather.9.cloned.1.call-done, ...), kind=kOutput, calls=%fused_computation.80 | convolution fusion | flops 10823727104 | bytes 34487808 | tf_op jit(solution)/shard_map/dot_general | solution.py:420
  666.5 4.3 bitcast_add_fusion
  670.8 3.2 convolution_convert_fusion.11.refs_1_
  674.0 22.3 %attend_backward.2 = (bf16[512,384]{1,0:T(8,128)(2,1)S(1)}, bf16[2048,896]{1,0:T(8,128)(2,1)}, f32[3,32,256]{2,1,0:T(8,128)S(1)}) custom-call(s32[4]{0:T(128)S(1)} %get-tuple-element.75.low_ref, s32[4]{0:T(128)S(1)} %get-tuple-element.74.high_ref, s32[1]{0:T(128)} %bitcast.3.base_ref, bf16[512,384]{1,0:T(8,128)(2,1)S(1)} %slice.125.refs_0_, ...), custom_call_target="tpu_custom_call" | custom-call | flops 4026531840 | bytes 12582912 | tf_op jit(solution)/shard_map/attend_backward/pallas_call | solution.py:333
  698.0 18.6 %convolution_convert_fusion = bf16[7168,1472]{0,1:T(8,128)(2,1)} fusion(bf16[512,3584]{1,0:T(8,128)(2,1)} %get-tuple-element.54, bf16[512,3584]{1,0:T(8,128)(2,1)} %get-tuple-element.53, f32[512,1472]{0,1:T(8,128)} %get-tuple-element.69, f32[1472]{0:T(1024)} %get-tuple-element.38, f32[512]{0:T(512)} %copy-done.65), kind=kOutput, calls=%fused_computation.2 | convolution fusion | flops 10832019456 | bytes 31465216 | tf_op jit(solution)/shard_map/dot_general | solution.py:424
  716.6 78.2 %reduce-scatter.9.cloned.1.call-done = bf16[512,896]{1,0:T(8,128)(2,1)} async-done(((bf16[2048,896]{1,0:T(8,128)(2,1)}), bf16[512,896]{1,0:T(8,128)(2,1)}) %reduce-scatter.9.cloned.1.call-update) | async-done | bytes 917520 | tf_op jit(solution)/shard_map/reduce_scatter | solution.py:513
  794.7 1.2 slice.132
  795.9 1.4 multiply_reduce_fusion.11
  797.4 6.6 multiply_reduce_fusion.2
  804.1 1.5 fusion.42
  805.5 19.0 %fusion.23 = (bf16[512,3584]{1,0:T(8,128)(2,1)}, bf16[512,3584]{1,0:T(8,128)(2,1)}) fusion(f32[512,7168]{1,0:T(8,128)} %fusion.6, bf16[12288,1472]{0,1:T(8,128)(2,1)} %all-gather.5.cloned.1.call-done, f32[512,1472]{0,1:T(8,128)S(1)} %fusion.42), kind=kOutput, calls=%fused_computation.35 | convolution fusion | flops 5447057408 | bytes 35586048 | tf_op jit(solution)/shard_map/dot_general | solution.py:414
  824.6 19.8 %multiply_reduce_fusion.3 = (f32[1472]{0:T(1024)}, f32[512]{0:T(512)S(1)}, f32[512,1472]{0,1:T(8,128)}) fusion(f32[512,1472]{0,1:T(8,128)} %get-tuple-element.65, f32[512]{0:T(512)S(1)} %copy-done.61, f32[1472]{0:T(1024)S(1)} %copy-done.45, bf16[12288,1472]{0,1:T(8,128)(2,1)} %all-gather.5.cloned.1.call-done, bf16[512,3584]{1,0:T(8,128)(2,1)} %get-tuple-element.52, ...), kind=kOutput, calls=%fused_computation.82 | convolution fusion | flops 10823727104 | bytes 34487808 | tf_op jit(solution)/shard_map/dot_general | solution.py:420
  844.4 4.3 subtract_add_fusion
  848.7 3.2 convolution_convert_fusion.10.refs_1_
  852.0 20.9 %attend_backward.3 = (bf16[512,384]{1,0:T(8,128)(2,1)S(1)}, bf16[2048,768]{1,0:T(8,128)(2,1)}, f32[3,32,256]{2,1,0:T(8,128)S(1)}) custom-call(s32[4]{0:T(128)S(1)} %get-tuple-element.75.low_ref, s32[4]{0:T(128)S(1)} %get-tuple-element.74.high_ref, s32[1]{0:T(128)} %bitcast.3.base_ref, bf16[512,384]{1,0:T(8,128)(2,1)S(1)} %copy-done.9, ...), custom_call_target="tpu_custom_call" | custom-call | flops 4026531840 | bytes 12582912 | tf_op jit(solution)/shard_map/attend_backward/pallas_call | solution.py:333
  874.5 2.9 convolution_convert_fusion.8
  877.5 10.4 fusion.82
  887.9 3.9 convolution_convert_fusion.4
  891.8 24.3 %pad_maximum_fusion.1 = bf16[12288,1472]{0,1:T(8,128)(2,1)} fusion(bf16[3584,1472]{0,1:T(8,128)(2,1)} %fusion.82, bf16[7168,1472]{0,1:T(8,128)(2,1)} %convolution_convert_fusion, bf16[384,1472]{0,1:T(8,128)(2,1)S(1)} %convolution_convert_fusion.8, bf16[1152,1472]{0,1:T(8,128)(2,1)} %convolution_convert_fusion.4), kind=kLoop, calls=%fused_computation.1 | loop fusion | flops 144703488 | bytes 72351744 | tf_op jit(solution)/shard_map/concatenate | solution.py:519
  916.1 48.4 %copy.37 = bf16[12288,1472]{1,0:T(8,128)(2,1)} copy(bf16[12288,1472]{0,1:T(8,128)(2,1)} %pad_maximum_fusion.1) | data formatting | bytes 72351744
  965.4 3.0 convolution_convert_fusion.9
  968.5 10.6 convolution_convert_fusion.3
  979.1 18.6 %convolution_convert_fusion.1 = bf16[7168,1472]{0,1:T(8,128)(2,1)} fusion(bf16[512,3584]{1,0:T(8,128)(2,1)} %get-tuple-element.52, bf16[512,3584]{1,0:T(8,128)(2,1)} %get-tuple-element.51, f32[512,1472]{0,1:T(8,128)S(1)} %copy-done.28, f32[1472]{0:T(1024)S(1)} %copy-done.46, f32[512]{0:T(512)S(1)} %copy-done.62), kind=kOutput, calls=%fused_computation.3 | convolution fusion | flops 10832019456 | bytes 31465216 | tf_op jit(solution)/shard_map/dot_general | solution.py:424
  997.7 1.4 constant_dynamic-update-slice_fusion
  999.1 6.7 convolution_convert_fusion.5
  1005.8 28.9 %pad_maximum_fusion = bf16[12288,1472]{0,1:T(8,128)(2,1)} fusion(bf16[3584,1472]{0,1:T(8,128)(2,1)} %convolution_convert_fusion.3, bf16[7168,1472]{0,1:T(8,128)(2,1)} %convolution_convert_fusion.1, bf16[384,1472]{0,1:T(8,128)(2,1)S(1)} %convolution_convert_fusion.9, bf16[1152,1472]{0,1:T(8,128)(2,1)} %convolution_convert_fusion.5), kind=kLoop, calls=%fused_computation | loop fusion | flops 144703488 | bytes 72351744 | tf_op jit(solution)/shard_map/concatenate | solution.py:519
  1034.7 46.0 %copy.35 = bf16[12288,1472]{1,0:T(8,128)(2,1)} copy(bf16[12288,1472]{0,1:T(8,128)(2,1)} %pad_maximum_fusion) | data formatting | bytes 72351744
  1081.7 12.4 fusion.38
  1094.6 7.6 fusion.53
  1102.3 62.2 %all-reduce = (f32[4,1472]{1,0:T(4,128)}, f32[1472]{0:T(1024)}, f32[32,6]{0,1:T(8,128)}) all-reduce(f32[4,1472]{1,0:T(4,128)S(1)} %pad_maximum_fusion.12, f32[1472]{0:T(1024)S(1)} %copy-done.56, f32[32,6]{0,1:T(8,128)S(1)} %add.205), channel_id=1, replica_groups=mesh['dp'=8,'seq'=4] {'dp','seq'}, use_global_device_ids=true, to_apply=%region_20.21 | all-reduce | flops 7552 | bytes 60416 | tf_op jit(solution)/shard_map/psum | solution.py:574
  1164.5 5.2 fusion.50
  1169.7 160.7 %reduce-scatter.15.cloned.1.call-done = bf16[384,1472]{1,0:T(8,128)(2,1)} async-done(((bf16[12288,1472]{1,0:T(8,128)(2,1)}), bf16[384,1472]{1,0:T(8,128)(2,1)}) %reduce-scatter.15.cloned.1.call-update) | async-done | bytes 1130512
  1330.4 2.3 copy.38
  1332.7 1.5 convert_element_type.114
  1334.2 351.4 %reduce-scatter.13.cloned.1.call-done = bf16[384,1472]{1,0:T(8,128)(2,1)} async-done(((bf16[12288,1472]{1,0:T(8,128)(2,1)}), bf16[384,1472]{1,0:T(8,128)(2,1)}) %reduce-scatter.13.cloned.1.call-update) | async-done | bytes 1130512
  1685.5 2.3 copy.36
  1687.8 1.5 convert_element_type.109
  (180 shorter events, 13.7 us)
Async XLA Ops:
  7.2 218.1 %copy-start.21 = (f32[1,512,1472]{1,2,0:T(8,128)S(1)}, f32[1,512,1472]{1,2,0:T(8,128)}, u32[]{:S(2)}) copy-start(f32[1,512,1472]{1,2,0:T(8,128)} %param.8) | copy-start | bytes 9043972
  7.2 218.1 %all-gather.5.cloned.1.call-start = ((), (), s32[]{:S(2)}) async-start(), calls=%async_computation.4 | async-start | bytes 37306368 | tf_op jit(solution)/shard_map/all_gather | solution.py:430
  7.9 284.8 %all-gather.7.cloned.1.call-start = ((), (), s32[]{:S(2)}) async-start(), calls=%async_computation.5 | async-start | bytes 3932160 | tf_op jit(solution)/shard_map/all_gather | solution.py:442
  9.5 220.1 %copy-start.42 = (f32[1472]{0:T(1024)}, f32[1472]{0:T(1024)S(1)}, u32[]{:S(2)}) copy-start(f32[1472]{0:T(1024)S(1)} %get-tuple-element.40) | copy-start | bytes 17668
  9.5 303.7 %copy-start.44 = (f32[1472]{0:T(1024)}, f32[1472]{0:T(1024)S(1)}, u32[]{:S(2)}) copy-start(f32[1472]{0:T(1024)S(1)} %get-tuple-element.39) | copy-start | bytes 17668
  9.5 501.2 %copy-start.47 = (f32[1472]{0:T(1024)}, f32[1472]{0:T(1024)S(1)}, u32[]{:S(2)}) copy-start(f32[1472]{0:T(1024)S(1)} %get-tuple-element.41) | copy-start | bytes 17668
  12.3 217.4 %copy-start.58 = (f32[512]{0:T(512)}, f32[512]{0:T(512)S(1)}, u32[]{:S(2)}) copy-start(f32[512]{0:T(512)S(1)} %get-tuple-element.57) | copy-start | bytes 6148
  230.7 2.0 copy-start.66
  230.7 7.5 copy-start.39
  231.6 279.1 %all-gather.9.cloned.1.call-start = ((), (), s32[]{:S(2)}) async-start(), calls=%async_computation.6 | async-start | bytes 37306368 | tf_op jit(solution)/shard_map/all_gather | solution.py:430
  232.4 355.6 %all-gather.11.cloned.1.call-start = ((), (), s32[]{:S(2)}) async-start(), calls=%async_computation.7 | async-start | bytes 4587520 | tf_op jit(solution)/shard_map/all_gather | solution.py:442
  239.8 68.8 %copy-start.8 = (bf16[512,384]{1,0:T(8,128)(2,1)}, bf16[512,384]{1,0:T(8,128)(2,1)S(1)}, u32[]{:S(2)}) copy-start(bf16[512,384]{1,0:T(8,128)(2,1)S(1)} %slice.117.refs_0_) | copy-start | bytes 1179652
  296.5 12.0 copy-start.22
  308.5 4.1 copy-start.4
  333.7 6.7 copy-start.27
  340.4 10.6 copy-start.31
  340.4 12.2 copy-start.40
  351.6 159.2 %copy-start.51 = (f32[512]{0:T(512)}, f32[512]{0:T(512)S(1)}, u32[]{:S(2)}) copy-start(f32[512]{0:T(512)S(1)} %get-tuple-element.61) | copy-start | bytes 6148
  517.0 70.9 %copy-start.1 = (f32[6,5,128,128]{3,2,1,0:T(8,128)S(1)}, f32[6,5,128,128]{3,2,1,0:T(8,128)}, u32[]{:S(2)}) copy-start(f32[6,5,128,128]{3,2,1,0:T(8,128)} %bias_tiles.1.refs_4_.refs_5_) | copy-start | bytes 5898244
  518.3 276.5 %reduce-scatter.9.cloned.1.call-start = ((), (), s32[]{:S(2)}) async-start(), calls=%async_computation.8 | async-start | bytes 4587520 | tf_op jit(solution)/shard_map/reduce_scatter | solution.py:513
  588.0 2.0 copy-start.2
  590.0 12.0 copy-start.24
  602.0 4.0 copy-start.6
  602.0 4.0 copy-start.12
  602.1 4.0 copy-start.50
  606.1 60.4 %copy-start.65 = (f32[512]{0:T(512)}, f32[512]{0:T(512)S(1)}, u32[]{:S(2)}) copy-start(f32[512]{0:T(512)S(1)} %get-tuple-element.63) | copy-start | bytes 6148
  670.8 3.2 copy-start.19
  670.8 3.2 copy-start.13
  697.0 300.6 %reduce-scatter.11.cloned.1.call-start = ((), (), s32[]{:S(2)}) async-start(), calls=%async_computation.9 | async-start | bytes 3932160 | tf_op jit(solution)/shard_map/reduce_scatter | solution.py:513
  698.0 99.4 %copy-start.15 = (bf16[512,384]{1,0:T(8,128)(2,1)S(1)}, bf16[512,384]{1,0:T(8,128)(2,1)}, u32[]{:S(2)}) copy-start(bf16[512,384]{1,0:T(8,128)(2,1)} %copy-done.14) | copy-start | bytes 1179652
  698.0 99.4 %copy-start.52 = (f32[512]{0:T(512)S(1)}, f32[512]{0:T(512)}, u32[]{:S(2)}) copy-start(f32[512]{0:T(512)} %copy-done.51) | copy-start | bytes 6148
  795.9 8.1 copy-start.35
  797.4 6.6 copy-start.20
  797.4 6.6 copy-start.25
  797.4 6.6 copy-start.41
  797.4 6.6 copy-start.48
  797.4 6.6 copy-start.64
  805.5 19.1 %copy-start.29 = (f32[512,1472]{0,1:T(8,128)}, f32[512,1472]{0,1:T(8,128)S(1)}, u32[]{:S(2)}) copy-start(f32[512,1472]{0,1:T(8,128)S(1)} %fusion.42) | copy-start | bytes 9043972
  805.5 19.0 %copy-start.45 = (f32[1472]{0:T(1024)S(1)}, f32[1472]{0:T(1024)}, u32[]{:S(2)}) copy-start(f32[1472]{0:T(1024)} %copy-done.44) | copy-start | bytes 17668
  805.5 19.0 %copy-start.61 = (f32[512]{0:T(512)S(1)}, f32[512]{0:T(512)}, u32[]{:S(2)}) copy-start(f32[512]{0:T(512)} %copy-done.60) | copy-start | bytes 6148
  824.6 19.8 %copy-start.63 = (f32[512]{0:T(512)S(1)}, f32[512]{0:T(512)}, u32[]{:S(2)}) copy-start(f32[512]{0:T(512)} %get-tuple-element.58) | copy-start | bytes 6148
  848.7 3.3 copy-start.17
  848.7 3.3 copy-start.9
  873.5 456.9 %reduce-scatter.15.cloned.1.call-start = ((), (), s32[]{:S(2)}) async-start(), calls=%async_computation.11 | async-start | bytes 38928384
  874.5 3.0 copy-start.32
  877.4 10.4 copy-start.16
  877.5 10.4 copy-start.26
  877.5 10.4 copy-start.36
  877.5 10.4 copy-start.49
  964.5 721.1 %reduce-scatter.13.cloned.1.call-start = ((), (), s32[]{:S(2)}) async-start(), calls=%async_computation.10 | async-start | bytes 38928384
  964.5 3.9 copy-start.30
  968.4 10.6 copy-start.28
  968.4 10.6 copy-start.46
  968.4 10.6 copy-start.62
  979.0 18.6 %copy-start.37 = (bf16[512,1152]{1,0:T(8,128)(2,1)S(1)}, bf16[512,1152]{1,0:T(8,128)(2,1)}, u32[]{:S(2)}) copy-start(bf16[512,1152]{1,0:T(8,128)(2,1)} %constant_dynamic-update-slice_fusion.1) | copy-start | bytes 3538948
  979.0 20.0 %copy-start.43 = (f32[1472]{0:T(1024)S(1)}, f32[1472]{0:T(1024)}, u32[]{:S(2)}) copy-start(f32[1472]{0:T(1024)} %copy-done.42) | copy-start | bytes 17668
  979.0 20.0 %copy-start.59 = (f32[512]{0:T(512)S(1)}, f32[512]{0:T(512)}, u32[]{:S(2)}) copy-start(f32[512]{0:T(512)} %copy-done.58) | copy-start | bytes 6148
  999.0 6.7 copy-start.38
  1081.7 12.4 copy-start.54
  1081.7 12.5 copy-start.55
  1081.7 12.5 copy-start.11
  1094.6 7.7 copy-start.56
  1094.6 69.9 %copy-start.18 = (f32[512,1472]{0,1:T(8,128)S(1)}, f32[512,1472]{0,1:T(8,128)}, u32[]{:S(2)}) copy-start(f32[512,1472]{0,1:T(8,128)} %copy-done.17) | copy-start | bytes 9043972
  1094.6 69.9 %copy-start.57 = (f32[512]{0:T(512)S(1)}, f32[512]{0:T(512)}, u32[]{:S(2)}) copy-start(f32[512]{0:T(512)} %get-tuple-element.56) | copy-start | bytes 6148
  (11 other events, 11.7 us)
Sparse Core Ops, SparseCore 0:
  10.9 214.3 all-gather.4
  231.8 60.9 all-gather.6
  295.7 215.0 all-gather.8
  518.4 69.5 all-gather.10
  697.2 97.5 reduce-scatter.8
  873.6 76.5 reduce-scatter.10
  964.6 365.7 reduce-scatter.14
  1337.9 347.5 reduce-scatter.12

commit v2 on v1

--- a/solution.py
+++ b/solution.py
@@ -5,6 +5,7 @@
 from jax import lax
 from jax.experimental import pallas as pl
 from jax.experimental.pallas import tpu as pltpu
+from jax.sharding import Mesh
 from jax.sharding import PartitionSpec as P
 
 HEADS = 6
@@ -13,7 +14,18 @@
 WIDE = 2 * BLOCK
 INNER = 384
 BUCKETS = 32
+FF = 3584
+REACH = 799
+HALO = 896
+TILE = 256
+ATTENTION_TILES = 4 * INNER // TILE
 OFFSETS = 5
+CHUNK = 384
+CUTS = (0, 384, 768, 1152, 1472)
+DEVICES = ("y", "x", "c", "z")
+epsilon = 1e-06
+gate_scale = -30.0
+gate_offset = -3.5
 masked_out = -1e30
 limits = (12, 16, 23, 32, 46, 64, 91)
 both_last = (((1,), (1,)), ((), ()))
@@ -108,7 +120,7 @@
     return jnp.concatenate([wide[:64, :BLOCK], wide[64:, BLOCK:]], axis=0)
 
 
-def forward_body(gated, low_ref, high_ref, base_ref, *refs):
+def forward_body(gated, low_ref, high_ref, *refs):
     query_ref, shared_ref, own_ref, segment_ref, bias_ref = refs[:5]
     mixed_ref, total_ref, turned_ref, score_ref = refs[5:]
     step = pl.program_id(0)
@@ -122,7 +134,7 @@
             turned_ref[:, rows] = shared_ref[rows, INNER : 2 * INNER].T
 
     first, last = low_ref[step], high_ref[step]
-    own_block = base_ref[0] + step
+    own_block = HALO // BLOCK + step
     own_segment = own_ref[0]
     masks = lane_masks()
     queries = [stacked(query_ref[:, pair_cols(pair)], masks) for pair in range(PAIRS)]
@@ -177,13 +189,13 @@
 
 
 def attend_forward(queries, shared, context):
-    lows, highs, base, own_rows, segment_wide, tiles = context
+    lows, highs, own_rows, segment_wide, tiles = context
     tokens, (length, width) = queries.shape[0], shared.shape
     steps, key_blocks = tokens // BLOCK, length // BLOCK
     return pl.pallas_call(
         functools.partial(forward_body, width > 2 * INNER),
         grid_spec=pltpu.PrefetchScalarGridSpec(
-            num_scalar_prefetch=3,
+            num_scalar_prefetch=2,
             grid=(steps,),
             in_specs=[
                 rows_spec(INNER),
@@ -212,10 +224,10 @@
             transcendentals=tokens * length * 3,
         ),
         name="attend_forward",
-    )(lows, highs, base, queries, shared, own_rows, segment_wide, tiles)
-
-
-def backward_body(gated, low_ref, high_ref, base_ref, *refs):
+    )(lows, highs, queries, shared, own_rows, segment_wide, tiles)
+
+
+def backward_body(gated, low_ref, high_ref, *refs):
     query_ref, grad_ref, shared_ref, own_ref, segment_ref, bias_ref, total_ref = refs[:7]
     grad_query_ref, grad_shared_ref, bucket_ref = refs[7:10]
     turned_ref, prob_ref, pull_ref, sum_ref, bias_sum_ref, turn_sum_ref = refs[10:]
@@ -233,7 +245,7 @@
             sum_ref[rows, :] = jnp.zeros((BLOCK, sum_ref.shape[1]), jnp.float32)
 
     first, last = low_ref[step], high_ref[step]
-    own_block = base_ref[0] + step
+    own_block = HALO // BLOCK + step
     own_segment = own_ref[0]
     masks = lane_masks()
     queries = [stacked(query_ref[:, pair_cols(pair)], masks) for pair in range(PAIRS)]
@@ -327,13 +339,13 @@
 
 
 def attend_backward(queries, grad_mixed, shared, log_total, context):
-    lows, highs, base, own_rows, segment_wide, tiles = context
+    lows, highs, own_rows, segment_wide, tiles = context
     tokens, (length, width) = queries.shape[0], shared.shape
     steps, key_blocks = tokens // BLOCK, length // BLOCK
     grad_query, grad_shared, bucket_sums = pl.pallas_call(
         functools.partial(backward_body, width > 2 * INNER),
         grid_spec=pltpu.PrefetchScalarGridSpec(
-            num_scalar_prefetch=3,
+            num_scalar_prefetch=2,
             grid=(steps,),
             in_specs=[
                 rows_spec(INNER),
@@ -370,27 +382,23 @@
             transcendentals=tokens * length * 3,
         ),
         name="attend_backward",
-    )(lows, highs, base, queries, grad_mixed, shared, own_rows, segment_wide, tiles, log_total)
+    )(lows, highs, queries, grad_mixed, shared, own_rows, segment_wide, tiles, log_total)
     table = jnp.sum(bucket_sums.reshape(PAIRS, BUCKETS, 2, BLOCK), axis=3)
     return grad_query, grad_shared, table.transpose(1, 0, 2).reshape(BUCKETS, HEADS)
 
 
 def attention_context(segment_row, first_pos, tokens, rel_bias):
-    length = segment_row.shape[0]
     steps = tokens // BLOCK
-    own = lax.dynamic_slice_in_dim(segment_row, first_pos, tokens, 0).reshape(steps, 1, BLOCK)
-    lows = jnp.sum(segment_row[None, :] < own[:, 0, :1], axis=1, dtype=jnp.int32) // BLOCK
-    ends = jnp.sum(segment_row[None, :] <= own[:, 0, BLOCK - 1 :], axis=1, dtype=jnp.int32)
+    padded = jnp.pad(segment_row, (HALO, 0), constant_values=-1)
+    padded = jnp.pad(padded, (0, HALO), constant_values=1000)
+    window = lax.dynamic_slice_in_dim(padded, first_pos, tokens + 2 * HALO, 0)
+    own = window[HALO : HALO + tokens].reshape(steps, 1, BLOCK)
+    lows = jnp.sum(window[None, :] < own[:, 0, :1], axis=1, dtype=jnp.int32) // BLOCK
+    ends = jnp.sum(window[None, :] <= own[:, 0, BLOCK - 1 :], axis=1, dtype=jnp.int32)
     highs = (ends + BLOCK - 1) // BLOCK
-    base = (first_pos // BLOCK).astype(jnp.int32).reshape(1)
-    segment_wide = jnp.broadcast_to(segment_row[:, None], (length, BLOCK))
-    return lows, highs, base, own, segment_wide, bias_tiles(rel_bias)
-
-HEAD_DIM = 64
-FF = 3584
-epsilon = 1e-06
-gate_scale = -30.0
-gate_offset = -3.5
+    segment_wide = jnp.broadcast_to(window[:, None], (window.shape[0], BLOCK))
+    return lows, highs, own, segment_wide, bias_tiles(rel_bias)
+
 
 def rms_forward(stream, gain_row):
     inverse = lax.rsqrt(jnp.mean(stream * stream, axis=1, keepdims=True) + epsilon)
@@ -426,20 +434,333 @@
     )
 
 
+def shift(value, axis, amount):
+    count = lax.axis_size(axis)
+    return lax.ppermute(value, axis, [(i, (i + amount) % count) for i in range(count)])
+
+
+def slide(value, amount):
+    count = lax.axis_size("z")
+    pairs = [(i, i + amount) for i in range(count) if 0 <= i + amount < count]
+    return lax.ppermute(value, "z", pairs)
+
+
+def halo_pieces(tokens):
+    pieces = []
+    distance, covered = 1, 0
+    while covered < HALO:
+        span = min(tokens, HALO - covered)
+        needed = min(span, -(-(REACH - covered) // 16) * 16)
+        pieces.append((distance, span, needed))
+        distance, covered = distance + 1, covered + span
+    return pieces
+
+
+def with_neighbours(own):
+    tokens = own.shape[0]
+    before, after = [], []
+    for distance, span, needed in halo_pieces(tokens):
+        if distance < lax.axis_size("z"):
+            left = slide(own[tokens - needed :], distance)
+            right = slide(own[:needed], -distance)
+            before.append(jnp.pad(left, ((span - needed, 0), (0, 0))))
+            after.append(jnp.pad(right, ((0, span - needed), (0, 0))))
+        else:
+            empty = jnp.zeros((span, own.shape[1]), own.dtype)
+            before.append(empty)
+            after.append(empty)
+    return jnp.concatenate(before[::-1] + [own] + after, axis=0)
+
+
+def from_neighbours(window, tokens):
+    total = window[HALO : HALO + tokens].astype(jnp.float32)
+    covered = 0
+    for distance, span, needed in halo_pieces(tokens):
+        if distance < lax.axis_size("z"):
+            left_end = HALO - covered
+            right_start = HALO + tokens + covered
+            back = slide(window[left_end - needed : left_end], -distance)
+            ahead = slide(window[right_start : right_start + needed], distance)
+            total = total + jnp.pad(
+                back.astype(jnp.float32), ((tokens - needed, 0), (0, 0))
+            )
+            total = total + jnp.pad(ahead.astype(jnp.float32), ((0, tokens - needed), (0, 0)))
+        covered += span
+    return total
+
+
+def sum_everywhere(value):
+    for axis in ("c", "x", "y", "z"):
+        count = lax.axis_size(axis)
+        bit = 1
+        while bit < count:
+            value = value + lax.ppermute(value, axis, [(i, i ^ bit) for i in range(count)])
+            bit *= 2
+    return value
+
+
+def pick(value, index, axis):
+    return lax.dynamic_index_in_dim(value, index, axis, keepdims=False)
+
+
+def stage_sends(value, axis_name, axis):
+    count, here = lax.axis_size(axis_name), lax.axis_index(axis_name)
+    return [pick(value, (here + k) % count, axis) for k in range(1, count)]
+
+
+def stage_moves(sends, axis_name):
+    return [shift(sent, axis_name, k + 1) for k, sent in enumerate(sends)]
+
+
+def grad_tiles_body(phase, attended, core_ref, *refs):
+    up_ref, hidden_ref, normed_ref, branch_ref = refs[:4]
+    outs = refs[-4:]
+    tile = source_tile(phase, pl.program_id(0), core_ref)
+
+    def put(*products):
+        turned = [(left[...].T, right) for left, right in products]
+        for out, start, end in zip(outs, CUTS[:-1], CUTS[1:]):
+            total = jnp.zeros((TILE, end - start), jnp.float32)
+            for left, right in turned:
+                total = total + jnp.dot(
+                    left, right[:, start:end], preferred_element_type=jnp.float32
+                )
+            out[:, : end - start] = total.astype(jnp.bfloat16)
+            if end - start < CHUNK:
+                out[:, end - start :] = jnp.zeros((TILE, CHUNK - end + start), jnp.bfloat16)
+
+    @pl.when(tile < ATTENTION_TILES)
+    def _():
+        if attended:
+            first_ref, second_ref, first_side_ref, second_side_ref = refs[4:8]
+            put((first_ref, first_side_ref), (second_ref, second_side_ref))
+        else:
+            put()
+
+    @pl.when((tile >= ATTENTION_TILES) & (tile < ATTENTION_TILES + 2 * FF // TILE))
+    def _():
+        put((up_ref, normed_ref))
+
+    @pl.when(tile >= ATTENTION_TILES + 2 * FF // TILE)
+    def _():
+        put((hidden_ref, branch_ref))
+
+
+def source_tile(phase, step, core_ref):
+    core = core_ref[0] if phase else 1 - core_ref[0]
+    unit = core_ref[1]
+    return (step // unit) * 2 * unit + core * unit + step % unit
+
+
+def grad_tiles(phase, up_grads, hidden, normed_two, branch, attention):
+    tokens, width = normed_two.shape
+    rows = 4 * INNER + 3 * FF
+    steps = rows // TILE // 2
+    unit = steps // (lax.axis_size("y") * lax.axis_size("x"))
+    core = jnp.stack([lax.axis_index("c").astype(jnp.int32), jnp.int32(unit)])
+    up_tiles = 2 * FF // TILE
+
+    def up_map(step, core_ref):
+        tile = source_tile(phase, step, core_ref)
+        return 0, jnp.clip(tile - ATTENTION_TILES, 0, up_tiles - 1)
+
+    def hidden_map(step, core_ref):
+        tile = source_tile(phase, step, core_ref)
+        return 0, jnp.clip(tile - ATTENTION_TILES - up_tiles, 0, FF // TILE - 1)
+
+    def attention_map(step, core_ref):
+        return 0, jnp.minimum(source_tile(phase, step, core_ref), ATTENTION_TILES - 1)
+
+    side = pl.BlockSpec((tokens, width), lambda *_: (0, 0), pipeline_mode=pl.Buffered(1))
+    column = (tokens, TILE)
+    operands = [up_grads, hidden, normed_two, branch]
+    in_specs = [pl.BlockSpec(column, up_map), pl.BlockSpec(column, hidden_map), side, side]
+    if attention is not None:
+        operands += attention
+        in_specs += [
+            pl.BlockSpec(column, attention_map),
+            pl.BlockSpec(column, attention_map),
+            side,
+            side,
+        ]
+    results = pl.pallas_call(
+        functools.partial(grad_tiles_body, phase, attention is not None),
+        grid_spec=pltpu.PrefetchScalarGridSpec(
+            num_scalar_prefetch=1,
+            grid=(steps,),
+            in_specs=in_specs,
+            out_specs=[pl.BlockSpec((TILE, CHUNK), lambda i, *_: (i, 0))] * 4,
+        ),
+        out_shape=[jax.ShapeDtypeStruct((rows // 2, CHUNK), jnp.bfloat16)] * 4,
+        compiler_params=pltpu.CompilerParams(vmem_limit_bytes=40 << 20),
+        cost_estimate=pl.CostEstimate(
+            flops=tokens * rows * width,
+            bytes_accessed=2 * rows * width,
+            transcendentals=0,
+        ),
+        name="grad_tiles",
+    )(core, *operands)
+    return list(results)
+
+
+def split_body(place_ref, kept_ref, moved_ref, left_ref, left_send_ref, right_ref, right_send_ref):
+    i, j = pl.program_id(0), pl.program_id(1)
+    both = kept_ref[0, 0].astype(jnp.float32) + moved_ref[0, 0].astype(jnp.float32)
+    both = both.astype(jnp.bfloat16)
+    left, right = both[:, 0], both[:, 1]
+
+    @pl.when(i < pl.num_programs(0) - 1)
+    def _():
+        left_send_ref[0, 0] = left
+
+    @pl.when(i == pl.num_programs(0) - 1)
+    def _():
+        left_ref[0] = left
+
+    @pl.when(j < pl.num_programs(1) - 1)
+    def _():
+        right_send_ref[0, 0] = right
+
+    @pl.when(j == pl.num_programs(1) - 1)
+    def _():
+        right_ref[0] = right
+
+
+def split_sums(kept, moved):
+    size_y, size_x, size_z = (lax.axis_size(axis) for axis in ("y", "x", "z"))
+    chunk = kept.shape[-1]
+    shape = (size_y, size_x, size_z, 2, kept.size // (2 * size_y * size_x * size_z * chunk), chunk)
+    piece = shape[2:3] + shape[4:]
+    place = jnp.stack([lax.axis_index("y"), lax.axis_index("x")]).astype(jnp.int32)
+    zeros = (0, 0, 0)
+
+    def row_of(i, place_ref):
+        return (place_ref[0] + 1 + i) % size_y
+
+    def column_of(j, place_ref):
+        return (place_ref[1] + 1 + j) % size_x
+
+    def in_map(i, j, place_ref):
+        return (row_of(i, place_ref), column_of(j, place_ref), 0) + zeros
+
+    def left_map(i, j, place_ref):
+        return (jnp.where(i == size_y - 1, column_of(j, place_ref), column_of(0, place_ref)),) + zeros
+
+    def left_send_map(i, j, place_ref):
+        column = jnp.where(i < size_y - 1, column_of(j, place_ref), place_ref[1])
+        return (jnp.minimum(i, size_y - 2), column) + zeros
+
+    def right_map(i, j, place_ref):
+        return (row_of(i, place_ref),) + zeros
+
+    def right_send_map(i, j, place_ref):
+        return (jnp.minimum(j, size_x - 2), row_of(i, place_ref)) + zeros
+
+    block = pl.BlockSpec((1, 1) + shape[2:], in_map)
+    left, left_sends, right, right_sends = pl.pallas_call(
+        split_body,
+        grid_spec=pltpu.PrefetchScalarGridSpec(
+            num_scalar_prefetch=1,
+            grid=(size_y, size_x),
+            in_specs=[block, block],
+            out_specs=[
+                pl.BlockSpec((1,) + piece, left_map),
+                pl.BlockSpec((1, 1) + piece, left_send_map),
+                pl.BlockSpec((1,) + piece, right_map),
+                pl.BlockSpec((1, 1) + piece, right_send_map),
+            ],
+        ),
+        out_shape=[
+            jax.ShapeDtypeStruct((size_x,) + piece, jnp.bfloat16),
+            jax.ShapeDtypeStruct((size_y - 1, size_x) + piece, jnp.bfloat16),
+            jax.ShapeDtypeStruct((size_y,) + piece, jnp.bfloat16),
+            jax.ShapeDtypeStruct((size_x - 1, size_y) + piece, jnp.bfloat16),
+        ],
+        compiler_params=pltpu.CompilerParams(vmem_limit_bytes=32 << 20),
+        cost_estimate=pl.CostEstimate(
+            flops=kept.size, bytes_accessed=6 * kept.size, transcendentals=0
+        ),
+        name="split_sums",
+    )(place, kept.reshape(shape), moved.reshape(shape))
+    return (
+        left,
+        [left_sends[k] for k in range(size_y - 1)],
+        right,
+        [right_sends[k] for k in range(size_x - 1)],
+    )
+
+
+def tied(first, second):
+    return lax.optimization_barrier((first, second))
+
+
+class Scatter:
+    def __init__(self):
+        self.waiting, self.flying, self.results = [], [], {}
+
+    def push(self, name, kept, moved):
+        self.waiting.append((name, kept, moved))
+
+    def busy(self):
+        return bool(self.waiting or self.flying)
+
+    def step(self, values, enter=1):
+        flying = [item[2:] for item in self.flying]
+        entering, self.waiting = self.waiting[:enter], self.waiting[enter:]
+        flying, values = tied(flying, values)
+        moves = []
+        for (name, stage, *_), (left, left_moved, right, right_moved) in zip(self.flying, flying):
+            if stage == 1:
+                left = total_of(left, left_moved)
+                right = total_of(right, right_moved)
+                left_sends, right_sends = stage_sends(left, "x", 0), stage_sends(right, "y", 0)
+                left = pick(left, lax.axis_index("x"), 0)
+                right = pick(right, lax.axis_index("y"), 0)
+                moves.append((name, 2, left, left_sends, right, right_sends))
+            elif stage == 2:
+                left = total_of(left, left_moved)
+                right = total_of(right, right_moved)
+                sends = [
+                    jnp.concatenate(pair, axis=0)
+                    for pair in zip(stage_sends(left, "z", 0), stage_sends(right, "z", 0))
+                ]
+                here = lax.axis_index("z")
+                own = jnp.concatenate([pick(left, here, 0), pick(right, here, 0)], axis=0)
+                moves.append((name, 3, own, sends, own[:0], []))
+            else:
+                total = left.astype(jnp.float32)
+                for part in left_moved:
+                    total = total + part.astype(jnp.float32)
+                self.results[name] = total
+        for name, kept, moved in entering:
+            left, left_sends, right, right_sends = split_sums(kept, moved)
+            moves.append((name, 1, left, left_sends, right, right_sends))
+        arrays, values = tied([item[2:] for item in moves], values)
+        self.flying = []
+        for (name, stage, *_), (left, left_sends, right, right_sends) in zip(moves, arrays):
+            first, second = {1: ("y", "x"), 2: ("x", "y"), 3: ("z", "z")}[stage]
+            left_moved = stage_moves(left_sends, first)
+            right_moved = stage_moves(right_sends, second)
+            self.flying.append((name, stage, left, left_moved, right, right_moved))
+        return values
+
+
+def total_of(value, moved):
+    total = value.astype(jnp.float32)
+    for part in moved:
+        total = total + part.astype(jnp.float32)
+    return total.astype(jnp.bfloat16)
+
+
 def fetch_rows(local_rows):
-    return lax.all_gather(local_rows, ("dp", "seq"), axis=0, tiled=True)
-
-
-def reduce_rows(grad_rows):
-    summed = lax.psum_scatter(grad_rows, ("dp", "seq"), scatter_dimension=0, tiled=True)
-    return summed.astype(jnp.float32)
+    return lax.all_gather(local_rows, DEVICES, axis=0, tiled=True)
 
 
 def share_keys(projected, gate_low):
     parts = [projected[:, INNER:]]
     if gate_low is not None:
         parts.append(jnp.broadcast_to(gate_low[:, None], (gate_low.shape[0], BLOCK)))
-    return lax.all_gather(jnp.concatenate(parts, axis=1), "seq", axis=0, tiled=True)
+    return with_neighbours(jnp.concatenate(parts, axis=1))
 
 
 def layer_forward(stream, gathered, gain_one, gain_two, gate_low, context):
@@ -475,7 +796,9 @@
     return (result, kept)
 
 
-def layer_backward(grad_out, kept, gathered, gain_one, gain_two, context):
+def layer_backward(
+    grad_out, kept, gathered, gain_one, gain_two, context, waiting, scatter, name, before_tiles
+):
     (
         stream,
         inverse_one,
@@ -493,45 +816,99 @@
     ) = kept
     w_down = gathered[4 * INNER + 2 * FF :]
     branch_low = grad_out.astype(jnp.bfloat16)
-    grad_down = outer_sum(hidden, branch_low).astype(jnp.bfloat16)
     grad_hidden = times_rows(branch_low, w_down)
     activated, gelu_pullback = jax.vjp(gelu_tanh, up_gelu)
     grad_gelu = gelu_pullback(grad_hidden * up_linear)[0]
     grad_ffn_low = jnp.concatenate([grad_gelu, grad_hidden * activated], axis=1).astype(
         jnp.bfloat16
     )
-    grad_ffn = outer_sum(grad_ffn_low, normed_two_low).astype(jnp.bfloat16)
+    if before_tiles:
+        grad_ffn_low, branch_low = scatter.step((grad_ffn_low, branch_low))
+    sent = grad_tiles(0, grad_ffn_low, hidden, normed_two_low, branch_low, waiting)
+    moved = [shift(part, "c", 1) for part in sent]
+    grad_ffn_low, branch_low, sent = lax.optimization_barrier((grad_ffn_low, branch_low, sent))
+    own = grad_tiles(1, grad_ffn_low, hidden, normed_two_low, branch_low, waiting)
+    for k in range(4):
+        scatter.push((name, k), own[k], moved[k])
+    grad_ffn_low, grad_out = scatter.step((grad_ffn_low, grad_out))
     grad_normed_two = times_plain(grad_ffn_low, gathered[4 * INNER : 4 * INNER + 2 * FF])
     grad_middle, grad_gain_two = rms_backward(middle, inverse_two, gain_two, grad_normed_two)
     grad_middle = grad_out + grad_middle
     middle_low = grad_middle.astype(jnp.bfloat16)
-    grad_attn_out = outer_sum(attended, middle_low).astype(jnp.bfloat16)
     grad_mixed = times_rows(middle_low, gathered[3 * INNER : 4 * INNER]).astype(jnp.bfloat16)
+    grad_mixed, grad_middle, middle_low = scatter.step((grad_mixed, grad_middle, middle_low))
     grad_query, grad_shared, grad_table = attend_backward(
         queries, grad_mixed, shared, log_total, context
     )
-    grad_own = lax.psum_scatter(grad_shared, "seq", scatter_dimension=0, tiled=True)
-    grad_input_low = jnp.concatenate([grad_query, grad_own[:, : 2 * INNER]], axis=1)
-    grad_gate = grad_own[:, 2 * INNER :].astype(jnp.float32)
-    grad_input_rows = outer_sum(grad_input_low, normed_low).astype(jnp.bfloat16)
+    grad_query, grad_shared, grad_table = scatter.step((grad_query, grad_shared, grad_table))
+    grad_own = from_neighbours(grad_shared, queries.shape[0])
+    grad_gate = grad_own[:, 2 * INNER :]
+    grad_input_low = jnp.concatenate(
+        [grad_query, grad_own[:, : 2 * INNER].astype(jnp.bfloat16)], axis=1
+    )
     grad_normed = times_plain(grad_input_low, gathered[: 3 * INNER])
     grad_stream, grad_gain_one = rms_backward(stream, inverse_one, gain_one, grad_normed)
-    grad_rows = jnp.concatenate([grad_input_rows, grad_attn_out, grad_ffn, grad_down], axis=0)
+    grad_stream = grad_middle + grad_stream
+    attention = [
+        jnp.pad(grad_input_low, ((0, 0), (0, INNER))),
+        jnp.pad(attended, ((0, 0), (3 * INNER, 0))),
+        normed_low,
+        middle_low,
+    ]
+    grad_stream, attention = scatter.step((grad_stream, attention))
     return (
-        grad_middle + grad_stream,
-        grad_rows,
+        grad_stream,
         grad_table,
         grad_gate,
         grad_gain_one,
         grad_gain_two,
-    )
+        attention,
+    )
+
+
+def push_last_attention(attention, scatter):
+    first, second, first_side, second_side = attention
+    rows = outer_sum(first, first_side) + outer_sum(second, second_side)
+    size_y, size_x, size_z = (lax.axis_size(axis) for axis in ("y", "x", "z"))
+    core = lax.axis_index("c")
+    width = rows.shape[1]
+    owners, part = owner_parts()
+    rows = rows.astype(jnp.bfloat16).reshape(owners, size_z, size_y, size_x, 2, -1, width)
+    rows = rows.transpose(2, 3, 4, 1, 0, 5, 6).reshape(size_y, size_x, 2, size_z, part, width)
+    kept, sent = pick(rows, core, 2), pick(rows, 1 - core, 2)
+    scatter.push("late", kept, shift(sent, "c", 1))
+
+
+def owner_parts():
+    size_y, size_x, size_z = (lax.axis_size(axis) for axis in ("y", "x", "z"))
+    block = (4 * INNER + 3 * FF) // (size_y * size_x * 2 * size_z)
+    owners = 4 * INNER // (block * size_z)
+    return owners, block * owners // (size_y * size_x * 2)
+
+
+def bring_to_owners(mine):
+    size_y, size_x = lax.axis_size("y"), lax.axis_size("x")
+    owners, part = owner_parts()
+    width = mine.shape[-1]
+    mine = mine.astype(jnp.bfloat16)[None]
+    for axis in ("c", "x", "y"):
+        count, here = lax.axis_size(axis), lax.axis_index(axis)
+        gathered = jnp.zeros((count,) + mine.shape, mine.dtype)
+        gathered = lax.dynamic_update_index_in_dim(gathered, mine, here, 0)
+        for k in range(1, count):
+            gathered = lax.dynamic_update_index_in_dim(
+                gathered, shift(mine, axis, k), (here - k) % count, 0
+            )
+        mine = gathered.reshape((-1,) + mine.shape[1:])
+    shape = (size_y, size_x, 2, owners, part // owners, width)
+    return mine.reshape(shape).transpose(3, 0, 1, 2, 4, 5).reshape(owners, -1, width)
 
 
 def per_device(
     inputs, layer3_rows, layer4_rows, norm_gains, gate_weight, rel_bias, segment_ids, cotangent
 ):
     seqs_here, tokens_here, width = inputs.shape
-    first_pos = lax.axis_index("seq") * tokens_here
+    first_pos = lax.axis_index("z") * tokens_here
     context = attention_context(segment_ids[0], first_pos, tokens_here, rel_bias)
     stream = inputs.reshape(tokens_here, width)
     gathered_three = fetch_rows(layer3_rows)
@@ -548,66 +925,81 @@
     after_four, kept_four = layer_forward(
         after_three, gathered_four, norm_gains[2], norm_gains[3], gate_low, context
     )
-    grad_three_out, rows_four, table_four, grad_gate, gain_four_one, gain_four_two = layer_backward(
-        cotangent.reshape(tokens_here, width),
-        kept_four,
-        gathered_four,
-        norm_gains[2],
-        norm_gains[3],
-        context,
-    )
-    local_four = reduce_rows(rows_four)
+    scatter = Scatter()
+    grad_three_out, table_four, grad_gate, gain_four_one, gain_four_two, attention_four = (
+        layer_backward(
+            cotangent.reshape(tokens_here, width),
+            kept_four,
+            gathered_four,
+            norm_gains[2],
+            norm_gains[3],
+            context,
+            None,
+            scatter,
+            "four",
+            False,
+        )
+    )
     grad_logit = grad_gate[:, 0] * gate_scale * sigmoid_value * (1.0 - sigmoid_value)
     grad_gate_weight = jnp.sum(grad_logit[:, None] * gate_normed, axis=0)
     gate_stream = stream_backward(after_three, gate_inverse, grad_logit[:, None] * gate_weight)
     grad_three_out = grad_three_out + gate_stream
-    grad_input, rows_three, table_three, unused, gain_three_one, gain_three_two = layer_backward(
-        grad_three_out,
-        kept_three,
-        gathered_three,
-        norm_gains[0],
-        norm_gains[1],
-        context,
-    )
-    local_three = reduce_rows(rows_three)
-    gains_grad = jnp.stack([gain_three_one, gain_three_two, gain_four_one, gain_four_two])
-    summed = lax.psum((gains_grad, grad_gate_weight, table_three + table_four), ("dp", "seq"))
+    grad_input, table_three, unused, gain_three_one, gain_three_two, attention_three = (
+        layer_backward(
+            grad_three_out,
+            kept_three,
+            gathered_three,
+            norm_gains[0],
+            norm_gains[1],
+            context,
+            attention_four,
+            scatter,
+            "three",
+            True,
+        )
+    )
+    push_last_attention(attention_three, scatter)
+    while scatter.busy():
+        grad_input = scatter.step(grad_input)
+    owner = (
+        (lax.axis_index("y") * lax.axis_size("x") + lax.axis_index("x")) * lax.axis_size("c")
+    ) + lax.axis_index("c")
+    late = bring_to_owners(scatter.results["late"]).astype(jnp.float32)
+    owners = late.shape[0]
+    mine = pick(late, jnp.minimum(owner, owners - 1), 0)
+    local_four, local_three = (
+        jnp.concatenate([scatter.results[name, k] for k in range(4)], axis=1)[:, :width]
+        for name in ("four", "three")
+    )
+    local_four = jnp.where(owner < owners, local_three, local_four)
+    local_three = jnp.where(owner < owners, mine, local_three)
+    table = jnp.pad((table_three + table_four).reshape(1, -1), ((0, 0), (0, width - 6 * BUCKETS)))
+    small = jnp.stack(
+        [gain_three_one, gain_three_two, gain_four_one, gain_four_two, grad_gate_weight, table[0]]
+    )
+    summed = sum_everywhere(small)
     return (
         after_four.reshape(inputs.shape),
         gate_mask.reshape(seqs_here, tokens_here),
         grad_input.reshape(inputs.shape),
         local_three,
         local_four,
-        summed[0],
-        summed[1],
-        summed[2],
+        summed[:4],
+        summed[4],
+        summed[5, : 6 * BUCKETS].reshape(BUCKETS, HEADS),
     )
 
 
 def solution(mesh):
-    placed = (
-        P("dp", "seq", None),
-        P(("dp", "seq"), None),
-        P(("dp", "seq"), None),
-        P(),
-        P(),
-        P(),
-        P("dp", None),
-        P("dp", "seq", None),
-    )
+    outer, inner = mesh.devices.shape
+    fine = Mesh(mesh.devices.reshape(outer // 4, 2, 2, inner), DEVICES)
+    batch = ("y", "x", "c")
+    tokens = P(batch, "z", None)
+    rows = P(DEVICES, None)
     return jax.shard_map(
         per_device,
-        mesh=mesh,
-        in_specs=placed,
-        out_specs=(
-            P("dp", "seq", None),
-            P("dp", "seq"),
-            P("dp", "seq", None),
-            P(("dp", "seq"), None),
-            P(("dp", "seq"), None),
-            P(),
-            P(),
-            P(),
-        ),
+        mesh=fine,
+        in_specs=(tokens, rows, rows, P(), P(), P(), P(batch, None), tokens),
+        out_specs=(tokens, P(batch, "z"), tokens, rows, rows, P(), P(), P()),
         check_vma=False,
     )

time: 1710 us -> 1450 us (0.85)
  waiting for transfers between devices: 1080 us -> 564 us
  Pallas kernels: 71.9 us -> 257 us
  starting transfers between devices: 0.62 us -> 174 us
  matrix products: 255 us -> 183 us
  blocking collectives: 62.2 us -> 0 us
  other arithmetic: 86.2 us -> 135 us
    unnamed x10 -> x2, waiting for transfers between devices: 513 us -> 1.38 us
    ppermute x0 -> x96, waiting for transfers between devices: none -> 244 us  [the longest x16 114 us: slide(): return lax.ppermute(value, 'z', pairs)]
    ppermute x0 -> x96, starting transfers between devices: none -> 174 us  [the longest x75 107 us: shift(): lax.ppermute(value, axis, [(i, (i + amount) % count) for i in range(count)])]
    all_gather x4 -> x2, waiting for transfers between devices: 492 us -> 318 us  [fetch_rows(): return lax.all_gather(local_rows, DEVICES, axis=0, tiled=True)]
    pallas_call x0 -> x13, Pallas kernels: none -> 151 us  [the longest x4 103 us: grad_tiles(): pl.pallas_call(functools.partial(grad_tiles_body, phase, attention is not...]
    reduce_scatter x2 -> x0, waiting for transfers between devices: 78.2 us -> none  [layer_backward(): lax.psum_scatter(grad_shared, 'seq', scatter_dimension=0, tiled=True)]
    psum x1 -> x0, blocking collectives: 62.2 us -> none  [per_device(): lax.psum((gains_grad, grad_gate_weight, table_three + table_four), ('dp',...]
    dot_general x8 -> x2, matrix products: 74.6 us -> 14.2 us  [outer_sum(): lax.dot_general(left_side, right_side, (((0,), (0,)), ((), ())), preferre...]
  transfers between devices with their start and end apart: 8 -> 98, of which waited for: 7 -> 28; matrix products, arithmetic and copies ran while one was open for 18% -> 22% of each run, Pallas kernels for 1% -> 13%
where the time goes in v2:
time: 1450 us
  waiting for transfers between devices  564 us (39%)
  Pallas kernels  257 us (18%)
  matrix products  183 us (13%)
  starting transfers between devices  174 us (12%)
  other arithmetic  135 us (9%)
  local copies, waits for them, and re-layouts  122 us (8%)
  between operations  17.1 us (1%)
    all_gather x2, waiting for transfers between devices, fetch_rows(): return lax.all_gather(local_rows, DEVICES, axis=0, tiled=True)  318 us
    ppermute x16, waiting for transfers between devices, slide(): return lax.ppermute(value, 'z', pairs)  114 us
    ppermute x75, starting transfers between devices, shift(): lax.ppermute(value, axis, [(i, (i + amount) % count) for i in range(count)])  107 us
    ppermute x75, waiting for transfers between devices, shift(): lax.ppermute(value, axis, [(i, (i + amount) % count) for i in range(count)])  106 us
    pallas_call x4, Pallas kernels, grad_tiles(): pl.pallas_call(functools.partial(grad_tiles_body, phase, attention is not...  103 us
    dot_general x8, matrix products, times_rows(): lax.dot_general(left_side, weight, (((1,), (1,)), ((), ())), preferred_el...  88.7 us
    dot_general x8, matrix products, times_plain(): return jnp.dot(left_side, weight, preferred_element_type=jnp.float32)  79.9 us
    ppermute x16, starting transfers between devices, slide(): return lax.ppermute(value, 'z', pairs)  64.4 us
  transfers between devices with their start and end apart: 98, of which 28 were waited for; matrix products, arithmetic and copies ran while one was open for 22% of the time, Pallas kernels for 13%

profile of v2, /device:TPU:24, one launch (start us, length us, event | category | flops | bytes accessed | tf_op | source)
XLA Modules:
  0.0 1451.9 jit_solution(2735213137641113293)
XLA Ops:
  14.9 210.4 %all-gather.3.cloned.1.call-done = bf16[12288,1472]{0,1:T(8,128)(2,1)} async-done(((bf16[384,1472]{0,1:T(8,128)(2,1)}), bf16[12288,1472]{0,1:T(8,128)(2,1)}) %all-gather.3.cloned.1.call-update) | async-done | bytes 36175888 | tf_op jit(solution)/shard_map/all_gather | solution.py:756
  225.3 4.6 convolution_convert_fusion.1
  234.6 5.5 collective-permute-start.2
  240.9 4.7 bias_tiles.1.refs_4_.refs_5_
  245.7 5.1 collective-permute-start.3
  250.9 45.9 %collective-permute-done = bf16[288,768]{1,0:T(8,128)(2,1)S(1)} collective-permute-done((bf16[288,768]{1,0:T(8,128)(2,1)S(1)}, bf16[288,768]{1,0:T(8,128)(2,1)S(1)}, u32[]{:S(2)}, u32[]{:S(2)}) %collective-permute-start) | collective-permute-done | bytes 442400 | tf_op jit(solution)/shard_map/ppermute | solution.py:445
  299.9 19.2 %attend_forward.2 = (bf16[512,384]{1,0:T(8,128)(2,1)S(1)}, f32[4,8,256]{2,1,0:T(8,128)S(1)}) custom-call(s32[4]{0:T(128)S(1)} %get-tuple-element.916.low_ref, s32[4]{0:T(128)S(1)} %get-tuple-element.915.high_ref, bf16[512,384]{1,0:T(8,128)(2,1)S(1)} %slice.208.refs_0_, bf16[2304,768]{1,0:T(8,128)(2,1)S(1)} %pad_dynamic-update-slice_fusion.2.refs_1_.refs_2_, ...), custom_call_target="tpu_custom_call" | custom-call | flops 1811939328 | bytes 8388608 | tf_op jit(solution)/shard_map/attend_forward/pallas_call | solution.py:195
  322.7 19.5 %fusion.6 = f32[512,7168]{1,0:T(8,128)} fusion(bf16[512,1472]{1,0:T(8,128)(2,1)S(1)} %multiply_convert_fusion.6.refs_2_, bf16[12288,1472]{0,1:T(8,128)(2,1)} %all-gather.3.cloned.1.call-done), kind=kOutput, calls=%fused_computation.6 | convolution fusion | flops 10804527104 | bytes 37289984 | tf_op jit(solution)/shard_map/dot_general | solution.py:422
  342.1 6.5 multiply_convert_fusion.3.refs_1_
  348.7 10.1 multiply_reduce_fusion.9
  362.7 108.1 %all-gather.5.cloned.1.call-done = bf16[12288,1472]{0,1:T(8,128)(2,1)} async-done(((bf16[384,1472]{0,1:T(8,128)(2,1)}), bf16[12288,1472]{0,1:T(8,128)(2,1)}) %all-gather.5.cloned.1.call-update) | async-done | bytes 36175888 | tf_op jit(solution)/shard_map/all_gather | solution.py:756
  470.7 4.6 convolution_convert_fusion
  493.0 5.7 collective-permute-start.7
  498.7 26.3 %collective-permute-done.4 = bf16[288,896]{1,0:T(8,128)(2,1)S(1)} collective-permute-done((bf16[288,896]{1,0:T(8,128)(2,1)S(1)}, bf16[288,896]{1,0:T(8,128)(2,1)S(1)}, u32[]{:S(2)}, u32[]{:S(2)}) %collective-permute-start.4) | collective-permute-done | bytes 516128 | tf_op jit(solution)/shard_map/ppermute | solution.py:445
  526.8 19.2 %attend_forward.3 = (bf16[512,384]{1,0:T(8,128)(2,1)S(1)}, f32[4,8,256]{2,1,0:T(8,128)S(1)}) custom-call(s32[4]{0:T(128)S(1)} %get-tuple-element.916.low_ref, s32[4]{0:T(128)S(1)} %get-tuple-element.915.high_ref, bf16[512,384]{1,0:T(8,128)(2,1)S(1)} %slice.218.refs_0_, bf16[2304,896]{1,0:T(8,128)(2,1)S(1)} %pad_dynamic-update-slice_fusion.refs_1_.refs_2_, ...), custom_call_target="tpu_custom_call" | custom-call | flops 1811939328 | bytes 8388608 | tf_op jit(solution)/shard_map/attend_forward/pallas_call | solution.py:195
  550.5 19.2 %fusion.2 = f32[512,7168]{1,0:T(8,128)} fusion(bf16[512,1472]{1,0:T(8,128)(2,1)S(1)} %multiply_convert_fusion.4.refs_2_, bf16[12288,1472]{0,1:T(8,128)(2,1)} %all-gather.5.cloned.1.call-done), kind=kOutput, calls=%fused_computation.2 | convolution fusion | flops 10804527104 | bytes 37289984 | tf_op jit(solution)/shard_map/dot_general | solution.py:422
  569.8 17.8 %fusion.32 = (bf16[512,3584]{1,0:T(8,128)(2,1)}, bf16[512,3584]{1,0:T(8,128)(2,1)}, bf16[512,3584]{1,0:T(8,128)(2,1)}) fusion(f32[512,7168]{1,0:T(8,128)} %fusion.2, bf16[512,1472]{1,0:T(8,128)(2,1)S(1)} %bitcast_convert_fusion.refs_3_, bf16[12288,1472]{0,1:T(8,128)(2,1)} %all-gather.5.cloned.1.call-done), kind=kOutput, calls=%fused_computation.37 | convolution fusion | flops 5449973760 | bytes 37748736 | tf_op jit(solution)/shard_map/dot_general | solution.py:422
  587.6 7.0 pad_maximum_fusion.refs_0_
  598.1 25.4 %grad_tiles.4 = (bf16[6144,384]{1,0:T(8,128)(2,1)}, bf16[6144,384]{1,0:T(8,128)(2,1)}, bf16[6144,384]{1,0:T(8,128)(2,1)}, bf16[6144,384]{1,0:T(8,128)(2,1)}) custom-call(s32[2]{0:T(128)S(1)} %pad_add_fusion.1.core_ref, bf16[512,7168]{1,0:T(8,128)(2,1)} %pad_maximum_fusion.refs_0_, bf16[512,3584]{1,0:T(8,128)(2,1)S(1)} %copy-done.74, ...), custom_call_target="tpu_custom_call" | custom-call | flops 9261023232 | bytes 36175872 | tf_op jit(solution)/shard_map/grad_tiles/pallas_call | solution.py:586
  630.0 22.6 %grad_tiles.5 = (bf16[6144,384]{1,0:T(8,128)(2,1)S(1)}, bf16[6144,384]{1,0:T(8,128)(2,1)}, bf16[6144,384]{1,0:T(8,128)(2,1)}, bf16[6144,384]{1,0:T(8,128)(2,1)}) custom-call(s32[2]{0:T(128)S(1)} %copy-done.71, bf16[512,7168]{1,0:T(8,128)(2,1)} %pad_maximum_fusion.refs_0_, bf16[512,3584]{1,0:T(8,128)(2,1)S(1)} %copy-done.75, ...), custom_call_target="tpu_custom_call" | custom-call | flops 9261023232 | bytes 36175872 | tf_op jit(solution)/shard_map/grad_tiles/pallas_call | solution.py:586
  652.7 6.5 split_sums.9
  661.3 6.2 split_sums.10
  669.6 20.7 %multiply_reduce_fusion.1 = (f32[1472]{0:T(1024)}, f32[512]{0:T(512)}, f32[512,1472]{1,0:T(8,128)}) fusion(f32[512,1472]{1,0:T(8,128)} %copy-done.83, f32[512]{0:T(512)} %copy-done.192, f32[1472]{0:T(1024)} %get-tuple-element.748, bf16[512,7168]{1,0:T(8,128)(2,1)} %pad_maximum_fusion.refs_0_, bf16[12288,1472]{0,1:T(8,128)(2,1)} %all-gather.5.cloned.1.call-done), kind=kOutput, calls=%fused_computation.71 | convolution fusion | flops 10809047040 | bytes 34621184 | tf_op jit(solution)/shard_map/dot_general | solution.py:428
  691.0 6.3 fusion.77
  712.9 4.9 split_sums.11
  721.9 32.4 %attend_backward.2 = (bf16[512,384]{1,0:T(8,128)(2,1)S(1)}, bf16[2304,896]{1,0:T(8,128)(2,1)}, f32[3,32,256]{2,1,0:T(8,128)S(1)}) custom-call(s32[4]{0:T(128)S(1)} %get-tuple-element.916.low_ref, s32[4]{0:T(128)S(1)} %get-tuple-element.915.high_ref, bf16[512,384]{1,0:T(8,128)(2,1)S(1)} %slice.218.refs_0_, bf16[512,384]{1,0:T(8,128)(2,1)S(1)} %copy-done.73, ...), custom_call_target="tpu_custom_call" | custom-call | flops 4529848320 | bytes 12582912 | tf_op jit(solution)/shard_map/attend_backward/pallas_call | solution.py:345
  770.5 18.4 %collective-permute-start.24 = (bf16[512,896]{1,0:T(8,128)(2,1)}, bf16[512,896]{1,0:T(8,128)(2,1)}, u32[]{:S(2)}, u32[]{:S(2)}) collective-permute-start(bf16[512,896]{1,0:T(8,128)(2,1)} %get-tuple-element.775), channel_id=1, source_target_pairs={{1,0},{2,1},{3,2},{5,4},{6,5},{7,6},{9,8},{10,9},{11,10},{13,12},{... | collective-permute-start | bytes 2752520 | tf_op jit(solution)/shard_map/ppermute | solution.py:445
  801.6 6.5 split_sums.12
  810.0 10.1 collective-permute-done.26
  820.1 14.9 %collective-permute-done.27 = bf16[288,896]{1,0:T(8,128)(2,1)} collective-permute-done((bf16[288,896]{1,0:T(8,128)(2,1)}, bf16[288,896]{1,0:T(8,128)(2,1)}, u32[]{:S(2)}, u32[]{:S(2)}) %collective-permute-start.27) | collective-permute-done | bytes 516128 | tf_op jit(solution)/shard_map/ppermute | solution.py:445
  840.1 5.8 multiply_reduce_fusion.2
  846.8 13.7 collective-permute-done.18
  862.1 8.1 collective-permute-done.19
  884.0 16.9 %fusion.24 = (bf16[512,3584]{1,0:T(8,128)(2,1)}, bf16[512,3584]{1,0:T(8,128)(2,1)}) fusion(f32[512,7168]{1,0:T(8,128)} %fusion.6, bf16[512,1472]{1,0:T(8,128)(2,1)S(1)} %get-tuple-element.495.refs_3_, bf16[12288,1472]{0,1:T(8,128)(2,1)} %all-gather.3.cloned.1.call-done), kind=kOutput, calls=%fused_computation.29 | convolution fusion | flops 5446303744 | bytes 34078720 | tf_op jit(solution)/shard_map/dot_general | solution.py:422
  903.7 7.0 pad_maximum_fusion.1.refs_0_
  926.7 25.6 %grad_tiles.6 = (bf16[6144,384]{1,0:T(8,128)(2,1)}, bf16[6144,384]{1,0:T(8,128)(2,1)}, bf16[6144,384]{1,0:T(8,128)(2,1)}, bf16[6144,384]{1,0:T(8,128)(2,1)}) custom-call(s32[2]{0:T(128)S(1)} %copy-done.72, bf16[512,7168]{1,0:T(8,128)(2,1)} %pad_maximum_fusion.1.refs_0_, bf16[512,3584]{1,0:T(8,128)(2,1)S(1)} %copy-done.8, bf16[512,1472]{1,0:T(8,128)(2,1)S(1)} %copy-done.18, ...), custom_call_target="tpu_custom_call" | custom-call | flops 9261023232 | bytes 36175872 | tf_op jit(solution)/shard_map/grad_tiles/pallas_call | solution.py:586
  953.2 5.5 collective-permute-start.36
  960.4 6.0 collective-permute-done.36
  966.4 13.2 collective-permute-start.38
  979.5 28.8 %grad_tiles.7 = (bf16[6144,384]{1,0:T(8,128)(2,1)}, bf16[6144,384]{1,0:T(8,128)(2,1)}, bf16[6144,384]{1,0:T(8,128)(2,1)}, bf16[6144,384]{1,0:T(8,128)(2,1)}) custom-call(s32[2]{0:T(128)S(1)} %copy-done.72, bf16[512,7168]{1,0:T(8,128)(2,1)} %pad_maximum_fusion.1.refs_0_, bf16[512,3584]{1,0:T(8,128)(2,1)S(1)} %copy-done.8, bf16[512,1472]{1,0:T(8,128)(2,1)S(1)} %copy-done.18, ...), custom_call_target="tpu_custom_call" | custom-call | flops 9261023232 | bytes 36175872 | tf_op jit(solution)/shard_map/grad_tiles/pallas_call | solution.py:586
  1020.6 20.6 %multiply_reduce_fusion.3 = (f32[1472]{0:T(1024)}, f32[512]{0:T(512)S(1)}, f32[512,1472]{1,0:T(8,128)}) fusion(f32[512,1472]{1,0:T(8,128)} %copy-done.85, f32[512]{0:T(512)S(1)} %copy-done.190, f32[1472]{0:T(1024)S(1)} %copy-done.169, bf16[512,7168]{1,0:T(8,128)(2,1)} %pad_maximum_fusion.1.refs_0_, bf16[12288,1472]{0,1:T(8,128)(2,1)} %all-gather.3.cloned.1.call-done), kind=kOutput, calls=%fused_computation.73 | convolution fusion | flops 10809047040 | bytes 34618880 | tf_op jit(solution)/shard_map/dot_general | solution.py:428
  1041.3 6.4 fusion.74
  1049.2 6.2 split_sums.14
  1059.0 10.7 collective-permute-done.43
  1080.1 4.9 split_sums.15
  1089.2 30.4 %attend_backward.3 = (bf16[512,384]{1,0:T(8,128)(2,1)S(1)}, bf16[2304,768]{1,0:T(8,128)(2,1)}, f32[3,32,256]{2,1,0:T(8,128)S(1)}) custom-call(s32[4]{0:T(128)S(1)} %get-tuple-element.916.low_ref, s32[4]{0:T(128)S(1)} %get-tuple-element.915.high_ref, bf16[512,384]{1,0:T(8,128)(2,1)S(1)} %copy-done.15, bf16[512,384]{1,0:T(8,128)(2,1)S(1)} %convolution_convert_fusion.2.refs_1_, ...), custom_call_target="tpu_custom_call" | custom-call | flops 4529848320 | bytes 12582912 | tf_op jit(solution)/shard_map/attend_backward/pallas_call | solution.py:345
  1133.2 6.1 collective-permute-start.60
  1141.5 4.8 collective-permute-start.62
  1150.7 15.6 %collective-permute-done.62 = bf16[288,768]{1,0:T(8,128)(2,1)} collective-permute-done((bf16[288,768]{1,0:T(8,128)(2,1)}, bf16[288,768]{1,0:T(8,128)(2,1)}, u32[]{:S(2)}, u32[]{:S(2)}) %collective-permute-start.62) | collective-permute-done | bytes 442400 | tf_op jit(solution)/shard_map/ppermute | solution.py:445
  1166.4 12.5 collective-permute-start.53
  1182.2 7.7 fusion.53
  1193.2 7.4 split_sums.16
  1200.5 12.6 collective-permute-start.58
  1218.4 24.7 %collective-permute-done.92 = f32[6,1472]{1,0:T(8,128)S(1)} collective-permute-done((f32[6,1472]{1,0:T(8,128)S(1)}, f32[6,1472]{1,0:T(8,128)S(1)}, u32[]{:S(2)}, u32[]{:S(2)}) %collective-permute-start.92) | collective-permute-done | bytes 35360 | tf_op jit(solution)/shard_map/ppermute | solution.py:497
  1262.8 6.0 fusion.83
  1273.0 8.3 fusion.16
  1281.3 6.6 copy.198
  1290.0 5.0 dynamic-slice_bitcast_fusion
  1319.7 9.9 fusion.39
  1349.2 11.7 collective-permute-done.78
  1376.9 14.0 collective-permute-done.81
  1401.0 8.6 collective-permute-done.86
  1414.2 6.1 collective-permute-done.89
  1429.4 6.5 collective-permute-done.90
  (821 shorter events, 336.6 us)
Async XLA Ops:
  7.2 218.1 %all-gather.3.cloned.1.call-start = ((), (), s32[]{:S(2)}) async-start(), calls=%async_computation | async-start | bytes 37306368 | tf_op jit(solution)/shard_map/all_gather | solution.py:756
  7.9 462.8 %all-gather.5.cloned.1.call-start = ((), (), s32[]{:S(2)}) async-start(), calls=%async_computation.1 | async-start | bytes 37306368 | tf_op jit(solution)/shard_map/all_gather | solution.py:756
  230.9 66.0 %collective-permute-start.1 = (bf16[512,768]{1,0:T(8,128)(2,1)}, bf16[512,768]{1,0:T(8,128)(2,1)}, u32[]{:S(2)}, u32[]{:S(2)}) collective-permute-start(bf16[512,768]{1,0:T(8,128)(2,1)} %slice.210), channel_id=1, source_target_pairs={{0,1},{1,2},{2,3},{4,5},{5,6},{6,7},{8,9},{9,10},{10,11},{12,13},{... | collective-permute-start | bytes 2359304 | tf_op jit(solution)/shard_map/ppermute | solution.py:445
  233.0 63.8 %collective-permute-start = (bf16[288,768]{1,0:T(8,128)(2,1)S(1)}, bf16[288,768]{1,0:T(8,128)(2,1)S(1)}, u32[]{:S(2)}, u32[]{:S(2)}) collective-permute-start(bf16[288,768]{1,0:T(8,128)(2,1)S(1)} %get-tuple-element.818), channel_id=1, source_target_pairs={{0,2},{1,3},{4,6},{5,7},{8,10},{9,11},{12,14},{13,15},{16,18},{17,... | collective-permute-start | bytes 1327112 | tf_op jit(solution)/shard_map/ppermute | solution.py:445
  234.6 63.7 %collective-permute-start.2 = (bf16[512,768]{1,0:T(8,128)(2,1)}, bf16[512,768]{1,0:T(8,128)(2,1)}, u32[]{:S(2)}, u32[]{:S(2)}) collective-permute-start(bf16[512,768]{1,0:T(8,128)(2,1)} %slice.210), channel_id=1, source_target_pairs={{1,0},{2,1},{3,2},{5,4},{6,5},{7,6},{9,8},{10,9},{11,10},{13,12},{... | collective-permute-start | bytes 2359304 | tf_op jit(solution)/shard_map/ppermute | solution.py:445
  245.7 53.7 %collective-permute-start.3 = (bf16[288,768]{1,0:T(8,128)(2,1)}, bf16[288,768]{1,0:T(8,128)(2,1)S(1)}, u32[]{:S(2)}, u32[]{:S(2)}) collective-permute-start(bf16[288,768]{1,0:T(8,128)(2,1)} %get-tuple-element.817), channel_id=1, source_target_pairs={{2,0},{3,1},{6,4},{7,5},{10,8},{11,9},{14,12},{15,13},{18,16},{19,... | collective-permute-start | bytes 1327112 | tf_op jit(solution)/shard_map/ppermute | solution.py:445
  477.3 47.8 %collective-permute-start.5 = (bf16[512,896]{1,0:T(8,128)(2,1)}, bf16[512,896]{1,0:T(8,128)(2,1)}, u32[]{:S(2)}, u32[]{:S(2)}) collective-permute-start(bf16[512,896]{1,0:T(8,128)(2,1)} %pad_maximum_fusion.8), channel_id=1, source_target_pairs={{0,1},{1,2},{2,3},{4,5},{5,6},{6,7},{8,9},{9,10},{10,11},{12,13},{... | collective-permute-start | bytes 2752520 | tf_op jit(solution)/shard_map/ppermute | solution.py:445
  482.3 44.2 %collective-permute-start.6 = (bf16[512,896]{1,0:T(8,128)(2,1)}, bf16[512,896]{1,0:T(8,128)(2,1)S(1)}, u32[]{:S(2)}, u32[]{:S(2)}) collective-permute-start(bf16[512,896]{1,0:T(8,128)(2,1)} %pad_maximum_fusion.8), channel_id=1, source_target_pairs={{1,0},{2,1},{3,2},{5,4},{6,5},{7,6},{9,8},{10,9},{11,10},{13,12},{... | collective-permute-start | bytes 2752520 | tf_op jit(solution)/shard_map/ppermute | solution.py:445
  488.2 36.8 %collective-permute-start.4 = (bf16[288,896]{1,0:T(8,128)(2,1)S(1)}, bf16[288,896]{1,0:T(8,128)(2,1)S(1)}, u32[]{:S(2)}, u32[]{:S(2)}) collective-permute-start(bf16[288,896]{1,0:T(8,128)(2,1)S(1)} %get-tuple-element.820), channel_id=1, source_target_pairs={{0,2},{1,3},{4,6},{5,7},{8,10},{9,11},{12,14},{13,15},{16,18},{17,... | collective-permute-start | bytes 1548296 | tf_op jit(solution)/shard_map/ppermute | solution.py:445
  493.0 33.7 %collective-permute-start.7 = (bf16[288,896]{1,0:T(8,128)(2,1)S(1)}, bf16[288,896]{1,0:T(8,128)(2,1)S(1)}, u32[]{:S(2)}, u32[]{:S(2)}) collective-permute-start(bf16[288,896]{1,0:T(8,128)(2,1)S(1)} %get-tuple-element.819), channel_id=1, source_target_pairs={{2,0},{3,1},{6,4},{7,5},{10,8},{11,9},{14,12},{15,13},{18,16},{19,... | collective-permute-start | bytes 1548296 | tf_op jit(solution)/shard_map/ppermute | solution.py:445
  623.5 29.2 %collective-permute-start.8 = (bf16[6144,384]{1,0:T(8,128)(2,1)}, bf16[6144,384]{1,0:T(8,128)(2,1)}, u32[]{:S(2)}, u32[]{:S(2)}) collective-permute-start(bf16[6144,384]{1,0:T(8,128)(2,1)} %get-tuple-element.355), channel_id=1, source_target_pairs={{0,4},{4,0},{1,5},{5,1},{2,6},{6,2},{3,7},{7,3},{8,12},{12,8},{9,1... | collective-permute-start | bytes 14155784 | tf_op jit(solution)/shard_map/ppermute | solution.py:439
  623.5 37.8 %collective-permute-start.11 = (bf16[6144,384]{1,0:T(8,128)(2,1)}, bf16[6144,384]{1,0:T(8,128)(2,1)}, u32[]{:S(2)}, u32[]{:S(2)}) collective-permute-start(bf16[6144,384]{1,0:T(8,128)(2,1)} %get-tuple-element.356), channel_id=1, source_target_pairs={{0,4},{4,0},{1,5},{5,1},{2,6},{6,2},{3,7},{7,3},{8,12},{12,8},{9,1... | collective-permute-start | bytes 14155784 | tf_op jit(solution)/shard_map/ppermute | solution.py:439
  624.1 175.2 %collective-permute-start.28 = (bf16[6144,384]{1,0:T(8,128)(2,1)}, bf16[6144,384]{1,0:T(8,128)(2,1)}, u32[]{:S(2)}, u32[]{:S(2)}) collective-permute-start(bf16[6144,384]{1,0:T(8,128)(2,1)} %get-tuple-element.358), channel_id=1, source_target_pairs={{0,4},{4,0},{1,5},{5,1},{2,6},{6,2},{3,7},{7,3},{8,12},{12,8},{9,1... | collective-permute-start | bytes 14155784 | tf_op jit(solution)/shard_map/ppermute | solution.py:439
  624.1 86.4 %collective-permute-start.16 = (bf16[6144,384]{1,0:T(8,128)(2,1)}, bf16[6144,384]{1,0:T(8,128)(2,1)}, u32[]{:S(2)}, u32[]{:S(2)}) collective-permute-start(bf16[6144,384]{1,0:T(8,128)(2,1)} %get-tuple-element.357), channel_id=1, source_target_pairs={{0,4},{4,0},{1,5},{5,1},{2,6},{6,2},{3,7},{7,3},{8,12},{12,8},{9,1... | collective-permute-start | bytes 14155784 | tf_op jit(solution)/shard_map/ppermute | solution.py:439
  661.3 39.6 %collective-permute-start.10 = (bf16[2,4,192,384]{3,2,1,0:T(8,128)(2,1)}, bf16[2,4,192,384]{3,2,1,0:T(8,128)(2,1)}, u32[]{:S(2)}, u32[]{:S(2)}) collective-permute-start(bf16[2,4,192,384]{3,2,1,0:T(8,128)(2,1)} %bitcast.12), channel_id=1, source_target_pairs={{0,8},{8,0},{1,9},{9,1},{2,10},{10,2},{3,11},{11,3},{4,12},{12,4},... | collective-permute-start | bytes 3538952 | tf_op jit(solution)/shard_map/ppermute | solution.py:439
  661.3 39.6 %collective-permute-start.9 = (bf16[2,4,192,384]{3,2,1,0:T(8,128)(2,1)}, bf16[2,4,192,384]{3,2,1,0:T(8,128)(2,1)}, u32[]{:S(2)}, u32[]{:S(2)}) collective-permute-start(bf16[2,4,192,384]{3,2,1,0:T(8,128)(2,1)} %bitcast.11), channel_id=1, source_target_pairs={{0,16},{16,0},{1,17},{17,1},{2,18},{18,2},{3,19},{19,3},{4,20},{20... | collective-permute-start | bytes 3538952 | tf_op jit(solution)/shard_map/ppermute | solution.py:439
  706.4 51.1 %collective-permute-start.14 = (bf16[2,4,192,384]{3,2,1,0:T(8,128)(2,1)}, bf16[2,4,192,384]{3,2,1,0:T(8,128)(2,1)}, u32[]{:S(2)}, u32[]{:S(2)}) collective-permute-start(bf16[2,4,192,384]{3,2,1,0:T(8,128)(2,1)} %bitcast.19), channel_id=1, source_target_pairs={{0,16},{16,0},{1,17},{17,1},{2,18},{18,2},{3,19},{19,3},{4,20},{20... | collective-permute-start | bytes 3538952 | tf_op jit(solution)/shard_map/ppermute | solution.py:439
  708.4 49.1 %collective-permute-start.15 = (bf16[2,4,192,384]{3,2,1,0:T(8,128)(2,1)}, bf16[2,4,192,384]{3,2,1,0:T(8,128)(2,1)}, u32[]{:S(2)}, u32[]{:S(2)}) collective-permute-start(bf16[2,4,192,384]{3,2,1,0:T(8,128)(2,1)} %bitcast.20), channel_id=1, source_target_pairs={{0,8},{8,0},{1,9},{9,1},{2,10},{10,2},{3,11},{11,3},{4,12},{12,4},... | collective-permute-start | bytes 3538952 | tf_op jit(solution)/shard_map/ppermute | solution.py:439
  710.5 47.0 %collective-permute-start.12 = (bf16[4,192,384]{2,1,0:T(8,128)(2,1)}, bf16[4,192,384]{2,1,0:T(8,128)(2,1)}, u32[]{:S(2)}, u32[]{:S(2)}) collective-permute-start(bf16[4,192,384]{2,1,0:T(8,128)(2,1)} %get-tuple-element.387), channel_id=1, source_target_pairs={{0,8},{8,0},{1,9},{9,1},{2,10},{10,2},{3,11},{11,3},{4,12},{12,4},... | collective-permute-start | bytes 1769480 | tf_op jit(solution)/shard_map/ppermute | solution.py:439
  710.5 47.0 %collective-permute-start.13 = (bf16[4,192,384]{2,1,0:T(8,128)(2,1)}, bf16[4,192,384]{2,1,0:T(8,128)(2,1)}, u32[]{:S(2)}, u32[]{:S(2)}) collective-permute-start(bf16[4,192,384]{2,1,0:T(8,128)(2,1)} %get-tuple-element.389), channel_id=1, source_target_pairs={{0,16},{16,0},{1,17},{17,1},{2,18},{18,2},{3,19},{19,3},{4,20},{20... | collective-permute-start | bytes 1769480 | tf_op jit(solution)/shard_map/ppermute | solution.py:439
  770.5 64.5 %collective-permute-start.24 = (bf16[512,896]{1,0:T(8,128)(2,1)}, bf16[512,896]{1,0:T(8,128)(2,1)}, u32[]{:S(2)}, u32[]{:S(2)}) collective-permute-start(bf16[512,896]{1,0:T(8,128)(2,1)} %get-tuple-element.775), channel_id=1, source_target_pairs={{1,0},{2,1},{3,2},{5,4},{6,5},{7,6},{9,8},{10,9},{11,10},{13,12},{... | collective-permute-start | bytes 2752520 | tf_op jit(solution)/shard_map/ppermute | solution.py:445
  789.0 48.2 %collective-permute-start.25 = (bf16[512,896]{1,0:T(8,128)(2,1)}, bf16[512,896]{1,0:T(8,128)(2,1)}, u32[]{:S(2)}, u32[]{:S(2)}) collective-permute-start(bf16[512,896]{1,0:T(8,128)(2,1)} %get-tuple-element.776), channel_id=1, source_target_pairs={{0,1},{1,2},{2,3},{4,5},{5,6},{6,7},{8,9},{9,10},{10,11},{12,13},{... | collective-permute-start | bytes 2752520 | tf_op jit(solution)/shard_map/ppermute | solution.py:445
  791.3 28.8 %collective-permute-start.26 = (bf16[288,896]{1,0:T(8,128)(2,1)}, bf16[288,896]{1,0:T(8,128)(2,1)}, u32[]{:S(2)}, u32[]{:S(2)}) collective-permute-start(bf16[288,896]{1,0:T(8,128)(2,1)} %get-tuple-element.773), channel_id=1, source_target_pairs={{2,0},{3,1},{6,4},{7,5},{10,8},{11,9},{14,12},{15,13},{18,16},{19,... | collective-permute-start | bytes 1548296 | tf_op jit(solution)/shard_map/ppermute | solution.py:445
  795.2 39.8 %collective-permute-start.27 = (bf16[288,896]{1,0:T(8,128)(2,1)}, bf16[288,896]{1,0:T(8,128)(2,1)}, u32[]{:S(2)}, u32[]{:S(2)}) collective-permute-start(bf16[288,896]{1,0:T(8,128)(2,1)} %get-tuple-element.774), channel_id=1, source_target_pairs={{0,2},{1,3},{4,6},{5,7},{8,10},{9,11},{12,14},{13,15},{16,18},{17,... | collective-permute-start | bytes 1548296 | tf_op jit(solution)/shard_map/ppermute | solution.py:445
  808.2 62.0 %collective-permute-start.22 = (bf16[2,4,192,384]{3,2,1,0:T(8,128)(2,1)S(1)}, bf16[2,4,192,384]{3,2,1,0:T(8,128)(2,1)S(1)}, u32[]{:S(2)}, u32[]{:S(2)}) collective-permute-start(bf16[2,4,192,384]{3,2,1,0:T(8,128)(2,1)S(1)} %bitcast.361), channel_id=1, source_target_pairs={{0,16},{16,0},{1,17},{17,1},{2,18},{18,2},{3,19},{19,3},{4,20},{20... | collective-permute-start | bytes 3538952 | tf_op jit(solution)/shard_map/ppermute | solution.py:439
  820.1 50.1 %collective-permute-start.23 = (bf16[2,4,192,384]{3,2,1,0:T(8,128)(2,1)S(1)}, bf16[2,4,192,384]{3,2,1,0:T(8,128)(2,1)S(1)}, u32[]{:S(2)}, u32[]{:S(2)}) collective-permute-start(bf16[2,4,192,384]{3,2,1,0:T(8,128)(2,1)S(1)} %bitcast.360), channel_id=1, source_target_pairs={{0,8},{8,0},{1,9},{9,1},{2,10},{10,2},{3,11},{11,3},{4,12},{12,4},... | collective-permute-start | bytes 3538952 | tf_op jit(solution)/shard_map/ppermute | solution.py:439
  835.0 35.2 %collective-permute-start.20 = (bf16[4,192,384]{2,1,0:T(8,128)(2,1)S(1)}, bf16[4,192,384]{2,1,0:T(8,128)(2,1)S(1)}, u32[]{:S(2)}, u32[]{:S(2)}) collective-permute-start(bf16[4,192,384]{2,1,0:T(8,128)(2,1)S(1)} %copy-done.127), channel_id=1, source_target_pairs={{0,8},{8,0},{1,9},{9,1},{2,10},{10,2},{3,11},{11,3},{4,12},{12,4},... | collective-permute-start | bytes 1769480 | tf_op jit(solution)/shard_map/ppermute | solution.py:439
  835.0 35.2 %collective-permute-start.21 = (bf16[4,192,384]{2,1,0:T(8,128)(2,1)S(1)}, bf16[4,192,384]{2,1,0:T(8,128)(2,1)S(1)}, u32[]{:S(2)}, u32[]{:S(2)}) collective-permute-start(bf16[4,192,384]{2,1,0:T(8,128)(2,1)S(1)} %copy-done.126), channel_id=1, source_target_pairs={{0,16},{16,0},{1,17},{17,1},{2,18},{18,2},{3,19},{19,3},{4,20},{20... | collective-permute-start | bytes 1769480 | tf_op jit(solution)/shard_map/ppermute | solution.py:439
  875.3 39.7 %collective-permute-start.34 = (bf16[2,4,192,384]{3,2,1,0:T(8,128)(2,1)}, bf16[2,4,192,384]{3,2,1,0:T(8,128)(2,1)}, u32[]{:S(2)}, u32[]{:S(2)}) collective-permute-start(bf16[2,4,192,384]{3,2,1,0:T(8,128)(2,1)} %bitcast.52), channel_id=1, source_target_pairs={{0,16},{16,0},{1,17},{17,1},{2,18},{18,2},{3,19},{19,3},{4,20},{20... | collective-permute-start | bytes 3538952 | tf_op jit(solution)/shard_map/ppermute | solution.py:439
  876.6 38.4 %collective-permute-start.35 = (bf16[2,4,192,384]{3,2,1,0:T(8,128)(2,1)}, bf16[2,4,192,384]{3,2,1,0:T(8,128)(2,1)}, u32[]{:S(2)}, u32[]{:S(2)}) collective-permute-start(bf16[2,4,192,384]{3,2,1,0:T(8,128)(2,1)} %bitcast.53), channel_id=1, source_target_pairs={{0,8},{8,0},{1,9},{9,1},{2,10},{10,2},{3,11},{11,3},{4,12},{12,4},... | collective-permute-start | bytes 3538952 | tf_op jit(solution)/shard_map/ppermute | solution.py:439
  878.2 36.7 %collective-permute-start.32 = (bf16[4,192,384]{2,1,0:T(8,128)(2,1)}, bf16[4,192,384]{2,1,0:T(8,128)(2,1)}, u32[]{:S(2)}, u32[]{:S(2)}) collective-permute-start(bf16[4,192,384]{2,1,0:T(8,128)(2,1)} %get-tuple-element.454), channel_id=1, source_target_pairs={{0,8},{8,0},{1,9},{9,1},{2,10},{10,2},{3,11},{11,3},{4,12},{12,4},... | collective-permute-start | bytes 1769480 | tf_op jit(solution)/shard_map/ppermute | solution.py:439
  952.4 60.1 %collective-permute-start.41 = (bf16[6144,384]{1,0:T(8,128)(2,1)}, bf16[6144,384]{1,0:T(8,128)(2,1)S(1)}, u32[]{:S(2)}, u32[]{:S(2)}) collective-permute-start(bf16[6144,384]{1,0:T(8,128)(2,1)} %get-tuple-element.486), channel_id=1, source_target_pairs={{0,4},{4,0},{1,5},{5,1},{2,6},{6,2},{3,7},{7,3},{8,12},{12,8},{9,1... | collective-permute-start | bytes 14155784 | tf_op jit(solution)/shard_map/ppermute | solution.py:439
  958.6 50.3 %collective-permute-start.39 = (bf16[4,192,384]{2,1,0:T(8,128)(2,1)}, bf16[4,192,384]{2,1,0:T(8,128)(2,1)S(1)}, u32[]{:S(2)}, u32[]{:S(2)}) collective-permute-start(bf16[4,192,384]{2,1,0:T(8,128)(2,1)} %get-tuple-element.477), channel_id=1, source_target_pairs={{0,8},{8,0},{1,9},{9,1},{2,10},{10,2},{3,11},{11,3},{4,12},{12,4},... | collective-permute-start | bytes 1769480 | tf_op jit(solution)/shard_map/ppermute | solution.py:439
  958.9 50.0 %collective-permute-start.40 = (bf16[4,192,384]{2,1,0:T(8,128)(2,1)S(1)}, bf16[4,192,384]{2,1,0:T(8,128)(2,1)S(1)}, u32[]{:S(2)}, u32[]{:S(2)}) collective-permute-start(bf16[4,192,384]{2,1,0:T(8,128)(2,1)S(1)} %copy-done.128), channel_id=1, source_target_pairs={{0,16},{16,0},{1,17},{17,1},{2,18},{18,2},{3,19},{19,3},{4,20},{20... | collective-permute-start | bytes 1769480 | tf_op jit(solution)/shard_map/ppermute | solution.py:439
  960.4 48.0 %collective-permute-start.37 = (bf16[384,384]{1,0:T(8,128)(2,1)}, bf16[384,384]{1,0:T(8,128)(2,1)S(1)}, u32[]{:S(2)}, u32[]{:S(2)}) collective-permute-start(bf16[384,384]{1,0:T(8,128)(2,1)} %pad_maximum_fusion.21), channel_id=1, source_target_pairs={{0,2},{1,3},{2,0},{3,1},{4,6},{5,7},{6,4},{7,5},{8,10},{9,11},{10,... | collective-permute-start | bytes 884744 | tf_op jit(solution)/shard_map/ppermute | solution.py:439
  966.4 42.1 %collective-permute-start.38 = (bf16[384,384]{1,0:T(8,128)(2,1)}, bf16[384,384]{1,0:T(8,128)(2,1)S(1)}, u32[]{:S(2)}, u32[]{:S(2)}) collective-permute-start(bf16[384,384]{1,0:T(8,128)(2,1)} %pad_maximum_fusion.22), channel_id=1, source_target_pairs={{0,3},{1,0},{2,1},{3,2},{4,7},{5,4},{6,5},{7,6},{8,11},{9,8},{10,9... | collective-permute-start | bytes 884744 | tf_op jit(solution)/shard_map/ppermute | solution.py:439
  1008.4 71.7 %collective-permute-start.52 = (bf16[6144,384]{1,0:T(8,128)(2,1)}, bf16[6144,384]{1,0:T(8,128)(2,1)}, u32[]{:S(2)}, u32[]{:S(2)}) collective-permute-start(bf16[6144,384]{1,0:T(8,128)(2,1)} %get-tuple-element.488), channel_id=1, source_target_pairs={{0,4},{4,0},{1,5},{5,1},{2,6},{6,2},{3,7},{7,3},{8,12},{12,8},{9,1... | collective-permute-start | bytes 14155784 | tf_op jit(solution)/shard_map/ppermute | solution.py:439
  1008.5 39.2 %collective-permute-start.47 = (bf16[6144,384]{1,0:T(8,128)(2,1)}, bf16[6144,384]{1,0:T(8,128)(2,1)}, u32[]{:S(2)}, u32[]{:S(2)}) collective-permute-start(bf16[6144,384]{1,0:T(8,128)(2,1)} %get-tuple-element.487), channel_id=1, source_target_pairs={{0,4},{4,0},{1,5},{5,1},{2,6},{6,2},{3,7},{7,3},{8,12},{12,8},{9,1... | collective-permute-start | bytes 14155784 | tf_op jit(solution)/shard_map/ppermute | solution.py:439
  1018.7 51.1 %collective-permute-start.45 = (bf16[2,4,192,384]{3,2,1,0:T(8,128)(2,1)}, bf16[2,4,192,384]{3,2,1,0:T(8,128)(2,1)}, u32[]{:S(2)}, u32[]{:S(2)}) collective-permute-start(bf16[2,4,192,384]{3,2,1,0:T(8,128)(2,1)} %bitcast.77), channel_id=1, source_target_pairs={{0,16},{16,0},{1,17},{17,1},{2,18},{18,2},{3,19},{19,3},{4,20},{20... | collective-permute-start | bytes 3538952 | tf_op jit(solution)/shard_map/ppermute | solution.py:439
  1020.1 49.7 %collective-permute-start.46 = (bf16[2,4,192,384]{3,2,1,0:T(8,128)(2,1)}, bf16[2,4,192,384]{3,2,1,0:T(8,128)(2,1)}, u32[]{:S(2)}, u32[]{:S(2)}) collective-permute-start(bf16[2,4,192,384]{3,2,1,0:T(8,128)(2,1)} %bitcast.78), channel_id=1, source_target_pairs={{0,8},{8,0},{1,9},{9,1},{2,10},{10,2},{3,11},{11,3},{4,12},{12,4},... | collective-permute-start | bytes 3538952 | tf_op jit(solution)/shard_map/ppermute | solution.py:439
  1020.4 35.0 %collective-permute-start.42 = (bf16[384,384]{1,0:T(8,128)(2,1)}, bf16[384,384]{1,0:T(8,128)(2,1)S(1)}, u32[]{:S(2)}, u32[]{:S(2)}) collective-permute-start(bf16[384,384]{1,0:T(8,128)(2,1)} %pad_maximum_fusion.24), channel_id=1, source_target_pairs={{0,1},{1,2},{2,3},{3,0},{4,5},{5,6},{6,7},{7,4},{8,9},{9,10},{10,1... | collective-permute-start | bytes 884744 | tf_op jit(solution)/shard_map/ppermute | solution.py:439
  1076.0 45.5 %collective-permute-start.50 = (bf16[2,4,192,384]{3,2,1,0:T(8,128)(2,1)}, bf16[2,4,192,384]{3,2,1,0:T(8,128)(2,1)}, u32[]{:S(2)}, u32[]{:S(2)}) collective-permute-start(bf16[2,4,192,384]{3,2,1,0:T(8,128)(2,1)} %bitcast.85), channel_id=1, source_target_pairs={{0,16},{16,0},{1,17},{17,1},{2,18},{18,2},{3,19},{19,3},{4,20},{20... | collective-permute-start | bytes 3538952 | tf_op jit(solution)/shard_map/ppermute | solution.py:439
  1076.6 44.9 %collective-permute-start.51 = (bf16[2,4,192,384]{3,2,1,0:T(8,128)(2,1)}, bf16[2,4,192,384]{3,2,1,0:T(8,128)(2,1)}, u32[]{:S(2)}, u32[]{:S(2)}) collective-permute-start(bf16[2,4,192,384]{3,2,1,0:T(8,128)(2,1)} %bitcast.86), channel_id=1, source_target_pairs={{0,8},{8,0},{1,9},{9,1},{2,10},{10,2},{3,11},{11,3},{4,12},{12,4},... | collective-permute-start | bytes 3538952 | tf_op jit(solution)/shard_map/ppermute | solution.py:439
  1078.4 43.1 %collective-permute-start.48 = (bf16[4,192,384]{2,1,0:T(8,128)(2,1)}, bf16[4,192,384]{2,1,0:T(8,128)(2,1)}, u32[]{:S(2)}, u32[]{:S(2)}) collective-permute-start(bf16[4,192,384]{2,1,0:T(8,128)(2,1)} %get-tuple-element.526), channel_id=1, source_target_pairs={{0,8},{8,0},{1,9},{9,1},{2,10},{10,2},{3,11},{11,3},{4,12},{12,4},... | collective-permute-start | bytes 1769480 | tf_op jit(solution)/shard_map/ppermute | solution.py:439
  1078.7 42.9 %collective-permute-start.49 = (bf16[4,192,384]{2,1,0:T(8,128)(2,1)}, bf16[4,192,384]{2,1,0:T(8,128)(2,1)}, u32[]{:S(2)}, u32[]{:S(2)}) collective-permute-start(bf16[4,192,384]{2,1,0:T(8,128)(2,1)} %get-tuple-element.528), channel_id=1, source_target_pairs={{0,16},{16,0},{1,17},{17,1},{2,18},{18,2},{3,19},{19,3},{4,20},{20... | collective-permute-start | bytes 1769480 | tf_op jit(solution)/shard_map/ppermute | solution.py:439
  1080.1 110.6 %collective-permute-start.64 = (bf16[6144,384]{1,0:T(8,128)(2,1)}, bf16[6144,384]{1,0:T(8,128)(2,1)}, u32[]{:S(2)}, u32[]{:S(2)}) collective-permute-start(bf16[6144,384]{1,0:T(8,128)(2,1)} %get-tuple-element.489), channel_id=1, source_target_pairs={{0,4},{4,0},{1,5},{5,1},{2,6},{6,2},{3,7},{7,3},{8,12},{12,8},{9,1... | collective-permute-start | bytes 14155784 | tf_op jit(solution)/shard_map/ppermute | solution.py:439
  1133.2 46.9 %collective-permute-start.60 = (bf16[512,768]{1,0:T(8,128)(2,1)S(1)}, bf16[512,768]{1,0:T(8,128)(2,1)S(1)}, u32[]{:S(2)}, u32[]{:S(2)}) collective-permute-start(bf16[512,768]{1,0:T(8,128)(2,1)S(1)} %get-tuple-element.779), channel_id=1, source_target_pairs={{1,0},{2,1},{3,2},{5,4},{6,5},{7,6},{9,8},{10,9},{11,10},{13,12},{... | collective-permute-start | bytes 2359304 | tf_op jit(solution)/shard_map/ppermute | solution.py:445
  1139.3 40.8 %collective-permute-start.61 = (bf16[512,768]{1,0:T(8,128)(2,1)S(1)}, bf16[512,768]{1,0:T(8,128)(2,1)}, u32[]{:S(2)}, u32[]{:S(2)}) collective-permute-start(bf16[512,768]{1,0:T(8,128)(2,1)S(1)} %get-tuple-element.780), channel_id=1, source_target_pairs={{0,1},{1,2},{2,3},{4,5},{5,6},{6,7},{8,9},{9,10},{10,11},{12,13},{... | collective-permute-start | bytes 2359304 | tf_op jit(solution)/shard_map/ppermute | solution.py:445
  1146.2 33.9 %collective-permute-start.63 = (bf16[288,768]{1,0:T(8,128)(2,1)S(1)}, bf16[288,768]{1,0:T(8,128)(2,1)}, u32[]{:S(2)}, u32[]{:S(2)}) collective-permute-start(bf16[288,768]{1,0:T(8,128)(2,1)S(1)} %get-tuple-element.778), channel_id=1, source_target_pairs={{0,2},{1,3},{4,6},{5,7},{8,10},{9,11},{12,14},{13,15},{16,18},{17,... | collective-permute-start | bytes 1327112 | tf_op jit(solution)/shard_map/ppermute | solution.py:445
  1166.4 49.7 %collective-permute-start.53 = (bf16[384,384]{1,0:T(8,128)(2,1)}, bf16[384,384]{1,0:T(8,128)(2,1)}, u32[]{:S(2)}, u32[]{:S(2)}) collective-permute-start(bf16[384,384]{1,0:T(8,128)(2,1)} %pad_maximum_fusion.28), channel_id=1, source_target_pairs={{0,1},{1,2},{2,3},{3,0},{4,5},{5,6},{6,7},{7,4},{8,9},{9,10},{10,1... | collective-permute-start | bytes 884744 | tf_op jit(solution)/shard_map/ppermute | solution.py:439
  1180.1 36.3 %collective-permute-start.54 = (bf16[384,384]{1,0:T(8,128)(2,1)}, bf16[384,384]{1,0:T(8,128)(2,1)}, u32[]{:S(2)}, u32[]{:S(2)}) collective-permute-start(bf16[384,384]{1,0:T(8,128)(2,1)} %pad_maximum_fusion.29), channel_id=1, source_target_pairs={{0,2},{1,3},{2,0},{3,1},{4,6},{5,7},{6,4},{7,5},{8,10},{9,11},{10,... | collective-permute-start | bytes 884744 | tf_op jit(solution)/shard_map/ppermute | solution.py:439
  1200.5 53.9 %collective-permute-start.58 = (bf16[2,4,192,384]{3,2,1,0:T(8,128)(2,1)S(1)}, bf16[2,4,192,384]{3,2,1,0:T(8,128)(2,1)S(1)}, u32[]{:S(2)}, u32[]{:S(2)}) collective-permute-start(bf16[2,4,192,384]{3,2,1,0:T(8,128)(2,1)S(1)} %bitcast.359), channel_id=1, source_target_pairs={{0,16},{16,0},{1,17},{17,1},{2,18},{18,2},{3,19},{19,3},{4,20},{20... | collective-permute-start | bytes 3538952 | tf_op jit(solution)/shard_map/ppermute | solution.py:439
  1213.1 41.3 %collective-permute-start.59 = (bf16[2,4,192,384]{3,2,1,0:T(8,128)(2,1)S(1)}, bf16[2,4,192,384]{3,2,1,0:T(8,128)(2,1)S(1)}, u32[]{:S(2)}, u32[]{:S(2)}) collective-permute-start(bf16[2,4,192,384]{3,2,1,0:T(8,128)(2,1)S(1)} %bitcast.358), channel_id=1, source_target_pairs={{0,8},{8,0},{1,9},{9,1},{2,10},{10,2},{3,11},{11,3},{4,12},{12,4},... | collective-permute-start | bytes 3538952 | tf_op jit(solution)/shard_map/ppermute | solution.py:439
  1214.2 28.8 %collective-permute-start.92 = (f32[6,1472]{1,0:T(8,128)S(1)}, f32[6,1472]{1,0:T(8,128)S(1)}, u32[]{:S(2)}, u32[]{:S(2)}) collective-permute-start(f32[6,1472]{1,0:T(8,128)S(1)} %add.880), channel_id=1, source_target_pairs={{0,8},{8,0},{1,9},{9,1},{2,10},{10,2},{3,11},{11,3},{4,12},{12,4},... | collective-permute-start | bytes 105992 | tf_op jit(solution)/shard_map/ppermute | solution.py:497
  1216.1 38.4 %collective-permute-start.56 = (bf16[4,192,384]{2,1,0:T(8,128)(2,1)S(1)}, bf16[4,192,384]{2,1,0:T(8,128)(2,1)S(1)}, u32[]{:S(2)}, u32[]{:S(2)}) collective-permute-start(bf16[4,192,384]{2,1,0:T(8,128)(2,1)S(1)} %copy-done.125), channel_id=1, source_target_pairs={{0,8},{8,0},{1,9},{9,1},{2,10},{10,2},{3,11},{11,3},{4,12},{12,4},... | collective-permute-start | bytes 1769480 | tf_op jit(solution)/shard_map/ppermute | solution.py:439
  1216.4 38.0 %collective-permute-start.57 = (bf16[4,192,384]{2,1,0:T(8,128)(2,1)S(1)}, bf16[4,192,384]{2,1,0:T(8,128)(2,1)S(1)}, u32[]{:S(2)}, u32[]{:S(2)}) collective-permute-start(bf16[4,192,384]{2,1,0:T(8,128)(2,1)S(1)} %copy-done.124), channel_id=1, source_target_pairs={{0,16},{16,0},{1,17},{17,1},{2,18},{18,2},{3,19},{19,3},{4,20},{20... | collective-permute-start | bytes 1769480 | tf_op jit(solution)/shard_map/ppermute | solution.py:439
  1260.3 40.2 %collective-permute-start.70 = (bf16[2,4,192,384]{3,2,1,0:T(8,128)(2,1)}, bf16[2,4,192,384]{3,2,1,0:T(8,128)(2,1)}, u32[]{:S(2)}, u32[]{:S(2)}) collective-permute-start(bf16[2,4,192,384]{3,2,1,0:T(8,128)(2,1)} %bitcast.118), channel_id=1, source_target_pairs={{0,16},{16,0},{1,17},{17,1},{2,18},{18,2},{3,19},{19,3},{4,20},{20... | collective-permute-start | bytes 3538952 | tf_op jit(solution)/shard_map/ppermute | solution.py:439
  1260.8 40.4 %collective-permute-start.71 = (bf16[2,4,192,384]{3,2,1,0:T(8,128)(2,1)}, bf16[2,4,192,384]{3,2,1,0:T(8,128)(2,1)}, u32[]{:S(2)}, u32[]{:S(2)}) collective-permute-start(bf16[2,4,192,384]{3,2,1,0:T(8,128)(2,1)} %bitcast.119), channel_id=1, source_target_pairs={{0,8},{8,0},{1,9},{9,1},{2,10},{10,2},{3,11},{11,3},{4,12},{12,4},... | collective-permute-start | bytes 3538952 | tf_op jit(solution)/shard_map/ppermute | solution.py:439
  1262.5 37.8 %collective-permute-start.68 = (bf16[4,192,384]{2,1,0:T(8,128)(2,1)}, bf16[4,192,384]{2,1,0:T(8,128)(2,1)S(1)}, u32[]{:S(2)}, u32[]{:S(2)}) collective-permute-start(bf16[4,192,384]{2,1,0:T(8,128)(2,1)} %get-tuple-element.593), channel_id=1, source_target_pairs={{0,8},{8,0},{1,9},{9,1},{2,10},{10,2},{3,11},{11,3},{4,12},{12,4},... | collective-permute-start | bytes 1769480 | tf_op jit(solution)/shard_map/ppermute | solution.py:439
  1268.7 31.7 %collective-permute-start.69 = (bf16[4,192,384]{2,1,0:T(8,128)(2,1)}, bf16[4,192,384]{2,1,0:T(8,128)(2,1)}, u32[]{:S(2)}, u32[]{:S(2)}) collective-permute-start(bf16[4,192,384]{2,1,0:T(8,128)(2,1)} %get-tuple-element.595), channel_id=1, source_target_pairs={{0,16},{16,0},{1,17},{17,1},{2,18},{18,2},{3,19},{19,3},{4,20},{20... | collective-permute-start | bytes 1769480 | tf_op jit(solution)/shard_map/ppermute | solution.py:439
  1300.3 34.9 %collective-permute-start.94 = (f32[6,1472]{1,0:T(8,128)}, f32[6,1472]{1,0:T(8,128)}, u32[]{:S(2)}, u32[]{:S(2)}) collective-permute-start(f32[6,1472]{1,0:T(8,128)} %add.882), channel_id=1, source_target_pairs={{0,1},{1,0},{2,3},{3,2},{4,5},{5,4},{6,7},{7,6},{8,9},{9,8},{10,11... | collective-permute-start | bytes 105992 | tf_op jit(solution)/shard_map/ppermute | solution.py:497
  1333.1 27.7 %collective-permute-start.76 = (bf16[4,192,384]{2,1,0:T(8,128)(2,1)}, bf16[4,192,384]{2,1,0:T(8,128)(2,1)S(1)}, u32[]{:S(2)}, u32[]{:S(2)}) collective-permute-start(bf16[4,192,384]{2,1,0:T(8,128)(2,1)} %get-tuple-element.623), channel_id=1, source_target_pairs={{0,8},{8,0},{1,9},{9,1},{2,10},{10,2},{3,11},{11,3},{4,12},{12,4},... | collective-permute-start | bytes 1769480 | tf_op jit(solution)/shard_map/ppermute | solution.py:439
  1334.6 26.3 %collective-permute-start.77 = (bf16[4,192,384]{2,1,0:T(8,128)(2,1)}, bf16[4,192,384]{2,1,0:T(8,128)(2,1)S(1)}, u32[]{:S(2)}, u32[]{:S(2)}) collective-permute-start(bf16[4,192,384]{2,1,0:T(8,128)(2,1)} %get-tuple-element.625), channel_id=1, source_target_pairs={{0,16},{16,0},{1,17},{17,1},{2,18},{18,2},{3,19},{19,3},{4,20},{20... | collective-permute-start | bytes 1769480 | tf_op jit(solution)/shard_map/ppermute | solution.py:439
  1335.3 25.6 %collective-permute-start.78 = (bf16[2,4,24,1472]{3,2,1,0:T(8,128)(2,1)S(1)}, bf16[2,4,24,1472]{3,2,1,0:T(8,128)(2,1)S(1)}, u32[]{:S(2)}, u32[]{:S(2)}) collective-permute-start(bf16[2,4,24,1472]{3,2,1,0:T(8,128)(2,1)S(1)} %bitcast.363), channel_id=1, source_target_pairs={{0,16},{16,0},{1,17},{17,1},{2,18},{18,2},{3,19},{19,3},{4,20},{20... | collective-permute-start | bytes 1695752 | tf_op jit(solution)/shard_map/ppermute | solution.py:439
  (242 other events, 4097.9 us)
Sparse Core Ops, SparseCore 0:
  10.9 214.3 all-gather.2
  228.2 242.5 all-gather.4

commit v3 on v2

--- a/solution.py
+++ b/solution.py
@@ -21,6 +21,7 @@
 ATTENTION_TILES = 4 * INNER // TILE
 OFFSETS = 5
 CHUNK = 384
+FORWARD_TILE = 512
 CUTS = (0, 384, 768, 1152, 1472)
 DEVICES = ("y", "x", "c", "z")
 epsilon = 1e-06
@@ -512,182 +513,217 @@
     return [shift(sent, axis_name, k + 1) for k, sent in enumerate(sends)]
 
 
-def grad_tiles_body(phase, attended, core_ref, *refs):
-    up_ref, hidden_ref, normed_ref, branch_ref = refs[:4]
-    outs = refs[-4:]
-    tile = source_tile(phase, pl.program_id(0), core_ref)
-
-    def put(*products):
-        turned = [(left[...].T, right) for left, right in products]
-        for out, start, end in zip(outs, CUTS[:-1], CUTS[1:]):
-            total = jnp.zeros((TILE, end - start), jnp.float32)
-            for left, right in turned:
-                total = total + jnp.dot(
-                    left, right[:, start:end], preferred_element_type=jnp.float32
-                )
-            out[:, : end - start] = total.astype(jnp.bfloat16)
-            if end - start < CHUNK:
-                out[:, end - start :] = jnp.zeros((TILE, CHUNK - end + start), jnp.bfloat16)
-
-    @pl.when(tile < ATTENTION_TILES)
+def gelu_parts(values):
+    squared = values * values
+    slope = jnp.tanh(0.7978845608028654 * (values + 0.044715 * values * squared))
+    active = 0.5 * values * (1.0 + slope)
+    inner = 0.7978845608028654 * (1.0 + 3.0 * 0.044715 * squared)
+    return active, 0.5 * (1.0 + slope) + 0.5 * values * (1.0 - slope * slope) * inner
+
+
+def ffn_forward_body(normed_ref, middle_ref, gelu_ref, linear_ref, down_ref, *outs):
+    result_ref, up_gelu_ref, up_linear_ref = outs
+
+    @pl.when(pl.program_id(0) == 0)
     def _():
-        if attended:
-            first_ref, second_ref, first_side_ref, second_side_ref = refs[4:8]
-            put((first_ref, first_side_ref), (second_ref, second_side_ref))
-        else:
-            put()
-
-    @pl.when((tile >= ATTENTION_TILES) & (tile < ATTENTION_TILES + 2 * FF // TILE))
+        result_ref[...] = middle_ref[...]
+
+    up_gelu = times_rows(normed_ref[...], gelu_ref[...])
+    up_linear = times_rows(normed_ref[...], linear_ref[...])
+    up_gelu_ref[...] = up_gelu
+    up_linear_ref[...] = up_linear
+    hidden = (gelu_tanh(up_gelu) * up_linear).astype(jnp.bfloat16)
+    result_ref[...] += times_plain(hidden, down_ref[...])
+
+
+def resident(shape):
+    return pl.BlockSpec(shape, lambda *_: (0,) * len(shape), pipeline_mode=pl.Buffered(1))
+
+
+def ffn_forward(normed, middle, gathered):
+    tokens, width = normed.shape
+    steps = FF // FORWARD_TILE
+    first = 4 * INNER // FORWARD_TILE
+
+    def weight(kind):
+        return pl.BlockSpec((FORWARD_TILE, width), lambda i: (first + kind * steps + i, 0))
+
+    hidden = pl.BlockSpec((tokens, FORWARD_TILE), lambda i: (0, i))
+    return pl.pallas_call(
+        ffn_forward_body,
+        grid=(steps,),
+        in_specs=[
+            resident((tokens, width)),
+            resident((tokens, width)),
+            weight(0),
+            weight(1),
+            weight(2),
+        ],
+        out_specs=[resident((tokens, width)), hidden, hidden],
+        out_shape=[
+            jax.ShapeDtypeStruct((tokens, width), jnp.float32),
+            jax.ShapeDtypeStruct((tokens, FF), jnp.float32),
+            jax.ShapeDtypeStruct((tokens, FF), jnp.float32),
+        ],
+        compiler_params=pltpu.CompilerParams(vmem_limit_bytes=48 << 20),
+        cost_estimate=pl.CostEstimate(
+            flops=6 * tokens * FF * width,
+            bytes_accessed=6 * FF * width + 8 * tokens * FF,
+            transcendentals=tokens * FF,
+        ),
+        name="ffn_forward",
+    )(normed, middle, gathered, gathered, gathered)
+
+
+def ffn_backward_body(attended, core_ref, *refs):
+    branch_ref, normed_ref, up_gelu_ref, up_linear_ref, gelu_ref, linear_ref, down_ref = refs[:7]
+    refs = refs[7:]
+    if attended:
+        first_ref, second_ref, first_side_ref, second_side_ref = refs[:4]
+        refs = refs[4:]
+    grad_ref, kept_refs, sent_refs = refs[0], refs[1:5], refs[5:9]
+    stage_ref, sems = refs[9], refs[10]
+    step = pl.program_id(0)
+    hidden_steps = FF // TILE
+    slot = step % 2
+    mine, unit, rows, columns = core_ref[0], core_ref[1], core_ref[2], core_ref[3]
+
+    def places(target):
+        unit_at, inside = target // (2 * unit), target % unit
+        swapped = (unit_at % columns) * rows + unit_at // columns
+        for k in range(4):
+            at = (unit_at if k % 2 == 0 else swapped) * unit + inside
+            yield k, pl.ds(pl.multiple_of(at * TILE, TILE), TILE)
+
+    def copy(kind, k, place, spot, where):
+        source = stage_ref.at[where, kind, :, k * CHUNK : (k + 1) * CHUNK]
+        return pltpu.make_async_copy(source, place[k].at[spot, :], sems.at[where, kind, k])
+
+    def wait(kind, where):
+        for k in range(4):
+            copy(kind, k, kept_refs, pl.ds(0, TILE), where).wait()
+
+    def put(kind, target, left, right):
+        product = jnp.dot(left, right, preferred_element_type=jnp.float32)
+        stage_ref[slot, kind, :, : CUTS[-1]] = product.astype(jnp.bfloat16)
+        own = (target // unit) % 2 == mine
+        spots = list(places(target))
+
+        @pl.when(own)
+        def _():
+            for k, spot in spots:
+                copy(kind, k, kept_refs, spot, slot).start()
+
+        @pl.when(jnp.logical_not(own))
+        def _():
+            for k, spot in spots:
+                copy(kind, k, sent_refs, spot, slot).start()
+
+    @pl.when(step == 0)
     def _():
-        put((up_ref, normed_ref))
-
-    @pl.when(tile >= ATTENTION_TILES + 2 * FF // TILE)
+        grad_ref[...] = jnp.zeros_like(grad_ref)
+        stage_ref[:, :, :, CUTS[-1] :] = jnp.zeros(
+            stage_ref.shape[:3] + (4 * CHUNK - CUTS[-1],), jnp.bfloat16
+        )
+
+    @pl.when((step >= 2) & (step < hidden_steps + 2))
     def _():
-        put((hidden_ref, branch_ref))
-
-
-def source_tile(phase, step, core_ref):
-    core = core_ref[0] if phase else 1 - core_ref[0]
-    unit = core_ref[1]
-    return (step // unit) * 2 * unit + core * unit + step % unit
-
-
-def grad_tiles(phase, up_grads, hidden, normed_two, branch, attention):
-    tokens, width = normed_two.shape
+        for kind in range(3):
+            wait(kind, slot)
+
+    if attended:
+
+        @pl.when(step >= hidden_steps + 2)
+        def _():
+            wait(0, slot)
+
+    @pl.when(step < hidden_steps)
+    def _():
+        grad_hidden = times_rows(branch_ref[...], down_ref[...])
+        active, slope = gelu_parts(up_gelu_ref[...])
+        linear = up_linear_ref[...]
+        hidden = (active * linear).astype(jnp.bfloat16)
+        grad_gelu = (grad_hidden * linear * slope).astype(jnp.bfloat16)
+        grad_linear = (grad_hidden * active).astype(jnp.bfloat16)
+        grad_ref[...] += times_plain(grad_gelu, gelu_ref[...]) + times_plain(
+            grad_linear, linear_ref[...]
+        )
+        put(0, ATTENTION_TILES + step, grad_gelu.T, normed_ref[...])
+        put(1, ATTENTION_TILES + hidden_steps + step, grad_linear.T, normed_ref[...])
+        put(2, ATTENTION_TILES + 2 * hidden_steps + step, hidden.T, branch_ref[...])
+
+    if attended:
+
+        @pl.when(step >= hidden_steps)
+        def _():
+            put(
+                0,
+                step - hidden_steps,
+                jnp.concatenate([first_ref[...], second_ref[...]], axis=0).T,
+                jnp.concatenate([first_side_ref[...], second_side_ref[...]], axis=0),
+            )
+
+    @pl.when(step == pl.num_programs(0) - 1)
+    def _():
+        for back in range(2):
+            for kind in range(1 if attended else 3):
+                wait(kind, back)
+
+
+def ffn_backward(branch, normed, up_gelu, up_linear, gathered, attention):
+    tokens, width = normed.shape
     rows = 4 * INNER + 3 * FF
-    steps = rows // TILE // 2
-    unit = steps // (lax.axis_size("y") * lax.axis_size("x"))
-    core = jnp.stack([lax.axis_index("c").astype(jnp.int32), jnp.int32(unit)])
-    up_tiles = 2 * FF // TILE
-
-    def up_map(step, core_ref):
-        tile = source_tile(phase, step, core_ref)
-        return 0, jnp.clip(tile - ATTENTION_TILES, 0, up_tiles - 1)
-
-    def hidden_map(step, core_ref):
-        tile = source_tile(phase, step, core_ref)
-        return 0, jnp.clip(tile - ATTENTION_TILES - up_tiles, 0, FF // TILE - 1)
-
-    def attention_map(step, core_ref):
-        return 0, jnp.minimum(source_tile(phase, step, core_ref), ATTENTION_TILES - 1)
-
-    side = pl.BlockSpec((tokens, width), lambda *_: (0, 0), pipeline_mode=pl.Buffered(1))
-    column = (tokens, TILE)
-    operands = [up_grads, hidden, normed_two, branch]
-    in_specs = [pl.BlockSpec(column, up_map), pl.BlockSpec(column, hidden_map), side, side]
+    hidden_steps = FF // TILE
+    size_y, size_x = lax.axis_size("y"), lax.axis_size("x")
+    unit = rows // TILE // (2 * size_y * size_x)
+    core = jnp.stack(
+        [
+            lax.axis_index("c").astype(jnp.int32),
+            jnp.int32(unit),
+            jnp.int32(size_y),
+            jnp.int32(size_x),
+        ]
+    )
+    last = hidden_steps - 1
+
+    def weight(kind):
+        first = ATTENTION_TILES + kind * hidden_steps
+        return pl.BlockSpec((TILE, width), lambda i, *_: (first + jnp.minimum(i, last), 0))
+
+    hidden = pl.BlockSpec((tokens, TILE), lambda i, *_: (0, jnp.minimum(i, last)))
+    late = pl.BlockSpec((tokens, TILE), lambda i, *_: (0, jnp.maximum(i - hidden_steps, 0)))
+    side = resident((tokens, width))
+    operands = [branch, normed, up_gelu, up_linear, gathered, gathered, gathered]
+    in_specs = [side, side, hidden, hidden, weight(0), weight(1), weight(2)]
+    steps = hidden_steps
     if attention is not None:
         operands += attention
-        in_specs += [
-            pl.BlockSpec(column, attention_map),
-            pl.BlockSpec(column, attention_map),
-            side,
-            side,
-        ]
+        in_specs += [late, late, side, side]
+        steps += ATTENTION_TILES
+    anywhere = pl.BlockSpec(memory_space=pl.ANY)
     results = pl.pallas_call(
-        functools.partial(grad_tiles_body, phase, attention is not None),
+        functools.partial(ffn_backward_body, attention is not None),
         grid_spec=pltpu.PrefetchScalarGridSpec(
             num_scalar_prefetch=1,
             grid=(steps,),
             in_specs=in_specs,
-            out_specs=[pl.BlockSpec((TILE, CHUNK), lambda i, *_: (i, 0))] * 4,
-        ),
-        out_shape=[jax.ShapeDtypeStruct((rows // 2, CHUNK), jnp.bfloat16)] * 4,
-        compiler_params=pltpu.CompilerParams(vmem_limit_bytes=40 << 20),
-        cost_estimate=pl.CostEstimate(
-            flops=tokens * rows * width,
-            bytes_accessed=2 * rows * width,
-            transcendentals=0,
-        ),
-        name="grad_tiles",
-    )(core, *operands)
-    return list(results)
-
-
-def split_body(place_ref, kept_ref, moved_ref, left_ref, left_send_ref, right_ref, right_send_ref):
-    i, j = pl.program_id(0), pl.program_id(1)
-    both = kept_ref[0, 0].astype(jnp.float32) + moved_ref[0, 0].astype(jnp.float32)
-    both = both.astype(jnp.bfloat16)
-    left, right = both[:, 0], both[:, 1]
-
-    @pl.when(i < pl.num_programs(0) - 1)
-    def _():
-        left_send_ref[0, 0] = left
-
-    @pl.when(i == pl.num_programs(0) - 1)
-    def _():
-        left_ref[0] = left
-
-    @pl.when(j < pl.num_programs(1) - 1)
-    def _():
-        right_send_ref[0, 0] = right
-
-    @pl.when(j == pl.num_programs(1) - 1)
-    def _():
-        right_ref[0] = right
-
-
-def split_sums(kept, moved):
-    size_y, size_x, size_z = (lax.axis_size(axis) for axis in ("y", "x", "z"))
-    chunk = kept.shape[-1]
-    shape = (size_y, size_x, size_z, 2, kept.size // (2 * size_y * size_x * size_z * chunk), chunk)
-    piece = shape[2:3] + shape[4:]
-    place = jnp.stack([lax.axis_index("y"), lax.axis_index("x")]).astype(jnp.int32)
-    zeros = (0, 0, 0)
-
-    def row_of(i, place_ref):
-        return (place_ref[0] + 1 + i) % size_y
-
-    def column_of(j, place_ref):
-        return (place_ref[1] + 1 + j) % size_x
-
-    def in_map(i, j, place_ref):
-        return (row_of(i, place_ref), column_of(j, place_ref), 0) + zeros
-
-    def left_map(i, j, place_ref):
-        return (jnp.where(i == size_y - 1, column_of(j, place_ref), column_of(0, place_ref)),) + zeros
-
-    def left_send_map(i, j, place_ref):
-        column = jnp.where(i < size_y - 1, column_of(j, place_ref), place_ref[1])
-        return (jnp.minimum(i, size_y - 2), column) + zeros
-
-    def right_map(i, j, place_ref):
-        return (row_of(i, place_ref),) + zeros
-
-    def right_send_map(i, j, place_ref):
-        return (jnp.minimum(j, size_x - 2), row_of(i, place_ref)) + zeros
-
-    block = pl.BlockSpec((1, 1) + shape[2:], in_map)
-    left, left_sends, right, right_sends = pl.pallas_call(
-        split_body,
-        grid_spec=pltpu.PrefetchScalarGridSpec(
-            num_scalar_prefetch=1,
-            grid=(size_y, size_x),
-            in_specs=[block, block],
-            out_specs=[
-                pl.BlockSpec((1,) + piece, left_map),
-                pl.BlockSpec((1, 1) + piece, left_send_map),
-                pl.BlockSpec((1,) + piece, right_map),
-                pl.BlockSpec((1, 1) + piece, right_send_map),
+            out_specs=[side] + [anywhere] * 8,
+            scratch_shapes=[
+                pltpu.VMEM((2, 3, TILE, 4 * CHUNK), jnp.bfloat16),
+                pltpu.SemaphoreType.DMA((2, 3, 4)),
             ],
         ),
-        out_shape=[
-            jax.ShapeDtypeStruct((size_x,) + piece, jnp.bfloat16),
-            jax.ShapeDtypeStruct((size_y - 1, size_x) + piece, jnp.bfloat16),
-            jax.ShapeDtypeStruct((size_y,) + piece, jnp.bfloat16),
-            jax.ShapeDtypeStruct((size_x - 1, size_y) + piece, jnp.bfloat16),
-        ],
-        compiler_params=pltpu.CompilerParams(vmem_limit_bytes=32 << 20),
+        out_shape=[jax.ShapeDtypeStruct((tokens, width), jnp.float32)]
+        + [jax.ShapeDtypeStruct((rows // 2, CHUNK), jnp.bfloat16)] * 8,
+        compiler_params=pltpu.CompilerParams(vmem_limit_bytes=52 << 20),
         cost_estimate=pl.CostEstimate(
-            flops=kept.size, bytes_accessed=6 * kept.size, transcendentals=0
+            flops=12 * tokens * FF * width,
+            bytes_accessed=12 * FF * width + 8 * tokens * FF,
+            transcendentals=tokens * FF,
         ),
-        name="split_sums",
-    )(place, kept.reshape(shape), moved.reshape(shape))
-    return (
-        left,
-        [left_sends[k] for k in range(size_y - 1)],
-        right,
-        [right_sends[k] for k in range(size_x - 1)],
-    )
+        name="ffn_backward",
+    )(core, *operands)
+    return results[0], list(results[1:5]), list(results[5:9])
 
 
 def tied(first, second):
@@ -698,50 +734,33 @@
     def __init__(self):
         self.waiting, self.flying, self.results = [], [], {}
 
-    def push(self, name, kept, moved):
-        self.waiting.append((name, kept, moved))
+    def push(self, name, route, kept, moved):
+        shape = tuple(lax.axis_size(axis) for axis in route) + (-1, kept.shape[-1])
+        self.waiting.append((name, route, kept.reshape(shape), [moved.reshape(shape)]))
 
     def busy(self):
         return bool(self.waiting or self.flying)
 
-    def step(self, values, enter=1):
+    def step(self, values, enter=2):
         flying = [item[2:] for item in self.flying]
+        flying, values = tied(flying, values)
         entering, self.waiting = self.waiting[:enter], self.waiting[enter:]
-        flying, values = tied(flying, values)
+        ready = [item[:2] + tuple(arrays) for item, arrays in zip(self.flying, flying)] + entering
         moves = []
-        for (name, stage, *_), (left, left_moved, right, right_moved) in zip(self.flying, flying):
-            if stage == 1:
-                left = total_of(left, left_moved)
-                right = total_of(right, right_moved)
-                left_sends, right_sends = stage_sends(left, "x", 0), stage_sends(right, "y", 0)
-                left = pick(left, lax.axis_index("x"), 0)
-                right = pick(right, lax.axis_index("y"), 0)
-                moves.append((name, 2, left, left_sends, right, right_sends))
-            elif stage == 2:
-                left = total_of(left, left_moved)
-                right = total_of(right, right_moved)
-                sends = [
-                    jnp.concatenate(pair, axis=0)
-                    for pair in zip(stage_sends(left, "z", 0), stage_sends(right, "z", 0))
-                ]
-                here = lax.axis_index("z")
-                own = jnp.concatenate([pick(left, here, 0), pick(right, here, 0)], axis=0)
-                moves.append((name, 3, own, sends, own[:0], []))
-            else:
-                total = left.astype(jnp.float32)
-                for part in left_moved:
-                    total = total + part.astype(jnp.float32)
-                self.results[name] = total
-        for name, kept, moved in entering:
-            left, left_sends, right, right_sends = split_sums(kept, moved)
-            moves.append((name, 1, left, left_sends, right, right_sends))
+        for name, route, kept, moved in ready:
+            if not route:
+                self.results[name] = kept.astype(jnp.float32) + sum(
+                    part.astype(jnp.float32) for part in moved
+                )
+                continue
+            total = total_of(kept, moved)
+            sends = stage_sends(total, route[0], 0)
+            moves.append((name, route, pick(total, lax.axis_index(route[0]), 0), sends))
         arrays, values = tied([item[2:] for item in moves], values)
-        self.flying = []
-        for (name, stage, *_), (left, left_sends, right, right_sends) in zip(moves, arrays):
-            first, second = {1: ("y", "x"), 2: ("x", "y"), 3: ("z", "z")}[stage]
-            left_moved = stage_moves(left_sends, first)
-            right_moved = stage_moves(right_sends, second)
-            self.flying.append((name, stage, left, left_moved, right, right_moved))
+        self.flying = [
+            (name, route[1:], kept, stage_moves(sends, route[0]))
+            for (name, route, *_), (kept, sends) in zip(moves, arrays)
+        ]
         return values
 
 
@@ -756,28 +775,23 @@
     return lax.all_gather(local_rows, DEVICES, axis=0, tiled=True)
 
 
-def share_keys(projected, gate_low):
-    parts = [projected[:, INNER:]]
-    if gate_low is not None:
-        parts.append(jnp.broadcast_to(gate_low[:, None], (gate_low.shape[0], BLOCK)))
-    return with_neighbours(jnp.concatenate(parts, axis=1))
-
-
-def layer_forward(stream, gathered, gain_one, gain_two, gate_low, context):
+def layer_forward(stream, gathered, gain_one, gain_two, gate_low, context, early):
+    tokens = stream.shape[0]
     normed, inverse_one = rms_forward(stream, gain_one)
     normed_low = normed.astype(jnp.bfloat16)
-    projected = times_rows(normed_low, gathered[: 3 * INNER]).astype(jnp.bfloat16)
-    queries = projected[:, :INNER]
-    shared = share_keys(projected, gate_low)
+    if early is None:
+        projected = times_rows(normed_low, gathered[: 3 * INNER]).astype(jnp.bfloat16)
+        queries = projected[:, :INNER]
+        wide_gate = jnp.broadcast_to(gate_low[:, None], (tokens, BLOCK))
+        shared = with_neighbours(jnp.concatenate([projected[:, INNER:], wide_gate], axis=1))
+    else:
+        queries = times_rows(normed_low, gathered[:INNER]).astype(jnp.bfloat16)
+        shared = times_rows(early, gathered[INNER : 3 * INNER]).astype(jnp.bfloat16)
     attended, log_total = attend_forward(queries, shared, context)
     middle = stream + times_plain(attended, gathered[3 * INNER : 4 * INNER])
     normed_two, inverse_two = rms_forward(middle, gain_two)
     normed_two_low = normed_two.astype(jnp.bfloat16)
-    up_both = times_rows(normed_two_low, gathered[4 * INNER : 4 * INNER + 2 * FF])
-    up_gelu = up_both[:, :FF]
-    up_linear = up_both[:, FF:]
-    hidden = (gelu_tanh(up_gelu) * up_linear).astype(jnp.bfloat16)
-    result = middle + times_plain(hidden, gathered[4 * INNER + 2 * FF :])
+    result, up_gelu, up_linear = ffn_forward(normed_two_low, middle, gathered)
     kept = (
         stream,
         inverse_one,
@@ -791,14 +805,11 @@
         normed_two_low,
         up_gelu,
         up_linear,
-        hidden,
     )
     return (result, kept)
 
 
-def layer_backward(
-    grad_out, kept, gathered, gain_one, gain_two, context, waiting, scatter, name, before_tiles
-):
+def layer_backward(grad_out, kept, gathered, gain_one, gain_two, context, waiting, scatter, name):
     (
         stream,
         inverse_one,
@@ -812,30 +823,19 @@
         normed_two_low,
         up_gelu,
         up_linear,
-        hidden,
     ) = kept
-    w_down = gathered[4 * INNER + 2 * FF :]
     branch_low = grad_out.astype(jnp.bfloat16)
-    grad_hidden = times_rows(branch_low, w_down)
-    activated, gelu_pullback = jax.vjp(gelu_tanh, up_gelu)
-    grad_gelu = gelu_pullback(grad_hidden * up_linear)[0]
-    grad_ffn_low = jnp.concatenate([grad_gelu, grad_hidden * activated], axis=1).astype(
-        jnp.bfloat16
-    )
-    if before_tiles:
-        grad_ffn_low, branch_low = scatter.step((grad_ffn_low, branch_low))
-    sent = grad_tiles(0, grad_ffn_low, hidden, normed_two_low, branch_low, waiting)
+    grad_normed_two, own, sent = ffn_backward(
+        branch_low, normed_two_low, up_gelu, up_linear, gathered, waiting
+    )
     moved = [shift(part, "c", 1) for part in sent]
-    grad_ffn_low, branch_low, sent = lax.optimization_barrier((grad_ffn_low, branch_low, sent))
-    own = grad_tiles(1, grad_ffn_low, hidden, normed_two_low, branch_low, waiting)
-    for k in range(4):
-        scatter.push((name, k), own[k], moved[k])
-    grad_ffn_low, grad_out = scatter.step((grad_ffn_low, grad_out))
-    grad_normed_two = times_plain(grad_ffn_low, gathered[4 * INNER : 4 * INNER + 2 * FF])
+    grad_normed_two, own = lax.optimization_barrier((grad_normed_two, own))
     grad_middle, grad_gain_two = rms_backward(middle, inverse_two, gain_two, grad_normed_two)
     grad_middle = grad_out + grad_middle
     middle_low = grad_middle.astype(jnp.bfloat16)
     grad_mixed = times_rows(middle_low, gathered[3 * INNER : 4 * INNER]).astype(jnp.bfloat16)
+    for k in range(4):
+        scatter.push((name, k), ("y", "x", "z") if k % 2 == 0 else ("x", "y", "z"), own[k], moved[k])
     grad_mixed, grad_middle, middle_low = scatter.step((grad_mixed, grad_middle, middle_low))
     grad_query, grad_shared, grad_table = attend_backward(
         queries, grad_mixed, shared, log_total, context
@@ -846,37 +846,48 @@
     grad_input_low = jnp.concatenate(
         [grad_query, grad_own[:, : 2 * INNER].astype(jnp.bfloat16)], axis=1
     )
+    grad_input_low, grad_gate = scatter.step((grad_input_low, grad_gate))
     grad_normed = times_plain(grad_input_low, gathered[: 3 * INNER])
     grad_stream, grad_gain_one = rms_backward(stream, inverse_one, gain_one, grad_normed)
     grad_stream = grad_middle + grad_stream
-    attention = [
-        jnp.pad(grad_input_low, ((0, 0), (0, INNER))),
-        jnp.pad(attended, ((0, 0), (3 * INNER, 0))),
-        normed_low,
-        middle_low,
-    ]
-    grad_stream, attention = scatter.step((grad_stream, attention))
     return (
         grad_stream,
         grad_table,
         grad_gate,
         grad_gain_one,
         grad_gain_two,
-        attention,
-    )
+        (grad_input_low, attended, normed_low, middle_low),
+    )
+
+
+def padded_attention(attention):
+    grad_input_low, attended, normed_low, middle_low = attention
+    return [
+        jnp.pad(grad_input_low, ((0, 0), (0, INNER))),
+        jnp.pad(attended, ((0, 0), (3 * INNER, 0))),
+        normed_low,
+        middle_low,
+    ]
 
 
 def push_last_attention(attention, scatter):
-    first, second, first_side, second_side = attention
-    rows = outer_sum(first, first_side) + outer_sum(second, second_side)
+    grad_input_low, attended, normed_low, middle_low = attention
     size_y, size_x, size_z = (lax.axis_size(axis) for axis in ("y", "x", "z"))
     core = lax.axis_index("c")
-    width = rows.shape[1]
+    width = normed_low.shape[1]
     owners, part = owner_parts()
-    rows = rows.astype(jnp.bfloat16).reshape(owners, size_z, size_y, size_x, 2, -1, width)
-    rows = rows.transpose(2, 3, 4, 1, 0, 5, 6).reshape(size_y, size_x, 2, size_z, part, width)
-    kept, sent = pick(rows, core, 2), pick(rows, 1 - core, 2)
-    scatter.push("late", kept, shift(sent, "c", 1))
+    rows = jnp.concatenate(
+        [
+            outer_sum(grad_input_low, normed_low).astype(jnp.bfloat16),
+            outer_sum(attended, middle_low).astype(jnp.bfloat16),
+        ],
+        axis=0,
+    )
+    rows = rows.reshape(owners, size_z, size_y, size_x, 2, -1, width)
+    rows = rows.transpose(4, 2, 3, 1, 0, 5, 6).reshape(2, -1, width)
+    kept, sent = pick(rows, core, 0), pick(rows, 1 - core, 0)
+    moved = shift(sent, "c", 1)
+    scatter.push("late", ("y", "x", "z"), kept, moved)
 
 
 def owner_parts():
@@ -911,9 +922,10 @@
     first_pos = lax.axis_index("z") * tokens_here
     context = attention_context(segment_ids[0], first_pos, tokens_here, rel_bias)
     stream = inputs.reshape(tokens_here, width)
+    early = with_neighbours(rms_forward(stream, norm_gains[0])[0].astype(jnp.bfloat16))
     gathered_three = fetch_rows(layer3_rows)
     after_three, kept_three = layer_forward(
-        stream, gathered_three, norm_gains[0], norm_gains[1], None, context
+        stream, gathered_three, norm_gains[0], norm_gains[1], None, context, early
     )
     gate_inverse = lax.rsqrt(jnp.mean(after_three * after_three, axis=1, keepdims=True) + epsilon)
     gate_normed = after_three * gate_inverse
@@ -923,7 +935,7 @@
     gate_low = gate_mask.astype(jnp.bfloat16)
     gathered_four = fetch_rows(layer4_rows)
     after_four, kept_four = layer_forward(
-        after_three, gathered_four, norm_gains[2], norm_gains[3], gate_low, context
+        after_three, gathered_four, norm_gains[2], norm_gains[3], gate_low, context, None
     )
     scatter = Scatter()
     grad_three_out, table_four, grad_gate, gain_four_one, gain_four_two, attention_four = (
@@ -937,13 +949,12 @@
             None,
             scatter,
             "four",
-            False,
         )
     )
     grad_logit = grad_gate[:, 0] * gate_scale * sigmoid_value * (1.0 - sigmoid_value)
     grad_gate_weight = jnp.sum(grad_logit[:, None] * gate_normed, axis=0)
     gate_stream = stream_backward(after_three, gate_inverse, grad_logit[:, None] * gate_weight)
-    grad_three_out = grad_three_out + gate_stream
+    grad_three_out = scatter.step(grad_three_out + gate_stream)
     grad_input, table_three, unused, gain_three_one, gain_three_two, attention_three = (
         layer_backward(
             grad_three_out,
@@ -952,10 +963,9 @@
             norm_gains[0],
             norm_gains[1],
             context,
-            attention_four,
+            padded_attention(attention_four),
             scatter,
             "three",
-            True,
         )
     )
     push_last_attention(attention_three, scatter)
@@ -964,11 +974,11 @@
     owner = (
         (lax.axis_index("y") * lax.axis_size("x") + lax.axis_index("x")) * lax.axis_size("c")
     ) + lax.axis_index("c")
-    late = bring_to_owners(scatter.results["late"]).astype(jnp.float32)
+    late = bring_to_owners(scatter.results["late"].reshape(-1, width)).astype(jnp.float32)
     owners = late.shape[0]
     mine = pick(late, jnp.minimum(owner, owners - 1), 0)
     local_four, local_three = (
-        jnp.concatenate([scatter.results[name, k] for k in range(4)], axis=1)[:, :width]
+        jnp.concatenate([scatter.results[name, k].reshape(-1, CHUNK) for k in range(4)], axis=1)[:, :width]
         for name in ("four", "three")
     )
     local_four = jnp.where(owner < owners, local_three, local_four)

time: 1450 us -> 1430 us (0.986)
  matrix products: 183 us -> 41.6 us
  waiting for transfers between devices: 564 us -> 695 us
  starting transfers between devices: 174 us -> 137 us
  local copies, waits for them, and re-layouts: 122 us -> 142 us
    ppermute x16, waiting for transfers between devices: 114 us -> 235 us  [slide(): return lax.ppermute(value, 'z', pairs)]
    ppermute x75 -> x57, waiting for transfers between devices: 106 us -> 174 us  [shift(): lax.ppermute(value, axis, [(i, (i + amount) % count) for i in range(count)])]
    dot_general x8 -> x5, matrix products: 88.7 us -> 21.6 us  [times_rows(): lax.dot_general(left_side, weight, (((1,), (1,)), ((), ())), preferred_el...]
    dot_general x8 -> x4, matrix products: 79.9 us -> 15.3 us  [times_plain(): return jnp.dot(left_side, weight, preferred_element_type=jnp.float32)]
    all_gather x2, waiting for transfers between devices: 318 us -> 264 us  [fetch_rows(): return lax.all_gather(local_rows, DEVICES, axis=0, tiled=True)]
    convert_element_type x36 -> x27, other arithmetic: 35.5 us -> 71.4 us  [total_of(): return total.astype(jnp.bfloat16)]
    ppermute x75 -> x57, starting transfers between devices: 107 us -> 73.7 us  [shift(): lax.ppermute(value, axis, [(i, (i + amount) % count) for i in range(count)])]
    concatenate x40 -> x3, other arithmetic: 37.4 us -> 4.63 us  [the longest x1 2.41 us: push_last_attention(): jnp.concatenate([outer_sum(grad_input_low, normed_low).astype(jnp.bfloat1...]
  transfers between devices with their start and end apart: 98 -> 80, of which waited for: 28 -> 32; matrix products, arithmetic and copies ran while one was open for 22% -> 16% of each run, Pallas kernels for 13% -> 6%
where the time goes in v3:
time: 1430 us; the launch traced here: 1420 us
  waiting for transfers between devices  695 us (49%)
  Pallas kernels  259 us (18%)
  local copies, waits for them, and re-layouts  142 us (10%)
  starting transfers between devices  137 us (10%)
  other arithmetic  127 us (9%)
  matrix products  41.6 us (3%)
  between operations  16.5 us (1%)
    all_gather x2, waiting for transfers between devices, fetch_rows(): return lax.all_gather(local_rows, DEVICES, axis=0, tiled=True)  264 us
    ppermute x16, waiting for transfers between devices, slide(): return lax.ppermute(value, 'z', pairs)  235 us
    ppermute x57, waiting for transfers between devices, shift(): lax.ppermute(value, axis, [(i, (i + amount) % count) for i in range(count)])  174 us
    pallas_call x2, Pallas kernels, ffn_backward(): pl.pallas_call(functools.partial(ffn_backward_body, attention is not None...  131 us
    ppermute x57, starting transfers between devices, shift(): lax.ppermute(value, axis, [(i, (i + amount) % count) for i in range(count)])  73.7 us
    convert_element_type x27, other arithmetic, total_of(): return total.astype(jnp.bfloat16)  71.4 us
    ppermute x16, starting transfers between devices, slide(): return lax.ppermute(value, 'z', pairs)  57 us
    pallas_call x2, Pallas kernels, ffn_forward(): pl.pallas_call(ffn_forward_body, grid=(steps,), in_specs=[resident((token...  50.5 us
  transfers between devices with their start and end apart: 80, of which 32 were waited for; matrix products, arithmetic and copies ran while one was open for 16% of the time, Pallas kernels for 6%

profile of v3, /device:TPU:24, one launch (start us, length us, event | category | flops | bytes accessed | tf_op | source)
XLA Modules:
  0.0 1418.2 jit_solution(8588415364198793140)
XLA Ops:
  21.3 5.8 collective-permute-start.2
  31.1 7.5 collective-permute-start.3
  39.4 4.7 bias_tiles.1.refs_4_.refs_5_
  44.7 120.0 %collective-permute-done = bf16[288,1472]{1,0:T(8,128)(2,1)} collective-permute-done((bf16[288,1472]{1,0:T(8,128)(2,1)}, bf16[288,1472]{1,0:T(8,128)(2,1)}, u32[]{:S(2)}, u32[]{:S(2)}) %collective-permute-start) | collective-permute-done | bytes 847904 | tf_op jit(solution)/shard_map/ppermute | solution.py:446
  180.4 105.4 %all-gather.3.cloned.1.call-done.gelu_ref.linear_ref.down_ref.refs_4_.refs_5_.refs_6_ = bf16[12288,1472]{1,0:T(8,128)(2,1)} async-done(((bf16[384,1472]{1,0:T(8,128)(2,1)}), bf16[12288,1472]{1,0:T(8,128)(2,1)}) %all-gather.3.cloned.1.call-update) | async-done | bytes 36175888 | tf_op jit(solution)/shard_map/all_gather | solution.py:775
  288.6 8.8 convolution_convert_fusion.1.refs_1_.refs_2_
  297.8 12.8 attend_forward.2
  314.9 25.5 %ffn_forward.2 = (f32[512,1472]{1,0:T(8,128)S(1)}, f32[512,3584]{1,0:T(8,128)}, f32[512,3584]{1,0:T(8,128)}) custom-call(bf16[512,1472]{1,0:T(8,128)(2,1)S(1)} %multiply_convert_fusion.2.normed_ref.refs_1_, f32[512,1472]{1,0:T(8,128)} %copy-done.29, bf16[12288,1472]{1,0:T(8,128)(2,1)} %all-gather.3.cloned.1.call-done.gelu_ref.linear_ref.down_ref.refs_4_.refs_5_.refs_6_, ...), custom_call_target="tpu_custom_call" | custom-call | flops 16206790656 | bytes 46333952 | tf_op jit(solution)/shard_map/ffn_forward/pallas_call | solution.py:552
  343.0 158.8 %all-gather.5.cloned.1.call-done.gelu_ref.linear_ref.down_ref.refs_4_.refs_5_.refs_6_ = bf16[12288,1472]{1,0:T(8,128)(2,1)} async-done(((bf16[384,1472]{1,0:T(8,128)(2,1)}), bf16[12288,1472]{1,0:T(8,128)(2,1)}) %all-gather.5.cloned.1.call-update) | async-done | bytes 36175888 | tf_op jit(solution)/shard_map/all_gather | solution.py:775
  501.8 4.7 fusion.19
  510.4 3.5 copy.163
  514.0 4.6 collective-permute-start.6
  524.3 5.5 collective-permute-start.7
  529.8 27.0 %collective-permute-done.4 = bf16[288,896]{1,0:T(8,128)(2,1)S(1)} collective-permute-done((bf16[288,896]{1,0:T(8,128)(2,1)S(1)}, bf16[288,896]{1,0:T(8,128)(2,1)S(1)}, u32[]{:S(2)}, u32[]{:S(2)}) %collective-permute-start.4) | collective-permute-done | bytes 516128 | tf_op jit(solution)/shard_map/ppermute | solution.py:446
  560.1 12.9 attend_forward.3
  577.2 25.0 %ffn_forward.3 = (f32[512,1472]{1,0:T(8,128)S(1)}, f32[512,3584]{1,0:T(8,128)}, f32[512,3584]{1,0:T(8,128)}) custom-call(bf16[512,1472]{1,0:T(8,128)(2,1)S(1)} %multiply_convert_fusion.normed_ref.refs_1_, f32[512,1472]{1,0:T(8,128)} %copy-done.31, bf16[12288,1472]{1,0:T(8,128)(2,1)} %all-gather.5.cloned.1.call-done.gelu_ref.linear_ref.down_ref.refs_4_.refs_5_.refs_6_, ...), custom_call_target="tpu_custom_call" | custom-call | flops 16206790656 | bytes 46333952 | tf_op jit(solution)/shard_map/ffn_forward/pallas_call | solution.py:552
  602.2 61.7 %ffn_backward.2 = (f32[512,1472]{1,0:T(8,128)}, bf16[6144,384]{1,0:T(8,128)(2,1)}, bf16[6144,384]{1,0:T(8,128)(2,1)}, bf16[6144,384]{1,0:T(8,128)(2,1)}, bf16[61...) custom-call(s32[4]{0:T(128)S(1)} %pad_add_fusion.core_ref, ...), custom_call_target="tpu_custom_call" | custom-call | flops 32413581312 | bytes 77987840 | tf_op jit(solution)/shard_map/ffn_backward/pallas_call | solution.py:704
  663.9 10.1 collective-permute-start.8
  674.6 4.5 multiply_reduce_fusion.1
  679.1 4.4 fusion.36
  686.6 5.0 add_convert_fusion.7
  694.4 3.7 add_convert_fusion.6
  702.1 5.8 add_convert_fusion.5
  707.9 24.1 %attend_backward.2 = (bf16[512,384]{1,0:T(8,128)(2,1)S(1)}, bf16[2304,896]{1,0:T(8,128)(2,1)}, f32[3,32,256]{2,1,0:T(8,128)S(1)}) custom-call(s32[4]{0:T(128)S(1)} %get-tuple-element.641.low_ref, s32[4]{0:T(128)S(1)} %get-tuple-element.640.high_ref, bf16[512,384]{1,0:T(8,128)(2,1)S(1)} %slice.177.refs_0_, ...), custom_call_target="tpu_custom_call" | custom-call | flops 4529848320 | bytes 12582912 | tf_op jit(solution)/shard_map/attend_backward/pallas_call | solution.py:346
  735.3 5.1 dynamic-slice_bitcast_fusion.10
  740.4 5.0 add_convert_fusion.4
  748.1 7.0 collective-permute-done.10
  772.3 13.3 collective-permute-start.20
  785.6 36.0 %collective-permute-done.21 = bf16[288,896]{1,0:T(8,128)(2,1)S(1)} collective-permute-done((bf16[288,896]{1,0:T(8,128)(2,1)S(1)}, bf16[288,896]{1,0:T(8,128)(2,1)S(1)}, u32[]{:S(2)}, u32[]{:S(2)}) %collective-permute-start.21) | collective-permute-done | bytes 516128 | tf_op jit(solution)/shard_map/ppermute | solution.py:446
  829.6 9.6 collective-permute-done.18
  842.9 5.1 collective-permute-done.14
  862.0 3.5 collective-permute-start.23
  868.6 5.3 multiply_reduce_fusion.2
  873.9 4.1 collective-permute-start.25
  878.0 23.9 %collective-permute-done.23 = bf16[384,384]{1,0:T(8,128)(2,1)S(1)} collective-permute-done((bf16[384,384]{1,0:T(8,128)(2,1)S(1)}, bf16[384,384]{1,0:T(8,128)(2,1)S(1)}, u32[]{:S(2)}, u32[]{:S(2)}) %collective-permute-start.23) | collective-permute-done | bytes 294944 | tf_op jit(solution)/shard_map/ppermute | solution.py:440
  904.9 9.6 collective-permute-done.26
  917.1 69.5 %ffn_backward.3 = (f32[512,1472]{1,0:T(8,128)}, bf16[6144,384]{1,0:T(8,128)(2,1)}, bf16[6144,384]{1,0:T(8,128)(2,1)}, bf16[6144,384]{1,0:T(8,128)(2,1)}, bf16[61...) custom-call(s32[4]{0:T(128)S(1)} %pad_add_fusion.core_ref, ...), custom_call_target="tpu_custom_call" | custom-call | flops 32413581312 | bytes 77987840 | tf_op jit(solution)/shard_map/ffn_backward/pallas_call | solution.py:704
  992.0 5.4 collective-permute-done.32
  998.9 14.6 %collective-permute-done.33 = bf16[384,384]{1,0:T(8,128)(2,1)S(1)} collective-permute-done((bf16[384,384]{1,0:T(8,128)(2,1)S(1)}, bf16[384,384]{1,0:T(8,128)(2,1)S(1)}, u32[]{:S(2)}, u32[]{:S(2)}) %collective-permute-start.33) | collective-permute-done | bytes 294944 | tf_op jit(solution)/shard_map/ppermute | solution.py:440
  1016.1 6.6 collective-permute-start.36
  1025.8 16.7 %collective-permute-done.36 = bf16[384,384]{1,0:T(8,128)(2,1)S(1)} collective-permute-done((bf16[384,384]{1,0:T(8,128)(2,1)S(1)}, bf16[384,384]{1,0:T(8,128)(2,1)S(1)}, u32[]{:S(2)}, u32[]{:S(2)}) %collective-permute-start.36) | collective-permute-done | bytes 294944 | tf_op jit(solution)/shard_map/ppermute | solution.py:440
  1043.3 5.0 add_convert_fusion.3
  1051.2 3.7 add_convert_fusion.2
  1061.4 5.9 add_convert_fusion.1
  1067.4 22.5 %attend_backward.3 = (bf16[512,384]{1,0:T(8,128)(2,1)S(1)}, bf16[2304,768]{1,0:T(8,128)(2,1)}, f32[3,32,256]{2,1,0:T(8,128)S(1)}) custom-call(s32[4]{0:T(128)S(1)} %get-tuple-element.641.low_ref, s32[4]{0:T(128)S(1)} %get-tuple-element.640.high_ref, bf16[512,384]{1,0:T(8,128)(2,1)S(1)} %copy-done.19, bf16[512,384]{1,0:T(8,128)(2,1)S(1)} %convolution_convert_fusion.3.refs_1_, ...), custom_call_target="tpu_custom_call" | custom-call | flops 4529848320 | bytes 12582912 | tf_op jit(solution)/shard_map/attend_backward/pallas_call | solution.py:346
  1090.2 4.4 dynamic-slice_bitcast_fusion.2
  1094.7 5.0 add_convert_fusion
  1102.4 10.4 collective-permute-done.38
  1128.7 5.5 collective-permute-start.48
  1134.2 32.0 %collective-permute-done.49 = bf16[288,768]{1,0:T(8,128)(2,1)S(1)} collective-permute-done((bf16[288,768]{1,0:T(8,128)(2,1)S(1)}, bf16[288,768]{1,0:T(8,128)(2,1)S(1)}, u32[]{:S(2)}, u32[]{:S(2)}) %collective-permute-start.49) | collective-permute-done | bytes 442400 | tf_op jit(solution)/shard_map/ppermute | solution.py:446
  1174.3 9.9 collective-permute-done.46
  1186.2 16.6 %collective-permute-done.42 = bf16[4,384,384]{2,1,0:T(8,128)(2,1)} collective-permute-done((bf16[4,384,384]{2,1,0:T(8,128)(2,1)}, bf16[4,384,384]{2,1,0:T(8,128)(2,1)}, u32[]{:S(2)}, u32[]{:S(2)}) %collective-permute-start.42) | collective-permute-done | bytes 1179680 | tf_op jit(solution)/shard_map/ppermute | solution.py:440
  1228.7 6.6 copy.171
  1240.4 4.4 copy.173
  1245.9 5.0 fusion.14
  1255.8 17.5 %collective-permute-done.54 = bf16[384,384]{1,0:T(8,128)(2,1)S(1)} collective-permute-done((bf16[384,384]{1,0:T(8,128)(2,1)S(1)}, bf16[384,384]{1,0:T(8,128)(2,1)S(1)}, u32[]{:S(2)}, u32[]{:S(2)}) %collective-permute-start.54) | collective-permute-done | bytes 294944 | tf_op jit(solution)/shard_map/ppermute | solution.py:440
  1277.5 4.4 copy.174
  1299.4 15.9 %collective-permute-done.75 = f32[6,1472]{1,0:T(8,128)S(1)} collective-permute-done((f32[6,1472]{1,0:T(8,128)S(1)}, f32[6,1472]{1,0:T(8,128)S(1)}, u32[]{:S(2)}, u32[]{:S(2)}) %collective-permute-start.75) | collective-permute-done | bytes 35360 | tf_op jit(solution)/shard_map/ppermute | solution.py:498
  1325.9 14.9 %collective-permute-done.63 = bf16[384,384]{1,0:T(8,128)(2,1)S(1)} collective-permute-done((bf16[384,384]{1,0:T(8,128)(2,1)}, bf16[384,384]{1,0:T(8,128)(2,1)S(1)}, u32[]{:S(2)}, u32[]{:S(2)}) %collective-permute-start.63) | collective-permute-done | bytes 294944 | tf_op jit(solution)/shard_map/ppermute | solution.py:440
  1353.1 4.2 collective-permute-done.66
  1357.6 4.4 collective-permute-start.68
  1365.9 8.7 collective-permute-done.68
  1380.1 6.3 collective-permute-done.71
  1395.5 6.8 collective-permute-done.72
  (627 shorter events, 289.6 us)
Async XLA Ops:
  7.2 278.6 %all-gather.3.cloned.1.call-start = ((), (), s32[]{:S(2)}) async-start(), calls=%async_computation | async-start | bytes 38928384 | tf_op jit(solution)/shard_map/all_gather | solution.py:775
  9.7 492.1 %all-gather.5.cloned.1.call-start = ((), (), s32[]{:S(2)}) async-start(), calls=%async_computation.1 | async-start | bytes 38928384 | tf_op jit(solution)/shard_map/all_gather | solution.py:775
  19.9 147.1 %collective-permute-start.1 = (bf16[512,1472]{0,1:T(8,128)(2,1)}, bf16[512,1472]{0,1:T(8,128)(2,1)}, u32[]{:S(2)}, u32[]{:S(2)}) collective-permute-start(bf16[512,1472]{0,1:T(8,128)(2,1)} %copy.155), channel_id=1, source_target_pairs={{0,1},{1,2},{2,3},{4,5},{5,6},{6,7},{8,9},{9,10},{10,11},{12,13},{... | collective-permute-start | bytes 4521992 | tf_op jit(solution)/shard_map/ppermute | solution.py:446
  21.3 148.3 %collective-permute-start.2 = (bf16[512,1472]{0,1:T(8,128)(2,1)}, bf16[512,1472]{0,1:T(8,128)(2,1)}, u32[]{:S(2)}, u32[]{:S(2)}) collective-permute-start(bf16[512,1472]{0,1:T(8,128)(2,1)} %copy.155), channel_id=1, source_target_pairs={{1,0},{2,1},{3,2},{5,4},{6,5},{7,6},{9,8},{10,9},{11,10},{13,12},{... | collective-permute-start | bytes 4521992 | tf_op jit(solution)/shard_map/ppermute | solution.py:446
  29.9 134.9 %collective-permute-start = (bf16[288,1472]{1,0:T(8,128)(2,1)}, bf16[288,1472]{1,0:T(8,128)(2,1)}, u32[]{:S(2)}, u32[]{:S(2)}) collective-permute-start(bf16[288,1472]{1,0:T(8,128)(2,1)} %get-tuple-element.585), channel_id=1, source_target_pairs={{0,2},{1,3},{4,6},{5,7},{8,10},{9,11},{12,14},{13,15},{16,18},{17,... | collective-permute-start | bytes 2543624 | tf_op jit(solution)/shard_map/ppermute | solution.py:446
  31.1 146.7 %collective-permute-start.3 = (bf16[288,1472]{1,0:T(8,128)(2,1)}, bf16[288,1472]{1,0:T(8,128)(2,1)}, u32[]{:S(2)}, u32[]{:S(2)}) collective-permute-start(bf16[288,1472]{1,0:T(8,128)(2,1)} %get-tuple-element.584), channel_id=1, source_target_pairs={{2,0},{3,1},{6,4},{7,5},{10,8},{11,9},{14,12},{15,13},{18,16},{19,... | collective-permute-start | bytes 2543624 | tf_op jit(solution)/shard_map/ppermute | solution.py:446
  509.1 47.8 %collective-permute-start.5 = (bf16[512,896]{1,0:T(8,128)(2,1)}, bf16[512,896]{1,0:T(8,128)(2,1)}, u32[]{:S(2)}, u32[]{:S(2)}) collective-permute-start(bf16[512,896]{1,0:T(8,128)(2,1)} %pad_maximum_fusion.7), channel_id=1, source_target_pairs={{0,1},{1,2},{2,3},{4,5},{5,6},{6,7},{8,9},{9,10},{10,11},{12,13},{... | collective-permute-start | bytes 2752520 | tf_op jit(solution)/shard_map/ppermute | solution.py:446
  514.0 44.4 %collective-permute-start.6 = (bf16[512,896]{1,0:T(8,128)(2,1)}, bf16[512,896]{1,0:T(8,128)(2,1)S(1)}, u32[]{:S(2)}, u32[]{:S(2)}) collective-permute-start(bf16[512,896]{1,0:T(8,128)(2,1)} %pad_maximum_fusion.7), channel_id=1, source_target_pairs={{1,0},{2,1},{3,2},{5,4},{6,5},{7,6},{9,8},{10,9},{11,10},{13,12},{... | collective-permute-start | bytes 2752520 | tf_op jit(solution)/shard_map/ppermute | solution.py:446
  519.8 37.0 %collective-permute-start.4 = (bf16[288,896]{1,0:T(8,128)(2,1)S(1)}, bf16[288,896]{1,0:T(8,128)(2,1)S(1)}, u32[]{:S(2)}, u32[]{:S(2)}) collective-permute-start(bf16[288,896]{1,0:T(8,128)(2,1)S(1)} %get-tuple-element.621), channel_id=1, source_target_pairs={{0,2},{1,3},{4,6},{5,7},{8,10},{9,11},{12,14},{13,15},{16,18},{17,... | collective-permute-start | bytes 1548296 | tf_op jit(solution)/shard_map/ppermute | solution.py:446
  524.3 34.2 %collective-permute-start.7 = (bf16[288,896]{1,0:T(8,128)(2,1)S(1)}, bf16[288,896]{1,0:T(8,128)(2,1)S(1)}, u32[]{:S(2)}, u32[]{:S(2)}) collective-permute-start(bf16[288,896]{1,0:T(8,128)(2,1)S(1)} %get-tuple-element.620), channel_id=1, source_target_pairs={{2,0},{3,1},{6,4},{7,5},{10,8},{11,9},{14,12},{15,13},{18,16},{19,... | collective-permute-start | bytes 1548296 | tf_op jit(solution)/shard_map/ppermute | solution.py:446
  663.9 22.7 %collective-permute-start.8 = (bf16[6144,384]{1,0:T(8,128)(2,1)}, bf16[6144,384]{1,0:T(8,128)(2,1)}, u32[]{:S(2)}, u32[]{:S(2)}) collective-permute-start(bf16[6144,384]{1,0:T(8,128)(2,1)} %get-tuple-element.247), channel_id=1, source_target_pairs={{0,4},{4,0},{1,5},{5,1},{2,6},{6,2},{3,7},{7,3},{8,12},{12,8},{9,1... | collective-permute-start | bytes 14155784 | tf_op jit(solution)/shard_map/ppermute | solution.py:440
  674.0 20.4 %collective-permute-start.9 = (bf16[6144,384]{1,0:T(8,128)(2,1)}, bf16[6144,384]{1,0:T(8,128)(2,1)}, u32[]{:S(2)}, u32[]{:S(2)}) collective-permute-start(bf16[6144,384]{1,0:T(8,128)(2,1)} %get-tuple-element.249), channel_id=1, source_target_pairs={{0,4},{4,0},{1,5},{5,1},{2,6},{6,2},{3,7},{7,3},{8,12},{12,8},{9,1... | collective-permute-start | bytes 14155784 | tf_op jit(solution)/shard_map/ppermute | solution.py:440
  674.1 27.2 %collective-permute-start.12 = (bf16[6144,384]{1,0:T(8,128)(2,1)}, bf16[6144,384]{1,0:T(8,128)(2,1)}, u32[]{:S(2)}, u32[]{:S(2)}) collective-permute-start(bf16[6144,384]{1,0:T(8,128)(2,1)} %get-tuple-element.268), channel_id=1, source_target_pairs={{0,4},{4,0},{1,5},{5,1},{2,6},{6,2},{3,7},{7,3},{8,12},{12,8},{9,1... | collective-permute-start | bytes 14155784 | tf_op jit(solution)/shard_map/ppermute | solution.py:440
  686.4 54.0 %collective-permute-start.13 = (bf16[6144,384]{1,0:T(8,128)(2,1)}, bf16[6144,384]{1,0:T(8,128)(2,1)}, u32[]{:S(2)}, u32[]{:S(2)}) collective-permute-start(bf16[6144,384]{1,0:T(8,128)(2,1)} %get-tuple-element.270), channel_id=1, source_target_pairs={{0,4},{4,0},{1,5},{5,1},{2,6},{6,2},{3,7},{7,3},{8,12},{12,8},{9,1... | collective-permute-start | bytes 14155784 | tf_op jit(solution)/shard_map/ppermute | solution.py:440
  701.2 53.9 %collective-permute-start.10 = (bf16[2,4,384,384]{3,2,1,0:T(8,128)(2,1)}, bf16[2,4,384,384]{3,2,1,0:T(8,128)(2,1)}, u32[]{:S(2)}, u32[]{:S(2)}) collective-permute-start(bf16[2,4,384,384]{3,2,1,0:T(8,128)(2,1)} %get-tuple-element.255), channel_id=1, source_target_pairs={{0,16},{16,0},{1,17},{17,1},{2,18},{18,2},{3,19},{19,3},{4,20},{20... | collective-permute-start | bytes 7077896 | tf_op jit(solution)/shard_map/ppermute | solution.py:440
  701.2 54.0 %collective-permute-start.11 = (bf16[2,4,384,384]{3,2,1,0:T(8,128)(2,1)}, bf16[2,4,384,384]{3,2,1,0:T(8,128)(2,1)}, u32[]{:S(2)}, u32[]{:S(2)}) collective-permute-start(bf16[2,4,384,384]{3,2,1,0:T(8,128)(2,1)} %get-tuple-element.257), channel_id=1, source_target_pairs={{0,8},{8,0},{1,9},{9,1},{2,10},{10,2},{3,11},{11,3},{4,12},{12,4},... | collective-permute-start | bytes 7077896 | tf_op jit(solution)/shard_map/ppermute | solution.py:440
  764.1 86.1 %collective-permute-start.16 = (bf16[2,4,384,384]{3,2,1,0:T(8,128)(2,1)}, bf16[2,4,384,384]{3,2,1,0:T(8,128)(2,1)}, u32[]{:S(2)}, u32[]{:S(2)}) collective-permute-start(bf16[2,4,384,384]{3,2,1,0:T(8,128)(2,1)} %get-tuple-element.279), channel_id=1, source_target_pairs={{0,16},{16,0},{1,17},{17,1},{2,18},{18,2},{3,19},{19,3},{4,20},{20... | collective-permute-start | bytes 7077896 | tf_op jit(solution)/shard_map/ppermute | solution.py:440
  765.7 84.4 %collective-permute-start.17 = (bf16[2,4,384,384]{3,2,1,0:T(8,128)(2,1)}, bf16[2,4,384,384]{3,2,1,0:T(8,128)(2,1)}, u32[]{:S(2)}, u32[]{:S(2)}) collective-permute-start(bf16[2,4,384,384]{3,2,1,0:T(8,128)(2,1)} %get-tuple-element.281), channel_id=1, source_target_pairs={{0,8},{8,0},{1,9},{9,1},{2,10},{10,2},{3,11},{11,3},{4,12},{12,4},... | collective-permute-start | bytes 7077896 | tf_op jit(solution)/shard_map/ppermute | solution.py:440
  769.6 55.4 %collective-permute-start.19 = (bf16[512,896]{1,0:T(8,128)(2,1)S(1)}, bf16[512,896]{1,0:T(8,128)(2,1)S(1)}, u32[]{:S(2)}, u32[]{:S(2)}) collective-permute-start(bf16[512,896]{1,0:T(8,128)(2,1)S(1)} %get-tuple-element.557), channel_id=1, source_target_pairs={{0,1},{1,2},{2,3},{4,5},{5,6},{6,7},{8,9},{9,10},{10,11},{12,13},{... | collective-permute-start | bytes 2752520 | tf_op jit(solution)/shard_map/ppermute | solution.py:446
  771.0 50.6 %collective-permute-start.21 = (bf16[288,896]{1,0:T(8,128)(2,1)S(1)}, bf16[288,896]{1,0:T(8,128)(2,1)S(1)}, u32[]{:S(2)}, u32[]{:S(2)}) collective-permute-start(bf16[288,896]{1,0:T(8,128)(2,1)S(1)} %get-tuple-element.555), channel_id=1, source_target_pairs={{0,2},{1,3},{4,6},{5,7},{8,10},{9,11},{12,14},{13,15},{16,18},{17,... | collective-permute-start | bytes 1548296 | tf_op jit(solution)/shard_map/ppermute | solution.py:446
  772.3 51.5 %collective-permute-start.20 = (bf16[288,896]{1,0:T(8,128)(2,1)S(1)}, bf16[288,896]{1,0:T(8,128)(2,1)S(1)}, u32[]{:S(2)}, u32[]{:S(2)}) collective-permute-start(bf16[288,896]{1,0:T(8,128)(2,1)S(1)} %get-tuple-element.554), channel_id=1, source_target_pairs={{2,0},{3,1},{6,4},{7,5},{10,8},{11,9},{14,12},{15,13},{18,16},{19,... | collective-permute-start | bytes 1548296 | tf_op jit(solution)/shard_map/ppermute | solution.py:446
  823.8 24.3 %collective-permute-start.14 = (bf16[4,384,384]{2,1,0:T(8,128)(2,1)}, bf16[4,384,384]{2,1,0:T(8,128)(2,1)}, u32[]{:S(2)}, u32[]{:S(2)}) collective-permute-start(bf16[4,384,384]{2,1,0:T(8,128)(2,1)} %get-tuple-element.275), channel_id=1, source_target_pairs={{0,8},{8,0},{1,9},{9,1},{2,10},{10,2},{3,11},{11,3},{4,12},{12,4},... | collective-permute-start | bytes 3538952 | tf_op jit(solution)/shard_map/ppermute | solution.py:440
  825.9 24.3 %collective-permute-start.15 = (bf16[4,384,384]{2,1,0:T(8,128)(2,1)}, bf16[4,384,384]{2,1,0:T(8,128)(2,1)}, u32[]{:S(2)}, u32[]{:S(2)}) collective-permute-start(bf16[4,384,384]{2,1,0:T(8,128)(2,1)} %get-tuple-element.277), channel_id=1, source_target_pairs={{0,16},{16,0},{1,17},{17,1},{2,18},{18,2},{3,19},{19,3},{4,20},{20... | collective-permute-start | bytes 3538952 | tf_op jit(solution)/shard_map/ppermute | solution.py:440
  862.0 39.9 %collective-permute-start.23 = (bf16[384,384]{1,0:T(8,128)(2,1)S(1)}, bf16[384,384]{1,0:T(8,128)(2,1)S(1)}, u32[]{:S(2)}, u32[]{:S(2)}) collective-permute-start(bf16[384,384]{1,0:T(8,128)(2,1)S(1)} %get-tuple-element.296), channel_id=1, source_target_pairs={{0,2},{1,3},{2,0},{3,1},{4,6},{5,7},{6,4},{7,5},{8,10},{9,11},{10,... | collective-permute-start | bytes 884744 | tf_op jit(solution)/shard_map/ppermute | solution.py:440
  865.6 36.4 %collective-permute-start.24 = (bf16[384,384]{1,0:T(8,128)(2,1)S(1)}, bf16[384,384]{1,0:T(8,128)(2,1)S(1)}, u32[]{:S(2)}, u32[]{:S(2)}) collective-permute-start(bf16[384,384]{1,0:T(8,128)(2,1)S(1)} %get-tuple-element.297), channel_id=1, source_target_pairs={{0,3},{1,0},{2,1},{3,2},{4,7},{5,4},{6,5},{7,6},{8,11},{9,8},{10,9... | collective-permute-start | bytes 884744 | tf_op jit(solution)/shard_map/ppermute | solution.py:440
  866.3 48.3 %collective-permute-start.28 = (bf16[4,384,384]{2,1,0:T(8,128)(2,1)S(1)}, bf16[4,384,384]{2,1,0:T(8,128)(2,1)S(1)}, u32[]{:S(2)}, u32[]{:S(2)}) collective-permute-start(bf16[4,384,384]{2,1,0:T(8,128)(2,1)S(1)} %get-tuple-element.303), channel_id=1, source_target_pairs={{0,8},{8,0},{1,9},{9,1},{2,10},{10,2},{3,11},{11,3},{4,12},{12,4},... | collective-permute-start | bytes 3538952 | tf_op jit(solution)/shard_map/ppermute | solution.py:440
  868.0 46.5 %collective-permute-start.29 = (bf16[4,384,384]{2,1,0:T(8,128)(2,1)S(1)}, bf16[4,384,384]{2,1,0:T(8,128)(2,1)S(1)}, u32[]{:S(2)}, u32[]{:S(2)}) collective-permute-start(bf16[4,384,384]{2,1,0:T(8,128)(2,1)S(1)} %get-tuple-element.305), channel_id=1, source_target_pairs={{0,16},{16,0},{1,17},{17,1},{2,18},{18,2},{3,19},{19,3},{4,20},{20... | collective-permute-start | bytes 3538952 | tf_op jit(solution)/shard_map/ppermute | solution.py:440
  873.9 30.9 %collective-permute-start.25 = (bf16[384,384]{1,0:T(8,128)(2,1)S(1)}, bf16[384,384]{1,0:T(8,128)(2,1)S(1)}, u32[]{:S(2)}, u32[]{:S(2)}) collective-permute-start(bf16[384,384]{1,0:T(8,128)(2,1)S(1)} %get-tuple-element.299), channel_id=1, source_target_pairs={{0,1},{1,2},{2,3},{3,0},{4,5},{5,6},{6,7},{7,4},{8,9},{9,10},{10,1... | collective-permute-start | bytes 884744 | tf_op jit(solution)/shard_map/ppermute | solution.py:440
  986.6 56.8 %collective-permute-start.30 = (bf16[6144,384]{1,0:T(8,128)(2,1)}, bf16[6144,384]{1,0:T(8,128)(2,1)}, u32[]{:S(2)}, u32[]{:S(2)}) collective-permute-start(bf16[6144,384]{1,0:T(8,128)(2,1)} %get-tuple-element.324), channel_id=1, source_target_pairs={{0,4},{4,0},{1,5},{5,1},{2,6},{6,2},{3,7},{7,3},{8,12},{12,8},{9,1... | collective-permute-start | bytes 14155784 | tf_op jit(solution)/shard_map/ppermute | solution.py:440
  986.7 64.5 %collective-permute-start.31 = (bf16[6144,384]{1,0:T(8,128)(2,1)}, bf16[6144,384]{1,0:T(8,128)(2,1)}, u32[]{:S(2)}, u32[]{:S(2)}) collective-permute-start(bf16[6144,384]{1,0:T(8,128)(2,1)} %get-tuple-element.326), channel_id=1, source_target_pairs={{0,4},{4,0},{1,5},{5,1},{2,6},{6,2},{3,7},{7,3},{8,12},{12,8},{9,1... | collective-permute-start | bytes 14155784 | tf_op jit(solution)/shard_map/ppermute | solution.py:440
  987.2 26.3 %collective-permute-start.33 = (bf16[384,384]{1,0:T(8,128)(2,1)S(1)}, bf16[384,384]{1,0:T(8,128)(2,1)S(1)}, u32[]{:S(2)}, u32[]{:S(2)}) collective-permute-start(bf16[384,384]{1,0:T(8,128)(2,1)S(1)} %get-tuple-element.329), channel_id=1, source_target_pairs={{0,2},{1,3},{2,0},{3,1},{4,6},{5,7},{6,4},{7,5},{8,10},{9,11},{10,... | collective-permute-start | bytes 884744 | tf_op jit(solution)/shard_map/ppermute | solution.py:440
  987.2 28.9 %collective-permute-start.34 = (bf16[384,384]{1,0:T(8,128)(2,1)S(1)}, bf16[384,384]{1,0:T(8,128)(2,1)S(1)}, u32[]{:S(2)}, u32[]{:S(2)}) collective-permute-start(bf16[384,384]{1,0:T(8,128)(2,1)S(1)} %get-tuple-element.330), channel_id=1, source_target_pairs={{0,3},{1,0},{2,1},{3,2},{4,7},{5,4},{6,5},{7,6},{8,11},{9,8},{10,9... | collective-permute-start | bytes 884744 | tf_op jit(solution)/shard_map/ppermute | solution.py:440
  997.4 25.2 %collective-permute-start.35 = (bf16[384,384]{1,0:T(8,128)(2,1)S(1)}, bf16[384,384]{1,0:T(8,128)(2,1)S(1)}, u32[]{:S(2)}, u32[]{:S(2)}) collective-permute-start(bf16[384,384]{1,0:T(8,128)(2,1)S(1)} %get-tuple-element.332), channel_id=1, source_target_pairs={{0,1},{1,2},{2,3},{3,0},{4,5},{5,6},{6,7},{7,4},{8,9},{9,10},{10,1... | collective-permute-start | bytes 884744 | tf_op jit(solution)/shard_map/ppermute | solution.py:440
  1013.5 47.9 %collective-permute-start.40 = (bf16[6144,384]{1,0:T(8,128)(2,1)}, bf16[6144,384]{1,0:T(8,128)(2,1)}, u32[]{:S(2)}, u32[]{:S(2)}) collective-permute-start(bf16[6144,384]{1,0:T(8,128)(2,1)} %get-tuple-element.353), channel_id=1, source_target_pairs={{0,4},{4,0},{1,5},{5,1},{2,6},{6,2},{3,7},{7,3},{8,12},{12,8},{9,1... | collective-permute-start | bytes 14155784 | tf_op jit(solution)/shard_map/ppermute | solution.py:440
  1016.1 26.4 %collective-permute-start.36 = (bf16[384,384]{1,0:T(8,128)(2,1)S(1)}, bf16[384,384]{1,0:T(8,128)(2,1)S(1)}, u32[]{:S(2)}, u32[]{:S(2)}) collective-permute-start(bf16[384,384]{1,0:T(8,128)(2,1)S(1)} %get-tuple-element.333), channel_id=1, source_target_pairs={{0,2},{1,3},{2,0},{3,1},{4,6},{5,7},{6,4},{7,5},{8,10},{9,11},{10,... | collective-permute-start | bytes 884744 | tf_op jit(solution)/shard_map/ppermute | solution.py:440
  1022.7 19.8 %collective-permute-start.37 = (bf16[384,384]{1,0:T(8,128)(2,1)S(1)}, bf16[384,384]{1,0:T(8,128)(2,1)S(1)}, u32[]{:S(2)}, u32[]{:S(2)}) collective-permute-start(bf16[384,384]{1,0:T(8,128)(2,1)S(1)} %get-tuple-element.334), channel_id=1, source_target_pairs={{0,3},{1,0},{2,1},{3,2},{4,7},{5,4},{6,5},{7,6},{8,11},{9,8},{10,9... | collective-permute-start | bytes 884744 | tf_op jit(solution)/shard_map/ppermute | solution.py:440
  1042.5 52.2 %collective-permute-start.41 = (bf16[6144,384]{1,0:T(8,128)(2,1)}, bf16[6144,384]{1,0:T(8,128)(2,1)}, u32[]{:S(2)}, u32[]{:S(2)}) collective-permute-start(bf16[6144,384]{1,0:T(8,128)(2,1)} %get-tuple-element.355), channel_id=1, source_target_pairs={{0,4},{4,0},{1,5},{5,1},{2,6},{6,2},{3,7},{7,3},{8,12},{12,8},{9,1... | collective-permute-start | bytes 14155784 | tf_op jit(solution)/shard_map/ppermute | solution.py:440
  1058.0 54.9 %collective-permute-start.38 = (bf16[2,4,384,384]{3,2,1,0:T(8,128)(2,1)}, bf16[2,4,384,384]{3,2,1,0:T(8,128)(2,1)}, u32[]{:S(2)}, u32[]{:S(2)}) collective-permute-start(bf16[2,4,384,384]{3,2,1,0:T(8,128)(2,1)} %get-tuple-element.340), channel_id=1, source_target_pairs={{0,16},{16,0},{1,17},{17,1},{2,18},{18,2},{3,19},{19,3},{4,20},{20... | collective-permute-start | bytes 7077896 | tf_op jit(solution)/shard_map/ppermute | solution.py:440
  1060.7 53.6 %collective-permute-start.39 = (bf16[2,4,384,384]{3,2,1,0:T(8,128)(2,1)}, bf16[2,4,384,384]{3,2,1,0:T(8,128)(2,1)}, u32[]{:S(2)}, u32[]{:S(2)}) collective-permute-start(bf16[2,4,384,384]{3,2,1,0:T(8,128)(2,1)} %get-tuple-element.342), channel_id=1, source_target_pairs={{0,8},{8,0},{1,9},{9,1},{2,10},{10,2},{3,11},{11,3},{4,12},{12,4},... | collective-permute-start | bytes 7077896 | tf_op jit(solution)/shard_map/ppermute | solution.py:440
  1123.2 79.5 %collective-permute-start.44 = (bf16[2,4,384,384]{3,2,1,0:T(8,128)(2,1)}, bf16[2,4,384,384]{3,2,1,0:T(8,128)(2,1)}, u32[]{:S(2)}, u32[]{:S(2)}) collective-permute-start(bf16[2,4,384,384]{3,2,1,0:T(8,128)(2,1)} %get-tuple-element.364), channel_id=1, source_target_pairs={{0,16},{16,0},{1,17},{17,1},{2,18},{18,2},{3,19},{19,3},{4,20},{20... | collective-permute-start | bytes 7077896 | tf_op jit(solution)/shard_map/ppermute | solution.py:440
  1123.6 79.2 %collective-permute-start.45 = (bf16[2,4,384,384]{3,2,1,0:T(8,128)(2,1)}, bf16[2,4,384,384]{3,2,1,0:T(8,128)(2,1)}, u32[]{:S(2)}, u32[]{:S(2)}) collective-permute-start(bf16[2,4,384,384]{3,2,1,0:T(8,128)(2,1)} %get-tuple-element.366), channel_id=1, source_target_pairs={{0,8},{8,0},{1,9},{9,1},{2,10},{10,2},{3,11},{11,3},{4,12},{12,4},... | collective-permute-start | bytes 7077896 | tf_op jit(solution)/shard_map/ppermute | solution.py:440
  1126.0 43.8 %collective-permute-start.47 = (bf16[512,768]{1,0:T(8,128)(2,1)S(1)}, bf16[512,768]{1,0:T(8,128)(2,1)S(1)}, u32[]{:S(2)}, u32[]{:S(2)}) collective-permute-start(bf16[512,768]{1,0:T(8,128)(2,1)S(1)} %get-tuple-element.561), channel_id=1, source_target_pairs={{0,1},{1,2},{2,3},{4,5},{5,6},{6,7},{8,9},{9,10},{10,11},{12,13},{... | collective-permute-start | bytes 2359304 | tf_op jit(solution)/shard_map/ppermute | solution.py:446
  1127.4 38.8 %collective-permute-start.49 = (bf16[288,768]{1,0:T(8,128)(2,1)S(1)}, bf16[288,768]{1,0:T(8,128)(2,1)S(1)}, u32[]{:S(2)}, u32[]{:S(2)}) collective-permute-start(bf16[288,768]{1,0:T(8,128)(2,1)S(1)} %get-tuple-element.559), channel_id=1, source_target_pairs={{0,2},{1,3},{4,6},{5,7},{8,10},{9,11},{12,14},{13,15},{16,18},{17,... | collective-permute-start | bytes 1327112 | tf_op jit(solution)/shard_map/ppermute | solution.py:446
  1128.7 39.7 %collective-permute-start.48 = (bf16[288,768]{1,0:T(8,128)(2,1)S(1)}, bf16[288,768]{1,0:T(8,128)(2,1)S(1)}, u32[]{:S(2)}, u32[]{:S(2)}) collective-permute-start(bf16[288,768]{1,0:T(8,128)(2,1)S(1)} %get-tuple-element.558), channel_id=1, source_target_pairs={{2,0},{3,1},{6,4},{7,5},{10,8},{11,9},{14,12},{15,13},{18,16},{19,... | collective-permute-start | bytes 1327112 | tf_op jit(solution)/shard_map/ppermute | solution.py:446
  1166.2 18.1 %collective-permute-start.46 = (bf16[512,768]{1,0:T(8,128)(2,1)}, bf16[512,768]{1,0:T(8,128)(2,1)}, u32[]{:S(2)}, u32[]{:S(2)}) collective-permute-start(bf16[512,768]{1,0:T(8,128)(2,1)} %get-tuple-element.560), channel_id=1, source_target_pairs={{1,0},{2,1},{3,2},{5,4},{6,5},{7,6},{9,8},{10,9},{11,10},{13,12},{... | collective-permute-start | bytes 2359304 | tf_op jit(solution)/shard_map/ppermute | solution.py:446
  1168.3 34.4 %collective-permute-start.42 = (bf16[4,384,384]{2,1,0:T(8,128)(2,1)}, bf16[4,384,384]{2,1,0:T(8,128)(2,1)}, u32[]{:S(2)}, u32[]{:S(2)}) collective-permute-start(bf16[4,384,384]{2,1,0:T(8,128)(2,1)} %get-tuple-element.360), channel_id=1, source_target_pairs={{0,8},{8,0},{1,9},{9,1},{2,10},{10,2},{3,11},{11,3},{4,12},{12,4},... | collective-permute-start | bytes 3538952 | tf_op jit(solution)/shard_map/ppermute | solution.py:440
  1170.7 32.0 %collective-permute-start.43 = (bf16[4,384,384]{2,1,0:T(8,128)(2,1)}, bf16[4,384,384]{2,1,0:T(8,128)(2,1)}, u32[]{:S(2)}, u32[]{:S(2)}) collective-permute-start(bf16[4,384,384]{2,1,0:T(8,128)(2,1)} %get-tuple-element.362), channel_id=1, source_target_pairs={{0,16},{16,0},{1,17},{17,1},{2,18},{18,2},{3,19},{19,3},{4,20},{20... | collective-permute-start | bytes 3538952 | tf_op jit(solution)/shard_map/ppermute | solution.py:440
  1217.1 27.7 %collective-permute-start.50 = (bf16[384,384]{1,0:T(8,128)(2,1)}, bf16[384,384]{1,0:T(8,128)(2,1)S(1)}, u32[]{:S(2)}, u32[]{:S(2)}) collective-permute-start(bf16[384,384]{1,0:T(8,128)(2,1)} %get-tuple-element.379), channel_id=1, source_target_pairs={{0,1},{1,2},{2,3},{3,0},{4,5},{5,6},{6,7},{7,4},{8,9},{9,10},{10,1... | collective-permute-start | bytes 884744 | tf_op jit(solution)/shard_map/ppermute | solution.py:440
  1217.1 28.7 %collective-permute-start.51 = (bf16[384,384]{1,0:T(8,128)(2,1)}, bf16[384,384]{1,0:T(8,128)(2,1)}, u32[]{:S(2)}, u32[]{:S(2)}) collective-permute-start(bf16[384,384]{1,0:T(8,128)(2,1)} %get-tuple-element.380), channel_id=1, source_target_pairs={{0,2},{1,3},{2,0},{3,1},{4,6},{5,7},{6,4},{7,5},{8,10},{9,11},{10,... | collective-permute-start | bytes 884744 | tf_op jit(solution)/shard_map/ppermute | solution.py:440
  1218.6 32.3 %collective-permute-start.52 = (bf16[384,384]{1,0:T(8,128)(2,1)}, bf16[384,384]{1,0:T(8,128)(2,1)}, u32[]{:S(2)}, u32[]{:S(2)}) collective-permute-start(bf16[384,384]{1,0:T(8,128)(2,1)} %get-tuple-element.381), channel_id=1, source_target_pairs={{0,3},{1,0},{2,1},{3,2},{4,7},{5,4},{6,5},{7,6},{8,11},{9,8},{10,9... | collective-permute-start | bytes 884744 | tf_op jit(solution)/shard_map/ppermute | solution.py:440
  1220.6 32.6 %collective-permute-start.53 = (bf16[384,384]{1,0:T(8,128)(2,1)}, bf16[384,384]{1,0:T(8,128)(2,1)}, u32[]{:S(2)}, u32[]{:S(2)}) collective-permute-start(bf16[384,384]{1,0:T(8,128)(2,1)} %get-tuple-element.383), channel_id=1, source_target_pairs={{0,1},{1,2},{2,3},{3,0},{4,5},{5,6},{6,7},{7,4},{8,9},{9,10},{10,1... | collective-permute-start | bytes 884744 | tf_op jit(solution)/shard_map/ppermute | solution.py:440
  1222.6 50.6 %collective-permute-start.56 = (bf16[4,384,384]{2,1,0:T(8,128)(2,1)}, bf16[4,384,384]{2,1,0:T(8,128)(2,1)}, u32[]{:S(2)}, u32[]{:S(2)}) collective-permute-start(bf16[4,384,384]{2,1,0:T(8,128)(2,1)} %get-tuple-element.387), channel_id=1, source_target_pairs={{0,8},{8,0},{1,9},{9,1},{2,10},{10,2},{3,11},{11,3},{4,12},{12,4},... | collective-permute-start | bytes 3538952 | tf_op jit(solution)/shard_map/ppermute | solution.py:440
  1244.8 28.4 %collective-permute-start.57 = (bf16[4,384,384]{2,1,0:T(8,128)(2,1)}, bf16[4,384,384]{2,1,0:T(8,128)(2,1)S(1)}, u32[]{:S(2)}, u32[]{:S(2)}) collective-permute-start(bf16[4,384,384]{2,1,0:T(8,128)(2,1)} %get-tuple-element.389), channel_id=1, source_target_pairs={{0,16},{16,0},{1,17},{17,1},{2,18},{18,2},{3,19},{19,3},{4,20},{20... | collective-permute-start | bytes 3538952 | tf_op jit(solution)/shard_map/ppermute | solution.py:440
  1245.8 31.7 %collective-permute-start.58 = (bf16[768,1472]{0,1:T(8,128)(2,1)}, bf16[768,1472]{0,1:T(8,128)(2,1)}, u32[]{:S(2)}, u32[]{:S(2)}) collective-permute-start(bf16[768,1472]{0,1:T(8,128)(2,1)} %bitcast.261), channel_id=1, source_target_pairs={{0,4},{4,0},{1,5},{5,1},{2,6},{6,2},{3,7},{7,3},{8,12},{12,8},{9,1... | collective-permute-start | bytes 6782984 | tf_op jit(solution)/shard_map/ppermute | solution.py:440
  1251.0 22.3 %collective-permute-start.54 = (bf16[384,384]{1,0:T(8,128)(2,1)S(1)}, bf16[384,384]{1,0:T(8,128)(2,1)S(1)}, u32[]{:S(2)}, u32[]{:S(2)}) collective-permute-start(bf16[384,384]{1,0:T(8,128)(2,1)S(1)} %copy-done.124), channel_id=1, source_target_pairs={{0,2},{1,3},{2,0},{3,1},{4,6},{5,7},{6,4},{7,5},{8,10},{9,11},{10,... | collective-permute-start | bytes 884744 | tf_op jit(solution)/shard_map/ppermute | solution.py:440
  1253.2 20.0 %collective-permute-start.55 = (bf16[384,384]{1,0:T(8,128)(2,1)S(1)}, bf16[384,384]{1,0:T(8,128)(2,1)S(1)}, u32[]{:S(2)}, u32[]{:S(2)}) collective-permute-start(bf16[384,384]{1,0:T(8,128)(2,1)S(1)} %copy-done.123), channel_id=1, source_target_pairs={{0,3},{1,0},{2,1},{3,2},{4,7},{5,4},{6,5},{7,6},{8,11},{9,8},{10,9... | collective-permute-start | bytes 884744 | tf_op jit(solution)/shard_map/ppermute | solution.py:440
  1286.1 56.2 %collective-permute-start.65 = (bf16[2,4,48,1472]{3,2,1,0:T(8,128)(2,1)}, bf16[2,4,48,1472]{3,2,1,0:T(8,128)(2,1)}, u32[]{:S(2)}, u32[]{:S(2)}) collective-permute-start(bf16[2,4,48,1472]{3,2,1,0:T(8,128)(2,1)} %get-tuple-element.407), channel_id=1, source_target_pairs={{0,16},{16,0},{1,17},{17,1},{2,18},{18,2},{3,19},{19,3},{4,20},{20... | collective-permute-start | bytes 3391496 | tf_op jit(solution)/shard_map/ppermute | solution.py:440
  1287.7 27.5 %collective-permute-start.59 = (bf16[384,384]{1,0:T(8,128)(2,1)}, bf16[384,384]{1,0:T(8,128)(2,1)}, u32[]{:S(2)}, u32[]{:S(2)}) collective-permute-start(bf16[384,384]{1,0:T(8,128)(2,1)} %get-tuple-element.399), channel_id=1, source_target_pairs={{0,1},{1,2},{2,3},{3,0},{4,5},{5,6},{6,7},{7,4},{8,9},{9,10},{10,1... | collective-permute-start | bytes 884744 | tf_op jit(solution)/shard_map/ppermute | solution.py:440
  1287.7 28.1 %collective-permute-start.60 = (bf16[384,384]{1,0:T(8,128)(2,1)}, bf16[384,384]{1,0:T(8,128)(2,1)}, u32[]{:S(2)}, u32[]{:S(2)}) collective-permute-start(bf16[384,384]{1,0:T(8,128)(2,1)} %get-tuple-element.400), channel_id=1, source_target_pairs={{0,2},{1,3},{2,0},{3,1},{4,6},{5,7},{6,4},{7,5},{8,10},{9,11},{10,... | collective-permute-start | bytes 884744 | tf_op jit(solution)/shard_map/ppermute | solution.py:440
  1293.7 21.6 %collective-permute-start.75 = (f32[6,1472]{1,0:T(8,128)S(1)}, f32[6,1472]{1,0:T(8,128)S(1)}, u32[]{:S(2)}, u32[]{:S(2)}) collective-permute-start(f32[6,1472]{1,0:T(8,128)S(1)} %add.728), channel_id=1, source_target_pairs={{0,16},{16,0},{1,17},{17,1},{2,18},{18,2},{3,19},{19,3},{4,20},{20... | collective-permute-start | bytes 105992 | tf_op jit(solution)/shard_map/ppermute | solution.py:498
  1297.3 25.2 %collective-permute-start.61 = (bf16[384,384]{1,0:T(8,128)(2,1)}, bf16[384,384]{1,0:T(8,128)(2,1)S(1)}, u32[]{:S(2)}, u32[]{:S(2)}) collective-permute-start(bf16[384,384]{1,0:T(8,128)(2,1)} %get-tuple-element.401), channel_id=1, source_target_pairs={{0,3},{1,0},{2,1},{3,2},{4,7},{5,4},{6,5},{7,6},{8,11},{9,8},{10,9... | collective-permute-start | bytes 884744 | tf_op jit(solution)/shard_map/ppermute | solution.py:440
  1315.3 25.6 %collective-permute-start.63 = (bf16[384,384]{1,0:T(8,128)(2,1)}, bf16[384,384]{1,0:T(8,128)(2,1)S(1)}, u32[]{:S(2)}, u32[]{:S(2)}) collective-permute-start(bf16[384,384]{1,0:T(8,128)(2,1)} %get-tuple-element.404), channel_id=1, source_target_pairs={{0,2},{1,3},{2,0},{3,1},{4,6},{5,7},{6,4},{7,5},{8,10},{9,11},{10,... | collective-permute-start | bytes 884744 | tf_op jit(solution)/shard_map/ppermute | solution.py:440
  1315.8 25.0 %collective-permute-start.64 = (bf16[384,384]{1,0:T(8,128)(2,1)}, bf16[384,384]{1,0:T(8,128)(2,1)S(1)}, u32[]{:S(2)}, u32[]{:S(2)}) collective-permute-start(bf16[384,384]{1,0:T(8,128)(2,1)} %get-tuple-element.405), channel_id=1, source_target_pairs={{0,3},{1,0},{2,1},{3,2},{4,7},{5,4},{6,5},{7,6},{8,11},{9,8},{10,9... | collective-permute-start | bytes 884744 | tf_op jit(solution)/shard_map/ppermute | solution.py:440
  1322.5 23.4 %collective-permute-start.76 = (f32[6,1472]{1,0:T(8,128)S(1)}, f32[6,1472]{1,0:T(8,128)S(1)}, u32[]{:S(2)}, u32[]{:S(2)}) collective-permute-start(f32[6,1472]{1,0:T(8,128)S(1)} %add.729), channel_id=1, source_target_pairs={{0,1},{1,0},{2,3},{3,2},{4,5},{5,4},{6,7},{7,6},{8,9},{9,8},{10,11... | collective-permute-start | bytes 105992 | tf_op jit(solution)/shard_map/ppermute | solution.py:498
  (178 other events, 3280.8 us)
Sparse Core Ops, SparseCore 0:
  11.4 274.3 all-gather.2
  288.6 213.1 all-gather.4

commit v4 on v3

--- a/solution.py
+++ b/solution.py
@@ -473,8 +473,8 @@
     return jnp.concatenate(before[::-1] + [own] + after, axis=0)
 
 
-def from_neighbours(window, tokens):
-    total = window[HALO : HALO + tokens].astype(jnp.float32)
+def start_back(window, tokens):
+    moved = []
     covered = 0
     for distance, span, needed in halo_pieces(tokens):
         if distance < lax.axis_size("z"):
@@ -482,11 +482,18 @@
             right_start = HALO + tokens + covered
             back = slide(window[left_end - needed : left_end], -distance)
             ahead = slide(window[right_start : right_start + needed], distance)
-            total = total + jnp.pad(
-                back.astype(jnp.float32), ((tokens - needed, 0), (0, 0))
-            )
-            total = total + jnp.pad(ahead.astype(jnp.float32), ((0, tokens - needed), (0, 0)))
+            moved.append((back, ahead))
         covered += span
+    return window[HALO : HALO + tokens], moved
+
+
+def finish_back(own, moved):
+    tokens = own.shape[0]
+    total = own.astype(jnp.float32)
+    for back, ahead in moved:
+        needed = back.shape[0]
+        total = total + jnp.pad(back.astype(jnp.float32), ((tokens - needed, 0), (0, 0)))
+        total = total + jnp.pad(ahead.astype(jnp.float32), ((0, tokens - needed), (0, 0)))
     return total
 
 
@@ -575,155 +582,228 @@
     )(normed, middle, gathered, gathered, gathered)
 
 
-def ffn_backward_body(attended, core_ref, *refs):
+def ffn_backward_body(core_ref, *refs):
     branch_ref, normed_ref, up_gelu_ref, up_linear_ref, gelu_ref, linear_ref, down_ref = refs[:7]
-    refs = refs[7:]
-    if attended:
-        first_ref, second_ref, first_side_ref, second_side_ref = refs[:4]
-        refs = refs[4:]
-    grad_ref, kept_refs, sent_refs = refs[0], refs[1:5], refs[5:9]
-    stage_ref, sems = refs[9], refs[10]
+    grad_ref, kept_ref, sent_ref, stage_ref, sems = refs[7:]
     step = pl.program_id(0)
     hidden_steps = FF // TILE
     slot = step % 2
-    mine, unit, rows, columns = core_ref[0], core_ref[1], core_ref[2], core_ref[3]
-
-    def places(target):
-        unit_at, inside = target // (2 * unit), target % unit
-        swapped = (unit_at % columns) * rows + unit_at // columns
-        for k in range(4):
-            at = (unit_at if k % 2 == 0 else swapped) * unit + inside
-            yield k, pl.ds(pl.multiple_of(at * TILE, TILE), TILE)
-
-    def copy(kind, k, place, spot, where):
-        source = stage_ref.at[where, kind, :, k * CHUNK : (k + 1) * CHUNK]
-        return pltpu.make_async_copy(source, place[k].at[spot, :], sems.at[where, kind, k])
-
-    def wait(kind, where):
-        for k in range(4):
-            copy(kind, k, kept_refs, pl.ds(0, TILE), where).wait()
-
-    def put(kind, target, left, right):
-        product = jnp.dot(left, right, preferred_element_type=jnp.float32)
-        stage_ref[slot, kind, :, : CUTS[-1]] = product.astype(jnp.bfloat16)
+    mine, unit = core_ref[0], core_ref[1]
+
+    def copy(kind, place, at, where):
+        spot = pl.ds(pl.multiple_of(at * TILE, TILE), TILE)
+        return pltpu.make_async_copy(
+            stage_ref.at[where, kind], place.at[spot, :], sems.at[where, kind]
+        )
+
+    def put(kind, turned):
+        target = ATTENTION_TILES + kind * hidden_steps + step
+        stage_ref[slot, kind] = turned
         own = (target // unit) % 2 == mine
-        spots = list(places(target))
+        at = (target // (2 * unit)) * unit + target % unit
 
         @pl.when(own)
         def _():
-            for k, spot in spots:
-                copy(kind, k, kept_refs, spot, slot).start()
+            copy(kind, kept_ref, at, slot).start()
 
         @pl.when(jnp.logical_not(own))
         def _():
-            for k, spot in spots:
-                copy(kind, k, sent_refs, spot, slot).start()
+            copy(kind, sent_ref, at, slot).start()
 
     @pl.when(step == 0)
     def _():
         grad_ref[...] = jnp.zeros_like(grad_ref)
-        stage_ref[:, :, :, CUTS[-1] :] = jnp.zeros(
-            stage_ref.shape[:3] + (4 * CHUNK - CUTS[-1],), jnp.bfloat16
-        )
-
-    @pl.when((step >= 2) & (step < hidden_steps + 2))
+
+    @pl.when(step >= 2)
     def _():
         for kind in range(3):
-            wait(kind, slot)
-
-    if attended:
-
-        @pl.when(step >= hidden_steps + 2)
-        def _():
-            wait(0, slot)
-
-    @pl.when(step < hidden_steps)
-    def _():
-        grad_hidden = times_rows(branch_ref[...], down_ref[...])
-        active, slope = gelu_parts(up_gelu_ref[...])
-        linear = up_linear_ref[...]
-        hidden = (active * linear).astype(jnp.bfloat16)
-        grad_gelu = (grad_hidden * linear * slope).astype(jnp.bfloat16)
-        grad_linear = (grad_hidden * active).astype(jnp.bfloat16)
-        grad_ref[...] += times_plain(grad_gelu, gelu_ref[...]) + times_plain(
-            grad_linear, linear_ref[...]
-        )
-        put(0, ATTENTION_TILES + step, grad_gelu.T, normed_ref[...])
-        put(1, ATTENTION_TILES + hidden_steps + step, grad_linear.T, normed_ref[...])
-        put(2, ATTENTION_TILES + 2 * hidden_steps + step, hidden.T, branch_ref[...])
-
-    if attended:
-
-        @pl.when(step >= hidden_steps)
-        def _():
-            put(
-                0,
-                step - hidden_steps,
-                jnp.concatenate([first_ref[...], second_ref[...]], axis=0).T,
-                jnp.concatenate([first_side_ref[...], second_side_ref[...]], axis=0),
-            )
-
-    @pl.when(step == pl.num_programs(0) - 1)
+            copy(kind, kept_ref, 0, slot).wait()
+
+    grad_hidden = times_rows(branch_ref[...], down_ref[...])
+    active, slope = gelu_parts(up_gelu_ref[...])
+    linear = up_linear_ref[...]
+    grad_gelu = (grad_hidden * linear * slope).astype(jnp.bfloat16)
+    grad_linear = (grad_hidden * active).astype(jnp.bfloat16)
+    put(2, (active * linear).astype(jnp.bfloat16).T)
+    put(0, grad_gelu.T)
+    put(1, grad_linear.T)
+    grad_ref[...] += times_plain(grad_gelu, gelu_ref[...]) + times_plain(
+        grad_linear, linear_ref[...]
+    )
+
+    @pl.when(step == hidden_steps - 1)
     def _():
         for back in range(2):
-            for kind in range(1 if attended else 3):
-                wait(kind, back)
-
-
-def ffn_backward(branch, normed, up_gelu, up_linear, gathered, attention):
+            for kind in range(3):
+                copy(kind, kept_ref, 0, back).wait()
+
+
+def unit_tiles(tile):
+    rows = 4 * INNER + 3 * FF
+    return rows // tile // (2 * lax.axis_size("y") * lax.axis_size("x"))
+
+
+def ffn_backward(branch, normed, up_gelu, up_linear, gathered):
     tokens, width = normed.shape
     rows = 4 * INNER + 3 * FF
-    hidden_steps = FF // TILE
+    steps = FF // TILE
+    core = jnp.stack([lax.axis_index("c").astype(jnp.int32), jnp.int32(unit_tiles(TILE))])
+
+    def weight(kind):
+        first = ATTENTION_TILES + kind * steps
+        return pl.BlockSpec((TILE, width), lambda i, *_: (first + i, 0))
+
+    hidden = pl.BlockSpec((tokens, TILE), lambda i, *_: (0, i))
+    side = resident((tokens, width))
+    anywhere = pl.BlockSpec(memory_space=pl.ANY)
+    return pl.pallas_call(
+        ffn_backward_body,
+        grid_spec=pltpu.PrefetchScalarGridSpec(
+            num_scalar_prefetch=1,
+            grid=(steps,),
+            in_specs=[side, side, hidden, hidden, weight(0), weight(1), weight(2)],
+            out_specs=[side, anywhere, anywhere],
+            scratch_shapes=[
+                pltpu.VMEM((2, 3, TILE, tokens), jnp.bfloat16),
+                pltpu.SemaphoreType.DMA((2, 3)),
+            ],
+        ),
+        out_shape=[jax.ShapeDtypeStruct((tokens, width), jnp.float32)]
+        + [jax.ShapeDtypeStruct((rows // 2, tokens), jnp.bfloat16)] * 2,
+        compiler_params=pltpu.CompilerParams(vmem_limit_bytes=48 << 20),
+        cost_estimate=pl.CostEstimate(
+            flops=6 * tokens * FF * width,
+            bytes_accessed=6 * FF * width + 14 * tokens * FF,
+            transcendentals=tokens * FF,
+        ),
+        name="ffn_backward",
+    )(core, branch, normed, up_gelu, up_linear, gathered, gathered, gathered)
+
+
+def weight_grads_body(route, tile, place_ref, *refs):
+    own_ref, other_ref = refs[:2]
+    normed_refs, branch_refs = refs[2:4], refs[4:6]
+    outs = refs[6:]
+    step = pl.program_id(0)
+    count = len(outs) // 2
+    per_place = pl.num_programs(0) // count
+    source = weight_source(route, tile, step, place_ref)
+    unit = place_ref[3]
+    at = (source // unit * 2 + place_ref[2]) * unit + source % unit
+    first, second = 4 * INNER // tile, (4 * INNER + 2 * FF) // tile
+
+    def put(product_of):
+        for turn in range(2):
+            chunk = 2 * turn + (0 if route == "y" else 1)
+            start, end = CUTS[chunk], CUTS[chunk + 1]
+            product = product_of(slice(start, end))
+            for k in range(count):
+
+                @pl.when(step // per_place == k)
+                def _(k=k, turn=turn, product=product, width=end - start):
+                    out = outs[2 * k + turn]
+                    out[:, :width] = product.astype(jnp.bfloat16)
+                    if width < CHUNK:
+                        out[:, width:] = jnp.zeros((tile, CHUNK - width), jnp.bfloat16)
+
+    def both(sides):
+        def product_of(columns):
+            return jnp.dot(
+                own_ref[...], sides[0][:, columns], preferred_element_type=jnp.float32
+            ) + jnp.dot(other_ref[...], sides[1][:, columns], preferred_element_type=jnp.float32)
+
+        return product_of
+
+    @pl.when(at < first)
+    def _():
+        put(lambda columns: jnp.zeros((tile, columns.stop - columns.start), jnp.float32))
+
+    @pl.when((at >= first) & (at < second))
+    def _():
+        put(both(normed_refs))
+
+    @pl.when(at >= second)
+    def _():
+        put(both(branch_refs))
+
+
+def weight_source(route, tile, step, place_ref):
+    size_y, size_x, unit = place_ref[4], place_ref[5], place_ref[3]
+    if route == "y":
+        size, others, here = size_y, size_x, place_ref[0]
+    else:
+        size, others, here = size_x, size_y, place_ref[1]
+    per_place = others * unit
+    goal = (here + 1 + step // per_place) % size
+    other = step % per_place // unit
+    row, column = (goal, other) if route == "y" else (other, goal)
+    return (row * size_x + column) * unit + step % unit
+
+
+def weight_grads(route, own, other, normed, branch):
+    rows, tokens = own.shape
+    width = normed[0].shape[1]
     size_y, size_x = lax.axis_size("y"), lax.axis_size("x")
-    unit = rows // TILE // (2 * size_y * size_x)
-    core = jnp.stack(
+    tile = 512 if unit_tiles(256) % 2 == 0 else 256
+    size = size_y if route == "y" else size_x
+    steps = rows // tile
+    per_place = steps // size
+    place = jnp.stack(
         [
+            lax.axis_index("y").astype(jnp.int32),
+            lax.axis_index("x").astype(jnp.int32),
             lax.axis_index("c").astype(jnp.int32),
-            jnp.int32(unit),
+            jnp.int32(unit_tiles(tile)),
             jnp.int32(size_y),
             jnp.int32(size_x),
         ]
     )
-    last = hidden_steps - 1
-
-    def weight(kind):
-        first = ATTENTION_TILES + kind * hidden_steps
-        return pl.BlockSpec((TILE, width), lambda i, *_: (first + jnp.minimum(i, last), 0))
-
-    hidden = pl.BlockSpec((tokens, TILE), lambda i, *_: (0, jnp.minimum(i, last)))
-    late = pl.BlockSpec((tokens, TILE), lambda i, *_: (0, jnp.maximum(i - hidden_steps, 0)))
+    source = pl.BlockSpec(
+        (tile, tokens), lambda i, place_ref: (weight_source(route, tile, i, place_ref), 0)
+    )
     side = resident((tokens, width))
-    operands = [branch, normed, up_gelu, up_linear, gathered, gathered, gathered]
-    in_specs = [side, side, hidden, hidden, weight(0), weight(1), weight(2)]
-    steps = hidden_steps
-    if attention is not None:
-        operands += attention
-        in_specs += [late, late, side, side]
-        steps += ATTENTION_TILES
-    anywhere = pl.BlockSpec(memory_space=pl.ANY)
+
+    def out_spec(k):
+        return pl.BlockSpec(
+            (tile, CHUNK), lambda i, *_: (jnp.clip(i - k * per_place, 0, per_place - 1), 0)
+        )
+
     results = pl.pallas_call(
-        functools.partial(ffn_backward_body, attention is not None),
+        functools.partial(weight_grads_body, route, tile),
         grid_spec=pltpu.PrefetchScalarGridSpec(
             num_scalar_prefetch=1,
             grid=(steps,),
-            in_specs=in_specs,
-            out_specs=[side] + [anywhere] * 8,
-            scratch_shapes=[
-                pltpu.VMEM((2, 3, TILE, 4 * CHUNK), jnp.bfloat16),
-                pltpu.SemaphoreType.DMA((2, 3, 4)),
-            ],
+            in_specs=[source, source, side, side, side, side],
+            out_specs=[out_spec(k) for k in range(size) for _ in range(2)],
         ),
-        out_shape=[jax.ShapeDtypeStruct((tokens, width), jnp.float32)]
-        + [jax.ShapeDtypeStruct((rows // 2, CHUNK), jnp.bfloat16)] * 8,
-        compiler_params=pltpu.CompilerParams(vmem_limit_bytes=52 << 20),
+        out_shape=[jax.ShapeDtypeStruct((rows // size, CHUNK), jnp.bfloat16)] * (2 * size),
+        compiler_params=pltpu.CompilerParams(vmem_limit_bytes=32 << 20),
         cost_estimate=pl.CostEstimate(
-            flops=12 * tokens * FF * width,
-            bytes_accessed=12 * FF * width + 8 * tokens * FF,
-            transcendentals=tokens * FF,
+            flops=2 * rows * tokens * width,
+            bytes_accessed=4 * rows * tokens + rows * width,
+            transcendentals=0,
         ),
-        name="ffn_backward",
-    )(core, *operands)
-    return results[0], list(results[1:5]), list(results[5:9])
+        name="weight_grads",
+    )(place, own, other, *normed, *branch)
+    return [[results[2 * k + turn] for k in range(size)] for turn in range(2)]
+
+
+def with_attention(route, chunk, arrays, rows):
+    size = lax.axis_size(route)
+    unit_rows = rows.shape[0]
+    owners = 4 * INNER // unit_rows
+    start, end = CUTS[chunk], CUTS[chunk + 1]
+    columns = jnp.pad(rows[:, start:end], ((0, 0), (0, CHUNK - end + start)))
+    filled = []
+    for k, array in enumerate(arrays):
+        here = (lax.axis_index(route) + 1 + k) % size == 0
+        here = here & (lax.axis_index("c") < owners)
+        filled.append(
+            lax.dynamic_update_slice(
+                array, jnp.where(here, columns, array[:unit_rows]), (0, 0)
+            )
+        )
+    return filled
 
 
 def tied(first, second):
@@ -732,35 +812,34 @@
 
 class Scatter:
     def __init__(self):
-        self.waiting, self.flying, self.results = [], [], {}
-
-    def push(self, name, route, kept, moved):
-        shape = tuple(lax.axis_size(axis) for axis in route) + (-1, kept.shape[-1])
-        self.waiting.append((name, route, kept.reshape(shape), [moved.reshape(shape)]))
-
-    def busy(self):
-        return bool(self.waiting or self.flying)
-
-    def step(self, values, enter=2):
-        flying = [item[2:] for item in self.flying]
-        flying, values = tied(flying, values)
-        entering, self.waiting = self.waiting[:enter], self.waiting[enter:]
-        ready = [item[:2] + tuple(arrays) for item, arrays in zip(self.flying, flying)] + entering
-        moves = []
-        for name, route, kept, moved in ready:
+        self.waiting, self.flying, self.results = {}, {}, {}
+
+    def push(self, name, route, kept, sends):
+        self.waiting[name] = (route, kept, sends)
+
+    def step(self, values, *names):
+        arrays = {name: self.flying[name][1:] for name in names if name in self.flying}
+        arrays, values = tied(arrays, values)
+        moves = {}
+        for name in names:
+            if name in self.waiting:
+                moves[name] = self.waiting.pop(name)
+                continue
+            route = self.flying.pop(name)[0]
+            kept, moved = arrays[name]
             if not route:
                 self.results[name] = kept.astype(jnp.float32) + sum(
                     part.astype(jnp.float32) for part in moved
                 )
                 continue
             total = total_of(kept, moved)
+            total = total.reshape((lax.axis_size(route[0]), -1) + total.shape[-1:])
             sends = stage_sends(total, route[0], 0)
-            moves.append((name, route, pick(total, lax.axis_index(route[0]), 0), sends))
-        arrays, values = tied([item[2:] for item in moves], values)
-        self.flying = [
-            (name, route[1:], kept, stage_moves(sends, route[0]))
-            for (name, route, *_), (kept, sends) in zip(moves, arrays)
-        ]
+            moves[name] = (route, pick(total, lax.axis_index(route[0]), 0), sends)
+        arrays, values = tied({name: move[1:] for name, move in moves.items()}, values)
+        for name, (route, *_) in moves.items():
+            kept, sends = arrays[name]
+            self.flying[name] = (route[1:], kept, stage_moves(sends, route[0]))
         return values
 
 
@@ -775,18 +854,15 @@
     return lax.all_gather(local_rows, DEVICES, axis=0, tiled=True)
 
 
-def layer_forward(stream, gathered, gain_one, gain_two, gate_low, context, early):
-    tokens = stream.shape[0]
+def layer_forward(stream, gathered, gain_one, gain_two, gate_low, context):
     normed, inverse_one = rms_forward(stream, gain_one)
     normed_low = normed.astype(jnp.bfloat16)
-    if early is None:
-        projected = times_rows(normed_low, gathered[: 3 * INNER]).astype(jnp.bfloat16)
-        queries = projected[:, :INNER]
-        wide_gate = jnp.broadcast_to(gate_low[:, None], (tokens, BLOCK))
-        shared = with_neighbours(jnp.concatenate([projected[:, INNER:], wide_gate], axis=1))
-    else:
-        queries = times_rows(normed_low, gathered[:INNER]).astype(jnp.bfloat16)
-        shared = times_rows(early, gathered[INNER : 3 * INNER]).astype(jnp.bfloat16)
+    projected = times_rows(normed_low, gathered[: 3 * INNER]).astype(jnp.bfloat16)
+    queries = projected[:, :INNER]
+    parts = [projected[:, INNER:]]
+    if gate_low is not None:
+        parts.append(jnp.broadcast_to(gate_low[:, None], (stream.shape[0], BLOCK)))
+    shared = with_neighbours(jnp.concatenate(parts, axis=1))
     attended, log_total = attend_forward(queries, shared, context)
     middle = stream + times_plain(attended, gathered[3 * INNER : 4 * INNER])
     normed_two, inverse_two = rms_forward(middle, gain_two)
@@ -809,7 +885,7 @@
     return (result, kept)
 
 
-def layer_backward(grad_out, kept, gathered, gain_one, gain_two, context, waiting, scatter, name):
+def layer_backward(grad_out, kept, gathered, gain_one, gain_two, context, scatter, name, steps):
     (
         stream,
         inverse_one,
@@ -824,95 +900,53 @@
         up_gelu,
         up_linear,
     ) = kept
+    tokens = queries.shape[0]
     branch_low = grad_out.astype(jnp.bfloat16)
+    normed_pair = (normed_two_low, shift(normed_two_low, "c", 1))
+    branch_pair = (branch_low, shift(branch_low, "c", 1))
     grad_normed_two, own, sent = ffn_backward(
-        branch_low, normed_two_low, up_gelu, up_linear, gathered, waiting
-    )
-    moved = [shift(part, "c", 1) for part in sent]
-    grad_normed_two, own = lax.optimization_barrier((grad_normed_two, own))
+        branch_low, normed_two_low, up_gelu, up_linear, gathered
+    )
+    other = shift(sent, "c", 1)
     grad_middle, grad_gain_two = rms_backward(middle, inverse_two, gain_two, grad_normed_two)
     grad_middle = grad_out + grad_middle
     middle_low = grad_middle.astype(jnp.bfloat16)
     grad_mixed = times_rows(middle_low, gathered[3 * INNER : 4 * INNER]).astype(jnp.bfloat16)
-    for k in range(4):
-        scatter.push((name, k), ("y", "x", "z") if k % 2 == 0 else ("x", "y", "z"), own[k], moved[k])
-    grad_mixed, grad_middle, middle_low = scatter.step((grad_mixed, grad_middle, middle_low))
+    grad_mixed, grad_middle, middle_low = steps[0]((grad_mixed, grad_middle, middle_low))
     grad_query, grad_shared, grad_table = attend_backward(
         queries, grad_mixed, shared, log_total, context
     )
-    grad_query, grad_shared, grad_table = scatter.step((grad_query, grad_shared, grad_table))
-    grad_own = from_neighbours(grad_shared, queries.shape[0])
+    grad_shared, own = lax.optimization_barrier((grad_shared, own))
+    moving = start_back(grad_shared, tokens)
+    routed = {
+        route: weight_grads(route, own, other, normed_pair, branch_pair) for route in ("y", "x")
+    }
+    output_rows = outer_sum(attended, middle_low).astype(jnp.bfloat16)
+    routed, output_rows, moving = steps[1]((routed, output_rows, moving))
+    grad_own = finish_back(*moving)
     grad_gate = grad_own[:, 2 * INNER :]
     grad_input_low = jnp.concatenate(
         [grad_query, grad_own[:, : 2 * INNER].astype(jnp.bfloat16)], axis=1
     )
-    grad_input_low, grad_gate = scatter.step((grad_input_low, grad_gate))
+    rows = jnp.concatenate(
+        [outer_sum(grad_input_low, normed_low).astype(jnp.bfloat16), output_rows], axis=0
+    )
+    unit_rows = unit_tiles(TILE) * TILE
+    core = lax.axis_index("c")
+    most = 4 * INNER // unit_rows - 1
+    kept_rows, sent_rows = (
+        lax.dynamic_slice_in_dim(rows, jnp.minimum(at, most) * unit_rows, unit_rows, 0)
+        for at in (core, 1 - core)
+    )
+    rows = total_of(kept_rows, [shift(sent_rows, "c", 1)])
+    for chunk in range(4):
+        route = ("y", "x", "z") if chunk % 2 == 0 else ("x", "y", "z")
+        arrays = with_attention(route[0], chunk, routed[route[0]][chunk // 2], rows)
+        scatter.push((name, chunk), route, arrays[-1], arrays[:-1])
+    grad_input_low, grad_gate = steps[2]((grad_input_low, grad_gate))
     grad_normed = times_plain(grad_input_low, gathered[: 3 * INNER])
     grad_stream, grad_gain_one = rms_backward(stream, inverse_one, gain_one, grad_normed)
-    grad_stream = grad_middle + grad_stream
-    return (
-        grad_stream,
-        grad_table,
-        grad_gate,
-        grad_gain_one,
-        grad_gain_two,
-        (grad_input_low, attended, normed_low, middle_low),
-    )
-
-
-def padded_attention(attention):
-    grad_input_low, attended, normed_low, middle_low = attention
-    return [
-        jnp.pad(grad_input_low, ((0, 0), (0, INNER))),
-        jnp.pad(attended, ((0, 0), (3 * INNER, 0))),
-        normed_low,
-        middle_low,
-    ]
-
-
-def push_last_attention(attention, scatter):
-    grad_input_low, attended, normed_low, middle_low = attention
-    size_y, size_x, size_z = (lax.axis_size(axis) for axis in ("y", "x", "z"))
-    core = lax.axis_index("c")
-    width = normed_low.shape[1]
-    owners, part = owner_parts()
-    rows = jnp.concatenate(
-        [
-            outer_sum(grad_input_low, normed_low).astype(jnp.bfloat16),
-            outer_sum(attended, middle_low).astype(jnp.bfloat16),
-        ],
-        axis=0,
-    )
-    rows = rows.reshape(owners, size_z, size_y, size_x, 2, -1, width)
-    rows = rows.transpose(4, 2, 3, 1, 0, 5, 6).reshape(2, -1, width)
-    kept, sent = pick(rows, core, 0), pick(rows, 1 - core, 0)
-    moved = shift(sent, "c", 1)
-    scatter.push("late", ("y", "x", "z"), kept, moved)
-
-
-def owner_parts():
-    size_y, size_x, size_z = (lax.axis_size(axis) for axis in ("y", "x", "z"))
-    block = (4 * INNER + 3 * FF) // (size_y * size_x * 2 * size_z)
-    owners = 4 * INNER // (block * size_z)
-    return owners, block * owners // (size_y * size_x * 2)
-
-
-def bring_to_owners(mine):
-    size_y, size_x = lax.axis_size("y"), lax.axis_size("x")
-    owners, part = owner_parts()
-    width = mine.shape[-1]
-    mine = mine.astype(jnp.bfloat16)[None]
-    for axis in ("c", "x", "y"):
-        count, here = lax.axis_size(axis), lax.axis_index(axis)
-        gathered = jnp.zeros((count,) + mine.shape, mine.dtype)
-        gathered = lax.dynamic_update_index_in_dim(gathered, mine, here, 0)
-        for k in range(1, count):
-            gathered = lax.dynamic_update_index_in_dim(
-                gathered, shift(mine, axis, k), (here - k) % count, 0
-            )
-        mine = gathered.reshape((-1,) + mine.shape[1:])
-    shape = (size_y, size_x, 2, owners, part // owners, width)
-    return mine.reshape(shape).transpose(3, 0, 1, 2, 4, 5).reshape(owners, -1, width)
+    return (grad_middle + grad_stream, grad_table, grad_gate, grad_gain_one, grad_gain_two)
 
 
 def per_device(
@@ -922,10 +956,9 @@
     first_pos = lax.axis_index("z") * tokens_here
     context = attention_context(segment_ids[0], first_pos, tokens_here, rel_bias)
     stream = inputs.reshape(tokens_here, width)
-    early = with_neighbours(rms_forward(stream, norm_gains[0])[0].astype(jnp.bfloat16))
     gathered_three = fetch_rows(layer3_rows)
     after_three, kept_three = layer_forward(
-        stream, gathered_three, norm_gains[0], norm_gains[1], None, context, early
+        stream, gathered_three, norm_gains[0], norm_gains[1], None, context
     )
     gate_inverse = lax.rsqrt(jnp.mean(after_three * after_three, axis=1, keepdims=True) + epsilon)
     gate_normed = after_three * gate_inverse
@@ -935,54 +968,55 @@
     gate_low = gate_mask.astype(jnp.bfloat16)
     gathered_four = fetch_rows(layer4_rows)
     after_four, kept_four = layer_forward(
-        after_three, gathered_four, norm_gains[2], norm_gains[3], gate_low, context, None
+        after_three, gathered_four, norm_gains[2], norm_gains[3], gate_low, context
     )
     scatter = Scatter()
-    grad_three_out, table_four, grad_gate, gain_four_one, gain_four_two, attention_four = (
-        layer_backward(
-            cotangent.reshape(tokens_here, width),
-            kept_four,
-            gathered_four,
-            norm_gains[2],
-            norm_gains[3],
-            context,
-            None,
-            scatter,
-            "four",
-        )
+
+    def step(*names):
+        return lambda values: scatter.step(values, *names)
+
+    four, three = ([(name, chunk) for chunk in range(4)] for name in ("four", "three"))
+    grad_three_out, table_four, grad_gate, gain_four_one, gain_four_two = layer_backward(
+        cotangent.reshape(tokens_here, width),
+        kept_four,
+        gathered_four,
+        norm_gains[2],
+        norm_gains[3],
+        context,
+        scatter,
+        "four",
+        [step(), step(), step(*four)],
     )
     grad_logit = grad_gate[:, 0] * gate_scale * sigmoid_value * (1.0 - sigmoid_value)
     grad_gate_weight = jnp.sum(grad_logit[:, None] * gate_normed, axis=0)
     gate_stream = stream_backward(after_three, gate_inverse, grad_logit[:, None] * gate_weight)
-    grad_three_out = scatter.step(grad_three_out + gate_stream)
-    grad_input, table_three, unused, gain_three_one, gain_three_two, attention_three = (
-        layer_backward(
-            grad_three_out,
-            kept_three,
-            gathered_three,
-            norm_gains[0],
-            norm_gains[1],
-            context,
-            padded_attention(attention_four),
-            scatter,
-            "three",
-        )
-    )
-    push_last_attention(attention_three, scatter)
-    while scatter.busy():
-        grad_input = scatter.step(grad_input)
-    owner = (
-        (lax.axis_index("y") * lax.axis_size("x") + lax.axis_index("x")) * lax.axis_size("c")
-    ) + lax.axis_index("c")
-    late = bring_to_owners(scatter.results["late"].reshape(-1, width)).astype(jnp.float32)
-    owners = late.shape[0]
-    mine = pick(late, jnp.minimum(owner, owners - 1), 0)
+    grad_input, table_three, unused, gain_three_one, gain_three_two = layer_backward(
+        grad_three_out + gate_stream,
+        kept_three,
+        gathered_three,
+        norm_gains[0],
+        norm_gains[1],
+        context,
+        scatter,
+        "three",
+        [step(*four[:2]), step(*four[2:]), step(*four[:2], *three[:2])],
+    )
+    for names in (
+        four[2:],
+        three[:2] + three[2:],
+        four[:2],
+        three[:2],
+        three[2:],
+        four[2:],
+        three[2:],
+        three[:2],
+        three[2:],
+    ):
+        grad_input = scatter.step(grad_input, *names)
     local_four, local_three = (
-        jnp.concatenate([scatter.results[name, k].reshape(-1, CHUNK) for k in range(4)], axis=1)[:, :width]
-        for name in ("four", "three")
-    )
-    local_four = jnp.where(owner < owners, local_three, local_four)
-    local_three = jnp.where(owner < owners, mine, local_three)
+        jnp.concatenate([scatter.results[name] for name in names], axis=1)[:, :width]
+        for names in (four, three)
+    )
     table = jnp.pad((table_three + table_four).reshape(1, -1), ((0, 0), (0, width - 6 * BUCKETS)))
     small = jnp.stack(
         [gain_three_one, gain_three_two, gain_four_one, gain_four_two, grad_gate_weight, table[0]]

time: 1430 us -> 1490 us (1.042)
  Pallas kernels: 259 us -> 292 us
  starting transfers between devices: 137 us -> 166 us
  waiting for transfers between devices: 695 us -> 674 us
    ppermute x16, waiting for transfers between devices: 235 us -> 74 us  [slide(): return lax.ppermute(value, 'z', pairs)]
    all_gather x2, waiting for transfers between devices: 264 us -> 330 us  [fetch_rows(): return lax.all_gather(local_rows, DEVICES, axis=0, tiled=True)]
    ppermute x57 -> x48, waiting for transfers between devices: 174 us -> 214 us  [shift(): lax.ppermute(value, axis, [(i, (i + amount) % count) for i in range(count)])]
    ppermute x5, waiting for transfers between devices: 21.7 us -> 55.7 us  [sum_everywhere(): lax.ppermute(value, axis, [(i, i ^ bit) for i in range(count)])]
    convert_element_type x27 -> x18, other arithmetic: 71.4 us -> 39.3 us  [total_of(): return total.astype(jnp.bfloat16)]
    pallas_call x2 -> x6, Pallas kernels: 131 us -> 162 us  [the longest x4 81.7 us: weight_grads(): pl.pallas_call(functools.partial(weight_grads_body, route, tile), grid_sp...]
    ppermute x16, starting transfers between devices: 57 us -> 87.1 us  [slide(): return lax.ppermute(value, 'z', pairs)]
    squeeze x27 -> x16, local copies, waits for them, and re-layouts: 46.6 us -> 18.4 us  [pick(): return lax.dynamic_index_in_dim(value, index, axis, keepdims=False)]
  transfers between devices with their start and end apart: 80 -> 71, of which waited for: 32 -> 24; matrix products, arithmetic and copies ran while one was open for 16% -> 15% of each run, Pallas kernels for 6% -> 14%
where the time goes in v4:
time: 1490 us; the launch traced here: 1470 us
  waiting for transfers between devices  674 us (45%)
  Pallas kernels  292 us (20%)
  starting transfers between devices  166 us (11%)
  local copies, waits for them, and re-layouts  156 us (10%)
  other arithmetic  123 us (8%)
  matrix products  47 us (3%)
  between operations  16.6 us (1%)
    all_gather x2, waiting for transfers between devices, fetch_rows(): return lax.all_gather(local_rows, DEVICES, axis=0, tiled=True)  330 us
    ppermute x48, waiting for transfers between devices, shift(): lax.ppermute(value, axis, [(i, (i + amount) % count) for i in range(count)])  214 us
    ppermute x16, starting transfers between devices, slide(): return lax.ppermute(value, 'z', pairs)  87.1 us
    pallas_call x4, Pallas kernels, weight_grads(): pl.pallas_call(functools.partial(weight_grads_body, route, tile), grid_sp...  81.7 us
    pallas_call x2, Pallas kernels, ffn_backward(): pl.pallas_call(ffn_backward_body, grid_spec=pltpu.PrefetchScalarGridSpec(...  80.3 us
    ppermute x48, starting transfers between devices, shift(): lax.ppermute(value, axis, [(i, (i + amount) % count) for i in range(count)])  75.1 us
    ppermute x16, waiting for transfers between devices, slide(): return lax.ppermute(value, 'z', pairs)  74 us
    unnamed x327, local copies, waits for them, and re-layouts  57.3 us
  transfers between devices with their start and end apart: 71, of which 24 were waited for; matrix products, arithmetic and copies ran while one was open for 15% of the time, Pallas kernels for 14%

profile of v4, /device:TPU:24, one launch (start us, length us, event | category | flops | bytes accessed | tf_op | source)
XLA Modules:
  0.0 1474.9 jit_solution(14316366611281366156)
XLA Ops:
  16.0 209.4 %all-gather.3.cloned.1.call-done.gelu_ref.linear_ref.down_ref.refs_4_.refs_5_.refs_6_ = bf16[12288,1472]{1,0:T(8,128)(2,1)} async-done(((bf16[384,1472]{1,0:T(8,128)(2,1)}), bf16[12288,1472]{1,0:T(8,128)(2,1)}) %all-gather.3.cloned.1.call-update) | async-done | bytes 36175888 | tf_op jit(solution)/shard_map/all_gather | solution.py:854
  234.6 5.5 collective-permute-start.2
  241.0 4.7 bias_tiles.1.refs_4_.refs_5_
  246.9 5.3 collective-permute-start.3
  252.2 45.7 %collective-permute-done = bf16[288,768]{1,0:T(8,128)(2,1)} collective-permute-done((bf16[288,768]{1,0:T(8,128)(2,1)}, bf16[288,768]{1,0:T(8,128)(2,1)}, u32[]{:S(2)}, u32[]{:S(2)}) %collective-permute-start) | collective-permute-done | bytes 442400 | tf_op jit(solution)/shard_map/ppermute | solution.py:446
  302.2 13.6 attend_forward.2
  319.9 24.8 %ffn_forward.2 = (f32[512,1472]{1,0:T(8,128)S(1)}, f32[512,3584]{1,0:T(8,128)}, f32[512,3584]{1,0:T(8,128)}) custom-call(bf16[512,1472]{1,0:T(8,128)(2,1)S(1)} %multiply_convert_fusion.2.normed_ref.refs_1_.refs_2_, f32[512,1472]{1,0:T(8,128)} %copy-done.69, ...), custom_call_target="tpu_custom_call" | custom-call | flops 16206790656 | bytes 46333952 | tf_op jit(solution)/shard_map/ffn_forward/pallas_call | solution.py:559
  346.7 121.0 %all-gather.5.cloned.1.call-done.gelu_ref.linear_ref.down_ref.refs_4_.refs_5_.refs_6_ = bf16[12288,1472]{1,0:T(8,128)(2,1)} async-done(((bf16[384,1472]{1,0:T(8,128)(2,1)}), bf16[12288,1472]{1,0:T(8,128)(2,1)}) %all-gather.5.cloned.1.call-update) | async-done | bytes 36175888 | tf_op jit(solution)/shard_map/all_gather | solution.py:854
  478.3 4.6 collective-permute-start.6
  488.9 5.5 collective-permute-start.7
  494.5 26.6 %collective-permute-done.4 = bf16[288,896]{1,0:T(8,128)(2,1)S(1)} collective-permute-done((bf16[288,896]{1,0:T(8,128)(2,1)S(1)}, bf16[288,896]{1,0:T(8,128)(2,1)S(1)}, u32[]{:S(2)}, u32[]{:S(2)}) %collective-permute-start.4) | collective-permute-done | bytes 516128 | tf_op jit(solution)/shard_map/ppermute | solution.py:446
  524.4 13.9 attend_forward.3
  542.7 24.6 %ffn_forward.3 = (f32[512,1472]{1,0:T(8,128)S(1)}, f32[512,3584]{1,0:T(8,128)}, f32[512,3584]{1,0:T(8,128)}) custom-call(bf16[512,1472]{1,0:T(8,128)(2,1)S(1)} %multiply_convert_fusion.normed_ref.refs_1_.refs_2_, f32[512,1472]{1,0:T(8,128)} %copy-done.71, ...), custom_call_target="tpu_custom_call" | custom-call | flops 16206790656 | bytes 46333952 | tf_op jit(solution)/shard_map/ffn_forward/pallas_call | solution.py:559
  569.0 40.2 %ffn_backward.2 = (f32[512,1472]{1,0:T(8,128)}, bf16[6144,512]{1,0:T(8,128)(2,1)}, bf16[6144,512]{1,0:T(8,128)(2,1)}) custom-call(s32[2]{0:T(128)S(1)} %pad_add_fusion.core_ref, bf16[512,1472]{1,0:T(8,128)(2,1)S(1)} %bitcast_convert_fusion.refs_0_.refs_4_, bf16[512,1472]{1,0:T(8,128)(2,1)S(1)} %multiply_convert_fusion.normed_ref.refs_1_.refs_2_, ...), custom_call_target="tpu_custom_call" | custom-call | flops 16206790656 | bytes 57344000 | tf_op jit(solution)/shard_map/ffn_backward/pallas_call | solution.py:659
  614.1 7.9 collective-permute-done.10
  627.3 4.4 multiply_reduce_fusion.1
  631.9 4.4 fusion.39
  638.8 24.7 %attend_backward.2 = (bf16[512,384]{1,0:T(8,128)(2,1)S(1)}, bf16[2304,896]{1,0:T(8,128)(2,1)}, f32[3,32,256]{2,1,0:T(8,128)S(1)}) custom-call(s32[4]{0:T(128)S(1)} %get-tuple-element.655.low_ref, s32[4]{0:T(128)S(1)} %get-tuple-element.654.high_ref, bf16[512,384]{1,0:T(8,128)(2,1)S(1)} %slice.276.refs_0_, ...), custom_call_target="tpu_custom_call" | custom-call | flops 4529848320 | bytes 12582912 | tf_op jit(solution)/shard_map/attend_backward/pallas_call | solution.py:346
  667.1 12.4 collective-permute-start.11
  683.1 21.2 %collective-permute-start.13 = (bf16[288,896]{1,0:T(8,128)(2,1)}, bf16[288,896]{1,0:T(8,128)(2,1)}, u32[]{:S(2)}, u32[]{:S(2)}) collective-permute-start(bf16[288,896]{1,0:T(8,128)(2,1)} %get-tuple-element.575), channel_id=1, source_target_pairs={{2,0},{3,1},{6,4},{7,5},{10,8},{11,9},{14,12},{15,13},{18,16},{19,... | collective-permute-start | bytes 1548296 | tf_op jit(solution)/shard_map/ppermute | solution.py:446
  718.4 20.3 %weight_grads.5 = (bf16[3072,384]{1,0:T(8,128)(2,1)}, bf16[3072,384]{1,0:T(8,128)(2,1)}, bf16[3072,384]{1,0:T(8,128)(2,1)S(1)}, bf16[3072,384]{1,0:T(8,128)(2,1)S(1)}) custom-call(s32[6]{0:T(128)S(1)} %copy-done.61, bf16[6144,512]{1,0:T(8,128)(2,1)S(1)} %copy-done.63, bf16[6144,512]{1,0:T(8,128)(2,1)} %collective-permute-done.8.refs_1_, ...), custom_call_target="tpu_custom_call" | custom-call | flops 9261023232 | bytes 21626880 | tf_op jit(solution)/shard_map/weight_grads/pallas_call | solution.py:771
  741.5 20.7 %weight_grads.4 = (bf16[3072,384]{1,0:T(8,128)(2,1)}, bf16[3072,384]{1,0:T(8,128)(2,1)}, bf16[3072,384]{1,0:T(8,128)(2,1)S(1)}, bf16[3072,384]{1,0:T(8,128)(2,1)}) custom-call(s32[6]{0:T(128)S(1)} %copy-done.61, bf16[6144,512]{1,0:T(8,128)(2,1)S(1)} %copy-done.63, bf16[6144,512]{1,0:T(8,128)(2,1)} %collective-permute-done.8.refs_1_, ...), custom_call_target="tpu_custom_call" | custom-call | flops 9261023232 | bytes 21626880 | tf_op jit(solution)/shard_map/weight_grads/pallas_call | solution.py:771
  771.4 5.7 copy.167
  777.1 5.0 pad_maximum_fusion
  782.2 6.8 copy.168
  789.0 7.0 collective-permute-start.15
  803.6 6.8 copy.169
  810.4 5.1 add_convert_fusion.1
  826.5 7.9 multiply_reduce_fusion.2
  837.2 40.1 %ffn_backward.3 = (f32[512,1472]{1,0:T(8,128)}, bf16[6144,512]{1,0:T(8,128)(2,1)}, bf16[6144,512]{1,0:T(8,128)(2,1)}) custom-call(s32[2]{0:T(128)S(1)} %pad_add_fusion.core_ref, bf16[512,1472]{1,0:T(8,128)(2,1)S(1)} %get-tuple-element.558.refs_0_.refs_4_, bf16[512,1472]{1,0:T(8,128)(2,1)S(1)} %copy-done.1, f32[512,3584]{1,0:T(8,128)} %get-tuple-element.296.refs_2_, ...), custom_call_target="tpu_custom_call" | custom-call | flops 16206790656 | bytes 57344000 | tf_op jit(solution)/shard_map/ffn_backward/pallas_call | solution.py:659
  883.5 4.4 multiply_reduce_fusion.3
  888.2 4.3 fusion.36
  901.3 30.9 %collective-permute-done.16 = bf16[3072,384]{1,0:T(8,128)(2,1)} collective-permute-done((bf16[3072,384]{1,0:T(8,128)(2,1)}, bf16[3072,384]{1,0:T(8,128)(2,1)}, u32[]{:S(2)}, u32[]{:S(2)}) %collective-permute-start.16) | collective-permute-done | bytes 2359328 | tf_op jit(solution)/shard_map/ppermute | solution.py:440
  944.8 23.3 %attend_backward.3 = (bf16[512,384]{1,0:T(8,128)(2,1)S(1)}, bf16[2304,768]{1,0:T(8,128)(2,1)}, f32[3,32,256]{2,1,0:T(8,128)S(1)}) custom-call(s32[4]{0:T(128)S(1)} %get-tuple-element.655.low_ref, s32[4]{0:T(128)S(1)} %get-tuple-element.654.high_ref, bf16[512,384]{1,0:T(8,128)(2,1)S(1)} %copy-done.46, bf16[512,384]{1,0:T(8,128)(2,1)S(1)} %copy-done.68, ...), custom_call_target="tpu_custom_call" | custom-call | flops 4529848320 | bytes 12582912 | tf_op jit(solution)/shard_map/attend_backward/pallas_call | solution.py:346
  977.3 19.5 %collective-permute-start.27 = (bf16[288,768]{1,0:T(8,128)(2,1)S(1)}, bf16[288,768]{1,0:T(8,128)(2,1)S(1)}, u32[]{:S(2)}, u32[]{:S(2)}) collective-permute-start(bf16[288,768]{1,0:T(8,128)(2,1)S(1)} %get-tuple-element.580), channel_id=1, source_target_pairs={{2,0},{3,1},{6,4},{7,5},{10,8},{11,9},{14,12},{15,13},{18,16},{19,... | collective-permute-start | bytes 1327112 | tf_op jit(solution)/shard_map/ppermute | solution.py:446
  996.8 20.1 %weight_grads.7 = (bf16[3072,384]{1,0:T(8,128)(2,1)S(1)}, bf16[3072,384]{1,0:T(8,128)(2,1)}, bf16[3072,384]{1,0:T(8,128)(2,1)S(1)}, bf16[3072,384]{1,0:T(8,128)(2,1)S(1)}) custom-call(s32[6]{0:T(128)S(1)} %copy-done.62, bf16[6144,512]{1,0:T(8,128)(2,1)S(1)} %bitcast.171, bf16[6144,512]{1,0:T(8,128)(2,1)} %collective-permute-done.22.refs_1_, ...), custom_call_target="tpu_custom_call" | custom-call | flops 9261023232 | bytes 21626880 | tf_op jit(solution)/shard_map/weight_grads/pallas_call | solution.py:771
  1022.5 20.7 %weight_grads.6 = (bf16[3072,384]{1,0:T(8,128)(2,1)S(1)}, bf16[3072,384]{1,0:T(8,128)(2,1)}, bf16[3072,384]{1,0:T(8,128)(2,1)S(1)}, bf16[3072,384]{1,0:T(8,128)(2,1)}) custom-call(s32[6]{0:T(128)S(1)} %copy-done.62, bf16[6144,512]{1,0:T(8,128)(2,1)S(1)} %bitcast.171, bf16[6144,512]{1,0:T(8,128)(2,1)} %collective-permute-done.22.refs_1_, ...), custom_call_target="tpu_custom_call" | custom-call | flops 9261023232 | bytes 21626880 | tf_op jit(solution)/shard_map/weight_grads/pallas_call | solution.py:771
  1060.3 5.8 copy.181
  1066.1 4.5 pad_maximum_fusion.1
  1070.7 6.9 copy.182
  1077.6 7.9 collective-permute-start.29
  1089.7 23.9 %collective-permute-done.18 = bf16[1536,384]{1,0:T(8,128)(2,1)} collective-permute-done((bf16[1536,384]{1,0:T(8,128)(2,1)}, bf16[1536,384]{1,0:T(8,128)(2,1)}, u32[]{:S(2)}, u32[]{:S(2)}) %collective-permute-start.18) | collective-permute-done | bytes 1179680 | tf_op jit(solution)/shard_map/ppermute | solution.py:440
  1121.0 6.9 copy.183
  1128.0 6.3 add_convert_fusion
  1137.5 4.3 select_dynamic-update-slice_fusion.2
  1141.8 8.4 fusion.11
  1152.7 6.3 fusion.8
  1165.0 41.9 %collective-permute-done.65 = f32[6,1472]{1,0:T(8,128)S(1)} collective-permute-done((f32[6,1472]{1,0:T(8,128)S(1)}, f32[6,1472]{1,0:T(8,128)S(1)}, u32[]{:S(2)}, u32[]{:S(2)}) %collective-permute-start.65) | collective-permute-done | bytes 35360 | tf_op jit(solution)/shard_map/ppermute | solution.py:505
  1217.3 7.0 collective-permute-done.67
  1232.2 6.7 collective-permute-done.68
  1244.7 5.6 collective-permute-done.41
  1251.8 13.1 collective-permute-done.42
  1268.6 6.4 collective-permute-done.43
  1282.9 33.3 %collective-permute-done.34 = bf16[3072,384]{1,0:T(8,128)(2,1)} collective-permute-done((bf16[3072,384]{1,0:T(8,128)(2,1)}, bf16[3072,384]{1,0:T(8,128)(2,1)}, u32[]{:S(2)}, u32[]{:S(2)}) %collective-permute-start.34) | collective-permute-done | bytes 2359328 | tf_op jit(solution)/shard_map/ppermute | solution.py:440
  1326.2 4.9 collective-permute-start.49
  1338.6 4.3 collective-permute-start.58
  1342.9 19.8 %collective-permute-done.50 = bf16[384,384]{1,0:T(8,128)(2,1)S(1)} collective-permute-done((bf16[384,384]{1,0:T(8,128)(2,1)S(1)}, bf16[384,384]{1,0:T(8,128)(2,1)S(1)}, u32[]{:S(2)}, u32[]{:S(2)}) %collective-permute-start.50) | collective-permute-done | bytes 294944 | tf_op jit(solution)/shard_map/ppermute | solution.py:440
  1362.8 4.8 collective-permute-start.60
  1367.9 4.4 collective-permute-start.62
  1376.2 18.2 %collective-permute-done.59 = bf16[384,384]{1,0:T(8,128)(2,1)S(1)} collective-permute-done((bf16[384,384]{1,0:T(8,128)(2,1)S(1)}, bf16[384,384]{1,0:T(8,128)(2,1)S(1)}, u32[]{:S(2)}, u32[]{:S(2)}) %collective-permute-start.59) | collective-permute-done | bytes 294944 | tf_op jit(solution)/shard_map/ppermute | solution.py:440
  1397.4 9.8 collective-permute-done.62
  1407.2 7.6 collective-permute-start.53
  1421.8 14.4 collective-permute-done.53
  1436.1 23.1 %collective-permute-done.56 = bf16[384,384]{1,0:T(8,128)(2,1)S(1)} collective-permute-done((bf16[384,384]{1,0:T(8,128)(2,1)}, bf16[384,384]{1,0:T(8,128)(2,1)S(1)}, u32[]{:S(2)}, u32[]{:S(2)}) %collective-permute-start.56) | collective-permute-done | bytes 294944 | tf_op jit(solution)/shard_map/ppermute | solution.py:440
  (582 shorter events, 282.5 us)
Async XLA Ops:
  7.2 218.2 %all-gather.3.cloned.1.call-start = ((), (), s32[]{:S(2)}) async-start(), calls=%async_computation | async-start | bytes 38928384 | tf_op jit(solution)/shard_map/all_gather | solution.py:854
  9.7 458.0 %all-gather.5.cloned.1.call-start = ((), (), s32[]{:S(2)}) async-start(), calls=%async_computation.1 | async-start | bytes 38928384 | tf_op jit(solution)/shard_map/all_gather | solution.py:854
  230.7 68.4 %collective-permute-start.1 = (bf16[512,768]{1,0:T(8,128)(2,1)}, bf16[512,768]{1,0:T(8,128)(2,1)}, u32[]{:S(2)}, u32[]{:S(2)}) collective-permute-start(bf16[512,768]{1,0:T(8,128)(2,1)} %slice.272), channel_id=1, source_target_pairs={{0,1},{1,2},{2,3},{4,5},{5,6},{6,7},{8,9},{9,10},{10,11},{12,13},{... | collective-permute-start | bytes 2359304 | tf_op jit(solution)/shard_map/ppermute | solution.py:446
  233.0 64.9 %collective-permute-start = (bf16[288,768]{1,0:T(8,128)(2,1)}, bf16[288,768]{1,0:T(8,128)(2,1)}, u32[]{:S(2)}, u32[]{:S(2)}) collective-permute-start(bf16[288,768]{1,0:T(8,128)(2,1)} %get-tuple-element.637), channel_id=1, source_target_pairs={{0,2},{1,3},{4,6},{5,7},{8,10},{9,11},{12,14},{13,15},{16,18},{17,... | collective-permute-start | bytes 1327112 | tf_op jit(solution)/shard_map/ppermute | solution.py:446
  234.6 65.8 %collective-permute-start.2 = (bf16[512,768]{1,0:T(8,128)(2,1)}, bf16[512,768]{1,0:T(8,128)(2,1)}, u32[]{:S(2)}, u32[]{:S(2)}) collective-permute-start(bf16[512,768]{1,0:T(8,128)(2,1)} %slice.272), channel_id=1, source_target_pairs={{1,0},{2,1},{3,2},{5,4},{6,5},{7,6},{9,8},{10,9},{11,10},{13,12},{... | collective-permute-start | bytes 2359304 | tf_op jit(solution)/shard_map/ppermute | solution.py:446
  246.9 54.8 %collective-permute-start.3 = (bf16[288,768]{1,0:T(8,128)(2,1)}, bf16[288,768]{1,0:T(8,128)(2,1)S(1)}, u32[]{:S(2)}, u32[]{:S(2)}) collective-permute-start(bf16[288,768]{1,0:T(8,128)(2,1)} %get-tuple-element.636), channel_id=1, source_target_pairs={{2,0},{3,1},{6,4},{7,5},{10,8},{11,9},{14,12},{15,13},{18,16},{19,... | collective-permute-start | bytes 1327112 | tf_op jit(solution)/shard_map/ppermute | solution.py:446
  473.3 47.8 %collective-permute-start.5 = (bf16[512,896]{1,0:T(8,128)(2,1)}, bf16[512,896]{1,0:T(8,128)(2,1)}, u32[]{:S(2)}, u32[]{:S(2)}) collective-permute-start(bf16[512,896]{1,0:T(8,128)(2,1)} %pad_maximum_fusion.8), channel_id=1, source_target_pairs={{0,1},{1,2},{2,3},{4,5},{5,6},{6,7},{8,9},{9,10},{10,11},{12,13},{... | collective-permute-start | bytes 2752520 | tf_op jit(solution)/shard_map/ppermute | solution.py:446
  478.3 44.4 %collective-permute-start.6 = (bf16[512,896]{1,0:T(8,128)(2,1)}, bf16[512,896]{1,0:T(8,128)(2,1)S(1)}, u32[]{:S(2)}, u32[]{:S(2)}) collective-permute-start(bf16[512,896]{1,0:T(8,128)(2,1)} %pad_maximum_fusion.8), channel_id=1, source_target_pairs={{1,0},{2,1},{3,2},{5,4},{6,5},{7,6},{9,8},{10,9},{11,10},{13,12},{... | collective-permute-start | bytes 2752520 | tf_op jit(solution)/shard_map/ppermute | solution.py:446
  484.1 37.0 %collective-permute-start.4 = (bf16[288,896]{1,0:T(8,128)(2,1)S(1)}, bf16[288,896]{1,0:T(8,128)(2,1)S(1)}, u32[]{:S(2)}, u32[]{:S(2)}) collective-permute-start(bf16[288,896]{1,0:T(8,128)(2,1)S(1)} %get-tuple-element.639), channel_id=1, source_target_pairs={{0,2},{1,3},{4,6},{5,7},{8,10},{9,11},{12,14},{13,15},{16,18},{17,... | collective-permute-start | bytes 1548296 | tf_op jit(solution)/shard_map/ppermute | solution.py:446
  488.9 33.9 %collective-permute-start.7 = (bf16[288,896]{1,0:T(8,128)(2,1)S(1)}, bf16[288,896]{1,0:T(8,128)(2,1)S(1)}, u32[]{:S(2)}, u32[]{:S(2)}) collective-permute-start(bf16[288,896]{1,0:T(8,128)(2,1)S(1)} %get-tuple-element.638), channel_id=1, source_target_pairs={{2,0},{3,1},{6,4},{7,5},{10,8},{11,9},{14,12},{15,13},{18,16},{19,... | collective-permute-start | bytes 1548296 | tf_op jit(solution)/shard_map/ppermute | solution.py:446
  609.2 100.8 %collective-permute-start.8 = (bf16[6144,512]{1,0:T(8,128)(2,1)}, bf16[6144,512]{1,0:T(8,128)(2,1)}, u32[]{:S(2)}, u32[]{:S(2)}) collective-permute-start(bf16[6144,512]{1,0:T(8,128)(2,1)} %get-tuple-element.261), channel_id=1, source_target_pairs={{0,4},{4,0},{1,5},{5,1},{2,6},{6,2},{3,7},{7,3},{8,12},{12,8},{9,1... | collective-permute-start | bytes 18874376 | tf_op jit(solution)/shard_map/ppermute | solution.py:440
  627.1 79.0 %collective-permute-start.9 = (bf16[512,1472]{0,1:T(8,128)(2,1)}, bf16[512,1472]{0,1:T(8,128)(2,1)}, u32[]{:S(2)}, u32[]{:S(2)}) collective-permute-start(bf16[512,1472]{0,1:T(8,128)(2,1)} %copy.160), channel_id=1, source_target_pairs={{0,4},{4,0},{1,5},{5,1},{2,6},{6,2},{3,7},{7,3},{8,12},{12,8},{9,1... | collective-permute-start | bytes 4521992 | tf_op jit(solution)/shard_map/ppermute | solution.py:440
  667.1 95.1 %collective-permute-start.11 = (bf16[512,896]{1,0:T(8,128)(2,1)}, bf16[512,896]{1,0:T(8,128)(2,1)}, u32[]{:S(2)}, u32[]{:S(2)}) collective-permute-start(bf16[512,896]{1,0:T(8,128)(2,1)} %get-tuple-element.577), channel_id=1, source_target_pairs={{1,0},{2,1},{3,2},{5,4},{6,5},{7,6},{9,8},{10,9},{11,10},{13,12},{... | collective-permute-start | bytes 2752520 | tf_op jit(solution)/shard_map/ppermute | solution.py:446
  679.5 82.7 %collective-permute-start.12 = (bf16[512,896]{1,0:T(8,128)(2,1)}, bf16[512,896]{1,0:T(8,128)(2,1)}, u32[]{:S(2)}, u32[]{:S(2)}) collective-permute-start(bf16[512,896]{1,0:T(8,128)(2,1)} %get-tuple-element.576), channel_id=1, source_target_pairs={{0,1},{1,2},{2,3},{4,5},{5,6},{6,7},{8,9},{9,10},{10,11},{12,13},{... | collective-permute-start | bytes 2752520 | tf_op jit(solution)/shard_map/ppermute | solution.py:446
  683.1 79.1 %collective-permute-start.13 = (bf16[288,896]{1,0:T(8,128)(2,1)}, bf16[288,896]{1,0:T(8,128)(2,1)}, u32[]{:S(2)}, u32[]{:S(2)}) collective-permute-start(bf16[288,896]{1,0:T(8,128)(2,1)} %get-tuple-element.575), channel_id=1, source_target_pairs={{2,0},{3,1},{6,4},{7,5},{10,8},{11,9},{14,12},{15,13},{18,16},{19,... | collective-permute-start | bytes 1548296 | tf_op jit(solution)/shard_map/ppermute | solution.py:446
  706.1 56.1 %collective-permute-start.14 = (bf16[288,896]{1,0:T(8,128)(2,1)}, bf16[288,896]{1,0:T(8,128)(2,1)}, u32[]{:S(2)}, u32[]{:S(2)}) collective-permute-start(bf16[288,896]{1,0:T(8,128)(2,1)} %get-tuple-element.574), channel_id=1, source_target_pairs={{0,2},{1,3},{4,6},{5,7},{8,10},{9,11},{12,14},{13,15},{16,18},{17,... | collective-permute-start | bytes 1548296 | tf_op jit(solution)/shard_map/ppermute | solution.py:446
  789.0 14.6 collective-permute-start.15
  800.1 79.6 %collective-permute-start.23 = (bf16[512,1472]{0,1:T(8,128)(2,1)}, bf16[512,1472]{0,1:T(8,128)(2,1)}, u32[]{:S(2)}, u32[]{:S(2)}) collective-permute-start(bf16[512,1472]{0,1:T(8,128)(2,1)} %copy.174), channel_id=1, source_target_pairs={{0,4},{4,0},{1,5},{5,1},{2,6},{6,2},{3,7},{7,3},{8,12},{12,8},{9,1... | collective-permute-start | bytes 4521992 | tf_op jit(solution)/shard_map/ppermute | solution.py:440
  877.3 99.9 %collective-permute-start.22 = (bf16[6144,512]{1,0:T(8,128)(2,1)}, bf16[6144,512]{1,0:T(8,128)(2,1)}, u32[]{:S(2)}, u32[]{:S(2)}) collective-permute-start(bf16[6144,512]{1,0:T(8,128)(2,1)} %get-tuple-element.320), channel_id=1, source_target_pairs={{0,4},{4,0},{1,5},{5,1},{2,6},{6,2},{3,7},{7,3},{8,12},{12,8},{9,1... | collective-permute-start | bytes 18874376 | tf_op jit(solution)/shard_map/ppermute | solution.py:440
  877.8 54.4 %collective-permute-start.16 = (bf16[3072,384]{1,0:T(8,128)(2,1)}, bf16[3072,384]{1,0:T(8,128)(2,1)}, u32[]{:S(2)}, u32[]{:S(2)}) collective-permute-start(bf16[3072,384]{1,0:T(8,128)(2,1)} %select_dynamic-update-slice_fusion.14), channel_id=1, source_target_pairs={{0,16},{16,0},{1,17},{17,1},{2,18},{18,2},{3,19},{19,3},{4,20},{20... | collective-permute-start | bytes 7077896 | tf_op jit(solution)/shard_map/ppermute | solution.py:440
  879.7 54.5 %collective-permute-start.17 = (bf16[3072,384]{1,0:T(8,128)(2,1)}, bf16[3072,384]{1,0:T(8,128)(2,1)}, u32[]{:S(2)}, u32[]{:S(2)}) collective-permute-start(bf16[3072,384]{1,0:T(8,128)(2,1)} %get-tuple-element.292), channel_id=1, source_target_pairs={{0,8},{8,0},{1,9},{9,1},{2,10},{10,2},{3,11},{11,3},{4,12},{12,4},... | collective-permute-start | bytes 7077896 | tf_op jit(solution)/shard_map/ppermute | solution.py:440
  883.4 13.3 collective-permute-start.24
  887.9 133.3 %collective-permute-start.20 = (bf16[3072,384]{1,0:T(8,128)(2,1)}, bf16[3072,384]{1,0:T(8,128)(2,1)}, u32[]{:S(2)}, u32[]{:S(2)}) collective-permute-start(bf16[3072,384]{1,0:T(8,128)(2,1)} %get-tuple-element.314), channel_id=1, source_target_pairs={{0,16},{16,0},{1,17},{17,1},{2,18},{18,2},{3,19},{19,3},{4,20},{20... | collective-permute-start | bytes 7077896 | tf_op jit(solution)/shard_map/ppermute | solution.py:440
  896.7 146.5 %collective-permute-start.21 = (bf16[3072,384]{1,0:T(8,128)(2,1)}, bf16[3072,384]{1,0:T(8,128)(2,1)}, u32[]{:S(2)}, u32[]{:S(2)}) collective-permute-start(bf16[3072,384]{1,0:T(8,128)(2,1)} %get-tuple-element.316), channel_id=1, source_target_pairs={{0,8},{8,0},{1,9},{9,1},{2,10},{10,2},{3,11},{11,3},{4,12},{12,4},... | collective-permute-start | bytes 7077896 | tf_op jit(solution)/shard_map/ppermute | solution.py:440
  970.0 74.8 %collective-permute-start.25 = (bf16[512,768]{1,0:T(8,128)(2,1)S(1)}, bf16[512,768]{1,0:T(8,128)(2,1)S(1)}, u32[]{:S(2)}, u32[]{:S(2)}) collective-permute-start(bf16[512,768]{1,0:T(8,128)(2,1)S(1)} %get-tuple-element.582), channel_id=1, source_target_pairs={{1,0},{2,1},{3,2},{5,4},{6,5},{7,6},{9,8},{10,9},{11,10},{13,12},{... | collective-permute-start | bytes 2359304 | tf_op jit(solution)/shard_map/ppermute | solution.py:446
  972.9 72.0 %collective-permute-start.26 = (bf16[512,768]{1,0:T(8,128)(2,1)S(1)}, bf16[512,768]{1,0:T(8,128)(2,1)S(1)}, u32[]{:S(2)}, u32[]{:S(2)}) collective-permute-start(bf16[512,768]{1,0:T(8,128)(2,1)S(1)} %get-tuple-element.581), channel_id=1, source_target_pairs={{0,1},{1,2},{2,3},{4,5},{5,6},{6,7},{8,9},{9,10},{10,11},{12,13},{... | collective-permute-start | bytes 2359304 | tf_op jit(solution)/shard_map/ppermute | solution.py:446
  977.3 66.0 %collective-permute-start.27 = (bf16[288,768]{1,0:T(8,128)(2,1)S(1)}, bf16[288,768]{1,0:T(8,128)(2,1)S(1)}, u32[]{:S(2)}, u32[]{:S(2)}) collective-permute-start(bf16[288,768]{1,0:T(8,128)(2,1)S(1)} %get-tuple-element.580), channel_id=1, source_target_pairs={{2,0},{3,1},{6,4},{7,5},{10,8},{11,9},{14,12},{15,13},{18,16},{19,... | collective-permute-start | bytes 1327112 | tf_op jit(solution)/shard_map/ppermute | solution.py:446
  1021.2 23.6 %collective-permute-start.28 = (bf16[288,768]{1,0:T(8,128)(2,1)S(1)}, bf16[288,768]{1,0:T(8,128)(2,1)S(1)}, u32[]{:S(2)}, u32[]{:S(2)}) collective-permute-start(bf16[288,768]{1,0:T(8,128)(2,1)S(1)} %get-tuple-element.579), channel_id=1, source_target_pairs={{0,2},{1,3},{4,6},{5,7},{8,10},{9,11},{12,14},{13,15},{16,18},{17,... | collective-permute-start | bytes 1327112 | tf_op jit(solution)/shard_map/ppermute | solution.py:446
  1077.6 43.4 %collective-permute-start.29 = (bf16[1536,1472]{0,1:T(8,128)(2,1)}, bf16[1536,1472]{0,1:T(8,128)(2,1)}, u32[]{:S(2)}, u32[]{:S(2)}) collective-permute-start(bf16[1536,1472]{0,1:T(8,128)(2,1)} %copy.182), channel_id=1, source_target_pairs={{0,4},{4,0},{1,5},{5,1},{2,6},{6,2},{3,7},{7,3},{8,12},{12,8},{9,1... | collective-permute-start | bytes 13565960 | tf_op jit(solution)/shard_map/ppermute | solution.py:440
  1085.4 28.2 %collective-permute-start.18 = (bf16[1536,384]{1,0:T(8,128)(2,1)}, bf16[1536,384]{1,0:T(8,128)(2,1)}, u32[]{:S(2)}, u32[]{:S(2)}) collective-permute-start(bf16[1536,384]{1,0:T(8,128)(2,1)} %get-tuple-element.307), channel_id=1, source_target_pairs={{0,8},{8,0},{1,9},{9,1},{2,10},{10,2},{3,11},{11,3},{4,12},{12,4},... | collective-permute-start | bytes 3538952 | tf_op jit(solution)/shard_map/ppermute | solution.py:440
  1085.4 28.3 %collective-permute-start.19 = (bf16[1536,384]{1,0:T(8,128)(2,1)}, bf16[1536,384]{1,0:T(8,128)(2,1)}, u32[]{:S(2)}, u32[]{:S(2)}) collective-permute-start(bf16[1536,384]{1,0:T(8,128)(2,1)} %get-tuple-element.309), channel_id=1, source_target_pairs={{0,16},{16,0},{1,17},{17,1},{2,18},{18,2},{3,19},{19,3},{4,20},{20... | collective-permute-start | bytes 3538952 | tf_op jit(solution)/shard_map/ppermute | solution.py:440
  1113.7 45.2 %collective-permute-start.32 = (bf16[1536,384]{1,0:T(8,128)(2,1)}, bf16[1536,384]{1,0:T(8,128)(2,1)}, u32[]{:S(2)}, u32[]{:S(2)}) collective-permute-start(bf16[1536,384]{1,0:T(8,128)(2,1)} %get-tuple-element.369), channel_id=1, source_target_pairs={{0,8},{8,0},{1,9},{9,1},{2,10},{10,2},{3,11},{11,3},{4,12},{12,4},... | collective-permute-start | bytes 3538952 | tf_op jit(solution)/shard_map/ppermute | solution.py:440
  1115.4 43.6 %collective-permute-start.33 = (bf16[1536,384]{1,0:T(8,128)(2,1)}, bf16[1536,384]{1,0:T(8,128)(2,1)}, u32[]{:S(2)}, u32[]{:S(2)}) collective-permute-start(bf16[1536,384]{1,0:T(8,128)(2,1)} %get-tuple-element.371), channel_id=1, source_target_pairs={{0,16},{16,0},{1,17},{17,1},{2,18},{18,2},{3,19},{19,3},{4,20},{20... | collective-permute-start | bytes 3538952 | tf_op jit(solution)/shard_map/ppermute | solution.py:440
  1150.5 76.4 %collective-permute-start.30 = (bf16[3072,384]{1,0:T(8,128)(2,1)}, bf16[3072,384]{1,0:T(8,128)(2,1)S(1)}, u32[]{:S(2)}, u32[]{:S(2)}) collective-permute-start(bf16[3072,384]{1,0:T(8,128)(2,1)} %select_dynamic-update-slice_fusion.6), channel_id=1, source_target_pairs={{0,16},{16,0},{1,17},{17,1},{2,18},{18,2},{3,19},{19,3},{4,20},{20... | collective-permute-start | bytes 7077896 | tf_op jit(solution)/shard_map/ppermute | solution.py:440
  1152.3 74.8 %collective-permute-start.31 = (bf16[3072,384]{1,0:T(8,128)(2,1)}, bf16[3072,384]{1,0:T(8,128)(2,1)S(1)}, u32[]{:S(2)}, u32[]{:S(2)}) collective-permute-start(bf16[3072,384]{1,0:T(8,128)(2,1)} %copy-done.49), channel_id=1, source_target_pairs={{0,8},{8,0},{1,9},{9,1},{2,10},{10,2},{3,11},{11,3},{4,12},{12,4},... | collective-permute-start | bytes 7077896 | tf_op jit(solution)/shard_map/ppermute | solution.py:440
  1162.3 44.6 %collective-permute-start.65 = (f32[6,1472]{1,0:T(8,128)S(1)}, f32[6,1472]{1,0:T(8,128)S(1)}, u32[]{:S(2)}, u32[]{:S(2)}) collective-permute-start(f32[6,1472]{1,0:T(8,128)S(1)} %add.632), channel_id=1, source_target_pairs={{0,8},{8,0},{1,9},{9,1},{2,10},{10,2},{3,11},{11,3},{4,12},{12,4},... | collective-permute-start | bytes 105992 | tf_op jit(solution)/shard_map/ppermute | solution.py:505
  1208.3 32.3 %collective-permute-start.38 = (bf16[384,384]{1,0:T(8,128)(2,1)S(1)}, bf16[384,384]{1,0:T(8,128)(2,1)}, u32[]{:S(2)}, u32[]{:S(2)}) collective-permute-start(bf16[384,384]{1,0:T(8,128)(2,1)S(1)} %copy-done.115), channel_id=1, source_target_pairs={{0,1},{1,2},{2,3},{3,0},{4,5},{5,6},{6,7},{7,4},{8,9},{9,10},{10,1... | collective-permute-start | bytes 884744 | tf_op jit(solution)/shard_map/ppermute | solution.py:440
  1211.4 29.6 %collective-permute-start.39 = (bf16[384,384]{1,0:T(8,128)(2,1)S(1)}, bf16[384,384]{1,0:T(8,128)(2,1)}, u32[]{:S(2)}, u32[]{:S(2)}) collective-permute-start(bf16[384,384]{1,0:T(8,128)(2,1)S(1)} %copy-done.114), channel_id=1, source_target_pairs={{0,2},{1,3},{2,0},{3,1},{4,6},{5,7},{6,4},{7,5},{8,10},{9,11},{10,... | collective-permute-start | bytes 884744 | tf_op jit(solution)/shard_map/ppermute | solution.py:440
  1211.9 12.5 collective-permute-start.67
  1224.4 16.9 %collective-permute-start.40 = (bf16[384,384]{1,0:T(8,128)(2,1)S(1)}, bf16[384,384]{1,0:T(8,128)(2,1)}, u32[]{:S(2)}, u32[]{:S(2)}) collective-permute-start(bf16[384,384]{1,0:T(8,128)(2,1)S(1)} %copy-done.113), channel_id=1, source_target_pairs={{0,3},{1,0},{2,1},{3,2},{4,7},{5,4},{6,5},{7,6},{8,11},{9,8},{10,9... | collective-permute-start | bytes 884744 | tf_op jit(solution)/shard_map/ppermute | solution.py:440
  1231.8 44.9 %collective-permute-start.36 = (bf16[1536,384]{1,0:T(8,128)(2,1)}, bf16[1536,384]{1,0:T(8,128)(2,1)}, u32[]{:S(2)}, u32[]{:S(2)}) collective-permute-start(bf16[1536,384]{1,0:T(8,128)(2,1)} %get-tuple-element.394), channel_id=1, source_target_pairs={{0,8},{8,0},{1,9},{9,1},{2,10},{10,2},{3,11},{11,3},{4,12},{12,4},... | collective-permute-start | bytes 3538952 | tf_op jit(solution)/shard_map/ppermute | solution.py:440
  1238.9 37.8 %collective-permute-start.37 = (bf16[1536,384]{1,0:T(8,128)(2,1)}, bf16[1536,384]{1,0:T(8,128)(2,1)}, u32[]{:S(2)}, u32[]{:S(2)}) collective-permute-start(bf16[1536,384]{1,0:T(8,128)(2,1)} %get-tuple-element.396), channel_id=1, source_target_pairs={{0,16},{16,0},{1,17},{17,1},{2,18},{18,2},{3,19},{19,3},{4,20},{20... | collective-permute-start | bytes 3538952 | tf_op jit(solution)/shard_map/ppermute | solution.py:440
  1240.6 75.6 %collective-permute-start.34 = (bf16[3072,384]{1,0:T(8,128)(2,1)}, bf16[3072,384]{1,0:T(8,128)(2,1)}, u32[]{:S(2)}, u32[]{:S(2)}) collective-permute-start(bf16[3072,384]{1,0:T(8,128)(2,1)} %get-tuple-element.390), channel_id=1, source_target_pairs={{0,16},{16,0},{1,17},{17,1},{2,18},{18,2},{3,19},{19,3},{4,20},{20... | collective-permute-start | bytes 7077896 | tf_op jit(solution)/shard_map/ppermute | solution.py:440
  1240.9 75.3 %collective-permute-start.35 = (bf16[3072,384]{1,0:T(8,128)(2,1)}, bf16[3072,384]{1,0:T(8,128)(2,1)}, u32[]{:S(2)}, u32[]{:S(2)}) collective-permute-start(bf16[3072,384]{1,0:T(8,128)(2,1)} %get-tuple-element.392), channel_id=1, source_target_pairs={{0,8},{8,0},{1,9},{9,1},{2,10},{10,2},{3,11},{11,3},{4,12},{12,4},... | collective-permute-start | bytes 7077896 | tf_op jit(solution)/shard_map/ppermute | solution.py:440
  1250.4 14.5 collective-permute-start.42
  1275.0 51.2 %collective-permute-start.46 = (bf16[384,384]{1,0:T(8,128)(2,1)}, bf16[384,384]{1,0:T(8,128)(2,1)S(1)}, u32[]{:S(2)}, u32[]{:S(2)}) collective-permute-start(bf16[384,384]{1,0:T(8,128)(2,1)} %get-tuple-element.423), channel_id=1, source_target_pairs={{0,1},{1,2},{2,3},{3,0},{4,5},{5,6},{6,7},{7,4},{8,9},{9,10},{10,1... | collective-permute-start | bytes 884744 | tf_op jit(solution)/shard_map/ppermute | solution.py:440
  1276.7 54.4 %collective-permute-start.47 = (bf16[384,384]{1,0:T(8,128)(2,1)}, bf16[384,384]{1,0:T(8,128)(2,1)S(1)}, u32[]{:S(2)}, u32[]{:S(2)}) collective-permute-start(bf16[384,384]{1,0:T(8,128)(2,1)} %get-tuple-element.424), channel_id=1, source_target_pairs={{0,2},{1,3},{2,0},{3,1},{4,6},{5,7},{6,4},{7,5},{8,10},{9,11},{10,... | collective-permute-start | bytes 884744 | tf_op jit(solution)/shard_map/ppermute | solution.py:440
  1276.7 54.4 %collective-permute-start.48 = (bf16[384,384]{1,0:T(8,128)(2,1)}, bf16[384,384]{1,0:T(8,128)(2,1)S(1)}, u32[]{:S(2)}, u32[]{:S(2)}) collective-permute-start(bf16[384,384]{1,0:T(8,128)(2,1)} %get-tuple-element.425), channel_id=1, source_target_pairs={{0,3},{1,0},{2,1},{3,2},{4,7},{5,4},{6,5},{7,6},{8,11},{9,8},{10,9... | collective-permute-start | bytes 884744 | tf_op jit(solution)/shard_map/ppermute | solution.py:440
  1323.5 44.4 %collective-permute-start.44 = (bf16[1536,384]{1,0:T(8,128)(2,1)S(1)}, bf16[1536,384]{1,0:T(8,128)(2,1)S(1)}, u32[]{:S(2)}, u32[]{:S(2)}) collective-permute-start(bf16[1536,384]{1,0:T(8,128)(2,1)S(1)} %get-tuple-element.419), channel_id=1, source_target_pairs={{0,8},{8,0},{1,9},{9,1},{2,10},{10,2},{3,11},{11,3},{4,12},{12,4},... | collective-permute-start | bytes 3538952 | tf_op jit(solution)/shard_map/ppermute | solution.py:440
  1323.9 44.0 %collective-permute-start.45 = (bf16[1536,384]{1,0:T(8,128)(2,1)S(1)}, bf16[1536,384]{1,0:T(8,128)(2,1)S(1)}, u32[]{:S(2)}, u32[]{:S(2)}) collective-permute-start(bf16[1536,384]{1,0:T(8,128)(2,1)S(1)} %get-tuple-element.421), channel_id=1, source_target_pairs={{0,16},{16,0},{1,17},{17,1},{2,18},{18,2},{3,19},{19,3},{4,20},{20... | collective-permute-start | bytes 3538952 | tf_op jit(solution)/shard_map/ppermute | solution.py:440
  1331.1 31.7 %collective-permute-start.50 = (bf16[384,384]{1,0:T(8,128)(2,1)S(1)}, bf16[384,384]{1,0:T(8,128)(2,1)S(1)}, u32[]{:S(2)}, u32[]{:S(2)}) collective-permute-start(bf16[384,384]{1,0:T(8,128)(2,1)S(1)} %copy-done.109), channel_id=1, source_target_pairs={{0,2},{1,3},{2,0},{3,1},{4,6},{5,7},{6,4},{7,5},{8,10},{9,11},{10,... | collective-permute-start | bytes 884744 | tf_op jit(solution)/shard_map/ppermute | solution.py:440
  1331.1 31.6 %collective-permute-start.51 = (bf16[384,384]{1,0:T(8,128)(2,1)S(1)}, bf16[384,384]{1,0:T(8,128)(2,1)S(1)}, u32[]{:S(2)}, u32[]{:S(2)}) collective-permute-start(bf16[384,384]{1,0:T(8,128)(2,1)S(1)} %copy-done.108), channel_id=1, source_target_pairs={{0,3},{1,0},{2,1},{3,2},{4,7},{5,4},{6,5},{7,6},{8,11},{9,8},{10,9... | collective-permute-start | bytes 884744 | tf_op jit(solution)/shard_map/ppermute | solution.py:440
  1338.6 36.3 %collective-permute-start.58 = (bf16[384,384]{1,0:T(8,128)(2,1)S(1)}, bf16[384,384]{1,0:T(8,128)(2,1)S(1)}, u32[]{:S(2)}, u32[]{:S(2)}) collective-permute-start(bf16[384,384]{1,0:T(8,128)(2,1)S(1)} %get-tuple-element.446), channel_id=1, source_target_pairs={{0,1},{1,2},{2,3},{3,0},{4,5},{5,6},{6,7},{7,4},{8,9},{9,10},{10,1... | collective-permute-start | bytes 884744 | tf_op jit(solution)/shard_map/ppermute | solution.py:440
  1362.8 31.6 %collective-permute-start.59 = (bf16[384,384]{1,0:T(8,128)(2,1)S(1)}, bf16[384,384]{1,0:T(8,128)(2,1)S(1)}, u32[]{:S(2)}, u32[]{:S(2)}) collective-permute-start(bf16[384,384]{1,0:T(8,128)(2,1)S(1)} %get-tuple-element.447), channel_id=1, source_target_pairs={{0,2},{1,3},{2,0},{3,1},{4,6},{5,7},{6,4},{7,5},{8,10},{9,11},{10,... | collective-permute-start | bytes 884744 | tf_op jit(solution)/shard_map/ppermute | solution.py:440
  1362.8 34.6 %collective-permute-start.60 = (bf16[384,384]{1,0:T(8,128)(2,1)}, bf16[384,384]{1,0:T(8,128)(2,1)}, u32[]{:S(2)}, u32[]{:S(2)}) collective-permute-start(bf16[384,384]{1,0:T(8,128)(2,1)} %get-tuple-element.448), channel_id=1, source_target_pairs={{0,3},{1,0},{2,1},{3,2},{4,7},{5,4},{6,5},{7,6},{8,11},{9,8},{10,9... | collective-permute-start | bytes 884744 | tf_op jit(solution)/shard_map/ppermute | solution.py:440
  1367.8 29.5 %collective-permute-start.61 = (bf16[384,384]{1,0:T(8,128)(2,1)}, bf16[384,384]{1,0:T(8,128)(2,1)}, u32[]{:S(2)}, u32[]{:S(2)}) collective-permute-start(bf16[384,384]{1,0:T(8,128)(2,1)} %get-tuple-element.450), channel_id=1, source_target_pairs={{0,1},{1,2},{2,3},{3,0},{4,5},{5,6},{6,7},{7,4},{8,9},{9,10},{10,1... | collective-permute-start | bytes 884744 | tf_op jit(solution)/shard_map/ppermute | solution.py:440
  1367.9 39.3 %collective-permute-start.62 = (bf16[384,384]{1,0:T(8,128)(2,1)}, bf16[384,384]{1,0:T(8,128)(2,1)}, u32[]{:S(2)}, u32[]{:S(2)}) collective-permute-start(bf16[384,384]{1,0:T(8,128)(2,1)} %get-tuple-element.451), channel_id=1, source_target_pairs={{0,2},{1,3},{2,0},{3,1},{4,6},{5,7},{6,4},{7,5},{8,10},{9,11},{10,... | collective-permute-start | bytes 884744 | tf_op jit(solution)/shard_map/ppermute | solution.py:440
  1374.9 32.3 %collective-permute-start.63 = (bf16[384,384]{1,0:T(8,128)(2,1)}, bf16[384,384]{1,0:T(8,128)(2,1)}, u32[]{:S(2)}, u32[]{:S(2)}) collective-permute-start(bf16[384,384]{1,0:T(8,128)(2,1)} %get-tuple-element.452), channel_id=1, source_target_pairs={{0,3},{1,0},{2,1},{3,2},{4,7},{5,4},{6,5},{7,6},{8,11},{9,8},{10,9... | collective-permute-start | bytes 884744 | tf_op jit(solution)/shard_map/ppermute | solution.py:440
  1395.1 23.5 %collective-permute-start.52 = (bf16[384,384]{1,0:T(8,128)(2,1)}, bf16[384,384]{1,0:T(8,128)(2,1)}, u32[]{:S(2)}, u32[]{:S(2)}) collective-permute-start(bf16[384,384]{1,0:T(8,128)(2,1)} %get-tuple-element.438), channel_id=1, source_target_pairs={{0,1},{1,2},{2,3},{3,0},{4,5},{5,6},{6,7},{7,4},{8,9},{9,10},{10,1... | collective-permute-start | bytes 884744 | tf_op jit(solution)/shard_map/ppermute | solution.py:440
  1407.2 29.0 %collective-permute-start.53 = (bf16[384,384]{1,0:T(8,128)(2,1)}, bf16[384,384]{1,0:T(8,128)(2,1)S(1)}, u32[]{:S(2)}, u32[]{:S(2)}) collective-permute-start(bf16[384,384]{1,0:T(8,128)(2,1)} %get-tuple-element.439), channel_id=1, source_target_pairs={{0,2},{1,3},{2,0},{3,1},{4,6},{5,7},{6,4},{7,5},{8,10},{9,11},{10,... | collective-permute-start | bytes 884744 | tf_op jit(solution)/shard_map/ppermute | solution.py:440
  1414.8 21.3 %collective-permute-start.54 = (bf16[384,384]{1,0:T(8,128)(2,1)}, bf16[384,384]{1,0:T(8,128)(2,1)S(1)}, u32[]{:S(2)}, u32[]{:S(2)}) collective-permute-start(bf16[384,384]{1,0:T(8,128)(2,1)} %get-tuple-element.440), channel_id=1, source_target_pairs={{0,3},{1,0},{2,1},{3,2},{4,7},{5,4},{6,5},{7,6},{8,11},{9,8},{10,9... | collective-permute-start | bytes 884744 | tf_op jit(solution)/shard_map/ppermute | solution.py:440
  1414.8 21.3 %collective-permute-start.55 = (bf16[384,384]{1,0:T(8,128)(2,1)}, bf16[384,384]{1,0:T(8,128)(2,1)S(1)}, u32[]{:S(2)}, u32[]{:S(2)}) collective-permute-start(bf16[384,384]{1,0:T(8,128)(2,1)} %get-tuple-element.442), channel_id=1, source_target_pairs={{0,1},{1,2},{2,3},{3,0},{4,5},{5,6},{6,7},{7,4},{8,9},{9,10},{10,1... | collective-permute-start | bytes 884744 | tf_op jit(solution)/shard_map/ppermute | solution.py:440
  1418.6 40.6 %collective-permute-start.56 = (bf16[384,384]{1,0:T(8,128)(2,1)}, bf16[384,384]{1,0:T(8,128)(2,1)S(1)}, u32[]{:S(2)}, u32[]{:S(2)}) collective-permute-start(bf16[384,384]{1,0:T(8,128)(2,1)} %get-tuple-element.443), channel_id=1, source_target_pairs={{0,2},{1,3},{2,0},{3,1},{4,6},{5,7},{6,4},{7,5},{8,10},{9,11},{10,... | collective-permute-start | bytes 884744 | tf_op jit(solution)/shard_map/ppermute | solution.py:440
  1418.6 40.6 %collective-permute-start.57 = (bf16[384,384]{1,0:T(8,128)(2,1)}, bf16[384,384]{1,0:T(8,128)(2,1)S(1)}, u32[]{:S(2)}, u32[]{:S(2)}) collective-permute-start(bf16[384,384]{1,0:T(8,128)(2,1)} %get-tuple-element.444), channel_id=1, source_target_pairs={{0,3},{1,0},{2,1},{3,2},{4,7},{5,4},{6,5},{7,6},{8,11},{9,8},{10,9... | collective-permute-start | bytes 884744 | tf_op jit(solution)/shard_map/ppermute | solution.py:440
  (164 other events, 3257.7 us)
Sparse Core Ops, SparseCore 0:
  11.4 213.9 all-gather.2
  228.8 238.8 all-gather.4

commit v5 on v4

--- a/solution.py
+++ b/solution.py
@@ -21,6 +21,7 @@
 ATTENTION_TILES = 4 * INNER // TILE
 OFFSETS = 5
 CHUNK = 384
+PADDED = 1536
 FORWARD_TILE = 512
 CUTS = (0, 384, 768, 1152, 1472)
 DEVICES = ("y", "x", "c", "z")
@@ -446,6 +447,21 @@
     return lax.ppermute(value, "z", pairs)
 
 
+def far_pair(near_start, near_end, distance):
+    count = lax.axis_size("z")
+    first_half = lax.axis_index("z") < distance
+    sent = jnp.where(first_half, near_end, near_start)
+    pairs = [(i, (i + distance) % count) for i in range(count)]
+    got = lax.ppermute(sent, "z", pairs)
+    return got
+
+
+def far_split(got, distance):
+    first_half = lax.axis_index("z") < distance
+    none = jnp.zeros_like(got)
+    return jnp.where(first_half, none, got), jnp.where(first_half, got, none)
+
+
 def halo_pieces(tokens):
     pieces = []
     distance, covered = 1, 0
@@ -462,8 +478,13 @@
     before, after = [], []
     for distance, span, needed in halo_pieces(tokens):
         if distance < lax.axis_size("z"):
-            left = slide(own[tokens - needed :], distance)
-            right = slide(own[:needed], -distance)
+            if 2 * distance == lax.axis_size("z"):
+                left, right = far_split(
+                    far_pair(own[:needed], own[tokens - needed :], distance), distance
+                )
+            else:
+                left = slide(own[tokens - needed :], distance)
+                right = slide(own[:needed], -distance)
             before.append(jnp.pad(left, ((span - needed, 0), (0, 0))))
             after.append(jnp.pad(right, ((0, span - needed), (0, 0))))
         else:
@@ -480,9 +501,12 @@
         if distance < lax.axis_size("z"):
             left_end = HALO - covered
             right_start = HALO + tokens + covered
-            back = slide(window[left_end - needed : left_end], -distance)
-            ahead = slide(window[right_start : right_start + needed], distance)
-            moved.append((back, ahead))
+            left = window[left_end - needed : left_end]
+            right = window[right_start : right_start + needed]
+            if 2 * distance == lax.axis_size("z"):
+                moved.append((far_pair(left, right, distance),))
+            else:
+                moved.append((slide(left, -distance), slide(right, distance)))
         covered += span
     return window[HALO : HALO + tokens], moved
 
@@ -490,21 +514,20 @@
 def finish_back(own, moved):
     tokens = own.shape[0]
     total = own.astype(jnp.float32)
-    for back, ahead in moved:
+    for distance, pair in enumerate(moved, 1):
+        if len(pair) == 1:
+            ahead, back = far_split(pair[0], distance)
+        else:
+            back, ahead = pair
         needed = back.shape[0]
         total = total + jnp.pad(back.astype(jnp.float32), ((tokens - needed, 0), (0, 0)))
         total = total + jnp.pad(ahead.astype(jnp.float32), ((0, tokens - needed), (0, 0)))
     return total
 
 
-def sum_everywhere(value):
-    for axis in ("c", "x", "y", "z"):
-        count = lax.axis_size(axis)
-        bit = 1
-        while bit < count:
-            value = value + lax.ppermute(value, axis, [(i, i ^ bit) for i in range(count)])
-            bit *= 2
-    return value
+def hop(value, axis, bit=1):
+    pairs = [(i, i ^ bit) for i in range(lax.axis_size(axis))]
+    return value + lax.ppermute(value, axis, pairs)
 
 
 def pick(value, index, axis):
@@ -685,7 +708,7 @@
     normed_refs, branch_refs = refs[2:4], refs[4:6]
     outs = refs[6:]
     step = pl.program_id(0)
-    count = len(outs) // 2
+    count = max(len(outs) // 2, 1)
     per_place = pl.num_programs(0) // count
     source = weight_source(route, tile, step, place_ref)
     unit = place_ref[3]
@@ -693,6 +716,10 @@
     first, second = 4 * INNER // tile, (4 * INNER + 2 * FF) // tile
 
     def put(product_of):
+        if route == "all":
+            outs[0][:, : CUTS[-1]] = product_of(slice(0, CUTS[-1])).astype(jnp.bfloat16)
+            outs[0][:, CUTS[-1] :] = jnp.zeros((tile, PADDED - CUTS[-1]), jnp.bfloat16)
+            return
         for turn in range(2):
             chunk = 2 * turn + (0 if route == "y" else 1)
             start, end = CUTS[chunk], CUTS[chunk + 1]
@@ -729,6 +756,8 @@
 
 def weight_source(route, tile, step, place_ref):
     size_y, size_x, unit = place_ref[4], place_ref[5], place_ref[3]
+    if route == "all":
+        return step
     if route == "y":
         size, others, here = size_y, size_x, place_ref[0]
     else:
@@ -740,12 +769,12 @@
     return (row * size_x + column) * unit + step % unit
 
 
-def weight_grads(route, own, other, normed, branch):
+def weight_grads(route, own, other, sides):
     rows, tokens = own.shape
-    width = normed[0].shape[1]
+    width = CUTS[-1]
     size_y, size_x = lax.axis_size("y"), lax.axis_size("x")
     tile = 512 if unit_tiles(256) % 2 == 0 else 256
-    size = size_y if route == "y" else size_x
+    size = {"y": size_y, "x": size_x, "all": 1}[route]
     steps = rows // tile
     per_place = steps // size
     place = jnp.stack(
@@ -761,22 +790,31 @@
     source = pl.BlockSpec(
         (tile, tokens), lambda i, place_ref: (weight_source(route, tile, i, place_ref), 0)
     )
-    side = resident((tokens, width))
+    side = [
+        pl.BlockSpec((tokens, PADDED), lambda i, *_, at=at: (at, 0), pipeline_mode=pl.Buffered(1))
+        for at in range(2)
+    ]
 
     def out_spec(k):
         return pl.BlockSpec(
             (tile, CHUNK), lambda i, *_: (jnp.clip(i - k * per_place, 0, per_place - 1), 0)
         )
 
+    if route == "all":
+        out_specs = [pl.BlockSpec((tile, PADDED), lambda i, *_: (i, 0))]
+        out_shape = [jax.ShapeDtypeStruct((rows, PADDED), jnp.bfloat16)]
+    else:
+        out_specs = [out_spec(k) for k in range(size) for _ in range(2)]
+        out_shape = [jax.ShapeDtypeStruct((rows // size, CHUNK), jnp.bfloat16)] * (2 * size)
     results = pl.pallas_call(
         functools.partial(weight_grads_body, route, tile),
         grid_spec=pltpu.PrefetchScalarGridSpec(
             num_scalar_prefetch=1,
             grid=(steps,),
-            in_specs=[source, source, side, side, side, side],
-            out_specs=[out_spec(k) for k in range(size) for _ in range(2)],
+            in_specs=[source, source, side[0], side[0], side[1], side[1]],
+            out_specs=out_specs,
         ),
-        out_shape=[jax.ShapeDtypeStruct((rows // size, CHUNK), jnp.bfloat16)] * (2 * size),
+        out_shape=out_shape,
         compiler_params=pltpu.CompilerParams(vmem_limit_bytes=32 << 20),
         cost_estimate=pl.CostEstimate(
             flops=2 * rows * tokens * width,
@@ -784,16 +822,59 @@
             transcendentals=0,
         ),
         name="weight_grads",
-    )(place, own, other, *normed, *branch)
+    )(place, own, other, *sides, *sides)
+    if route == "all":
+        return results[0]
     return [[results[2 * k + turn] for k in range(size)] for turn in range(2)]
 
 
+def attention_rows_body(grad_ref, first_side_ref, second_side_ref, out_ref):
+    turned = grad_ref[...].T
+
+    def put(side_ref):
+        product = jnp.dot(turned, side_ref[...], preferred_element_type=jnp.float32)
+        out_ref[:, : CUTS[-1]] = product.astype(jnp.bfloat16)
+        out_ref[:, CUTS[-1] :] = jnp.zeros((BLOCK, PADDED - CUTS[-1]), jnp.bfloat16)
+
+    @pl.when(pl.program_id(0) < 3 * INNER // BLOCK)
+    def _():
+        put(first_side_ref)
+
+    @pl.when(pl.program_id(0) >= 3 * INNER // BLOCK)
+    def _():
+        put(second_side_ref)
+
+
+def attention_rows(grads, first_side, second_side):
+    tokens, width = first_side.shape
+    return pl.pallas_call(
+        attention_rows_body,
+        grid=(4 * INNER // BLOCK,),
+        in_specs=[
+            pl.BlockSpec((tokens, BLOCK), lambda i: (0, i)),
+            resident((tokens, width)),
+            resident((tokens, width)),
+        ],
+        out_specs=pl.BlockSpec((BLOCK, PADDED), lambda i: (i, 0)),
+        out_shape=jax.ShapeDtypeStruct((4 * INNER, PADDED), jnp.bfloat16),
+        cost_estimate=pl.CostEstimate(
+            flops=8 * tokens * INNER * width,
+            bytes_accessed=8 * INNER * PADDED + 8 * tokens * width,
+            transcendentals=0,
+        ),
+        name="attention_rows",
+    )(grads, first_side, second_side)
+
+
 def with_attention(route, chunk, arrays, rows):
+    unit_rows = rows.shape[0]
+    if route == "all":
+        here = lax.axis_index("c") < 4 * INNER // unit_rows
+        filled = jnp.where(here, rows, arrays[0][:unit_rows])
+        return [lax.dynamic_update_slice(arrays[0], filled, (0, 0))]
     size = lax.axis_size(route)
-    unit_rows = rows.shape[0]
     owners = 4 * INNER // unit_rows
-    start, end = CUTS[chunk], CUTS[chunk + 1]
-    columns = jnp.pad(rows[:, start:end], ((0, 0), (0, CHUNK - end + start)))
+    columns = rows[:, chunk * CHUNK : (chunk + 1) * CHUNK]
     filled = []
     for k, array in enumerate(arrays):
         here = (lax.axis_index(route) + 1 + k) % size == 0
@@ -885,7 +966,7 @@
     return (result, kept)
 
 
-def layer_backward(grad_out, kept, gathered, gain_one, gain_two, context, scatter, name, steps):
+def layer_backward(grad_out, kept, gathered, gain_one, gain_two, context, tail):
     (
         stream,
         inverse_one,
@@ -902,8 +983,9 @@
     ) = kept
     tokens = queries.shape[0]
     branch_low = grad_out.astype(jnp.bfloat16)
-    normed_pair = (normed_two_low, shift(normed_two_low, "c", 1))
-    branch_pair = (branch_low, shift(branch_low, "c", 1))
+    sides = jnp.concatenate([normed_two_low, branch_low], axis=0)
+    sides = jnp.pad(sides, ((0, 0), (0, PADDED - sides.shape[1])))
+    sides = (sides, shift(sides, "c", 1))
     grad_normed_two, own, sent = ffn_backward(
         branch_low, normed_two_low, up_gelu, up_linear, gathered
     )
@@ -912,41 +994,50 @@
     grad_middle = grad_out + grad_middle
     middle_low = grad_middle.astype(jnp.bfloat16)
     grad_mixed = times_rows(middle_low, gathered[3 * INNER : 4 * INNER]).astype(jnp.bfloat16)
-    grad_mixed, grad_middle, middle_low = steps[0]((grad_mixed, grad_middle, middle_low))
     grad_query, grad_shared, grad_table = attend_backward(
         queries, grad_mixed, shared, log_total, context
     )
     grad_shared, own = lax.optimization_barrier((grad_shared, own))
     moving = start_back(grad_shared, tokens)
+    routes = ("y", "x") if tail else ("all",)
     routed = {
-        route: weight_grads(route, own, other, normed_pair, branch_pair) for route in ("y", "x")
+        route: weight_grads(route, own, other, sides) for route in routes
     }
-    output_rows = outer_sum(attended, middle_low).astype(jnp.bfloat16)
-    routed, output_rows, moving = steps[1]((routed, output_rows, moving))
+    routed, moving = lax.optimization_barrier((routed, moving))
     grad_own = finish_back(*moving)
     grad_gate = grad_own[:, 2 * INNER :]
     grad_input_low = jnp.concatenate(
         [grad_query, grad_own[:, : 2 * INNER].astype(jnp.bfloat16)], axis=1
     )
-    rows = jnp.concatenate(
-        [outer_sum(grad_input_low, normed_low).astype(jnp.bfloat16), output_rows], axis=0
+    rows = attention_rows(
+        jnp.concatenate([grad_input_low, attended], axis=1), normed_low, middle_low
     )
     unit_rows = unit_tiles(TILE) * TILE
     core = lax.axis_index("c")
-    most = 4 * INNER // unit_rows - 1
+    owners = 4 * INNER // unit_rows
     kept_rows, sent_rows = (
-        lax.dynamic_slice_in_dim(rows, jnp.minimum(at, most) * unit_rows, unit_rows, 0)
+        lax.dynamic_slice_in_dim(rows, jnp.minimum(at, owners - 1) * unit_rows, unit_rows, 0)
+        if owners > 1
+        else rows
         for at in (core, 1 - core)
     )
     rows = total_of(kept_rows, [shift(sent_rows, "c", 1)])
-    for chunk in range(4):
-        route = ("y", "x", "z") if chunk % 2 == 0 else ("x", "y", "z")
-        arrays = with_attention(route[0], chunk, routed[route[0]][chunk // 2], rows)
-        scatter.push((name, chunk), route, arrays[-1], arrays[:-1])
-    grad_input_low, grad_gate = steps[2]((grad_input_low, grad_gate))
+    if tail:
+        scatter = Scatter()
+        for chunk in range(4):
+            route = ("y", "x", "z") if chunk % 2 == 0 else ("x", "y", "z")
+            arrays = with_attention(route[0], chunk, routed[route[0]][chunk // 2], rows)
+            scatter.push(chunk, route, arrays[-1], arrays[:-1])
+        grad_input_low = scatter.step(grad_input_low, 0, 1, 2, 3)
+    else:
+        scatter = with_attention("all", 0, [routed["all"]], rows)[0]
+        scatter, grad_input_low, grad_gate = lax.optimization_barrier(
+            (scatter, grad_input_low, grad_gate)
+        )
+        scatter = lax.psum_scatter(scatter, ("y", "x", "z"), scatter_dimension=0, tiled=True)
     grad_normed = times_plain(grad_input_low, gathered[: 3 * INNER])
     grad_stream, grad_gain_one = rms_backward(stream, inverse_one, gain_one, grad_normed)
-    return (grad_middle + grad_stream, grad_table, grad_gate, grad_gain_one, grad_gain_two)
+    return (grad_middle + grad_stream, grad_table, grad_gate, grad_gain_one, grad_gain_two, scatter)
 
 
 def per_device(
@@ -970,58 +1061,50 @@
     after_four, kept_four = layer_forward(
         after_three, gathered_four, norm_gains[2], norm_gains[3], gate_low, context
     )
-    scatter = Scatter()
-
-    def step(*names):
-        return lambda values: scatter.step(values, *names)
-
-    four, three = ([(name, chunk) for chunk in range(4)] for name in ("four", "three"))
-    grad_three_out, table_four, grad_gate, gain_four_one, gain_four_two = layer_backward(
-        cotangent.reshape(tokens_here, width),
-        kept_four,
-        gathered_four,
-        norm_gains[2],
-        norm_gains[3],
-        context,
-        scatter,
-        "four",
-        [step(), step(), step(*four)],
+    grad_three_out, table_four, grad_gate, gain_four_one, gain_four_two, local_four = (
+        layer_backward(
+            cotangent.reshape(tokens_here, width),
+            kept_four,
+            gathered_four,
+            norm_gains[2],
+            norm_gains[3],
+            context,
+            False,
+        )
     )
     grad_logit = grad_gate[:, 0] * gate_scale * sigmoid_value * (1.0 - sigmoid_value)
     grad_gate_weight = jnp.sum(grad_logit[:, None] * gate_normed, axis=0)
     gate_stream = stream_backward(after_three, gate_inverse, grad_logit[:, None] * gate_weight)
-    grad_input, table_three, unused, gain_three_one, gain_three_two = layer_backward(
+    grad_input, table_three, unused, gain_three_one, gain_three_two, scatter = layer_backward(
         grad_three_out + gate_stream,
         kept_three,
         gathered_three,
         norm_gains[0],
         norm_gains[1],
         context,
-        scatter,
-        "three",
-        [step(*four[:2]), step(*four[2:]), step(*four[:2], *three[:2])],
-    )
-    for names in (
-        four[2:],
-        three[:2] + three[2:],
-        four[:2],
-        three[:2],
-        three[2:],
-        four[2:],
-        three[2:],
-        three[:2],
-        three[2:],
-    ):
-        grad_input = scatter.step(grad_input, *names)
-    local_four, local_three = (
-        jnp.concatenate([scatter.results[name] for name in names], axis=1)[:, :width]
-        for names in (four, three)
+        True,
     )
     table = jnp.pad((table_three + table_four).reshape(1, -1), ((0, 0), (0, width - 6 * BUCKETS)))
-    small = jnp.stack(
+    small_sums = jnp.stack(
         [gain_three_one, gain_three_two, gain_four_one, gain_four_two, grad_gate_weight, table[0]]
     )
-    summed = sum_everywhere(small)
+    small = hop(small_sums, "c")
+    small = scatter.step(small, 0, 1)
+    small = hop(small, "z", 1)
+    small = scatter.step(small, 2, 3)
+    for bit in range(2, lax.axis_size("z")):
+        if bit & (bit - 1) == 0:
+            small = hop(small, "z", bit)
+    small = scatter.step(small, 0, 1)
+    small = scatter.step(small, 2, 3)
+    small = hop(small, "x")
+    for bit in range(1, lax.axis_size("y")):
+        if bit & (bit - 1) == 0:
+            small = hop(small, "y", bit)
+    summed = scatter.step(small, 0, 1)
+    summed = scatter.step(summed, 2, 3)
+    local_three = jnp.concatenate([scatter.results[chunk] for chunk in range(4)], axis=1)
+    local_three, local_four = local_three[:, :width], local_four[:, :width].astype(jnp.float32)
     return (
         after_four.reshape(inputs.shape),
         gate_mask.reshape(seqs_here, tokens_here),

time: 1490 us -> 1270 us (0.85)
  waiting for transfers between devices: 674 us -> 579 us
  local copies, waits for them, and re-layouts: 156 us -> 77.9 us
  other arithmetic: 123 us -> 96.8 us
  Pallas kernels: 292 us -> 309 us
    ppermute x16 -> x8, waiting for transfers between devices: 74 us -> 14.3 us  [slide(): return lax.ppermute(value, 'z', pairs)]
    ppermute x48 -> x26, waiting for transfers between devices: 214 us -> 165 us  [shift(): lax.ppermute(value, axis, [(i, (i + amount) % count) for i in range(count)])]
    ppermute x16 -> x8, starting transfers between devices: 87.1 us -> 39.9 us  [slide(): return lax.ppermute(value, 'z', pairs)]
    ppermute x6 -> x0, local copies, waits for them, and re-layouts: 23.2 us -> none  [shift(): lax.ppermute(value, axis, [(i, (i + amount) % count) for i in range(count)])]
    pallas_call x0 -> x2, Pallas kernels: none -> 22.6 us  [attention_rows(): pl.pallas_call(attention_rows_body, grid=(4 * INNER // BLOCK,), in_specs=...]
    convert_element_type x6 -> x0, local copies, waits for them, and re-layouts: 21.2 us -> none  [the longest x2 11.6 us: layer_backward(): outer_sum(grad_input_low, normed_low).astype(jnp.bfloat16)]
    convert_element_type x18 -> x9, other arithmetic: 39.3 us -> 21 us  [total_of(): return total.astype(jnp.bfloat16)]
    pallas_call x4 -> x3, Pallas kernels: 81.7 us -> 64.2 us  [weight_grads(): pl.pallas_call(functools.partial(weight_grads_body, route, tile), grid_sp...]
  transfers between devices with their start and end apart: 71 -> 46, of which waited for: 24 -> 16; matrix products, arithmetic and copies ran while one was open for 15% -> 12% of each run, Pallas kernels for 14% -> 17%
where the time goes in v5:
time: 1270 us
  waiting for transfers between devices  579 us (46%)
  Pallas kernels  309 us (24%)
  starting transfers between devices  153 us (12%)
  other arithmetic  96.8 us (8%)
  local copies, waits for them, and re-layouts  77.9 us (6%)
  matrix products  33.6 us (3%)
  between operations  15.5 us (1%)
    all_gather x2, waiting for transfers between devices, fetch_rows(): return lax.all_gather(local_rows, DEVICES, axis=0, tiled=True)  330 us
    ppermute x26, waiting for transfers between devices, shift(): lax.ppermute(value, axis, [(i, (i + amount) % count) for i in range(count)])  165 us
    ppermute x26, starting transfers between devices, shift(): lax.ppermute(value, axis, [(i, (i + amount) % count) for i in range(count)])  91.9 us
    pallas_call x2, Pallas kernels, ffn_backward(): pl.pallas_call(ffn_backward_body, grid_spec=pltpu.PrefetchScalarGridSpec(...  80.5 us
    ppermute x4, waiting for transfers between devices, far_pair(): got = lax.ppermute(sent, 'z', pairs)  70 us
    pallas_call x3, Pallas kernels, weight_grads(): pl.pallas_call(functools.partial(weight_grads_body, route, tile), grid_sp...  64.2 us
    pallas_call x2, Pallas kernels, attend_backward(): pl.pallas_call(functools.partial(backward_body, width > 2 * INNER), grid_...  55.3 us
    unnamed x233, local copies, waits for them, and re-layouts  53.9 us
  transfers between devices with their start and end apart: 46, of which 16 were waited for; matrix products, arithmetic and copies ran while one was open for 12% of the time, Pallas kernels for 17%

profile of v5, /device:TPU:24, one launch (start us, length us, event | category | flops | bytes accessed | tf_op | source)
XLA Modules:
  0.0 1265.1 jit_solution(4829240666006390096)
XLA Ops:
  18.1 207.3 %all-gather.3.cloned.1.call-done.gelu_ref.linear_ref.down_ref.refs_4_.refs_5_.refs_6_ = bf16[12288,1472]{1,0:T(8,128)(2,1)} async-done(((bf16[384,1472]{1,0:T(8,128)(2,1)}), bf16[12288,1472]{1,0:T(8,128)(2,1)}) %all-gather.3.cloned.1.call-update) | async-done | bytes 36175888 | tf_op jit(solution)/shard_map/all_gather | solution.py:935
  225.4 4.7 fusion.29
  234.4 6.0 collective-permute-start.2
  241.1 4.7 bias_tiles.1.refs_4_.refs_5_
  245.8 3.5 copy.109
  250.4 22.7 %collective-permute-done = bf16[288,768]{1,0:T(8,128)(2,1)} collective-permute-done((bf16[288,768]{1,0:T(8,128)(2,1)}, bf16[288,768]{1,0:T(8,128)(2,1)}, u32[]{:S(2)}, u32[]{:S(2)}) %collective-permute-start) | collective-permute-done | bytes 442400 | tf_op jit(solution)/shard_map/ppermute | solution.py:455
  274.2 14.3 %collective-permute-done.1 = bf16[512,768]{1,0:T(8,128)(2,1)} collective-permute-done((bf16[512,768]{1,0:T(8,128)(2,1)}, bf16[512,768]{1,0:T(8,128)(2,1)}, u32[]{:S(2)}, u32[]{:S(2)}) %collective-permute-start.1) | collective-permute-done | bytes 786464 | tf_op jit(solution)/shard_map/ppermute | solution.py:447
  291.4 16.4 %attend_forward.2 = (bf16[512,384]{1,0:T(8,128)(2,1)S(1)}, f32[4,8,256]{2,1,0:T(8,128)S(1)}) custom-call(s32[4]{0:T(128)S(1)} %get-tuple-element.403.low_ref, s32[4]{0:T(128)S(1)} %get-tuple-element.402.high_ref, bf16[512,384]{1,0:T(8,128)(2,1)S(1)} %slice.226.refs_0_, bf16[2304,768]{1,0:T(8,128)(2,1)S(1)} %pad_dynamic-update-slice_fusion.2.refs_1_.refs_2_, ...), custom_call_target="tpu_custom_call" | custom-call | flops 1811939328 | bytes 8388608 | tf_op jit(solution)/shard_map/attend_forward/pallas_call | solution.py:197
  312.0 24.9 %ffn_forward.2 = (f32[512,1472]{1,0:T(8,128)S(1)}, f32[512,3584]{1,0:T(8,128)}, f32[512,3584]{1,0:T(8,128)}) custom-call(bf16[512,1472]{1,0:T(8,128)(2,1)S(1)} %multiply_convert_fusion.2.normed_ref.refs_1_, f32[512,1472]{1,0:T(8,128)} %copy-done.52, bf16[12288,1472]{1,0:T(8,128)(2,1)} %all-gather.3.cloned.1.call-done.gelu_ref.linear_ref.down_ref.refs_4_.refs_5_.refs_6_, ...), custom_call_target="tpu_custom_call" | custom-call | flops 16206790656 | bytes 46333952 | tf_op jit(solution)/shard_map/ffn_forward/pallas_call | solution.py:582
  340.1 122.7 %all-gather.5.cloned.1.call-done.gelu_ref.linear_ref.down_ref.refs_4_.refs_5_.refs_6_ = bf16[12288,1472]{1,0:T(8,128)(2,1)} async-done(((bf16[384,1472]{1,0:T(8,128)(2,1)}), bf16[12288,1472]{1,0:T(8,128)(2,1)}) %all-gather.5.cloned.1.call-update) | async-done | bytes 36175888 | tf_op jit(solution)/shard_map/all_gather | solution.py:935
  462.8 4.7 fusion.32
  469.8 4.4 collective-permute-start.5
  479.2 40.3 %collective-permute-done.3 = bf16[288,896]{1,0:T(8,128)(2,1)} collective-permute-done((bf16[288,896]{1,0:T(8,128)(2,1)}, bf16[288,896]{1,0:T(8,128)(2,1)}, u32[]{:S(2)}, u32[]{:S(2)}) %collective-permute-start.3) | collective-permute-done | bytes 516128 | tf_op jit(solution)/shard_map/ppermute | solution.py:455
  523.8 16.6 %attend_forward.3 = (bf16[512,384]{1,0:T(8,128)(2,1)S(1)}, f32[4,8,256]{2,1,0:T(8,128)S(1)}) custom-call(s32[4]{0:T(128)S(1)} %get-tuple-element.403.low_ref, s32[4]{0:T(128)S(1)} %get-tuple-element.402.high_ref, bf16[512,384]{1,0:T(8,128)(2,1)S(1)} %slice.232.refs_0_, bf16[2304,896]{1,0:T(8,128)(2,1)S(1)} %pad_dynamic-update-slice_fusion.refs_1_.refs_2_, ...), custom_call_target="tpu_custom_call" | custom-call | flops 1811939328 | bytes 8388608 | tf_op jit(solution)/shard_map/attend_forward/pallas_call | solution.py:197
  544.8 24.2 %ffn_forward.3 = (f32[512,1472]{1,0:T(8,128)S(1)}, f32[512,3584]{1,0:T(8,128)}, f32[512,3584]{1,0:T(8,128)}) custom-call(bf16[512,1472]{1,0:T(8,128)(2,1)S(1)} %multiply_convert_fusion.normed_ref.refs_1_, f32[512,1472]{1,0:T(8,128)} %copy-done.54, bf16[12288,1472]{1,0:T(8,128)(2,1)} %all-gather.5.cloned.1.call-done.gelu_ref.linear_ref.down_ref.refs_4_.refs_5_.refs_6_, ...), custom_call_target="tpu_custom_call" | custom-call | flops 16206790656 | bytes 46333952 | tf_op jit(solution)/shard_map/ffn_forward/pallas_call | solution.py:582
  570.7 40.2 %ffn_backward.2 = (f32[512,1472]{1,0:T(8,128)}, bf16[6144,512]{1,0:T(8,128)(2,1)}, bf16[6144,512]{1,0:T(8,128)(2,1)}) custom-call(s32[2]{0:T(128)S(1)} %pad_add_fusion.core_ref, bf16[512,1472]{1,0:T(8,128)(2,1)S(1)} %copy-done.6, bf16[512,1472]{1,0:T(8,128)(2,1)S(1)} %multiply_convert_fusion.normed_ref.refs_1_, f32[512,3584]{1,0:T(8,128)} %get-tuple-element.141.refs_2_, ...), custom_call_target="tpu_custom_call" | custom-call | flops 16206790656 | bytes 57344000 | tf_op jit(solution)/shard_map/ffn_backward/pallas_call | solution.py:682
  614.8 4.4 multiply_reduce_fusion.1
  619.5 4.4 fusion.47
  623.9 2.9 convolution_convert_fusion.1.refs_1_
  626.9 28.6 %attend_backward.2 = (bf16[512,384]{1,0:T(8,128)(2,1)S(1)}, bf16[2304,896]{1,0:T(8,128)(2,1)}, f32[3,32,256]{2,1,0:T(8,128)S(1)}) custom-call(s32[4]{0:T(128)S(1)} %get-tuple-element.403.low_ref, s32[4]{0:T(128)S(1)} %get-tuple-element.402.high_ref, bf16[512,384]{1,0:T(8,128)(2,1)S(1)} %copy-done.29, bf16[512,384]{1,0:T(8,128)(2,1)S(1)} %convolution_convert_fusion.1.refs_1_, ...), custom_call_target="tpu_custom_call" | custom-call | flops 4529848320 | bytes 12582912 | tf_op jit(solution)/shard_map/attend_backward/pallas_call | solution.py:347
  658.9 15.8 %collective-permute-start.8 = (bf16[512,896]{1,0:T(8,128)(2,1)S(1)}, bf16[512,896]{1,0:T(8,128)(2,1)S(1)}, u32[]{:S(2)}, u32[]{:S(2)}) collective-permute-start(bf16[512,896]{1,0:T(8,128)(2,1)S(1)} %get-tuple-element.349), channel_id=1, source_target_pairs={{1,0},{2,1},{3,2},{5,4},{6,5},{7,6},{9,8},{10,9},{11,10},{13,12},{... | collective-permute-start | bytes 2752520 | tf_op jit(solution)/shard_map/ppermute | solution.py:447
  676.0 3.2 collective-permute-start.10
  679.2 23.9 %weight_grads.3 = bf16[6144,1536]{1,0:T(8,128)(2,1)} custom-call(s32[6]{0:T(128)S(1)} %stack.48.place_ref, bf16[6144,512]{1,0:T(8,128)(2,1)S(1)} %bitcast.108, bf16[6144,512]{1,0:T(8,128)(2,1)} %collective-permute-done.6.refs_1_, bf16[1024,1536]{1,0:T(8,128)(2,1)} %fusion.9.refs_2_.refs_4_, bf16[1024,1536]{1,0:T(8,128)(2,1)} %collective-permute-done.7.refs_3_.refs_5_, ...), custom_call_target="tpu_custom_call" | custom-call | flops 9261023232 | bytes 21626880 | tf_op jit(solution)/shard_map/weight_grads/pallas_call | solution.py:809
  703.1 7.0 collective-permute-done.10
  713.5 11.3 attention_rows.2
  724.8 6.7 collective-permute-start.11
  733.8 5.6 collective-permute-done.11
  739.4 9.2 fusion.5
  751.4 5.6 multiply_reduce_fusion.2
  758.7 40.3 %ffn_backward.3 = (f32[512,1472]{1,0:T(8,128)}, bf16[6144,512]{1,0:T(8,128)(2,1)}, bf16[6144,512]{1,0:T(8,128)(2,1)}) custom-call(s32[2]{0:T(128)S(1)} %copy-done.43, bf16[512,1472]{1,0:T(8,128)(2,1)S(1)} %get-tuple-element.334.refs_0_, bf16[512,1472]{1,0:T(8,128)(2,1)S(1)} %copy-done.1, f32[512,3584]{1,0:T(8,128)} %get-tuple-element.158.refs_2_, ...), custom_call_target="tpu_custom_call" | custom-call | flops 16206790656 | bytes 57344000 | tf_op jit(solution)/shard_map/ffn_backward/pallas_call | solution.py:682
  805.4 2.9 convolution_convert_fusion.refs_1_
  808.3 26.7 %attend_backward.3 = (bf16[512,384]{1,0:T(8,128)(2,1)S(1)}, bf16[2304,768]{1,0:T(8,128)(2,1)}, f32[3,32,256]{2,1,0:T(8,128)S(1)}) custom-call(s32[4]{0:T(128)S(1)} %get-tuple-element.403.low_ref, s32[4]{0:T(128)S(1)} %get-tuple-element.402.high_ref, bf16[512,384]{1,0:T(8,128)(2,1)S(1)} %copy-done.33, bf16[512,384]{1,0:T(8,128)(2,1)S(1)} %convolution_convert_fusion.refs_1_, ...), custom_call_target="tpu_custom_call" | custom-call | flops 4529848320 | bytes 12582912 | tf_op jit(solution)/shard_map/attend_backward/pallas_call | solution.py:347
  836.2 5.6 collective-permute-start.16
  845.1 8.5 collective-permute-start.14
  855.3 2.8 copy-done.44
  860.0 20.1 %weight_grads.5 = (bf16[3072,384]{1,0:T(8,128)(2,1)}, bf16[3072,384]{1,0:T(8,128)(2,1)S(1)}, bf16[3072,384]{1,0:T(8,128)(2,1)S(1)}, bf16[3072,384]{1,0:T(8,128)(2,1)S(1)}) custom-call(s32[6]{0:T(128)S(1)} %stack.48.place_ref, bf16[6144,512]{1,0:T(8,128)(2,1)S(1)} %copy-done.44, bf16[6144,512]{1,0:T(8,128)(2,1)} %collective-permute-done.12.refs_1_, ...), custom_call_target="tpu_custom_call" | custom-call | flops 9261023232 | bytes 21626880 | tf_op jit(solution)/shard_map/weight_grads/pallas_call | solution.py:809
  882.9 20.3 %weight_grads.4 = (bf16[3072,384]{1,0:T(8,128)(2,1)}, bf16[3072,384]{1,0:T(8,128)(2,1)S(1)}, bf16[3072,384]{1,0:T(8,128)(2,1)S(1)}, bf16[3072,384]{1,0:T(8,128)(2,1)S(1)}) custom-call(s32[6]{0:T(128)S(1)} %stack.48.place_ref, bf16[6144,512]{1,0:T(8,128)(2,1)S(1)} %copy-done.44, bf16[6144,512]{1,0:T(8,128)(2,1)} %collective-permute-done.12.refs_1_, ...), custom_call_target="tpu_custom_call" | custom-call | flops 9261023232 | bytes 21626880 | tf_op jit(solution)/shard_map/weight_grads/pallas_call | solution.py:809
  910.2 11.3 attention_rows.3
  921.5 8.6 collective-permute-start.17
  932.3 5.6 collective-permute-done.17
  937.9 7.4 add_convert_fusion
  945.3 4.0 select_dynamic-update-slice_fusion.4
  949.8 6.1 select_dynamic-update-slice_fusion
  959.5 9.1 collective-permute-start.19
  969.4 7.9 fusion.20
  979.7 57.9 %collective-permute-done.18 = bf16[3072,384]{1,0:T(8,128)(2,1)} collective-permute-done((bf16[3072,384]{1,0:T(8,128)(2,1)}, bf16[3072,384]{1,0:T(8,128)(2,1)}, u32[]{:S(2)}, u32[]{:S(2)}) %collective-permute-start.18) | collective-permute-done | bytes 2359328 | tf_op jit(solution)/shard_map/ppermute | solution.py:441
  1037.6 3.0 add_convert_fusion.5
  1046.7 11.0 collective-permute-start.21
  1058.4 39.8 %collective-permute-done.23 = bf16[3072,384]{1,0:T(8,128)(2,1)} collective-permute-done((bf16[3072,384]{1,0:T(8,128)(2,1)}, bf16[3072,384]{1,0:T(8,128)(2,1)}, u32[]{:S(2)}, u32[]{:S(2)}) %collective-permute-start.23) | collective-permute-done | bytes 2359328 | tf_op jit(solution)/shard_map/ppermute | solution.py:441
  1106.7 9.2 collective-permute-start.33
  1117.5 6.0 collective-permute-done.22
  1130.4 10.8 collective-permute-done.33
  1141.2 6.7 collective-permute-done.34
  1150.8 9.3 collective-permute-start.35
  1164.3 3.7 collective-permute-start.30
  1168.5 3.3 collective-permute-start.37
  1171.9 4.5 fusion.17
  1178.7 8.0 collective-permute-start.38
  1186.8 6.0 collective-permute-start.39
  1192.8 8.8 collective-permute-done.31
  1201.6 5.1 collective-permute-start.40
  1206.7 15.6 %collective-permute-start.41 = (bf16[384,384]{1,0:T(8,128)(2,1)}, bf16[384,384]{1,0:T(8,128)(2,1)S(1)}, u32[]{:S(2)}, u32[]{:S(2)}) collective-permute-start(bf16[384,384]{1,0:T(8,128)(2,1)} %get-tuple-element.253), channel_id=1, source_target_pairs={{0,2},{1,3},{2,0},{3,1},{4,6},{5,7},{6,4},{7,5},{8,10},{9,11},{10,... | collective-permute-start | bytes 884744 | tf_op jit(solution)/shard_map/ppermute | solution.py:441
  1224.9 12.9 %collective-permute-done.38 = bf16[384,384]{1,0:T(8,128)(2,1)S(1)} collective-permute-done((bf16[384,384]{1,0:T(8,128)(2,1)}, bf16[384,384]{1,0:T(8,128)(2,1)S(1)}, u32[]{:S(2)}, u32[]{:S(2)}) %collective-permute-start.38) | collective-permute-done | bytes 294944 | tf_op jit(solution)/shard_map/ppermute | solution.py:441
  1237.9 10.7 collective-permute-done.41
  (402 shorter events, 144.0 us)
Async XLA Ops:
  7.2 218.2 %all-gather.3.cloned.1.call-start = ((), (), s32[]{:S(2)}) async-start(), calls=%async_computation.1 | async-start | bytes 38928384 | tf_op jit(solution)/shard_map/all_gather | solution.py:935
  9.7 453.1 %all-gather.5.cloned.1.call-start = ((), (), s32[]{:S(2)}) async-start(), calls=%async_computation.2 | async-start | bytes 38928384 | tf_op jit(solution)/shard_map/all_gather | solution.py:935
  11.9 1243.0 %reduce-scatter.2.cloned.1.call-start = ((), (), s32[]{:S(2)}) async-start(), calls=%async_computation.3 | async-start | bytes 20054016 | tf_op jit(solution)/shard_map/reduce_scatter | solution.py:1037
  14.4 293.4 %copy-start.51 = (f32[1,512,1472]{2,1,0:T(8,128)}, f32[1,512,1472]{2,1,0:T(8,128)S(1)}, u32[]{:S(2)}) copy-start(f32[1,512,1472]{2,1,0:T(8,128)S(1)} %copy.103) | copy-start | bytes 9043972
  15.1 295.9 %copy-start.78 = (f32[1472]{0:T(1024)}, f32[1472]{0:T(1024)S(1)}, u32[]{:S(2)}) copy-start(f32[1472]{0:T(1024)S(1)} %get-tuple-element.325) | copy-start | bytes 17668
  15.1 322.7 %copy-start.82 = (f32[1472]{0:T(1024)}, f32[1472]{0:T(1024)S(1)}, u32[]{:S(2)}) copy-start(f32[1472]{0:T(1024)S(1)} %get-tuple-element.327) | copy-start | bytes 17668
  18.1 222.3 %copy-start.105 = (f32[32,6]{0,1:T(8,128)S(1)}, f32[32,6]{0,1:T(8,128)}, u32[]{:S(2)}) copy-start(f32[32,6]{0,1:T(8,128)} %param.13) | copy-start | bytes 2308
  231.9 41.2 %collective-permute-start = (bf16[288,768]{1,0:T(8,128)(2,1)}, bf16[288,768]{1,0:T(8,128)(2,1)}, u32[]{:S(2)}, u32[]{:S(2)}) collective-permute-start(bf16[288,768]{1,0:T(8,128)(2,1)} %slice_select_fusion.1), channel_id=1, source_target_pairs={{0,2},{1,3},{2,0},{3,1},{4,6},{5,7},{6,4},{7,5},{8,10},{9,11},{10,... | collective-permute-start | bytes 1327112 | tf_op jit(solution)/shard_map/ppermute | solution.py:455
  232.6 55.9 %collective-permute-start.1 = (bf16[512,768]{1,0:T(8,128)(2,1)}, bf16[512,768]{1,0:T(8,128)(2,1)}, u32[]{:S(2)}, u32[]{:S(2)}) collective-permute-start(bf16[512,768]{1,0:T(8,128)(2,1)} %slice.229), channel_id=1, source_target_pairs={{0,1},{1,2},{2,3},{4,5},{5,6},{6,7},{8,9},{9,10},{10,11},{12,13},{... | collective-permute-start | bytes 2359304 | tf_op jit(solution)/shard_map/ppermute | solution.py:447
  234.4 55.4 %collective-permute-start.2 = (bf16[512,768]{1,0:T(8,128)(2,1)}, bf16[512,768]{1,0:T(8,128)(2,1)}, u32[]{:S(2)}, u32[]{:S(2)}) collective-permute-start(bf16[512,768]{1,0:T(8,128)(2,1)} %slice.229), channel_id=1, source_target_pairs={{1,0},{2,1},{3,2},{5,4},{6,5},{7,6},{9,8},{10,9},{11,10},{13,12},{... | collective-permute-start | bytes 2359304 | tf_op jit(solution)/shard_map/ppermute | solution.py:447
  250.4 40.9 %copy-start.32 = (bf16[512,384]{1,0:T(8,128)(2,1)}, bf16[512,384]{1,0:T(8,128)(2,1)S(1)}, u32[]{:S(2)}) copy-start(bf16[512,384]{1,0:T(8,128)(2,1)S(1)} %slice.226.refs_0_) | copy-start | bytes 1179652
  337.8 129.7 %copy-start.94 = (f32[512]{0:T(512)}, f32[512]{0:T(512)S(1)}, u32[]{:S(2)}) copy-start(f32[512]{0:T(512)S(1)} %get-tuple-element.393) | copy-start | bytes 6148
  340.1 127.4 %copy-start.96 = (f32[512]{0:T(512)}, f32[512]{0:T(512)S(1)}, u32[]{:S(2)}) copy-start(f32[512]{0:T(512)S(1)} %get-tuple-element.339) | copy-start | bytes 6148
  469.8 52.6 %collective-permute-start.5 = (bf16[512,896]{1,0:T(8,128)(2,1)}, bf16[512,896]{1,0:T(8,128)(2,1)}, u32[]{:S(2)}, u32[]{:S(2)}) collective-permute-start(bf16[512,896]{1,0:T(8,128)(2,1)} %pad_maximum_fusion.3), channel_id=1, source_target_pairs={{1,0},{2,1},{3,2},{5,4},{6,5},{7,6},{9,8},{10,9},{11,10},{13,12},{... | collective-permute-start | bytes 2752520 | tf_op jit(solution)/shard_map/ppermute | solution.py:447
  474.2 46.6 %collective-permute-start.4 = (bf16[512,896]{1,0:T(8,128)(2,1)}, bf16[512,896]{1,0:T(8,128)(2,1)}, u32[]{:S(2)}, u32[]{:S(2)}) collective-permute-start(bf16[512,896]{1,0:T(8,128)(2,1)} %pad_maximum_fusion.3), channel_id=1, source_target_pairs={{0,1},{1,2},{2,3},{4,5},{5,6},{6,7},{8,9},{9,10},{10,11},{12,13},{... | collective-permute-start | bytes 2752520 | tf_op jit(solution)/shard_map/ppermute | solution.py:447
  475.5 44.1 %collective-permute-start.3 = (bf16[288,896]{1,0:T(8,128)(2,1)}, bf16[288,896]{1,0:T(8,128)(2,1)}, u32[]{:S(2)}, u32[]{:S(2)}) collective-permute-start(bf16[288,896]{1,0:T(8,128)(2,1)} %fusion.40), channel_id=1, source_target_pairs={{0,2},{1,3},{2,0},{3,1},{4,6},{5,7},{6,4},{7,5},{8,10},{9,11},{10,... | collective-permute-start | bytes 1548296 | tf_op jit(solution)/shard_map/ppermute | solution.py:455
  478.0 44.2 %copy-start.59 = (bf16[512,768]{1,0:T(8,128)(2,1)S(1)}, bf16[512,768]{1,0:T(8,128)(2,1)}, u32[]{:S(2)}) copy-start(bf16[512,768]{1,0:T(8,128)(2,1)} %copy-done.58) | copy-start | bytes 2359300
  478.1 92.6 %copy-start.42 = (s32[2]{0:T(128)}, s32[2]{0:T(128)S(1)}, u32[]{:S(2)}) copy-start(s32[2]{0:T(128)S(1)} %pad_add_fusion.core_ref) | copy-start | bytes 28
  479.2 44.6 %copy-start.28 = (bf16[512,384]{1,0:T(8,128)(2,1)}, bf16[512,384]{1,0:T(8,128)(2,1)S(1)}, u32[]{:S(2)}) copy-start(bf16[512,384]{1,0:T(8,128)(2,1)S(1)} %slice.232.refs_0_) | copy-start | bytes 1179652
  610.9 68.3 %collective-permute-start.6 = (bf16[6144,512]{1,0:T(8,128)(2,1)}, bf16[6144,512]{1,0:T(8,128)(2,1)}, u32[]{:S(2)}, u32[]{:S(2)}) collective-permute-start(bf16[6144,512]{1,0:T(8,128)(2,1)} %get-tuple-element.148), channel_id=1, source_target_pairs={{0,4},{4,0},{1,5},{5,1},{2,6},{6,2},{3,7},{7,3},{8,12},{12,8},{9,1... | collective-permute-start | bytes 18874376 | tf_op jit(solution)/shard_map/ppermute | solution.py:441
  613.1 66.2 %collective-permute-start.7 = (bf16[1024,1536]{1,0:T(8,128)(2,1)}, bf16[1024,1536]{1,0:T(8,128)(2,1)}, u32[]{:S(2)}, u32[]{:S(2)}) collective-permute-start(bf16[1024,1536]{1,0:T(8,128)(2,1)} %fusion.9.refs_2_.refs_4_), channel_id=1, source_target_pairs={{0,4},{4,0},{1,5},{5,1},{2,6},{6,2},{3,7},{7,3},{8,12},{12,8},{9,1... | collective-permute-start | bytes 9437192 | tf_op jit(solution)/shard_map/ppermute | solution.py:441
  626.8 52.4 %slice-start = ((s8[6291456]{0:T(1024)(128)(4,1)}), s8[4194304]{0:T(1024)(128)(4,1)S(1)}, s32[]{:S(2)}) async-start(s8[6291456]{0:T(1024)(128)(4,1)} %bitcast.107), calls=%async_computation.4 | async-start | bytes 8388608
  626.9 52.4 %slice-start.1 = ((s8[6291456]{0:T(1024)(128)(4,1)}), s8[2097152]{0:T(1024)(128)(4,1)S(1)}, s32[]{:S(2)}) async-start(s8[6291456]{0:T(1024)(128)(4,1)} %bitcast.107), calls=%async_computation.5 | async-start | bytes 4194304
  655.5 55.3 %copy-start.30 = (bf16[512,384]{1,0:T(8,128)(2,1)}, bf16[512,384]{1,0:T(8,128)(2,1)S(1)}, u32[]{:S(2)}) copy-start(bf16[512,384]{1,0:T(8,128)(2,1)S(1)} %get-tuple-element.151) | copy-start | bytes 1179652
  657.6 52.5 %collective-permute-start.9 = (bf16[512,896]{1,0:T(8,128)(2,1)S(1)}, bf16[512,896]{1,0:T(8,128)(2,1)S(1)}, u32[]{:S(2)}, u32[]{:S(2)}) collective-permute-start(bf16[512,896]{1,0:T(8,128)(2,1)S(1)} %get-tuple-element.348), channel_id=1, source_target_pairs={{0,1},{1,2},{2,3},{4,5},{5,6},{6,7},{8,9},{9,10},{10,11},{12,13},{... | collective-permute-start | bytes 2752520 | tf_op jit(solution)/shard_map/ppermute | solution.py:447
  658.9 51.2 %collective-permute-start.8 = (bf16[512,896]{1,0:T(8,128)(2,1)S(1)}, bf16[512,896]{1,0:T(8,128)(2,1)S(1)}, u32[]{:S(2)}, u32[]{:S(2)}) collective-permute-start(bf16[512,896]{1,0:T(8,128)(2,1)S(1)} %get-tuple-element.349), channel_id=1, source_target_pairs={{1,0},{2,1},{3,2},{5,4},{6,5},{7,6},{9,8},{10,9},{11,10},{13,12},{... | collective-permute-start | bytes 2752520 | tf_op jit(solution)/shard_map/ppermute | solution.py:447
  676.0 34.1 %collective-permute-start.10 = (bf16[288,896]{1,0:T(8,128)(2,1)S(1)}, bf16[288,896]{1,0:T(8,128)(2,1)S(1)}, u32[]{:S(2)}, u32[]{:S(2)}) collective-permute-start(bf16[288,896]{1,0:T(8,128)(2,1)S(1)} %slice_select_fusion), channel_id=1, source_target_pairs={{0,2},{1,3},{2,0},{3,1},{4,6},{5,7},{6,4},{7,5},{8,10},{9,11},{10,... | collective-permute-start | bytes 1548296 | tf_op jit(solution)/shard_map/ppermute | solution.py:455
  724.8 14.6 %collective-permute-start.11 = (bf16[1536,1536]{1,0:T(8,128)(2,1)}, bf16[1536,1536]{1,0:T(8,128)(2,1)}, u32[]{:S(2)}, u32[]{:S(2)}) collective-permute-start(bf16[1536,1536]{1,0:T(8,128)(2,1)} %attention_rows.2), channel_id=1, source_target_pairs={{0,4},{4,0},{1,5},{5,1},{2,6},{6,2},{3,7},{7,3},{8,12},{12,8},{9,1... | collective-permute-start | bytes 14155784 | tf_op jit(solution)/shard_map/ppermute | solution.py:441
  758.7 41.3 %copy-start.79 = (f32[1472]{0:T(1024)S(1)}, f32[1472]{0:T(1024)}, u32[]{:S(2)}) copy-start(f32[1472]{0:T(1024)} %copy-done.78) | copy-start | bytes 17668
  799.1 56.2 %collective-permute-start.12 = (bf16[6144,512]{1,0:T(8,128)(2,1)}, bf16[6144,512]{1,0:T(8,128)(2,1)}, u32[]{:S(2)}, u32[]{:S(2)}) collective-permute-start(bf16[6144,512]{1,0:T(8,128)(2,1)} %get-tuple-element.165), channel_id=1, source_target_pairs={{0,4},{4,0},{1,5},{5,1},{2,6},{6,2},{3,7},{7,3},{8,12},{12,8},{9,1... | collective-permute-start | bytes 18874376 | tf_op jit(solution)/shard_map/ppermute | solution.py:441
  799.8 53.8 %collective-permute-start.13 = (bf16[1024,1536]{1,0:T(8,128)(2,1)S(1)}, bf16[1024,1536]{1,0:T(8,128)(2,1)S(1)}, u32[]{:S(2)}, u32[]{:S(2)}) collective-permute-start(bf16[1024,1536]{1,0:T(8,128)(2,1)S(1)} %fusion.10.refs_2_.refs_4_), channel_id=1, source_target_pairs={{0,4},{4,0},{1,5},{5,1},{2,6},{6,2},{3,7},{7,3},{8,12},{12,8},{9,1... | collective-permute-start | bytes 9437192 | tf_op jit(solution)/shard_map/ppermute | solution.py:441
  836.2 71.2 %collective-permute-start.16 = (bf16[288,768]{1,0:T(8,128)(2,1)S(1)}, bf16[288,768]{1,0:T(8,128)(2,1)S(1)}, u32[]{:S(2)}, u32[]{:S(2)}) collective-permute-start(bf16[288,768]{1,0:T(8,128)(2,1)S(1)} %slice_select_fusion.2), channel_id=1, source_target_pairs={{0,2},{1,3},{2,0},{3,1},{4,6},{5,7},{6,4},{7,5},{8,10},{9,11},{10,... | collective-permute-start | bytes 1327112 | tf_op jit(solution)/shard_map/ppermute | solution.py:455
  843.8 63.7 %collective-permute-start.15 = (bf16[512,768]{1,0:T(8,128)(2,1)S(1)}, bf16[512,768]{1,0:T(8,128)(2,1)S(1)}, u32[]{:S(2)}, u32[]{:S(2)}) collective-permute-start(bf16[512,768]{1,0:T(8,128)(2,1)S(1)} %get-tuple-element.351), channel_id=1, source_target_pairs={{0,1},{1,2},{2,3},{4,5},{5,6},{6,7},{8,9},{9,10},{10,11},{12,13},{... | collective-permute-start | bytes 2359304 | tf_op jit(solution)/shard_map/ppermute | solution.py:447
  845.1 62.4 %collective-permute-start.14 = (bf16[512,768]{1,0:T(8,128)(2,1)S(1)}, bf16[512,768]{1,0:T(8,128)(2,1)S(1)}, u32[]{:S(2)}, u32[]{:S(2)}) collective-permute-start(bf16[512,768]{1,0:T(8,128)(2,1)S(1)} %get-tuple-element.352), channel_id=1, source_target_pairs={{1,0},{2,1},{3,2},{5,4},{6,5},{7,6},{9,8},{10,9},{11,10},{13,12},{... | collective-permute-start | bytes 2359304 | tf_op jit(solution)/shard_map/ppermute | solution.py:447
  921.5 16.4 %collective-permute-start.17 = (bf16[1536,1536]{1,0:T(8,128)(2,1)}, bf16[1536,1536]{1,0:T(8,128)(2,1)}, u32[]{:S(2)}, u32[]{:S(2)}) collective-permute-start(bf16[1536,1536]{1,0:T(8,128)(2,1)} %attention_rows.3), channel_id=1, source_target_pairs={{0,4},{4,0},{1,5},{5,1},{2,6},{6,2},{3,7},{7,3},{8,12},{12,8},{9,1... | collective-permute-start | bytes 14155784 | tf_op jit(solution)/shard_map/ppermute | solution.py:441
  959.5 78.1 %collective-permute-start.18 = (bf16[3072,384]{1,0:T(8,128)(2,1)}, bf16[3072,384]{1,0:T(8,128)(2,1)}, u32[]{:S(2)}, u32[]{:S(2)}) collective-permute-start(bf16[3072,384]{1,0:T(8,128)(2,1)} %get-tuple-element.190), channel_id=1, source_target_pairs={{0,16},{16,0},{1,17},{17,1},{2,18},{18,2},{3,19},{19,3},{4,20},{20... | collective-permute-start | bytes 7077896 | tf_op jit(solution)/shard_map/ppermute | solution.py:441
  959.5 78.1 %collective-permute-start.19 = (bf16[3072,384]{1,0:T(8,128)(2,1)}, bf16[3072,384]{1,0:T(8,128)(2,1)}, u32[]{:S(2)}, u32[]{:S(2)}) collective-permute-start(bf16[3072,384]{1,0:T(8,128)(2,1)} %get-tuple-element.192), channel_id=1, source_target_pairs={{0,8},{8,0},{1,9},{9,1},{2,10},{10,2},{3,11},{11,3},{4,12},{12,4},... | collective-permute-start | bytes 7077896 | tf_op jit(solution)/shard_map/ppermute | solution.py:441
  977.4 2.3 collective-permute-start.20
  977.7 120.4 %collective-permute-start.23 = (bf16[3072,384]{1,0:T(8,128)(2,1)}, bf16[3072,384]{1,0:T(8,128)(2,1)}, u32[]{:S(2)}, u32[]{:S(2)}) collective-permute-start(bf16[3072,384]{1,0:T(8,128)(2,1)} %copy-done.36), channel_id=1, source_target_pairs={{0,16},{16,0},{1,17},{17,1},{2,18},{18,2},{3,19},{19,3},{4,20},{20... | collective-permute-start | bytes 7077896 | tf_op jit(solution)/shard_map/ppermute | solution.py:441
  979.6 118.5 %collective-permute-start.24 = (bf16[3072,384]{1,0:T(8,128)(2,1)}, bf16[3072,384]{1,0:T(8,128)(2,1)}, u32[]{:S(2)}, u32[]{:S(2)}) collective-permute-start(bf16[3072,384]{1,0:T(8,128)(2,1)} %copy-done.39), channel_id=1, source_target_pairs={{0,8},{8,0},{1,9},{9,1},{2,10},{10,2},{3,11},{11,3},{4,12},{12,4},... | collective-permute-start | bytes 7077896 | tf_op jit(solution)/shard_map/ppermute | solution.py:441
  1046.7 11.0 collective-permute-start.25
  1046.7 70.7 %collective-permute-start.21 = (bf16[1536,384]{1,0:T(8,128)(2,1)}, bf16[1536,384]{1,0:T(8,128)(2,1)}, u32[]{:S(2)}, u32[]{:S(2)}) collective-permute-start(bf16[1536,384]{1,0:T(8,128)(2,1)} %get-tuple-element.201), channel_id=1, source_target_pairs={{0,8},{8,0},{1,9},{9,1},{2,10},{10,2},{3,11},{11,3},{4,12},{12,4},... | collective-permute-start | bytes 3538952 | tf_op jit(solution)/shard_map/ppermute | solution.py:441
  1057.7 65.7 %collective-permute-start.22 = (bf16[1536,384]{1,0:T(8,128)(2,1)}, bf16[1536,384]{1,0:T(8,128)(2,1)}, u32[]{:S(2)}, u32[]{:S(2)}) collective-permute-start(bf16[1536,384]{1,0:T(8,128)(2,1)} %get-tuple-element.203), channel_id=1, source_target_pairs={{0,16},{16,0},{1,17},{17,1},{2,18},{18,2},{3,19},{19,3},{4,20},{20... | collective-permute-start | bytes 3538952 | tf_op jit(solution)/shard_map/ppermute | solution.py:441
  1106.4 9.6 collective-permute-start.26
  1106.7 34.5 %collective-permute-start.33 = (bf16[1536,384]{1,0:T(8,128)(2,1)}, bf16[1536,384]{1,0:T(8,128)(2,1)S(1)}, u32[]{:S(2)}, u32[]{:S(2)}) collective-permute-start(bf16[1536,384]{1,0:T(8,128)(2,1)} %get-tuple-element.229), channel_id=1, source_target_pairs={{0,8},{8,0},{1,9},{9,1},{2,10},{10,2},{3,11},{11,3},{4,12},{12,4},... | collective-permute-start | bytes 3538952 | tf_op jit(solution)/shard_map/ppermute | solution.py:441
  1115.9 32.0 %collective-permute-start.34 = (bf16[1536,384]{1,0:T(8,128)(2,1)}, bf16[1536,384]{1,0:T(8,128)(2,1)S(1)}, u32[]{:S(2)}, u32[]{:S(2)}) collective-permute-start(bf16[1536,384]{1,0:T(8,128)(2,1)} %get-tuple-element.231), channel_id=1, source_target_pairs={{0,16},{16,0},{1,17},{17,1},{2,18},{18,2},{3,19},{19,3},{4,20},{20... | collective-permute-start | bytes 3538952 | tf_op jit(solution)/shard_map/ppermute | solution.py:441
  1128.8 39.2 %collective-permute-start.27 = (bf16[384,384]{1,0:T(8,128)(2,1)}, bf16[384,384]{1,0:T(8,128)(2,1)S(1)}, u32[]{:S(2)}, u32[]{:S(2)}) collective-permute-start(bf16[384,384]{1,0:T(8,128)(2,1)} %get-tuple-element.221), channel_id=1, source_target_pairs={{0,1},{1,2},{2,3},{3,0},{4,5},{5,6},{6,7},{7,4},{8,9},{9,10},{10,1... | collective-permute-start | bytes 884744 | tf_op jit(solution)/shard_map/ppermute | solution.py:441
  1128.8 39.7 %collective-permute-start.28 = (bf16[384,384]{1,0:T(8,128)(2,1)}, bf16[384,384]{1,0:T(8,128)(2,1)}, u32[]{:S(2)}, u32[]{:S(2)}) collective-permute-start(bf16[384,384]{1,0:T(8,128)(2,1)} %get-tuple-element.222), channel_id=1, source_target_pairs={{0,2},{1,3},{2,0},{3,1},{4,6},{5,7},{6,4},{7,5},{8,10},{9,11},{10,... | collective-permute-start | bytes 884744 | tf_op jit(solution)/shard_map/ppermute | solution.py:441
  1150.8 11.6 collective-permute-start.35
  1163.2 4.8 collective-permute-start.36
  1164.1 14.6 %collective-permute-start.29 = (bf16[384,384]{1,0:T(8,128)(2,1)}, bf16[384,384]{1,0:T(8,128)(2,1)}, u32[]{:S(2)}, u32[]{:S(2)}) collective-permute-start(bf16[384,384]{1,0:T(8,128)(2,1)} %get-tuple-element.223), channel_id=1, source_target_pairs={{0,3},{1,0},{2,1},{3,2},{4,7},{5,4},{6,5},{7,6},{8,11},{9,8},{10,9... | collective-permute-start | bytes 884744 | tf_op jit(solution)/shard_map/ppermute | solution.py:441
  1164.3 22.5 %collective-permute-start.30 = (bf16[384,384]{1,0:T(8,128)(2,1)}, bf16[384,384]{1,0:T(8,128)(2,1)}, u32[]{:S(2)}, u32[]{:S(2)}) collective-permute-start(bf16[384,384]{1,0:T(8,128)(2,1)} %get-tuple-element.225), channel_id=1, source_target_pairs={{0,1},{1,2},{2,3},{3,0},{4,5},{5,6},{6,7},{7,4},{8,9},{9,10},{10,1... | collective-permute-start | bytes 884744 | tf_op jit(solution)/shard_map/ppermute | solution.py:441
  1168.0 33.6 %collective-permute-start.31 = (bf16[384,384]{1,0:T(8,128)(2,1)}, bf16[384,384]{1,0:T(8,128)(2,1)}, u32[]{:S(2)}, u32[]{:S(2)}) collective-permute-start(bf16[384,384]{1,0:T(8,128)(2,1)} %get-tuple-element.226), channel_id=1, source_target_pairs={{0,2},{1,3},{2,0},{3,1},{4,6},{5,7},{6,4},{7,5},{8,10},{9,11},{10,... | collective-permute-start | bytes 884744 | tf_op jit(solution)/shard_map/ppermute | solution.py:441
  1168.0 38.7 %collective-permute-start.32 = (bf16[384,384]{1,0:T(8,128)(2,1)}, bf16[384,384]{1,0:T(8,128)(2,1)}, u32[]{:S(2)}, u32[]{:S(2)}) collective-permute-start(bf16[384,384]{1,0:T(8,128)(2,1)} %get-tuple-element.227), channel_id=1, source_target_pairs={{0,3},{1,0},{2,1},{3,2},{4,7},{5,4},{6,5},{7,6},{8,11},{9,8},{10,9... | collective-permute-start | bytes 884744 | tf_op jit(solution)/shard_map/ppermute | solution.py:441
  1168.5 53.7 %collective-permute-start.37 = (bf16[384,384]{1,0:T(8,128)(2,1)}, bf16[384,384]{1,0:T(8,128)(2,1)}, u32[]{:S(2)}, u32[]{:S(2)}) collective-permute-start(bf16[384,384]{1,0:T(8,128)(2,1)} %get-tuple-element.248), channel_id=1, source_target_pairs={{0,1},{1,2},{2,3},{3,0},{4,5},{5,6},{6,7},{7,4},{8,9},{9,10},{10,1... | collective-permute-start | bytes 884744 | tf_op jit(solution)/shard_map/ppermute | solution.py:441
  1176.4 45.9 %copy-start.72 = (bf16[384,384]{1,0:T(8,128)(2,1)S(1)}, bf16[384,384]{1,0:T(8,128)(2,1)}, u32[]{:S(2)}) copy-start(bf16[384,384]{1,0:T(8,128)(2,1)} %get-tuple-element.239) | copy-start | bytes 884740
  1178.7 71.3 %copy-start.73 = (bf16[384,384]{1,0:T(8,128)(2,1)S(1)}, bf16[384,384]{1,0:T(8,128)(2,1)}, u32[]{:S(2)}) copy-start(bf16[384,384]{1,0:T(8,128)(2,1)} %get-tuple-element.256) | copy-start | bytes 884740
  1178.7 72.4 %copy-start.74 = (bf16[384,384]{1,0:T(8,128)(2,1)S(1)}, bf16[384,384]{1,0:T(8,128)(2,1)}, u32[]{:S(2)}) copy-start(bf16[384,384]{1,0:T(8,128)(2,1)} %get-tuple-element.260) | copy-start | bytes 884740
  1178.7 72.4 %copy-start.77 = (f32[6,1472]{1,0:T(8,128)}, f32[6,1472]{1,0:T(8,128)S(1)}, u32[]{:S(2)}) copy-start(f32[6,1472]{1,0:T(8,128)S(1)} %add.466) | copy-start | bytes 105988
  1178.7 59.1 %collective-permute-start.38 = (bf16[384,384]{1,0:T(8,128)(2,1)}, bf16[384,384]{1,0:T(8,128)(2,1)S(1)}, u32[]{:S(2)}, u32[]{:S(2)}) collective-permute-start(bf16[384,384]{1,0:T(8,128)(2,1)} %get-tuple-element.249), channel_id=1, source_target_pairs={{0,2},{1,3},{2,0},{3,1},{4,6},{5,7},{6,4},{7,5},{8,10},{9,11},{10,... | collective-permute-start | bytes 884744 | tf_op jit(solution)/shard_map/ppermute | solution.py:441
  1186.8 51.1 %collective-permute-start.39 = (bf16[384,384]{1,0:T(8,128)(2,1)}, bf16[384,384]{1,0:T(8,128)(2,1)S(1)}, u32[]{:S(2)}, u32[]{:S(2)}) collective-permute-start(bf16[384,384]{1,0:T(8,128)(2,1)} %get-tuple-element.250), channel_id=1, source_target_pairs={{0,3},{1,0},{2,1},{3,2},{4,7},{5,4},{6,5},{7,6},{8,11},{9,8},{10,9... | collective-permute-start | bytes 884744 | tf_op jit(solution)/shard_map/ppermute | solution.py:441
  1201.6 36.2 %collective-permute-start.40 = (bf16[384,384]{1,0:T(8,128)(2,1)}, bf16[384,384]{1,0:T(8,128)(2,1)S(1)}, u32[]{:S(2)}, u32[]{:S(2)}) collective-permute-start(bf16[384,384]{1,0:T(8,128)(2,1)} %get-tuple-element.252), channel_id=1, source_target_pairs={{0,1},{1,2},{2,3},{3,0},{4,5},{5,6},{6,7},{7,4},{8,9},{9,10},{10,1... | collective-permute-start | bytes 884744 | tf_op jit(solution)/shard_map/ppermute | solution.py:441
  1206.7 41.9 %collective-permute-start.41 = (bf16[384,384]{1,0:T(8,128)(2,1)}, bf16[384,384]{1,0:T(8,128)(2,1)S(1)}, u32[]{:S(2)}, u32[]{:S(2)}) collective-permute-start(bf16[384,384]{1,0:T(8,128)(2,1)} %get-tuple-element.253), channel_id=1, source_target_pairs={{0,2},{1,3},{2,0},{3,1},{4,6},{5,7},{6,4},{7,5},{8,10},{9,11},{10,... | collective-permute-start | bytes 884744 | tf_op jit(solution)/shard_map/ppermute | solution.py:441
  1222.3 26.3 %collective-permute-start.42 = (bf16[384,384]{1,0:T(8,128)(2,1)}, bf16[384,384]{1,0:T(8,128)(2,1)S(1)}, u32[]{:S(2)}, u32[]{:S(2)}) collective-permute-start(bf16[384,384]{1,0:T(8,128)(2,1)} %get-tuple-element.254), channel_id=1, source_target_pairs={{0,3},{1,0},{2,1},{3,2},{4,7},{5,4},{6,5},{7,6},{8,11},{9,8},{10,9... | collective-permute-start | bytes 884744 | tf_op jit(solution)/shard_map/ppermute | solution.py:441
  (91 other events, 617.4 us)
Sparse Core Ops, SparseCore 0:
  11.4 213.9 all-gather.2
  228.2 234.5 all-gather.4
  748.8 337.6 reduce-scatter.1

commit v6 on v5

--- a/solution.py
+++ b/solution.py
@@ -609,29 +609,34 @@
     branch_ref, normed_ref, up_gelu_ref, up_linear_ref, gelu_ref, linear_ref, down_ref = refs[:7]
     grad_ref, kept_ref, sent_ref, stage_ref, sems = refs[7:]
     step = pl.program_id(0)
-    hidden_steps = FF // TILE
     slot = step % 2
     mine, unit = core_ref[0], core_ref[1]
-
-    def copy(kind, place, at, where):
+    parts = FORWARD_TILE // TILE
+
+    def copy(kind, part, place, at, where):
         spot = pl.ds(pl.multiple_of(at * TILE, TILE), TILE)
-        return pltpu.make_async_copy(
-            stage_ref.at[where, kind], place.at[spot, :], sems.at[where, kind]
-        )
+        source = stage_ref.at[where, kind, part * TILE : (part + 1) * TILE, :]
+        return pltpu.make_async_copy(source, place.at[spot, :], sems.at[where, kind, part])
+
+    def wait(where):
+        for kind in range(3):
+            for part in range(parts):
+                copy(kind, part, kept_ref, 0, where).wait()
 
     def put(kind, turned):
-        target = ATTENTION_TILES + kind * hidden_steps + step
         stage_ref[slot, kind] = turned
-        own = (target // unit) % 2 == mine
-        at = (target // (2 * unit)) * unit + target % unit
-
-        @pl.when(own)
-        def _():
-            copy(kind, kept_ref, at, slot).start()
-
-        @pl.when(jnp.logical_not(own))
-        def _():
-            copy(kind, sent_ref, at, slot).start()
+        for part in range(parts):
+            target = ATTENTION_TILES + kind * (FF // TILE) + step * parts + part
+            own = (target // unit) % 2 == mine
+            at = (target // (2 * unit)) * unit + target % unit
+
+            @pl.when(own)
+            def _(part=part, at=at):
+                copy(kind, part, kept_ref, at, slot).start()
+
+            @pl.when(jnp.logical_not(own))
+            def _(part=part, at=at):
+                copy(kind, part, sent_ref, at, slot).start()
 
     @pl.when(step == 0)
     def _():
@@ -639,8 +644,7 @@
 
     @pl.when(step >= 2)
     def _():
-        for kind in range(3):
-            copy(kind, kept_ref, 0, slot).wait()
+        wait(slot)
 
     grad_hidden = times_rows(branch_ref[...], down_ref[...])
     active, slope = gelu_parts(up_gelu_ref[...])
@@ -654,11 +658,10 @@
         grad_linear, linear_ref[...]
     )
 
-    @pl.when(step == hidden_steps - 1)
+    @pl.when(step == pl.num_programs(0) - 1)
     def _():
-        for back in range(2):
-            for kind in range(3):
-                copy(kind, kept_ref, 0, back).wait()
+        wait(0)
+        wait(1)
 
 
 def unit_tiles(tile):
@@ -669,14 +672,14 @@
 def ffn_backward(branch, normed, up_gelu, up_linear, gathered):
     tokens, width = normed.shape
     rows = 4 * INNER + 3 * FF
-    steps = FF // TILE
+    steps = FF // FORWARD_TILE
     core = jnp.stack([lax.axis_index("c").astype(jnp.int32), jnp.int32(unit_tiles(TILE))])
 
     def weight(kind):
-        first = ATTENTION_TILES + kind * steps
-        return pl.BlockSpec((TILE, width), lambda i, *_: (first + i, 0))
-
-    hidden = pl.BlockSpec((tokens, TILE), lambda i, *_: (0, i))
+        first = 4 * INNER // FORWARD_TILE + kind * steps
+        return pl.BlockSpec((FORWARD_TILE, width), lambda i, *_: (first + i, 0))
+
+    hidden = pl.BlockSpec((tokens, FORWARD_TILE), lambda i, *_: (0, i))
     side = resident((tokens, width))
     anywhere = pl.BlockSpec(memory_space=pl.ANY)
     return pl.pallas_call(
@@ -687,13 +690,13 @@
             in_specs=[side, side, hidden, hidden, weight(0), weight(1), weight(2)],
             out_specs=[side, anywhere, anywhere],
             scratch_shapes=[
-                pltpu.VMEM((2, 3, TILE, tokens), jnp.bfloat16),
-                pltpu.SemaphoreType.DMA((2, 3)),
+                pltpu.VMEM((2, 3, FORWARD_TILE, tokens), jnp.bfloat16),
+                pltpu.SemaphoreType.DMA((2, 3, FORWARD_TILE // TILE)),
             ],
         ),
         out_shape=[jax.ShapeDtypeStruct((tokens, width), jnp.float32)]
         + [jax.ShapeDtypeStruct((rows // 2, tokens), jnp.bfloat16)] * 2,
-        compiler_params=pltpu.CompilerParams(vmem_limit_bytes=48 << 20),
+        compiler_params=pltpu.CompilerParams(vmem_limit_bytes=56 << 20),
         cost_estimate=pl.CostEstimate(
             flops=6 * tokens * FF * width,
             bytes_accessed=6 * FF * width + 14 * tokens * FF,
@@ -703,188 +706,246 @@
     )(core, branch, normed, up_gelu, up_linear, gathered, gathered, gathered)
 
 
-def weight_grads_body(route, tile, place_ref, *refs):
-    own_ref, other_ref = refs[:2]
-    normed_refs, branch_refs = refs[2:4], refs[4:6]
-    outs = refs[6:]
+def spots_of(unit_at, place_ref):
+    here_y, here_x, size_y, size_x = place_ref[0], place_ref[1], place_ref[4], place_ref[5]
+    row, column = unit_at // size_x, unit_at % size_x
+    return (
+        ((row + 2 * size_y - here_y - 1) % size_y, column),
+        ((column + 2 * size_x - here_x - 1) % size_x, row),
+    )
+
+
+def weight_grads_body(tail, tile, place_ref, *refs):
+    own_ref, other_ref, normed_ref, branch_ref, other_normed_ref, other_branch_ref = refs[:6]
+    refs = refs[6:]
     step = pl.program_id(0)
-    count = max(len(outs) // 2, 1)
-    per_place = pl.num_programs(0) // count
-    source = weight_source(route, tile, step, place_ref)
     unit = place_ref[3]
-    at = (source // unit * 2 + place_ref[2]) * unit + source % unit
+    at = (step // unit * 2 + place_ref[2]) * unit + step % unit
     first, second = 4 * INNER // tile, (4 * INNER + 2 * FF) // tile
-
-    def put(product_of):
-        if route == "all":
-            outs[0][:, : CUTS[-1]] = product_of(slice(0, CUTS[-1])).astype(jnp.bfloat16)
-            outs[0][:, CUTS[-1] :] = jnp.zeros((tile, PADDED - CUTS[-1]), jnp.bfloat16)
+    slot = step % 2
+    if tail:
+        stage_ref, sems = refs[-2:]
+        places = split_places(refs[:-2])
+
+    def copy(chunk, place, row, where):
+        source = stage_ref.at[where, :, chunk * CHUNK : (chunk + 1) * CHUNK]
+        spot = pl.ds(pl.multiple_of(row * tile, tile), tile)
+        return pltpu.make_async_copy(source, place.at[spot, :], sems.at[where, chunk])
+
+    def wait(where):
+        for chunk in range(4):
+            copy(chunk, places[chunk % 2][0][chunk // 2], 0, where).wait()
+
+    def put(product):
+        if not tail:
+            refs[0][:, : CUTS[-1]] = product.astype(jnp.bfloat16)
+            refs[0][:, CUTS[-1] :] = jnp.zeros((tile, PADDED - CUTS[-1]), jnp.bfloat16)
             return
-        for turn in range(2):
-            chunk = 2 * turn + (0 if route == "y" else 1)
-            start, end = CUTS[chunk], CUTS[chunk + 1]
-            product = product_of(slice(start, end))
-            for k in range(count):
-
-                @pl.when(step // per_place == k)
-                def _(k=k, turn=turn, product=product, width=end - start):
-                    out = outs[2 * k + turn]
-                    out[:, :width] = product.astype(jnp.bfloat16)
-                    if width < CHUNK:
-                        out[:, width:] = jnp.zeros((tile, CHUNK - width), jnp.bfloat16)
-
-    def both(sides):
-        def product_of(columns):
-            return jnp.dot(
-                own_ref[...], sides[0][:, columns], preferred_element_type=jnp.float32
-            ) + jnp.dot(other_ref[...], sides[1][:, columns], preferred_element_type=jnp.float32)
-
-        return product_of
+        stage_ref[slot, :, : CUTS[-1]] = product.astype(jnp.bfloat16)
+        spots = spots_of(step // unit, place_ref)
+        for chunk in range(4):
+            which, position = spots[chunk % 2]
+            for k, pair in enumerate(places[chunk % 2]):
+
+                @pl.when(which == k)
+                def _(chunk=chunk, place=pair[chunk // 2], row=position * unit + step % unit):
+                    copy(chunk, place, row, slot).start()
+
+    def both(side_ref, other_side_ref):
+        return jnp.dot(
+            own_ref[...], side_ref[:, : CUTS[-1]], preferred_element_type=jnp.float32
+        ) + jnp.dot(
+            other_ref[...], other_side_ref[:, : CUTS[-1]], preferred_element_type=jnp.float32
+        )
+
+    if tail:
+
+        @pl.when(step < 2)
+        def _():
+            stage_ref[slot, :, CUTS[-1] :] = jnp.zeros((tile, PADDED - CUTS[-1]), jnp.bfloat16)
+
+        @pl.when(step >= 2)
+        def _():
+            wait(slot)
 
     @pl.when(at < first)
     def _():
-        put(lambda columns: jnp.zeros((tile, columns.stop - columns.start), jnp.float32))
+        put(jnp.zeros((tile, CUTS[-1]), jnp.float32))
 
     @pl.when((at >= first) & (at < second))
     def _():
-        put(both(normed_refs))
+        put(both(normed_ref, other_normed_ref))
 
     @pl.when(at >= second)
     def _():
-        put(both(branch_refs))
-
-
-def weight_source(route, tile, step, place_ref):
-    size_y, size_x, unit = place_ref[4], place_ref[5], place_ref[3]
-    if route == "all":
-        return step
-    if route == "y":
-        size, others, here = size_y, size_x, place_ref[0]
-    else:
-        size, others, here = size_x, size_y, place_ref[1]
-    per_place = others * unit
-    goal = (here + 1 + step // per_place) % size
-    other = step % per_place // unit
-    row, column = (goal, other) if route == "y" else (other, goal)
-    return (row * size_x + column) * unit + step % unit
-
-
-def weight_grads(route, own, other, sides):
-    rows, tokens = own.shape
-    width = CUTS[-1]
+        put(both(branch_ref, other_branch_ref))
+
+    if tail:
+
+        @pl.when(step == pl.num_programs(0) - 1)
+        def _():
+            wait(0)
+            wait(1)
+
+
+def split_places(refs):
     size_y, size_x = lax.axis_size("y"), lax.axis_size("x")
-    tile = 512 if unit_tiles(256) % 2 == 0 else 256
-    size = {"y": size_y, "x": size_x, "all": 1}[route]
-    steps = rows // tile
-    per_place = steps // size
-    place = jnp.stack(
+    along_y = [refs[2 * k : 2 * k + 2] for k in range(size_y)]
+    along_x = [refs[2 * size_y + 2 * k : 2 * size_y + 2 * k + 2] for k in range(size_x)]
+    return along_y, along_x
+
+
+def place_of(tile):
+    return jnp.stack(
         [
             lax.axis_index("y").astype(jnp.int32),
             lax.axis_index("x").astype(jnp.int32),
             lax.axis_index("c").astype(jnp.int32),
             jnp.int32(unit_tiles(tile)),
-            jnp.int32(size_y),
-            jnp.int32(size_x),
+            jnp.int32(lax.axis_size("y")),
+            jnp.int32(lax.axis_size("x")),
         ]
     )
-    source = pl.BlockSpec(
-        (tile, tokens), lambda i, place_ref: (weight_source(route, tile, i, place_ref), 0)
-    )
-    side = [
-        pl.BlockSpec((tokens, PADDED), lambda i, *_, at=at: (at, 0), pipeline_mode=pl.Buffered(1))
-        for at in range(2)
-    ]
-
-    def out_spec(k):
-        return pl.BlockSpec(
-            (tile, CHUNK), lambda i, *_: (jnp.clip(i - k * per_place, 0, per_place - 1), 0)
-        )
-
-    if route == "all":
+
+
+def half_side(tokens, at):
+    return pl.BlockSpec(
+        (tokens, PADDED), lambda i, *_: (at, 0), pipeline_mode=pl.Buffered(1)
+    )
+
+
+def weight_grads(tail, own, other, sides):
+    rows, tokens = own.shape
+    tile = 512 if unit_tiles(256) % 2 == 0 else 256
+    steps = rows // tile
+    source = pl.BlockSpec((tile, tokens), lambda i, *_: (i, 0))
+    halves = [half_side(tokens, 0), half_side(tokens, 1)]
+    scratch = []
+    if tail:
+        sizes = [lax.axis_size("y")] * 2 * lax.axis_size("y")
+        sizes += [lax.axis_size("x")] * 2 * lax.axis_size("x")
+        out_specs = [pl.BlockSpec(memory_space=pl.ANY)] * len(sizes)
+        out_shape = [jax.ShapeDtypeStruct((rows // n, CHUNK), jnp.bfloat16) for n in sizes]
+        scratch = [pltpu.VMEM((2, tile, PADDED), jnp.bfloat16), pltpu.SemaphoreType.DMA((2, 4))]
+    else:
         out_specs = [pl.BlockSpec((tile, PADDED), lambda i, *_: (i, 0))]
         out_shape = [jax.ShapeDtypeStruct((rows, PADDED), jnp.bfloat16)]
-    else:
-        out_specs = [out_spec(k) for k in range(size) for _ in range(2)]
-        out_shape = [jax.ShapeDtypeStruct((rows // size, CHUNK), jnp.bfloat16)] * (2 * size)
-    results = pl.pallas_call(
-        functools.partial(weight_grads_body, route, tile),
+    return pl.pallas_call(
+        functools.partial(weight_grads_body, tail, tile),
         grid_spec=pltpu.PrefetchScalarGridSpec(
             num_scalar_prefetch=1,
             grid=(steps,),
-            in_specs=[source, source, side[0], side[0], side[1], side[1]],
+            in_specs=[source, source] + halves * 2,
             out_specs=out_specs,
+            scratch_shapes=scratch,
         ),
         out_shape=out_shape,
-        compiler_params=pltpu.CompilerParams(vmem_limit_bytes=32 << 20),
+        compiler_params=pltpu.CompilerParams(vmem_limit_bytes=40 << 20),
         cost_estimate=pl.CostEstimate(
-            flops=2 * rows * tokens * width,
-            bytes_accessed=4 * rows * tokens + rows * width,
+            flops=4 * rows * tokens * CUTS[-1],
+            bytes_accessed=4 * rows * tokens + 2 * rows * PADDED,
             transcendentals=0,
         ),
         name="weight_grads",
-    )(place, own, other, *sides, *sides)
-    if route == "all":
-        return results[0]
-    return [[results[2 * k + turn] for k in range(size)] for turn in range(2)]
-
-
-def attention_rows_body(grad_ref, first_side_ref, second_side_ref, out_ref):
-    turned = grad_ref[...].T
-
-    def put(side_ref):
-        product = jnp.dot(turned, side_ref[...], preferred_element_type=jnp.float32)
-        out_ref[:, : CUTS[-1]] = product.astype(jnp.bfloat16)
-        out_ref[:, CUTS[-1] :] = jnp.zeros((BLOCK, PADDED - CUTS[-1]), jnp.bfloat16)
-
-    @pl.when(pl.program_id(0) < 3 * INNER // BLOCK)
+    )(place_of(tile), own, other, sides[0], sides[0], sides[1], sides[1])
+
+
+def attention_fill_body(tail, owners, place_ref, *refs):
+    own_ref, other_ref, first_ref, second_ref, other_first_ref, other_second_ref = refs[:6]
+    outs = refs[6 + (len(refs) - 8) // 2 : -2]
+    stage_ref, sems = refs[-2:]
+    step = pl.program_id(0)
+    slot = step % 2
+    tile = jnp.minimum(place_ref[2], owners - 1) * pl.num_programs(0) + step
+
+    def copy(chunk, place, row, where):
+        width = CHUNK if tail else PADDED
+        source = stage_ref.at[where, :, chunk * width : (chunk + 1) * width]
+        spot = pl.ds(pl.multiple_of(row * INNER, INNER), INNER)
+        return pltpu.make_async_copy(source, place.at[spot, :], sems.at[where, chunk])
+
+    places = split_places(outs) if tail else None
+
+    def wait(where):
+        for chunk in range(4 if tail else 1):
+            place = places[chunk % 2][0][chunk // 2] if tail else outs[0]
+            copy(chunk, place, 0, where).wait()
+
+    def put(side_ref, other_side_ref):
+        product = jnp.dot(
+            own_ref[...].T, side_ref[:, : CUTS[-1]], preferred_element_type=jnp.float32
+        ) + jnp.dot(
+            other_ref[...].T, other_side_ref[:, : CUTS[-1]], preferred_element_type=jnp.float32
+        )
+        stage_ref[slot, :, : CUTS[-1]] = product.astype(jnp.bfloat16)
+        stage_ref[slot, :, CUTS[-1] :] = jnp.zeros((INNER, PADDED - CUTS[-1]), jnp.bfloat16)
+        if not tail:
+            copy(0, outs[0], step, slot).start()
+            return
+        spots = spots_of(0, place_ref)
+        for chunk in range(4):
+            which, _ = spots[chunk % 2]
+            for k, pair in enumerate(places[chunk % 2]):
+
+                @pl.when(which == k)
+                def _(chunk=chunk, place=pair[chunk // 2]):
+                    copy(chunk, place, step, slot).start()
+
+    @pl.when(place_ref[2] < owners)
     def _():
-        put(first_side_ref)
-
-    @pl.when(pl.program_id(0) >= 3 * INNER // BLOCK)
-    def _():
-        put(second_side_ref)
-
-
-def attention_rows(grads, first_side, second_side):
-    tokens, width = first_side.shape
+        @pl.when(step >= 2)
+        def _():
+            wait(slot)
+
+        @pl.when(tile < 3)
+        def _():
+            put(first_ref, other_first_ref)
+
+        @pl.when(tile >= 3)
+        def _():
+            put(second_ref, other_second_ref)
+
+        @pl.when(step == pl.num_programs(0) - 1)
+        def _():
+            wait(0)
+            wait(1)
+
+
+def attention_fill(tail, arrays, own, other, sides):
+    tokens = own.shape[0]
+    unit_rows = unit_tiles(TILE) * TILE
+    owners = 4 * INNER // unit_rows
+    steps = unit_rows // INNER
+
+    def column(i, place_ref):
+        return 0, jnp.minimum(place_ref[2], owners - 1) * steps + i
+
+    halves = [half_side(tokens, 0), half_side(tokens, 1)]
+    anywhere = pl.BlockSpec(memory_space=pl.ANY)
     return pl.pallas_call(
-        attention_rows_body,
-        grid=(4 * INNER // BLOCK,),
-        in_specs=[
-            pl.BlockSpec((tokens, BLOCK), lambda i: (0, i)),
-            resident((tokens, width)),
-            resident((tokens, width)),
-        ],
-        out_specs=pl.BlockSpec((BLOCK, PADDED), lambda i: (i, 0)),
-        out_shape=jax.ShapeDtypeStruct((4 * INNER, PADDED), jnp.bfloat16),
+        functools.partial(attention_fill_body, tail, owners),
+        grid_spec=pltpu.PrefetchScalarGridSpec(
+            num_scalar_prefetch=1,
+            grid=(steps,),
+            in_specs=[pl.BlockSpec((tokens, INNER), column)] * 2
+            + halves * 2
+            + [anywhere] * len(arrays),
+            out_specs=[anywhere] * len(arrays),
+            scratch_shapes=[
+                pltpu.VMEM((2, INNER, PADDED), jnp.bfloat16),
+                pltpu.SemaphoreType.DMA((2, 4)),
+            ],
+        ),
+        out_shape=[jax.ShapeDtypeStruct(array.shape, array.dtype) for array in arrays],
+        input_output_aliases={7 + k: k for k in range(len(arrays))},
+        compiler_params=pltpu.CompilerParams(vmem_limit_bytes=32 << 20),
         cost_estimate=pl.CostEstimate(
-            flops=8 * tokens * INNER * width,
-            bytes_accessed=8 * INNER * PADDED + 8 * tokens * width,
+            flops=4 * unit_rows * tokens * CUTS[-1],
+            bytes_accessed=4 * unit_rows * tokens + 2 * unit_rows * PADDED,
             transcendentals=0,
         ),
-        name="attention_rows",
-    )(grads, first_side, second_side)
-
-
-def with_attention(route, chunk, arrays, rows):
-    unit_rows = rows.shape[0]
-    if route == "all":
-        here = lax.axis_index("c") < 4 * INNER // unit_rows
-        filled = jnp.where(here, rows, arrays[0][:unit_rows])
-        return [lax.dynamic_update_slice(arrays[0], filled, (0, 0))]
-    size = lax.axis_size(route)
-    owners = 4 * INNER // unit_rows
-    columns = rows[:, chunk * CHUNK : (chunk + 1) * CHUNK]
-    filled = []
-    for k, array in enumerate(arrays):
-        here = (lax.axis_index(route) + 1 + k) % size == 0
-        here = here & (lax.axis_index("c") < owners)
-        filled.append(
-            lax.dynamic_update_slice(
-                array, jnp.where(here, columns, array[:unit_rows]), (0, 0)
-            )
-        )
-    return filled
+        name="attention_fill",
+    )(place_of(TILE), own, other, sides[0], sides[0], sides[1], sides[1], *arrays)
 
 
 def tied(first, second):
@@ -993,48 +1054,36 @@
     grad_middle, grad_gain_two = rms_backward(middle, inverse_two, gain_two, grad_normed_two)
     grad_middle = grad_out + grad_middle
     middle_low = grad_middle.astype(jnp.bfloat16)
+    late_sides = jnp.concatenate([normed_low, middle_low], axis=0)
+    late_sides = jnp.pad(late_sides, ((0, 0), (0, PADDED - late_sides.shape[1])))
+    late_sides = (late_sides, shift(late_sides, "c", 1))
     grad_mixed = times_rows(middle_low, gathered[3 * INNER : 4 * INNER]).astype(jnp.bfloat16)
     grad_query, grad_shared, grad_table = attend_backward(
         queries, grad_mixed, shared, log_total, context
     )
     grad_shared, own = lax.optimization_barrier((grad_shared, own))
     moving = start_back(grad_shared, tokens)
-    routes = ("y", "x") if tail else ("all",)
-    routed = {
-        route: weight_grads(route, own, other, sides) for route in routes
-    }
-    routed, moving = lax.optimization_barrier((routed, moving))
+    arrays = weight_grads(tail, own, other, sides)
+    arrays, moving = lax.optimization_barrier((arrays, moving))
     grad_own = finish_back(*moving)
     grad_gate = grad_own[:, 2 * INNER :]
     grad_input_low = jnp.concatenate(
         [grad_query, grad_own[:, : 2 * INNER].astype(jnp.bfloat16)], axis=1
     )
-    rows = attention_rows(
-        jnp.concatenate([grad_input_low, attended], axis=1), normed_low, middle_low
-    )
-    unit_rows = unit_tiles(TILE) * TILE
-    core = lax.axis_index("c")
-    owners = 4 * INNER // unit_rows
-    kept_rows, sent_rows = (
-        lax.dynamic_slice_in_dim(rows, jnp.minimum(at, owners - 1) * unit_rows, unit_rows, 0)
-        if owners > 1
-        else rows
-        for at in (core, 1 - core)
-    )
-    rows = total_of(kept_rows, [shift(sent_rows, "c", 1)])
+    late = jnp.concatenate([grad_input_low, attended], axis=1)
+    arrays = attention_fill(tail, arrays, late, shift(late, "c", 1), late_sides)
     if tail:
         scatter = Scatter()
         for chunk in range(4):
             route = ("y", "x", "z") if chunk % 2 == 0 else ("x", "y", "z")
-            arrays = with_attention(route[0], chunk, routed[route[0]][chunk // 2], rows)
-            scatter.push(chunk, route, arrays[-1], arrays[:-1])
-        grad_input_low = scatter.step(grad_input_low, 0, 1, 2, 3)
+            ordered = [pair[chunk // 2] for pair in split_places(arrays)[chunk % 2]]
+            scatter.push(chunk, route, ordered[-1], ordered[:-1])
+        grad_input_low = scatter.step(grad_input_low, 0, 1)
     else:
-        scatter = with_attention("all", 0, [routed["all"]], rows)[0]
-        scatter, grad_input_low, grad_gate = lax.optimization_barrier(
-            (scatter, grad_input_low, grad_gate)
+        arrays, grad_input_low, grad_gate = lax.optimization_barrier(
+            (arrays, grad_input_low, grad_gate)
         )
-        scatter = lax.psum_scatter(scatter, ("y", "x", "z"), scatter_dimension=0, tiled=True)
+        scatter = lax.psum_scatter(arrays[0], ("y", "x", "z"), scatter_dimension=0, tiled=True)
     grad_normed = times_plain(grad_input_low, gathered[: 3 * INNER])
     grad_stream, grad_gain_one = rms_backward(stream, inverse_one, gain_one, grad_normed)
     return (grad_middle + grad_stream, grad_table, grad_gate, grad_gain_one, grad_gain_two, scatter)
@@ -1090,12 +1139,13 @@
     )
     small = hop(small_sums, "c")
     small = scatter.step(small, 0, 1)
+    small = scatter.step(small, 2, 3)
     small = hop(small, "z", 1)
-    small = scatter.step(small, 2, 3)
+    small = scatter.step(small, 0, 1)
     for bit in range(2, lax.axis_size("z")):
         if bit & (bit - 1) == 0:
             small = hop(small, "z", bit)
-    small = scatter.step(small, 0, 1)
+    small = scatter.step(small, 2, 3)
     small = scatter.step(small, 2, 3)
     small = hop(small, "x")
     for bit in range(1, lax.axis_size("y")):

time: 1270 us -> 1210 us (0.953)
  starting transfers between devices: 153 us -> 87.1 us
  waiting for transfers between devices: 579 us -> 626 us
  other arithmetic: 96.8 us -> 73.5 us
  local copies, waits for them, and re-layouts: 77.9 us -> 63 us
    ppermute x26 -> x28, starting transfers between devices: 91.9 us -> 51.4 us  [shift(): lax.ppermute(value, axis, [(i, (i + amount) % count) for i in range(count)])]
    ppermute x26 -> x28, waiting for transfers between devices: 165 us -> 202 us  [shift(): lax.ppermute(value, axis, [(i, (i + amount) % count) for i in range(count)])]
    dynamic_update_slice x3 -> x0, other arithmetic: 19.3 us -> none  [the longest x2 10.1 us: with_attention(): lax.dynamic_update_slice(array, jnp.where(here, columns, array[:unit_rows...]
    pallas_call x5 -> x4, Pallas kernels: 86.8 us -> 67.7 us  [the longest x2 46.7 us: weight_grads(): pl.pallas_call(functools.partial(weight_grads_body, tail, tile), grid_spe...]
    pallas_call x2, Pallas kernels: 55.3 us -> 74 us  [attend_backward(): pl.pallas_call(functools.partial(backward_body, width > 2 * INNER), grid_...]
    pallas_call x2, Pallas kernels: 80.5 us -> 66 us  [ffn_backward(): pl.pallas_call(ffn_backward_body, grid_spec=pltpu.PrefetchScalarGridSpec(...]
    unnamed x233 -> x211, local copies, waits for them, and re-layouts: 53.9 us -> 39.7 us
    ppermute x8, starting transfers between devices: 39.9 us -> 25.6 us  [slide(): return lax.ppermute(value, 'z', pairs)]
  transfers between devices with their start and end apart: 46 -> 48, of which waited for: 16 -> 23; matrix products, arithmetic and copies ran while one was open for 12% -> 11% of each run, Pallas kernels for 17% -> 18%
where the time goes in v6:
time: 1210 us
  waiting for transfers between devices  626 us (52%)
  Pallas kernels  309 us (26%)
  starting transfers between devices  87.1 us (7%)
  other arithmetic  73.5 us (6%)
  local copies, waits for them, and re-layouts  63 us (5%)
  matrix products  33.2 us (3%)
  between operations  15.6 us (1%)
    all_gather x2, waiting for transfers between devices, fetch_rows(): return lax.all_gather(local_rows, DEVICES, axis=0, tiled=True)  323 us
    ppermute x28, waiting for transfers between devices, shift(): lax.ppermute(value, axis, [(i, (i + amount) % count) for i in range(count)])  202 us
    pallas_call x2, Pallas kernels, attend_backward(): pl.pallas_call(functools.partial(backward_body, width > 2 * INNER), grid_...  74 us
    pallas_call x2, Pallas kernels, ffn_backward(): pl.pallas_call(ffn_backward_body, grid_spec=pltpu.PrefetchScalarGridSpec(...  66 us
    ppermute x4, waiting for transfers between devices, far_pair(): got = lax.ppermute(sent, 'z', pairs)  65.2 us
    ppermute x28, starting transfers between devices, shift(): lax.ppermute(value, axis, [(i, (i + amount) % count) for i in range(count)])  51.4 us
    pallas_call x2, Pallas kernels, ffn_forward(): pl.pallas_call(ffn_forward_body, grid=(steps,), in_specs=[resident((token...  49.6 us
    pallas_call x2, Pallas kernels, attend_forward(): pl.pallas_call(functools.partial(forward_body, width > 2 * INNER), grid_s...  47 us
  transfers between devices with their start and end apart: 48, of which 23 were waited for; matrix products, arithmetic and copies ran while one was open for 11% of the time, Pallas kernels for 18%

profile of v6, /device:TPU:24, one launch (start us, length us, event | category | flops | bytes accessed | tf_op | source)
XLA Modules:
  0.0 1207.1 jit_solution(11989701866412768427)
XLA Ops:
  7.2 2.5 copy.113
  12.0 2.4 copy.112
  18.1 207.3 %all-gather.3.cloned.1.call-done.gelu_ref.linear_ref.down_ref.refs_4_.refs_5_.refs_6_ = bf16[12288,1472]{1,0:T(8,128)(2,1)} async-done(((bf16[384,1472]{1,0:T(8,128)(2,1)}), bf16[12288,1472]{1,0:T(8,128)(2,1)}) %all-gather.3.cloned.1.call-update) | async-done | bytes 36175888 | tf_op jit(solution)/shard_map/all_gather | solution.py:996
  225.4 4.7 fusion.33
  234.4 6.0 collective-permute-start.2
  241.2 4.7 bias_tiles.1.refs_4_.refs_5_
  245.9 3.5 copy.118
  250.5 22.6 %collective-permute-done = bf16[288,768]{1,0:T(8,128)(2,1)} collective-permute-done((bf16[288,768]{1,0:T(8,128)(2,1)}, bf16[288,768]{1,0:T(8,128)(2,1)}, u32[]{:S(2)}, u32[]{:S(2)}) %collective-permute-start) | collective-permute-done | bytes 442400 | tf_op jit(solution)/shard_map/ppermute | solution.py:455
  274.3 14.3 %collective-permute-done.1 = bf16[512,768]{1,0:T(8,128)(2,1)} collective-permute-done((bf16[512,768]{1,0:T(8,128)(2,1)}, bf16[512,768]{1,0:T(8,128)(2,1)}, u32[]{:S(2)}, u32[]{:S(2)}) %collective-permute-start.1) | collective-permute-done | bytes 786464 | tf_op jit(solution)/shard_map/ppermute | solution.py:447
  291.4 23.4 %attend_forward.2 = (bf16[512,384]{1,0:T(8,128)(2,1)S(1)}, f32[4,8,256]{2,1,0:T(8,128)S(1)}) custom-call(s32[4]{0:T(128)S(1)} %get-tuple-element.413.low_ref, s32[4]{0:T(128)S(1)} %get-tuple-element.412.high_ref, bf16[512,384]{1,0:T(8,128)(2,1)S(1)} %slice.174.refs_0_, bf16[2304,768]{1,0:T(8,128)(2,1)S(1)} %pad_dynamic-update-slice_fusion.2.refs_1_.refs_2_, ...), custom_call_target="tpu_custom_call" | custom-call | flops 1811939328 | bytes 8388608 | tf_op jit(solution)/shard_map/attend_forward/pallas_call | solution.py:197
  314.9 2.5 multiply_reduce_fusion.10
  319.1 24.9 %ffn_forward.2 = (f32[512,1472]{1,0:T(8,128)S(1)}, f32[512,3584]{1,0:T(8,128)}, f32[512,3584]{1,0:T(8,128)}) custom-call(bf16[512,1472]{1,0:T(8,128)(2,1)S(1)} %multiply_convert_fusion.2.normed_ref.refs_1_, f32[512,1472]{1,0:T(8,128)} %copy-done.39, bf16[12288,1472]{1,0:T(8,128)(2,1)} %all-gather.3.cloned.1.call-done.gelu_ref.linear_ref.down_ref.refs_4_.refs_5_.refs_6_, ...), custom_call_target="tpu_custom_call" | custom-call | flops 16206790656 | bytes 46333952 | tf_op jit(solution)/shard_map/ffn_forward/pallas_call | solution.py:582
  347.2 115.9 %all-gather.5.cloned.1.call-done.gelu_ref.linear_ref.down_ref.refs_4_.refs_5_.refs_6_ = bf16[12288,1472]{1,0:T(8,128)(2,1)} async-done(((bf16[384,1472]{1,0:T(8,128)(2,1)}), bf16[12288,1472]{1,0:T(8,128)(2,1)}) %all-gather.5.cloned.1.call-update) | async-done | bytes 36175888 | tf_op jit(solution)/shard_map/all_gather | solution.py:996
  463.1 4.7 fusion.36
  470.1 4.4 collective-permute-start.5
  480.1 39.8 %collective-permute-done.3 = bf16[288,896]{1,0:T(8,128)(2,1)} collective-permute-done((bf16[288,896]{1,0:T(8,128)(2,1)}, bf16[288,896]{1,0:T(8,128)(2,1)}, u32[]{:S(2)}, u32[]{:S(2)}) %collective-permute-start.3) | collective-permute-done | bytes 516128 | tf_op jit(solution)/shard_map/ppermute | solution.py:455
  524.1 23.6 %attend_forward.3 = (bf16[512,384]{1,0:T(8,128)(2,1)S(1)}, f32[4,8,256]{2,1,0:T(8,128)S(1)}) custom-call(s32[4]{0:T(128)S(1)} %get-tuple-element.413.low_ref, s32[4]{0:T(128)S(1)} %get-tuple-element.412.high_ref, bf16[512,384]{1,0:T(8,128)(2,1)S(1)} %slice.180.refs_0_, bf16[2304,896]{1,0:T(8,128)(2,1)S(1)} %pad_dynamic-update-slice_fusion.refs_1_.refs_2_, ...), custom_call_target="tpu_custom_call" | custom-call | flops 1811939328 | bytes 8388608 | tf_op jit(solution)/shard_map/attend_forward/pallas_call | solution.py:197
  547.8 2.4 multiply_reduce_fusion.7
  551.9 24.6 %ffn_forward.3 = (f32[512,1472]{1,0:T(8,128)S(1)}, f32[512,3584]{1,0:T(8,128)}, f32[512,3584]{1,0:T(8,128)}) custom-call(bf16[512,1472]{1,0:T(8,128)(2,1)S(1)} %multiply_convert_fusion.normed_ref.refs_1_, f32[512,1472]{1,0:T(8,128)} %copy-done.41, bf16[12288,1472]{1,0:T(8,128)(2,1)} %all-gather.5.cloned.1.call-done.gelu_ref.linear_ref.down_ref.refs_4_.refs_5_.refs_6_, ...), custom_call_target="tpu_custom_call" | custom-call | flops 16206790656 | bytes 46333952 | tf_op jit(solution)/shard_map/ffn_forward/pallas_call | solution.py:582
  576.6 32.6 %ffn_backward.2 = (f32[512,1472]{1,0:T(8,128)}, bf16[6144,512]{1,0:T(8,128)(2,1)}, bf16[6144,512]{1,0:T(8,128)(2,1)}) custom-call(s32[2]{0:T(128)} %pad_add_fusion.core_ref, bf16[512,1472]{1,0:T(8,128)(2,1)} %bitcast_convert_fusion.refs_0_, bf16[512,1472]{1,0:T(8,128)(2,1)} %copy-done.2, f32[512,3584]{1,0:T(8,128)} %get-tuple-element.150.refs_2_, ...), custom_call_target="tpu_custom_call" | custom-call | flops 16206790656 | bytes 57344000 | tf_op jit(solution)/shard_map/ffn_backward/pallas_call | solution.py:685
  610.5 2.3 fusion.11.refs_2_.refs_3_
  616.6 2.5 fusion.51
  619.2 2.9 convolution_convert_fusion.1.refs_1_
  622.1 38.0 %attend_backward.2 = (bf16[512,384]{1,0:T(8,128)(2,1)S(1)}, bf16[2304,896]{1,0:T(8,128)(2,1)}, f32[3,32,256]{2,1,0:T(8,128)S(1)}) custom-call(s32[4]{0:T(128)S(1)} %get-tuple-element.413.low_ref, s32[4]{0:T(128)S(1)} %get-tuple-element.412.high_ref, bf16[512,384]{1,0:T(8,128)(2,1)S(1)} %copy-done.28, bf16[512,384]{1,0:T(8,128)(2,1)S(1)} %convolution_convert_fusion.1.refs_1_, ...), custom_call_target="tpu_custom_call" | custom-call | flops 4529848320 | bytes 12582912 | tf_op jit(solution)/shard_map/attend_backward/pallas_call | solution.py:347
  661.7 2.7 fusion.52
  665.7 4.6 collective-permute-start.8
  670.4 3.4 fusion.12.refs_2_.refs_3_
  673.8 21.8 %weight_grads.2.refs_6_ = bf16[6144,1536]{1,0:T(8,128)(2,1)} custom-call(s32[6]{0:T(128)S(1)} %stack.55.place_ref, bf16[6144,512]{1,0:T(8,128)(2,1)S(1)} %bitcast.114, bf16[6144,512]{1,0:T(8,128)(2,1)} %collective-permute-done.6.refs_1_, bf16[1024,1536]{1,0:T(8,128)(2,1)S(1)} %fusion.11.refs_2_.refs_3_, bf16[1024,1536]{1,0:T(8,128)(2,1)S(1)} %fusion.11.refs_2_.refs_3_, ...), custom_call_target="tpu_custom_call" | custom-call | flops 18522046464 | bytes 31457280 | tf_op jit(solution)/shard_map/weight_grads/pallas_call | solution.py:833
  698.2 3.6 collective-permute-start.11
  702.6 2.4 pad_maximum_fusion.6
  705.2 10.6 attention_fill.2
  718.5 5.6 multiply_reduce_fusion.2
  724.2 2.5 fusion.49
  726.7 33.4 %ffn_backward.3 = (f32[512,1472]{1,0:T(8,128)}, bf16[6144,512]{1,0:T(8,128)(2,1)}, bf16[6144,512]{1,0:T(8,128)(2,1)}) custom-call(s32[2]{0:T(128)} %pad_add_fusion.core_ref, bf16[512,1472]{1,0:T(8,128)(2,1)} %get-tuple-element.352.refs_0_, bf16[512,1472]{1,0:T(8,128)(2,1)} %copy-done, f32[512,3584]{1,0:T(8,128)} %get-tuple-element.167.refs_2_, ...), custom_call_target="tpu_custom_call" | custom-call | flops 16206790656 | bytes 57344000 | tf_op jit(solution)/shard_map/ffn_backward/pallas_call | solution.py:685
  764.9 2.4 fusion.48
  767.4 2.4 convolution_convert_fusion.refs_1_
  769.9 36.0 %attend_backward.3 = (bf16[512,384]{1,0:T(8,128)(2,1)S(1)}, bf16[2304,768]{1,0:T(8,128)(2,1)}, f32[3,32,256]{2,1,0:T(8,128)S(1)}) custom-call(s32[4]{0:T(128)S(1)} %get-tuple-element.413.low_ref, s32[4]{0:T(128)S(1)} %get-tuple-element.412.high_ref, bf16[512,384]{1,0:T(8,128)(2,1)S(1)} %copy-done.31, bf16[512,384]{1,0:T(8,128)(2,1)S(1)} %convolution_convert_fusion.refs_1_, ...), custom_call_target="tpu_custom_call" | custom-call | flops 4529848320 | bytes 12582912 | tf_op jit(solution)/shard_map/attend_backward/pallas_call | solution.py:347
  808.0 2.6 fusion.53
  811.9 5.5 collective-permute-start.15
  817.8 24.9 %weight_grads.3 = (bf16[3072,384]{1,0:T(8,128)(2,1)}, bf16[3072,384]{1,0:T(8,128)(2,1)S(1)}, bf16[3072,384]{1,0:T(8,128)(2,1)S(1)}, bf16[3072,384]{1,0:T(8,128)(...) custom-call(s32[6]{0:T(128)S(1)} %stack.55.place_ref, ...), custom_call_target="tpu_custom_call" | custom-call | flops 18522046464 | bytes 31457280 | tf_op jit(solution)/shard_map/weight_grads/pallas_call | solution.py:833
  842.7 2.8 collective-permute-done.17
  845.5 11.9 collective-permute-done.16
  864.4 10.4 attention_fill.3
  883.6 7.9 fusion.24
  893.5 59.2 %collective-permute-done.20 = bf16[3072,384]{1,0:T(8,128)(2,1)} collective-permute-done((bf16[3072,384]{1,0:T(8,128)(2,1)}, bf16[3072,384]{1,0:T(8,128)(2,1)}, u32[]{:S(2)}, u32[]{:S(2)}) %collective-permute-start.20) | collective-permute-done | bytes 2359328 | tf_op jit(solution)/shard_map/ppermute | solution.py:441
  952.8 2.3 add_convert_fusion.3
  967.4 5.4 collective-permute-done.25
  973.6 18.5 %collective-permute-done.23 = bf16[1536,384]{1,0:T(8,128)(2,1)} collective-permute-done((bf16[1536,384]{1,0:T(8,128)(2,1)}, bf16[1536,384]{1,0:T(8,128)(2,1)}, u32[]{:S(2)}, u32[]{:S(2)}) %collective-permute-start.23) | collective-permute-done | bytes 1179680 | tf_op jit(solution)/shard_map/ppermute | solution.py:441
  992.1 7.7 collective-permute-done.24
  1005.7 3.0 collective-permute-start.34
  1010.7 55.9 %collective-permute-done.32 = bf16[3072,384]{1,0:T(8,128)(2,1)} collective-permute-done((bf16[3072,384]{1,0:T(8,128)(2,1)S(1)}, bf16[3072,384]{1,0:T(8,128)(2,1)}, u32[]{:S(2)}, u32[]{:S(2)}) %collective-permute-start.32) | collective-permute-done | bytes 2359328 | tf_op jit(solution)/shard_map/ppermute | solution.py:441
  1066.6 2.3 add_convert_fusion.1
  1077.7 22.0 %collective-permute-done.35 = bf16[1536,384]{1,0:T(8,128)(2,1)S(1)} collective-permute-done((bf16[1536,384]{1,0:T(8,128)(2,1)S(1)}, bf16[1536,384]{1,0:T(8,128)(2,1)S(1)}, u32[]{:S(2)}, u32[]{:S(2)}) %collective-permute-start.35) | collective-permute-done | bytes 1179680 | tf_op jit(solution)/shard_map/ppermute | solution.py:441
  1104.2 2.3 copy.127
  1110.5 3.4 collective-permute-start.29
  1114.5 3.3 collective-permute-start.39
  1117.7 4.5 fusion.21
  1122.2 2.3 copy.128
  1124.6 9.9 collective-permute-start.40
  1134.5 16.3 %collective-permute-done.30 = bf16[384,384]{1,0:T(8,128)(2,1)} collective-permute-done((bf16[384,384]{1,0:T(8,128)(2,1)}, bf16[384,384]{1,0:T(8,128)(2,1)}, u32[]{:S(2)}, u32[]{:S(2)}) %collective-permute-start.30) | collective-permute-done | bytes 294944 | tf_op jit(solution)/shard_map/ppermute | solution.py:441
  1150.7 3.6 collective-permute-start.42
  1154.3 13.2 %collective-permute-start.43 = (bf16[384,384]{1,0:T(8,128)(2,1)}, bf16[384,384]{1,0:T(8,128)(2,1)S(1)}, u32[]{:S(2)}, u32[]{:S(2)}) collective-permute-start(bf16[384,384]{1,0:T(8,128)(2,1)} %get-tuple-element.271), channel_id=1, source_target_pairs={{0,2},{1,3},{2,0},{3,1},{4,6},{5,7},{6,4},{7,5},{8,10},{9,11},{10,... | collective-permute-start | bytes 884744 | tf_op jit(solution)/shard_map/ppermute | solution.py:441
  1171.2 9.3 collective-permute-done.40
  1180.6 10.0 collective-permute-done.43
  (382 shorter events, 127.3 us)
Async XLA Ops:
  7.2 218.2 %all-gather.3.cloned.1.call-start = ((), (), s32[]{:S(2)}) async-start(), calls=%async_computation.1 | async-start | bytes 38928384 | tf_op jit(solution)/shard_map/all_gather | solution.py:996
  9.7 453.4 %all-gather.5.cloned.1.call-start = ((), (), s32[]{:S(2)}) async-start(), calls=%async_computation.2 | async-start | bytes 38928384 | tf_op jit(solution)/shard_map/all_gather | solution.py:996
  11.9 1185.1 %reduce-scatter.2.cloned.1.call-start = ((), (), s32[]{:S(2)}) async-start(), calls=%async_computation.3 | async-start | bytes 20054016 | tf_op jit(solution)/shard_map/reduce_scatter | solution.py:1086
  14.4 300.5 %copy-start.38 = (f32[1,512,1472]{2,1,0:T(8,128)}, f32[1,512,1472]{2,1,0:T(8,128)S(1)}, u32[]{:S(2)}) copy-start(f32[1,512,1472]{2,1,0:T(8,128)S(1)} %copy.112) | copy-start | bytes 9043972
  15.1 303.0 %copy-start.67 = (f32[1472]{0:T(1024)}, f32[1472]{0:T(1024)S(1)}, u32[]{:S(2)}) copy-start(f32[1472]{0:T(1024)S(1)} %get-tuple-element.343) | copy-start | bytes 17668
  15.1 329.8 %copy-start.71 = (f32[1472]{0:T(1024)}, f32[1472]{0:T(1024)S(1)}, u32[]{:S(2)}) copy-start(f32[1472]{0:T(1024)S(1)} %get-tuple-element.345) | copy-start | bytes 17668
  18.1 222.4 %copy-start.94 = (f32[32,6]{0,1:T(8,128)S(1)}, f32[32,6]{0,1:T(8,128)}, u32[]{:S(2)}) copy-start(f32[32,6]{0,1:T(8,128)} %param.13) | copy-start | bytes 2308
  232.0 41.2 %collective-permute-start = (bf16[288,768]{1,0:T(8,128)(2,1)}, bf16[288,768]{1,0:T(8,128)(2,1)}, u32[]{:S(2)}, u32[]{:S(2)}) collective-permute-start(bf16[288,768]{1,0:T(8,128)(2,1)} %slice_select_fusion.1), channel_id=1, source_target_pairs={{0,2},{1,3},{2,0},{3,1},{4,6},{5,7},{6,4},{7,5},{8,10},{9,11},{10,... | collective-permute-start | bytes 1327112 | tf_op jit(solution)/shard_map/ppermute | solution.py:455
  232.6 55.9 %collective-permute-start.1 = (bf16[512,768]{1,0:T(8,128)(2,1)}, bf16[512,768]{1,0:T(8,128)(2,1)}, u32[]{:S(2)}, u32[]{:S(2)}) collective-permute-start(bf16[512,768]{1,0:T(8,128)(2,1)} %slice.177), channel_id=1, source_target_pairs={{0,1},{1,2},{2,3},{4,5},{5,6},{6,7},{8,9},{9,10},{10,11},{12,13},{... | collective-permute-start | bytes 2359304 | tf_op jit(solution)/shard_map/ppermute | solution.py:447
  234.4 55.4 %collective-permute-start.2 = (bf16[512,768]{1,0:T(8,128)(2,1)}, bf16[512,768]{1,0:T(8,128)(2,1)}, u32[]{:S(2)}, u32[]{:S(2)}) collective-permute-start(bf16[512,768]{1,0:T(8,128)(2,1)} %slice.177), channel_id=1, source_target_pairs={{1,0},{2,1},{3,2},{5,4},{6,5},{7,6},{9,8},{10,9},{11,10},{13,12},{... | collective-permute-start | bytes 2359304 | tf_op jit(solution)/shard_map/ppermute | solution.py:447
  249.4 40.3 %copy-start.55 = (bf16[512,1152]{1,0:T(8,128)(2,1)S(1)}, bf16[512,1152]{1,0:T(8,128)(2,1)}, u32[]{:S(2)}) copy-start(bf16[512,1152]{1,0:T(8,128)(2,1)} %copy-done.54) | copy-start | bytes 3538948
  250.5 40.9 %copy-start.30 = (bf16[512,384]{1,0:T(8,128)(2,1)}, bf16[512,384]{1,0:T(8,128)(2,1)S(1)}, u32[]{:S(2)}) copy-start(bf16[512,384]{1,0:T(8,128)(2,1)S(1)} %slice.174.refs_0_) | copy-start | bytes 1179652
  344.9 123.0 %copy-start.83 = (f32[512]{0:T(512)}, f32[512]{0:T(512)S(1)}, u32[]{:S(2)}) copy-start(f32[512]{0:T(512)S(1)} %get-tuple-element.403) | copy-start | bytes 6148
  347.2 120.7 %copy-start.85 = (f32[512]{0:T(512)}, f32[512]{0:T(512)S(1)}, u32[]{:S(2)}) copy-start(f32[512]{0:T(512)S(1)} %get-tuple-element.357) | copy-start | bytes 6148
  470.1 52.6 %collective-permute-start.5 = (bf16[512,896]{1,0:T(8,128)(2,1)}, bf16[512,896]{1,0:T(8,128)(2,1)}, u32[]{:S(2)}, u32[]{:S(2)}) collective-permute-start(bf16[512,896]{1,0:T(8,128)(2,1)} %pad_maximum_fusion.3), channel_id=1, source_target_pairs={{1,0},{2,1},{3,2},{5,4},{6,5},{7,6},{9,8},{10,9},{11,10},{13,12},{... | collective-permute-start | bytes 2752520 | tf_op jit(solution)/shard_map/ppermute | solution.py:447
  474.5 46.6 %collective-permute-start.4 = (bf16[512,896]{1,0:T(8,128)(2,1)}, bf16[512,896]{1,0:T(8,128)(2,1)}, u32[]{:S(2)}, u32[]{:S(2)}) collective-permute-start(bf16[512,896]{1,0:T(8,128)(2,1)} %pad_maximum_fusion.3), channel_id=1, source_target_pairs={{0,1},{1,2},{2,3},{4,5},{5,6},{6,7},{8,9},{9,10},{10,11},{12,13},{... | collective-permute-start | bytes 2752520 | tf_op jit(solution)/shard_map/ppermute | solution.py:447
  475.8 44.1 %collective-permute-start.3 = (bf16[288,896]{1,0:T(8,128)(2,1)}, bf16[288,896]{1,0:T(8,128)(2,1)}, u32[]{:S(2)}, u32[]{:S(2)}) collective-permute-start(bf16[288,896]{1,0:T(8,128)(2,1)} %fusion.44), channel_id=1, source_target_pairs={{0,2},{1,3},{2,0},{3,1},{4,6},{5,7},{6,4},{7,5},{8,10},{9,11},{10,... | collective-permute-start | bytes 1548296 | tf_op jit(solution)/shard_map/ppermute | solution.py:455
  478.3 44.2 %copy-start.49 = (bf16[512,768]{1,0:T(8,128)(2,1)S(1)}, bf16[512,768]{1,0:T(8,128)(2,1)}, u32[]{:S(2)}) copy-start(bf16[512,768]{1,0:T(8,128)(2,1)} %copy-done.48) | copy-start | bytes 2359300
  480.1 44.1 %copy-start.27 = (bf16[512,384]{1,0:T(8,128)(2,1)}, bf16[512,384]{1,0:T(8,128)(2,1)S(1)}, u32[]{:S(2)}) copy-start(bf16[512,384]{1,0:T(8,128)(2,1)S(1)} %slice.180.refs_0_) | copy-start | bytes 1179652
  609.2 64.6 %collective-permute-start.6 = (bf16[6144,512]{1,0:T(8,128)(2,1)}, bf16[6144,512]{1,0:T(8,128)(2,1)}, u32[]{:S(2)}, u32[]{:S(2)}) collective-permute-start(bf16[6144,512]{1,0:T(8,128)(2,1)} %get-tuple-element.158), channel_id=1, source_target_pairs={{0,4},{4,0},{1,5},{5,1},{2,6},{6,2},{3,7},{7,3},{8,12},{12,8},{9,1... | collective-permute-start | bytes 18874376 | tf_op jit(solution)/shard_map/ppermute | solution.py:441
  612.9 60.9 %collective-permute-start.7 = (bf16[1024,1536]{1,0:T(8,128)(2,1)S(1)}, bf16[1024,1536]{1,0:T(8,128)(2,1)S(1)}, u32[]{:S(2)}, u32[]{:S(2)}) collective-permute-start(bf16[1024,1536]{1,0:T(8,128)(2,1)S(1)} %fusion.11.refs_2_.refs_3_), channel_id=1, source_target_pairs={{0,4},{4,0},{1,5},{5,1},{2,6},{6,2},{3,7},{7,3},{8,12},{12,8},{9,1... | collective-permute-start | bytes 9437192 | tf_op jit(solution)/shard_map/ppermute | solution.py:441
  660.1 36.2 %copy-start.29 = (bf16[512,384]{1,0:T(8,128)(2,1)}, bf16[512,384]{1,0:T(8,128)(2,1)S(1)}, u32[]{:S(2)}) copy-start(bf16[512,384]{1,0:T(8,128)(2,1)S(1)} %get-tuple-element.154) | copy-start | bytes 1179652
  661.6 34.0 %collective-permute-start.10 = (bf16[288,896]{1,0:T(8,128)(2,1)S(1)}, bf16[288,896]{1,0:T(8,128)(2,1)S(1)}, u32[]{:S(2)}, u32[]{:S(2)}) collective-permute-start(bf16[288,896]{1,0:T(8,128)(2,1)S(1)} %slice_select_fusion), channel_id=1, source_target_pairs={{0,2},{1,3},{2,0},{3,1},{4,6},{5,7},{6,4},{7,5},{8,10},{9,11},{10,... | collective-permute-start | bytes 1548296 | tf_op jit(solution)/shard_map/ppermute | solution.py:455
  664.4 31.3 %collective-permute-start.9 = (bf16[512,896]{1,0:T(8,128)(2,1)S(1)}, bf16[512,896]{1,0:T(8,128)(2,1)S(1)}, u32[]{:S(2)}, u32[]{:S(2)}) collective-permute-start(bf16[512,896]{1,0:T(8,128)(2,1)S(1)} %get-tuple-element.358), channel_id=1, source_target_pairs={{0,1},{1,2},{2,3},{4,5},{5,6},{6,7},{8,9},{9,10},{10,11},{12,13},{... | collective-permute-start | bytes 2752520 | tf_op jit(solution)/shard_map/ppermute | solution.py:447
  665.7 30.0 %collective-permute-start.8 = (bf16[512,896]{1,0:T(8,128)(2,1)S(1)}, bf16[512,896]{1,0:T(8,128)(2,1)S(1)}, u32[]{:S(2)}, u32[]{:S(2)}) collective-permute-start(bf16[512,896]{1,0:T(8,128)(2,1)S(1)} %get-tuple-element.359), channel_id=1, source_target_pairs={{1,0},{2,1},{3,2},{5,4},{6,5},{7,6},{9,8},{10,9},{11,10},{13,12},{... | collective-permute-start | bytes 2752520 | tf_op jit(solution)/shard_map/ppermute | solution.py:447
  673.8 31.1 %collective-permute-start.12 = (bf16[1024,1536]{1,0:T(8,128)(2,1)}, bf16[1024,1536]{1,0:T(8,128)(2,1)}, u32[]{:S(2)}, u32[]{:S(2)}) collective-permute-start(bf16[1024,1536]{1,0:T(8,128)(2,1)} %fusion.12.refs_2_.refs_3_), channel_id=1, source_target_pairs={{0,4},{4,0},{1,5},{5,1},{2,6},{6,2},{3,7},{7,3},{8,12},{12,8},{9,1... | collective-permute-start | bytes 9437192 | tf_op jit(solution)/shard_map/ppermute | solution.py:441
  698.2 7.0 collective-permute-start.11
  760.2 57.6 %collective-permute-start.13 = (bf16[6144,512]{1,0:T(8,128)(2,1)}, bf16[6144,512]{1,0:T(8,128)(2,1)}, u32[]{:S(2)}, u32[]{:S(2)}) collective-permute-start(bf16[6144,512]{1,0:T(8,128)(2,1)} %get-tuple-element.175), channel_id=1, source_target_pairs={{0,4},{4,0},{1,5},{5,1},{2,6},{6,2},{3,7},{7,3},{8,12},{12,8},{9,1... | collective-permute-start | bytes 18874376 | tf_op jit(solution)/shard_map/ppermute | solution.py:441
  762.2 55.5 %collective-permute-start.14 = (bf16[1024,1536]{1,0:T(8,128)(2,1)}, bf16[1024,1536]{1,0:T(8,128)(2,1)}, u32[]{:S(2)}, u32[]{:S(2)}) collective-permute-start(bf16[1024,1536]{1,0:T(8,128)(2,1)} %fusion.13.refs_2_.refs_3_), channel_id=1, source_target_pairs={{0,4},{4,0},{1,5},{5,1},{2,6},{6,2},{3,7},{7,3},{8,12},{12,8},{9,1... | collective-permute-start | bytes 9437192 | tf_op jit(solution)/shard_map/ppermute | solution.py:441
  808.0 37.5 %collective-permute-start.17 = (bf16[288,768]{1,0:T(8,128)(2,1)}, bf16[288,768]{1,0:T(8,128)(2,1)}, u32[]{:S(2)}, u32[]{:S(2)}) collective-permute-start(bf16[288,768]{1,0:T(8,128)(2,1)} %slice_select_fusion.2), channel_id=1, source_target_pairs={{0,2},{1,3},{2,0},{3,1},{4,6},{5,7},{6,4},{7,5},{8,10},{9,11},{10,... | collective-permute-start | bytes 1327112 | tf_op jit(solution)/shard_map/ppermute | solution.py:455
  810.6 46.8 %collective-permute-start.16 = (bf16[512,768]{1,0:T(8,128)(2,1)}, bf16[512,768]{1,0:T(8,128)(2,1)}, u32[]{:S(2)}, u32[]{:S(2)}) collective-permute-start(bf16[512,768]{1,0:T(8,128)(2,1)} %get-tuple-element.361), channel_id=1, source_target_pairs={{0,1},{1,2},{2,3},{4,5},{5,6},{6,7},{8,9},{9,10},{10,11},{12,13},{... | collective-permute-start | bytes 2359304 | tf_op jit(solution)/shard_map/ppermute | solution.py:447
  811.9 45.5 %collective-permute-start.15 = (bf16[512,768]{1,0:T(8,128)(2,1)S(1)}, bf16[512,768]{1,0:T(8,128)(2,1)}, u32[]{:S(2)}, u32[]{:S(2)}) collective-permute-start(bf16[512,768]{1,0:T(8,128)(2,1)S(1)} %get-tuple-element.362), channel_id=1, source_target_pairs={{1,0},{2,1},{3,2},{5,4},{6,5},{7,6},{9,8},{10,9},{11,10},{13,12},{... | collective-permute-start | bytes 2359304 | tf_op jit(solution)/shard_map/ppermute | solution.py:447
  817.7 44.0 %collective-permute-start.19 = (bf16[1024,1536]{1,0:T(8,128)(2,1)S(1)}, bf16[1024,1536]{1,0:T(8,128)(2,1)S(1)}, u32[]{:S(2)}, u32[]{:S(2)}) collective-permute-start(bf16[1024,1536]{1,0:T(8,128)(2,1)S(1)} %fusion.14.refs_2_.refs_3_), channel_id=1, source_target_pairs={{0,4},{4,0},{1,5},{5,1},{2,6},{6,2},{3,7},{7,3},{8,12},{12,8},{9,1... | collective-permute-start | bytes 9437192 | tf_op jit(solution)/shard_map/ppermute | solution.py:441
  860.5 3.5 collective-permute-start.18
  880.5 72.2 %collective-permute-start.20 = (bf16[3072,384]{1,0:T(8,128)(2,1)}, bf16[3072,384]{1,0:T(8,128)(2,1)}, u32[]{:S(2)}, u32[]{:S(2)}) collective-permute-start(bf16[3072,384]{1,0:T(8,128)(2,1)} %get-tuple-element.203), channel_id=1, source_target_pairs={{0,16},{16,0},{1,17},{17,1},{2,18},{18,2},{3,19},{19,3},{4,20},{20... | collective-permute-start | bytes 7077896 | tf_op jit(solution)/shard_map/ppermute | solution.py:441
  881.0 71.7 %collective-permute-start.21 = (bf16[3072,384]{1,0:T(8,128)(2,1)}, bf16[3072,384]{1,0:T(8,128)(2,1)}, u32[]{:S(2)}, u32[]{:S(2)}) collective-permute-start(bf16[3072,384]{1,0:T(8,128)(2,1)} %get-tuple-element.205), channel_id=1, source_target_pairs={{0,8},{8,0},{1,9},{9,1},{2,10},{10,2},{3,11},{11,3},{4,12},{12,4},... | collective-permute-start | bytes 7077896 | tf_op jit(solution)/shard_map/ppermute | solution.py:441
  891.6 1.3 collective-permute-start.22
  961.2 30.9 %collective-permute-start.23 = (bf16[1536,384]{1,0:T(8,128)(2,1)}, bf16[1536,384]{1,0:T(8,128)(2,1)}, u32[]{:S(2)}, u32[]{:S(2)}) collective-permute-start(bf16[1536,384]{1,0:T(8,128)(2,1)} %get-tuple-element.214), channel_id=1, source_target_pairs={{0,8},{8,0},{1,9},{9,1},{2,10},{10,2},{3,11},{11,3},{4,12},{12,4},... | collective-permute-start | bytes 3538952 | tf_op jit(solution)/shard_map/ppermute | solution.py:441
  962.0 37.8 %collective-permute-start.24 = (bf16[1536,384]{1,0:T(8,128)(2,1)}, bf16[1536,384]{1,0:T(8,128)(2,1)}, u32[]{:S(2)}, u32[]{:S(2)}) collective-permute-start(bf16[1536,384]{1,0:T(8,128)(2,1)} %get-tuple-element.216), channel_id=1, source_target_pairs={{0,16},{16,0},{1,17},{17,1},{2,18},{18,2},{3,19},{19,3},{4,20},{20... | collective-permute-start | bytes 3538952 | tf_op jit(solution)/shard_map/ppermute | solution.py:441
  963.4 103.2 %collective-permute-start.32 = (bf16[3072,384]{1,0:T(8,128)(2,1)S(1)}, bf16[3072,384]{1,0:T(8,128)(2,1)}, u32[]{:S(2)}, u32[]{:S(2)}) collective-permute-start(bf16[3072,384]{1,0:T(8,128)(2,1)S(1)} %copy-done.24), channel_id=1, source_target_pairs={{0,16},{16,0},{1,17},{17,1},{2,18},{18,2},{3,19},{19,3},{4,20},{20... | collective-permute-start | bytes 7077896 | tf_op jit(solution)/shard_map/ppermute | solution.py:441
  964.0 102.5 %collective-permute-start.33 = (bf16[3072,384]{1,0:T(8,128)(2,1)}, bf16[3072,384]{1,0:T(8,128)(2,1)}, u32[]{:S(2)}, u32[]{:S(2)}) collective-permute-start(bf16[3072,384]{1,0:T(8,128)(2,1)} %get-tuple-element.239), channel_id=1, source_target_pairs={{0,8},{8,0},{1,9},{9,1},{2,10},{10,2},{3,11},{11,3},{4,12},{12,4},... | collective-permute-start | bytes 7077896 | tf_op jit(solution)/shard_map/ppermute | solution.py:441
  965.2 7.5 collective-permute-start.25
  1002.8 63.8 %copy-start.12 = (bf16[3072,384]{1,0:T(8,128)(2,1)S(1)}, bf16[3072,384]{1,0:T(8,128)(2,1)}, u32[]{:S(2)}) copy-start(bf16[3072,384]{1,0:T(8,128)(2,1)} %copy-done.11) | copy-start | bytes 7077892
  1005.7 5.1 collective-permute-start.34
  1073.1 26.7 %collective-permute-start.35 = (bf16[1536,384]{1,0:T(8,128)(2,1)S(1)}, bf16[1536,384]{1,0:T(8,128)(2,1)S(1)}, u32[]{:S(2)}, u32[]{:S(2)}) collective-permute-start(bf16[1536,384]{1,0:T(8,128)(2,1)S(1)} %get-tuple-element.247), channel_id=1, source_target_pairs={{0,8},{8,0},{1,9},{9,1},{2,10},{10,2},{3,11},{11,3},{4,12},{12,4},... | collective-permute-start | bytes 3538952 | tf_op jit(solution)/shard_map/ppermute | solution.py:441
  1073.8 26.3 %collective-permute-start.36 = (bf16[1536,384]{1,0:T(8,128)(2,1)S(1)}, bf16[1536,384]{1,0:T(8,128)(2,1)S(1)}, u32[]{:S(2)}, u32[]{:S(2)}) collective-permute-start(bf16[1536,384]{1,0:T(8,128)(2,1)S(1)} %get-tuple-element.249), channel_id=1, source_target_pairs={{0,16},{16,0},{1,17},{17,1},{2,18},{18,2},{3,19},{19,3},{4,20},{20... | collective-permute-start | bytes 3538952 | tf_op jit(solution)/shard_map/ppermute | solution.py:441
  1075.2 38.6 %collective-permute-start.26 = (bf16[384,384]{1,0:T(8,128)(2,1)}, bf16[384,384]{1,0:T(8,128)(2,1)S(1)}, u32[]{:S(2)}, u32[]{:S(2)}) collective-permute-start(bf16[384,384]{1,0:T(8,128)(2,1)} %get-tuple-element.229), channel_id=1, source_target_pairs={{0,1},{1,2},{2,3},{3,0},{4,5},{5,6},{6,7},{7,4},{8,9},{9,10},{10,1... | collective-permute-start | bytes 884744 | tf_op jit(solution)/shard_map/ppermute | solution.py:441
  1076.8 37.0 %collective-permute-start.27 = (bf16[384,384]{1,0:T(8,128)(2,1)}, bf16[384,384]{1,0:T(8,128)(2,1)}, u32[]{:S(2)}, u32[]{:S(2)}) collective-permute-start(bf16[384,384]{1,0:T(8,128)(2,1)} %get-tuple-element.230), channel_id=1, source_target_pairs={{0,2},{1,3},{2,0},{3,1},{4,6},{5,7},{6,4},{7,5},{8,10},{9,11},{10,... | collective-permute-start | bytes 884744 | tf_op jit(solution)/shard_map/ppermute | solution.py:441
  1102.8 4.2 collective-permute-start.37
  1107.8 6.6 collective-permute-start.38
  1110.0 14.6 %collective-permute-start.28 = (bf16[384,384]{1,0:T(8,128)(2,1)}, bf16[384,384]{1,0:T(8,128)(2,1)}, u32[]{:S(2)}, u32[]{:S(2)}) collective-permute-start(bf16[384,384]{1,0:T(8,128)(2,1)} %get-tuple-element.231), channel_id=1, source_target_pairs={{0,3},{1,0},{2,1},{3,2},{4,7},{5,4},{6,5},{7,6},{8,11},{9,8},{10,9... | collective-permute-start | bytes 884744 | tf_op jit(solution)/shard_map/ppermute | solution.py:441
  1110.5 24.0 %collective-permute-start.29 = (bf16[384,384]{1,0:T(8,128)(2,1)}, bf16[384,384]{1,0:T(8,128)(2,1)}, u32[]{:S(2)}, u32[]{:S(2)}) collective-permute-start(bf16[384,384]{1,0:T(8,128)(2,1)} %get-tuple-element.233), channel_id=1, source_target_pairs={{0,1},{1,2},{2,3},{3,0},{4,5},{5,6},{6,7},{7,4},{8,9},{9,10},{10,1... | collective-permute-start | bytes 884744 | tf_op jit(solution)/shard_map/ppermute | solution.py:441
  1113.8 36.9 %collective-permute-start.30 = (bf16[384,384]{1,0:T(8,128)(2,1)}, bf16[384,384]{1,0:T(8,128)(2,1)}, u32[]{:S(2)}, u32[]{:S(2)}) collective-permute-start(bf16[384,384]{1,0:T(8,128)(2,1)} %get-tuple-element.234), channel_id=1, source_target_pairs={{0,2},{1,3},{2,0},{3,1},{4,6},{5,7},{6,4},{7,5},{8,10},{9,11},{10,... | collective-permute-start | bytes 884744 | tf_op jit(solution)/shard_map/ppermute | solution.py:441
  1113.9 40.5 %collective-permute-start.31 = (bf16[384,384]{1,0:T(8,128)(2,1)}, bf16[384,384]{1,0:T(8,128)(2,1)}, u32[]{:S(2)}, u32[]{:S(2)}) collective-permute-start(bf16[384,384]{1,0:T(8,128)(2,1)} %get-tuple-element.235), channel_id=1, source_target_pairs={{0,3},{1,0},{2,1},{3,2},{4,7},{5,4},{6,5},{7,6},{8,11},{9,8},{10,9... | collective-permute-start | bytes 884744 | tf_op jit(solution)/shard_map/ppermute | solution.py:441
  1114.5 53.0 %collective-permute-start.39 = (bf16[384,384]{1,0:T(8,128)(2,1)}, bf16[384,384]{1,0:T(8,128)(2,1)}, u32[]{:S(2)}, u32[]{:S(2)}) collective-permute-start(bf16[384,384]{1,0:T(8,128)(2,1)} %get-tuple-element.266), channel_id=1, source_target_pairs={{0,1},{1,2},{2,3},{3,0},{4,5},{5,6},{6,7},{7,4},{8,9},{9,10},{10,1... | collective-permute-start | bytes 884744 | tf_op jit(solution)/shard_map/ppermute | solution.py:441
  1122.2 46.4 %copy-start.61 = (bf16[384,384]{1,0:T(8,128)(2,1)S(1)}, bf16[384,384]{1,0:T(8,128)(2,1)}, u32[]{:S(2)}) copy-start(bf16[384,384]{1,0:T(8,128)(2,1)} %get-tuple-element.257) | copy-start | bytes 884740
  1124.6 67.5 %copy-start.62 = (bf16[384,384]{1,0:T(8,128)(2,1)S(1)}, bf16[384,384]{1,0:T(8,128)(2,1)}, u32[]{:S(2)}) copy-start(bf16[384,384]{1,0:T(8,128)(2,1)} %get-tuple-element.274) | copy-start | bytes 884740
  1124.6 68.6 %copy-start.63 = (bf16[384,384]{1,0:T(8,128)(2,1)S(1)}, bf16[384,384]{1,0:T(8,128)(2,1)}, u32[]{:S(2)}) copy-start(bf16[384,384]{1,0:T(8,128)(2,1)} %get-tuple-element.278) | copy-start | bytes 884740
  1124.6 68.5 %copy-start.66 = (f32[6,1472]{1,0:T(8,128)}, f32[6,1472]{1,0:T(8,128)S(1)}, u32[]{:S(2)}) copy-start(f32[6,1472]{1,0:T(8,128)S(1)} %add.432) | copy-start | bytes 105988
  1124.6 56.0 %collective-permute-start.40 = (bf16[384,384]{1,0:T(8,128)(2,1)}, bf16[384,384]{1,0:T(8,128)(2,1)S(1)}, u32[]{:S(2)}, u32[]{:S(2)}) collective-permute-start(bf16[384,384]{1,0:T(8,128)(2,1)} %get-tuple-element.267), channel_id=1, source_target_pairs={{0,2},{1,3},{2,0},{3,1},{4,6},{5,7},{6,4},{7,5},{8,10},{9,11},{10,... | collective-permute-start | bytes 884744 | tf_op jit(solution)/shard_map/ppermute | solution.py:441
  1134.5 46.1 %collective-permute-start.41 = (bf16[384,384]{1,0:T(8,128)(2,1)}, bf16[384,384]{1,0:T(8,128)(2,1)S(1)}, u32[]{:S(2)}, u32[]{:S(2)}) collective-permute-start(bf16[384,384]{1,0:T(8,128)(2,1)} %get-tuple-element.268), channel_id=1, source_target_pairs={{0,3},{1,0},{2,1},{3,2},{4,7},{5,4},{6,5},{7,6},{8,11},{9,8},{10,9... | collective-permute-start | bytes 884744 | tf_op jit(solution)/shard_map/ppermute | solution.py:441
  1150.7 29.8 %collective-permute-start.42 = (bf16[384,384]{1,0:T(8,128)(2,1)}, bf16[384,384]{1,0:T(8,128)(2,1)S(1)}, u32[]{:S(2)}, u32[]{:S(2)}) collective-permute-start(bf16[384,384]{1,0:T(8,128)(2,1)} %get-tuple-element.270), channel_id=1, source_target_pairs={{0,1},{1,2},{2,3},{3,0},{4,5},{5,6},{6,7},{7,4},{8,9},{9,10},{10,1... | collective-permute-start | bytes 884744 | tf_op jit(solution)/shard_map/ppermute | solution.py:441
  1154.3 36.2 %collective-permute-start.43 = (bf16[384,384]{1,0:T(8,128)(2,1)}, bf16[384,384]{1,0:T(8,128)(2,1)S(1)}, u32[]{:S(2)}, u32[]{:S(2)}) collective-permute-start(bf16[384,384]{1,0:T(8,128)(2,1)} %get-tuple-element.271), channel_id=1, source_target_pairs={{0,2},{1,3},{2,0},{3,1},{4,6},{5,7},{6,4},{7,5},{8,10},{9,11},{10,... | collective-permute-start | bytes 884744 | tf_op jit(solution)/shard_map/ppermute | solution.py:441
  1167.5 23.1 %collective-permute-start.44 = (bf16[384,384]{1,0:T(8,128)(2,1)}, bf16[384,384]{1,0:T(8,128)(2,1)S(1)}, u32[]{:S(2)}, u32[]{:S(2)}) collective-permute-start(bf16[384,384]{1,0:T(8,128)(2,1)} %get-tuple-element.272), channel_id=1, source_target_pairs={{0,3},{1,0},{2,1},{3,2},{4,7},{5,4},{6,5},{7,6},{8,11},{9,8},{10,9... | collective-permute-start | bytes 884744 | tf_op jit(solution)/shard_map/ppermute | solution.py:441
  (82 other events, 682.1 us)
Sparse Core Ops, SparseCore 0:
  11.4 213.9 all-gather.2
  228.8 234.3 all-gather.4
  716.0 352.9 reduce-scatter.1

commit v7 on v6

--- a/solution.py
+++ b/solution.py
@@ -978,6 +978,12 @@
             total = total.reshape((lax.axis_size(route[0]), -1) + total.shape[-1:])
             sends = stage_sends(total, route[0], 0)
             moves[name] = (route, pick(total, lax.axis_index(route[0]), 0), sends)
+        if moves and all(move[0] == ("z",) for move in moves.values()):
+            kept = jnp.concatenate([move[1] for move in moves.values()], axis=-1)
+            sends = [
+                jnp.concatenate(parts, axis=-1) for parts in zip(*(m[2] for m in moves.values()))
+            ]
+            moves = {tuple(moves): (("z",), kept, sends)}
         arrays, values = tied({name: move[1:] for name, move in moves.items()}, values)
         for name, (route, *_) in moves.items():
             kept, sends = arrays[name]
@@ -996,17 +1002,49 @@
     return lax.all_gather(local_rows, DEVICES, axis=0, tiled=True)
 
 
-def layer_forward(stream, gathered, gain_one, gain_two, gate_low, context):
+def from_first(value, axis):
+    result = value
+    here = lax.axis_index(axis)
+    for k in range(1, lax.axis_size(axis)):
+        result = jnp.where(here == k, lax.ppermute(value, axis, [(0, k)]), result)
+    return result
+
+
+def placed(own, axis, order):
+    here, count = lax.axis_index(axis), lax.axis_size(axis)
+    whole_axis = jnp.zeros(own.shape[:order] + (count,) + own.shape[order:], own.dtype)
+    whole_axis = lax.dynamic_update_index_in_dim(whole_axis, own, here, order)
+    for k in range(1, count):
+        moved = shift(own, axis, k)
+        whole_axis = lax.dynamic_update_index_in_dim(whole_axis, moved, (here - k) % count, order)
+    return whole_axis
+
+
+def attention_weights(local_rows):
+    block, width = local_rows.shape
+    owners = 4 * INNER // (block * lax.axis_size("z"))
+    if owners == 1:
+        halves = local_rows.reshape(2, block // 2, width)
+        own = jnp.where(
+            lax.axis_index("c") == 0, halves[0], lax.ppermute(halves[1], "c", [(0, 1)])
+        )
+    else:
+        own = local_rows
+    own = from_first(from_first(own, "x"), "y")
+    return placed(placed(own, "z", 0), "c", 1 if owners == 1 else 0).reshape(4 * INNER, width)
+
+
+def layer_forward(stream, gathered, attention, gain_one, gain_two, gate_low, context):
     normed, inverse_one = rms_forward(stream, gain_one)
     normed_low = normed.astype(jnp.bfloat16)
-    projected = times_rows(normed_low, gathered[: 3 * INNER]).astype(jnp.bfloat16)
+    projected = times_rows(normed_low, attention[: 3 * INNER]).astype(jnp.bfloat16)
     queries = projected[:, :INNER]
     parts = [projected[:, INNER:]]
     if gate_low is not None:
         parts.append(jnp.broadcast_to(gate_low[:, None], (stream.shape[0], BLOCK)))
     shared = with_neighbours(jnp.concatenate(parts, axis=1))
     attended, log_total = attend_forward(queries, shared, context)
-    middle = stream + times_plain(attended, gathered[3 * INNER : 4 * INNER])
+    middle = stream + times_plain(attended, attention[3 * INNER :])
     normed_two, inverse_two = rms_forward(middle, gain_two)
     normed_two_low = normed_two.astype(jnp.bfloat16)
     result, up_gelu, up_linear = ffn_forward(normed_two_low, middle, gathered)
@@ -1097,8 +1135,16 @@
     context = attention_context(segment_ids[0], first_pos, tokens_here, rel_bias)
     stream = inputs.reshape(tokens_here, width)
     gathered_three = fetch_rows(layer3_rows)
+    attention_four = attention_weights(layer4_rows)
+    stream, attention_four = tied(stream, attention_four)
     after_three, kept_three = layer_forward(
-        stream, gathered_three, norm_gains[0], norm_gains[1], None, context
+        stream,
+        gathered_three,
+        gathered_three[: 4 * INNER],
+        norm_gains[0],
+        norm_gains[1],
+        None,
+        context,
     )
     gate_inverse = lax.rsqrt(jnp.mean(after_three * after_three, axis=1, keepdims=True) + epsilon)
     gate_normed = after_three * gate_inverse
@@ -1108,7 +1154,13 @@
     gate_low = gate_mask.astype(jnp.bfloat16)
     gathered_four = fetch_rows(layer4_rows)
     after_four, kept_four = layer_forward(
-        after_three, gathered_four, norm_gains[2], norm_gains[3], gate_low, context
+        after_three,
+        gathered_four,
+        attention_four,
+        norm_gains[2],
+        norm_gains[3],
+        gate_low,
+        context,
     )
     grad_three_out, table_four, grad_gate, gain_four_one, gain_four_two, local_four = (
         layer_backward(
@@ -1145,15 +1197,15 @@
     for bit in range(2, lax.axis_size("z")):
         if bit & (bit - 1) == 0:
             small = hop(small, "z", bit)
+    small = scatter.step(small, (0, 1))
     small = scatter.step(small, 2, 3)
     small = scatter.step(small, 2, 3)
     small = hop(small, "x")
     for bit in range(1, lax.axis_size("y")):
         if bit & (bit - 1) == 0:
             small = hop(small, "y", bit)
-    summed = scatter.step(small, 0, 1)
-    summed = scatter.step(summed, 2, 3)
-    local_three = jnp.concatenate([scatter.results[chunk] for chunk in range(4)], axis=1)
+    summed = scatter.step(small, (2, 3))
+    local_three = jnp.concatenate([scatter.results[pair] for pair in ((0, 1), (2, 3))], axis=1)
     local_three, local_four = local_three[:, :width], local_four[:, :width].astype(jnp.float32)
     return (
         after_four.reshape(inputs.shape),

time: 1210 us -> 1220 us (level)
  starting transfers between devices: 87.1 us -> 152 us
  Pallas kernels: 309 us -> 262 us
  waiting for transfers between devices: 626 us -> 595 us
  local copies, waits for them, and re-layouts: 63 us -> 81.4 us
    all_gather x2, waiting for transfers between devices: 323 us -> 94.6 us  [fetch_rows(): return lax.all_gather(local_rows, DEVICES, axis=0, tiled=True)]
    ppermute x28 -> x26, waiting for transfers between devices: 202 us -> 299 us  [shift(): lax.ppermute(value, axis, [(i, (i + amount) % count) for i in range(count)])]
    ppermute x4, waiting for transfers between devices: 65.2 us -> 134 us  [far_pair(): got = lax.ppermute(sent, 'z', pairs)]
    ppermute x0 -> x3, waiting for transfers between devices: none -> 35.3 us  [the longest x2 33.7 us: from_first(): result = jnp.where(here == k, lax.ppermute(value, axis, [(0, k)]), result)]
    ppermute x4, starting transfers between devices: 1.91 us -> 28.3 us  [far_pair(): got = lax.ppermute(sent, 'z', pairs)]
    pallas_call x2, Pallas kernels: 74 us -> 48.4 us  [attend_backward(): pl.pallas_call(functools.partial(backward_body, width > 2 * INNER), grid_...]
    ppermute x8, starting transfers between devices: 25.6 us -> 49.8 us  [slide(): return lax.ppermute(value, 'z', pairs)]
    pallas_call x2, Pallas kernels: 47 us -> 27.3 us  [attend_forward(): pl.pallas_call(functools.partial(forward_body, width > 2 * INNER), grid_s...]
  transfers between devices with their start and end apart: 48 -> 49, of which waited for: 23 -> 27; matrix products, arithmetic and copies ran while one was open for 11% -> 13% of each run, Pallas kernels for 18% -> 16%
where the time goes in v7:
time: 1220 us; the launch traced here: 1210 us
  waiting for transfers between devices  595 us (49%)
  Pallas kernels  262 us (21%)
  starting transfers between devices  152 us (12%)
  local copies, waits for them, and re-layouts  81.4 us (7%)
  other arithmetic  71.8 us (6%)
  matrix products  32.1 us (3%)
  between operations  15.6 us (1%)
    ppermute x26, waiting for transfers between devices, shift(): lax.ppermute(value, axis, [(i, (i + amount) % count) for i in range(count)])  299 us
    ppermute x4, waiting for transfers between devices, far_pair(): got = lax.ppermute(sent, 'z', pairs)  134 us
    all_gather x2, waiting for transfers between devices, fetch_rows(): return lax.all_gather(local_rows, DEVICES, axis=0, tiled=True)  94.6 us
    pallas_call x2, Pallas kernels, ffn_backward(): pl.pallas_call(ffn_backward_body, grid_spec=pltpu.PrefetchScalarGridSpec(...  65.5 us
    ppermute x26, starting transfers between devices, shift(): lax.ppermute(value, axis, [(i, (i + amount) % count) for i in range(count)])  52.8 us
    ppermute x8, starting transfers between devices, slide(): return lax.ppermute(value, 'z', pairs)  49.8 us
    pallas_call x2, Pallas kernels, ffn_forward(): pl.pallas_call(ffn_forward_body, grid=(steps,), in_specs=[resident((token...  48.8 us
    pallas_call x2, Pallas kernels, attend_backward(): pl.pallas_call(functools.partial(backward_body, width > 2 * INNER), grid_...  48.4 us
  transfers between devices with their start and end apart: 49, of which 27 were waited for; matrix products, arithmetic and copies ran while one was open for 13% of the time, Pallas kernels for 16%

profile of v7, /device:TPU:24, one launch (start us, length us, event | category | flops | bytes accessed | tf_op | source)
XLA Modules:
  0.0 1209.4 jit_solution(8572439756621034214)
XLA Ops:
  17.5 3.4 collective-permute-start.1
  21.0 21.5 %collective-permute-done.1 = bf16[192,1472]{1,0:T(8,128)(2,1)S(1)} collective-permute-done((bf16[192,1472]{1,0:T(8,128)(2,1)S(1)}, bf16[192,1472]{1,0:T(8,128)(2,1)S(1)}, u32[]{:S(2)}, u32[]{:S(2)}) %collective-permute-start.1) | collective-permute-done | bytes 565280 | tf_op jit(solution)/shard_map/ppermute | solution.py:1009
  42.5 3.5 collective-permute-start.2
  46.0 12.2 %collective-permute-done.2 = bf16[192,1472]{1,0:T(8,128)(2,1)S(1)} collective-permute-done((bf16[192,1472]{1,0:T(8,128)(2,1)S(1)}, bf16[192,1472]{1,0:T(8,128)(2,1)S(1)}, u32[]{:S(2)}, u32[]{:S(2)}) %collective-permute-start.2) | collective-permute-done | bytes 565280 | tf_op jit(solution)/shard_map/ppermute | solution.py:1009
  63.2 36.5 %collective-permute-done.3 = bf16[192,1472]{1,0:T(8,128)(2,1)S(1)} collective-permute-done((bf16[192,1472]{1,0:T(8,128)(2,1)S(1)}, bf16[192,1472]{1,0:T(8,128)(2,1)S(1)}, u32[]{:S(2)}, u32[]{:S(2)}) %collective-permute-start.3) | collective-permute-done | bytes 565280 | tf_op jit(solution)/shard_map/ppermute | solution.py:441
  100.5 60.9 %collective-permute-done.4 = bf16[192,1472]{1,0:T(8,128)(2,1)S(1)} collective-permute-done((bf16[192,1472]{1,0:T(8,128)(2,1)S(1)}, bf16[192,1472]{1,0:T(8,128)(2,1)S(1)}, u32[]{:S(2)}, u32[]{:S(2)}) %collective-permute-start.4) | collective-permute-done | bytes 565280 | tf_op jit(solution)/shard_map/ppermute | solution.py:441
  166.3 3.5 broadcast_in_dim.28
  169.8 4.3 bitcast_dynamic-update-slice_fusion
  174.1 3.8 bitcast_dynamic-update-slice_fusion.1
  180.9 94.6 %all-gather.3.cloned.1.call-done.gelu_ref.linear_ref.down_ref.refs_4_.refs_5_.refs_6_ = bf16[12288,1472]{1,0:T(8,128)(2,1)} async-done(((bf16[384,1472]{1,0:T(8,128)(2,1)}), bf16[12288,1472]{1,0:T(8,128)(2,1)}) %all-gather.3.cloned.1.call-update) | async-done | bytes 36175888 | tf_op jit(solution)/shard_map/all_gather | solution.py:1002
  275.5 4.7 fusion.23
  284.5 6.0 collective-permute-start.9
  291.3 4.7 bias_tiles.1.refs_4_.refs_5_
  296.0 3.6 copy.137
  300.7 22.5 %collective-permute-done.7 = bf16[288,768]{1,0:T(8,128)(2,1)} collective-permute-done((bf16[288,768]{1,0:T(8,128)(2,1)}, bf16[288,768]{1,0:T(8,128)(2,1)}, u32[]{:S(2)}, u32[]{:S(2)}) %collective-permute-start.7) | collective-permute-done | bytes 442400 | tf_op jit(solution)/shard_map/ppermute | solution.py:455
  324.4 14.3 %collective-permute-done.8 = bf16[512,768]{1,0:T(8,128)(2,1)} collective-permute-done((bf16[512,768]{1,0:T(8,128)(2,1)}, bf16[512,768]{1,0:T(8,128)(2,1)}, u32[]{:S(2)}, u32[]{:S(2)}) %collective-permute-start.8) | collective-permute-done | bytes 786464 | tf_op jit(solution)/shard_map/ppermute | solution.py:447
  341.6 13.6 %attend_forward.2 = (bf16[512,384]{1,0:T(8,128)(2,1)S(1)}, f32[4,8,256]{2,1,0:T(8,128)S(1)}) custom-call(s32[4]{0:T(128)S(1)} %get-tuple-element.387.low_ref, s32[4]{0:T(128)S(1)} %get-tuple-element.386.high_ref, bf16[512,384]{1,0:T(8,128)(2,1)S(1)} %slice.195.refs_0_, bf16[2304,768]{1,0:T(8,128)(2,1)S(1)} %pad_dynamic-update-slice_fusion.2.refs_1_.refs_2_, ...), custom_call_target="tpu_custom_call" | custom-call | flops 1811939328 | bytes 8388608 | tf_op jit(solution)/shard_map/attend_forward/pallas_call | solution.py:197
  355.2 2.5 multiply_reduce_fusion.12
  359.4 24.8 %ffn_forward.2 = (f32[512,1472]{1,0:T(8,128)S(1)}, f32[512,3584]{1,0:T(8,128)}, f32[512,3584]{1,0:T(8,128)}) custom-call(bf16[512,1472]{1,0:T(8,128)(2,1)S(1)} %multiply_convert_fusion.2.normed_ref.refs_1_, f32[512,1472]{1,0:T(8,128)} %copy-done.39, bf16[12288,1472]{1,0:T(8,128)(2,1)} %all-gather.3.cloned.1.call-done.gelu_ref.linear_ref.down_ref.refs_4_.refs_5_.refs_6_, ...), custom_call_target="tpu_custom_call" | custom-call | flops 16206790656 | bytes 46333952 | tf_op jit(solution)/shard_map/ffn_forward/pallas_call | solution.py:582
  386.9 4.2 fusion.26
  392.6 23.0 %collective-permute-start.12 = (bf16[512,896]{1,0:T(8,128)(2,1)S(1)}, bf16[512,896]{1,0:T(8,128)(2,1)S(1)}, u32[]{:S(2)}, u32[]{:S(2)}) collective-permute-start(bf16[512,896]{1,0:T(8,128)(2,1)S(1)} %pad_maximum_fusion.1), channel_id=1, source_target_pairs={{1,0},{2,1},{3,2},{5,4},{6,5},{7,6},{9,8},{10,9},{11,10},{13,12},{... | collective-permute-start | bytes 2752520 | tf_op jit(solution)/shard_map/ppermute | solution.py:447
  417.0 9.3 collective-permute-start.10
  428.3 110.7 %collective-permute-done.10 = bf16[288,896]{1,0:T(8,128)(2,1)S(1)} collective-permute-done((bf16[288,896]{1,0:T(8,128)(2,1)S(1)}, bf16[288,896]{1,0:T(8,128)(2,1)S(1)}, u32[]{:S(2)}, u32[]{:S(2)}) %collective-permute-start.10) | collective-permute-done | bytes 516128 | tf_op jit(solution)/shard_map/ppermute | solution.py:455
  539.7 13.8 %attend_forward.3 = (bf16[512,384]{1,0:T(8,128)(2,1)S(1)}, f32[4,8,256]{2,1,0:T(8,128)S(1)}) custom-call(s32[4]{0:T(128)S(1)} %get-tuple-element.387.low_ref, s32[4]{0:T(128)S(1)} %get-tuple-element.386.high_ref, bf16[512,384]{1,0:T(8,128)(2,1)S(1)} %slice.200.refs_0_, bf16[2304,896]{1,0:T(8,128)(2,1)S(1)} %pad_dynamic-update-slice_fusion.refs_1_.refs_2_, ...), custom_call_target="tpu_custom_call" | custom-call | flops 1811939328 | bytes 8388608 | tf_op jit(solution)/shard_map/attend_forward/pallas_call | solution.py:197
  560.5 24.0 %ffn_forward.3 = (f32[512,1472]{1,0:T(8,128)S(1)}, f32[512,3584]{1,0:T(8,128)}, f32[512,3584]{1,0:T(8,128)}) custom-call(bf16[512,1472]{1,0:T(8,128)(2,1)S(1)} %copy-done.2, f32[512,1472]{1,0:T(8,128)} %copy-done.41, bf16[12288,1472]{1,0:T(8,128)(2,1)} %all-gather.5.cloned.1.call-done.gelu_ref.linear_ref.down_ref.refs_4_.refs_5_.refs_6_, ...), custom_call_target="tpu_custom_call" | custom-call | flops 16206790656 | bytes 46333952 | tf_op jit(solution)/shard_map/ffn_forward/pallas_call | solution.py:582
  586.2 32.2 %ffn_backward.2 = (f32[512,1472]{1,0:T(8,128)}, bf16[6144,512]{1,0:T(8,128)(2,1)}, bf16[6144,512]{1,0:T(8,128)(2,1)}) custom-call(s32[2]{0:T(128)} %pad_add_fusion.core_ref, bf16[512,1472]{1,0:T(8,128)(2,1)} %bitcast_convert_fusion.refs_0_, bf16[512,1472]{1,0:T(8,128)(2,1)} %multiply_convert_fusion.normed_ref.refs_1_, ...), custom_call_target="tpu_custom_call" | custom-call | flops 16206790656 | bytes 57344000 | tf_op jit(solution)/shard_map/ffn_backward/pallas_call | solution.py:685
  618.4 10.7 collective-permute-start.13
  636.4 2.5 fusion.41
  638.9 2.9 convolution_convert_fusion.1.refs_1_
  641.8 25.2 %attend_backward.2 = (bf16[512,384]{1,0:T(8,128)(2,1)S(1)}, bf16[2304,896]{1,0:T(8,128)(2,1)}, f32[3,32,256]{2,1,0:T(8,128)S(1)}) custom-call(s32[4]{0:T(128)S(1)} %get-tuple-element.387.low_ref, s32[4]{0:T(128)S(1)} %get-tuple-element.386.high_ref, bf16[512,384]{1,0:T(8,128)(2,1)S(1)} %copy-done.27, bf16[512,384]{1,0:T(8,128)(2,1)S(1)} %convolution_convert_fusion.1.refs_1_, ...), custom_call_target="tpu_custom_call" | custom-call | flops 4529848320 | bytes 12582912 | tf_op jit(solution)/shard_map/attend_backward/pallas_call | solution.py:347
  668.6 7.0 collective-permute-start.17
  678.8 10.2 collective-permute-start.15
  689.0 3.5 fusion.16.refs_2_.refs_3_
  692.5 5.2 collective-permute-start.19
  697.7 21.8 %weight_grads.2.refs_6_ = bf16[6144,1536]{1,0:T(8,128)(2,1)} custom-call(s32[6]{0:T(128)S(1)} %stack.55.place_ref, bf16[6144,512]{1,0:T(8,128)(2,1)S(1)} %bitcast.103, bf16[6144,512]{1,0:T(8,128)(2,1)} %collective-permute-done.13.refs_1_, bf16[1024,1536]{1,0:T(8,128)(2,1)S(1)} %fusion.15.refs_2_.refs_3_, bf16[1024,1536]{1,0:T(8,128)(2,1)S(1)} %fusion.15.refs_2_.refs_3_, ...), custom_call_target="tpu_custom_call" | custom-call | flops 18522046464 | bytes 31457280 | tf_op jit(solution)/shard_map/weight_grads/pallas_call | solution.py:833
  722.1 3.1 collective-permute-start.18
  728.6 10.6 attention_fill.2
  741.9 5.6 multiply_reduce_fusion.2
  747.6 2.5 fusion.39
  750.1 33.3 %ffn_backward.3 = (f32[512,1472]{1,0:T(8,128)}, bf16[6144,512]{1,0:T(8,128)(2,1)}, bf16[6144,512]{1,0:T(8,128)(2,1)}) custom-call(s32[2]{0:T(128)} %pad_add_fusion.core_ref, bf16[512,1472]{1,0:T(8,128)(2,1)} %get-tuple-element.324.refs_0_, bf16[512,1472]{1,0:T(8,128)(2,1)} %copy-done, f32[512,3584]{1,0:T(8,128)} %get-tuple-element.155.refs_2_, ...), custom_call_target="tpu_custom_call" | custom-call | flops 16206790656 | bytes 57344000 | tf_op jit(solution)/shard_map/ffn_backward/pallas_call | solution.py:685
  788.3 2.5 fusion.38
  793.3 23.2 %attend_backward.3 = (bf16[512,384]{1,0:T(8,128)(2,1)S(1)}, bf16[2304,768]{1,0:T(8,128)(2,1)}, f32[3,32,256]{2,1,0:T(8,128)S(1)}) custom-call(s32[4]{0:T(128)S(1)} %get-tuple-element.387.low_ref, s32[4]{0:T(128)S(1)} %get-tuple-element.386.high_ref, bf16[512,384]{1,0:T(8,128)(2,1)S(1)} %copy-done.30, bf16[512,384]{1,0:T(8,128)(2,1)S(1)} %convolution_convert_fusion.refs_1_, ...), custom_call_target="tpu_custom_call" | custom-call | flops 4529848320 | bytes 12582912 | tf_op jit(solution)/shard_map/attend_backward/pallas_call | solution.py:347
  818.6 11.5 collective-permute-start.24
  830.1 2.7 fusion.43
  834.0 5.5 collective-permute-start.22
  839.8 2.9 collective-permute-start.26
  842.8 24.5 %weight_grads.3 = (bf16[3072,384]{1,0:T(8,128)(2,1)}, bf16[3072,384]{1,0:T(8,128)(2,1)S(1)}, bf16[3072,384]{1,0:T(8,128)(2,1)S(1)}, bf16[3072,384]{1,0:T(8,128)(...) custom-call(s32[6]{0:T(128)S(1)} %stack.55.place_ref, ...), custom_call_target="tpu_custom_call" | custom-call | flops 18522046464 | bytes 31457280 | tf_op jit(solution)/shard_map/weight_grads/pallas_call | solution.py:833
  868.1 6.3 collective-permute-done.23
  882.0 10.7 attention_fill.3
  899.8 2.9 collective-permute-start.27
  904.7 7.3 multiply_reduce_fusion.4
  914.0 57.3 %collective-permute-done.27 = bf16[3072,384]{1,0:T(8,128)(2,1)} collective-permute-done((bf16[3072,384]{1,0:T(8,128)(2,1)}, bf16[3072,384]{1,0:T(8,128)(2,1)}, u32[]{:S(2)}, u32[]{:S(2)}) %collective-permute-start.27) | collective-permute-done | bytes 2359328 | tf_op jit(solution)/shard_map/ppermute | solution.py:441
  981.9 4.3 collective-permute-start.32
  988.2 3.3 collective-permute-done.32
  992.3 19.0 %collective-permute-done.30 = bf16[1536,384]{1,0:T(8,128)(2,1)} collective-permute-done((bf16[1536,384]{1,0:T(8,128)(2,1)}, bf16[1536,384]{1,0:T(8,128)(2,1)}, u32[]{:S(2)}, u32[]{:S(2)}) %collective-permute-start.30) | collective-permute-done | bytes 1179680 | tf_op jit(solution)/shard_map/ppermute | solution.py:441
  1011.3 8.0 collective-permute-done.31
  1024.2 4.5 collective-permute-start.36
  1030.6 5.0 collective-permute-done.36
  1037.2 7.2 collective-permute-done.33
  1044.4 55.3 %collective-permute-done.34 = bf16[384,768]{1,0:T(8,128)(2,1)S(1)} collective-permute-done((bf16[384,768]{1,0:T(8,128)(2,1)S(1)}, bf16[384,768]{1,0:T(8,128)(2,1)S(1)}, u32[]{:S(2)}, u32[]{:S(2)}) %collective-permute-start.34) | collective-permute-done | bytes 589856 | tf_op jit(solution)/shard_map/ppermute | solution.py:441
  1110.5 12.7 %collective-permute-done.39 = bf16[1536,384]{1,0:T(8,128)(2,1)} collective-permute-done((bf16[1536,384]{1,0:T(8,128)(2,1)}, bf16[1536,384]{1,0:T(8,128)(2,1)}, u32[]{:S(2)}, u32[]{:S(2)}) %collective-permute-start.39) | collective-permute-done | bytes 1179680 | tf_op jit(solution)/shard_map/ppermute | solution.py:441
  1132.2 11.0 collective-permute-start.42
  1146.0 2.6 copy.147
  1153.8 39.3 %collective-permute-done.42 = bf16[384,768]{1,0:T(8,128)(2,1)} collective-permute-done((bf16[384,768]{1,0:T(8,128)(2,1)}, bf16[384,768]{1,0:T(8,128)(2,1)}, u32[]{:S(2)}, u32[]{:S(2)}) %collective-permute-start.42) | collective-permute-done | bytes 589856 | tf_op jit(solution)/shard_map/ppermute | solution.py:441
  (401 shorter events, 162.3 us)
Async XLA Ops:
  7.2 268.4 %all-gather.3.cloned.1.call-start = ((), (), s32[]{:S(2)}) async-start(), calls=%async_computation.1 | async-start | bytes 38928384 | tf_op jit(solution)/shard_map/all_gather | solution.py:1002
  9.7 549.4 %all-gather.5.cloned.1.call-start = ((), (), s32[]{:S(2)}) async-start(), calls=%async_computation.2 | async-start | bytes 38928384 | tf_op jit(solution)/shard_map/all_gather | solution.py:1002
  11.9 1187.2 %reduce-scatter.2.cloned.1.call-start = ((), (), s32[]{:S(2)}) async-start(), calls=%async_computation.3 | async-start | bytes 20054016 | tf_op jit(solution)/shard_map/reduce_scatter | solution.py:1124
  13.0 3.4 collective-permute-start
  17.5 24.9 %collective-permute-start.1 = (bf16[192,1472]{1,0:T(8,128)(2,1)S(1)}, bf16[192,1472]{1,0:T(8,128)(2,1)S(1)}, u32[]{:S(2)}, u32[]{:S(2)}) collective-permute-start(bf16[192,1472]{1,0:T(8,128)(2,1)S(1)} %slice_select_fusion), channel_id=1, source_target_pairs={{0,8},{1,9},{2,10},{3,11},{4,12},{5,13},{6,14},{7,15},{16,24},{17,... | collective-permute-start | bytes 1695752 | tf_op jit(solution)/shard_map/ppermute | solution.py:1009
  42.5 15.7 %collective-permute-start.2 = (bf16[192,1472]{1,0:T(8,128)(2,1)S(1)}, bf16[192,1472]{1,0:T(8,128)(2,1)S(1)}, u32[]{:S(2)}, u32[]{:S(2)}) collective-permute-start(bf16[192,1472]{1,0:T(8,128)(2,1)S(1)} %broadcast_select_fusion), channel_id=1, source_target_pairs={{0,16},{1,17},{2,18},{3,19},{4,20},{5,21},{6,22},{7,23},{8,24},{9,... | collective-permute-start | bytes 1695752 | tf_op jit(solution)/shard_map/ppermute | solution.py:1009
  59.8 103.3 %copy-start.90 = (s32[1,2048]{1,0:T(1,128)S(1)}, s32[1,2048]{1,0:T(1,128)}, u32[]{:S(2)}) copy-start(s32[1,2048]{1,0:T(1,128)} %param.14) | copy-start | bytes 24580
  60.8 38.8 %collective-permute-start.3 = (bf16[192,1472]{1,0:T(8,128)(2,1)S(1)}, bf16[192,1472]{1,0:T(8,128)(2,1)S(1)}, u32[]{:S(2)}, u32[]{:S(2)}) collective-permute-start(bf16[192,1472]{1,0:T(8,128)(2,1)S(1)} %get-tuple-element.331), channel_id=1, source_target_pairs={{0,1},{1,2},{2,3},{3,0},{4,5},{5,6},{6,7},{7,4},{8,9},{9,10},{10,1... | collective-permute-start | bytes 1695752 | tf_op jit(solution)/shard_map/ppermute | solution.py:441
  61.0 100.4 %collective-permute-start.4 = (bf16[192,1472]{1,0:T(8,128)(2,1)S(1)}, bf16[192,1472]{1,0:T(8,128)(2,1)S(1)}, u32[]{:S(2)}, u32[]{:S(2)}) collective-permute-start(bf16[192,1472]{1,0:T(8,128)(2,1)S(1)} %get-tuple-element.331), channel_id=1, source_target_pairs={{0,2},{1,3},{2,0},{3,1},{4,6},{5,7},{6,4},{7,5},{8,10},{9,11},{10,... | collective-permute-start | bytes 1695752 | tf_op jit(solution)/shard_map/ppermute | solution.py:441
  62.7 99.5 %collective-permute-start.5 = (bf16[192,1472]{1,0:T(8,128)(2,1)S(1)}, bf16[192,1472]{1,0:T(8,128)(2,1)S(1)}, u32[]{:S(2)}, u32[]{:S(2)}) collective-permute-start(bf16[192,1472]{1,0:T(8,128)(2,1)S(1)} %get-tuple-element.331), channel_id=1, source_target_pairs={{0,3},{1,0},{2,1},{3,2},{4,7},{5,4},{6,5},{7,6},{8,11},{9,8},{10,9... | collective-permute-start | bytes 1695752 | tf_op jit(solution)/shard_map/ppermute | solution.py:441
  163.1 11.0 collective-permute-start.6
  165.6 189.6 %copy-start.37 = (f32[1,512,1472]{2,1,0:T(8,128)}, f32[1,512,1472]{2,1,0:T(8,128)S(1)}, u32[]{:S(2)}) copy-start(f32[1,512,1472]{2,1,0:T(8,128)S(1)} %copy.128) | copy-start | bytes 9043972
  166.3 192.1 %copy-start.67 = (f32[1472]{0:T(1024)}, f32[1472]{0:T(1024)S(1)}, u32[]{:S(2)}) copy-start(f32[1472]{0:T(1024)S(1)} %get-tuple-element.315) | copy-start | bytes 17668
  166.3 218.8 %copy-start.71 = (f32[1472]{0:T(1024)}, f32[1472]{0:T(1024)S(1)}, u32[]{:S(2)}) copy-start(f32[1472]{0:T(1024)S(1)} %get-tuple-element.317) | copy-start | bytes 17668
  180.9 109.7 %copy-start.94 = (f32[32,6]{0,1:T(8,128)S(1)}, f32[32,6]{0,1:T(8,128)}, u32[]{:S(2)}) copy-start(f32[32,6]{0,1:T(8,128)} %param.13) | copy-start | bytes 2308
  282.1 41.1 %collective-permute-start.7 = (bf16[288,768]{1,0:T(8,128)(2,1)}, bf16[288,768]{1,0:T(8,128)(2,1)}, u32[]{:S(2)}, u32[]{:S(2)}) collective-permute-start(bf16[288,768]{1,0:T(8,128)(2,1)} %slice_select_fusion.2), channel_id=1, source_target_pairs={{0,2},{1,3},{2,0},{3,1},{4,6},{5,7},{6,4},{7,5},{8,10},{9,11},{10,... | collective-permute-start | bytes 1327112 | tf_op jit(solution)/shard_map/ppermute | solution.py:455
  282.7 55.9 %collective-permute-start.8 = (bf16[512,768]{1,0:T(8,128)(2,1)}, bf16[512,768]{1,0:T(8,128)(2,1)}, u32[]{:S(2)}, u32[]{:S(2)}) collective-permute-start(bf16[512,768]{1,0:T(8,128)(2,1)} %slice.198), channel_id=1, source_target_pairs={{0,1},{1,2},{2,3},{4,5},{5,6},{6,7},{8,9},{9,10},{10,11},{12,13},{... | collective-permute-start | bytes 2359304 | tf_op jit(solution)/shard_map/ppermute | solution.py:447
  284.5 55.4 %collective-permute-start.9 = (bf16[512,768]{1,0:T(8,128)(2,1)}, bf16[512,768]{1,0:T(8,128)(2,1)}, u32[]{:S(2)}, u32[]{:S(2)}) collective-permute-start(bf16[512,768]{1,0:T(8,128)(2,1)} %slice.198), channel_id=1, source_target_pairs={{1,0},{2,1},{3,2},{5,4},{6,5},{7,6},{9,8},{10,9},{11,10},{13,12},{... | collective-permute-start | bytes 2359304 | tf_op jit(solution)/shard_map/ppermute | solution.py:447
  299.6 40.3 %copy-start.54 = (bf16[512,1152]{1,0:T(8,128)(2,1)S(1)}, bf16[512,1152]{1,0:T(8,128)(2,1)}, u32[]{:S(2)}) copy-start(bf16[512,1152]{1,0:T(8,128)(2,1)} %copy-done.53) | copy-start | bytes 3538948
  300.7 40.8 %copy-start.29 = (bf16[512,384]{1,0:T(8,128)(2,1)}, bf16[512,384]{1,0:T(8,128)(2,1)S(1)}, u32[]{:S(2)}) copy-start(bf16[512,384]{1,0:T(8,128)(2,1)S(1)} %slice.195.refs_0_) | copy-start | bytes 1179652
  341.5 198.1 %copy-start.6 = (s32[2304,128]{1,0:T(8,128)}, s32[2304,128]{1,0:T(8,128)S(1)}, u32[]{:S(2)}) copy-start(s32[2304,128]{1,0:T(8,128)S(1)} %broadcast_in_dim.62.refs_3_.refs_4_) | copy-start | bytes 3538948
  391.1 35.2 %copy-start.44 = (f32[1,512,1472]{2,1,0:T(8,128)S(1)}, f32[1,512,1472]{2,1,0:T(8,128)}, u32[]{:S(2)}) copy-start(f32[1,512,1472]{2,1,0:T(8,128)} %copy.137) | copy-start | bytes 9043972
  392.6 146.9 %collective-permute-start.12 = (bf16[512,896]{1,0:T(8,128)(2,1)S(1)}, bf16[512,896]{1,0:T(8,128)(2,1)S(1)}, u32[]{:S(2)}, u32[]{:S(2)}) collective-permute-start(bf16[512,896]{1,0:T(8,128)(2,1)S(1)} %pad_maximum_fusion.1), channel_id=1, source_target_pairs={{1,0},{2,1},{3,2},{5,4},{6,5},{7,6},{9,8},{10,9},{11,10},{13,12},{... | collective-permute-start | bytes 2752520 | tf_op jit(solution)/shard_map/ppermute | solution.py:447
  415.5 123.6 %collective-permute-start.11 = (bf16[512,896]{1,0:T(8,128)(2,1)S(1)}, bf16[512,896]{1,0:T(8,128)(2,1)S(1)}, u32[]{:S(2)}, u32[]{:S(2)}) collective-permute-start(bf16[512,896]{1,0:T(8,128)(2,1)S(1)} %pad_maximum_fusion.1), channel_id=1, source_target_pairs={{0,1},{1,2},{2,3},{4,5},{5,6},{6,7},{8,9},{9,10},{10,11},{12,13},{... | collective-permute-start | bytes 2752520 | tf_op jit(solution)/shard_map/ppermute | solution.py:447
  417.0 122.0 %collective-permute-start.10 = (bf16[288,896]{1,0:T(8,128)(2,1)S(1)}, bf16[288,896]{1,0:T(8,128)(2,1)S(1)}, u32[]{:S(2)}, u32[]{:S(2)}) collective-permute-start(bf16[288,896]{1,0:T(8,128)(2,1)S(1)} %fusion.34), channel_id=1, source_target_pairs={{0,2},{1,3},{2,0},{3,1},{4,6},{5,7},{6,4},{7,5},{8,10},{9,11},{10,... | collective-permute-start | bytes 1548296 | tf_op jit(solution)/shard_map/ppermute | solution.py:455
  428.3 111.4 %copy-start.26 = (bf16[512,384]{1,0:T(8,128)(2,1)}, bf16[512,384]{1,0:T(8,128)(2,1)S(1)}, u32[]{:S(2)}) copy-start(bf16[512,384]{1,0:T(8,128)(2,1)S(1)} %slice.200.refs_0_) | copy-start | bytes 1179652
  618.4 79.3 %collective-permute-start.13 = (bf16[6144,512]{1,0:T(8,128)(2,1)}, bf16[6144,512]{1,0:T(8,128)(2,1)}, u32[]{:S(2)}, u32[]{:S(2)}) collective-permute-start(bf16[6144,512]{1,0:T(8,128)(2,1)} %get-tuple-element.146), channel_id=1, source_target_pairs={{0,4},{4,0},{1,5},{5,1},{2,6},{6,2},{3,7},{7,3},{8,12},{12,8},{9,1... | collective-permute-start | bytes 18874376 | tf_op jit(solution)/shard_map/ppermute | solution.py:441
  632.6 59.8 %collective-permute-start.14 = (bf16[1024,1536]{1,0:T(8,128)(2,1)S(1)}, bf16[1024,1536]{1,0:T(8,128)(2,1)S(1)}, u32[]{:S(2)}, u32[]{:S(2)}) collective-permute-start(bf16[1024,1536]{1,0:T(8,128)(2,1)S(1)} %fusion.15.refs_2_.refs_3_), channel_id=1, source_target_pairs={{0,4},{4,0},{1,5},{5,1},{2,6},{6,2},{3,7},{7,3},{8,12},{12,8},{9,1... | collective-permute-start | bytes 9437192 | tf_op jit(solution)/shard_map/ppermute | solution.py:441
  667.1 53.2 %copy-start.28 = (bf16[512,384]{1,0:T(8,128)(2,1)}, bf16[512,384]{1,0:T(8,128)(2,1)S(1)}, u32[]{:S(2)}) copy-start(bf16[512,384]{1,0:T(8,128)(2,1)S(1)} %get-tuple-element.142) | copy-start | bytes 1179652
  668.6 51.0 %collective-permute-start.17 = (bf16[288,896]{1,0:T(8,128)(2,1)S(1)}, bf16[288,896]{1,0:T(8,128)(2,1)S(1)}, u32[]{:S(2)}, u32[]{:S(2)}) collective-permute-start(bf16[288,896]{1,0:T(8,128)(2,1)S(1)} %slice_select_fusion.1), channel_id=1, source_target_pairs={{0,2},{1,3},{2,0},{3,1},{4,6},{5,7},{6,4},{7,5},{8,10},{9,11},{10,... | collective-permute-start | bytes 1548296 | tf_op jit(solution)/shard_map/ppermute | solution.py:455
  677.5 42.1 %collective-permute-start.16 = (bf16[512,896]{1,0:T(8,128)(2,1)S(1)}, bf16[512,896]{1,0:T(8,128)(2,1)S(1)}, u32[]{:S(2)}, u32[]{:S(2)}) collective-permute-start(bf16[512,896]{1,0:T(8,128)(2,1)S(1)} %get-tuple-element.332), channel_id=1, source_target_pairs={{0,1},{1,2},{2,3},{4,5},{5,6},{6,7},{8,9},{9,10},{10,11},{12,13},{... | collective-permute-start | bytes 2752520 | tf_op jit(solution)/shard_map/ppermute | solution.py:447
  678.8 40.8 %collective-permute-start.15 = (bf16[512,896]{1,0:T(8,128)(2,1)S(1)}, bf16[512,896]{1,0:T(8,128)(2,1)S(1)}, u32[]{:S(2)}, u32[]{:S(2)}) collective-permute-start(bf16[512,896]{1,0:T(8,128)(2,1)S(1)} %get-tuple-element.333), channel_id=1, source_target_pairs={{1,0},{2,1},{3,2},{5,4},{6,5},{7,6},{9,8},{10,9},{11,10},{13,12},{... | collective-permute-start | bytes 2752520 | tf_op jit(solution)/shard_map/ppermute | solution.py:447
  692.5 35.9 %collective-permute-start.19 = (bf16[1024,1536]{1,0:T(8,128)(2,1)}, bf16[1024,1536]{1,0:T(8,128)(2,1)}, u32[]{:S(2)}, u32[]{:S(2)}) collective-permute-start(bf16[1024,1536]{1,0:T(8,128)(2,1)} %fusion.16.refs_2_.refs_3_), channel_id=1, source_target_pairs={{0,4},{4,0},{1,5},{5,1},{2,6},{6,2},{3,7},{7,3},{8,12},{12,8},{9,1... | collective-permute-start | bytes 9437192 | tf_op jit(solution)/shard_map/ppermute | solution.py:441
  722.1 6.5 collective-permute-start.18
  750.1 35.9 %copy-start.68 = (f32[1472]{0:T(1024)S(1)}, f32[1472]{0:T(1024)}, u32[]{:S(2)}) copy-start(f32[1472]{0:T(1024)} %copy-done.67) | copy-start | bytes 17668
  783.4 59.3 %collective-permute-start.20 = (bf16[6144,512]{1,0:T(8,128)(2,1)}, bf16[6144,512]{1,0:T(8,128)(2,1)}, u32[]{:S(2)}, u32[]{:S(2)}) collective-permute-start(bf16[6144,512]{1,0:T(8,128)(2,1)} %get-tuple-element.163), channel_id=1, source_target_pairs={{0,4},{4,0},{1,5},{5,1},{2,6},{6,2},{3,7},{7,3},{8,12},{12,8},{9,1... | collective-permute-start | bytes 18874376 | tf_op jit(solution)/shard_map/ppermute | solution.py:441
  785.5 54.4 %collective-permute-start.21 = (bf16[1024,1536]{1,0:T(8,128)(2,1)}, bf16[1024,1536]{1,0:T(8,128)(2,1)}, u32[]{:S(2)}, u32[]{:S(2)}) collective-permute-start(bf16[1024,1536]{1,0:T(8,128)(2,1)} %fusion.17.refs_2_.refs_3_), channel_id=1, source_target_pairs={{0,4},{4,0},{1,5},{5,1},{2,6},{6,2},{3,7},{7,3},{8,12},{12,8},{9,1... | collective-permute-start | bytes 9437192 | tf_op jit(solution)/shard_map/ppermute | solution.py:441
  818.6 49.6 %collective-permute-start.24 = (bf16[288,768]{1,0:T(8,128)(2,1)}, bf16[288,768]{1,0:T(8,128)(2,1)}, u32[]{:S(2)}, u32[]{:S(2)}) collective-permute-start(bf16[288,768]{1,0:T(8,128)(2,1)} %slice_select_fusion.3), channel_id=1, source_target_pairs={{0,2},{1,3},{2,0},{3,1},{4,6},{5,7},{6,4},{7,5},{8,10},{9,11},{10,... | collective-permute-start | bytes 1327112 | tf_op jit(solution)/shard_map/ppermute | solution.py:455
  832.7 41.7 %collective-permute-start.23 = (bf16[512,768]{1,0:T(8,128)(2,1)}, bf16[512,768]{1,0:T(8,128)(2,1)}, u32[]{:S(2)}, u32[]{:S(2)}) collective-permute-start(bf16[512,768]{1,0:T(8,128)(2,1)} %get-tuple-element.335), channel_id=1, source_target_pairs={{0,1},{1,2},{2,3},{4,5},{5,6},{6,7},{8,9},{9,10},{10,11},{12,13},{... | collective-permute-start | bytes 2359304 | tf_op jit(solution)/shard_map/ppermute | solution.py:447
  834.0 40.9 %collective-permute-start.22 = (bf16[512,768]{1,0:T(8,128)(2,1)S(1)}, bf16[512,768]{1,0:T(8,128)(2,1)}, u32[]{:S(2)}, u32[]{:S(2)}) collective-permute-start(bf16[512,768]{1,0:T(8,128)(2,1)S(1)} %get-tuple-element.336), channel_id=1, source_target_pairs={{1,0},{2,1},{3,2},{5,4},{6,5},{7,6},{9,8},{10,9},{11,10},{13,12},{... | collective-permute-start | bytes 2359304 | tf_op jit(solution)/shard_map/ppermute | solution.py:447
  839.8 40.2 %collective-permute-start.26 = (bf16[1024,1536]{1,0:T(8,128)(2,1)S(1)}, bf16[1024,1536]{1,0:T(8,128)(2,1)S(1)}, u32[]{:S(2)}, u32[]{:S(2)}) collective-permute-start(bf16[1024,1536]{1,0:T(8,128)(2,1)S(1)} %fusion.18.refs_2_.refs_3_), channel_id=1, source_target_pairs={{0,4},{4,0},{1,5},{5,1},{2,6},{6,2},{3,7},{7,3},{8,12},{12,8},{9,1... | collective-permute-start | bytes 9437192 | tf_op jit(solution)/shard_map/ppermute | solution.py:441
  877.9 4.1 collective-permute-start.25
  899.8 71.5 %collective-permute-start.27 = (bf16[3072,384]{1,0:T(8,128)(2,1)}, bf16[3072,384]{1,0:T(8,128)(2,1)}, u32[]{:S(2)}, u32[]{:S(2)}) collective-permute-start(bf16[3072,384]{1,0:T(8,128)(2,1)} %get-tuple-element.191), channel_id=1, source_target_pairs={{0,16},{16,0},{1,17},{17,1},{2,18},{18,2},{3,19},{19,3},{4,20},{20... | collective-permute-start | bytes 7077896 | tf_op jit(solution)/shard_map/ppermute | solution.py:441
  902.7 68.6 %collective-permute-start.28 = (bf16[3072,384]{1,0:T(8,128)(2,1)}, bf16[3072,384]{1,0:T(8,128)(2,1)}, u32[]{:S(2)}, u32[]{:S(2)}) collective-permute-start(bf16[3072,384]{1,0:T(8,128)(2,1)} %get-tuple-element.193), channel_id=1, source_target_pairs={{0,8},{8,0},{1,9},{9,1},{2,10},{10,2},{3,11},{11,3},{4,12},{12,4},... | collective-permute-start | bytes 7077896 | tf_op jit(solution)/shard_map/ppermute | solution.py:441
  912.1 1.3 collective-permute-start.29
  979.9 31.4 %collective-permute-start.30 = (bf16[1536,384]{1,0:T(8,128)(2,1)}, bf16[1536,384]{1,0:T(8,128)(2,1)}, u32[]{:S(2)}, u32[]{:S(2)}) collective-permute-start(bf16[1536,384]{1,0:T(8,128)(2,1)} %get-tuple-element.202), channel_id=1, source_target_pairs={{0,8},{8,0},{1,9},{9,1},{2,10},{10,2},{3,11},{11,3},{4,12},{12,4},... | collective-permute-start | bytes 3538952 | tf_op jit(solution)/shard_map/ppermute | solution.py:441
  981.8 37.5 %collective-permute-start.31 = (bf16[1536,384]{1,0:T(8,128)(2,1)}, bf16[1536,384]{1,0:T(8,128)(2,1)}, u32[]{:S(2)}, u32[]{:S(2)}) collective-permute-start(bf16[1536,384]{1,0:T(8,128)(2,1)} %get-tuple-element.204), channel_id=1, source_target_pairs={{0,16},{16,0},{1,17},{17,1},{2,18},{18,2},{3,19},{19,3},{4,20},{20... | collective-permute-start | bytes 3538952 | tf_op jit(solution)/shard_map/ppermute | solution.py:441
  981.9 9.6 collective-permute-start.32
  986.2 113.5 %collective-permute-start.37 = (bf16[3072,384]{1,0:T(8,128)(2,1)S(1)}, bf16[3072,384]{1,0:T(8,128)(2,1)S(1)}, u32[]{:S(2)}, u32[]{:S(2)}) collective-permute-start(bf16[3072,384]{1,0:T(8,128)(2,1)S(1)} %copy-done.22), channel_id=1, source_target_pairs={{0,16},{16,0},{1,17},{17,1},{2,18},{18,2},{3,19},{19,3},{4,20},{20... | collective-permute-start | bytes 7077896 | tf_op jit(solution)/shard_map/ppermute | solution.py:441
  987.6 113.1 %collective-permute-start.38 = (bf16[3072,384]{1,0:T(8,128)(2,1)}, bf16[3072,384]{1,0:T(8,128)(2,1)S(1)}, u32[]{:S(2)}, u32[]{:S(2)}) collective-permute-start(bf16[3072,384]{1,0:T(8,128)(2,1)} %copy-done.23), channel_id=1, source_target_pairs={{0,8},{8,0},{1,9},{9,1},{2,10},{10,2},{3,11},{11,3},{4,12},{12,4},... | collective-permute-start | bytes 7077896 | tf_op jit(solution)/shard_map/ppermute | solution.py:441
  1022.9 77.8 %copy-start.10 = (bf16[3072,384]{1,0:T(8,128)(2,1)S(1)}, bf16[3072,384]{1,0:T(8,128)(2,1)}, u32[]{:S(2)}) copy-start(bf16[3072,384]{1,0:T(8,128)(2,1)} %copy-done.9) | copy-start | bytes 7077892
  1024.2 11.4 collective-permute-start.36
  1028.6 15.8 %collective-permute-start.33 = (bf16[384,768]{1,0:T(8,128)(2,1)S(1)}, bf16[384,768]{1,0:T(8,128)(2,1)S(1)}, u32[]{:S(2)}, u32[]{:S(2)}) collective-permute-start(bf16[384,768]{1,0:T(8,128)(2,1)S(1)} %pad_maximum_fusion.7), channel_id=1, source_target_pairs={{0,1},{1,2},{2,3},{3,0},{4,5},{5,6},{6,7},{7,4},{8,9},{9,10},{10,1... | collective-permute-start | bytes 1769480 | tf_op jit(solution)/shard_map/ppermute | solution.py:441
  1030.6 69.1 %collective-permute-start.34 = (bf16[384,768]{1,0:T(8,128)(2,1)S(1)}, bf16[384,768]{1,0:T(8,128)(2,1)S(1)}, u32[]{:S(2)}, u32[]{:S(2)}) collective-permute-start(bf16[384,768]{1,0:T(8,128)(2,1)S(1)} %pad_maximum_fusion.8), channel_id=1, source_target_pairs={{0,2},{1,3},{2,0},{3,1},{4,6},{5,7},{6,4},{7,5},{8,10},{9,11},{10,... | collective-permute-start | bytes 1769480 | tf_op jit(solution)/shard_map/ppermute | solution.py:441
  1035.6 64.1 %collective-permute-start.35 = (bf16[384,768]{1,0:T(8,128)(2,1)S(1)}, bf16[384,768]{1,0:T(8,128)(2,1)S(1)}, u32[]{:S(2)}, u32[]{:S(2)}) collective-permute-start(bf16[384,768]{1,0:T(8,128)(2,1)S(1)} %pad_maximum_fusion.9), channel_id=1, source_target_pairs={{0,3},{1,0},{2,1},{3,2},{4,7},{5,4},{6,5},{7,6},{8,11},{9,8},{10,9... | collective-permute-start | bytes 1769480 | tf_op jit(solution)/shard_map/ppermute | solution.py:441
  1044.4 55.3 %copy-start.64 = (bf16[384,768]{1,0:T(8,128)(2,1)}, bf16[384,768]{1,0:T(8,128)(2,1)S(1)}, u32[]{:S(2)}) copy-start(bf16[384,768]{1,0:T(8,128)(2,1)S(1)} %collective-permute-done.33) | copy-start | bytes 1769476
  1106.1 17.0 %collective-permute-start.39 = (bf16[1536,384]{1,0:T(8,128)(2,1)}, bf16[1536,384]{1,0:T(8,128)(2,1)}, u32[]{:S(2)}, u32[]{:S(2)}) collective-permute-start(bf16[1536,384]{1,0:T(8,128)(2,1)} %get-tuple-element.236), channel_id=1, source_target_pairs={{0,8},{8,0},{1,9},{9,1},{2,10},{10,2},{3,11},{11,3},{4,12},{12,4},... | collective-permute-start | bytes 3538952 | tf_op jit(solution)/shard_map/ppermute | solution.py:441
  1106.8 16.5 %collective-permute-start.40 = (bf16[1536,384]{1,0:T(8,128)(2,1)}, bf16[1536,384]{1,0:T(8,128)(2,1)}, u32[]{:S(2)}, u32[]{:S(2)}) collective-permute-start(bf16[1536,384]{1,0:T(8,128)(2,1)} %get-tuple-element.238), channel_id=1, source_target_pairs={{0,16},{16,0},{1,17},{17,1},{2,18},{18,2},{3,19},{19,3},{4,20},{20... | collective-permute-start | bytes 3538952 | tf_op jit(solution)/shard_map/ppermute | solution.py:441
  1130.8 17.8 %collective-permute-start.44 = (f32[6,1472]{1,0:T(8,128)S(1)}, f32[6,1472]{1,0:T(8,128)S(1)}, u32[]{:S(2)}, u32[]{:S(2)}) collective-permute-start(f32[6,1472]{1,0:T(8,128)S(1)} %add.451), channel_id=1, source_target_pairs={{0,8},{8,0},{1,9},{9,1},{2,10},{10,2},{3,11},{11,3},{4,12},{12,4},... | collective-permute-start | bytes 105992 | tf_op jit(solution)/shard_map/ppermute | solution.py:530
  1132.2 21.6 %collective-permute-start.41 = (bf16[384,768]{1,0:T(8,128)(2,1)}, bf16[384,768]{1,0:T(8,128)(2,1)}, u32[]{:S(2)}, u32[]{:S(2)}) collective-permute-start(bf16[384,768]{1,0:T(8,128)(2,1)} %pad_maximum_fusion.11), channel_id=1, source_target_pairs={{0,1},{1,2},{2,3},{3,0},{4,5},{5,6},{6,7},{7,4},{8,9},{9,10},{10,1... | collective-permute-start | bytes 1769480 | tf_op jit(solution)/shard_map/ppermute | solution.py:441
  1132.2 60.9 %collective-permute-start.42 = (bf16[384,768]{1,0:T(8,128)(2,1)}, bf16[384,768]{1,0:T(8,128)(2,1)}, u32[]{:S(2)}, u32[]{:S(2)}) collective-permute-start(bf16[384,768]{1,0:T(8,128)(2,1)} %pad_maximum_fusion.12), channel_id=1, source_target_pairs={{0,2},{1,3},{2,0},{3,1},{4,6},{5,7},{6,4},{7,5},{8,10},{9,11},{10,... | collective-permute-start | bytes 1769480 | tf_op jit(solution)/shard_map/ppermute | solution.py:441
  1143.2 49.9 %collective-permute-start.43 = (bf16[384,768]{1,0:T(8,128)(2,1)}, bf16[384,768]{1,0:T(8,128)(2,1)}, u32[]{:S(2)}, u32[]{:S(2)}) collective-permute-start(bf16[384,768]{1,0:T(8,128)(2,1)} %pad_maximum_fusion.13), channel_id=1, source_target_pairs={{0,3},{1,0},{2,1},{3,2},{4,7},{5,4},{6,5},{7,6},{8,11},{9,8},{10,9... | collective-permute-start | bytes 1769480 | tf_op jit(solution)/shard_map/ppermute | solution.py:441
  1148.6 44.5 %copy-start.62 = (bf16[384,768]{1,0:T(8,128)(2,1)S(1)}, bf16[384,768]{1,0:T(8,128)(2,1)}, u32[]{:S(2)}) copy-start(bf16[384,768]{1,0:T(8,128)(2,1)} %pad_maximum_fusion.10) | copy-start | bytes 1769476
  1148.6 4.2 collective-permute-start.45
  (83 other events, 696.1 us)
Sparse Core Ops, SparseCore 0:
  11.4 264.1 all-gather.2
  278.3 273.5 all-gather.4
  739.4 361.6 reduce-scatter.1

commit v8 on v6

--- a/solution.py
+++ b/solution.py
@@ -103,8 +103,12 @@
     return pl.ds(pl.multiple_of(block * BLOCK, BLOCK), BLOCK)
 
 
+def wide_rows(block):
+    return pl.ds(pl.multiple_of(block * WIDE, WIDE), WIDE)
+
+
 def fold(values):
-    return values.reshape(BLOCK // 8, 8, WIDE)
+    return values.reshape(values.shape[0] // 8, 8, WIDE)
 
 
 def shift_tile(gated, rows, own_segment, segment_ref, shared_ref):
@@ -114,8 +118,21 @@
     return jnp.concatenate([shift, shift], axis=1)
 
 
-def bias_pair(bias_ref, pair, offset):
-    return jnp.concatenate([bias_ref[2 * pair, offset], bias_ref[2 * pair + 1, offset]], axis=1)
+def used_blocks(low_ref, high_ref):
+    last = pl.num_programs(0) - 1
+    return low_ref[0] // 2 * 2, (high_ref[last] + 1) // 2 * 2
+
+
+def tile_offsets(block, own_block):
+    return [jnp.clip(2 * block + k - own_block, -2, 2) + 2 for k in range(2)]
+
+
+def bias_pair(bias_ref, pair, offsets):
+    halves = [
+        jnp.concatenate([bias_ref[2 * pair, at], bias_ref[2 * pair + 1, at]], axis=1)
+        for at in offsets
+    ]
+    return jnp.concatenate(halves, axis=0)
 
 
 def pick_heads(wide):
@@ -124,27 +141,26 @@
 
 def forward_body(gated, low_ref, high_ref, *refs):
     query_ref, shared_ref, own_ref, segment_ref, bias_ref = refs[:5]
-    mixed_ref, total_ref, turned_ref, score_ref = refs[5:]
+    mixed_ref, total_ref, turned_ref, score_ref, sum_ref = refs[5:]
     step = pl.program_id(0)
-    key_blocks = shared_ref.shape[0] // BLOCK
 
     @pl.when(step == 0)
     def _():
-        @pl.loop(0, key_blocks)
+        @pl.loop(*used_blocks(low_ref, high_ref))
         def _(block):
             rows = block_rows(block)
             turned_ref[:, rows] = shared_ref[rows, INNER : 2 * INNER].T
 
-    first, last = low_ref[step], high_ref[step]
+    first, last = low_ref[step] // 2, (high_ref[step] + 1) // 2
     own_block = HALO // BLOCK + step
     own_segment = own_ref[0]
     masks = lane_masks()
     queries = [stacked(query_ref[:, pair_cols(pair)], masks) for pair in range(PAIRS)]
 
     def scores(block, peaks):
-        rows = block_rows(block)
+        rows = wide_rows(block)
         shift = shift_tile(gated, rows, own_segment, segment_ref, shared_ref)
-        offset = jnp.clip(block - own_block, -2, 2) + 2
+        offsets = tile_offsets(block, own_block)
         new_peaks = []
         for pair in range(PAIRS):
             score = lax.dot_general(
@@ -153,33 +169,34 @@
                 both_last,
                 preferred_element_type=jnp.float32,
             )
-            score = score + bias_pair(bias_ref, pair, offset) + shift
+            score = score + bias_pair(bias_ref, pair, offsets) + shift
             score_ref[pair, block] = score
             new_peaks.append(jnp.maximum(peaks[pair], jnp.max(fold(score), axis=0)))
         return tuple(new_peaks)
 
     start = jnp.full((8, WIDE), -3e38, jnp.float32)
     peaks = lax.fori_loop(first, last, scores, (start,) * PAIRS)
-    for pair in range(PAIRS):
-        peak = jnp.max(peaks[pair], axis=0, keepdims=True)
-
-        def mix(block, carry, pair=pair, peak=peak):
-            total, mixed = carry
-            weight = jnp.exp(score_ref[pair, block] - peak)
-            total = total + jnp.sum(fold(weight), axis=0)
-            mixed = mixed + jnp.dot(
-                turned_ref[pair_cols(pair), block_rows(block)],
+    peaks = [jnp.max(peak, axis=0, keepdims=True) for peak in peaks]
+    sum_ref[...] = jnp.zeros_like(sum_ref)
+
+    def mix(block, totals):
+        new_totals = []
+        for pair in range(PAIRS):
+            weight = jnp.exp(score_ref[pair, block] - peaks[pair])
+            new_totals.append(totals[pair] + jnp.sum(fold(weight), axis=0))
+            sum_ref[pair] += jnp.dot(
+                turned_ref[pair_cols(pair), wide_rows(block)],
                 weight.astype(jnp.bfloat16),
                 preferred_element_type=jnp.float32,
             )
-            return total, mixed
-
-        zero = (jnp.zeros((8, WIDE), jnp.float32), jnp.zeros((BLOCK, WIDE), jnp.float32))
-        total, mixed = lax.fori_loop(first, last, mix, zero)
-        row_total = jnp.sum(total, axis=0, keepdims=True)
-        mixed = pick_heads(mixed * (1.0 / row_total))
+        return tuple(new_totals)
+
+    totals = lax.fori_loop(first, last, mix, (jnp.zeros((8, WIDE), jnp.float32),) * PAIRS)
+    for pair in range(PAIRS):
+        row_total = jnp.sum(totals[pair], axis=0, keepdims=True)
+        mixed = pick_heads(sum_ref[pair] * (1.0 / row_total))
         mixed_ref[:, pair_cols(pair)] = mixed.T.astype(jnp.bfloat16)
-        total_ref[0, pair : pair + 1, :] = peak + jnp.log(row_total)
+        total_ref[0, pair : pair + 1, :] = peaks[pair] + jnp.log(row_total)
 
 
 def whole(shape):
@@ -212,7 +229,8 @@
             ],
             scratch_shapes=[
                 pltpu.VMEM((INNER, length), jnp.bfloat16),
-                pltpu.VMEM((PAIRS, key_blocks, BLOCK, WIDE), jnp.float32),
+                pltpu.VMEM((PAIRS, key_blocks // 2, WIDE, WIDE), jnp.float32),
+                pltpu.VMEM((PAIRS, BLOCK, WIDE), jnp.float32),
             ],
         ),
         out_shape=[
@@ -234,19 +252,18 @@
     grad_query_ref, grad_shared_ref, bucket_ref = refs[7:10]
     turned_ref, prob_ref, pull_ref, sum_ref, bias_sum_ref, turn_sum_ref = refs[10:]
     step = pl.program_id(0)
-    key_blocks = shared_ref.shape[0] // BLOCK
 
     @pl.when(step == 0)
     def _():
         bias_sum_ref[...] = jnp.zeros_like(bias_sum_ref)
 
-        @pl.loop(0, key_blocks)
+        @pl.loop(*used_blocks(low_ref, high_ref))
         def _(block):
             rows = block_rows(block)
             turned_ref[:, rows] = shared_ref[rows, :INNER].T
             sum_ref[rows, :] = jnp.zeros((BLOCK, sum_ref.shape[1]), jnp.float32)
 
-    first, last = low_ref[step], high_ref[step]
+    first, last = low_ref[step] // 2, (high_ref[step] + 1) // 2
     own_block = HALO // BLOCK + step
     own_segment = own_ref[0]
     masks = lane_masks()
@@ -255,9 +272,9 @@
     totals = [total_ref[0, pair : pair + 1, :] for pair in range(PAIRS)]
 
     def weights(block, deltas):
-        rows = block_rows(block)
+        rows = wide_rows(block)
         shift = shift_tile(gated, rows, own_segment, segment_ref, shared_ref)
-        offset = jnp.clip(block - own_block, -2, 2) + 2
+        offsets = tile_offsets(block, own_block)
         new_deltas = []
         for pair in range(PAIRS):
             cols = pair_cols(pair)
@@ -270,7 +287,7 @@
                 both_last,
                 preferred_element_type=jnp.float32,
             )
-            prob = jnp.exp(score + bias_pair(bias_ref, pair, offset) + shift - totals[pair])
+            prob = jnp.exp(score + bias_pair(bias_ref, pair, offsets) + shift - totals[pair])
             prob_ref[pair, block] = prob
             pull_ref[pair, block] = pull
             sum_ref[rows, value_cols(pair)] += jnp.dot(
@@ -286,13 +303,14 @@
 
     @pl.loop(first, last)
     def _(block):
-        rows = block_rows(block)
-        offset = jnp.clip(block - own_block, -2, 2) + 2
-        gate_part = jnp.zeros((BLOCK, BLOCK), jnp.float32)
+        rows = wide_rows(block)
+        offsets = tile_offsets(block, own_block)
+        gate_part = jnp.zeros((WIDE, BLOCK), jnp.float32)
         for pair in range(PAIRS):
             cols = pair_cols(pair)
             grad_score = prob_ref[pair, block] * (pull_ref[pair, block] - deltas[pair])
-            bias_sum_ref[pair, offset] += grad_score
+            bias_sum_ref[pair, offsets[0]] += grad_score[:BLOCK]
+            bias_sum_ref[pair, offsets[1]] += grad_score[BLOCK:]
             if gated:
                 gate_part = gate_part + (grad_score[:, :BLOCK] + grad_score[:, BLOCK:])
             score_low = grad_score.astype(jnp.bfloat16)
@@ -310,7 +328,9 @@
 
     @pl.when(step == pl.num_programs(0) - 1)
     def _():
-        @pl.loop(0, key_blocks)
+        grad_shared_ref[...] = jnp.zeros_like(grad_shared_ref)
+
+        @pl.loop(*used_blocks(low_ref, high_ref))
         def _(block):
             rows = block_rows(block)
             both = slice(0, 2 * INNER)
@@ -365,8 +385,8 @@
             ],
             scratch_shapes=[
                 pltpu.VMEM((INNER, length), jnp.bfloat16),
-                pltpu.VMEM((PAIRS, key_blocks, BLOCK, WIDE), jnp.float32),
-                pltpu.VMEM((PAIRS, key_blocks, BLOCK, WIDE), jnp.float32),
+                pltpu.VMEM((PAIRS, key_blocks // 2, WIDE, WIDE), jnp.float32),
+                pltpu.VMEM((PAIRS, key_blocks // 2, WIDE, WIDE), jnp.float32),
                 pltpu.VMEM((length, width), jnp.float32),
                 pltpu.VMEM((PAIRS, OFFSETS, BLOCK, WIDE), jnp.float32),
                 pltpu.VMEM((PAIRS, BLOCK, WIDE), jnp.float32),
@@ -978,6 +998,12 @@
             total = total.reshape((lax.axis_size(route[0]), -1) + total.shape[-1:])
             sends = stage_sends(total, route[0], 0)
             moves[name] = (route, pick(total, lax.axis_index(route[0]), 0), sends)
+        if moves and all(move[0] == ("z",) for move in moves.values()):
+            kept = jnp.concatenate([move[1] for move in moves.values()], axis=-1)
+            sends = [
+                jnp.concatenate(parts, axis=-1) for parts in zip(*(m[2] for m in moves.values()))
+            ]
+            moves = {tuple(moves): (("z",), kept, sends)}
         arrays, values = tied({name: move[1:] for name, move in moves.items()}, values)
         for name, (route, *_) in moves.items():
             kept, sends = arrays[name]
@@ -1145,15 +1171,15 @@
     for bit in range(2, lax.axis_size("z")):
         if bit & (bit - 1) == 0:
             small = hop(small, "z", bit)
+    small = scatter.step(small, (0, 1))
     small = scatter.step(small, 2, 3)
     small = scatter.step(small, 2, 3)
     small = hop(small, "x")
     for bit in range(1, lax.axis_size("y")):
         if bit & (bit - 1) == 0:
             small = hop(small, "y", bit)
-    summed = scatter.step(small, 0, 1)
-    summed = scatter.step(summed, 2, 3)
-    local_three = jnp.concatenate([scatter.results[chunk] for chunk in range(4)], axis=1)
+    summed = scatter.step(small, (2, 3))
+    local_three = jnp.concatenate([scatter.results[pair] for pair in ((0, 1), (2, 3))], axis=1)
     local_three, local_four = local_three[:, :width], local_four[:, :width].astype(jnp.float32)
     return (
         after_four.reshape(inputs.shape),

time: 1210 us -> 1180 us (0.975)
  Pallas kernels: 309 us -> 240 us
  waiting for transfers between devices: 626 us -> 649 us
  starting transfers between devices: 87.1 us -> 106 us
    pallas_call x2, Pallas kernels: 74 us -> 38.6 us  [attend_backward(): pl.pallas_call(functools.partial(backward_body, width > 2 * INNER), grid_...]
    pallas_call x2, Pallas kernels: 47 us -> 12.7 us  [attend_forward(): pl.pallas_call(functools.partial(forward_body, width > 2 * INNER), grid_s...]
    ppermute x4, starting transfers between devices: 1.91 us -> 26.2 us  [far_pair(): got = lax.ppermute(sent, 'z', pairs)]
    all_gather x2, waiting for transfers between devices: 323 us -> 340 us  [fetch_rows(): return lax.all_gather(local_rows, DEVICES, axis=0, tiled=True)]
    ppermute x28 -> x22, starting transfers between devices: 51.4 us -> 44.7 us  [shift(): lax.ppermute(value, axis, [(i, (i + amount) % count) for i in range(count)])]
    unnamed x211 -> x219, local copies, waits for them, and re-layouts: 39.7 us -> 41.8 us
    ppermute x28 -> x22, waiting for transfers between devices: 202 us -> 203 us  [shift(): lax.ppermute(value, axis, [(i, (i + amount) % count) for i in range(count)])]
  transfers between devices with their start and end apart: 48 -> 42, of which waited for: 23 -> 23; matrix products, arithmetic and copies ran while one was open for 11% -> 11% of each run, Pallas kernels for 18% -> 14%
where the time goes in v8:
time: 1180 us
  waiting for transfers between devices  649 us (55%)
  Pallas kernels  240 us (20%)
  starting transfers between devices  106 us (9%)
  other arithmetic  72.2 us (6%)
  local copies, waits for them, and re-layouts  62.6 us (5%)
  matrix products  32.5 us (3%)
  between operations  15.6 us (1%)
    all_gather x2, waiting for transfers between devices, fetch_rows(): return lax.all_gather(local_rows, DEVICES, axis=0, tiled=True)  340 us
    ppermute x22, waiting for transfers between devices, shift(): lax.ppermute(value, axis, [(i, (i + amount) % count) for i in range(count)])  203 us
    ppermute x4, waiting for transfers between devices, far_pair(): got = lax.ppermute(sent, 'z', pairs)  67.1 us
    pallas_call x2, Pallas kernels, ffn_backward(): pl.pallas_call(ffn_backward_body, grid_spec=pltpu.PrefetchScalarGridSpec(...  66.1 us
    pallas_call x2, Pallas kernels, ffn_forward(): pl.pallas_call(ffn_forward_body, grid=(steps,), in_specs=[resident((token...  49.4 us
    pallas_call x2, Pallas kernels, weight_grads(): pl.pallas_call(functools.partial(weight_grads_body, tail, tile), grid_spe...  47 us
    ppermute x22, starting transfers between devices, shift(): lax.ppermute(value, axis, [(i, (i + amount) % count) for i in range(count)])  44.7 us
    unnamed x219, local copies, waits for them, and re-layouts  41.8 us
  transfers between devices with their start and end apart: 42, of which 23 were waited for; matrix products, arithmetic and copies ran while one was open for 11% of the time, Pallas kernels for 14%

profile of v8, /device:TPU:24, one launch (start us, length us, event | category | flops | bytes accessed | tf_op | source)
XLA Modules:
  0.0 1177.8 jit_solution(13882106699566463579)
XLA Ops:
  7.2 2.5 copy.113
  12.0 2.4 copy.112
  18.1 207.3 %all-gather.3.cloned.1.call-done.gelu_ref.linear_ref.down_ref.refs_4_.refs_5_.refs_6_ = bf16[12288,1472]{1,0:T(8,128)(2,1)} async-done(((bf16[384,1472]{1,0:T(8,128)(2,1)}), bf16[12288,1472]{1,0:T(8,128)(2,1)}) %all-gather.3.cloned.1.call-update) | async-done | bytes 36175888 | tf_op jit(solution)/shard_map/all_gather | solution.py:1022
  225.4 4.7 fusion.33
  234.4 6.1 collective-permute-start.2
  241.3 4.7 bias_tiles.1.refs_4_.refs_5_
  246.0 3.5 copy.118
  250.7 22.5 %collective-permute-done = bf16[288,768]{1,0:T(8,128)(2,1)} collective-permute-done((bf16[288,768]{1,0:T(8,128)(2,1)}, bf16[288,768]{1,0:T(8,128)(2,1)}, u32[]{:S(2)}, u32[]{:S(2)}) %collective-permute-start) | collective-permute-done | bytes 442400 | tf_op jit(solution)/shard_map/ppermute | solution.py:475
  274.3 14.3 %collective-permute-done.1 = bf16[512,768]{1,0:T(8,128)(2,1)} collective-permute-done((bf16[512,768]{1,0:T(8,128)(2,1)}, bf16[512,768]{1,0:T(8,128)(2,1)}, u32[]{:S(2)}, u32[]{:S(2)}) %collective-permute-start.1) | collective-permute-done | bytes 786464 | tf_op jit(solution)/shard_map/ppermute | solution.py:467
  291.4 6.3 attend_forward.2
  297.8 2.5 multiply_reduce_fusion.10
  302.0 24.9 %ffn_forward.2 = (f32[512,1472]{1,0:T(8,128)S(1)}, f32[512,3584]{1,0:T(8,128)}, f32[512,3584]{1,0:T(8,128)}) custom-call(bf16[512,1472]{1,0:T(8,128)(2,1)S(1)} %multiply_convert_fusion.2.normed_ref.refs_1_, f32[512,1472]{1,0:T(8,128)} %copy-done.41, bf16[12288,1472]{1,0:T(8,128)(2,1)} %all-gather.3.cloned.1.call-done.gelu_ref.linear_ref.down_ref.refs_4_.refs_5_.refs_6_, ...), custom_call_target="tpu_custom_call" | custom-call | flops 16206790656 | bytes 46333952 | tf_op jit(solution)/shard_map/ffn_forward/pallas_call | solution.py:602
  330.1 133.0 %all-gather.5.cloned.1.call-done.gelu_ref.linear_ref.down_ref.refs_4_.refs_5_.refs_6_ = bf16[12288,1472]{1,0:T(8,128)(2,1)} async-done(((bf16[384,1472]{1,0:T(8,128)(2,1)}), bf16[12288,1472]{1,0:T(8,128)(2,1)}) %all-gather.5.cloned.1.call-update) | async-done | bytes 36175888 | tf_op jit(solution)/shard_map/all_gather | solution.py:1022
  463.1 4.7 fusion.36
  470.0 4.4 collective-permute-start.5
  480.5 39.3 %collective-permute-done.3 = bf16[288,896]{1,0:T(8,128)(2,1)} collective-permute-done((bf16[288,896]{1,0:T(8,128)(2,1)}, bf16[288,896]{1,0:T(8,128)(2,1)}, u32[]{:S(2)}, u32[]{:S(2)}) %collective-permute-start.3) | collective-permute-done | bytes 516128 | tf_op jit(solution)/shard_map/ppermute | solution.py:475
  524.1 6.3 attend_forward.3
  530.4 2.4 multiply_reduce_fusion.7
  534.5 24.6 %ffn_forward.3 = (f32[512,1472]{1,0:T(8,128)S(1)}, f32[512,3584]{1,0:T(8,128)}, f32[512,3584]{1,0:T(8,128)}) custom-call(bf16[512,1472]{1,0:T(8,128)(2,1)S(1)} %multiply_convert_fusion.normed_ref.refs_1_, f32[512,1472]{1,0:T(8,128)} %copy-done.43, bf16[12288,1472]{1,0:T(8,128)(2,1)} %all-gather.5.cloned.1.call-done.gelu_ref.linear_ref.down_ref.refs_4_.refs_5_.refs_6_, ...), custom_call_target="tpu_custom_call" | custom-call | flops 16206790656 | bytes 46333952 | tf_op jit(solution)/shard_map/ffn_forward/pallas_call | solution.py:602
  559.1 32.7 %ffn_backward.2 = (f32[512,1472]{1,0:T(8,128)}, bf16[6144,512]{1,0:T(8,128)(2,1)}, bf16[6144,512]{1,0:T(8,128)(2,1)}) custom-call(s32[2]{0:T(128)} %pad_add_fusion.core_ref, bf16[512,1472]{1,0:T(8,128)(2,1)} %bitcast_convert_fusion.refs_0_, bf16[512,1472]{1,0:T(8,128)(2,1)} %copy-done.2, f32[512,3584]{1,0:T(8,128)} %get-tuple-element.134.refs_2_, ...), custom_call_target="tpu_custom_call" | custom-call | flops 16206790656 | bytes 57344000 | tf_op jit(solution)/shard_map/ffn_backward/pallas_call | solution.py:705
  591.8 3.4 collective-permute-start.6
  596.4 2.3 fusion.11.refs_2_.refs_3_
  600.2 2.3 multiply_reduce_fusion.1
  602.5 2.5 fusion.51
  605.0 2.9 convolution_convert_fusion.1.refs_1_
  607.9 19.8 %attend_backward.2 = (bf16[512,384]{1,0:T(8,128)(2,1)S(1)}, bf16[2304,896]{1,0:T(8,128)(2,1)}, f32[3,32,256]{2,1,0:T(8,128)S(1)}) custom-call(s32[4]{0:T(128)S(1)} %get-tuple-element.381.low_ref, s32[4]{0:T(128)S(1)} %get-tuple-element.380.high_ref, bf16[512,384]{1,0:T(8,128)(2,1)S(1)} %copy-done.29, bf16[512,384]{1,0:T(8,128)(2,1)S(1)} %convolution_convert_fusion.1.refs_1_, ...), custom_call_target="tpu_custom_call" | custom-call | flops 4529848320 | bytes 12582912 | tf_op jit(solution)/shard_map/attend_backward/pallas_call | solution.py:367
  629.2 10.2 collective-permute-start.10
  642.7 4.6 collective-permute-start.8
  647.3 3.5 fusion.12.refs_2_.refs_3_
  650.8 22.0 %weight_grads.2.refs_6_ = bf16[6144,1536]{1,0:T(8,128)(2,1)} custom-call(s32[6]{0:T(128)S(1)} %stack.55.place_ref, bf16[6144,512]{1,0:T(8,128)(2,1)S(1)} %bitcast.114, bf16[6144,512]{1,0:T(8,128)(2,1)} %collective-permute-done.6.refs_1_, bf16[1024,1536]{1,0:T(8,128)(2,1)S(1)} %fusion.11.refs_2_.refs_3_, bf16[1024,1536]{1,0:T(8,128)(2,1)S(1)} %fusion.11.refs_2_.refs_3_, ...), custom_call_target="tpu_custom_call" | custom-call | flops 18522046464 | bytes 31457280 | tf_op jit(solution)/shard_map/weight_grads/pallas_call | solution.py:853
  672.9 3.0 collective-permute-done.9
  679.7 2.4 pad_maximum_fusion.4
  682.4 10.6 attention_fill.2
  695.7 5.6 multiply_reduce_fusion.2
  701.4 2.5 fusion.49
  703.9 33.4 %ffn_backward.3 = (f32[512,1472]{1,0:T(8,128)}, bf16[6144,512]{1,0:T(8,128)(2,1)}, bf16[6144,512]{1,0:T(8,128)(2,1)}) custom-call(s32[2]{0:T(128)} %pad_add_fusion.core_ref, bf16[512,1472]{1,0:T(8,128)(2,1)} %get-tuple-element.320.refs_0_, bf16[512,1472]{1,0:T(8,128)(2,1)} %copy-done, f32[512,3584]{1,0:T(8,128)} %get-tuple-element.151.refs_2_, ...), custom_call_target="tpu_custom_call" | custom-call | flops 16206790656 | bytes 57344000 | tf_op jit(solution)/shard_map/ffn_backward/pallas_call | solution.py:705
  742.1 2.4 fusion.48
  744.6 2.4 convolution_convert_fusion.refs_1_
  747.0 18.8 %attend_backward.3 = (bf16[512,384]{1,0:T(8,128)(2,1)S(1)}, bf16[2304,768]{1,0:T(8,128)(2,1)}, f32[3,32,256]{2,1,0:T(8,128)S(1)}) custom-call(s32[4]{0:T(128)S(1)} %get-tuple-element.381.low_ref, s32[4]{0:T(128)S(1)} %get-tuple-element.380.high_ref, bf16[512,384]{1,0:T(8,128)(2,1)S(1)} %copy-done.32, bf16[512,384]{1,0:T(8,128)(2,1)S(1)} %convolution_convert_fusion.refs_1_, ...), custom_call_target="tpu_custom_call" | custom-call | flops 4529848320 | bytes 12582912 | tf_op jit(solution)/shard_map/attend_backward/pallas_call | solution.py:367
  765.9 2.1 slice_select_fusion.2
  767.9 14.1 %collective-permute-start.17 = (bf16[288,768]{1,0:T(8,128)(2,1)}, bf16[288,768]{1,0:T(8,128)(2,1)}, u32[]{:S(2)}, u32[]{:S(2)}) collective-permute-start(bf16[288,768]{1,0:T(8,128)(2,1)} %slice_select_fusion.2), channel_id=1, source_target_pairs={{0,2},{1,3},{2,0},{3,1},{4,6},{5,7},{6,4},{7,5},{8,10},{9,11},{10,... | collective-permute-start | bytes 1327112 | tf_op jit(solution)/shard_map/ppermute | solution.py:475
  782.1 2.6 fusion.53
  786.0 5.5 collective-permute-start.15
  791.9 25.0 %weight_grads.3 = (bf16[3072,384]{1,0:T(8,128)(2,1)}, bf16[3072,384]{1,0:T(8,128)(2,1)S(1)}, bf16[3072,384]{1,0:T(8,128)(2,1)S(1)}, bf16[3072,384]{1,0:T(8,128)(...) custom-call(s32[6]{0:T(128)S(1)} %stack.55.place_ref, ...), custom_call_target="tpu_custom_call" | custom-call | flops 18522046464 | bytes 31457280 | tf_op jit(solution)/shard_map/weight_grads/pallas_call | solution.py:853
  816.9 5.3 collective-permute-done.17
  822.2 15.4 %collective-permute-done.16 = bf16[512,768]{1,0:T(8,128)(2,1)} collective-permute-done((bf16[512,768]{1,0:T(8,128)(2,1)}, bf16[512,768]{1,0:T(8,128)(2,1)}, u32[]{:S(2)}, u32[]{:S(2)}) %collective-permute-start.16) | collective-permute-done | bytes 786464 | tf_op jit(solution)/shard_map/ppermute | solution.py:467
  841.9 2.2 collective-permute-done.18.refs_1_
  844.4 10.8 attention_fill.3
  862.2 2.4 collective-permute-start.20
  866.7 7.3 fusion.24
  876.0 58.7 %collective-permute-done.20 = bf16[3072,384]{1,0:T(8,128)(2,1)} collective-permute-done((bf16[3072,384]{1,0:T(8,128)(2,1)}, bf16[3072,384]{1,0:T(8,128)(2,1)}, u32[]{:S(2)}, u32[]{:S(2)}) %collective-permute-start.20) | collective-permute-done | bytes 2359328 | tf_op jit(solution)/shard_map/ppermute | solution.py:461
  936.2 2.3 add_convert_fusion.3
  941.0 2.4 add_convert_fusion.2
  947.1 3.7 collective-permute-start.25
  952.9 3.4 collective-permute-done.25
  957.1 21.3 %collective-permute-done.23 = bf16[1536,384]{1,0:T(8,128)(2,1)} collective-permute-done((bf16[1536,384]{1,0:T(8,128)(2,1)}, bf16[1536,384]{1,0:T(8,128)(2,1)}, u32[]{:S(2)}, u32[]{:S(2)}) %collective-permute-start.23) | collective-permute-done | bytes 1179680 | tf_op jit(solution)/shard_map/ppermute | solution.py:461
  978.4 7.9 collective-permute-done.24
  997.3 16.4 %collective-permute-start.28 = (bf16[384,768]{1,0:T(8,128)(2,1)S(1)}, bf16[384,768]{1,0:T(8,128)(2,1)S(1)}, u32[]{:S(2)}, u32[]{:S(2)}) collective-permute-start(bf16[384,768]{1,0:T(8,128)(2,1)S(1)} %pad_maximum_fusion.9), channel_id=1, source_target_pairs={{0,3},{1,0},{2,1},{3,2},{4,7},{5,4},{6,5},{7,6},{8,11},{9,8},{10,9... | collective-permute-start | bytes 1769480 | tf_op jit(solution)/shard_map/ppermute | solution.py:461
  1013.7 55.0 %collective-permute-done.27 = bf16[384,768]{1,0:T(8,128)(2,1)S(1)} collective-permute-done((bf16[384,768]{1,0:T(8,128)(2,1)S(1)}, bf16[384,768]{1,0:T(8,128)(2,1)S(1)}, u32[]{:S(2)}, u32[]{:S(2)}) %collective-permute-start.27) | collective-permute-done | bytes 589856 | tf_op jit(solution)/shard_map/ppermute | solution.py:461
  1077.1 2.3 copy.127
  1079.4 15.4 %collective-permute-done.32 = bf16[1536,384]{1,0:T(8,128)(2,1)} collective-permute-done((bf16[1536,384]{1,0:T(8,128)(2,1)}, bf16[1536,384]{1,0:T(8,128)(2,1)}, u32[]{:S(2)}, u32[]{:S(2)}) %collective-permute-start.32) | collective-permute-done | bytes 1179680 | tf_op jit(solution)/shard_map/ppermute | solution.py:461
  1104.1 8.3 collective-permute-start.35
  1115.2 2.5 copy.128
  1122.5 39.1 %collective-permute-done.35 = bf16[384,768]{1,0:T(8,128)(2,1)} collective-permute-done((bf16[384,768]{1,0:T(8,128)(2,1)}, bf16[384,768]{1,0:T(8,128)(2,1)}, u32[]{:S(2)}, u32[]{:S(2)}) %collective-permute-start.35) | collective-permute-done | bytes 589856 | tf_op jit(solution)/shard_map/ppermute | solution.py:461
  (384 shorter events, 127.2 us)
Async XLA Ops:
  7.2 218.2 %all-gather.3.cloned.1.call-start = ((), (), s32[]{:S(2)}) async-start(), calls=%async_computation.1 | async-start | bytes 38928384 | tf_op jit(solution)/shard_map/all_gather | solution.py:1022
  9.7 453.3 %all-gather.5.cloned.1.call-start = ((), (), s32[]{:S(2)}) async-start(), calls=%async_computation.2 | async-start | bytes 38928384 | tf_op jit(solution)/shard_map/all_gather | solution.py:1022
  11.9 1155.8 %reduce-scatter.2.cloned.1.call-start = ((), (), s32[]{:S(2)}) async-start(), calls=%async_computation.3 | async-start | bytes 20054016 | tf_op jit(solution)/shard_map/reduce_scatter | solution.py:1112
  14.4 283.5 %copy-start.39 = (f32[1,512,1472]{2,1,0:T(8,128)}, f32[1,512,1472]{2,1,0:T(8,128)S(1)}, u32[]{:S(2)}) copy-start(f32[1,512,1472]{2,1,0:T(8,128)S(1)} %copy.112) | copy-start | bytes 9043972
  15.1 285.9 %copy-start.71 = (f32[1472]{0:T(1024)}, f32[1472]{0:T(1024)S(1)}, u32[]{:S(2)}) copy-start(f32[1472]{0:T(1024)S(1)} %get-tuple-element.311) | copy-start | bytes 17668
  15.1 312.7 %copy-start.75 = (f32[1472]{0:T(1024)}, f32[1472]{0:T(1024)S(1)}, u32[]{:S(2)}) copy-start(f32[1472]{0:T(1024)S(1)} %get-tuple-element.313) | copy-start | bytes 17668
  18.1 222.5 %copy-start.98 = (f32[32,6]{0,1:T(8,128)S(1)}, f32[32,6]{0,1:T(8,128)}, u32[]{:S(2)}) copy-start(f32[32,6]{0,1:T(8,128)} %param.13) | copy-start | bytes 2308
  232.0 41.2 %collective-permute-start = (bf16[288,768]{1,0:T(8,128)(2,1)}, bf16[288,768]{1,0:T(8,128)(2,1)}, u32[]{:S(2)}, u32[]{:S(2)}) collective-permute-start(bf16[288,768]{1,0:T(8,128)(2,1)} %slice_select_fusion.1), channel_id=1, source_target_pairs={{0,2},{1,3},{2,0},{3,1},{4,6},{5,7},{6,4},{7,5},{8,10},{9,11},{10,... | collective-permute-start | bytes 1327112 | tf_op jit(solution)/shard_map/ppermute | solution.py:475
  232.6 55.9 %collective-permute-start.1 = (bf16[512,768]{1,0:T(8,128)(2,1)}, bf16[512,768]{1,0:T(8,128)(2,1)}, u32[]{:S(2)}, u32[]{:S(2)}) collective-permute-start(bf16[512,768]{1,0:T(8,128)(2,1)} %slice.177), channel_id=1, source_target_pairs={{0,1},{1,2},{2,3},{4,5},{5,6},{6,7},{8,9},{9,10},{10,11},{12,13},{... | collective-permute-start | bytes 2359304 | tf_op jit(solution)/shard_map/ppermute | solution.py:467
  234.4 55.4 %collective-permute-start.2 = (bf16[512,768]{1,0:T(8,128)(2,1)}, bf16[512,768]{1,0:T(8,128)(2,1)}, u32[]{:S(2)}, u32[]{:S(2)}) collective-permute-start(bf16[512,768]{1,0:T(8,128)(2,1)} %slice.177), channel_id=1, source_target_pairs={{1,0},{2,1},{3,2},{5,4},{6,5},{7,6},{9,8},{10,9},{11,10},{13,12},{... | collective-permute-start | bytes 2359304 | tf_op jit(solution)/shard_map/ppermute | solution.py:467
  249.5 40.2 %copy-start.58 = (bf16[512,1152]{1,0:T(8,128)(2,1)S(1)}, bf16[512,1152]{1,0:T(8,128)(2,1)}, u32[]{:S(2)}) copy-start(bf16[512,1152]{1,0:T(8,128)(2,1)} %copy-done.57) | copy-start | bytes 3538948
  250.7 40.8 %copy-start.31 = (bf16[512,384]{1,0:T(8,128)(2,1)}, bf16[512,384]{1,0:T(8,128)(2,1)S(1)}, u32[]{:S(2)}) copy-start(bf16[512,384]{1,0:T(8,128)(2,1)S(1)} %slice.174.refs_0_) | copy-start | bytes 1179652
  301.0 25.8 %copy-start.82 = (f32[512]{0:T(512)}, f32[512]{0:T(512)S(1)}, u32[]{:S(2)}) copy-start(f32[512]{0:T(512)S(1)} %get-tuple-element.369) | copy-start | bytes 6148
  327.8 140.0 %copy-start.87 = (f32[512]{0:T(512)}, f32[512]{0:T(512)S(1)}, u32[]{:S(2)}) copy-start(f32[512]{0:T(512)S(1)} %get-tuple-element.371) | copy-start | bytes 6148
  330.1 137.7 %copy-start.89 = (f32[512]{0:T(512)}, f32[512]{0:T(512)S(1)}, u32[]{:S(2)}) copy-start(f32[512]{0:T(512)S(1)} %get-tuple-element.325) | copy-start | bytes 6148
  470.0 52.6 %collective-permute-start.5 = (bf16[512,896]{1,0:T(8,128)(2,1)}, bf16[512,896]{1,0:T(8,128)(2,1)}, u32[]{:S(2)}, u32[]{:S(2)}) collective-permute-start(bf16[512,896]{1,0:T(8,128)(2,1)} %pad_maximum_fusion.1), channel_id=1, source_target_pairs={{1,0},{2,1},{3,2},{5,4},{6,5},{7,6},{9,8},{10,9},{11,10},{13,12},{... | collective-permute-start | bytes 2752520 | tf_op jit(solution)/shard_map/ppermute | solution.py:467
  474.4 46.6 %collective-permute-start.4 = (bf16[512,896]{1,0:T(8,128)(2,1)}, bf16[512,896]{1,0:T(8,128)(2,1)}, u32[]{:S(2)}, u32[]{:S(2)}) collective-permute-start(bf16[512,896]{1,0:T(8,128)(2,1)} %pad_maximum_fusion.1), channel_id=1, source_target_pairs={{0,1},{1,2},{2,3},{4,5},{5,6},{6,7},{8,9},{9,10},{10,11},{12,13},{... | collective-permute-start | bytes 2752520 | tf_op jit(solution)/shard_map/ppermute | solution.py:467
  476.2 43.6 %collective-permute-start.3 = (bf16[288,896]{1,0:T(8,128)(2,1)}, bf16[288,896]{1,0:T(8,128)(2,1)}, u32[]{:S(2)}, u32[]{:S(2)}) collective-permute-start(bf16[288,896]{1,0:T(8,128)(2,1)} %fusion.44), channel_id=1, source_target_pairs={{0,2},{1,3},{2,0},{3,1},{4,6},{5,7},{6,4},{7,5},{8,10},{9,11},{10,... | collective-permute-start | bytes 1548296 | tf_op jit(solution)/shard_map/ppermute | solution.py:475
  478.8 43.7 %copy-start.51 = (bf16[512,768]{1,0:T(8,128)(2,1)S(1)}, bf16[512,768]{1,0:T(8,128)(2,1)}, u32[]{:S(2)}) copy-start(bf16[512,768]{1,0:T(8,128)(2,1)} %copy-done.50) | copy-start | bytes 2359300
  480.5 43.5 %copy-start.28 = (bf16[512,384]{1,0:T(8,128)(2,1)}, bf16[512,384]{1,0:T(8,128)(2,1)S(1)}, u32[]{:S(2)}) copy-start(bf16[512,384]{1,0:T(8,128)(2,1)S(1)} %slice.180.refs_0_) | copy-start | bytes 1179652
  533.4 25.7 %copy-start.84 = (f32[512]{0:T(512)}, f32[512]{0:T(512)S(1)}, u32[]{:S(2)}) copy-start(f32[512]{0:T(512)S(1)} %get-tuple-element.373) | copy-start | bytes 6148
  559.1 32.7 %copy-start.21 = (f32[512,1472]{1,0:T(8,128)}, f32[512,1472]{1,0:T(8,128)S(1)}, u32[]{:S(2)}) copy-start(f32[512,1472]{1,0:T(8,128)S(1)} %get-tuple-element.133) | copy-start | bytes 9043972
  591.8 59.0 %collective-permute-start.6 = (bf16[6144,512]{1,0:T(8,128)(2,1)}, bf16[6144,512]{1,0:T(8,128)(2,1)}, u32[]{:S(2)}, u32[]{:S(2)}) collective-permute-start(bf16[6144,512]{1,0:T(8,128)(2,1)} %get-tuple-element.142), channel_id=1, source_target_pairs={{0,4},{4,0},{1,5},{5,1},{2,6},{6,2},{3,7},{7,3},{8,12},{12,8},{9,1... | collective-permute-start | bytes 18874376 | tf_op jit(solution)/shard_map/ppermute | solution.py:461
  598.7 52.1 %collective-permute-start.7 = (bf16[1024,1536]{1,0:T(8,128)(2,1)S(1)}, bf16[1024,1536]{1,0:T(8,128)(2,1)S(1)}, u32[]{:S(2)}, u32[]{:S(2)}) collective-permute-start(bf16[1024,1536]{1,0:T(8,128)(2,1)S(1)} %fusion.11.refs_2_.refs_3_), channel_id=1, source_target_pairs={{0,4},{4,0},{1,5},{5,1},{2,6},{6,2},{3,7},{7,3},{8,12},{12,8},{9,1... | collective-permute-start | bytes 9437192 | tf_op jit(solution)/shard_map/ppermute | solution.py:461
  627.7 48.8 %copy-start.30 = (bf16[512,384]{1,0:T(8,128)(2,1)}, bf16[512,384]{1,0:T(8,128)(2,1)S(1)}, u32[]{:S(2)}) copy-start(bf16[512,384]{1,0:T(8,128)(2,1)S(1)} %get-tuple-element.138) | copy-start | bytes 1179652
  629.2 43.7 %collective-permute-start.10 = (bf16[288,896]{1,0:T(8,128)(2,1)S(1)}, bf16[288,896]{1,0:T(8,128)(2,1)S(1)}, u32[]{:S(2)}, u32[]{:S(2)}) collective-permute-start(bf16[288,896]{1,0:T(8,128)(2,1)S(1)} %slice_select_fusion), channel_id=1, source_target_pairs={{0,2},{1,3},{2,0},{3,1},{4,6},{5,7},{6,4},{7,5},{8,10},{9,11},{10,... | collective-permute-start | bytes 1548296 | tf_op jit(solution)/shard_map/ppermute | solution.py:475
  641.4 34.4 %collective-permute-start.9 = (bf16[512,896]{1,0:T(8,128)(2,1)S(1)}, bf16[512,896]{1,0:T(8,128)(2,1)S(1)}, u32[]{:S(2)}, u32[]{:S(2)}) collective-permute-start(bf16[512,896]{1,0:T(8,128)(2,1)S(1)} %get-tuple-element.326), channel_id=1, source_target_pairs={{0,1},{1,2},{2,3},{4,5},{5,6},{6,7},{8,9},{9,10},{10,11},{12,13},{... | collective-permute-start | bytes 2752520 | tf_op jit(solution)/shard_map/ppermute | solution.py:467
  642.7 33.2 %collective-permute-start.8 = (bf16[512,896]{1,0:T(8,128)(2,1)S(1)}, bf16[512,896]{1,0:T(8,128)(2,1)S(1)}, u32[]{:S(2)}, u32[]{:S(2)}) collective-permute-start(bf16[512,896]{1,0:T(8,128)(2,1)S(1)} %get-tuple-element.327), channel_id=1, source_target_pairs={{1,0},{2,1},{3,2},{5,4},{6,5},{7,6},{9,8},{10,9},{11,10},{13,12},{... | collective-permute-start | bytes 2752520 | tf_op jit(solution)/shard_map/ppermute | solution.py:467
  650.8 31.3 %collective-permute-start.12 = (bf16[1024,1536]{1,0:T(8,128)(2,1)}, bf16[1024,1536]{1,0:T(8,128)(2,1)}, u32[]{:S(2)}, u32[]{:S(2)}) collective-permute-start(bf16[1024,1536]{1,0:T(8,128)(2,1)} %fusion.12.refs_2_.refs_3_), channel_id=1, source_target_pairs={{0,4},{4,0},{1,5},{5,1},{2,6},{6,2},{3,7},{7,3},{8,12},{12,8},{9,1... | collective-permute-start | bytes 9437192 | tf_op jit(solution)/shard_map/ppermute | solution.py:461
  678.4 4.0 collective-permute-start.11
  703.9 33.5 %copy-start.1 = (bf16[512,1472]{1,0:T(8,128)(2,1)S(1)}, bf16[512,1472]{1,0:T(8,128)(2,1)}, u32[]{:S(2)}) copy-start(bf16[512,1472]{1,0:T(8,128)(2,1)} %copy-done) | copy-start | bytes 4521988
  703.9 33.5 %copy-start.48 = (bf16[512,1472]{1,0:T(8,128)(2,1)S(1)}, bf16[512,1472]{1,0:T(8,128)(2,1)}, u32[]{:S(2)}) copy-start(bf16[512,1472]{1,0:T(8,128)(2,1)} %get-tuple-element.320.refs_0_) | copy-start | bytes 4521988
  703.9 35.9 %copy-start.72 = (f32[1472]{0:T(1024)S(1)}, f32[1472]{0:T(1024)}, u32[]{:S(2)}) copy-start(f32[1472]{0:T(1024)} %copy-done.71) | copy-start | bytes 17668
  737.3 54.6 %collective-permute-start.13 = (bf16[6144,512]{1,0:T(8,128)(2,1)}, bf16[6144,512]{1,0:T(8,128)(2,1)}, u32[]{:S(2)}, u32[]{:S(2)}) collective-permute-start(bf16[6144,512]{1,0:T(8,128)(2,1)} %get-tuple-element.159), channel_id=1, source_target_pairs={{0,4},{4,0},{1,5},{5,1},{2,6},{6,2},{3,7},{7,3},{8,12},{12,8},{9,1... | collective-permute-start | bytes 18874376 | tf_op jit(solution)/shard_map/ppermute | solution.py:461
  739.4 52.4 %collective-permute-start.14 = (bf16[1024,1536]{1,0:T(8,128)(2,1)}, bf16[1024,1536]{1,0:T(8,128)(2,1)}, u32[]{:S(2)}, u32[]{:S(2)}) collective-permute-start(bf16[1024,1536]{1,0:T(8,128)(2,1)} %fusion.13.refs_2_.refs_3_), channel_id=1, source_target_pairs={{0,4},{4,0},{1,5},{5,1},{2,6},{6,2},{3,7},{7,3},{8,12},{12,8},{9,1... | collective-permute-start | bytes 9437192 | tf_op jit(solution)/shard_map/ppermute | solution.py:461
  765.9 25.6 %copy-start.59 = (bf16[512,1472]{1,0:T(8,128)(2,1)S(1)}, bf16[512,1472]{1,0:T(8,128)(2,1)}, u32[]{:S(2)}) copy-start(bf16[512,1472]{1,0:T(8,128)(2,1)} %fusion.17) | copy-start | bytes 4521988
  767.9 54.2 %collective-permute-start.17 = (bf16[288,768]{1,0:T(8,128)(2,1)}, bf16[288,768]{1,0:T(8,128)(2,1)}, u32[]{:S(2)}, u32[]{:S(2)}) collective-permute-start(bf16[288,768]{1,0:T(8,128)(2,1)} %slice_select_fusion.2), channel_id=1, source_target_pairs={{0,2},{1,3},{2,0},{3,1},{4,6},{5,7},{6,4},{7,5},{8,10},{9,11},{10,... | collective-permute-start | bytes 1327112 | tf_op jit(solution)/shard_map/ppermute | solution.py:475
  784.7 52.9 %collective-permute-start.16 = (bf16[512,768]{1,0:T(8,128)(2,1)}, bf16[512,768]{1,0:T(8,128)(2,1)}, u32[]{:S(2)}, u32[]{:S(2)}) collective-permute-start(bf16[512,768]{1,0:T(8,128)(2,1)} %get-tuple-element.329), channel_id=1, source_target_pairs={{0,1},{1,2},{2,3},{4,5},{5,6},{6,7},{8,9},{9,10},{10,11},{12,13},{... | collective-permute-start | bytes 2359304 | tf_op jit(solution)/shard_map/ppermute | solution.py:467
  786.0 51.6 %collective-permute-start.15 = (bf16[512,768]{1,0:T(8,128)(2,1)S(1)}, bf16[512,768]{1,0:T(8,128)(2,1)}, u32[]{:S(2)}, u32[]{:S(2)}) collective-permute-start(bf16[512,768]{1,0:T(8,128)(2,1)S(1)} %get-tuple-element.330), channel_id=1, source_target_pairs={{1,0},{2,1},{3,2},{5,4},{6,5},{7,6},{9,8},{10,9},{11,10},{13,12},{... | collective-permute-start | bytes 2359304 | tf_op jit(solution)/shard_map/ppermute | solution.py:467
  791.8 25.1 %copy-start.45 = (bf16[1024,1536]{1,0:T(8,128)(2,1)}, bf16[1024,1536]{1,0:T(8,128)(2,1)S(1)}, u32[]{:S(2)}) copy-start(bf16[1024,1536]{1,0:T(8,128)(2,1)S(1)} %fusion.14.refs_2_.refs_3_) | copy-start | bytes 9437188
  791.8 50.1 %collective-permute-start.19 = (bf16[1024,1536]{1,0:T(8,128)(2,1)S(1)}, bf16[1024,1536]{1,0:T(8,128)(2,1)S(1)}, u32[]{:S(2)}, u32[]{:S(2)}) collective-permute-start(bf16[1024,1536]{1,0:T(8,128)(2,1)S(1)} %fusion.14.refs_2_.refs_3_), channel_id=1, source_target_pairs={{0,4},{4,0},{1,5},{5,1},{2,6},{6,2},{3,7},{7,3},{8,12},{12,8},{9,1... | collective-permute-start | bytes 9437192 | tf_op jit(solution)/shard_map/ppermute | solution.py:461
  840.6 3.5 collective-permute-start.18
  862.2 72.5 %collective-permute-start.20 = (bf16[3072,384]{1,0:T(8,128)(2,1)}, bf16[3072,384]{1,0:T(8,128)(2,1)}, u32[]{:S(2)}, u32[]{:S(2)}) collective-permute-start(bf16[3072,384]{1,0:T(8,128)(2,1)} %get-tuple-element.187), channel_id=1, source_target_pairs={{0,16},{16,0},{1,17},{17,1},{2,18},{18,2},{3,19},{19,3},{4,20},{20... | collective-permute-start | bytes 7077896 | tf_op jit(solution)/shard_map/ppermute | solution.py:461
  864.5 71.6 %collective-permute-start.21 = (bf16[3072,384]{1,0:T(8,128)(2,1)}, bf16[3072,384]{1,0:T(8,128)(2,1)}, u32[]{:S(2)}, u32[]{:S(2)}) collective-permute-start(bf16[3072,384]{1,0:T(8,128)(2,1)} %get-tuple-element.189), channel_id=1, source_target_pairs={{0,8},{8,0},{1,9},{9,1},{2,10},{10,2},{3,11},{11,3},{4,12},{12,4},... | collective-permute-start | bytes 7077896 | tf_op jit(solution)/shard_map/ppermute | solution.py:461
  874.1 1.3 collective-permute-start.22
  944.7 33.7 %collective-permute-start.23 = (bf16[1536,384]{1,0:T(8,128)(2,1)}, bf16[1536,384]{1,0:T(8,128)(2,1)}, u32[]{:S(2)}, u32[]{:S(2)}) collective-permute-start(bf16[1536,384]{1,0:T(8,128)(2,1)} %get-tuple-element.198), channel_id=1, source_target_pairs={{0,8},{8,0},{1,9},{9,1},{2,10},{10,2},{3,11},{11,3},{4,12},{12,4},... | collective-permute-start | bytes 3538952 | tf_op jit(solution)/shard_map/ppermute | solution.py:461
  945.9 40.4 %collective-permute-start.24 = (bf16[1536,384]{1,0:T(8,128)(2,1)}, bf16[1536,384]{1,0:T(8,128)(2,1)}, u32[]{:S(2)}, u32[]{:S(2)}) collective-permute-start(bf16[1536,384]{1,0:T(8,128)(2,1)} %get-tuple-element.200), channel_id=1, source_target_pairs={{0,16},{16,0},{1,17},{17,1},{2,18},{18,2},{3,19},{19,3},{4,20},{20... | collective-permute-start | bytes 3538952 | tf_op jit(solution)/shard_map/ppermute | solution.py:461
  947.1 9.2 collective-permute-start.25
  950.8 117.9 %collective-permute-start.30 = (bf16[3072,384]{1,0:T(8,128)(2,1)S(1)}, bf16[3072,384]{1,0:T(8,128)(2,1)S(1)}, u32[]{:S(2)}, u32[]{:S(2)}) collective-permute-start(bf16[3072,384]{1,0:T(8,128)(2,1)S(1)} %copy-done.24), channel_id=1, source_target_pairs={{0,16},{16,0},{1,17},{17,1},{2,18},{18,2},{3,19},{19,3},{4,20},{20... | collective-permute-start | bytes 7077896 | tf_op jit(solution)/shard_map/ppermute | solution.py:461
  951.7 118.1 %collective-permute-start.31 = (bf16[3072,384]{1,0:T(8,128)(2,1)}, bf16[3072,384]{1,0:T(8,128)(2,1)S(1)}, u32[]{:S(2)}, u32[]{:S(2)}) collective-permute-start(bf16[3072,384]{1,0:T(8,128)(2,1)} %copy-done.25), channel_id=1, source_target_pairs={{0,8},{8,0},{1,9},{9,1},{2,10},{10,2},{3,11},{11,3},{4,12},{12,4},... | collective-permute-start | bytes 7077896 | tf_op jit(solution)/shard_map/ppermute | solution.py:461
  989.9 79.8 %copy-start.12 = (bf16[3072,384]{1,0:T(8,128)(2,1)S(1)}, bf16[3072,384]{1,0:T(8,128)(2,1)}, u32[]{:S(2)}) copy-start(bf16[3072,384]{1,0:T(8,128)(2,1)} %copy-done.11) | copy-start | bytes 7077892
  991.1 6.1 collective-permute-start.29
  993.2 20.5 %collective-permute-start.26 = (bf16[384,768]{1,0:T(8,128)(2,1)S(1)}, bf16[384,768]{1,0:T(8,128)(2,1)S(1)}, u32[]{:S(2)}, u32[]{:S(2)}) collective-permute-start(bf16[384,768]{1,0:T(8,128)(2,1)S(1)} %pad_maximum_fusion.7), channel_id=1, source_target_pairs={{0,1},{1,2},{2,3},{3,0},{4,5},{5,6},{6,7},{7,4},{8,9},{9,10},{10,1... | collective-permute-start | bytes 1769480 | tf_op jit(solution)/shard_map/ppermute | solution.py:461
  994.3 74.5 %collective-permute-start.27 = (bf16[384,768]{1,0:T(8,128)(2,1)S(1)}, bf16[384,768]{1,0:T(8,128)(2,1)S(1)}, u32[]{:S(2)}, u32[]{:S(2)}) collective-permute-start(bf16[384,768]{1,0:T(8,128)(2,1)S(1)} %pad_maximum_fusion.8), channel_id=1, source_target_pairs={{0,2},{1,3},{2,0},{3,1},{4,6},{5,7},{6,4},{7,5},{8,10},{9,11},{10,... | collective-permute-start | bytes 1769480 | tf_op jit(solution)/shard_map/ppermute | solution.py:461
  997.3 71.5 %collective-permute-start.28 = (bf16[384,768]{1,0:T(8,128)(2,1)S(1)}, bf16[384,768]{1,0:T(8,128)(2,1)S(1)}, u32[]{:S(2)}, u32[]{:S(2)}) collective-permute-start(bf16[384,768]{1,0:T(8,128)(2,1)S(1)} %pad_maximum_fusion.9), channel_id=1, source_target_pairs={{0,3},{1,0},{2,1},{3,2},{4,7},{5,4},{6,5},{7,6},{8,11},{9,8},{10,9... | collective-permute-start | bytes 1769480 | tf_op jit(solution)/shard_map/ppermute | solution.py:461
  1013.7 55.1 %copy-start.68 = (bf16[384,768]{1,0:T(8,128)(2,1)}, bf16[384,768]{1,0:T(8,128)(2,1)S(1)}, u32[]{:S(2)}) copy-start(bf16[384,768]{1,0:T(8,128)(2,1)S(1)} %collective-permute-done.26) | copy-start | bytes 1769476
  1075.2 19.7 %collective-permute-start.32 = (bf16[1536,384]{1,0:T(8,128)(2,1)}, bf16[1536,384]{1,0:T(8,128)(2,1)}, u32[]{:S(2)}, u32[]{:S(2)}) collective-permute-start(bf16[1536,384]{1,0:T(8,128)(2,1)} %get-tuple-element.232), channel_id=1, source_target_pairs={{0,8},{8,0},{1,9},{9,1},{2,10},{10,2},{3,11},{11,3},{4,12},{12,4},... | collective-permute-start | bytes 3538952 | tf_op jit(solution)/shard_map/ppermute | solution.py:461
  1075.9 19.3 %collective-permute-start.33 = (bf16[1536,384]{1,0:T(8,128)(2,1)}, bf16[1536,384]{1,0:T(8,128)(2,1)}, u32[]{:S(2)}, u32[]{:S(2)}) collective-permute-start(bf16[1536,384]{1,0:T(8,128)(2,1)} %get-tuple-element.234), channel_id=1, source_target_pairs={{0,16},{16,0},{1,17},{17,1},{2,18},{18,2},{3,19},{19,3},{4,20},{20... | collective-permute-start | bytes 3538952 | tf_op jit(solution)/shard_map/ppermute | solution.py:461
  1102.7 15.0 %collective-permute-start.37 = (f32[6,1472]{1,0:T(8,128)S(1)}, f32[6,1472]{1,0:T(8,128)S(1)}, u32[]{:S(2)}, u32[]{:S(2)}) collective-permute-start(f32[6,1472]{1,0:T(8,128)S(1)} %add.408), channel_id=1, source_target_pairs={{0,8},{8,0},{1,9},{9,1},{2,10},{10,2},{3,11},{11,3},{4,12},{12,4},... | collective-permute-start | bytes 105992 | tf_op jit(solution)/shard_map/ppermute | solution.py:550
  1104.1 18.4 %collective-permute-start.34 = (bf16[384,768]{1,0:T(8,128)(2,1)}, bf16[384,768]{1,0:T(8,128)(2,1)}, u32[]{:S(2)}, u32[]{:S(2)}) collective-permute-start(bf16[384,768]{1,0:T(8,128)(2,1)} %pad_maximum_fusion.11), channel_id=1, source_target_pairs={{0,1},{1,2},{2,3},{3,0},{4,5},{5,6},{6,7},{7,4},{8,9},{9,10},{10,1... | collective-permute-start | bytes 1769480 | tf_op jit(solution)/shard_map/ppermute | solution.py:461
  1104.1 57.5 %collective-permute-start.35 = (bf16[384,768]{1,0:T(8,128)(2,1)}, bf16[384,768]{1,0:T(8,128)(2,1)}, u32[]{:S(2)}, u32[]{:S(2)}) collective-permute-start(bf16[384,768]{1,0:T(8,128)(2,1)} %pad_maximum_fusion.12), channel_id=1, source_target_pairs={{0,2},{1,3},{2,0},{3,1},{4,6},{5,7},{6,4},{7,5},{8,10},{9,11},{10,... | collective-permute-start | bytes 1769480 | tf_op jit(solution)/shard_map/ppermute | solution.py:461
  1112.4 49.3 %collective-permute-start.36 = (bf16[384,768]{1,0:T(8,128)(2,1)}, bf16[384,768]{1,0:T(8,128)(2,1)}, u32[]{:S(2)}, u32[]{:S(2)}) collective-permute-start(bf16[384,768]{1,0:T(8,128)(2,1)} %pad_maximum_fusion.13), channel_id=1, source_target_pairs={{0,3},{1,0},{2,1},{3,2},{4,7},{5,4},{6,5},{7,6},{8,11},{9,8},{10,9... | collective-permute-start | bytes 1769480 | tf_op jit(solution)/shard_map/ppermute | solution.py:461
  1117.6 44.0 %copy-start.65 = (bf16[384,768]{1,0:T(8,128)(2,1)S(1)}, bf16[384,768]{1,0:T(8,128)(2,1)}, u32[]{:S(2)}) copy-start(bf16[384,768]{1,0:T(8,128)(2,1)} %pad_maximum_fusion.10) | copy-start | bytes 1769476
  1117.7 4.2 collective-permute-start.38
  (80 other events, 534.6 us)
Sparse Core Ops, SparseCore 0:
  11.4 213.9 all-gather.2
  228.8 234.2 all-gather.4
  693.2 373.7 reduce-scatter.1

commit v9 on v8

--- a/solution.py
+++ b/solution.py
@@ -735,41 +735,20 @@
     )
 
 
-def weight_grads_body(tail, tile, place_ref, *refs):
+def weight_grads_body(chunks, tile, place_ref, *refs):
     own_ref, other_ref, normed_ref, branch_ref, other_normed_ref, other_branch_ref = refs[:6]
-    refs = refs[6:]
+    stage_ref, sems = refs[-2:]
     step = pl.program_id(0)
     unit = place_ref[3]
     at = (step // unit * 2 + place_ref[2]) * unit + step % unit
     first, second = 4 * INNER // tile, (4 * INNER + 2 * FF) // tile
     slot = step % 2
-    if tail:
-        stage_ref, sems = refs[-2:]
-        places = split_places(refs[:-2])
-
-    def copy(chunk, place, row, where):
-        source = stage_ref.at[where, :, chunk * CHUNK : (chunk + 1) * CHUNK]
-        spot = pl.ds(pl.multiple_of(row * tile, tile), tile)
-        return pltpu.make_async_copy(source, place.at[spot, :], sems.at[where, chunk])
-
-    def wait(where):
-        for chunk in range(4):
-            copy(chunk, places[chunk % 2][0][chunk // 2], 0, where).wait()
+    places = split_places(refs[6:-2], chunks)
+    start, wait = place_copies(chunks, stage_ref, sems, places, tile)
 
     def put(product):
-        if not tail:
-            refs[0][:, : CUTS[-1]] = product.astype(jnp.bfloat16)
-            refs[0][:, CUTS[-1] :] = jnp.zeros((tile, PADDED - CUTS[-1]), jnp.bfloat16)
-            return
         stage_ref[slot, :, : CUTS[-1]] = product.astype(jnp.bfloat16)
-        spots = spots_of(step // unit, place_ref)
-        for chunk in range(4):
-            which, position = spots[chunk % 2]
-            for k, pair in enumerate(places[chunk % 2]):
-
-                @pl.when(which == k)
-                def _(chunk=chunk, place=pair[chunk // 2], row=position * unit + step % unit):
-                    copy(chunk, place, row, slot).start()
+        start(spots_of(step // unit, place_ref), unit, step % unit, step, slot)
 
     def both(side_ref, other_side_ref):
         return jnp.dot(
@@ -778,15 +757,13 @@
             other_ref[...], other_side_ref[:, : CUTS[-1]], preferred_element_type=jnp.float32
         )
 
-    if tail:
-
-        @pl.when(step < 2)
-        def _():
-            stage_ref[slot, :, CUTS[-1] :] = jnp.zeros((tile, PADDED - CUTS[-1]), jnp.bfloat16)
-
-        @pl.when(step >= 2)
-        def _():
-            wait(slot)
+    @pl.when(step < 2)
+    def _():
+        stage_ref[slot, :, CUTS[-1] :] = jnp.zeros((tile, PADDED - CUTS[-1]), jnp.bfloat16)
+
+    @pl.when(step >= 2)
+    def _():
+        wait(slot)
 
     @pl.when(at < first)
     def _():
@@ -800,19 +777,60 @@
     def _():
         put(both(branch_ref, other_branch_ref))
 
-    if tail:
-
-        @pl.when(step == pl.num_programs(0) - 1)
-        def _():
-            wait(0)
-            wait(1)
-
-
-def split_places(refs):
-    size_y, size_x = lax.axis_size("y"), lax.axis_size("x")
-    along_y = [refs[2 * k : 2 * k + 2] for k in range(size_y)]
-    along_x = [refs[2 * size_y + 2 * k : 2 * size_y + 2 * k + 2] for k in range(size_x)]
-    return along_y, along_x
+    @pl.when(step == pl.num_programs(0) - 1)
+    def _():
+        wait(0)
+        wait(1)
+
+
+def split_places(refs, chunks):
+    size_y, size_x, per = lax.axis_size("y"), lax.axis_size("x"), chunks // 2
+    refs = list(refs)
+    along_y = [refs[per * k : per * (k + 1)] for k in range(size_y)]
+    refs = refs[per * size_y :]
+    along_x = [refs[per * k : per * (k + 1)] for k in range(size_x)]
+    return along_y, along_x, refs[per * size_x :]
+
+
+def array_shapes(chunks, rows):
+    shapes = [(rows // lax.axis_size("y"), CHUNK)] * (chunks // 2 * lax.axis_size("y"))
+    shapes += [(rows // lax.axis_size("x"), CHUNK)] * (chunks // 2 * lax.axis_size("x"))
+    if chunks < 4:
+        shapes.append((rows, PADDED - chunks * CHUNK))
+    return [jax.ShapeDtypeStruct(shape, jnp.bfloat16) for shape in shapes]
+
+
+def place_copies(chunks, stage_ref, sems, places, tile):
+    along = places[:2]
+    rest = places[2]
+
+    def copy(lane, place, row, where):
+        start = lane * CHUNK
+        end = PADDED if lane == chunks else start + CHUNK
+        spot = pl.ds(pl.multiple_of(row * tile, tile), tile)
+        return pltpu.make_async_copy(
+            stage_ref.at[where, :, start:end], place.at[spot, :], sems.at[where, lane]
+        )
+
+    def start(spots, unit, inside, row, where):
+        for chunk in range(chunks):
+            which, position = spots[chunk % 2]
+            for k, group in enumerate(along[chunk % 2]):
+
+                @pl.when(which == k)
+                def _(chunk=chunk, place=group[chunk // 2], at=position * unit + inside):
+                    copy(chunk, place, at, where).start()
+
+        for place in rest:
+            copy(chunks, place, row, where).start()
+
+    def wait(where):
+        for chunk in range(chunks):
+            copy(chunk, along[chunk % 2][0][chunk // 2], 0, where).wait()
+        for place in rest:
+            copy(chunks, place, 0, where).wait()
+
+    return start, wait
 
 
 def place_of(tile):
@@ -834,30 +852,23 @@
     )
 
 
-def weight_grads(tail, own, other, sides):
+def weight_grads(chunks, own, other, sides):
     rows, tokens = own.shape
     tile = 512 if unit_tiles(256) % 2 == 0 else 256
-    steps = rows // tile
     source = pl.BlockSpec((tile, tokens), lambda i, *_: (i, 0))
     halves = [half_side(tokens, 0), half_side(tokens, 1)]
-    scratch = []
-    if tail:
-        sizes = [lax.axis_size("y")] * 2 * lax.axis_size("y")
-        sizes += [lax.axis_size("x")] * 2 * lax.axis_size("x")
-        out_specs = [pl.BlockSpec(memory_space=pl.ANY)] * len(sizes)
-        out_shape = [jax.ShapeDtypeStruct((rows // n, CHUNK), jnp.bfloat16) for n in sizes]
-        scratch = [pltpu.VMEM((2, tile, PADDED), jnp.bfloat16), pltpu.SemaphoreType.DMA((2, 4))]
-    else:
-        out_specs = [pl.BlockSpec((tile, PADDED), lambda i, *_: (i, 0))]
-        out_shape = [jax.ShapeDtypeStruct((rows, PADDED), jnp.bfloat16)]
+    out_shape = array_shapes(chunks, rows)
     return pl.pallas_call(
-        functools.partial(weight_grads_body, tail, tile),
+        functools.partial(weight_grads_body, chunks, tile),
         grid_spec=pltpu.PrefetchScalarGridSpec(
             num_scalar_prefetch=1,
-            grid=(steps,),
+            grid=(rows // tile,),
             in_specs=[source, source] + halves * 2,
-            out_specs=out_specs,
-            scratch_shapes=scratch,
+            out_specs=[pl.BlockSpec(memory_space=pl.ANY)] * len(out_shape),
+            scratch_shapes=[
+                pltpu.VMEM((2, tile, PADDED), jnp.bfloat16),
+                pltpu.SemaphoreType.DMA((2, 5)),
+            ],
         ),
         out_shape=out_shape,
         compiler_params=pltpu.CompilerParams(vmem_limit_bytes=40 << 20),
@@ -870,26 +881,14 @@
     )(place_of(tile), own, other, sides[0], sides[0], sides[1], sides[1])
 
 
-def attention_fill_body(tail, owners, place_ref, *refs):
+def attention_fill_body(chunks, owners, place_ref, *refs):
     own_ref, other_ref, first_ref, second_ref, other_first_ref, other_second_ref = refs[:6]
     outs = refs[6 + (len(refs) - 8) // 2 : -2]
     stage_ref, sems = refs[-2:]
     step = pl.program_id(0)
     slot = step % 2
     tile = jnp.minimum(place_ref[2], owners - 1) * pl.num_programs(0) + step
-
-    def copy(chunk, place, row, where):
-        width = CHUNK if tail else PADDED
-        source = stage_ref.at[where, :, chunk * width : (chunk + 1) * width]
-        spot = pl.ds(pl.multiple_of(row * INNER, INNER), INNER)
-        return pltpu.make_async_copy(source, place.at[spot, :], sems.at[where, chunk])
-
-    places = split_places(outs) if tail else None
-
-    def wait(where):
-        for chunk in range(4 if tail else 1):
-            place = places[chunk % 2][0][chunk // 2] if tail else outs[0]
-            copy(chunk, place, 0, where).wait()
+    start, wait = place_copies(chunks, stage_ref, sems, split_places(outs, chunks), INNER)
 
     def put(side_ref, other_side_ref):
         product = jnp.dot(
@@ -899,17 +898,7 @@
         )
         stage_ref[slot, :, : CUTS[-1]] = product.astype(jnp.bfloat16)
         stage_ref[slot, :, CUTS[-1] :] = jnp.zeros((INNER, PADDED - CUTS[-1]), jnp.bfloat16)
-        if not tail:
-            copy(0, outs[0], step, slot).start()
-            return
-        spots = spots_of(0, place_ref)
-        for chunk in range(4):
-            which, _ = spots[chunk % 2]
-            for k, pair in enumerate(places[chunk % 2]):
-
-                @pl.when(which == k)
-                def _(chunk=chunk, place=pair[chunk // 2]):
-                    copy(chunk, place, step, slot).start()
+        start(spots_of(0, place_ref), 0, step, step, slot)
 
     @pl.when(place_ref[2] < owners)
     def _():
@@ -931,7 +920,7 @@
             wait(1)
 
 
-def attention_fill(tail, arrays, own, other, sides):
+def attention_fill(chunks, arrays, own, other, sides):
     tokens = own.shape[0]
     unit_rows = unit_tiles(TILE) * TILE
     owners = 4 * INNER // unit_rows
@@ -943,7 +932,7 @@
     halves = [half_side(tokens, 0), half_side(tokens, 1)]
     anywhere = pl.BlockSpec(memory_space=pl.ANY)
     return pl.pallas_call(
-        functools.partial(attention_fill_body, tail, owners),
+        functools.partial(attention_fill_body, chunks, owners),
         grid_spec=pltpu.PrefetchScalarGridSpec(
             num_scalar_prefetch=1,
             grid=(steps,),
@@ -953,7 +942,7 @@
             out_specs=[anywhere] * len(arrays),
             scratch_shapes=[
                 pltpu.VMEM((2, INNER, PADDED), jnp.bfloat16),
-                pltpu.SemaphoreType.DMA((2, 4)),
+                pltpu.SemaphoreType.DMA((2, 5)),
             ],
         ),
         out_shape=[jax.ShapeDtypeStruct(array.shape, array.dtype) for array in arrays],
@@ -979,14 +968,10 @@
     def push(self, name, route, kept, sends):
         self.waiting[name] = (route, kept, sends)
 
-    def step(self, values, *names):
-        arrays = {name: self.flying[name][1:] for name in names if name in self.flying}
-        arrays, values = tied(arrays, values)
+    def settle(self, values, *names):
+        arrays, values = tied({name: self.flying[name][1:] for name in names}, values)
         moves = {}
         for name in names:
-            if name in self.waiting:
-                moves[name] = self.waiting.pop(name)
-                continue
             route = self.flying.pop(name)[0]
             kept, moved = arrays[name]
             if not route:
@@ -1006,9 +991,20 @@
             moves = {tuple(moves): (("z",), kept, sends)}
         arrays, values = tied({name: move[1:] for name, move in moves.items()}, values)
         for name, (route, *_) in moves.items():
+            self.waiting[name] = (route,) + tuple(arrays[name])
+        return values
+
+    def start(self, values, *names):
+        arrays, values = tied({name: self.waiting[name][1:] for name in names}, values)
+        for name in names:
+            route = self.waiting.pop(name)[0]
             kept, sends = arrays[name]
             self.flying[name] = (route[1:], kept, stage_moves(sends, route[0]))
         return values
+
+    def step(self, values, *names):
+        values = self.settle(values, *(name for name in names if name in self.flying))
+        return self.start(values, *self.waiting) if self.waiting else values
 
 
 def total_of(value, moved):
@@ -1053,7 +1049,7 @@
     return (result, kept)
 
 
-def layer_backward(grad_out, kept, gathered, gain_one, gain_two, context, tail):
+def layer_backward(grad_out, kept, gathered, gain_one, gain_two, context, before):
     (
         stream,
         inverse_one,
@@ -1076,6 +1072,9 @@
     grad_normed_two, own, sent = ffn_backward(
         branch_low, normed_two_low, up_gelu, up_linear, gathered
     )
+    if before is not None:
+        grad_normed_two, own, sent = before.settle((grad_normed_two, own, sent), 0, 1)
+        grad_normed_two, own, sent = before.start((grad_normed_two, own, sent), 0, 1)
     other = shift(sent, "c", 1)
     grad_middle, grad_gain_two = rms_backward(middle, inverse_two, gain_two, grad_normed_two)
     grad_middle = grad_out + grad_middle
@@ -1087,32 +1086,37 @@
     grad_query, grad_shared, grad_table = attend_backward(
         queries, grad_mixed, shared, log_total, context
     )
+    if before is not None:
+        grad_query, grad_shared = before.settle((grad_query, grad_shared), 0, 1)
     grad_shared, own = lax.optimization_barrier((grad_shared, own))
     moving = start_back(grad_shared, tokens)
-    arrays = weight_grads(tail, own, other, sides)
+    chunks = 2 if before is None else 4
+    arrays = weight_grads(chunks, own, other, sides)
     arrays, moving = lax.optimization_barrier((arrays, moving))
+    if before is not None:
+        arrays, moving = before.start((arrays, moving), (0, 1))
     grad_own = finish_back(*moving)
     grad_gate = grad_own[:, 2 * INNER :]
     grad_input_low = jnp.concatenate(
         [grad_query, grad_own[:, : 2 * INNER].astype(jnp.bfloat16)], axis=1
     )
     late = jnp.concatenate([grad_input_low, attended], axis=1)
-    arrays = attention_fill(tail, arrays, late, shift(late, "c", 1), late_sides)
-    if tail:
-        scatter = Scatter()
-        for chunk in range(4):
-            route = ("y", "x", "z") if chunk % 2 == 0 else ("x", "y", "z")
-            ordered = [pair[chunk // 2] for pair in split_places(arrays)[chunk % 2]]
-            scatter.push(chunk, route, ordered[-1], ordered[:-1])
-        grad_input_low = scatter.step(grad_input_low, 0, 1)
-    else:
-        arrays, grad_input_low, grad_gate = lax.optimization_barrier(
-            (arrays, grad_input_low, grad_gate)
+    arrays = attention_fill(chunks, arrays, late, shift(late, "c", 1), late_sides)
+    scatter = Scatter()
+    along_y, along_x, rest = split_places(arrays, chunks)
+    for chunk in range(chunks):
+        route = ("y", "x", "z") if chunk % 2 == 0 else ("x", "y", "z")
+        ordered = [group[chunk // 2] for group in (along_y, along_x)[chunk % 2]]
+        scatter.push(chunk, route, ordered[-1], ordered[:-1])
+    grad_input_low, grad_gate = scatter.start((grad_input_low, grad_gate), 0, 1)
+    if rest:
+        grad_input_low, grad_gate, rest = lax.optimization_barrier(
+            (grad_input_low, grad_gate, rest)
         )
-        scatter = lax.psum_scatter(arrays[0], ("y", "x", "z"), scatter_dimension=0, tiled=True)
+        rest = lax.psum_scatter(rest[0], ("y", "x", "z"), scatter_dimension=0, tiled=True)
     grad_normed = times_plain(grad_input_low, gathered[: 3 * INNER])
     grad_stream, grad_gain_one = rms_backward(stream, inverse_one, gain_one, grad_normed)
-    return (grad_middle + grad_stream, grad_table, grad_gate, grad_gain_one, grad_gain_two, scatter)
+    return (grad_middle + grad_stream, grad_table, grad_gate, grad_gain_one, grad_gain_two, scatter, rest)
 
 
 def per_device(
@@ -1136,7 +1140,7 @@
     after_four, kept_four = layer_forward(
         after_three, gathered_four, norm_gains[2], norm_gains[3], gate_low, context
     )
-    grad_three_out, table_four, grad_gate, gain_four_one, gain_four_two, local_four = (
+    grad_three_out, table_four, grad_gate, gain_four_one, gain_four_two, before, rest = (
         layer_backward(
             cotangent.reshape(tokens_here, width),
             kept_four,
@@ -1144,43 +1148,46 @@
             norm_gains[2],
             norm_gains[3],
             context,
-            False,
+            None,
         )
     )
     grad_logit = grad_gate[:, 0] * gate_scale * sigmoid_value * (1.0 - sigmoid_value)
     grad_gate_weight = jnp.sum(grad_logit[:, None] * gate_normed, axis=0)
     gate_stream = stream_backward(after_three, gate_inverse, grad_logit[:, None] * gate_weight)
-    grad_input, table_three, unused, gain_three_one, gain_three_two, scatter = layer_backward(
+    grad_input, table_three, unused, gain_three_one, gain_three_two, scatter, _ = layer_backward(
         grad_three_out + gate_stream,
         kept_three,
         gathered_three,
         norm_gains[0],
         norm_gains[1],
         context,
-        True,
+        before,
     )
     table = jnp.pad((table_three + table_four).reshape(1, -1), ((0, 0), (0, width - 6 * BUCKETS)))
     small_sums = jnp.stack(
         [gain_three_one, gain_three_two, gain_four_one, gain_four_two, grad_gate_weight, table[0]]
     )
     small = hop(small_sums, "c")
-    small = scatter.step(small, 0, 1)
-    small = scatter.step(small, 2, 3)
+    small, rest = before.settle((small, rest), (0, 1))
+    small = scatter.settle(small, 0, 1)
+    small = scatter.start(small, 0, 1)
+    small = scatter.start(small, 2, 3)
     small = hop(small, "z", 1)
     small = scatter.step(small, 0, 1)
     for bit in range(2, lax.axis_size("z")):
         if bit & (bit - 1) == 0:
             small = hop(small, "z", bit)
-    small = scatter.step(small, (0, 1))
+    small = scatter.settle(small, (0, 1))
     small = scatter.step(small, 2, 3)
     small = scatter.step(small, 2, 3)
     small = hop(small, "x")
     for bit in range(1, lax.axis_size("y")):
         if bit & (bit - 1) == 0:
             small = hop(small, "y", bit)
-    summed = scatter.step(small, (2, 3))
+    summed = scatter.settle(small, (2, 3))
     local_three = jnp.concatenate([scatter.results[pair] for pair in ((0, 1), (2, 3))], axis=1)
-    local_three, local_four = local_three[:, :width], local_four[:, :width].astype(jnp.float32)
+    local_four = jnp.concatenate([before.results[(0, 1)], rest.astype(jnp.float32)], axis=1)
+    local_three, local_four = local_three[:, :width], local_four[:, :width]
     return (
         after_four.reshape(inputs.shape),
         gate_mask.reshape(seqs_here, tokens_here),

time: 1180 us -> 1200 us (1.017)
  local copies, waits for them, and re-layouts: 62.6 us -> 86.1 us
  starting transfers between devices: 106 us -> 87.8 us
  other arithmetic: 72.2 us -> 84.5 us
    unnamed x219 -> x265, local copies, waits for them, and re-layouts: 41.8 us -> 59.8 us
    ppermute x22 -> x29, starting transfers between devices: 44.7 us -> 33.2 us  [shift(): lax.ppermute(value, axis, [(i, (i + amount) % count) for i in range(count)])]
    ppermute x22 -> x29, waiting for transfers between devices: 203 us -> 206 us  [shift(): lax.ppermute(value, axis, [(i, (i + amount) % count) for i in range(count)])]
  transfers between devices with their start and end apart: 42 -> 49, of which waited for: 23 -> 23; matrix products, arithmetic and copies ran while one was open for 11% -> 11% of each run, Pallas kernels for 14% -> 14%
where the time goes in v9:
time: 1200 us
  waiting for transfers between devices  648 us (54%)
  Pallas kernels  247 us (21%)
  starting transfers between devices  87.8 us (7%)
  local copies, waits for them, and re-layouts  86.1 us (7%)
  other arithmetic  84.5 us (7%)
  matrix products  34.1 us (3%)
  between operations  15.6 us (1%)
    all_gather x2, waiting for transfers between devices, fetch_rows(): return lax.all_gather(local_rows, DEVICES, axis=0, tiled=True)  340 us
    ppermute x29, waiting for transfers between devices, shift(): lax.ppermute(value, axis, [(i, (i + amount) % count) for i in range(count)])  206 us
    pallas_call x2, Pallas kernels, ffn_backward(): pl.pallas_call(ffn_backward_body, grid_spec=pltpu.PrefetchScalarGridSpec(...  64.9 us
    ppermute x4, waiting for transfers between devices, far_pair(): got = lax.ppermute(sent, 'z', pairs)  64.2 us
    unnamed x265, local copies, waits for them, and re-layouts  59.8 us
    pallas_call x2, Pallas kernels, ffn_forward(): pl.pallas_call(ffn_forward_body, grid=(steps,), in_specs=[resident((token...  49.4 us
    pallas_call x2, Pallas kernels, weight_grads(): pl.pallas_call(functools.partial(weight_grads_body, chunks, tile), grid_s...  48.2 us
    pallas_call x2, Pallas kernels, attend_backward(): pl.pallas_call(functools.partial(backward_body, width > 2 * INNER), grid_...  43.8 us
  transfers between devices with their start and end apart: 49, of which 23 were waited for; matrix products, arithmetic and copies ran while one was open for 11% of the time, Pallas kernels for 14%

profile of v9, /device:TPU:24, one launch (start us, length us, event | category | flops | bytes accessed | tf_op | source)
XLA Modules:
  0.0 1202.3 jit_solution(2063677658792887326)
XLA Ops:
  7.2 2.5 copy.117
  12.0 2.4 copy.116
  17.5 207.9 %all-gather.3.cloned.1.call-done.gelu_ref.linear_ref.down_ref.refs_4_.refs_5_.refs_6_ = bf16[12288,1472]{1,0:T(8,128)(2,1)} async-done(((bf16[384,1472]{1,0:T(8,128)(2,1)}), bf16[12288,1472]{1,0:T(8,128)(2,1)}) %all-gather.3.cloned.1.call-update) | async-done | bytes 36175888 | tf_op jit(solution)/shard_map/all_gather | solution.py:1018
  225.4 4.7 fusion.33
  234.4 6.1 collective-permute-start.2
  241.2 4.7 bias_tiles.1.refs_4_.refs_5_
  246.0 3.5 copy.122
  250.6 22.5 %collective-permute-done = bf16[288,768]{1,0:T(8,128)(2,1)} collective-permute-done((bf16[288,768]{1,0:T(8,128)(2,1)}, bf16[288,768]{1,0:T(8,128)(2,1)}, u32[]{:S(2)}, u32[]{:S(2)}) %collective-permute-start) | collective-permute-done | bytes 442400 | tf_op jit(solution)/shard_map/ppermute | solution.py:475
  274.2 14.3 %collective-permute-done.1 = bf16[512,768]{1,0:T(8,128)(2,1)} collective-permute-done((bf16[512,768]{1,0:T(8,128)(2,1)}, bf16[512,768]{1,0:T(8,128)(2,1)}, u32[]{:S(2)}, u32[]{:S(2)}) %collective-permute-start.1) | collective-permute-done | bytes 786464 | tf_op jit(solution)/shard_map/ppermute | solution.py:467
  291.6 7.4 attend_forward.2
  299.0 2.5 multiply_reduce_fusion.10
  303.1 24.8 %ffn_forward.2 = (f32[512,1472]{1,0:T(8,128)S(1)}, f32[512,3584]{1,0:T(8,128)}, f32[512,3584]{1,0:T(8,128)}) custom-call(bf16[512,1472]{1,0:T(8,128)(2,1)S(1)} %multiply_convert_fusion.2.normed_ref.refs_1_, f32[512,1472]{1,0:T(8,128)} %copy-done.51, bf16[12288,1472]{1,0:T(8,128)(2,1)} %all-gather.3.cloned.1.call-done.gelu_ref.linear_ref.down_ref.refs_4_.refs_5_.refs_6_, ...), custom_call_target="tpu_custom_call" | custom-call | flops 16206790656 | bytes 46333952 | tf_op jit(solution)/shard_map/ffn_forward/pallas_call | solution.py:602
  331.1 131.9 %all-gather.5.cloned.1.call-done.gelu_ref.linear_ref.down_ref.refs_4_.refs_5_.refs_6_ = bf16[12288,1472]{1,0:T(8,128)(2,1)} async-done(((bf16[384,1472]{1,0:T(8,128)(2,1)}), bf16[12288,1472]{1,0:T(8,128)(2,1)}) %all-gather.5.cloned.1.call-update) | async-done | bytes 36175888 | tf_op jit(solution)/shard_map/all_gather | solution.py:1018
  463.0 4.7 fusion.36
  469.9 4.6 collective-permute-start.5
  480.6 39.3 %collective-permute-done.3 = bf16[288,896]{1,0:T(8,128)(2,1)} collective-permute-done((bf16[288,896]{1,0:T(8,128)(2,1)}, bf16[288,896]{1,0:T(8,128)(2,1)}, u32[]{:S(2)}, u32[]{:S(2)}) %collective-permute-start.3) | collective-permute-done | bytes 516128 | tf_op jit(solution)/shard_map/ppermute | solution.py:475
  524.5 7.4 attend_forward.3
  532.0 2.4 multiply_reduce_fusion.7
  536.3 24.6 %ffn_forward.3 = (f32[512,1472]{1,0:T(8,128)S(1)}, f32[512,3584]{1,0:T(8,128)}, f32[512,3584]{1,0:T(8,128)}) custom-call(bf16[512,1472]{1,0:T(8,128)(2,1)S(1)} %multiply_convert_fusion.normed_ref.refs_1_, f32[512,1472]{1,0:T(8,128)} %copy-done.53, bf16[12288,1472]{1,0:T(8,128)(2,1)} %all-gather.5.cloned.1.call-done.gelu_ref.linear_ref.down_ref.refs_4_.refs_5_.refs_6_, ...), custom_call_target="tpu_custom_call" | custom-call | flops 16206790656 | bytes 46333952 | tf_op jit(solution)/shard_map/ffn_forward/pallas_call | solution.py:602
  562.5 32.2 %ffn_backward.2 = (f32[512,1472]{1,0:T(8,128)}, bf16[6144,512]{1,0:T(8,128)(2,1)}, bf16[6144,512]{1,0:T(8,128)(2,1)}) custom-call(s32[2]{0:T(128)} %pad_add_fusion.core_ref, bf16[512,1472]{1,0:T(8,128)(2,1)} %bitcast_convert_fusion.refs_0_, bf16[512,1472]{1,0:T(8,128)(2,1)} %copy-done.2, f32[512,3584]{1,0:T(8,128)} %get-tuple-element.204.refs_2_, ...), custom_call_target="tpu_custom_call" | custom-call | flops 16206790656 | bytes 57344000 | tf_op jit(solution)/shard_map/ffn_backward/pallas_call | solution.py:705
  596.1 2.3 fusion.11.refs_2_.refs_3_
  599.9 2.3 multiply_reduce_fusion.1
  602.2 2.4 fusion.51
  604.6 2.9 convolution_convert_fusion.1.refs_1_
  607.5 22.3 %attend_backward.2 = (bf16[512,384]{1,0:T(8,128)(2,1)S(1)}, bf16[2304,896]{1,0:T(8,128)(2,1)}, f32[3,32,256]{2,1,0:T(8,128)S(1)}) custom-call(s32[4]{0:T(128)S(1)} %get-tuple-element.533.low_ref, s32[4]{0:T(128)S(1)} %get-tuple-element.532.high_ref, bf16[512,384]{1,0:T(8,128)(2,1)S(1)} %copy-done.39, bf16[512,384]{1,0:T(8,128)(2,1)S(1)} %convolution_convert_fusion.1.refs_1_, ...), custom_call_target="tpu_custom_call" | custom-call | flops 4529848320 | bytes 12582912 | tf_op jit(solution)/shard_map/attend_backward/pallas_call | solution.py:367
  631.3 19.8 %collective-permute-start.10 = (bf16[288,896]{1,0:T(8,128)(2,1)S(1)}, bf16[288,896]{1,0:T(8,128)(2,1)S(1)}, u32[]{:S(2)}, u32[]{:S(2)}) collective-permute-start(bf16[288,896]{1,0:T(8,128)(2,1)S(1)} %slice_select_fusion), channel_id=1, source_target_pairs={{0,2},{1,3},{2,0},{3,1},{4,6},{5,7},{6,4},{7,5},{8,10},{9,11},{10,... | collective-permute-start | bytes 1548296 | tf_op jit(solution)/shard_map/ppermute | solution.py:475
  654.4 4.6 collective-permute-start.8
  661.0 23.8 %weight_grads.2 = (bf16[3072,384]{1,0:T(8,128)(2,1)S(1)}, bf16[3072,384]{1,0:T(8,128)(2,1)S(1)}, bf16[3072,384]{1,0:T(8,128)(2,1)S(1)}, bf16[3072,384]{1,0:T(8,128)(2,1)S(1)}, bf16[6144,768]{1,0:T(8,128)(2,1)}) custom-call(s32[6]{0:T(128)S(1)} %stack.55.place_ref, bf16[6144,512]{1,0:T(8,128)(2,1)} %get-tuple-element.211.refs_0_, ...), custom_call_target="tpu_custom_call" | custom-call | flops 18522046464 | bytes 31457280 | tf_op jit(solution)/shard_map/weight_grads/pallas_call | solution.py:861
  691.2 4.1 collective-permute-start.11
  697.6 2.5 pad_maximum_fusion.5
  705.1 10.7 attention_fill.2
  723.6 5.5 multiply_reduce_fusion.2
  729.1 3.0 fusion.49
  732.1 32.7 %ffn_backward.3 = (f32[512,1472]{1,0:T(8,128)}, bf16[6144,512]{1,0:T(8,128)(2,1)}, bf16[6144,512]{1,0:T(8,128)(2,1)}) custom-call(s32[2]{0:T(128)} %pad_add_fusion.core_ref, bf16[512,1472]{1,0:T(8,128)(2,1)} %get-tuple-element.460.refs_0_, bf16[512,1472]{1,0:T(8,128)(2,1)} %copy-done, f32[512,3584]{1,0:T(8,128)} %get-tuple-element.241.refs_2_, ...), custom_call_target="tpu_custom_call" | custom-call | flops 16206790656 | bytes 57344000 | tf_op jit(solution)/shard_map/ffn_backward/pallas_call | solution.py:705
  764.8 21.6 %collective-permute-done.13 = bf16[3072,384]{1,0:T(8,128)(2,1)} collective-permute-done((bf16[3072,384]{1,0:T(8,128)(2,1)}, bf16[3072,384]{1,0:T(8,128)(2,1)}, u32[]{:S(2)}, u32[]{:S(2)}) %collective-permute-start.13) | collective-permute-done | bytes 2359328 | tf_op jit(solution)/shard_map/ppermute | solution.py:461
  787.8 2.3 add_convert_fusion.5
  802.1 2.4 fusion.48
  804.9 3.5 convolution_convert_fusion.refs_1_
  808.5 21.5 %attend_backward.3 = (bf16[512,384]{1,0:T(8,128)(2,1)S(1)}, bf16[2304,768]{1,0:T(8,128)(2,1)}, f32[3,32,256]{2,1,0:T(8,128)S(1)}) custom-call(s32[4]{0:T(128)S(1)} %get-tuple-element.533.low_ref, s32[4]{0:T(128)S(1)} %get-tuple-element.532.high_ref, bf16[512,384]{1,0:T(8,128)(2,1)S(1)} %copy-done.42, bf16[512,384]{1,0:T(8,128)(2,1)S(1)} %convolution_convert_fusion.refs_1_, ...), custom_call_target="tpu_custom_call" | custom-call | flops 4529848320 | bytes 12582912 | tf_op jit(solution)/shard_map/attend_backward/pallas_call | solution.py:367
  829.9 8.5 collective-permute-done.15
  846.1 5.0 collective-permute-start.21
  853.4 5.5 collective-permute-start.19
  858.9 24.4 %weight_grads.3 = (bf16[3072,384]{1,0:T(8,128)(2,1)}, bf16[3072,384]{1,0:T(8,128)(2,1)}, bf16[3072,384]{1,0:T(8,128)(2,1)S(1)}, bf16[3072,384]{1,0:T(8,128)(2,1)...) custom-call(s32[6]{0:T(128)S(1)} %stack.55.place_ref, ...), custom_call_target="tpu_custom_call" | custom-call | flops 18522046464 | bytes 31457280 | tf_op jit(solution)/shard_map/weight_grads/pallas_call | solution.py:861
  883.3 2.4 collective-permute-done.21
  885.8 17.4 %collective-permute-done.20 = bf16[512,768]{1,0:T(8,128)(2,1)S(1)} collective-permute-done((bf16[512,768]{1,0:T(8,128)(2,1)}, bf16[512,768]{1,0:T(8,128)(2,1)S(1)}, u32[]{:S(2)}, u32[]{:S(2)}) %collective-permute-start.20) | collective-permute-done | bytes 786464 | tf_op jit(solution)/shard_map/ppermute | solution.py:467
  910.4 10.2 attention_fill.3
  930.4 8.0 fusion.24
  941.3 7.8 collective-permute-start.27
  950.7 11.2 collective-permute-done.26
  962.0 39.1 %collective-permute-done.27 = bf16[384,768]{1,0:T(8,128)(2,1)} collective-permute-done((bf16[384,768]{1,0:T(8,128)(2,1)S(1)}, bf16[384,768]{1,0:T(8,128)(2,1)}, u32[]{:S(2)}, u32[]{:S(2)}) %collective-permute-start.27) | collective-permute-done | bytes 589856 | tf_op jit(solution)/shard_map/ppermute | solution.py:461
  1001.1 2.3 add_convert_fusion.3
  1005.0 2.3 add_convert_fusion.2
  1013.1 23.4 %collective-permute-done.30 = bf16[1536,384]{1,0:T(8,128)(2,1)S(1)} collective-permute-done((bf16[1536,384]{1,0:T(8,128)(2,1)S(1)}, bf16[1536,384]{1,0:T(8,128)(2,1)S(1)}, u32[]{:S(2)}, u32[]{:S(2)}) %collective-permute-start.30) | collective-permute-done | bytes 1179680 | tf_op jit(solution)/shard_map/ppermute | solution.py:461
  1041.7 2.9 collective-permute-start.34
  1044.6 2.6 collective-permute-done.36
  1047.9 3.6 copy.131
  1053.0 3.7 collective-permute-done.33
  1056.7 37.0 %collective-permute-done.34 = bf16[384,768]{1,0:T(8,128)(2,1)S(1)} collective-permute-done((bf16[384,768]{1,0:T(8,128)(2,1)}, bf16[384,768]{1,0:T(8,128)(2,1)S(1)}, u32[]{:S(2)}, u32[]{:S(2)}) %collective-permute-start.34) | collective-permute-done | bytes 589856 | tf_op jit(solution)/shard_map/ppermute | solution.py:461
  1093.8 2.5 add_convert_fusion.1
  1098.8 2.4 add_convert_fusion
  1105.4 2.3 copy.132
  1110.8 16.3 %collective-permute-done.39 = bf16[1536,384]{1,0:T(8,128)(2,1)} collective-permute-done((bf16[1536,384]{1,0:T(8,128)(2,1)}, bf16[1536,384]{1,0:T(8,128)(2,1)}, u32[]{:S(2)}, u32[]{:S(2)}) %collective-permute-start.39) | collective-permute-done | bytes 1179680 | tf_op jit(solution)/shard_map/ppermute | solution.py:461
  1135.1 4.2 collective-permute-start.42
  1150.0 39.6 %collective-permute-done.42 = bf16[384,768]{1,0:T(8,128)(2,1)} collective-permute-done((bf16[384,768]{1,0:T(8,128)(2,1)}, bf16[384,768]{1,0:T(8,128)(2,1)}, u32[]{:S(2)}, u32[]{:S(2)}) %collective-permute-start.42) | collective-permute-done | bytes 589856 | tf_op jit(solution)/shard_map/ppermute | solution.py:461
  (457 shorter events, 161.7 us)
Async XLA Ops:
  7.2 218.2 %all-gather.3.cloned.1.call-start = ((), (), s32[]{:S(2)}) async-start(), calls=%async_computation.1 | async-start | bytes 38928384 | tf_op jit(solution)/shard_map/all_gather | solution.py:1018
  9.7 453.3 %all-gather.5.cloned.1.call-start = ((), (), s32[]{:S(2)}) async-start(), calls=%async_computation.2 | async-start | bytes 38928384 | tf_op jit(solution)/shard_map/all_gather | solution.py:1018
  11.8 989.2 %reduce-scatter.2.cloned.1.call-start = ((), (), s32[]{:S(2)}) async-start(), calls=%async_computation.3 | async-start | bytes 10027008 | tf_op jit(solution)/shard_map/reduce_scatter | solution.py:1116
  14.4 284.6 %copy-start.49 = (f32[1,512,1472]{2,1,0:T(8,128)}, f32[1,512,1472]{2,1,0:T(8,128)S(1)}, u32[]{:S(2)}) copy-start(f32[1,512,1472]{2,1,0:T(8,128)S(1)} %copy.116) | copy-start | bytes 9043972
  15.1 287.1 %copy-start.95 = (f32[1472]{0:T(1024)}, f32[1472]{0:T(1024)S(1)}, u32[]{:S(2)}) copy-start(f32[1472]{0:T(1024)S(1)} %get-tuple-element.451) | copy-start | bytes 17668
  15.1 313.7 %copy-start.99 = (f32[1472]{0:T(1024)}, f32[1472]{0:T(1024)S(1)}, u32[]{:S(2)}) copy-start(f32[1472]{0:T(1024)S(1)} %get-tuple-element.453) | copy-start | bytes 17668
  232.0 41.1 %collective-permute-start = (bf16[288,768]{1,0:T(8,128)(2,1)}, bf16[288,768]{1,0:T(8,128)(2,1)}, u32[]{:S(2)}, u32[]{:S(2)}) collective-permute-start(bf16[288,768]{1,0:T(8,128)(2,1)} %slice_select_fusion.1), channel_id=1, source_target_pairs={{0,2},{1,3},{2,0},{3,1},{4,6},{5,7},{6,4},{7,5},{8,10},{9,11},{10,... | collective-permute-start | bytes 1327112 | tf_op jit(solution)/shard_map/ppermute | solution.py:475
  232.6 55.9 %collective-permute-start.1 = (bf16[512,768]{1,0:T(8,128)(2,1)}, bf16[512,768]{1,0:T(8,128)(2,1)}, u32[]{:S(2)}, u32[]{:S(2)}) collective-permute-start(bf16[512,768]{1,0:T(8,128)(2,1)} %slice.177), channel_id=1, source_target_pairs={{0,1},{1,2},{2,3},{4,5},{5,6},{6,7},{8,9},{9,10},{10,11},{12,13},{... | collective-permute-start | bytes 2359304 | tf_op jit(solution)/shard_map/ppermute | solution.py:467
  234.4 55.4 %collective-permute-start.2 = (bf16[512,768]{1,0:T(8,128)(2,1)}, bf16[512,768]{1,0:T(8,128)(2,1)}, u32[]{:S(2)}, u32[]{:S(2)}) collective-permute-start(bf16[512,768]{1,0:T(8,128)(2,1)} %slice.177), channel_id=1, source_target_pairs={{1,0},{2,1},{3,2},{5,4},{6,5},{7,6},{9,8},{10,9},{11,10},{13,12},{... | collective-permute-start | bytes 2359304 | tf_op jit(solution)/shard_map/ppermute | solution.py:467
  249.5 40.2 %copy-start.69 = (bf16[512,1152]{1,0:T(8,128)(2,1)S(1)}, bf16[512,1152]{1,0:T(8,128)(2,1)}, u32[]{:S(2)}) copy-start(bf16[512,1152]{1,0:T(8,128)(2,1)} %copy-done.68) | copy-start | bytes 3538948
  250.6 40.9 %copy-start.41 = (bf16[512,384]{1,0:T(8,128)(2,1)}, bf16[512,384]{1,0:T(8,128)(2,1)S(1)}, u32[]{:S(2)}) copy-start(bf16[512,384]{1,0:T(8,128)(2,1)S(1)} %slice.174.refs_0_) | copy-start | bytes 1179652
  331.1 136.7 %copy-start.114 = (f32[512]{0:T(512)}, f32[512]{0:T(512)S(1)}, u32[]{:S(2)}) copy-start(f32[512]{0:T(512)S(1)} %get-tuple-element.465) | copy-start | bytes 6148
  469.9 52.6 %collective-permute-start.5 = (bf16[512,896]{1,0:T(8,128)(2,1)}, bf16[512,896]{1,0:T(8,128)(2,1)}, u32[]{:S(2)}, u32[]{:S(2)}) collective-permute-start(bf16[512,896]{1,0:T(8,128)(2,1)} %pad_maximum_fusion.2), channel_id=1, source_target_pairs={{1,0},{2,1},{3,2},{5,4},{6,5},{7,6},{9,8},{10,9},{11,10},{13,12},{... | collective-permute-start | bytes 2752520 | tf_op jit(solution)/shard_map/ppermute | solution.py:467
  474.5 46.5 %collective-permute-start.4 = (bf16[512,896]{1,0:T(8,128)(2,1)}, bf16[512,896]{1,0:T(8,128)(2,1)}, u32[]{:S(2)}, u32[]{:S(2)}) collective-permute-start(bf16[512,896]{1,0:T(8,128)(2,1)} %pad_maximum_fusion.2), channel_id=1, source_target_pairs={{0,1},{1,2},{2,3},{4,5},{5,6},{6,7},{8,9},{9,10},{10,11},{12,13},{... | collective-permute-start | bytes 2752520 | tf_op jit(solution)/shard_map/ppermute | solution.py:467
  476.3 43.5 %collective-permute-start.3 = (bf16[288,896]{1,0:T(8,128)(2,1)}, bf16[288,896]{1,0:T(8,128)(2,1)}, u32[]{:S(2)}, u32[]{:S(2)}) collective-permute-start(bf16[288,896]{1,0:T(8,128)(2,1)} %fusion.44), channel_id=1, source_target_pairs={{0,2},{1,3},{2,0},{3,1},{4,6},{5,7},{6,4},{7,5},{8,10},{9,11},{10,... | collective-permute-start | bytes 1548296 | tf_op jit(solution)/shard_map/ppermute | solution.py:475
  480.5 43.5 %copy-start.38 = (bf16[512,384]{1,0:T(8,128)(2,1)}, bf16[512,384]{1,0:T(8,128)(2,1)S(1)}, u32[]{:S(2)}) copy-start(bf16[512,384]{1,0:T(8,128)(2,1)S(1)} %slice.180.refs_0_) | copy-start | bytes 1179652
  480.6 41.8 %copy-start.61 = (bf16[512,768]{1,0:T(8,128)(2,1)S(1)}, bf16[512,768]{1,0:T(8,128)(2,1)}, u32[]{:S(2)}) copy-start(bf16[512,768]{1,0:T(8,128)(2,1)} %copy-done.60) | copy-start | bytes 2359300
  594.8 66.3 %collective-permute-start.6 = (bf16[6144,512]{1,0:T(8,128)(2,1)}, bf16[6144,512]{1,0:T(8,128)(2,1)}, u32[]{:S(2)}, u32[]{:S(2)}) collective-permute-start(bf16[6144,512]{1,0:T(8,128)(2,1)} %get-tuple-element.212), channel_id=1, source_target_pairs={{0,4},{4,0},{1,5},{5,1},{2,6},{6,2},{3,7},{7,3},{8,12},{12,8},{9,1... | collective-permute-start | bytes 18874376 | tf_op jit(solution)/shard_map/ppermute | solution.py:461
  598.4 62.6 %collective-permute-start.7 = (bf16[1024,1536]{1,0:T(8,128)(2,1)S(1)}, bf16[1024,1536]{1,0:T(8,128)(2,1)}, u32[]{:S(2)}, u32[]{:S(2)}) collective-permute-start(bf16[1024,1536]{1,0:T(8,128)(2,1)S(1)} %fusion.11.refs_2_.refs_3_), channel_id=1, source_target_pairs={{0,4},{4,0},{1,5},{5,1},{2,6},{6,2},{3,7},{7,3},{8,12},{12,8},{9,1... | collective-permute-start | bytes 9437192 | tf_op jit(solution)/shard_map/ppermute | solution.py:461
  629.9 59.4 %copy-start.40 = (bf16[512,384]{1,0:T(8,128)(2,1)}, bf16[512,384]{1,0:T(8,128)(2,1)S(1)}, u32[]{:S(2)}) copy-start(bf16[512,384]{1,0:T(8,128)(2,1)S(1)} %get-tuple-element.208) | copy-start | bytes 1179652
  631.3 27.7 %copy-start.71 = (bf16[512,1472]{1,0:T(8,128)(2,1)S(1)}, bf16[512,1472]{1,0:T(8,128)(2,1)}, u32[]{:S(2)}) copy-start(bf16[512,1472]{1,0:T(8,128)(2,1)} %get-tuple-element.473) | copy-start | bytes 4521988
  631.3 54.9 %collective-permute-start.10 = (bf16[288,896]{1,0:T(8,128)(2,1)S(1)}, bf16[288,896]{1,0:T(8,128)(2,1)S(1)}, u32[]{:S(2)}, u32[]{:S(2)}) collective-permute-start(bf16[288,896]{1,0:T(8,128)(2,1)S(1)} %slice_select_fusion), channel_id=1, source_target_pairs={{0,2},{1,3},{2,0},{3,1},{4,6},{5,7},{6,4},{7,5},{8,10},{9,11},{10,... | collective-permute-start | bytes 1548296 | tf_op jit(solution)/shard_map/ppermute | solution.py:475
  653.0 33.2 %collective-permute-start.9 = (bf16[512,896]{1,0:T(8,128)(2,1)S(1)}, bf16[512,896]{1,0:T(8,128)(2,1)S(1)}, u32[]{:S(2)}, u32[]{:S(2)}) collective-permute-start(bf16[512,896]{1,0:T(8,128)(2,1)S(1)} %get-tuple-element.466), channel_id=1, source_target_pairs={{0,1},{1,2},{2,3},{4,5},{5,6},{6,7},{8,9},{9,10},{10,11},{12,13},{... | collective-permute-start | bytes 2752520 | tf_op jit(solution)/shard_map/ppermute | solution.py:467
  654.4 31.9 %collective-permute-start.8 = (bf16[512,896]{1,0:T(8,128)(2,1)S(1)}, bf16[512,896]{1,0:T(8,128)(2,1)S(1)}, u32[]{:S(2)}, u32[]{:S(2)}) collective-permute-start(bf16[512,896]{1,0:T(8,128)(2,1)S(1)} %get-tuple-element.467), channel_id=1, source_target_pairs={{1,0},{2,1},{3,2},{5,4},{6,5},{7,6},{9,8},{10,9},{11,10},{13,12},{... | collective-permute-start | bytes 2752520 | tf_op jit(solution)/shard_map/ppermute | solution.py:467
  661.0 39.1 %collective-permute-start.12 = (bf16[1024,1536]{1,0:T(8,128)(2,1)}, bf16[1024,1536]{1,0:T(8,128)(2,1)}, u32[]{:S(2)}, u32[]{:S(2)}) collective-permute-start(bf16[1024,1536]{1,0:T(8,128)(2,1)} %fusion.12.refs_2_.refs_3_), channel_id=1, source_target_pairs={{0,4},{4,0},{1,5},{5,1},{2,6},{6,2},{3,7},{7,3},{8,12},{12,8},{9,1... | collective-permute-start | bytes 9437192 | tf_op jit(solution)/shard_map/ppermute | solution.py:461
  691.2 8.9 collective-permute-start.11
  721.5 64.8 %collective-permute-start.13 = (bf16[3072,384]{1,0:T(8,128)(2,1)}, bf16[3072,384]{1,0:T(8,128)(2,1)}, u32[]{:S(2)}, u32[]{:S(2)}) collective-permute-start(bf16[3072,384]{1,0:T(8,128)(2,1)} %copy-done.32), channel_id=1, source_target_pairs={{0,16},{16,0},{1,17},{17,1},{2,18},{18,2},{3,19},{19,3},{4,20},{20... | collective-permute-start | bytes 7077896 | tf_op jit(solution)/shard_map/ppermute | solution.py:461
  721.6 64.7 %collective-permute-start.14 = (bf16[3072,384]{1,0:T(8,128)(2,1)}, bf16[3072,384]{1,0:T(8,128)(2,1)S(1)}, u32[]{:S(2)}, u32[]{:S(2)}) collective-permute-start(bf16[3072,384]{1,0:T(8,128)(2,1)} %copy-done.35), channel_id=1, source_target_pairs={{0,8},{8,0},{1,9},{9,1},{2,10},{10,2},{3,11},{11,3},{4,12},{12,4},... | collective-permute-start | bytes 7077896 | tf_op jit(solution)/shard_map/ppermute | solution.py:461
  732.1 55.7 %copy-start.14 = (bf16[3072,384]{1,0:T(8,128)(2,1)S(1)}, bf16[3072,384]{1,0:T(8,128)(2,1)}, u32[]{:S(2)}) copy-start(bf16[3072,384]{1,0:T(8,128)(2,1)} %copy-done.13) | copy-start | bytes 7077892
  795.7 63.2 %collective-permute-start.17 = (bf16[6144,512]{1,0:T(8,128)(2,1)}, bf16[6144,512]{1,0:T(8,128)(2,1)}, u32[]{:S(2)}, u32[]{:S(2)}) collective-permute-start(bf16[6144,512]{1,0:T(8,128)(2,1)} %get-tuple-element.275), channel_id=1, source_target_pairs={{0,4},{4,0},{1,5},{5,1},{2,6},{6,2},{3,7},{7,3},{8,12},{12,8},{9,1... | collective-permute-start | bytes 18874376 | tf_op jit(solution)/shard_map/ppermute | solution.py:461
  798.8 54.6 %collective-permute-start.18 = (bf16[1024,1536]{1,0:T(8,128)(2,1)}, bf16[1024,1536]{1,0:T(8,128)(2,1)}, u32[]{:S(2)}, u32[]{:S(2)}) collective-permute-start(bf16[1024,1536]{1,0:T(8,128)(2,1)} %fusion.13.refs_2_.refs_3_), channel_id=1, source_target_pairs={{0,4},{4,0},{1,5},{5,1},{2,6},{6,2},{3,7},{7,3},{8,12},{12,8},{9,1... | collective-permute-start | bytes 9437192 | tf_op jit(solution)/shard_map/ppermute | solution.py:461
  798.8 39.7 %collective-permute-start.15 = (bf16[1536,384]{1,0:T(8,128)(2,1)}, bf16[1536,384]{1,0:T(8,128)(2,1)S(1)}, u32[]{:S(2)}, u32[]{:S(2)}) collective-permute-start(bf16[1536,384]{1,0:T(8,128)(2,1)} %get-tuple-element.255), channel_id=1, source_target_pairs={{0,8},{8,0},{1,9},{9,1},{2,10},{10,2},{3,11},{11,3},{4,12},{12,4},... | collective-permute-start | bytes 3538952 | tf_op jit(solution)/shard_map/ppermute | solution.py:461
  799.0 39.4 %collective-permute-start.16 = (bf16[1536,384]{1,0:T(8,128)(2,1)}, bf16[1536,384]{1,0:T(8,128)(2,1)S(1)}, u32[]{:S(2)}, u32[]{:S(2)}) collective-permute-start(bf16[1536,384]{1,0:T(8,128)(2,1)} %get-tuple-element.257), channel_id=1, source_target_pairs={{0,16},{16,0},{1,17},{17,1},{2,18},{18,2},{3,19},{19,3},{4,20},{20... | collective-permute-start | bytes 3538952 | tf_op jit(solution)/shard_map/ppermute | solution.py:461
  804.9 102.9 %collective-permute-start.23 = (bf16[1024,1536]{1,0:T(8,128)(2,1)S(1)}, bf16[1024,1536]{1,0:T(8,128)(2,1)S(1)}, u32[]{:S(2)}, u32[]{:S(2)}) collective-permute-start(bf16[1024,1536]{1,0:T(8,128)(2,1)S(1)} %fusion.14.refs_2_.refs_3_), channel_id=1, source_target_pairs={{0,4},{4,0},{1,5},{5,1},{2,6},{6,2},{3,7},{7,3},{8,12},{12,8},{9,1... | collective-permute-start | bytes 9437192 | tf_op jit(solution)/shard_map/ppermute | solution.py:461
  808.4 31.0 %copy-start.75 = (bf16[1536,384]{1,0:T(8,128)(2,1)S(1)}, bf16[1536,384]{1,0:T(8,128)(2,1)}, u32[]{:S(2)}) copy-start(bf16[1536,384]{1,0:T(8,128)(2,1)} %get-tuple-element.261) | copy-start | bytes 3538948
  846.1 39.7 %collective-permute-start.21 = (bf16[288,768]{1,0:T(8,128)(2,1)}, bf16[288,768]{1,0:T(8,128)(2,1)S(1)}, u32[]{:S(2)}, u32[]{:S(2)}) collective-permute-start(bf16[288,768]{1,0:T(8,128)(2,1)} %slice_select_fusion.2), channel_id=1, source_target_pairs={{0,2},{1,3},{2,0},{3,1},{4,6},{5,7},{6,4},{7,5},{8,10},{9,11},{10,... | collective-permute-start | bytes 1327112 | tf_op jit(solution)/shard_map/ppermute | solution.py:475
  852.1 51.1 %collective-permute-start.20 = (bf16[512,768]{1,0:T(8,128)(2,1)}, bf16[512,768]{1,0:T(8,128)(2,1)S(1)}, u32[]{:S(2)}, u32[]{:S(2)}) collective-permute-start(bf16[512,768]{1,0:T(8,128)(2,1)} %get-tuple-element.469), channel_id=1, source_target_pairs={{0,1},{1,2},{2,3},{4,5},{5,6},{6,7},{8,9},{9,10},{10,11},{12,13},{... | collective-permute-start | bytes 2359304 | tf_op jit(solution)/shard_map/ppermute | solution.py:467
  853.4 49.8 %collective-permute-start.19 = (bf16[512,768]{1,0:T(8,128)(2,1)S(1)}, bf16[512,768]{1,0:T(8,128)(2,1)}, u32[]{:S(2)}, u32[]{:S(2)}) collective-permute-start(bf16[512,768]{1,0:T(8,128)(2,1)S(1)} %get-tuple-element.470), channel_id=1, source_target_pairs={{1,0},{2,1},{3,2},{5,4},{6,5},{7,6},{9,8},{10,9},{11,10},{13,12},{... | collective-permute-start | bytes 2359304 | tf_op jit(solution)/shard_map/ppermute | solution.py:467
  906.5 3.5 collective-permute-start.22
  924.9 76.2 %collective-permute-start.24 = (bf16[3072,384]{1,0:T(8,128)(2,1)}, bf16[3072,384]{1,0:T(8,128)(2,1)}, u32[]{:S(2)}, u32[]{:S(2)}) collective-permute-start(bf16[3072,384]{1,0:T(8,128)(2,1)} %get-tuple-element.315), channel_id=1, source_target_pairs={{0,16},{16,0},{1,17},{17,1},{2,18},{18,2},{3,19},{19,3},{4,20},{20... | collective-permute-start | bytes 7077896 | tf_op jit(solution)/shard_map/ppermute | solution.py:461
  926.3 74.8 %collective-permute-start.25 = (bf16[3072,384]{1,0:T(8,128)(2,1)}, bf16[3072,384]{1,0:T(8,128)(2,1)}, u32[]{:S(2)}, u32[]{:S(2)}) collective-permute-start(bf16[3072,384]{1,0:T(8,128)(2,1)} %get-tuple-element.317), channel_id=1, source_target_pairs={{0,8},{8,0},{1,9},{9,1},{2,10},{10,2},{3,11},{11,3},{4,12},{12,4},... | collective-permute-start | bytes 7077896 | tf_op jit(solution)/shard_map/ppermute | solution.py:461
  940.4 8.7 collective-permute-start.29
  940.4 21.5 %collective-permute-start.26 = (bf16[384,768]{1,0:T(8,128)(2,1)}, bf16[384,768]{1,0:T(8,128)(2,1)}, u32[]{:S(2)}, u32[]{:S(2)}) collective-permute-start(bf16[384,768]{1,0:T(8,128)(2,1)} %pad_maximum_fusion.8), channel_id=1, source_target_pairs={{0,1},{1,2},{2,3},{3,0},{4,5},{5,6},{6,7},{7,4},{8,9},{9,10},{10,1... | collective-permute-start | bytes 1769480 | tf_op jit(solution)/shard_map/ppermute | solution.py:461
  941.3 59.7 %collective-permute-start.27 = (bf16[384,768]{1,0:T(8,128)(2,1)S(1)}, bf16[384,768]{1,0:T(8,128)(2,1)}, u32[]{:S(2)}, u32[]{:S(2)}) collective-permute-start(bf16[384,768]{1,0:T(8,128)(2,1)S(1)} %copy-done.91), channel_id=1, source_target_pairs={{0,2},{1,3},{2,0},{3,1},{4,6},{5,7},{6,4},{7,5},{8,10},{9,11},{10,... | collective-permute-start | bytes 1769480 | tf_op jit(solution)/shard_map/ppermute | solution.py:461
  949.1 51.9 %collective-permute-start.28 = (bf16[384,768]{1,0:T(8,128)(2,1)S(1)}, bf16[384,768]{1,0:T(8,128)(2,1)}, u32[]{:S(2)}, u32[]{:S(2)}) collective-permute-start(bf16[384,768]{1,0:T(8,128)(2,1)S(1)} %copy-done.90), channel_id=1, source_target_pairs={{0,3},{1,0},{2,1},{3,2},{4,7},{5,4},{6,5},{7,6},{8,11},{9,8},{10,9... | collective-permute-start | bytes 1769480 | tf_op jit(solution)/shard_map/ppermute | solution.py:461
  1007.6 28.9 %collective-permute-start.30 = (bf16[1536,384]{1,0:T(8,128)(2,1)S(1)}, bf16[1536,384]{1,0:T(8,128)(2,1)S(1)}, u32[]{:S(2)}, u32[]{:S(2)}) collective-permute-start(bf16[1536,384]{1,0:T(8,128)(2,1)S(1)} %get-tuple-element.334), channel_id=1, source_target_pairs={{0,8},{8,0},{1,9},{9,1},{2,10},{10,2},{3,11},{11,3},{4,12},{12,4},... | collective-permute-start | bytes 3538952 | tf_op jit(solution)/shard_map/ppermute | solution.py:461
  1008.4 28.9 %collective-permute-start.31 = (bf16[1536,384]{1,0:T(8,128)(2,1)S(1)}, bf16[1536,384]{1,0:T(8,128)(2,1)S(1)}, u32[]{:S(2)}, u32[]{:S(2)}) collective-permute-start(bf16[1536,384]{1,0:T(8,128)(2,1)S(1)} %get-tuple-element.336), channel_id=1, source_target_pairs={{0,16},{16,0},{1,17},{17,1},{2,18},{18,2},{3,19},{19,3},{4,20},{20... | collective-permute-start | bytes 3538952 | tf_op jit(solution)/shard_map/ppermute | solution.py:461
  1009.0 4.1 collective-permute-start.32
  1009.0 84.7 %collective-permute-start.37 = (bf16[3072,384]{1,0:T(8,128)(2,1)}, bf16[3072,384]{1,0:T(8,128)(2,1)}, u32[]{:S(2)}, u32[]{:S(2)}) collective-permute-start(bf16[3072,384]{1,0:T(8,128)(2,1)} %get-tuple-element.358), channel_id=1, source_target_pairs={{0,16},{16,0},{1,17},{17,1},{2,18},{18,2},{3,19},{19,3},{4,20},{20... | collective-permute-start | bytes 7077896 | tf_op jit(solution)/shard_map/ppermute | solution.py:461
  1010.5 83.3 %collective-permute-start.38 = (bf16[3072,384]{1,0:T(8,128)(2,1)}, bf16[3072,384]{1,0:T(8,128)(2,1)}, u32[]{:S(2)}, u32[]{:S(2)}) collective-permute-start(bf16[3072,384]{1,0:T(8,128)(2,1)} %get-tuple-element.360), channel_id=1, source_target_pairs={{0,8},{8,0},{1,9},{9,1},{2,10},{10,2},{3,11},{11,3},{4,12},{12,4},... | collective-permute-start | bytes 7077896 | tf_op jit(solution)/shard_map/ppermute | solution.py:461
  1013.1 28.6 %copy-start.94 = (f32[6,1472]{1,0:T(8,128)}, f32[6,1472]{1,0:T(8,128)S(1)}, u32[]{:S(2)}) copy-start(f32[6,1472]{1,0:T(8,128)S(1)} %add.458) | copy-start | bytes 105988
  1041.7 5.6 collective-permute-start.36
  1041.7 15.0 %collective-permute-start.33 = (bf16[384,768]{1,0:T(8,128)(2,1)}, bf16[384,768]{1,0:T(8,128)(2,1)S(1)}, u32[]{:S(2)}, u32[]{:S(2)}) collective-permute-start(bf16[384,768]{1,0:T(8,128)(2,1)} %pad_maximum_fusion.12), channel_id=1, source_target_pairs={{0,1},{1,2},{2,3},{3,0},{4,5},{5,6},{6,7},{7,4},{8,9},{9,10},{10,1... | collective-permute-start | bytes 1769480 | tf_op jit(solution)/shard_map/ppermute | solution.py:461
  1041.7 52.0 %collective-permute-start.34 = (bf16[384,768]{1,0:T(8,128)(2,1)}, bf16[384,768]{1,0:T(8,128)(2,1)S(1)}, u32[]{:S(2)}, u32[]{:S(2)}) collective-permute-start(bf16[384,768]{1,0:T(8,128)(2,1)} %pad_maximum_fusion.13), channel_id=1, source_target_pairs={{0,2},{1,3},{2,0},{3,1},{4,6},{5,7},{6,4},{7,5},{8,10},{9,11},{10,... | collective-permute-start | bytes 1769480 | tf_op jit(solution)/shard_map/ppermute | solution.py:461
  1047.3 46.5 %collective-permute-start.35 = (bf16[384,768]{1,0:T(8,128)(2,1)}, bf16[384,768]{1,0:T(8,128)(2,1)}, u32[]{:S(2)}, u32[]{:S(2)}) collective-permute-start(bf16[384,768]{1,0:T(8,128)(2,1)} %pad_maximum_fusion.14), channel_id=1, source_target_pairs={{0,3},{1,0},{2,1},{3,2},{4,7},{5,4},{6,5},{7,6},{8,11},{9,8},{10,9... | collective-permute-start | bytes 1769480 | tf_op jit(solution)/shard_map/ppermute | solution.py:461
  1047.9 45.9 %copy-start.20 = (bf16[3072,384]{1,0:T(8,128)(2,1)S(1)}, bf16[3072,384]{1,0:T(8,128)(2,1)}, u32[]{:S(2)}) copy-start(bf16[3072,384]{1,0:T(8,128)(2,1)} %copy-done.19) | copy-start | bytes 7077892
  1056.7 39.5 %copy-start.88 = (bf16[384,768]{1,0:T(8,128)(2,1)}, bf16[384,768]{1,0:T(8,128)(2,1)S(1)}, u32[]{:S(2)}) copy-start(bf16[384,768]{1,0:T(8,128)(2,1)S(1)} %collective-permute-done.33) | copy-start | bytes 1769476
  1102.9 24.2 %collective-permute-start.39 = (bf16[1536,384]{1,0:T(8,128)(2,1)}, bf16[1536,384]{1,0:T(8,128)(2,1)}, u32[]{:S(2)}, u32[]{:S(2)}) collective-permute-start(bf16[1536,384]{1,0:T(8,128)(2,1)} %get-tuple-element.368), channel_id=1, source_target_pairs={{0,8},{8,0},{1,9},{9,1},{2,10},{10,2},{3,11},{11,3},{4,12},{12,4},... | collective-permute-start | bytes 3538952 | tf_op jit(solution)/shard_map/ppermute | solution.py:461
  1104.1 23.9 %collective-permute-start.40 = (bf16[1536,384]{1,0:T(8,128)(2,1)}, bf16[1536,384]{1,0:T(8,128)(2,1)}, u32[]{:S(2)}, u32[]{:S(2)}) collective-permute-start(bf16[1536,384]{1,0:T(8,128)(2,1)} %get-tuple-element.370), channel_id=1, source_target_pairs={{0,16},{16,0},{1,17},{17,1},{2,18},{18,2},{3,19},{19,3},{4,20},{20... | collective-permute-start | bytes 3538952 | tf_op jit(solution)/shard_map/ppermute | solution.py:461
  1134.2 9.3 collective-permute-start.44
  1135.1 14.9 %collective-permute-start.41 = (bf16[384,768]{1,0:T(8,128)(2,1)}, bf16[384,768]{1,0:T(8,128)(2,1)}, u32[]{:S(2)}, u32[]{:S(2)}) collective-permute-start(bf16[384,768]{1,0:T(8,128)(2,1)} %pad_maximum_fusion.16), channel_id=1, source_target_pairs={{0,1},{1,2},{2,3},{3,0},{4,5},{5,6},{6,7},{7,4},{8,9},{9,10},{10,1... | collective-permute-start | bytes 1769480 | tf_op jit(solution)/shard_map/ppermute | solution.py:461
  1135.1 54.5 %collective-permute-start.42 = (bf16[384,768]{1,0:T(8,128)(2,1)}, bf16[384,768]{1,0:T(8,128)(2,1)}, u32[]{:S(2)}, u32[]{:S(2)}) collective-permute-start(bf16[384,768]{1,0:T(8,128)(2,1)} %pad_maximum_fusion.17), channel_id=1, source_target_pairs={{0,2},{1,3},{2,0},{3,1},{4,6},{5,7},{6,4},{7,5},{8,10},{9,11},{10,... | collective-permute-start | bytes 1769480 | tf_op jit(solution)/shard_map/ppermute | solution.py:461
  1139.3 50.3 %collective-permute-start.43 = (bf16[384,768]{1,0:T(8,128)(2,1)}, bf16[384,768]{1,0:T(8,128)(2,1)}, u32[]{:S(2)}, u32[]{:S(2)}) collective-permute-start(bf16[384,768]{1,0:T(8,128)(2,1)} %pad_maximum_fusion.18), channel_id=1, source_target_pairs={{0,3},{1,0},{2,1},{3,2},{4,7},{5,4},{6,5},{7,6},{8,11},{9,8},{10,9... | collective-permute-start | bytes 1769480 | tf_op jit(solution)/shard_map/ppermute | solution.py:461
  1144.3 4.1 collective-permute-start.45
  (110 other events, 562.7 us)
Sparse Core Ops, SparseCore 0:
  11.4 213.9 all-gather.2
  228.8 234.2 all-gather.4
  721.6 210.3 reduce-scatter.1

commit v10 on v9

--- a/solution.py
+++ b/solution.py
@@ -20,10 +20,9 @@
 TILE = 256
 ATTENTION_TILES = 4 * INNER // TILE
 OFFSETS = 5
-CHUNK = 384
 PADDED = 1536
 FORWARD_TILE = 512
-CUTS = (0, 384, 768, 1152, 1472)
+CUTS = (0, 1472)
 DEVICES = ("y", "x", "c", "z")
 epsilon = 1e-06
 gate_scale = -30.0
@@ -793,10 +792,11 @@
 
 
 def array_shapes(chunks, rows):
-    shapes = [(rows // lax.axis_size("y"), CHUNK)] * (chunks // 2 * lax.axis_size("y"))
-    shapes += [(rows // lax.axis_size("x"), CHUNK)] * (chunks // 2 * lax.axis_size("x"))
+    columns = chunk_width(chunks)
+    shapes = [(rows // lax.axis_size("y"), columns)] * (chunks // 2 * lax.axis_size("y"))
+    shapes += [(rows // lax.axis_size("x"), columns)] * (chunks // 2 * lax.axis_size("x"))
     if chunks < 4:
-        shapes.append((rows, PADDED - chunks * CHUNK))
+        shapes.append((rows, PADDED - chunks * columns))
     return [jax.ShapeDtypeStruct(shape, jnp.bfloat16) for shape in shapes]
 
 
@@ -805,8 +805,8 @@
     rest = places[2]
 
     def copy(lane, place, row, where):
-        start = lane * CHUNK
-        end = PADDED if lane == chunks else start + CHUNK
+        start = lane * chunk_width(chunks)
+        end = PADDED if lane == chunks else start + chunk_width(chunks)
         spot = pl.ds(pl.multiple_of(row * tile, tile), tile)
         return pltpu.make_async_copy(
             stage_ref.at[where, :, start:end], place.at[spot, :], sems.at[where, lane]
@@ -961,6 +961,10 @@
     return lax.optimization_barrier((first, second))
 
 
+def chunk_width(chunks):
+    return PADDED // 4 if chunks == 4 else PADDED // 6
+
+
 class Scatter:
     def __init__(self):
         self.waiting, self.flying, self.results = {}, {}, {}
@@ -1003,8 +1007,9 @@
         return values
 
     def step(self, values, *names):
-        values = self.settle(values, *(name for name in names if name in self.flying))
-        return self.start(values, *self.waiting) if self.waiting else values
+        others = set(self.waiting)
+        values = self.settle(values, *names)
+        return self.start(values, *(name for name in self.waiting if name not in others))
 
 
 def total_of(value, moved):
@@ -1073,8 +1078,7 @@
         branch_low, normed_two_low, up_gelu, up_linear, gathered
     )
     if before is not None:
-        grad_normed_two, own, sent = before.settle((grad_normed_two, own, sent), 0, 1)
-        grad_normed_two, own, sent = before.start((grad_normed_two, own, sent), 0, 1)
+        grad_normed_two, own, sent = before.step((grad_normed_two, own, sent), 0, 1)
     other = shift(sent, "c", 1)
     grad_middle, grad_gain_two = rms_backward(middle, inverse_two, gain_two, grad_normed_two)
     grad_middle = grad_out + grad_middle
@@ -1168,16 +1172,14 @@
         [gain_three_one, gain_three_two, gain_four_one, gain_four_two, grad_gate_weight, table[0]]
     )
     small = hop(small_sums, "c")
-    small, rest = before.settle((small, rest), (0, 1))
-    small = scatter.settle(small, 0, 1)
-    small = scatter.start(small, 0, 1)
+    small = before.settle(small, (0, 1))
+    small = scatter.step(small, 0, 1)
     small = scatter.start(small, 2, 3)
-    small = hop(small, "z", 1)
     small = scatter.step(small, 0, 1)
-    for bit in range(2, lax.axis_size("z")):
+    small, rest = scatter.settle((small, rest), (0, 1))
+    for bit in range(1, lax.axis_size("z")):
         if bit & (bit - 1) == 0:
             small = hop(small, "z", bit)
-    small = scatter.settle(small, (0, 1))
     small = scatter.step(small, 2, 3)
     small = scatter.step(small, 2, 3)
     small = hop(small, "x")

time: 1200 us -> 1150 us (0.958); the launches traced: 1200 us -> 1140 us
  waiting for transfers between devices: 648 us -> 600 us
  local copies, waits for them, and re-layouts: 86.1 us -> 71.4 us
    ppermute x29, waiting for transfers between devices: 206 us -> 175 us  [shift(): lax.ppermute(value, axis, [(i, (i + amount) % count) for i in range(count)])]
    ppermute x8, waiting for transfers between devices: 31.7 us -> 18.1 us  [slide(): return lax.ppermute(value, 'z', pairs)]
    unnamed x265 -> x267, local copies, waits for them, and re-layouts: 59.8 us -> 51.2 us
  transfers between devices with their start and end apart: 49 -> 49, of which waited for: 23 -> 20; matrix products, arithmetic and copies ran while one was open for 11% -> 11% of each run, Pallas kernels for 14% -> 16%
where the time goes in v10:
time: 1150 us; the launch traced here: 1140 us
  waiting for transfers between devices  600 us (52%)
  Pallas kernels  251 us (22%)
  starting transfers between devices  88 us (8%)
  other arithmetic  77.5 us (7%)
  local copies, waits for them, and re-layouts  71.4 us (6%)
  matrix products  34.7 us (3%)
  between operations  15.9 us (1%)
    all_gather x2, waiting for transfers between devices, fetch_rows(): return lax.all_gather(local_rows, DEVICES, axis=0, tiled=True)  341 us
    ppermute x29, waiting for transfers between devices, shift(): lax.ppermute(value, axis, [(i, (i + amount) % count) for i in range(count)])  175 us
    pallas_call x2, Pallas kernels, ffn_backward(): pl.pallas_call(ffn_backward_body, grid_spec=pltpu.PrefetchScalarGridSpec(...  65.1 us
    ppermute x4, waiting for transfers between devices, far_pair(): got = lax.ppermute(sent, 'z', pairs)  62.1 us
    unnamed x267, local copies, waits for them, and re-layouts  51.2 us
    pallas_call x2, Pallas kernels, attend_backward(): pl.pallas_call(functools.partial(backward_body, width > 2 * INNER), grid_...  50.1 us
    pallas_call x2, Pallas kernels, ffn_forward(): pl.pallas_call(ffn_forward_body, grid=(steps,), in_specs=[resident((token...  49.4 us
    pallas_call x2, Pallas kernels, weight_grads(): pl.pallas_call(functools.partial(weight_grads_body, chunks, tile), grid_s...  47.2 us
  transfers between devices with their start and end apart: 49, of which 20 were waited for; matrix products, arithmetic and copies ran while one was open for 11% of the time, Pallas kernels for 16%

profile of v10, /device:TPU:24, one launch (start us, length us, event | category | flops | bytes accessed | tf_op | source)
XLA Modules:
  0.0 1138.4 jit_solution(16709562325781950544)
XLA Ops:
  7.2 2.5 copy.117
  12.0 2.4 copy.116
  17.5 207.9 %all-gather.3.cloned.1.call-done.gelu_ref.linear_ref.down_ref.refs_4_.refs_5_.refs_6_ = bf16[12288,1472]{1,0:T(8,128)(2,1)} async-done(((bf16[384,1472]{1,0:T(8,128)(2,1)}), bf16[12288,1472]{1,0:T(8,128)(2,1)}) %all-gather.3.cloned.1.call-update) | async-done | bytes 36175888 | tf_op jit(solution)/shard_map/all_gather | solution.py:1023
  225.4 4.7 fusion.33
  234.5 6.0 collective-permute-start.2
  241.2 4.7 bias_tiles.1.refs_4_.refs_5_
  246.0 3.5 copy.122
  250.7 22.5 %collective-permute-done = bf16[288,768]{1,0:T(8,128)(2,1)} collective-permute-done((bf16[288,768]{1,0:T(8,128)(2,1)}, bf16[288,768]{1,0:T(8,128)(2,1)}, u32[]{:S(2)}, u32[]{:S(2)}) %collective-permute-start) | collective-permute-done | bytes 442400 | tf_op jit(solution)/shard_map/ppermute | solution.py:474
  274.3 14.3 %collective-permute-done.1 = bf16[512,768]{1,0:T(8,128)(2,1)} collective-permute-done((bf16[512,768]{1,0:T(8,128)(2,1)}, bf16[512,768]{1,0:T(8,128)(2,1)}, u32[]{:S(2)}, u32[]{:S(2)}) %collective-permute-start.1) | collective-permute-done | bytes 786464 | tf_op jit(solution)/shard_map/ppermute | solution.py:466
  291.5 6.7 attend_forward.2
  298.3 2.5 multiply_reduce_fusion.10
  302.4 24.8 %ffn_forward.2 = (f32[512,1472]{1,0:T(8,128)S(1)}, f32[512,3584]{1,0:T(8,128)}, f32[512,3584]{1,0:T(8,128)}) custom-call(bf16[512,1472]{1,0:T(8,128)(2,1)S(1)} %multiply_convert_fusion.2.normed_ref.refs_1_, f32[512,1472]{1,0:T(8,128)} %copy-done.51, bf16[12288,1472]{1,0:T(8,128)(2,1)} %all-gather.3.cloned.1.call-done.gelu_ref.linear_ref.down_ref.refs_4_.refs_5_.refs_6_, ...), custom_call_target="tpu_custom_call" | custom-call | flops 16206790656 | bytes 46333952 | tf_op jit(solution)/shard_map/ffn_forward/pallas_call | solution.py:601
  330.4 132.7 %all-gather.5.cloned.1.call-done.gelu_ref.linear_ref.down_ref.refs_4_.refs_5_.refs_6_ = bf16[12288,1472]{1,0:T(8,128)(2,1)} async-done(((bf16[384,1472]{1,0:T(8,128)(2,1)}), bf16[12288,1472]{1,0:T(8,128)(2,1)}) %all-gather.5.cloned.1.call-update) | async-done | bytes 36175888 | tf_op jit(solution)/shard_map/all_gather | solution.py:1023
  463.1 4.7 fusion.36
  470.0 4.5 collective-permute-start.5
  480.4 39.5 %collective-permute-done.3 = bf16[288,896]{1,0:T(8,128)(2,1)} collective-permute-done((bf16[288,896]{1,0:T(8,128)(2,1)}, bf16[288,896]{1,0:T(8,128)(2,1)}, u32[]{:S(2)}, u32[]{:S(2)}) %collective-permute-start.3) | collective-permute-done | bytes 516128 | tf_op jit(solution)/shard_map/ppermute | solution.py:474
  524.2 6.7 attend_forward.3
  530.9 2.3 multiply_reduce_fusion.7
  535.2 24.6 %ffn_forward.3 = (f32[512,1472]{1,0:T(8,128)S(1)}, f32[512,3584]{1,0:T(8,128)}, f32[512,3584]{1,0:T(8,128)}) custom-call(bf16[512,1472]{1,0:T(8,128)(2,1)S(1)} %multiply_convert_fusion.normed_ref.refs_1_, f32[512,1472]{1,0:T(8,128)} %copy-done.53, bf16[12288,1472]{1,0:T(8,128)(2,1)} %all-gather.5.cloned.1.call-done.gelu_ref.linear_ref.down_ref.refs_4_.refs_5_.refs_6_, ...), custom_call_target="tpu_custom_call" | custom-call | flops 16206790656 | bytes 46333952 | tf_op jit(solution)/shard_map/ffn_forward/pallas_call | solution.py:601
  561.5 32.2 %ffn_backward.2 = (f32[512,1472]{1,0:T(8,128)}, bf16[6144,512]{1,0:T(8,128)(2,1)}, bf16[6144,512]{1,0:T(8,128)(2,1)}) custom-call(s32[2]{0:T(128)} %pad_add_fusion.core_ref, bf16[512,1472]{1,0:T(8,128)(2,1)} %bitcast_convert_fusion.refs_0_, bf16[512,1472]{1,0:T(8,128)(2,1)} %copy-done.2, f32[512,3584]{1,0:T(8,128)} %get-tuple-element.204.refs_2_, ...), custom_call_target="tpu_custom_call" | custom-call | flops 16206790656 | bytes 57344000 | tf_op jit(solution)/shard_map/ffn_backward/pallas_call | solution.py:704
  595.1 2.3 fusion.11.refs_2_.refs_3_
  598.9 2.3 multiply_reduce_fusion.1
  601.2 2.5 fusion.51
  603.7 2.9 convolution_convert_fusion.1.refs_1_
  606.7 30.4 %attend_backward.2 = (bf16[512,384]{1,0:T(8,128)(2,1)S(1)}, bf16[2304,896]{1,0:T(8,128)(2,1)}, f32[3,32,256]{2,1,0:T(8,128)S(1)}) custom-call(s32[4]{0:T(128)S(1)} %get-tuple-element.533.low_ref, s32[4]{0:T(128)S(1)} %get-tuple-element.532.high_ref, bf16[512,384]{1,0:T(8,128)(2,1)S(1)} %copy-done.39, bf16[512,384]{1,0:T(8,128)(2,1)S(1)} %convolution_convert_fusion.1.refs_1_, ...), custom_call_target="tpu_custom_call" | custom-call | flops 4529848320 | bytes 12582912 | tf_op jit(solution)/shard_map/attend_backward/pallas_call | solution.py:366
  638.5 12.3 %collective-permute-start.10 = (bf16[288,896]{1,0:T(8,128)(2,1)S(1)}, bf16[288,896]{1,0:T(8,128)(2,1)S(1)}, u32[]{:S(2)}, u32[]{:S(2)}) collective-permute-start(bf16[288,896]{1,0:T(8,128)(2,1)S(1)} %slice_select_fusion), channel_id=1, source_target_pairs={{0,2},{1,3},{2,0},{3,1},{4,6},{5,7},{6,4},{7,5},{8,10},{9,11},{10,... | collective-permute-start | bytes 1548296 | tf_op jit(solution)/shard_map/ppermute | solution.py:474
  654.2 4.6 collective-permute-start.8
  662.0 22.5 %weight_grads.2 = (bf16[3072,256]{1,0:T(8,128)(2,1)S(1)}, bf16[3072,256]{1,0:T(8,128)(2,1)S(1)}, bf16[3072,256]{1,0:T(8,128)(2,1)S(1)}, bf16[3072,256]{1,0:T(8,128)(2,1)S(1)}, bf16[6144,1024]{1,0:T(8,128)(2,1)}) custom-call(s32[6]{0:T(128)S(1)} %stack.55.place_ref, bf16[6144,512]{1,0:T(8,128)(2,1)} %get-tuple-element.211.refs_0_, ...), custom_call_target="tpu_custom_call" | custom-call | flops 18522046464 | bytes 31457280 | tf_op jit(solution)/shard_map/weight_grads/pallas_call | solution.py:861
  684.6 3.8 collective-permute-done.9
  694.8 2.5 pad_maximum_fusion.5
  701.5 10.7 attention_fill.2
  717.0 3.1 collective-permute-start.13
  721.2 6.1 multiply_reduce_fusion.2
  727.3 3.0 fusion.49
  730.3 32.9 %ffn_backward.3 = (f32[512,1472]{1,0:T(8,128)}, bf16[6144,512]{1,0:T(8,128)(2,1)}, bf16[6144,512]{1,0:T(8,128)(2,1)}) custom-call(s32[2]{0:T(128)} %pad_add_fusion.core_ref, bf16[512,1472]{1,0:T(8,128)(2,1)} %get-tuple-element.460.refs_0_, bf16[512,1472]{1,0:T(8,128)(2,1)} %copy-done, f32[512,3584]{1,0:T(8,128)} %get-tuple-element.241.refs_2_, ...), custom_call_target="tpu_custom_call" | custom-call | flops 16206790656 | bytes 57344000 | tf_op jit(solution)/shard_map/ffn_backward/pallas_call | solution.py:704
  772.6 2.1 collective-permute-start.15
  776.1 2.5 fusion.48
  779.3 3.6 convolution_convert_fusion.refs_1_
  783.0 19.8 %attend_backward.3 = (bf16[512,384]{1,0:T(8,128)(2,1)S(1)}, bf16[2304,768]{1,0:T(8,128)(2,1)}, f32[3,32,256]{2,1,0:T(8,128)S(1)}) custom-call(s32[4]{0:T(128)S(1)} %get-tuple-element.533.low_ref, s32[4]{0:T(128)S(1)} %get-tuple-element.532.high_ref, bf16[512,384]{1,0:T(8,128)(2,1)S(1)} %copy-done.42, bf16[512,384]{1,0:T(8,128)(2,1)S(1)} %convolution_convert_fusion.refs_1_, ...), custom_call_target="tpu_custom_call" | custom-call | flops 4529848320 | bytes 12582912 | tf_op jit(solution)/shard_map/attend_backward/pallas_call | solution.py:366
  806.6 11.3 collective-permute-start.21
  819.3 5.5 collective-permute-start.19
  824.8 24.7 %weight_grads.3 = (bf16[3072,384]{1,0:T(8,128)(2,1)}, bf16[3072,384]{1,0:T(8,128)(2,1)}, bf16[3072,384]{1,0:T(8,128)(2,1)S(1)}, bf16[3072,384]{1,0:T(8,128)(2,1)...) custom-call(s32[6]{0:T(128)S(1)} %stack.55.place_ref, ...), custom_call_target="tpu_custom_call" | custom-call | flops 18522046464 | bytes 31457280 | tf_op jit(solution)/shard_map/weight_grads/pallas_call | solution.py:861
  853.5 4.5 collective-permute-start.22
  861.1 10.2 attention_fill.3
  877.3 7.9 fusion.24
  885.9 3.5 collective-permute-start.27
  890.8 7.1 collective-permute-done.26
  897.9 39.1 %collective-permute-done.27 = bf16[384,512]{1,0:T(8,128)(2,1)S(1)} collective-permute-done((bf16[384,512]{1,0:T(8,128)(2,1)}, bf16[384,512]{1,0:T(8,128)(2,1)S(1)}, u32[]{:S(2)}, u32[]{:S(2)}) %collective-permute-start.27) | collective-permute-done | bytes 393248 | tf_op jit(solution)/shard_map/ppermute | solution.py:460
  937.0 3.3 collective-permute-done.24
  940.3 2.3 add_convert_fusion.3
  944.3 2.3 add_convert_fusion.2
  950.9 24.9 %collective-permute-done.30 = bf16[1536,384]{1,0:T(8,128)(2,1)S(1)} collective-permute-done((bf16[1536,384]{1,0:T(8,128)(2,1)S(1)}, bf16[1536,384]{1,0:T(8,128)(2,1)S(1)}, u32[]{:S(2)}, u32[]{:S(2)}) %collective-permute-start.30) | collective-permute-done | bytes 1179680 | tf_op jit(solution)/shard_map/ppermute | solution.py:460
  980.5 16.0 %collective-permute-done.32 = bf16[384,768]{1,0:T(8,128)(2,1)} collective-permute-done((bf16[384,768]{1,0:T(8,128)(2,1)S(1)}, bf16[384,768]{1,0:T(8,128)(2,1)}, u32[]{:S(2)}, u32[]{:S(2)}) %collective-permute-start.32) | collective-permute-done | bytes 589856 | tf_op jit(solution)/shard_map/ppermute | solution.py:460
  996.6 20.8 %collective-permute-done.33 = bf16[384,768]{1,0:T(8,128)(2,1)} collective-permute-done((bf16[384,768]{1,0:T(8,128)(2,1)S(1)}, bf16[384,768]{1,0:T(8,128)(2,1)}, u32[]{:S(2)}, u32[]{:S(2)}) %collective-permute-start.33) | collective-permute-done | bytes 589856 | tf_op jit(solution)/shard_map/ppermute | solution.py:460
  1017.4 2.6 collective-permute-start.37
  1020.0 2.1 collective-permute-done.37
  1022.1 4.1 collective-permute-start.38
  1026.2 3.6 copy.131
  1030.5 2.3 add_convert_fusion.1
  1035.3 2.4 add_convert_fusion
  1041.8 2.3 copy.132
  1045.6 20.6 %collective-permute-done.39 = bf16[1536,384]{1,0:T(8,128)(2,1)} collective-permute-done((bf16[1536,384]{1,0:T(8,128)(2,1)}, bf16[1536,384]{1,0:T(8,128)(2,1)}, u32[]{:S(2)}, u32[]{:S(2)}) %collective-permute-start.39) | collective-permute-done | bytes 1179680 | tf_op jit(solution)/shard_map/ppermute | solution.py:460
  1085.2 4.2 collective-permute-done.41
  1089.4 36.1 %collective-permute-done.42 = bf16[384,768]{1,0:T(8,128)(2,1)} collective-permute-done((bf16[384,768]{1,0:T(8,128)(2,1)}, bf16[384,768]{1,0:T(8,128)(2,1)}, u32[]{:S(2)}, u32[]{:S(2)}) %collective-permute-start.42) | collective-permute-done | bytes 589856 | tf_op jit(solution)/shard_map/ppermute | solution.py:460
  (459 shorter events, 139.4 us)
Async XLA Ops:
  7.2 218.2 %all-gather.3.cloned.1.call-start = ((), (), s32[]{:S(2)}) async-start(), calls=%async_computation.1 | async-start | bytes 38928384 | tf_op jit(solution)/shard_map/all_gather | solution.py:1023
  9.7 453.3 %all-gather.5.cloned.1.call-start = ((), (), s32[]{:S(2)}) async-start(), calls=%async_computation.2 | async-start | bytes 38928384 | tf_op jit(solution)/shard_map/all_gather | solution.py:1023
  11.9 1005.5 %reduce-scatter.2.cloned.1.call-start = ((), (), s32[]{:S(2)}) async-start(), calls=%async_computation.3 | async-start | bytes 13369344 | tf_op jit(solution)/shard_map/reduce_scatter | solution.py:1120
  14.4 283.9 %copy-start.49 = (f32[1,512,1472]{2,1,0:T(8,128)}, f32[1,512,1472]{2,1,0:T(8,128)S(1)}, u32[]{:S(2)}) copy-start(f32[1,512,1472]{2,1,0:T(8,128)S(1)} %copy.116) | copy-start | bytes 9043972
  15.1 286.3 %copy-start.94 = (f32[1472]{0:T(1024)}, f32[1472]{0:T(1024)S(1)}, u32[]{:S(2)}) copy-start(f32[1472]{0:T(1024)S(1)} %get-tuple-element.451) | copy-start | bytes 17668
  15.1 313.0 %copy-start.98 = (f32[1472]{0:T(1024)}, f32[1472]{0:T(1024)S(1)}, u32[]{:S(2)}) copy-start(f32[1472]{0:T(1024)S(1)} %get-tuple-element.453) | copy-start | bytes 17668
  16.0 214.1 %copy-start.114 = (f32[512]{0:T(512)}, f32[512]{0:T(512)S(1)}, u32[]{:S(2)}) copy-start(f32[512]{0:T(512)S(1)} %get-tuple-element.519) | copy-start | bytes 6148
  17.5 223.0 %copy-start.123 = (f32[32,6]{0,1:T(8,128)S(1)}, f32[32,6]{0,1:T(8,128)}, u32[]{:S(2)}) copy-start(f32[32,6]{0,1:T(8,128)} %param.13) | copy-start | bytes 2308
  232.1 41.1 %collective-permute-start = (bf16[288,768]{1,0:T(8,128)(2,1)}, bf16[288,768]{1,0:T(8,128)(2,1)}, u32[]{:S(2)}, u32[]{:S(2)}) collective-permute-start(bf16[288,768]{1,0:T(8,128)(2,1)} %slice_select_fusion.1), channel_id=1, source_target_pairs={{0,2},{1,3},{2,0},{3,1},{4,6},{5,7},{6,4},{7,5},{8,10},{9,11},{10,... | collective-permute-start | bytes 1327112 | tf_op jit(solution)/shard_map/ppermute | solution.py:474
  232.7 55.9 %collective-permute-start.1 = (bf16[512,768]{1,0:T(8,128)(2,1)}, bf16[512,768]{1,0:T(8,128)(2,1)}, u32[]{:S(2)}, u32[]{:S(2)}) collective-permute-start(bf16[512,768]{1,0:T(8,128)(2,1)} %slice.177), channel_id=1, source_target_pairs={{0,1},{1,2},{2,3},{4,5},{5,6},{6,7},{8,9},{9,10},{10,11},{12,13},{... | collective-permute-start | bytes 2359304 | tf_op jit(solution)/shard_map/ppermute | solution.py:466
  234.5 55.4 %collective-permute-start.2 = (bf16[512,768]{1,0:T(8,128)(2,1)}, bf16[512,768]{1,0:T(8,128)(2,1)}, u32[]{:S(2)}, u32[]{:S(2)}) collective-permute-start(bf16[512,768]{1,0:T(8,128)(2,1)} %slice.177), channel_id=1, source_target_pairs={{1,0},{2,1},{3,2},{5,4},{6,5},{7,6},{9,8},{10,9},{11,10},{13,12},{... | collective-permute-start | bytes 2359304 | tf_op jit(solution)/shard_map/ppermute | solution.py:466
  249.5 40.3 %copy-start.69 = (bf16[512,1152]{1,0:T(8,128)(2,1)S(1)}, bf16[512,1152]{1,0:T(8,128)(2,1)}, u32[]{:S(2)}) copy-start(bf16[512,1152]{1,0:T(8,128)(2,1)} %copy-done.68) | copy-start | bytes 3538948
  250.6 40.8 %copy-start.41 = (bf16[512,384]{1,0:T(8,128)(2,1)}, bf16[512,384]{1,0:T(8,128)(2,1)S(1)}, u32[]{:S(2)}) copy-start(bf16[512,384]{1,0:T(8,128)(2,1)S(1)} %slice.174.refs_0_) | copy-start | bytes 1179652
  328.1 139.7 %copy-start.111 = (f32[512]{0:T(512)}, f32[512]{0:T(512)S(1)}, u32[]{:S(2)}) copy-start(f32[512]{0:T(512)S(1)} %get-tuple-element.523) | copy-start | bytes 6148
  330.4 137.4 %copy-start.113 = (f32[512]{0:T(512)}, f32[512]{0:T(512)S(1)}, u32[]{:S(2)}) copy-start(f32[512]{0:T(512)S(1)} %get-tuple-element.465) | copy-start | bytes 6148
  470.0 52.7 %collective-permute-start.5 = (bf16[512,896]{1,0:T(8,128)(2,1)}, bf16[512,896]{1,0:T(8,128)(2,1)}, u32[]{:S(2)}, u32[]{:S(2)}) collective-permute-start(bf16[512,896]{1,0:T(8,128)(2,1)} %pad_maximum_fusion.2), channel_id=1, source_target_pairs={{1,0},{2,1},{3,2},{5,4},{6,5},{7,6},{9,8},{10,9},{11,10},{13,12},{... | collective-permute-start | bytes 2752520 | tf_op jit(solution)/shard_map/ppermute | solution.py:466
  474.5 46.6 %collective-permute-start.4 = (bf16[512,896]{1,0:T(8,128)(2,1)}, bf16[512,896]{1,0:T(8,128)(2,1)}, u32[]{:S(2)}, u32[]{:S(2)}) collective-permute-start(bf16[512,896]{1,0:T(8,128)(2,1)} %pad_maximum_fusion.2), channel_id=1, source_target_pairs={{0,1},{1,2},{2,3},{4,5},{5,6},{6,7},{8,9},{9,10},{10,11},{12,13},{... | collective-permute-start | bytes 2752520 | tf_op jit(solution)/shard_map/ppermute | solution.py:466
  476.1 43.8 %collective-permute-start.3 = (bf16[288,896]{1,0:T(8,128)(2,1)}, bf16[288,896]{1,0:T(8,128)(2,1)}, u32[]{:S(2)}, u32[]{:S(2)}) collective-permute-start(bf16[288,896]{1,0:T(8,128)(2,1)} %fusion.44), channel_id=1, source_target_pairs={{0,2},{1,3},{2,0},{3,1},{4,6},{5,7},{6,4},{7,5},{8,10},{9,11},{10,... | collective-permute-start | bytes 1548296 | tf_op jit(solution)/shard_map/ppermute | solution.py:474
  478.7 43.9 %copy-start.61 = (bf16[512,768]{1,0:T(8,128)(2,1)S(1)}, bf16[512,768]{1,0:T(8,128)(2,1)}, u32[]{:S(2)}) copy-start(bf16[512,768]{1,0:T(8,128)(2,1)} %copy-done.60) | copy-start | bytes 2359300
  480.4 43.8 %copy-start.38 = (bf16[512,384]{1,0:T(8,128)(2,1)}, bf16[512,384]{1,0:T(8,128)(2,1)S(1)}, u32[]{:S(2)}) copy-start(bf16[512,384]{1,0:T(8,128)(2,1)S(1)} %slice.180.refs_0_) | copy-start | bytes 1179652
  593.7 68.3 %collective-permute-start.6 = (bf16[6144,512]{1,0:T(8,128)(2,1)}, bf16[6144,512]{1,0:T(8,128)(2,1)}, u32[]{:S(2)}, u32[]{:S(2)}) collective-permute-start(bf16[6144,512]{1,0:T(8,128)(2,1)} %get-tuple-element.212), channel_id=1, source_target_pairs={{0,4},{4,0},{1,5},{5,1},{2,6},{6,2},{3,7},{7,3},{8,12},{12,8},{9,1... | collective-permute-start | bytes 18874376 | tf_op jit(solution)/shard_map/ppermute | solution.py:460
  597.5 63.3 %collective-permute-start.7 = (bf16[1024,1536]{1,0:T(8,128)(2,1)S(1)}, bf16[1024,1536]{1,0:T(8,128)(2,1)S(1)}, u32[]{:S(2)}, u32[]{:S(2)}) collective-permute-start(bf16[1024,1536]{1,0:T(8,128)(2,1)S(1)} %fusion.11.refs_2_.refs_3_), channel_id=1, source_target_pairs={{0,4},{4,0},{1,5},{5,1},{2,6},{6,2},{3,7},{7,3},{8,12},{12,8},{9,1... | collective-permute-start | bytes 9437192 | tf_op jit(solution)/shard_map/ppermute | solution.py:460
  637.0 52.1 %copy-start.40 = (bf16[512,384]{1,0:T(8,128)(2,1)}, bf16[512,384]{1,0:T(8,128)(2,1)S(1)}, u32[]{:S(2)}) copy-start(bf16[512,384]{1,0:T(8,128)(2,1)S(1)} %get-tuple-element.208) | copy-start | bytes 1179652
  638.5 46.1 %collective-permute-start.10 = (bf16[288,896]{1,0:T(8,128)(2,1)S(1)}, bf16[288,896]{1,0:T(8,128)(2,1)S(1)}, u32[]{:S(2)}, u32[]{:S(2)}) collective-permute-start(bf16[288,896]{1,0:T(8,128)(2,1)S(1)} %slice_select_fusion), channel_id=1, source_target_pairs={{0,2},{1,3},{2,0},{3,1},{4,6},{5,7},{6,4},{7,5},{8,10},{9,11},{10,... | collective-permute-start | bytes 1548296 | tf_op jit(solution)/shard_map/ppermute | solution.py:474
  652.9 35.5 %collective-permute-start.9 = (bf16[512,896]{1,0:T(8,128)(2,1)S(1)}, bf16[512,896]{1,0:T(8,128)(2,1)S(1)}, u32[]{:S(2)}, u32[]{:S(2)}) collective-permute-start(bf16[512,896]{1,0:T(8,128)(2,1)S(1)} %get-tuple-element.466), channel_id=1, source_target_pairs={{0,1},{1,2},{2,3},{4,5},{5,6},{6,7},{8,9},{9,10},{10,11},{12,13},{... | collective-permute-start | bytes 2752520 | tf_op jit(solution)/shard_map/ppermute | solution.py:466
  654.2 34.2 %collective-permute-start.8 = (bf16[512,896]{1,0:T(8,128)(2,1)S(1)}, bf16[512,896]{1,0:T(8,128)(2,1)S(1)}, u32[]{:S(2)}, u32[]{:S(2)}) collective-permute-start(bf16[512,896]{1,0:T(8,128)(2,1)S(1)} %get-tuple-element.467), channel_id=1, source_target_pairs={{1,0},{2,1},{3,2},{5,4},{6,5},{7,6},{9,8},{10,9},{11,10},{13,12},{... | collective-permute-start | bytes 2752520 | tf_op jit(solution)/shard_map/ppermute | solution.py:466
  660.8 36.5 %collective-permute-start.12 = (bf16[1024,1536]{1,0:T(8,128)(2,1)}, bf16[1024,1536]{1,0:T(8,128)(2,1)}, u32[]{:S(2)}, u32[]{:S(2)}) collective-permute-start(bf16[1024,1536]{1,0:T(8,128)(2,1)} %fusion.12.refs_2_.refs_3_), channel_id=1, source_target_pairs={{0,4},{4,0},{1,5},{5,1},{2,6},{6,2},{3,7},{7,3},{8,12},{12,8},{9,1... | collective-permute-start | bytes 9437192 | tf_op jit(solution)/shard_map/ppermute | solution.py:460
  691.0 6.3 collective-permute-start.11
  717.0 46.2 %collective-permute-start.13 = (bf16[3072,256]{1,0:T(8,128)(2,1)}, bf16[3072,256]{1,0:T(8,128)(2,1)S(1)}, u32[]{:S(2)}, u32[]{:S(2)}) collective-permute-start(bf16[3072,256]{1,0:T(8,128)(2,1)} %copy-done.32), channel_id=1, source_target_pairs={{0,16},{16,0},{1,17},{17,1},{2,18},{18,2},{3,19},{19,3},{4,20},{20... | collective-permute-start | bytes 4718600 | tf_op jit(solution)/shard_map/ppermute | solution.py:460
  720.1 43.2 %collective-permute-start.14 = (bf16[3072,256]{1,0:T(8,128)(2,1)}, bf16[3072,256]{1,0:T(8,128)(2,1)S(1)}, u32[]{:S(2)}, u32[]{:S(2)}) collective-permute-start(bf16[3072,256]{1,0:T(8,128)(2,1)} %copy-done.35), channel_id=1, source_target_pairs={{0,8},{8,0},{1,9},{9,1},{2,10},{10,2},{3,11},{11,3},{4,12},{12,4},... | collective-permute-start | bytes 4718600 | tf_op jit(solution)/shard_map/ppermute | solution.py:460
  730.3 34.6 %copy-start.22 = (bf16[3072,256]{1,0:T(8,128)(2,1)S(1)}, bf16[3072,256]{1,0:T(8,128)(2,1)}, u32[]{:S(2)}) copy-start(bf16[3072,256]{1,0:T(8,128)(2,1)} %copy-done.21) | copy-start | bytes 4718596
  769.9 54.9 %collective-permute-start.17 = (bf16[6144,512]{1,0:T(8,128)(2,1)}, bf16[6144,512]{1,0:T(8,128)(2,1)}, u32[]{:S(2)}, u32[]{:S(2)}) collective-permute-start(bf16[6144,512]{1,0:T(8,128)(2,1)} %get-tuple-element.275), channel_id=1, source_target_pairs={{0,4},{4,0},{1,5},{5,1},{2,6},{6,2},{3,7},{7,3},{8,12},{12,8},{9,1... | collective-permute-start | bytes 18874376 | tf_op jit(solution)/shard_map/ppermute | solution.py:460
  772.6 46.7 %collective-permute-start.18 = (bf16[1024,1536]{1,0:T(8,128)(2,1)}, bf16[1024,1536]{1,0:T(8,128)(2,1)}, u32[]{:S(2)}, u32[]{:S(2)}) collective-permute-start(bf16[1024,1536]{1,0:T(8,128)(2,1)} %fusion.13.refs_2_.refs_3_), channel_id=1, source_target_pairs={{0,4},{4,0},{1,5},{5,1},{2,6},{6,2},{3,7},{7,3},{8,12},{12,8},{9,1... | collective-permute-start | bytes 9437192 | tf_op jit(solution)/shard_map/ppermute | solution.py:460
  772.6 30.1 %collective-permute-start.15 = (bf16[1536,256]{1,0:T(8,128)(2,1)}, bf16[1536,256]{1,0:T(8,128)(2,1)S(1)}, u32[]{:S(2)}, u32[]{:S(2)}) collective-permute-start(bf16[1536,256]{1,0:T(8,128)(2,1)} %get-tuple-element.255), channel_id=1, source_target_pairs={{0,8},{8,0},{1,9},{9,1},{2,10},{10,2},{3,11},{11,3},{4,12},{12,4},... | collective-permute-start | bytes 2359304 | tf_op jit(solution)/shard_map/ppermute | solution.py:460
  774.8 28.0 %collective-permute-start.16 = (bf16[1536,256]{1,0:T(8,128)(2,1)}, bf16[1536,256]{1,0:T(8,128)(2,1)S(1)}, u32[]{:S(2)}, u32[]{:S(2)}) collective-permute-start(bf16[1536,256]{1,0:T(8,128)(2,1)} %get-tuple-element.257), channel_id=1, source_target_pairs={{0,16},{16,0},{1,17},{17,1},{2,18},{18,2},{3,19},{19,3},{4,20},{20... | collective-permute-start | bytes 2359304 | tf_op jit(solution)/shard_map/ppermute | solution.py:460
  779.0 80.2 %collective-permute-start.23 = (bf16[1024,1536]{1,0:T(8,128)(2,1)S(1)}, bf16[1024,1536]{1,0:T(8,128)(2,1)S(1)}, u32[]{:S(2)}, u32[]{:S(2)}) collective-permute-start(bf16[1024,1536]{1,0:T(8,128)(2,1)S(1)} %fusion.14.refs_2_.refs_3_), channel_id=1, source_target_pairs={{0,4},{4,0},{1,5},{5,1},{2,6},{6,2},{3,7},{7,3},{8,12},{12,8},{9,1... | collective-permute-start | bytes 9437192 | tf_op jit(solution)/shard_map/ppermute | solution.py:460
  806.6 42.9 %collective-permute-start.21 = (bf16[288,768]{1,0:T(8,128)(2,1)S(1)}, bf16[288,768]{1,0:T(8,128)(2,1)S(1)}, u32[]{:S(2)}, u32[]{:S(2)}) collective-permute-start(bf16[288,768]{1,0:T(8,128)(2,1)S(1)} %slice_select_fusion.2), channel_id=1, source_target_pairs={{0,2},{1,3},{2,0},{3,1},{4,6},{5,7},{6,4},{7,5},{8,10},{9,11},{10,... | collective-permute-start | bytes 1327112 | tf_op jit(solution)/shard_map/ppermute | solution.py:474
  818.0 31.5 %collective-permute-start.20 = (bf16[512,768]{1,0:T(8,128)(2,1)S(1)}, bf16[512,768]{1,0:T(8,128)(2,1)}, u32[]{:S(2)}, u32[]{:S(2)}) collective-permute-start(bf16[512,768]{1,0:T(8,128)(2,1)S(1)} %get-tuple-element.469), channel_id=1, source_target_pairs={{0,1},{1,2},{2,3},{4,5},{5,6},{6,7},{8,9},{9,10},{10,11},{12,13},{... | collective-permute-start | bytes 2359304 | tf_op jit(solution)/shard_map/ppermute | solution.py:466
  819.3 30.2 %collective-permute-start.19 = (bf16[512,768]{1,0:T(8,128)(2,1)S(1)}, bf16[512,768]{1,0:T(8,128)(2,1)}, u32[]{:S(2)}, u32[]{:S(2)}) collective-permute-start(bf16[512,768]{1,0:T(8,128)(2,1)S(1)} %get-tuple-element.470), channel_id=1, source_target_pairs={{1,0},{2,1},{3,2},{5,4},{6,5},{7,6},{9,8},{10,9},{11,10},{13,12},{... | collective-permute-start | bytes 2359304 | tf_op jit(solution)/shard_map/ppermute | solution.py:466
  853.5 7.5 collective-permute-start.22
  875.5 64.7 %collective-permute-start.24 = (bf16[3072,384]{1,0:T(8,128)(2,1)}, bf16[3072,384]{1,0:T(8,128)(2,1)}, u32[]{:S(2)}, u32[]{:S(2)}) collective-permute-start(bf16[3072,384]{1,0:T(8,128)(2,1)} %get-tuple-element.315), channel_id=1, source_target_pairs={{0,16},{16,0},{1,17},{17,1},{2,18},{18,2},{3,19},{19,3},{4,20},{20... | collective-permute-start | bytes 7077896 | tf_op jit(solution)/shard_map/ppermute | solution.py:460
  876.4 63.8 %collective-permute-start.25 = (bf16[3072,384]{1,0:T(8,128)(2,1)}, bf16[3072,384]{1,0:T(8,128)(2,1)}, u32[]{:S(2)}, u32[]{:S(2)}) collective-permute-start(bf16[3072,384]{1,0:T(8,128)(2,1)} %get-tuple-element.317), channel_id=1, source_target_pairs={{0,8},{8,0},{1,9},{9,1},{2,10},{10,2},{3,11},{11,3},{4,12},{12,4},... | collective-permute-start | bytes 7077896 | tf_op jit(solution)/shard_map/ppermute | solution.py:460
  885.9 3.5 collective-permute-start.29
  885.9 12.0 %collective-permute-start.26 = (bf16[384,512]{1,0:T(8,128)(2,1)}, bf16[384,512]{1,0:T(8,128)(2,1)S(1)}, u32[]{:S(2)}, u32[]{:S(2)}) collective-permute-start(bf16[384,512]{1,0:T(8,128)(2,1)} %pad_maximum_fusion.16), channel_id=1, source_target_pairs={{0,1},{1,2},{2,3},{3,0},{4,5},{5,6},{6,7},{7,4},{8,9},{9,10},{10,1... | collective-permute-start | bytes 1179656 | tf_op jit(solution)/shard_map/ppermute | solution.py:460
  885.9 51.1 %collective-permute-start.27 = (bf16[384,512]{1,0:T(8,128)(2,1)}, bf16[384,512]{1,0:T(8,128)(2,1)S(1)}, u32[]{:S(2)}, u32[]{:S(2)}) collective-permute-start(bf16[384,512]{1,0:T(8,128)(2,1)} %pad_maximum_fusion.17), channel_id=1, source_target_pairs={{0,2},{1,3},{2,0},{3,1},{4,6},{5,7},{6,4},{7,5},{8,10},{9,11},{10,... | collective-permute-start | bytes 1179656 | tf_op jit(solution)/shard_map/ppermute | solution.py:460
  889.4 47.6 %collective-permute-start.28 = (bf16[384,512]{1,0:T(8,128)(2,1)}, bf16[384,512]{1,0:T(8,128)(2,1)S(1)}, u32[]{:S(2)}, u32[]{:S(2)}) collective-permute-start(bf16[384,512]{1,0:T(8,128)(2,1)} %pad_maximum_fusion.18), channel_id=1, source_target_pairs={{0,3},{1,0},{2,1},{3,2},{4,7},{5,4},{6,5},{7,6},{8,11},{9,8},{10,9... | collective-permute-start | bytes 1179656 | tf_op jit(solution)/shard_map/ppermute | solution.py:460
  897.9 44.7 %copy-start.89 = (bf16[384,512]{1,0:T(8,128)(2,1)}, bf16[384,512]{1,0:T(8,128)(2,1)S(1)}, u32[]{:S(2)}) copy-start(bf16[384,512]{1,0:T(8,128)(2,1)S(1)} %collective-permute-done.26) | copy-start | bytes 1179652
  946.8 29.0 %collective-permute-start.30 = (bf16[1536,384]{1,0:T(8,128)(2,1)S(1)}, bf16[1536,384]{1,0:T(8,128)(2,1)S(1)}, u32[]{:S(2)}, u32[]{:S(2)}) collective-permute-start(bf16[1536,384]{1,0:T(8,128)(2,1)S(1)} %get-tuple-element.331), channel_id=1, source_target_pairs={{0,8},{8,0},{1,9},{9,1},{2,10},{10,2},{3,11},{11,3},{4,12},{12,4},... | collective-permute-start | bytes 3538952 | tf_op jit(solution)/shard_map/ppermute | solution.py:460
  946.9 29.0 %collective-permute-start.31 = (bf16[1536,384]{1,0:T(8,128)(2,1)S(1)}, bf16[1536,384]{1,0:T(8,128)(2,1)S(1)}, u32[]{:S(2)}, u32[]{:S(2)}) collective-permute-start(bf16[1536,384]{1,0:T(8,128)(2,1)S(1)} %get-tuple-element.333), channel_id=1, source_target_pairs={{0,16},{16,0},{1,17},{17,1},{2,18},{18,2},{3,19},{19,3},{4,20},{20... | collective-permute-start | bytes 3538952 | tf_op jit(solution)/shard_map/ppermute | solution.py:460
  947.3 83.2 %collective-permute-start.35 = (bf16[3072,384]{1,0:T(8,128)(2,1)}, bf16[3072,384]{1,0:T(8,128)(2,1)}, u32[]{:S(2)}, u32[]{:S(2)}) collective-permute-start(bf16[3072,384]{1,0:T(8,128)(2,1)} %get-tuple-element.356), channel_id=1, source_target_pairs={{0,16},{16,0},{1,17},{17,1},{2,18},{18,2},{3,19},{19,3},{4,20},{20... | collective-permute-start | bytes 7077896 | tf_op jit(solution)/shard_map/ppermute | solution.py:460
  948.9 81.5 %collective-permute-start.36 = (bf16[3072,384]{1,0:T(8,128)(2,1)}, bf16[3072,384]{1,0:T(8,128)(2,1)}, u32[]{:S(2)}, u32[]{:S(2)}) collective-permute-start(bf16[3072,384]{1,0:T(8,128)(2,1)} %get-tuple-element.358), channel_id=1, source_target_pairs={{0,8},{8,0},{1,9},{9,1},{2,10},{10,2},{3,11},{11,3},{4,12},{12,4},... | collective-permute-start | bytes 7077896 | tf_op jit(solution)/shard_map/ppermute | solution.py:460
  976.6 40.8 %copy-start.92 = (f32[6,1472]{1,0:T(8,128)S(1)}, f32[6,1472]{1,0:T(8,128)}, u32[]{:S(2)}) copy-start(f32[6,1472]{1,0:T(8,128)} %add.457) | copy-start | bytes 105988
  977.8 18.8 %collective-permute-start.32 = (bf16[384,768]{1,0:T(8,128)(2,1)S(1)}, bf16[384,768]{1,0:T(8,128)(2,1)}, u32[]{:S(2)}, u32[]{:S(2)}) collective-permute-start(bf16[384,768]{1,0:T(8,128)(2,1)S(1)} %pad_maximum_fusion.8), channel_id=1, source_target_pairs={{0,1},{1,2},{2,3},{3,0},{4,5},{5,6},{6,7},{7,4},{8,9},{9,10},{10,1... | collective-permute-start | bytes 1769480 | tf_op jit(solution)/shard_map/ppermute | solution.py:460
  978.0 39.4 %collective-permute-start.33 = (bf16[384,768]{1,0:T(8,128)(2,1)S(1)}, bf16[384,768]{1,0:T(8,128)(2,1)}, u32[]{:S(2)}, u32[]{:S(2)}) collective-permute-start(bf16[384,768]{1,0:T(8,128)(2,1)S(1)} %pad_maximum_fusion.9), channel_id=1, source_target_pairs={{0,2},{1,3},{2,0},{3,1},{4,6},{5,7},{6,4},{7,5},{8,10},{9,11},{10,... | collective-permute-start | bytes 1769480 | tf_op jit(solution)/shard_map/ppermute | solution.py:460
  979.2 38.2 %collective-permute-start.34 = (bf16[384,768]{1,0:T(8,128)(2,1)S(1)}, bf16[384,768]{1,0:T(8,128)(2,1)}, u32[]{:S(2)}, u32[]{:S(2)}) collective-permute-start(bf16[384,768]{1,0:T(8,128)(2,1)S(1)} %pad_maximum_fusion.10), channel_id=1, source_target_pairs={{0,3},{1,0},{2,1},{3,2},{4,7},{5,4},{6,5},{7,6},{8,11},{9,8},{10,9... | collective-permute-start | bytes 1769480 | tf_op jit(solution)/shard_map/ppermute | solution.py:460
  1017.4 4.7 collective-permute-start.37
  1022.1 7.7 collective-permute-start.38
  1039.4 26.8 %collective-permute-start.39 = (bf16[1536,384]{1,0:T(8,128)(2,1)}, bf16[1536,384]{1,0:T(8,128)(2,1)}, u32[]{:S(2)}, u32[]{:S(2)}) collective-permute-start(bf16[1536,384]{1,0:T(8,128)(2,1)} %get-tuple-element.368), channel_id=1, source_target_pairs={{0,8},{8,0},{1,9},{9,1},{2,10},{10,2},{3,11},{11,3},{4,12},{12,4},... | collective-permute-start | bytes 3538952 | tf_op jit(solution)/shard_map/ppermute | solution.py:460
  1040.8 26.5 %collective-permute-start.40 = (bf16[1536,384]{1,0:T(8,128)(2,1)}, bf16[1536,384]{1,0:T(8,128)(2,1)}, u32[]{:S(2)}, u32[]{:S(2)}) collective-permute-start(bf16[1536,384]{1,0:T(8,128)(2,1)} %get-tuple-element.370), channel_id=1, source_target_pairs={{0,16},{16,0},{1,17},{17,1},{2,18},{18,2},{3,19},{19,3},{4,20},{20... | collective-permute-start | bytes 3538952 | tf_op jit(solution)/shard_map/ppermute | solution.py:460
  1074.3 5.0 collective-permute-start.44
  1074.9 14.5 %collective-permute-start.41 = (bf16[384,768]{1,0:T(8,128)(2,1)}, bf16[384,768]{1,0:T(8,128)(2,1)}, u32[]{:S(2)}, u32[]{:S(2)}) collective-permute-start(bf16[384,768]{1,0:T(8,128)(2,1)} %pad_maximum_fusion.12), channel_id=1, source_target_pairs={{0,1},{1,2},{2,3},{3,0},{4,5},{5,6},{6,7},{7,4},{8,9},{9,10},{10,1... | collective-permute-start | bytes 1769480 | tf_op jit(solution)/shard_map/ppermute | solution.py:460
  1075.3 50.2 %collective-permute-start.42 = (bf16[384,768]{1,0:T(8,128)(2,1)}, bf16[384,768]{1,0:T(8,128)(2,1)}, u32[]{:S(2)}, u32[]{:S(2)}) collective-permute-start(bf16[384,768]{1,0:T(8,128)(2,1)} %pad_maximum_fusion.13), channel_id=1, source_target_pairs={{0,2},{1,3},{2,0},{3,1},{4,6},{5,7},{6,4},{7,5},{8,10},{9,11},{10,... | collective-permute-start | bytes 1769480 | tf_op jit(solution)/shard_map/ppermute | solution.py:460
  1076.7 48.8 %collective-permute-start.43 = (bf16[384,768]{1,0:T(8,128)(2,1)}, bf16[384,768]{1,0:T(8,128)(2,1)}, u32[]{:S(2)}, u32[]{:S(2)}) collective-permute-start(bf16[384,768]{1,0:T(8,128)(2,1)} %pad_maximum_fusion.14), channel_id=1, source_target_pairs={{0,3},{1,0},{2,1},{3,2},{4,7},{5,4},{6,5},{7,6},{8,11},{9,8},{10,9... | collective-permute-start | bytes 1769480 | tf_op jit(solution)/shard_map/ppermute | solution.py:460
  1079.9 4.4 collective-permute-start.45
  (111 other events, 713.6 us)
Sparse Core Ops, SparseCore 0:
  11.4 213.9 all-gather.2
  228.8 234.2 all-gather.4
  717.1 225.5 reduce-scatter.1

commit v11 on v10

--- a/solution.py
+++ b/solution.py
@@ -570,92 +570,124 @@
     return active, 0.5 * (1.0 + slope) + 0.5 * values * (1.0 - slope * slope) * inner
 
 
-def ffn_forward_body(normed_ref, middle_ref, gelu_ref, linear_ref, down_ref, *outs):
-    result_ref, up_gelu_ref, up_linear_ref = outs
-
-    @pl.when(pl.program_id(0) == 0)
+def turned_rows(core_ref, kept_ref, sent_ref, stage_ref, sems):
+    mine, unit = core_ref[0], core_ref[1]
+    parts = FORWARD_TILE // TILE
+
+    def copy(lane, part, place, at, where):
+        spot = pl.ds(pl.multiple_of(at * TILE, TILE), TILE)
+        source = stage_ref.at[where, lane, part * TILE : (part + 1) * TILE, :]
+        return pltpu.make_async_copy(source, place.at[spot, :], sems.at[where, lane, part])
+
+    def put(lane, kind, step, turned):
+        slot = step % 2
+        stage_ref[slot, lane] = turned
+        for part in range(parts):
+            target = ATTENTION_TILES + kind * (FF // TILE) + step * parts + part
+            own = (target // unit) % 2 == mine
+            at = (target // (2 * unit)) * unit + target % unit
+
+            @pl.when(own)
+            def _(part=part, at=at):
+                copy(lane, part, kept_ref, at, slot).start()
+
+            @pl.when(jnp.logical_not(own))
+            def _(part=part, at=at):
+                copy(lane, part, sent_ref, at, slot).start()
+
+    def wait(lanes, where):
+        for lane in range(lanes):
+            for part in range(parts):
+                copy(lane, part, kept_ref, 0, where).wait()
+
+    return put, wait
+
+
+def ffn_forward_body(core_ref, *refs):
+    normed_ref, middle_ref, gelu_ref, linear_ref, down_ref = refs[:5]
+    result_ref, gelu_factor_ref, linear_factor_ref, kept_ref, sent_ref, stage_ref, sems = refs[5:]
+    step = pl.program_id(0)
+    put, wait = turned_rows(core_ref, kept_ref, sent_ref, stage_ref, sems)
+
+    @pl.when(step == 0)
     def _():
         result_ref[...] = middle_ref[...]
 
-    up_gelu = times_rows(normed_ref[...], gelu_ref[...])
-    up_linear = times_rows(normed_ref[...], linear_ref[...])
-    up_gelu_ref[...] = up_gelu
-    up_linear_ref[...] = up_linear
-    hidden = (gelu_tanh(up_gelu) * up_linear).astype(jnp.bfloat16)
+    @pl.when(step >= 2)
+    def _():
+        wait(1, step % 2)
+
+    active, slope = gelu_parts(times_rows(normed_ref[...], gelu_ref[...]))
+    linear = times_rows(normed_ref[...], linear_ref[...])
+    gelu_factor_ref[...] = slope * linear
+    linear_factor_ref[...] = active
+    hidden = (active * linear).astype(jnp.bfloat16)
+    put(0, 2, step, hidden.T)
     result_ref[...] += times_plain(hidden, down_ref[...])
+
+    @pl.when(step == pl.num_programs(0) - 1)
+    def _():
+        wait(1, 0)
+        wait(1, 1)
 
 
 def resident(shape):
     return pl.BlockSpec(shape, lambda *_: (0,) * len(shape), pipeline_mode=pl.Buffered(1))
 
 
+def core_units():
+    return jnp.stack([lax.axis_index("c").astype(jnp.int32), jnp.int32(unit_tiles(TILE))])
+
+
+def hidden_weight(kind, width):
+    first = (4 * INNER + kind * FF) // FORWARD_TILE
+    return pl.BlockSpec((FORWARD_TILE, width), lambda i, *_: (first + i, 0))
+
+
+def turned_scratch(lanes, tokens):
+    return [
+        pltpu.VMEM((2, lanes, FORWARD_TILE, tokens), jnp.bfloat16),
+        pltpu.SemaphoreType.DMA((2, lanes, FORWARD_TILE // TILE)),
+    ]
+
+
 def ffn_forward(normed, middle, gathered):
     tokens, width = normed.shape
-    steps = FF // FORWARD_TILE
-    first = 4 * INNER // FORWARD_TILE
-
-    def weight(kind):
-        return pl.BlockSpec((FORWARD_TILE, width), lambda i: (first + kind * steps + i, 0))
-
-    hidden = pl.BlockSpec((tokens, FORWARD_TILE), lambda i: (0, i))
+    half = (4 * INNER + 3 * FF) // 2
+    hidden = pl.BlockSpec((tokens, FORWARD_TILE), lambda i, *_: (0, i))
+    side = resident((tokens, width))
+    anywhere = pl.BlockSpec(memory_space=pl.ANY)
     return pl.pallas_call(
         ffn_forward_body,
-        grid=(steps,),
-        in_specs=[
-            resident((tokens, width)),
-            resident((tokens, width)),
-            weight(0),
-            weight(1),
-            weight(2),
-        ],
-        out_specs=[resident((tokens, width)), hidden, hidden],
+        grid_spec=pltpu.PrefetchScalarGridSpec(
+            num_scalar_prefetch=1,
+            grid=(FF // FORWARD_TILE,),
+            in_specs=[side, side] + [hidden_weight(kind, width) for kind in range(3)],
+            out_specs=[side, hidden, hidden, anywhere, anywhere],
+            scratch_shapes=turned_scratch(1, tokens),
+        ),
         out_shape=[
             jax.ShapeDtypeStruct((tokens, width), jnp.float32),
             jax.ShapeDtypeStruct((tokens, FF), jnp.float32),
             jax.ShapeDtypeStruct((tokens, FF), jnp.float32),
+            jax.ShapeDtypeStruct((half, tokens), jnp.bfloat16),
+            jax.ShapeDtypeStruct((half, tokens), jnp.bfloat16),
         ],
-        compiler_params=pltpu.CompilerParams(vmem_limit_bytes=48 << 20),
+        compiler_params=pltpu.CompilerParams(vmem_limit_bytes=52 << 20),
         cost_estimate=pl.CostEstimate(
             flops=6 * tokens * FF * width,
-            bytes_accessed=6 * FF * width + 8 * tokens * FF,
+            bytes_accessed=6 * FF * width + 10 * tokens * FF,
             transcendentals=tokens * FF,
         ),
         name="ffn_forward",
-    )(normed, middle, gathered, gathered, gathered)
+    )(core_units(), normed, middle, gathered, gathered, gathered)
 
 
 def ffn_backward_body(core_ref, *refs):
-    branch_ref, normed_ref, up_gelu_ref, up_linear_ref, gelu_ref, linear_ref, down_ref = refs[:7]
-    grad_ref, kept_ref, sent_ref, stage_ref, sems = refs[7:]
+    branch_ref, gelu_factor_ref, linear_factor_ref, gelu_ref, linear_ref, down_ref = refs[:6]
+    grad_ref, kept_ref, sent_ref, stage_ref, sems = refs[8:]
     step = pl.program_id(0)
-    slot = step % 2
-    mine, unit = core_ref[0], core_ref[1]
-    parts = FORWARD_TILE // TILE
-
-    def copy(kind, part, place, at, where):
-        spot = pl.ds(pl.multiple_of(at * TILE, TILE), TILE)
-        source = stage_ref.at[where, kind, part * TILE : (part + 1) * TILE, :]
-        return pltpu.make_async_copy(source, place.at[spot, :], sems.at[where, kind, part])
-
-    def wait(where):
-        for kind in range(3):
-            for part in range(parts):
-                copy(kind, part, kept_ref, 0, where).wait()
-
-    def put(kind, turned):
-        stage_ref[slot, kind] = turned
-        for part in range(parts):
-            target = ATTENTION_TILES + kind * (FF // TILE) + step * parts + part
-            own = (target // unit) % 2 == mine
-            at = (target // (2 * unit)) * unit + target % unit
-
-            @pl.when(own)
-            def _(part=part, at=at):
-                copy(kind, part, kept_ref, at, slot).start()
-
-            @pl.when(jnp.logical_not(own))
-            def _(part=part, at=at):
-                copy(kind, part, sent_ref, at, slot).start()
+    put, wait = turned_rows(core_ref, kept_ref, sent_ref, stage_ref, sems)
 
     @pl.when(step == 0)
     def _():
@@ -663,24 +695,21 @@
 
     @pl.when(step >= 2)
     def _():
-        wait(slot)
+        wait(2, step % 2)
 
     grad_hidden = times_rows(branch_ref[...], down_ref[...])
-    active, slope = gelu_parts(up_gelu_ref[...])
-    linear = up_linear_ref[...]
-    grad_gelu = (grad_hidden * linear * slope).astype(jnp.bfloat16)
-    grad_linear = (grad_hidden * active).astype(jnp.bfloat16)
-    put(2, (active * linear).astype(jnp.bfloat16).T)
-    put(0, grad_gelu.T)
-    put(1, grad_linear.T)
+    grad_gelu = (grad_hidden * gelu_factor_ref[...]).astype(jnp.bfloat16)
+    grad_linear = (grad_hidden * linear_factor_ref[...]).astype(jnp.bfloat16)
+    put(0, 0, step, grad_gelu.T)
+    put(1, 1, step, grad_linear.T)
     grad_ref[...] += times_plain(grad_gelu, gelu_ref[...]) + times_plain(
         grad_linear, linear_ref[...]
     )
 
     @pl.when(step == pl.num_programs(0) - 1)
     def _():
-        wait(0)
-        wait(1)
+        wait(2, 0)
+        wait(2, 1)
 
 
 def unit_tiles(tile):
@@ -688,16 +717,8 @@
     return rows // tile // (2 * lax.axis_size("y") * lax.axis_size("x"))
 
 
-def ffn_backward(branch, normed, up_gelu, up_linear, gathered):
-    tokens, width = normed.shape
-    rows = 4 * INNER + 3 * FF
-    steps = FF // FORWARD_TILE
-    core = jnp.stack([lax.axis_index("c").astype(jnp.int32), jnp.int32(unit_tiles(TILE))])
-
-    def weight(kind):
-        first = 4 * INNER // FORWARD_TILE + kind * steps
-        return pl.BlockSpec((FORWARD_TILE, width), lambda i, *_: (first + i, 0))
-
+def ffn_backward(branch, gelu_factor, linear_factor, gathered, kept, sent):
+    tokens, width = branch.shape
     hidden = pl.BlockSpec((tokens, FORWARD_TILE), lambda i, *_: (0, i))
     side = resident((tokens, width))
     anywhere = pl.BlockSpec(memory_space=pl.ANY)
@@ -705,24 +726,27 @@
         ffn_backward_body,
         grid_spec=pltpu.PrefetchScalarGridSpec(
             num_scalar_prefetch=1,
-            grid=(steps,),
-            in_specs=[side, side, hidden, hidden, weight(0), weight(1), weight(2)],
+            grid=(FF // FORWARD_TILE,),
+            in_specs=[side, hidden, hidden]
+            + [hidden_weight(kind, width) for kind in range(3)]
+            + [anywhere, anywhere],
             out_specs=[side, anywhere, anywhere],
-            scratch_shapes=[
-                pltpu.VMEM((2, 3, FORWARD_TILE, tokens), jnp.bfloat16),
-                pltpu.SemaphoreType.DMA((2, 3, FORWARD_TILE // TILE)),
-            ],
+            scratch_shapes=turned_scratch(2, tokens),
         ),
-        out_shape=[jax.ShapeDtypeStruct((tokens, width), jnp.float32)]
-        + [jax.ShapeDtypeStruct((rows // 2, tokens), jnp.bfloat16)] * 2,
-        compiler_params=pltpu.CompilerParams(vmem_limit_bytes=56 << 20),
+        out_shape=[
+            jax.ShapeDtypeStruct((tokens, width), jnp.float32),
+            jax.ShapeDtypeStruct(kept.shape, kept.dtype),
+            jax.ShapeDtypeStruct(sent.shape, sent.dtype),
+        ],
+        input_output_aliases={7: 1, 8: 2},
+        compiler_params=pltpu.CompilerParams(vmem_limit_bytes=52 << 20),
         cost_estimate=pl.CostEstimate(
             flops=6 * tokens * FF * width,
-            bytes_accessed=6 * FF * width + 14 * tokens * FF,
-            transcendentals=tokens * FF,
+            bytes_accessed=6 * FF * width + 12 * tokens * FF,
+            transcendentals=0,
         ),
         name="ffn_backward",
-    )(core, branch, normed, up_gelu, up_linear, gathered, gathered, gathered)
+    )(core_units(), branch, gelu_factor, linear_factor, gathered, gathered, gathered, kept, sent)
 
 
 def spots_of(unit_at, place_ref):
@@ -882,15 +906,14 @@
 
 
 def attention_fill_body(chunks, owners, place_ref, *refs):
-    own_ref, other_ref, first_ref, second_ref, other_first_ref, other_second_ref = refs[:6]
-    outs = refs[6 + (len(refs) - 8) // 2 : -2]
+    own_ref, other_ref, side_ref, other_side_ref = refs[:4]
+    outs = refs[4 + (len(refs) - 6) // 2 : -2]
     stage_ref, sems = refs[-2:]
     step = pl.program_id(0)
     slot = step % 2
-    tile = jnp.minimum(place_ref[2], owners - 1) * pl.num_programs(0) + step
     start, wait = place_copies(chunks, stage_ref, sems, split_places(outs, chunks), INNER)
 
-    def put(side_ref, other_side_ref):
+    def put():
         product = jnp.dot(
             own_ref[...].T, side_ref[:, : CUTS[-1]], preferred_element_type=jnp.float32
         ) + jnp.dot(
@@ -906,13 +929,7 @@
         def _():
             wait(slot)
 
-        @pl.when(tile < 3)
-        def _():
-            put(first_ref, other_first_ref)
-
-        @pl.when(tile >= 3)
-        def _():
-            put(second_ref, other_second_ref)
+        put()
 
         @pl.when(step == pl.num_programs(0) - 1)
         def _():
@@ -929,7 +946,9 @@
     def column(i, place_ref):
         return 0, jnp.minimum(place_ref[2], owners - 1) * steps + i
 
-    halves = [half_side(tokens, 0), half_side(tokens, 1)]
+    def half(i, place_ref):
+        return jnp.where(column(i, place_ref)[1] < 3, 0, 1), 0
+
     anywhere = pl.BlockSpec(memory_space=pl.ANY)
     return pl.pallas_call(
         functools.partial(attention_fill_body, chunks, owners),
@@ -937,7 +956,7 @@
             num_scalar_prefetch=1,
             grid=(steps,),
             in_specs=[pl.BlockSpec((tokens, INNER), column)] * 2
-            + halves * 2
+            + [pl.BlockSpec((tokens, PADDED), half)] * 2
             + [anywhere] * len(arrays),
             out_specs=[anywhere] * len(arrays),
             scratch_shapes=[
@@ -946,7 +965,7 @@
             ],
         ),
         out_shape=[jax.ShapeDtypeStruct(array.shape, array.dtype) for array in arrays],
-        input_output_aliases={7 + k: k for k in range(len(arrays))},
+        input_output_aliases={5 + k: k for k in range(len(arrays))},
         compiler_params=pltpu.CompilerParams(vmem_limit_bytes=32 << 20),
         cost_estimate=pl.CostEstimate(
             flops=4 * unit_rows * tokens * CUTS[-1],
@@ -954,7 +973,7 @@
             transcendentals=0,
         ),
         name="attention_fill",
-    )(place_of(TILE), own, other, sides[0], sides[0], sides[1], sides[1], *arrays)
+    )(place_of(TILE), own, other, *sides, *arrays)
 
 
 def tied(first, second):
@@ -1036,7 +1055,7 @@
     middle = stream + times_plain(attended, gathered[3 * INNER : 4 * INNER])
     normed_two, inverse_two = rms_forward(middle, gain_two)
     normed_two_low = normed_two.astype(jnp.bfloat16)
-    result, up_gelu, up_linear = ffn_forward(normed_two_low, middle, gathered)
+    result, *factors = ffn_forward(normed_two_low, middle, gathered)
     kept = (
         stream,
         inverse_one,
@@ -1048,8 +1067,7 @@
         middle,
         inverse_two,
         normed_two_low,
-        up_gelu,
-        up_linear,
+        factors,
     )
     return (result, kept)
 
@@ -1066,8 +1084,7 @@
         middle,
         inverse_two,
         normed_two_low,
-        up_gelu,
-        up_linear,
+        factors,
     ) = kept
     tokens = queries.shape[0]
     branch_low = grad_out.astype(jnp.bfloat16)
@@ -1075,7 +1092,7 @@
     sides = jnp.pad(sides, ((0, 0), (0, PADDED - sides.shape[1])))
     sides = (sides, shift(sides, "c", 1))
     grad_normed_two, own, sent = ffn_backward(
-        branch_low, normed_two_low, up_gelu, up_linear, gathered
+        branch_low, factors[0], factors[1], gathered, factors[2], factors[3]
     )
     if before is not None:
         grad_normed_two, own, sent = before.step((grad_normed_two, own, sent), 0, 1)
@@ -1177,10 +1194,10 @@
     small = scatter.start(small, 2, 3)
     small = scatter.step(small, 0, 1)
     small, rest = scatter.settle((small, rest), (0, 1))
+    small = scatter.step(small, 2, 3)
     for bit in range(1, lax.axis_size("z")):
         if bit & (bit - 1) == 0:
             small = hop(small, "z", bit)
-    small = scatter.step(small, 2, 3)
     small = scatter.step(small, 2, 3)
     small = hop(small, "x")
     for bit in range(1, lax.axis_size("y")):

time: 1150 us -> 1150 us (level)
  waiting for transfers between devices: 600 us -> 636 us
  Pallas kernels: 251 us -> 232 us
    ppermute x4, waiting for transfers between devices: 62.1 us -> 97.3 us  [far_pair(): got = lax.ppermute(sent, 'z', pairs)]
    pallas_call x2, Pallas kernels: 50.1 us -> 37.9 us  [attend_backward(): pl.pallas_call(functools.partial(backward_body, width > 2 * INNER), grid_...]
    pallas_call x2, Pallas kernels: 65.1 us -> 53.3 us  [ffn_backward(): pl.pallas_call(ffn_backward_body, grid_spec=pltpu.PrefetchScalarGridSpec(...]
    unnamed x267 -> x261, local copies, waits for them, and re-layouts: 51.2 us -> 45.3 us
  transfers between devices with their start and end apart: 49 -> 49, of which waited for: 20 -> 25; matrix products, arithmetic and copies ran while one was open for 11% -> 11% of each run, Pallas kernels for 16% -> 14%
where the time goes in v11:
time: 1150 us; the launch traced here: 1140 us
  waiting for transfers between devices  636 us (55%)
  Pallas kernels  232 us (20%)
  starting transfers between devices  78.5 us (7%)
  other arithmetic  76.2 us (7%)
  local copies, waits for them, and re-layouts  64.6 us (6%)
  matrix products  33.9 us (3%)
  between operations  15.8 us (1%)
    all_gather x2, waiting for transfers between devices, fetch_rows(): return lax.all_gather(local_rows, DEVICES, axis=0, tiled=True)  336 us
    ppermute x29, waiting for transfers between devices, shift(): lax.ppermute(value, axis, [(i, (i + amount) % count) for i in range(count)])  179 us
    ppermute x4, waiting for transfers between devices, far_pair(): got = lax.ppermute(sent, 'z', pairs)  97.3 us
    pallas_call x2, Pallas kernels, ffn_forward(): pl.pallas_call(ffn_forward_body, grid_spec=pltpu.PrefetchScalarGridSpec(n...  56.3 us
    pallas_call x2, Pallas kernels, ffn_backward(): pl.pallas_call(ffn_backward_body, grid_spec=pltpu.PrefetchScalarGridSpec(...  53.3 us
    pallas_call x2, Pallas kernels, weight_grads(): pl.pallas_call(functools.partial(weight_grads_body, chunks, tile), grid_s...  47.8 us
    unnamed x261, local copies, waits for them, and re-layouts  45.3 us
    pallas_call x2, Pallas kernels, attend_backward(): pl.pallas_call(functools.partial(backward_body, width > 2 * INNER), grid_...  37.9 us
  transfers between devices with their start and end apart: 49, of which 25 were waited for; matrix products, arithmetic and copies ran while one was open for 11% of the time, Pallas kernels for 14%

profile of v11, /device:TPU:24, one launch (start us, length us, event | category | flops | bytes accessed | tf_op | source)
XLA Modules:
  0.0 1137.0 jit_solution(12777845435100733796)
XLA Ops:
  7.2 2.5 copy.121
  9.8 2.0 copy.124
  12.0 2.4 copy.120
  18.1 207.3 %all-gather.3.cloned.1.call-done.refs_2_.refs_3_.refs_4_.refs_5_ = bf16[12288,1472]{1,0:T(8,128)(2,1)} async-done(((bf16[384,1472]{1,0:T(8,128)(2,1)}), bf16[12288,1472]{1,0:T(8,128)(2,1)}) %all-gather.3.cloned.1.call-update) | async-done | bytes 36175888 | tf_op jit(solution)/shard_map/all_gather | solution.py:1042
  225.4 4.7 fusion.33
  233.3 6.1 collective-permute-start.2
  240.2 4.7 bias_tiles.1.refs_4_.refs_5_
  244.9 3.6 copy.126
  248.5 23.5 %collective-permute-done = bf16[288,768]{1,0:T(8,128)(2,1)S(1)} collective-permute-done((bf16[288,768]{1,0:T(8,128)(2,1)S(1)}, bf16[288,768]{1,0:T(8,128)(2,1)S(1)}, u32[]{:S(2)}, u32[]{:S(2)}) %collective-permute-start) | collective-permute-done | bytes 442400 | tf_op jit(solution)/shard_map/ppermute | solution.py:474
  272.1 15.6 %collective-permute-done.1 = bf16[512,768]{1,0:T(8,128)(2,1)} collective-permute-done((bf16[512,768]{1,0:T(8,128)(2,1)}, bf16[512,768]{1,0:T(8,128)(2,1)}, u32[]{:S(2)}, u32[]{:S(2)}) %collective-permute-start.1) | collective-permute-done | bytes 786464 | tf_op jit(solution)/shard_map/ppermute | solution.py:466
  290.6 6.2 attend_forward.2
  296.9 2.5 multiply_reduce_fusion.10
  301.0 28.2 %ffn_forward.2 = (f32[512,1472]{1,0:T(8,128)}, f32[512,3584]{1,0:T(8,128)}, f32[512,3584]{1,0:T(8,128)}, bf16[6144,512]{1,0:T(8,128)(2,1)}, bf16[6144,512]{1,0:T(8,128)(2,1)}) custom-call(s32[2]{0:T(128)S(1)} %pad_add_fusion.core_ref, bf16[512,1472]{1,0:T(8,128)(2,1)S(1)} %multiply_convert_fusion.2.refs_0_, f32[512,1472]{1,0:T(8,128)} %copy-done.54, ...), custom_call_target="tpu_custom_call" | custom-call | flops 16206790656 | bytes 50003968 | tf_op jit(solution)/shard_map/ffn_forward/pallas_call | solution.py:660
  329.2 2.5 multiply_reduce_fusion.9
  334.2 128.5 %all-gather.5.cloned.1.call-done.refs_2_.refs_3_.refs_4_.refs_5_ = bf16[12288,1472]{1,0:T(8,128)(2,1)} async-done(((bf16[384,1472]{1,0:T(8,128)(2,1)}), bf16[12288,1472]{1,0:T(8,128)(2,1)}) %all-gather.5.cloned.1.call-update) | async-done | bytes 36175888 | tf_op jit(solution)/shard_map/all_gather | solution.py:1042
  462.7 4.2 fusion.36
  469.3 5.1 collective-permute-start.5
  475.7 39.8 %collective-permute-done.3 = bf16[288,896]{1,0:T(8,128)(2,1)S(1)} collective-permute-done((bf16[288,896]{1,0:T(8,128)(2,1)S(1)}, bf16[288,896]{1,0:T(8,128)(2,1)S(1)}, u32[]{:S(2)}, u32[]{:S(2)}) %collective-permute-start.3) | collective-permute-done | bytes 516128 | tf_op jit(solution)/shard_map/ppermute | solution.py:474
  517.0 6.2 attend_forward.3
  523.2 2.5 multiply_reduce_fusion.7
  527.4 28.1 %ffn_forward.3 = (f32[512,1472]{1,0:T(8,128)}, f32[512,3584]{1,0:T(8,128)}, f32[512,3584]{1,0:T(8,128)}, bf16[6144,512]{1,0:T(8,128)(2,1)}, bf16[6144,512]{1,0:T(8,128)(2,1)}) custom-call(s32[2]{0:T(128)S(1)} %pad_add_fusion.core_ref, bf16[512,1472]{1,0:T(8,128)(2,1)S(1)} %multiply_convert_fusion.refs_0_, f32[512,1472]{1,0:T(8,128)} %copy-done.56, ...), custom_call_target="tpu_custom_call" | custom-call | flops 16206790656 | bytes 50003968 | tf_op jit(solution)/shard_map/ffn_forward/pallas_call | solution.py:660
  555.5 26.0 %ffn_backward.2 = (f32[512,1472]{1,0:T(8,128)}, bf16[6144,512]{1,0:T(8,128)(2,1)}, bf16[6144,512]{1,0:T(8,128)(2,1)}) custom-call(s32[2]{0:T(128)S(1)} %pad_add_fusion.core_ref, bf16[512,1472]{1,0:T(8,128)(2,1)S(1)} %bitcast_convert_fusion.refs_0_, f32[512,3584]{1,0:T(8,128)} %get-tuple-element.208.refs_1_, ...), custom_call_target="tpu_custom_call", output_to_operand_aliasing={{1}: (7, {}), {2}: (8, {})} | custom-call | flops 16206790656 | bytes 53673984 | tf_op jit(solution)/shard_map/ffn_backward/pallas_call | solution.py:725
  586.8 2.3 multiply_reduce_fusion.1
  589.1 2.5 fusion.51
  591.6 2.4 convolution_convert_fusion.1.refs_1_
  594.0 19.5 %attend_backward.2 = (bf16[512,384]{1,0:T(8,128)(2,1)S(1)}, bf16[2304,896]{1,0:T(8,128)(2,1)}, f32[3,32,256]{2,1,0:T(8,128)S(1)}) custom-call(s32[4]{0:T(128)S(1)} %get-tuple-element.541.low_ref, s32[4]{0:T(128)S(1)} %get-tuple-element.540.high_ref, bf16[512,384]{1,0:T(8,128)(2,1)S(1)} %copy-done.31, bf16[512,384]{1,0:T(8,128)(2,1)S(1)} %convolution_convert_fusion.1.refs_1_, ...), custom_call_target="tpu_custom_call" | custom-call | flops 4529848320 | bytes 12582912 | tf_op jit(solution)/shard_map/attend_backward/pallas_call | solution.py:366
  613.5 2.2 fusion.52
  615.7 9.3 collective-permute-start.8
  627.6 11.6 %collective-permute-start.10 = (bf16[288,896]{1,0:T(8,128)(2,1)S(1)}, bf16[288,896]{1,0:T(8,128)(2,1)S(1)}, u32[]{:S(2)}, u32[]{:S(2)}) collective-permute-start(bf16[288,896]{1,0:T(8,128)(2,1)S(1)} %slice_select_fusion), channel_id=1, source_target_pairs={{0,2},{1,3},{2,0},{3,1},{4,6},{5,7},{6,4},{7,5},{8,10},{9,11},{10,... | collective-permute-start | bytes 1548296 | tf_op jit(solution)/shard_map/ppermute | solution.py:474
  641.3 22.7 %weight_grads.2 = (bf16[3072,256]{1,0:T(8,128)(2,1)S(1)}, bf16[3072,256]{1,0:T(8,128)(2,1)S(1)}, bf16[3072,256]{1,0:T(8,128)(2,1)S(1)}, bf16[3072,256]{1,0:T(8,128)(2,1)S(1)}, bf16[6144,1024]{1,0:T(8,128)(2,1)}) custom-call(s32[6]{0:T(128)S(1)} %copy-done.45, bf16[6144,512]{1,0:T(8,128)(2,1)} %get-tuple-element.217.refs_0_, ...), custom_call_target="tpu_custom_call" | custom-call | flops 18522046464 | bytes 31457280 | tf_op jit(solution)/shard_map/weight_grads/pallas_call | solution.py:885
  664.0 14.8 %collective-permute-done.10 = bf16[288,896]{1,0:T(8,128)(2,1)S(1)} collective-permute-done((bf16[288,896]{1,0:T(8,128)(2,1)S(1)}, bf16[288,896]{1,0:T(8,128)(2,1)S(1)}, u32[]{:S(2)}, u32[]{:S(2)}) %collective-permute-start.10) | collective-permute-done | bytes 516128 | tf_op jit(solution)/shard_map/ppermute | solution.py:474
  683.7 2.5 pad_maximum_fusion.5
  691.1 10.5 attention_fill.2
  706.3 3.1 collective-permute-start.13
  712.5 6.6 multiply_reduce_fusion.2
  719.1 2.7 fusion.49
  721.9 27.3 %ffn_backward.3 = (f32[512,1472]{1,0:T(8,128)}, bf16[6144,512]{1,0:T(8,128)(2,1)}, bf16[6144,512]{1,0:T(8,128)(2,1)}) custom-call(s32[2]{0:T(128)S(1)} %pad_add_fusion.core_ref, bf16[512,1472]{1,0:T(8,128)(2,1)S(1)} %get-tuple-element.468.refs_0_, f32[512,3584]{1,0:T(8,128)} %get-tuple-element.247.refs_1_, ...), custom_call_target="tpu_custom_call", output_to_operand_aliasing={{1}: (7, {}), {2}: (8, {})} | custom-call | flops 16206790656 | bytes 53673984 | tf_op jit(solution)/shard_map/ffn_backward/pallas_call | solution.py:725
  762.6 2.1 multiply_reduce_fusion.3
  764.8 2.5 fusion.48
  768.0 3.5 convolution_convert_fusion.refs_1_
  771.6 18.4 %attend_backward.3 = (bf16[512,384]{1,0:T(8,128)(2,1)S(1)}, bf16[2304,768]{1,0:T(8,128)(2,1)}, f32[3,32,256]{2,1,0:T(8,128)S(1)}) custom-call(s32[4]{0:T(128)S(1)} %get-tuple-element.541.low_ref, s32[4]{0:T(128)S(1)} %get-tuple-element.540.high_ref, bf16[512,384]{1,0:T(8,128)(2,1)S(1)} %copy-done.34, bf16[512,384]{1,0:T(8,128)(2,1)S(1)} %convolution_convert_fusion.refs_1_, ...), custom_call_target="tpu_custom_call" | custom-call | flops 4529848320 | bytes 12582912 | tf_op jit(solution)/shard_map/attend_backward/pallas_call | solution.py:366
  795.2 2.2 collective-permute-start.19
  798.8 13.6 %collective-permute-start.21 = (bf16[288,768]{1,0:T(8,128)(2,1)S(1)}, bf16[288,768]{1,0:T(8,128)(2,1)S(1)}, u32[]{:S(2)}, u32[]{:S(2)}) collective-permute-start(bf16[288,768]{1,0:T(8,128)(2,1)S(1)} %slice_select_fusion.2), channel_id=1, source_target_pairs={{0,2},{1,3},{2,0},{3,1},{4,6},{5,7},{6,4},{7,5},{8,10},{9,11},{10,... | collective-permute-start | bytes 1327112 | tf_op jit(solution)/shard_map/ppermute | solution.py:474
  812.4 25.1 %weight_grads.3 = (bf16[3072,384]{1,0:T(8,128)(2,1)}, bf16[3072,384]{1,0:T(8,128)(2,1)}, bf16[3072,384]{1,0:T(8,128)(2,1)S(1)}, bf16[3072,384]{1,0:T(8,128)(2,1)...) custom-call(s32[6]{0:T(128)S(1)} %copy-done.46, ...), custom_call_target="tpu_custom_call" | custom-call | flops 18522046464 | bytes 31457280 | tf_op jit(solution)/shard_map/weight_grads/pallas_call | solution.py:885
  837.5 19.2 %collective-permute-done.21 = bf16[288,768]{1,0:T(8,128)(2,1)S(1)} collective-permute-done((bf16[288,768]{1,0:T(8,128)(2,1)S(1)}, bf16[288,768]{1,0:T(8,128)(2,1)S(1)}, u32[]{:S(2)}, u32[]{:S(2)}) %collective-permute-start.21) | collective-permute-done | bytes 442400 | tf_op jit(solution)/shard_map/ppermute | solution.py:474
  860.0 2.2 collective-permute-done.22.refs_1_
  862.3 9.6 attention_fill.3
  878.3 7.5 fusion.24
  889.9 9.6 collective-permute-done.26
  899.5 32.0 %collective-permute-done.27 = bf16[384,512]{1,0:T(8,128)(2,1)S(1)} collective-permute-done((bf16[384,512]{1,0:T(8,128)(2,1)}, bf16[384,512]{1,0:T(8,128)(2,1)S(1)}, u32[]{:S(2)}, u32[]{:S(2)}) %collective-permute-start.27) | collective-permute-done | bytes 393248 | tf_op jit(solution)/shard_map/ppermute | solution.py:460
  931.5 10.4 collective-permute-done.24
  941.9 3.0 add_convert_fusion.2
  945.2 2.3 add_convert_fusion.3
  951.8 24.9 %collective-permute-done.30 = bf16[1536,384]{1,0:T(8,128)(2,1)S(1)} collective-permute-done((bf16[1536,384]{1,0:T(8,128)(2,1)S(1)}, bf16[1536,384]{1,0:T(8,128)(2,1)S(1)}, u32[]{:S(2)}, u32[]{:S(2)}) %collective-permute-start.30) | collective-permute-done | bytes 1179680 | tf_op jit(solution)/shard_map/ppermute | solution.py:460
  984.0 3.6 copy.135
  987.6 8.2 collective-permute-done.32
  995.9 36.0 %collective-permute-done.33 = bf16[384,768]{1,0:T(8,128)(2,1)} collective-permute-done((bf16[384,768]{1,0:T(8,128)(2,1)}, bf16[384,768]{1,0:T(8,128)(2,1)}, u32[]{:S(2)}, u32[]{:S(2)}) %collective-permute-start.33) | collective-permute-done | bytes 589856 | tf_op jit(solution)/shard_map/ppermute | solution.py:460
  1031.9 2.3 add_convert_fusion
  1036.7 2.4 add_convert_fusion.1
  1044.8 2.3 copy.136
  1050.7 4.1 collective-permute-done.40
  1054.8 12.1 %collective-permute-done.37 = bf16[1536,384]{1,0:T(8,128)(2,1)} collective-permute-done((bf16[1536,384]{1,0:T(8,128)(2,1)}, bf16[1536,384]{1,0:T(8,128)(2,1)}, u32[]{:S(2)}, u32[]{:S(2)}) %collective-permute-start.37) | collective-permute-done | bytes 1179680 | tf_op jit(solution)/shard_map/ppermute | solution.py:460
  1085.4 4.5 collective-permute-done.41
  1089.8 34.3 %collective-permute-done.42 = bf16[384,768]{1,0:T(8,128)(2,1)} collective-permute-done((bf16[384,768]{1,0:T(8,128)(2,1)}, bf16[384,768]{1,0:T(8,128)(2,1)}, u32[]{:S(2)}, u32[]{:S(2)}) %collective-permute-start.42) | collective-permute-done | bytes 589856 | tf_op jit(solution)/shard_map/ppermute | solution.py:460
  (453 shorter events, 131.2 us)
Async XLA Ops:
  7.2 218.2 %all-gather.3.cloned.1.call-start = ((), (), s32[]{:S(2)}) async-start(), calls=%async_computation.1 | async-start | bytes 38928384 | tf_op jit(solution)/shard_map/all_gather | solution.py:1042
  9.7 453.0 %all-gather.5.cloned.1.call-start = ((), (), s32[]{:S(2)}) async-start(), calls=%async_computation.2 | async-start | bytes 38928384 | tf_op jit(solution)/shard_map/all_gather | solution.py:1042
  11.9 1020.0 %reduce-scatter.2.cloned.1.call-start = ((), (), s32[]{:S(2)}) async-start(), calls=%async_computation.3 | async-start | bytes 13369344 | tf_op jit(solution)/shard_map/reduce_scatter | solution.py:1137
  15.7 284.3 %copy-start.91 = (f32[1472]{0:T(1024)}, f32[1472]{0:T(1024)S(1)}, u32[]{:S(2)}) copy-start(f32[1472]{0:T(1024)S(1)} %get-tuple-element.459) | copy-start | bytes 17668
  16.6 213.5 %copy-start.111 = (f32[512]{0:T(512)}, f32[512]{0:T(512)S(1)}, u32[]{:S(2)}) copy-start(f32[512]{0:T(512)S(1)} %get-tuple-element.527) | copy-start | bytes 6148
  18.1 221.4 %copy-start.121 = (f32[32,6]{0,1:T(8,128)S(1)}, f32[32,6]{0,1:T(8,128)}, u32[]{:S(2)}) copy-start(f32[32,6]{0,1:T(8,128)} %param.13) | copy-start | bytes 2308
  231.1 40.9 %collective-permute-start = (bf16[288,768]{1,0:T(8,128)(2,1)S(1)}, bf16[288,768]{1,0:T(8,128)(2,1)S(1)}, u32[]{:S(2)}, u32[]{:S(2)}) collective-permute-start(bf16[288,768]{1,0:T(8,128)(2,1)S(1)} %slice_select_fusion.1), channel_id=1, source_target_pairs={{0,2},{1,3},{2,0},{3,1},{4,6},{5,7},{6,4},{7,5},{8,10},{9,11},{10,... | collective-permute-start | bytes 1327112 | tf_op jit(solution)/shard_map/ppermute | solution.py:474
  231.8 55.9 %collective-permute-start.1 = (bf16[512,768]{1,0:T(8,128)(2,1)}, bf16[512,768]{1,0:T(8,128)(2,1)}, u32[]{:S(2)}, u32[]{:S(2)}) collective-permute-start(bf16[512,768]{1,0:T(8,128)(2,1)} %slice.177), channel_id=1, source_target_pairs={{0,1},{1,2},{2,3},{4,5},{5,6},{6,7},{8,9},{9,10},{10,11},{12,13},{... | collective-permute-start | bytes 2359304 | tf_op jit(solution)/shard_map/ppermute | solution.py:466
  233.3 55.6 %collective-permute-start.2 = (bf16[512,768]{1,0:T(8,128)(2,1)}, bf16[512,768]{1,0:T(8,128)(2,1)}, u32[]{:S(2)}, u32[]{:S(2)}) collective-permute-start(bf16[512,768]{1,0:T(8,128)(2,1)} %slice.177), channel_id=1, source_target_pairs={{1,0},{2,1},{3,2},{5,4},{6,5},{7,6},{9,8},{10,9},{11,10},{13,12},{... | collective-permute-start | bytes 2359304 | tf_op jit(solution)/shard_map/ppermute | solution.py:466
  248.5 42.1 %copy-start.33 = (bf16[512,384]{1,0:T(8,128)(2,1)}, bf16[512,384]{1,0:T(8,128)(2,1)S(1)}, u32[]{:S(2)}) copy-start(bf16[512,384]{1,0:T(8,128)(2,1)S(1)} %slice.174.refs_0_) | copy-start | bytes 1179652
  300.0 29.2 %copy-start.103 = (f32[512]{0:T(512)}, f32[512]{0:T(512)S(1)}, u32[]{:S(2)}) copy-start(f32[512]{0:T(512)S(1)} %get-tuple-element.529) | copy-start | bytes 6148
  301.0 28.2 %copy-start.1 = (bf16[512,1472]{1,0:T(8,128)(2,1)}, bf16[512,1472]{1,0:T(8,128)(2,1)S(1)}, u32[]{:S(2)}) copy-start(bf16[512,1472]{1,0:T(8,128)(2,1)S(1)} %multiply_convert_fusion.2.refs_0_) | copy-start | bytes 4521988
  301.0 31.9 %copy-start.99 = (f32[1472]{0:T(1024)S(1)}, f32[1472]{0:T(1024)}, u32[]{:S(2)}) copy-start(f32[1472]{0:T(1024)} %param.12) | copy-start | bytes 17668
  334.2 132.8 %copy-start.71 = (bf16[512,1472]{1,0:T(8,128)(2,1)}, bf16[512,1472]{1,0:T(8,128)(2,1)S(1)}, u32[]{:S(2)}) copy-start(bf16[512,1472]{1,0:T(8,128)(2,1)S(1)} %get-tuple-element.481) | copy-start | bytes 4521988
  468.0 47.7 %collective-permute-start.4 = (bf16[512,896]{1,0:T(8,128)(2,1)S(1)}, bf16[512,896]{1,0:T(8,128)(2,1)S(1)}, u32[]{:S(2)}, u32[]{:S(2)}) collective-permute-start(bf16[512,896]{1,0:T(8,128)(2,1)S(1)} %pad_maximum_fusion.2), channel_id=1, source_target_pairs={{0,1},{1,2},{2,3},{4,5},{5,6},{6,7},{8,9},{9,10},{10,11},{12,13},{... | collective-permute-start | bytes 2752520 | tf_op jit(solution)/shard_map/ppermute | solution.py:466
  469.3 46.7 %collective-permute-start.5 = (bf16[512,896]{1,0:T(8,128)(2,1)S(1)}, bf16[512,896]{1,0:T(8,128)(2,1)S(1)}, u32[]{:S(2)}, u32[]{:S(2)}) collective-permute-start(bf16[512,896]{1,0:T(8,128)(2,1)S(1)} %pad_maximum_fusion.2), channel_id=1, source_target_pairs={{1,0},{2,1},{3,2},{5,4},{6,5},{7,6},{9,8},{10,9},{11,10},{13,12},{... | collective-permute-start | bytes 2752520 | tf_op jit(solution)/shard_map/ppermute | solution.py:466
  474.5 41.1 %collective-permute-start.3 = (bf16[288,896]{1,0:T(8,128)(2,1)S(1)}, bf16[288,896]{1,0:T(8,128)(2,1)S(1)}, u32[]{:S(2)}, u32[]{:S(2)}) collective-permute-start(bf16[288,896]{1,0:T(8,128)(2,1)S(1)} %fusion.44), channel_id=1, source_target_pairs={{0,2},{1,3},{2,0},{3,1},{4,6},{5,7},{6,4},{7,5},{8,10},{9,11},{10,... | collective-permute-start | bytes 1548296 | tf_op jit(solution)/shard_map/ppermute | solution.py:474
  475.7 40.5 %copy-start.30 = (bf16[512,384]{1,0:T(8,128)(2,1)}, bf16[512,384]{1,0:T(8,128)(2,1)S(1)}, u32[]{:S(2)}) copy-start(bf16[512,384]{1,0:T(8,128)(2,1)S(1)} %slice.180.refs_0_) | copy-start | bytes 1179652
  526.4 29.2 %copy-start.105 = (f32[512]{0:T(512)}, f32[512]{0:T(512)S(1)}, u32[]{:S(2)}) copy-start(f32[512]{0:T(512)S(1)} %get-tuple-element.533) | copy-start | bytes 6148
  581.6 59.7 %collective-permute-start.6 = (bf16[6144,512]{1,0:T(8,128)(2,1)}, bf16[6144,512]{1,0:T(8,128)(2,1)}, u32[]{:S(2)}, u32[]{:S(2)}) collective-permute-start(bf16[6144,512]{1,0:T(8,128)(2,1)} %get-tuple-element.218), channel_id=1, source_target_pairs={{0,4},{4,0},{1,5},{5,1},{2,6},{6,2},{3,7},{7,3},{8,12},{12,8},{9,1... | collective-permute-start | bytes 18874376 | tf_op jit(solution)/shard_map/ppermute | solution.py:460
  585.4 55.9 %collective-permute-start.7 = (bf16[1024,1536]{1,0:T(8,128)(2,1)S(1)}, bf16[1024,1536]{1,0:T(8,128)(2,1)S(1)}, u32[]{:S(2)}, u32[]{:S(2)}) collective-permute-start(bf16[1024,1536]{1,0:T(8,128)(2,1)S(1)} %fusion.11.refs_2_.refs_3_), channel_id=1, source_target_pairs={{0,4},{4,0},{1,5},{5,1},{2,6},{6,2},{3,7},{7,3},{8,12},{12,8},{9,1... | collective-permute-start | bytes 9437192 | tf_op jit(solution)/shard_map/ppermute | solution.py:460
  613.5 66.0 %copy-start.32 = (bf16[512,384]{1,0:T(8,128)(2,1)}, bf16[512,384]{1,0:T(8,128)(2,1)S(1)}, u32[]{:S(2)}) copy-start(bf16[512,384]{1,0:T(8,128)(2,1)S(1)} %get-tuple-element.214) | copy-start | bytes 1179652
  615.7 63.1 %collective-permute-start.8 = (bf16[512,896]{1,0:T(8,128)(2,1)S(1)}, bf16[512,896]{1,0:T(8,128)(2,1)S(1)}, u32[]{:S(2)}, u32[]{:S(2)}) collective-permute-start(bf16[512,896]{1,0:T(8,128)(2,1)S(1)} %get-tuple-element.475), channel_id=1, source_target_pairs={{1,0},{2,1},{3,2},{5,4},{6,5},{7,6},{9,8},{10,9},{11,10},{13,12},{... | collective-permute-start | bytes 2752520 | tf_op jit(solution)/shard_map/ppermute | solution.py:466
  625.0 53.8 %collective-permute-start.9 = (bf16[512,896]{1,0:T(8,128)(2,1)S(1)}, bf16[512,896]{1,0:T(8,128)(2,1)S(1)}, u32[]{:S(2)}, u32[]{:S(2)}) collective-permute-start(bf16[512,896]{1,0:T(8,128)(2,1)S(1)} %get-tuple-element.474), channel_id=1, source_target_pairs={{0,1},{1,2},{2,3},{4,5},{5,6},{6,7},{8,9},{9,10},{10,11},{12,13},{... | collective-permute-start | bytes 2752520 | tf_op jit(solution)/shard_map/ppermute | solution.py:466
  627.6 51.2 %collective-permute-start.10 = (bf16[288,896]{1,0:T(8,128)(2,1)S(1)}, bf16[288,896]{1,0:T(8,128)(2,1)S(1)}, u32[]{:S(2)}, u32[]{:S(2)}) collective-permute-start(bf16[288,896]{1,0:T(8,128)(2,1)S(1)} %slice_select_fusion), channel_id=1, source_target_pairs={{0,2},{1,3},{2,0},{3,1},{4,6},{5,7},{6,4},{7,5},{8,10},{9,11},{10,... | collective-permute-start | bytes 1548296 | tf_op jit(solution)/shard_map/ppermute | solution.py:474
  641.3 45.0 %collective-permute-start.12 = (bf16[1024,1536]{1,0:T(8,128)(2,1)}, bf16[1024,1536]{1,0:T(8,128)(2,1)}, u32[]{:S(2)}, u32[]{:S(2)}) collective-permute-start(bf16[1024,1536]{1,0:T(8,128)(2,1)} %fusion.12.refs_2_), channel_id=1, source_target_pairs={{0,4},{4,0},{1,5},{5,1},{2,6},{6,2},{3,7},{7,3},{8,12},{12,8},{9,1... | collective-permute-start | bytes 9437192 | tf_op jit(solution)/shard_map/ppermute | solution.py:460
  680.9 5.3 collective-permute-start.11
  706.3 43.6 %collective-permute-start.13 = (bf16[3072,256]{1,0:T(8,128)(2,1)}, bf16[3072,256]{1,0:T(8,128)(2,1)}, u32[]{:S(2)}, u32[]{:S(2)}) collective-permute-start(bf16[3072,256]{1,0:T(8,128)(2,1)} %copy-done.37), channel_id=1, source_target_pairs={{0,16},{16,0},{1,17},{17,1},{2,18},{18,2},{3,19},{19,3},{4,20},{20... | collective-permute-start | bytes 4718600 | tf_op jit(solution)/shard_map/ppermute | solution.py:460
  709.4 42.1 %collective-permute-start.14 = (bf16[3072,256]{1,0:T(8,128)(2,1)}, bf16[3072,256]{1,0:T(8,128)(2,1)}, u32[]{:S(2)}, u32[]{:S(2)}) collective-permute-start(bf16[3072,256]{1,0:T(8,128)(2,1)} %copy-done.40), channel_id=1, source_target_pairs={{0,8},{8,0},{1,9},{9,1},{2,10},{10,2},{3,11},{11,3},{4,12},{12,4},... | collective-permute-start | bytes 4718600 | tf_op jit(solution)/shard_map/ppermute | solution.py:460
  721.9 29.6 %copy-start.23 = (bf16[3072,256]{1,0:T(8,128)(2,1)S(1)}, bf16[3072,256]{1,0:T(8,128)(2,1)}, u32[]{:S(2)}) copy-start(bf16[3072,256]{1,0:T(8,128)(2,1)} %copy-done.22) | copy-start | bytes 4718596
  757.9 54.4 %collective-permute-start.17 = (bf16[6144,512]{1,0:T(8,128)(2,1)}, bf16[6144,512]{1,0:T(8,128)(2,1)}, u32[]{:S(2)}, u32[]{:S(2)}) collective-permute-start(bf16[6144,512]{1,0:T(8,128)(2,1)} %get-tuple-element.283), channel_id=1, source_target_pairs={{0,4},{4,0},{1,5},{5,1},{2,6},{6,2},{3,7},{7,3},{8,12},{12,8},{9,1... | collective-permute-start | bytes 18874376 | tf_op jit(solution)/shard_map/ppermute | solution.py:460
  759.9 38.9 %collective-permute-start.18 = (bf16[1024,1536]{1,0:T(8,128)(2,1)S(1)}, bf16[1024,1536]{1,0:T(8,128)(2,1)}, u32[]{:S(2)}, u32[]{:S(2)}) collective-permute-start(bf16[1024,1536]{1,0:T(8,128)(2,1)S(1)} %fusion.13.refs_2_.refs_3_), channel_id=1, source_target_pairs={{0,4},{4,0},{1,5},{5,1},{2,6},{6,2},{3,7},{7,3},{8,12},{12,8},{9,1... | collective-permute-start | bytes 9437192 | tf_op jit(solution)/shard_map/ppermute | solution.py:460
  760.4 29.6 %collective-permute-start.15 = (bf16[1536,256]{1,0:T(8,128)(2,1)}, bf16[1536,256]{1,0:T(8,128)(2,1)S(1)}, u32[]{:S(2)}, u32[]{:S(2)}) collective-permute-start(bf16[1536,256]{1,0:T(8,128)(2,1)} %get-tuple-element.263), channel_id=1, source_target_pairs={{0,8},{8,0},{1,9},{9,1},{2,10},{10,2},{3,11},{11,3},{4,12},{12,4},... | collective-permute-start | bytes 2359304 | tf_op jit(solution)/shard_map/ppermute | solution.py:460
  762.2 27.9 %collective-permute-start.16 = (bf16[1536,256]{1,0:T(8,128)(2,1)}, bf16[1536,256]{1,0:T(8,128)(2,1)S(1)}, u32[]{:S(2)}, u32[]{:S(2)}) collective-permute-start(bf16[1536,256]{1,0:T(8,128)(2,1)} %get-tuple-element.265), channel_id=1, source_target_pairs={{0,16},{16,0},{1,17},{17,1},{2,18},{18,2},{3,19},{19,3},{4,20},{20... | collective-permute-start | bytes 2359304 | tf_op jit(solution)/shard_map/ppermute | solution.py:460
  767.7 92.4 %collective-permute-start.23 = (bf16[1024,1536]{1,0:T(8,128)(2,1)S(1)}, bf16[1024,1536]{1,0:T(8,128)(2,1)}, u32[]{:S(2)}, u32[]{:S(2)}) collective-permute-start(bf16[1024,1536]{1,0:T(8,128)(2,1)S(1)} %fusion.14.refs_2_), channel_id=1, source_target_pairs={{0,4},{4,0},{1,5},{5,1},{2,6},{6,2},{3,7},{7,3},{8,12},{12,8},{9,1... | collective-permute-start | bytes 9437192 | tf_op jit(solution)/shard_map/ppermute | solution.py:460
  795.2 61.5 %collective-permute-start.19 = (bf16[512,768]{1,0:T(8,128)(2,1)S(1)}, bf16[512,768]{1,0:T(8,128)(2,1)}, u32[]{:S(2)}, u32[]{:S(2)}) collective-permute-start(bf16[512,768]{1,0:T(8,128)(2,1)S(1)} %get-tuple-element.478), channel_id=1, source_target_pairs={{1,0},{2,1},{3,2},{5,4},{6,5},{7,6},{9,8},{10,9},{11,10},{13,12},{... | collective-permute-start | bytes 2359304 | tf_op jit(solution)/shard_map/ppermute | solution.py:466
  797.4 59.3 %collective-permute-start.20 = (bf16[512,768]{1,0:T(8,128)(2,1)S(1)}, bf16[512,768]{1,0:T(8,128)(2,1)}, u32[]{:S(2)}, u32[]{:S(2)}) collective-permute-start(bf16[512,768]{1,0:T(8,128)(2,1)S(1)} %get-tuple-element.477), channel_id=1, source_target_pairs={{0,1},{1,2},{2,3},{4,5},{5,6},{6,7},{8,9},{9,10},{10,11},{12,13},{... | collective-permute-start | bytes 2359304 | tf_op jit(solution)/shard_map/ppermute | solution.py:466
  798.8 57.9 %collective-permute-start.21 = (bf16[288,768]{1,0:T(8,128)(2,1)S(1)}, bf16[288,768]{1,0:T(8,128)(2,1)S(1)}, u32[]{:S(2)}, u32[]{:S(2)}) collective-permute-start(bf16[288,768]{1,0:T(8,128)(2,1)S(1)} %slice_select_fusion.2), channel_id=1, source_target_pairs={{0,2},{1,3},{2,0},{3,1},{4,6},{5,7},{6,4},{7,5},{8,10},{9,11},{10,... | collective-permute-start | bytes 1327112 | tf_op jit(solution)/shard_map/ppermute | solution.py:474
  858.8 3.5 collective-permute-start.22
  876.2 65.7 %collective-permute-start.24 = (bf16[3072,384]{1,0:T(8,128)(2,1)}, bf16[3072,384]{1,0:T(8,128)(2,1)}, u32[]{:S(2)}, u32[]{:S(2)}) collective-permute-start(bf16[3072,384]{1,0:T(8,128)(2,1)} %get-tuple-element.323), channel_id=1, source_target_pairs={{0,16},{16,0},{1,17},{17,1},{2,18},{18,2},{3,19},{19,3},{4,20},{20... | collective-permute-start | bytes 7077896 | tf_op jit(solution)/shard_map/ppermute | solution.py:460
  876.2 65.7 %collective-permute-start.25 = (bf16[3072,384]{1,0:T(8,128)(2,1)}, bf16[3072,384]{1,0:T(8,128)(2,1)}, u32[]{:S(2)}, u32[]{:S(2)}) collective-permute-start(bf16[3072,384]{1,0:T(8,128)(2,1)} %get-tuple-element.325), channel_id=1, source_target_pairs={{0,8},{8,0},{1,9},{9,1},{2,10},{10,2},{3,11},{11,3},{4,12},{12,4},... | collective-permute-start | bytes 7077896 | tf_op jit(solution)/shard_map/ppermute | solution.py:460
  886.5 1.4 collective-permute-start.29
  886.5 13.0 %collective-permute-start.26 = (bf16[384,512]{1,0:T(8,128)(2,1)}, bf16[384,512]{1,0:T(8,128)(2,1)S(1)}, u32[]{:S(2)}, u32[]{:S(2)}) collective-permute-start(bf16[384,512]{1,0:T(8,128)(2,1)} %pad_maximum_fusion.16), channel_id=1, source_target_pairs={{0,1},{1,2},{2,3},{3,0},{4,5},{5,6},{6,7},{7,4},{8,9},{9,10},{10,1... | collective-permute-start | bytes 1179656 | tf_op jit(solution)/shard_map/ppermute | solution.py:460
  886.5 45.0 %collective-permute-start.27 = (bf16[384,512]{1,0:T(8,128)(2,1)}, bf16[384,512]{1,0:T(8,128)(2,1)S(1)}, u32[]{:S(2)}, u32[]{:S(2)}) collective-permute-start(bf16[384,512]{1,0:T(8,128)(2,1)} %pad_maximum_fusion.17), channel_id=1, source_target_pairs={{0,2},{1,3},{2,0},{3,1},{4,6},{5,7},{6,4},{7,5},{8,10},{9,11},{10,... | collective-permute-start | bytes 1179656 | tf_op jit(solution)/shard_map/ppermute | solution.py:460
  887.9 43.6 %collective-permute-start.28 = (bf16[384,512]{1,0:T(8,128)(2,1)}, bf16[384,512]{1,0:T(8,128)(2,1)S(1)}, u32[]{:S(2)}, u32[]{:S(2)}) collective-permute-start(bf16[384,512]{1,0:T(8,128)(2,1)} %pad_maximum_fusion.18), channel_id=1, source_target_pairs={{0,3},{1,0},{2,1},{3,2},{4,7},{5,4},{6,5},{7,6},{8,11},{9,8},{10,9... | collective-permute-start | bytes 1179656 | tf_op jit(solution)/shard_map/ppermute | solution.py:460
  899.5 45.4 %copy-start.88 = (bf16[384,512]{1,0:T(8,128)(2,1)}, bf16[384,512]{1,0:T(8,128)(2,1)S(1)}, u32[]{:S(2)}) copy-start(bf16[384,512]{1,0:T(8,128)(2,1)S(1)} %collective-permute-done.26) | copy-start | bytes 1179652
  947.7 29.0 %collective-permute-start.30 = (bf16[1536,384]{1,0:T(8,128)(2,1)S(1)}, bf16[1536,384]{1,0:T(8,128)(2,1)S(1)}, u32[]{:S(2)}, u32[]{:S(2)}) collective-permute-start(bf16[1536,384]{1,0:T(8,128)(2,1)S(1)} %get-tuple-element.339), channel_id=1, source_target_pairs={{0,8},{8,0},{1,9},{9,1},{2,10},{10,2},{3,11},{11,3},{4,12},{12,4},... | collective-permute-start | bytes 3538952 | tf_op jit(solution)/shard_map/ppermute | solution.py:460
  948.5 28.9 %collective-permute-start.31 = (bf16[1536,384]{1,0:T(8,128)(2,1)S(1)}, bf16[1536,384]{1,0:T(8,128)(2,1)S(1)}, u32[]{:S(2)}, u32[]{:S(2)}) collective-permute-start(bf16[1536,384]{1,0:T(8,128)(2,1)S(1)} %get-tuple-element.341), channel_id=1, source_target_pairs={{0,16},{16,0},{1,17},{17,1},{2,18},{18,2},{3,19},{19,3},{4,20},{20... | collective-permute-start | bytes 3538952 | tf_op jit(solution)/shard_map/ppermute | solution.py:460
  948.8 83.1 %collective-permute-start.35 = (bf16[3072,384]{1,0:T(8,128)(2,1)}, bf16[3072,384]{1,0:T(8,128)(2,1)}, u32[]{:S(2)}, u32[]{:S(2)}) collective-permute-start(bf16[3072,384]{1,0:T(8,128)(2,1)} %get-tuple-element.364), channel_id=1, source_target_pairs={{0,16},{16,0},{1,17},{17,1},{2,18},{18,2},{3,19},{19,3},{4,20},{20... | collective-permute-start | bytes 7077896 | tf_op jit(solution)/shard_map/ppermute | solution.py:460
  950.5 81.4 %collective-permute-start.36 = (bf16[3072,384]{1,0:T(8,128)(2,1)}, bf16[3072,384]{1,0:T(8,128)(2,1)}, u32[]{:S(2)}, u32[]{:S(2)}) collective-permute-start(bf16[3072,384]{1,0:T(8,128)(2,1)} %get-tuple-element.366), channel_id=1, source_target_pairs={{0,8},{8,0},{1,9},{9,1},{2,10},{10,2},{3,11},{11,3},{4,12},{12,4},... | collective-permute-start | bytes 7077896 | tf_op jit(solution)/shard_map/ppermute | solution.py:460
  981.8 50.1 %copy-start.15 = (bf16[3072,384]{1,0:T(8,128)(2,1)S(1)}, bf16[3072,384]{1,0:T(8,128)(2,1)}, u32[]{:S(2)}) copy-start(bf16[3072,384]{1,0:T(8,128)(2,1)} %copy-done.14) | copy-start | bytes 7077892
  981.8 14.1 %collective-permute-start.32 = (bf16[384,768]{1,0:T(8,128)(2,1)}, bf16[384,768]{1,0:T(8,128)(2,1)S(1)}, u32[]{:S(2)}, u32[]{:S(2)}) collective-permute-start(bf16[384,768]{1,0:T(8,128)(2,1)} %pad_maximum_fusion.8), channel_id=1, source_target_pairs={{0,1},{1,2},{2,3},{3,0},{4,5},{5,6},{6,7},{7,4},{8,9},{9,10},{10,1... | collective-permute-start | bytes 1769480 | tf_op jit(solution)/shard_map/ppermute | solution.py:460
  981.8 50.1 %collective-permute-start.33 = (bf16[384,768]{1,0:T(8,128)(2,1)}, bf16[384,768]{1,0:T(8,128)(2,1)}, u32[]{:S(2)}, u32[]{:S(2)}) collective-permute-start(bf16[384,768]{1,0:T(8,128)(2,1)} %pad_maximum_fusion.9), channel_id=1, source_target_pairs={{0,2},{1,3},{2,0},{3,1},{4,6},{5,7},{6,4},{7,5},{8,10},{9,11},{10,... | collective-permute-start | bytes 1769480 | tf_op jit(solution)/shard_map/ppermute | solution.py:460
  982.0 49.9 %collective-permute-start.34 = (bf16[384,768]{1,0:T(8,128)(2,1)}, bf16[384,768]{1,0:T(8,128)(2,1)}, u32[]{:S(2)}, u32[]{:S(2)}) collective-permute-start(bf16[384,768]{1,0:T(8,128)(2,1)} %pad_maximum_fusion.10), channel_id=1, source_target_pairs={{0,3},{1,0},{2,1},{3,2},{4,7},{5,4},{6,5},{7,6},{8,11},{9,8},{10,9... | collective-permute-start | bytes 1769480 | tf_op jit(solution)/shard_map/ppermute | solution.py:460
  995.9 38.3 %copy-start.86 = (bf16[384,768]{1,0:T(8,128)(2,1)}, bf16[384,768]{1,0:T(8,128)(2,1)S(1)}, u32[]{:S(2)}) copy-start(bf16[384,768]{1,0:T(8,128)(2,1)S(1)} %collective-permute-done.32) | copy-start | bytes 1769476
  1040.8 26.1 %collective-permute-start.37 = (bf16[1536,384]{1,0:T(8,128)(2,1)}, bf16[1536,384]{1,0:T(8,128)(2,1)}, u32[]{:S(2)}, u32[]{:S(2)}) collective-permute-start(bf16[1536,384]{1,0:T(8,128)(2,1)} %get-tuple-element.376), channel_id=1, source_target_pairs={{0,8},{8,0},{1,9},{9,1},{2,10},{10,2},{3,11},{11,3},{4,12},{12,4},... | collective-permute-start | bytes 3538952 | tf_op jit(solution)/shard_map/ppermute | solution.py:460
  1042.6 25.7 %collective-permute-start.38 = (bf16[1536,384]{1,0:T(8,128)(2,1)}, bf16[1536,384]{1,0:T(8,128)(2,1)}, u32[]{:S(2)}, u32[]{:S(2)}) collective-permute-start(bf16[1536,384]{1,0:T(8,128)(2,1)} %get-tuple-element.378), channel_id=1, source_target_pairs={{0,16},{16,0},{1,17},{17,1},{2,18},{18,2},{3,19},{19,3},{4,20},{20... | collective-permute-start | bytes 3538952 | tf_op jit(solution)/shard_map/ppermute | solution.py:460
  1044.0 4.4 collective-permute-start.39
  1049.2 5.6 collective-permute-start.40
  1075.4 4.1 collective-permute-start.44
  1075.7 14.1 %collective-permute-start.41 = (bf16[384,768]{1,0:T(8,128)(2,1)}, bf16[384,768]{1,0:T(8,128)(2,1)}, u32[]{:S(2)}, u32[]{:S(2)}) collective-permute-start(bf16[384,768]{1,0:T(8,128)(2,1)} %pad_maximum_fusion.12), channel_id=1, source_target_pairs={{0,1},{1,2},{2,3},{3,0},{4,5},{5,6},{6,7},{7,4},{8,9},{9,10},{10,1... | collective-permute-start | bytes 1769480 | tf_op jit(solution)/shard_map/ppermute | solution.py:460
  1075.7 48.4 %collective-permute-start.42 = (bf16[384,768]{1,0:T(8,128)(2,1)}, bf16[384,768]{1,0:T(8,128)(2,1)}, u32[]{:S(2)}, u32[]{:S(2)}) collective-permute-start(bf16[384,768]{1,0:T(8,128)(2,1)} %pad_maximum_fusion.13), channel_id=1, source_target_pairs={{0,2},{1,3},{2,0},{3,1},{4,6},{5,7},{6,4},{7,5},{8,10},{9,11},{10,... | collective-permute-start | bytes 1769480 | tf_op jit(solution)/shard_map/ppermute | solution.py:460
  1075.7 48.4 %collective-permute-start.43 = (bf16[384,768]{1,0:T(8,128)(2,1)}, bf16[384,768]{1,0:T(8,128)(2,1)}, u32[]{:S(2)}, u32[]{:S(2)}) collective-permute-start(bf16[384,768]{1,0:T(8,128)(2,1)} %pad_maximum_fusion.14), channel_id=1, source_target_pairs={{0,3},{1,0},{2,1},{3,2},{4,7},{5,4},{6,5},{7,6},{8,11},{9,8},{10,9... | collective-permute-start | bytes 1769480 | tf_op jit(solution)/shard_map/ppermute | solution.py:460
  1080.1 4.4 collective-permute-start.45
  (108 other events, 762.5 us)
Sparse Core Ops, SparseCore 0:
  11.4 213.9 all-gather.2
  228.8 233.8 all-gather.4
  711.4 226.5 reduce-scatter.1

commit v12 on v11

--- a/solution.py
+++ b/solution.py
@@ -140,7 +140,7 @@
 
 def forward_body(gated, low_ref, high_ref, *refs):
     query_ref, shared_ref, own_ref, segment_ref, bias_ref = refs[:5]
-    mixed_ref, total_ref, turned_ref, score_ref, sum_ref = refs[5:]
+    mixed_ref, full_ref, total_ref, turned_ref, score_ref, sum_ref = refs[5:]
     step = pl.program_id(0)
 
     @pl.when(step == 0)
@@ -194,7 +194,8 @@
     for pair in range(PAIRS):
         row_total = jnp.sum(totals[pair], axis=0, keepdims=True)
         mixed = pick_heads(sum_ref[pair] * (1.0 / row_total))
-        mixed_ref[:, pair_cols(pair)] = mixed.T.astype(jnp.bfloat16)
+        full_ref[:, pair_cols(pair)] = mixed.T
+        mixed_ref[:, pair_cols(pair)] = full_ref[:, pair_cols(pair)].astype(jnp.bfloat16)
         total_ref[0, pair : pair + 1, :] = peaks[pair] + jnp.log(row_total)
 
 
@@ -224,6 +225,7 @@
             ],
             out_specs=[
                 rows_spec(INNER),
+                rows_spec(INNER),
                 pl.BlockSpec((1, 8, WIDE), lambda i, *_: (i, 0, 0)),
             ],
             scratch_shapes=[
@@ -234,6 +236,7 @@
         ),
         out_shape=[
             jax.ShapeDtypeStruct((tokens, INNER), jnp.bfloat16),
+            jax.ShapeDtypeStruct((tokens, INNER), jnp.float32),
             jax.ShapeDtypeStruct((steps, 8, WIDE), jnp.float32),
         ],
         compiler_params=pltpu.CompilerParams(vmem_limit_bytes=40 << 20),
@@ -247,9 +250,9 @@
 
 
 def backward_body(gated, low_ref, high_ref, *refs):
-    query_ref, grad_ref, shared_ref, own_ref, segment_ref, bias_ref, total_ref = refs[:7]
-    grad_query_ref, grad_shared_ref, bucket_ref = refs[7:10]
-    turned_ref, prob_ref, pull_ref, sum_ref, bias_sum_ref, turn_sum_ref = refs[10:]
+    query_ref, grad_ref, full_ref, shared_ref, own_ref, segment_ref, bias_ref, total_ref = refs[:8]
+    grad_query_ref, grad_shared_ref, bucket_ref = refs[8:11]
+    turned_ref, sum_ref, bias_sum_ref, turn_sum_ref = refs[11:]
     step = pl.program_id(0)
 
     @pl.when(step == 0)
@@ -270,11 +273,20 @@
     grads = [stacked(grad_ref[:, pair_cols(pair)], masks) for pair in range(PAIRS)]
     totals = [total_ref[0, pair : pair + 1, :] for pair in range(PAIRS)]
 
-    def weights(block, deltas):
+    deltas = []
+    for pair in range(PAIRS):
+        cols = pair_cols(pair)
+        product = (grad_ref[:, cols].astype(jnp.float32) * full_ref[:, cols]).T
+        halves = [jnp.sum(half, axis=0, keepdims=True) for half in (product[:64], product[64:])]
+        deltas.append(jnp.concatenate(halves, axis=1))
+    turn_sum_ref[...] = jnp.zeros_like(turn_sum_ref)
+
+    @pl.loop(first, last)
+    def _(block):
         rows = wide_rows(block)
         shift = shift_tile(gated, rows, own_segment, segment_ref, shared_ref)
         offsets = tile_offsets(block, own_block)
-        new_deltas = []
+        gate_part = jnp.zeros((WIDE, BLOCK), jnp.float32)
         for pair in range(PAIRS):
             cols = pair_cols(pair)
             score = lax.dot_general(
@@ -287,27 +299,10 @@
                 preferred_element_type=jnp.float32,
             )
             prob = jnp.exp(score + bias_pair(bias_ref, pair, offsets) + shift - totals[pair])
-            prob_ref[pair, block] = prob
-            pull_ref[pair, block] = pull
             sum_ref[rows, value_cols(pair)] += jnp.dot(
                 prob.astype(jnp.bfloat16), grads[pair], preferred_element_type=jnp.float32
             )
-            new_deltas.append(deltas[pair] + jnp.sum(fold(prob * pull), axis=0))
-        return tuple(new_deltas)
-
-    start = jnp.zeros((8, WIDE), jnp.float32)
-    deltas = lax.fori_loop(first, last, weights, (start,) * PAIRS)
-    deltas = [jnp.sum(delta, axis=0, keepdims=True) for delta in deltas]
-    turn_sum_ref[...] = jnp.zeros_like(turn_sum_ref)
-
-    @pl.loop(first, last)
-    def _(block):
-        rows = wide_rows(block)
-        offsets = tile_offsets(block, own_block)
-        gate_part = jnp.zeros((WIDE, BLOCK), jnp.float32)
-        for pair in range(PAIRS):
-            cols = pair_cols(pair)
-            grad_score = prob_ref[pair, block] * (pull_ref[pair, block] - deltas[pair])
+            grad_score = prob * (pull - deltas[pair])
             bias_sum_ref[pair, offsets[0]] += grad_score[:BLOCK]
             bias_sum_ref[pair, offsets[1]] += grad_score[BLOCK:]
             if gated:
@@ -359,16 +354,17 @@
                 bucket_ref[pair, bucket : bucket + 1, :] = jnp.sum(part, axis=0, keepdims=True)
 
 
-def attend_backward(queries, grad_mixed, shared, log_total, context):
+def attend_backward(queries, grad_mixed, full, shared, log_total, context):
     lows, highs, own_rows, segment_wide, tiles = context
     tokens, (length, width) = queries.shape[0], shared.shape
-    steps, key_blocks = tokens // BLOCK, length // BLOCK
+    steps = tokens // BLOCK
     grad_query, grad_shared, bucket_sums = pl.pallas_call(
         functools.partial(backward_body, width > 2 * INNER),
         grid_spec=pltpu.PrefetchScalarGridSpec(
             num_scalar_prefetch=2,
             grid=(steps,),
             in_specs=[
+                rows_spec(INNER),
                 rows_spec(INNER),
                 rows_spec(INNER),
                 whole((length, width)),
@@ -384,8 +380,6 @@
             ],
             scratch_shapes=[
                 pltpu.VMEM((INNER, length), jnp.bfloat16),
-                pltpu.VMEM((PAIRS, key_blocks // 2, WIDE, WIDE), jnp.float32),
-                pltpu.VMEM((PAIRS, key_blocks // 2, WIDE, WIDE), jnp.float32),
                 pltpu.VMEM((length, width), jnp.float32),
                 pltpu.VMEM((PAIRS, OFFSETS, BLOCK, WIDE), jnp.float32),
                 pltpu.VMEM((PAIRS, BLOCK, WIDE), jnp.float32),
@@ -403,7 +397,7 @@
             transcendentals=tokens * length * 3,
         ),
         name="attend_backward",
-    )(lows, highs, queries, grad_mixed, shared, own_rows, segment_wide, tiles, log_total)
+    )(lows, highs, queries, grad_mixed, full, shared, own_rows, segment_wide, tiles, log_total)
     table = jnp.sum(bucket_sums.reshape(PAIRS, BUCKETS, 2, BLOCK), axis=3)
     return grad_query, grad_shared, table.transpose(1, 0, 2).reshape(BUCKETS, HEADS)
 
@@ -1051,7 +1045,7 @@
     if gate_low is not None:
         parts.append(jnp.broadcast_to(gate_low[:, None], (stream.shape[0], BLOCK)))
     shared = with_neighbours(jnp.concatenate(parts, axis=1))
-    attended, log_total = attend_forward(queries, shared, context)
+    attended, full, log_total = attend_forward(queries, shared, context)
     middle = stream + times_plain(attended, gathered[3 * INNER : 4 * INNER])
     normed_two, inverse_two = rms_forward(middle, gain_two)
     normed_two_low = normed_two.astype(jnp.bfloat16)
@@ -1063,6 +1057,7 @@
         queries,
         shared,
         attended,
+        full,
         log_total,
         middle,
         inverse_two,
@@ -1080,6 +1075,7 @@
         queries,
         shared,
         attended,
+        full,
         log_total,
         middle,
         inverse_two,
@@ -1105,7 +1101,7 @@
     late_sides = (late_sides, shift(late_sides, "c", 1))
     grad_mixed = times_rows(middle_low, gathered[3 * INNER : 4 * INNER]).astype(jnp.bfloat16)
     grad_query, grad_shared, grad_table = attend_backward(
-        queries, grad_mixed, shared, log_total, context
+        queries, grad_mixed, full, shared, log_total, context
     )
     if before is not None:
         grad_query, grad_shared = before.settle((grad_query, grad_shared), 0, 1)

time: 1150 us -> 1110 us (0.965)
  waiting for transfers between devices: 636 us -> 596 us
    ppermute x29, waiting for transfers between devices: 179 us -> 149 us  [shift(): lax.ppermute(value, axis, [(i, (i + amount) % count) for i in range(count)])]
    unnamed x261 -> x271, local copies, waits for them, and re-layouts: 45.3 us -> 44.4 us
  transfers between devices with their start and end apart: 49 -> 49, of which waited for: 25 -> 26; matrix products, arithmetic and copies ran while one was open for 11% -> 11% of each run, Pallas kernels for 14% -> 15%
where the time goes in v12:
time: 1110 us; the launch traced here: 1100 us
  waiting for transfers between devices  596 us (54%)
  Pallas kernels  239 us (22%)
  other arithmetic  76.3 us (7%)
  starting transfers between devices  70.8 us (6%)
  local copies, waits for them, and re-layouts  64 us (6%)
  matrix products  34.9 us (3%)
  between operations  15.9 us (1%)
    all_gather x2, waiting for transfers between devices, fetch_rows(): return lax.all_gather(local_rows, DEVICES, axis=0, tiled=True)  333 us
    ppermute x29, waiting for transfers between devices, shift(): lax.ppermute(value, axis, [(i, (i + amount) % count) for i in range(count)])  149 us
    ppermute x4, waiting for transfers between devices, far_pair(): got = lax.ppermute(sent, 'z', pairs)  90 us
    pallas_call x2, Pallas kernels, ffn_forward(): pl.pallas_call(ffn_forward_body, grid_spec=pltpu.PrefetchScalarGridSpec(n...  56.3 us
    pallas_call x2, Pallas kernels, ffn_backward(): pl.pallas_call(ffn_backward_body, grid_spec=pltpu.PrefetchScalarGridSpec(...  53.4 us
    pallas_call x2, Pallas kernels, weight_grads(): pl.pallas_call(functools.partial(weight_grads_body, chunks, tile), grid_s...  47.6 us
    unnamed x271, local copies, waits for them, and re-layouts  44.4 us
    pallas_call x2, Pallas kernels, attend_backward(): pl.pallas_call(functools.partial(backward_body, width > 2 * INNER), grid_...  40.8 us
  transfers between devices with their start and end apart: 49, of which 26 were waited for; matrix products, arithmetic and copies ran while one was open for 11% of the time, Pallas kernels for 15%

profile of v12, /device:TPU:24, one launch (start us, length us, event | category | flops | bytes accessed | tf_op | source)
XLA Modules:
  0.0 1097.1 jit_solution(9756860845659733059)
XLA Ops:
  7.2 2.5 copy.121
  12.0 2.4 copy.120
  18.2 207.2 %all-gather.3.cloned.1.call-done.refs_2_.refs_3_.refs_4_.refs_5_ = bf16[12288,1472]{1,0:T(8,128)(2,1)} async-done(((bf16[384,1472]{1,0:T(8,128)(2,1)}), bf16[12288,1472]{1,0:T(8,128)(2,1)}) %all-gather.3.cloned.1.call-update) | async-done | bytes 36175888 | tf_op jit(solution)/shard_map/all_gather | solution.py:1036
  225.4 4.7 fusion.33
  233.3 6.1 collective-permute-start.2
  240.2 4.7 bias_tiles.1.refs_4_.refs_6_
  244.9 3.5 copy.126
  248.5 23.5 %collective-permute-done = bf16[288,768]{1,0:T(8,128)(2,1)S(1)} collective-permute-done((bf16[288,768]{1,0:T(8,128)(2,1)S(1)}, bf16[288,768]{1,0:T(8,128)(2,1)S(1)}, u32[]{:S(2)}, u32[]{:S(2)}) %collective-permute-start) | collective-permute-done | bytes 442400 | tf_op jit(solution)/shard_map/ppermute | solution.py:468
  272.1 15.6 %collective-permute-done.1 = bf16[512,768]{1,0:T(8,128)(2,1)} collective-permute-done((bf16[512,768]{1,0:T(8,128)(2,1)}, bf16[512,768]{1,0:T(8,128)(2,1)}, u32[]{:S(2)}, u32[]{:S(2)}) %collective-permute-start.1) | collective-permute-done | bytes 786464 | tf_op jit(solution)/shard_map/ppermute | solution.py:460
  290.6 8.1 attend_forward.2
  298.8 2.8 multiply_reduce_fusion.10
  303.2 28.2 %ffn_forward.2 = (f32[512,1472]{1,0:T(8,128)}, f32[512,3584]{1,0:T(8,128)}, f32[512,3584]{1,0:T(8,128)}, bf16[6144,512]{1,0:T(8,128)(2,1)}, bf16[6144,512]{1,0:T(8,128)(2,1)}) custom-call(s32[2]{0:T(128)S(1)} %pad_add_fusion.core_ref, bf16[512,1472]{1,0:T(8,128)(2,1)S(1)} %multiply_convert_fusion.2.refs_0_, f32[512,1472]{1,0:T(8,128)} %copy-done.58, ...), custom_call_target="tpu_custom_call" | custom-call | flops 16206790656 | bytes 50003968 | tf_op jit(solution)/shard_map/ffn_forward/pallas_call | solution.py:654
  331.4 2.3 multiply_reduce_fusion.9
  336.2 126.2 %all-gather.5.cloned.1.call-done.refs_2_.refs_3_.refs_4_.refs_5_ = bf16[12288,1472]{1,0:T(8,128)(2,1)} async-done(((bf16[384,1472]{1,0:T(8,128)(2,1)}), bf16[12288,1472]{1,0:T(8,128)(2,1)}) %all-gather.5.cloned.1.call-update) | async-done | bytes 36175888 | tf_op jit(solution)/shard_map/all_gather | solution.py:1036
  462.4 4.2 fusion.36
  469.0 5.1 collective-permute-start.5
  475.5 39.8 %collective-permute-done.3 = bf16[288,896]{1,0:T(8,128)(2,1)S(1)} collective-permute-done((bf16[288,896]{1,0:T(8,128)(2,1)S(1)}, bf16[288,896]{1,0:T(8,128)(2,1)S(1)}, u32[]{:S(2)}, u32[]{:S(2)}) %collective-permute-start.3) | collective-permute-done | bytes 516128 | tf_op jit(solution)/shard_map/ppermute | solution.py:468
  516.7 8.1 attend_forward.3
  524.8 2.8 multiply_reduce_fusion.7
  529.3 28.1 %ffn_forward.3 = (f32[512,1472]{1,0:T(8,128)}, f32[512,3584]{1,0:T(8,128)}, f32[512,3584]{1,0:T(8,128)}, bf16[6144,512]{1,0:T(8,128)(2,1)}, bf16[6144,512]{1,0:T(8,128)(2,1)}) custom-call(s32[2]{0:T(128)S(1)} %pad_add_fusion.core_ref, bf16[512,1472]{1,0:T(8,128)(2,1)S(1)} %multiply_convert_fusion.refs_0_, f32[512,1472]{1,0:T(8,128)} %copy-done.60, ...), custom_call_target="tpu_custom_call" | custom-call | flops 16206790656 | bytes 50003968 | tf_op jit(solution)/shard_map/ffn_forward/pallas_call | solution.py:654
  557.5 26.0 %ffn_backward.2 = (f32[512,1472]{1,0:T(8,128)}, bf16[6144,512]{1,0:T(8,128)(2,1)}, bf16[6144,512]{1,0:T(8,128)(2,1)}) custom-call(s32[2]{0:T(128)S(1)} %pad_add_fusion.core_ref, bf16[512,1472]{1,0:T(8,128)(2,1)S(1)} %bitcast_convert_fusion.refs_0_, f32[512,3584]{1,0:T(8,128)} %get-tuple-element.210.refs_1_, ...), custom_call_target="tpu_custom_call", output_to_operand_aliasing={{1}: (7, {}), {2}: (8, {})} | custom-call | flops 16206790656 | bytes 53673984 | tf_op jit(solution)/shard_map/ffn_backward/pallas_call | solution.py:719
  588.9 2.3 multiply_reduce_fusion.1
  591.2 2.5 fusion.51
  593.7 2.9 convolution_convert_fusion.1.refs_1_
  596.6 20.9 %attend_backward.2 = (bf16[512,384]{1,0:T(8,128)(2,1)S(1)}, bf16[2304,896]{1,0:T(8,128)(2,1)}, f32[3,32,256]{2,1,0:T(8,128)S(1)}) custom-call(s32[4]{0:T(128)S(1)} %get-tuple-element.545.low_ref, s32[4]{0:T(128)S(1)} %get-tuple-element.544.high_ref, bf16[512,384]{1,0:T(8,128)(2,1)S(1)} %copy-done.31, bf16[512,384]{1,0:T(8,128)(2,1)S(1)} %convolution_convert_fusion.1.refs_1_, ...), custom_call_target="tpu_custom_call" | custom-call | flops 4529848320 | bytes 12582912 | tf_op jit(solution)/shard_map/attend_backward/pallas_call | solution.py:361
  619.7 2.2 collective-permute-start.8
  624.5 11.9 %collective-permute-start.10 = (bf16[288,896]{1,0:T(8,128)(2,1)S(1)}, bf16[288,896]{1,0:T(8,128)(2,1)S(1)}, u32[]{:S(2)}, u32[]{:S(2)}) collective-permute-start(bf16[288,896]{1,0:T(8,128)(2,1)S(1)} %slice_select_fusion), channel_id=1, source_target_pairs={{0,2},{1,3},{2,0},{3,1},{4,6},{5,7},{6,4},{7,5},{8,10},{9,11},{10,... | collective-permute-start | bytes 1548296 | tf_op jit(solution)/shard_map/ppermute | solution.py:468
  638.5 22.7 %weight_grads.2 = (bf16[3072,256]{1,0:T(8,128)(2,1)S(1)}, bf16[3072,256]{1,0:T(8,128)(2,1)S(1)}, bf16[3072,256]{1,0:T(8,128)(2,1)S(1)}, bf16[3072,256]{1,0:T(8,128)(2,1)S(1)}, bf16[6144,1024]{1,0:T(8,128)(2,1)}) custom-call(s32[6]{0:T(128)S(1)} %copy-done.45, bf16[6144,512]{1,0:T(8,128)(2,1)} %get-tuple-element.220.refs_0_, ...), custom_call_target="tpu_custom_call" | custom-call | flops 18522046464 | bytes 31457280 | tf_op jit(solution)/shard_map/weight_grads/pallas_call | solution.py:879
  661.3 16.7 %collective-permute-done.10 = bf16[288,896]{1,0:T(8,128)(2,1)S(1)} collective-permute-done((bf16[288,896]{1,0:T(8,128)(2,1)S(1)}, bf16[288,896]{1,0:T(8,128)(2,1)S(1)}, u32[]{:S(2)}, u32[]{:S(2)}) %collective-permute-start.10) | collective-permute-done | bytes 516128 | tf_op jit(solution)/shard_map/ppermute | solution.py:468
  682.9 2.5 pad_maximum_fusion.5
  690.4 10.4 attention_fill.2
  709.0 6.6 multiply_reduce_fusion.2
  715.7 2.7 fusion.49
  718.4 27.3 %ffn_backward.3 = (f32[512,1472]{1,0:T(8,128)}, bf16[6144,512]{1,0:T(8,128)(2,1)}, bf16[6144,512]{1,0:T(8,128)(2,1)}) custom-call(s32[2]{0:T(128)S(1)} %pad_add_fusion.core_ref, bf16[512,1472]{1,0:T(8,128)(2,1)S(1)} %get-tuple-element.472.refs_0_, f32[512,3584]{1,0:T(8,128)} %get-tuple-element.250.refs_1_, ...), custom_call_target="tpu_custom_call", output_to_operand_aliasing={{1}: (7, {}), {2}: (8, {})} | custom-call | flops 16206790656 | bytes 53673984 | tf_op jit(solution)/shard_map/ffn_backward/pallas_call | solution.py:719
  745.8 2.6 collective-permute-done.13
  763.6 2.5 fusion.48
  766.5 3.5 convolution_convert_fusion.refs_1_
  770.0 19.9 %attend_backward.3 = (bf16[512,384]{1,0:T(8,128)(2,1)S(1)}, bf16[2304,768]{1,0:T(8,128)(2,1)}, f32[3,32,256]{2,1,0:T(8,128)S(1)}) custom-call(s32[4]{0:T(128)S(1)} %get-tuple-element.545.low_ref, s32[4]{0:T(128)S(1)} %get-tuple-element.544.high_ref, bf16[512,384]{1,0:T(8,128)(2,1)S(1)} %copy-done.34, bf16[512,384]{1,0:T(8,128)(2,1)S(1)} %convolution_convert_fusion.refs_1_, ...), custom_call_target="tpu_custom_call" | custom-call | flops 4529848320 | bytes 12582912 | tf_op jit(solution)/shard_map/attend_backward/pallas_call | solution.py:361
  797.9 7.9 collective-permute-start.21
  805.8 24.9 %weight_grads.3 = (bf16[3072,384]{1,0:T(8,128)(2,1)}, bf16[3072,384]{1,0:T(8,128)(2,1)}, bf16[3072,384]{1,0:T(8,128)(2,1)S(1)}, bf16[3072,384]{1,0:T(8,128)(2,1)...) custom-call(s32[6]{0:T(128)S(1)} %copy-done.46, ...), custom_call_target="tpu_custom_call" | custom-call | flops 18522046464 | bytes 31457280 | tf_op jit(solution)/shard_map/weight_grads/pallas_call | solution.py:879
  830.7 10.1 collective-permute-done.21
  844.1 2.2 collective-permute-done.22.refs_1_
  846.3 9.5 attention_fill.3
  860.1 4.6 collective-permute-start.25
  865.5 7.4 fusion.24
  877.1 9.0 collective-permute-done.26
  886.1 24.6 %collective-permute-done.27 = bf16[384,512]{1,0:T(8,128)(2,1)S(1)} collective-permute-done((bf16[384,512]{1,0:T(8,128)(2,1)}, bf16[384,512]{1,0:T(8,128)(2,1)S(1)}, u32[]{:S(2)}, u32[]{:S(2)}) %collective-permute-start.27) | collective-permute-done | bytes 393248 | tf_op jit(solution)/shard_map/ppermute | solution.py:454
  910.7 16.0 %collective-permute-done.24 = bf16[3072,384]{1,0:T(8,128)(2,1)} collective-permute-done((bf16[3072,384]{1,0:T(8,128)(2,1)}, bf16[3072,384]{1,0:T(8,128)(2,1)}, u32[]{:S(2)}, u32[]{:S(2)}) %collective-permute-start.24) | collective-permute-done | bytes 2359328 | tf_op jit(solution)/shard_map/ppermute | solution.py:454
  926.7 3.1 add_convert_fusion.2
  930.1 2.3 add_convert_fusion.3
  932.6 4.3 collective-permute-start.30
  939.0 24.8 %collective-permute-done.30 = bf16[1536,384]{1,0:T(8,128)(2,1)S(1)} collective-permute-done((bf16[1536,384]{1,0:T(8,128)(2,1)S(1)}, bf16[1536,384]{1,0:T(8,128)(2,1)S(1)}, u32[]{:S(2)}, u32[]{:S(2)}) %collective-permute-start.30) | collective-permute-done | bytes 1179680 | tf_op jit(solution)/shard_map/ppermute | solution.py:454
  972.2 3.6 copy.135
  975.9 5.3 collective-permute-done.32
  981.1 17.3 %collective-permute-done.33 = bf16[384,768]{1,0:T(8,128)(2,1)} collective-permute-done((bf16[384,768]{1,0:T(8,128)(2,1)}, bf16[384,768]{1,0:T(8,128)(2,1)}, u32[]{:S(2)}, u32[]{:S(2)}) %collective-permute-start.33) | collective-permute-done | bytes 589856 | tf_op jit(solution)/shard_map/ppermute | solution.py:454
  998.5 3.2 collective-permute-done.35
  1001.7 2.3 add_convert_fusion
  1006.5 2.4 add_convert_fusion.1
  1010.6 2.6 collective-permute-start.37
  1015.5 2.3 copy.136
  1021.4 4.1 collective-permute-done.40
  1025.5 3.8 collective-permute-done.37
  1047.8 6.3 collective-permute-done.41
  1054.1 30.1 %collective-permute-done.42 = bf16[384,768]{1,0:T(8,128)(2,1)} collective-permute-done((bf16[384,768]{1,0:T(8,128)(2,1)}, bf16[384,768]{1,0:T(8,128)(2,1)}, u32[]{:S(2)}, u32[]{:S(2)}) %collective-permute-start.42) | collective-permute-done | bytes 589856 | tf_op jit(solution)/shard_map/ppermute | solution.py:454
  (463 shorter events, 135.2 us)
Async XLA Ops:
  7.2 218.2 %all-gather.3.cloned.1.call-start = ((), (), s32[]{:S(2)}) async-start(), calls=%async_computation.1 | async-start | bytes 38928384 | tf_op jit(solution)/shard_map/all_gather | solution.py:1036
  9.7 452.7 %all-gather.5.cloned.1.call-start = ((), (), s32[]{:S(2)}) async-start(), calls=%async_computation.2 | async-start | bytes 38928384 | tf_op jit(solution)/shard_map/all_gather | solution.py:1036
  11.9 986.6 %reduce-scatter.2.cloned.1.call-start = ((), (), s32[]{:S(2)}) async-start(), calls=%async_computation.3 | async-start | bytes 13369344 | tf_op jit(solution)/shard_map/reduce_scatter | solution.py:1133
  15.8 286.4 %copy-start.96 = (f32[1472]{0:T(1024)}, f32[1472]{0:T(1024)S(1)}, u32[]{:S(2)}) copy-start(f32[1472]{0:T(1024)S(1)} %get-tuple-element.463) | copy-start | bytes 17668
  16.7 213.4 %copy-start.116 = (f32[512]{0:T(512)}, f32[512]{0:T(512)S(1)}, u32[]{:S(2)}) copy-start(f32[512]{0:T(512)S(1)} %get-tuple-element.531) | copy-start | bytes 6148
  18.2 221.3 %copy-start.126 = (f32[32,6]{0,1:T(8,128)S(1)}, f32[32,6]{0,1:T(8,128)}, u32[]{:S(2)}) copy-start(f32[32,6]{0,1:T(8,128)} %param.13) | copy-start | bytes 2308
  231.1 40.9 %collective-permute-start = (bf16[288,768]{1,0:T(8,128)(2,1)S(1)}, bf16[288,768]{1,0:T(8,128)(2,1)S(1)}, u32[]{:S(2)}, u32[]{:S(2)}) collective-permute-start(bf16[288,768]{1,0:T(8,128)(2,1)S(1)} %slice_select_fusion.1), channel_id=1, source_target_pairs={{0,2},{1,3},{2,0},{3,1},{4,6},{5,7},{6,4},{7,5},{8,10},{9,11},{10,... | collective-permute-start | bytes 1327112 | tf_op jit(solution)/shard_map/ppermute | solution.py:468
  231.8 55.9 %collective-permute-start.1 = (bf16[512,768]{1,0:T(8,128)(2,1)}, bf16[512,768]{1,0:T(8,128)(2,1)}, u32[]{:S(2)}, u32[]{:S(2)}) collective-permute-start(bf16[512,768]{1,0:T(8,128)(2,1)} %slice.177), channel_id=1, source_target_pairs={{0,1},{1,2},{2,3},{4,5},{5,6},{6,7},{8,9},{9,10},{10,11},{12,13},{... | collective-permute-start | bytes 2359304 | tf_op jit(solution)/shard_map/ppermute | solution.py:460
  233.3 55.6 %collective-permute-start.2 = (bf16[512,768]{1,0:T(8,128)(2,1)}, bf16[512,768]{1,0:T(8,128)(2,1)}, u32[]{:S(2)}, u32[]{:S(2)}) collective-permute-start(bf16[512,768]{1,0:T(8,128)(2,1)} %slice.177), channel_id=1, source_target_pairs={{1,0},{2,1},{3,2},{5,4},{6,5},{7,6},{9,8},{10,9},{11,10},{13,12},{... | collective-permute-start | bytes 2359304 | tf_op jit(solution)/shard_map/ppermute | solution.py:460
  248.5 42.1 %copy-start.33 = (bf16[512,384]{1,0:T(8,128)(2,1)}, bf16[512,384]{1,0:T(8,128)(2,1)S(1)}, u32[]{:S(2)}) copy-start(bf16[512,384]{1,0:T(8,128)(2,1)S(1)} %slice.174.refs_0_) | copy-start | bytes 1179652
  302.2 29.2 %copy-start.108 = (f32[512]{0:T(512)}, f32[512]{0:T(512)S(1)}, u32[]{:S(2)}) copy-start(f32[512]{0:T(512)S(1)} %get-tuple-element.533) | copy-start | bytes 6148
  303.2 28.2 %copy-start.1 = (bf16[512,1472]{1,0:T(8,128)(2,1)}, bf16[512,1472]{1,0:T(8,128)(2,1)S(1)}, u32[]{:S(2)}) copy-start(bf16[512,1472]{1,0:T(8,128)(2,1)S(1)} %multiply_convert_fusion.2.refs_0_) | copy-start | bytes 4521988
  303.2 31.8 %copy-start.104 = (f32[1472]{0:T(1024)S(1)}, f32[1472]{0:T(1024)}, u32[]{:S(2)}) copy-start(f32[1472]{0:T(1024)} %param.12) | copy-start | bytes 17668
  336.2 130.5 %copy-start.75 = (bf16[512,1472]{1,0:T(8,128)(2,1)}, bf16[512,1472]{1,0:T(8,128)(2,1)S(1)}, u32[]{:S(2)}) copy-start(bf16[512,1472]{1,0:T(8,128)(2,1)S(1)} %get-tuple-element.485) | copy-start | bytes 4521988
  467.7 47.7 %collective-permute-start.4 = (bf16[512,896]{1,0:T(8,128)(2,1)S(1)}, bf16[512,896]{1,0:T(8,128)(2,1)S(1)}, u32[]{:S(2)}, u32[]{:S(2)}) collective-permute-start(bf16[512,896]{1,0:T(8,128)(2,1)S(1)} %pad_maximum_fusion.2), channel_id=1, source_target_pairs={{0,1},{1,2},{2,3},{4,5},{5,6},{6,7},{8,9},{9,10},{10,11},{12,13},{... | collective-permute-start | bytes 2752520 | tf_op jit(solution)/shard_map/ppermute | solution.py:460
  469.0 46.7 %collective-permute-start.5 = (bf16[512,896]{1,0:T(8,128)(2,1)S(1)}, bf16[512,896]{1,0:T(8,128)(2,1)S(1)}, u32[]{:S(2)}, u32[]{:S(2)}) collective-permute-start(bf16[512,896]{1,0:T(8,128)(2,1)S(1)} %pad_maximum_fusion.2), channel_id=1, source_target_pairs={{1,0},{2,1},{3,2},{5,4},{6,5},{7,6},{9,8},{10,9},{11,10},{13,12},{... | collective-permute-start | bytes 2752520 | tf_op jit(solution)/shard_map/ppermute | solution.py:460
  474.2 41.1 %collective-permute-start.3 = (bf16[288,896]{1,0:T(8,128)(2,1)S(1)}, bf16[288,896]{1,0:T(8,128)(2,1)S(1)}, u32[]{:S(2)}, u32[]{:S(2)}) collective-permute-start(bf16[288,896]{1,0:T(8,128)(2,1)S(1)} %fusion.44), channel_id=1, source_target_pairs={{0,2},{1,3},{2,0},{3,1},{4,6},{5,7},{6,4},{7,5},{8,10},{9,11},{10,... | collective-permute-start | bytes 1548296 | tf_op jit(solution)/shard_map/ppermute | solution.py:468
  475.4 40.5 %copy-start.30 = (bf16[512,384]{1,0:T(8,128)(2,1)}, bf16[512,384]{1,0:T(8,128)(2,1)S(1)}, u32[]{:S(2)}) copy-start(bf16[512,384]{1,0:T(8,128)(2,1)S(1)} %slice.180.refs_0_) | copy-start | bytes 1179652
  528.3 29.2 %copy-start.110 = (f32[512]{0:T(512)}, f32[512]{0:T(512)S(1)}, u32[]{:S(2)}) copy-start(f32[512]{0:T(512)S(1)} %get-tuple-element.537) | copy-start | bytes 6148
  529.3 28.1 %copy-start.3 = (bf16[512,1472]{1,0:T(8,128)(2,1)}, bf16[512,1472]{1,0:T(8,128)(2,1)S(1)}, u32[]{:S(2)}) copy-start(bf16[512,1472]{1,0:T(8,128)(2,1)S(1)} %multiply_convert_fusion.refs_0_) | copy-start | bytes 4521988
  583.5 54.9 %collective-permute-start.6 = (bf16[6144,512]{1,0:T(8,128)(2,1)}, bf16[6144,512]{1,0:T(8,128)(2,1)}, u32[]{:S(2)}, u32[]{:S(2)}) collective-permute-start(bf16[6144,512]{1,0:T(8,128)(2,1)} %get-tuple-element.221), channel_id=1, source_target_pairs={{0,4},{4,0},{1,5},{5,1},{2,6},{6,2},{3,7},{7,3},{8,12},{12,8},{9,1... | collective-permute-start | bytes 18874376 | tf_op jit(solution)/shard_map/ppermute | solution.py:454
  587.4 51.1 %collective-permute-start.7 = (bf16[1024,1536]{1,0:T(8,128)(2,1)S(1)}, bf16[1024,1536]{1,0:T(8,128)(2,1)S(1)}, u32[]{:S(2)}, u32[]{:S(2)}) collective-permute-start(bf16[1024,1536]{1,0:T(8,128)(2,1)S(1)} %fusion.11.refs_2_.refs_3_), channel_id=1, source_target_pairs={{0,4},{4,0},{1,5},{5,1},{2,6},{6,2},{3,7},{7,3},{8,12},{12,8},{9,1... | collective-permute-start | bytes 9437192 | tf_op jit(solution)/shard_map/ppermute | solution.py:454
  617.5 61.1 %copy-start.32 = (bf16[512,384]{1,0:T(8,128)(2,1)}, bf16[512,384]{1,0:T(8,128)(2,1)S(1)}, u32[]{:S(2)}) copy-start(bf16[512,384]{1,0:T(8,128)(2,1)S(1)} %get-tuple-element.217) | copy-start | bytes 1179652
  619.7 58.2 %collective-permute-start.8 = (bf16[512,896]{1,0:T(8,128)(2,1)S(1)}, bf16[512,896]{1,0:T(8,128)(2,1)S(1)}, u32[]{:S(2)}, u32[]{:S(2)}) collective-permute-start(bf16[512,896]{1,0:T(8,128)(2,1)S(1)} %get-tuple-element.479), channel_id=1, source_target_pairs={{1,0},{2,1},{3,2},{5,4},{6,5},{7,6},{9,8},{10,9},{11,10},{13,12},{... | collective-permute-start | bytes 2752520 | tf_op jit(solution)/shard_map/ppermute | solution.py:460
  621.9 56.0 %collective-permute-start.9 = (bf16[512,896]{1,0:T(8,128)(2,1)S(1)}, bf16[512,896]{1,0:T(8,128)(2,1)S(1)}, u32[]{:S(2)}, u32[]{:S(2)}) collective-permute-start(bf16[512,896]{1,0:T(8,128)(2,1)S(1)} %get-tuple-element.478), channel_id=1, source_target_pairs={{0,1},{1,2},{2,3},{4,5},{5,6},{6,7},{8,9},{9,10},{10,11},{12,13},{... | collective-permute-start | bytes 2752520 | tf_op jit(solution)/shard_map/ppermute | solution.py:460
  624.5 53.4 %collective-permute-start.10 = (bf16[288,896]{1,0:T(8,128)(2,1)S(1)}, bf16[288,896]{1,0:T(8,128)(2,1)S(1)}, u32[]{:S(2)}, u32[]{:S(2)}) collective-permute-start(bf16[288,896]{1,0:T(8,128)(2,1)S(1)} %slice_select_fusion), channel_id=1, source_target_pairs={{0,2},{1,3},{2,0},{3,1},{4,6},{5,7},{6,4},{7,5},{8,10},{9,11},{10,... | collective-permute-start | bytes 1548296 | tf_op jit(solution)/shard_map/ppermute | solution.py:468
  638.5 47.0 %collective-permute-start.12 = (bf16[1024,1536]{1,0:T(8,128)(2,1)}, bf16[1024,1536]{1,0:T(8,128)(2,1)}, u32[]{:S(2)}, u32[]{:S(2)}) collective-permute-start(bf16[1024,1536]{1,0:T(8,128)(2,1)} %fusion.12.refs_2_), channel_id=1, source_target_pairs={{0,4},{4,0},{1,5},{5,1},{2,6},{6,2},{3,7},{7,3},{8,12},{12,8},{9,1... | collective-permute-start | bytes 9437192 | tf_op jit(solution)/shard_map/ppermute | solution.py:454
  680.0 5.4 collective-permute-start.11
  705.5 42.9 %collective-permute-start.13 = (bf16[3072,256]{1,0:T(8,128)(2,1)}, bf16[3072,256]{1,0:T(8,128)(2,1)}, u32[]{:S(2)}, u32[]{:S(2)}) collective-permute-start(bf16[3072,256]{1,0:T(8,128)(2,1)} %copy-done.37), channel_id=1, source_target_pairs={{0,16},{16,0},{1,17},{17,1},{2,18},{18,2},{3,19},{19,3},{4,20},{20... | collective-permute-start | bytes 4718600 | tf_op jit(solution)/shard_map/ppermute | solution.py:454
  706.7 42.6 %collective-permute-start.14 = (bf16[3072,256]{1,0:T(8,128)(2,1)}, bf16[3072,256]{1,0:T(8,128)(2,1)}, u32[]{:S(2)}, u32[]{:S(2)}) collective-permute-start(bf16[3072,256]{1,0:T(8,128)(2,1)} %copy-done.40), channel_id=1, source_target_pairs={{0,8},{8,0},{1,9},{9,1},{2,10},{10,2},{3,11},{11,3},{4,12},{12,4},... | collective-permute-start | bytes 4718600 | tf_op jit(solution)/shard_map/ppermute | solution.py:454
  718.4 30.8 %copy-start.23 = (bf16[3072,256]{1,0:T(8,128)(2,1)S(1)}, bf16[3072,256]{1,0:T(8,128)(2,1)}, u32[]{:S(2)}) copy-start(bf16[3072,256]{1,0:T(8,128)(2,1)} %copy-done.22) | copy-start | bytes 4718596
  755.7 50.1 %collective-permute-start.17 = (bf16[6144,512]{1,0:T(8,128)(2,1)}, bf16[6144,512]{1,0:T(8,128)(2,1)}, u32[]{:S(2)}, u32[]{:S(2)}) collective-permute-start(bf16[6144,512]{1,0:T(8,128)(2,1)} %get-tuple-element.287), channel_id=1, source_target_pairs={{0,4},{4,0},{1,5},{5,1},{2,6},{6,2},{3,7},{7,3},{8,12},{12,8},{9,1... | collective-permute-start | bytes 18874376 | tf_op jit(solution)/shard_map/ppermute | solution.py:454
  757.7 40.2 %collective-permute-start.18 = (bf16[1024,1536]{1,0:T(8,128)(2,1)S(1)}, bf16[1024,1536]{1,0:T(8,128)(2,1)}, u32[]{:S(2)}, u32[]{:S(2)}) collective-permute-start(bf16[1024,1536]{1,0:T(8,128)(2,1)S(1)} %fusion.13.refs_2_.refs_3_), channel_id=1, source_target_pairs={{0,4},{4,0},{1,5},{5,1},{2,6},{6,2},{3,7},{7,3},{8,12},{12,8},{9,1... | collective-permute-start | bytes 9437192 | tf_op jit(solution)/shard_map/ppermute | solution.py:454
  758.2 31.7 %collective-permute-start.15 = (bf16[1536,256]{1,0:T(8,128)(2,1)}, bf16[1536,256]{1,0:T(8,128)(2,1)}, u32[]{:S(2)}, u32[]{:S(2)}) collective-permute-start(bf16[1536,256]{1,0:T(8,128)(2,1)} %get-tuple-element.266), channel_id=1, source_target_pairs={{0,8},{8,0},{1,9},{9,1},{2,10},{10,2},{3,11},{11,3},{4,12},{12,4},... | collective-permute-start | bytes 2359304 | tf_op jit(solution)/shard_map/ppermute | solution.py:454
  759.6 30.3 %collective-permute-start.16 = (bf16[1536,256]{1,0:T(8,128)(2,1)}, bf16[1536,256]{1,0:T(8,128)(2,1)S(1)}, u32[]{:S(2)}, u32[]{:S(2)}) collective-permute-start(bf16[1536,256]{1,0:T(8,128)(2,1)} %get-tuple-element.268), channel_id=1, source_target_pairs={{0,16},{16,0},{1,17},{17,1},{2,18},{18,2},{3,19},{19,3},{4,20},{20... | collective-permute-start | bytes 2359304 | tf_op jit(solution)/shard_map/ppermute | solution.py:454
  766.4 77.6 %collective-permute-start.23 = (bf16[1024,1536]{1,0:T(8,128)(2,1)S(1)}, bf16[1024,1536]{1,0:T(8,128)(2,1)}, u32[]{:S(2)}, u32[]{:S(2)}) collective-permute-start(bf16[1024,1536]{1,0:T(8,128)(2,1)S(1)} %fusion.14.refs_2_), channel_id=1, source_target_pairs={{0,4},{4,0},{1,5},{5,1},{2,6},{6,2},{3,7},{7,3},{8,12},{12,8},{9,1... | collective-permute-start | bytes 9437192 | tf_op jit(solution)/shard_map/ppermute | solution.py:454
  794.3 46.4 %collective-permute-start.19 = (bf16[512,768]{1,0:T(8,128)(2,1)S(1)}, bf16[512,768]{1,0:T(8,128)(2,1)}, u32[]{:S(2)}, u32[]{:S(2)}) collective-permute-start(bf16[512,768]{1,0:T(8,128)(2,1)S(1)} %get-tuple-element.482), channel_id=1, source_target_pairs={{1,0},{2,1},{3,2},{5,4},{6,5},{7,6},{9,8},{10,9},{11,10},{13,12},{... | collective-permute-start | bytes 2359304 | tf_op jit(solution)/shard_map/ppermute | solution.py:460
  796.5 44.2 %collective-permute-start.20 = (bf16[512,768]{1,0:T(8,128)(2,1)S(1)}, bf16[512,768]{1,0:T(8,128)(2,1)}, u32[]{:S(2)}, u32[]{:S(2)}) collective-permute-start(bf16[512,768]{1,0:T(8,128)(2,1)S(1)} %get-tuple-element.481), channel_id=1, source_target_pairs={{0,1},{1,2},{2,3},{4,5},{5,6},{6,7},{8,9},{9,10},{10,11},{12,13},{... | collective-permute-start | bytes 2359304 | tf_op jit(solution)/shard_map/ppermute | solution.py:460
  797.9 42.9 %collective-permute-start.21 = (bf16[288,768]{1,0:T(8,128)(2,1)S(1)}, bf16[288,768]{1,0:T(8,128)(2,1)S(1)}, u32[]{:S(2)}, u32[]{:S(2)}) collective-permute-start(bf16[288,768]{1,0:T(8,128)(2,1)S(1)} %slice_select_fusion.2), channel_id=1, source_target_pairs={{0,2},{1,3},{2,0},{3,1},{4,6},{5,7},{6,4},{7,5},{8,10},{9,11},{10,... | collective-permute-start | bytes 1327112 | tf_op jit(solution)/shard_map/ppermute | solution.py:468
  842.8 3.5 collective-permute-start.22
  860.1 66.6 %collective-permute-start.24 = (bf16[3072,384]{1,0:T(8,128)(2,1)}, bf16[3072,384]{1,0:T(8,128)(2,1)}, u32[]{:S(2)}, u32[]{:S(2)}) collective-permute-start(bf16[3072,384]{1,0:T(8,128)(2,1)} %get-tuple-element.327), channel_id=1, source_target_pairs={{0,16},{16,0},{1,17},{17,1},{2,18},{18,2},{3,19},{19,3},{4,20},{20... | collective-permute-start | bytes 7077896 | tf_op jit(solution)/shard_map/ppermute | solution.py:454
  860.1 66.6 %collective-permute-start.25 = (bf16[3072,384]{1,0:T(8,128)(2,1)}, bf16[3072,384]{1,0:T(8,128)(2,1)}, u32[]{:S(2)}, u32[]{:S(2)}) collective-permute-start(bf16[3072,384]{1,0:T(8,128)(2,1)} %get-tuple-element.329), channel_id=1, source_target_pairs={{0,8},{8,0},{1,9},{9,1},{2,10},{10,2},{3,11},{11,3},{4,12},{12,4},... | collective-permute-start | bytes 7077896 | tf_op jit(solution)/shard_map/ppermute | solution.py:454
  873.6 1.4 collective-permute-start.29
  873.6 12.4 %collective-permute-start.26 = (bf16[384,512]{1,0:T(8,128)(2,1)}, bf16[384,512]{1,0:T(8,128)(2,1)S(1)}, u32[]{:S(2)}, u32[]{:S(2)}) collective-permute-start(bf16[384,512]{1,0:T(8,128)(2,1)} %pad_maximum_fusion.16), channel_id=1, source_target_pairs={{0,1},{1,2},{2,3},{3,0},{4,5},{5,6},{6,7},{7,4},{8,9},{9,10},{10,1... | collective-permute-start | bytes 1179656 | tf_op jit(solution)/shard_map/ppermute | solution.py:454
  873.6 37.0 %collective-permute-start.27 = (bf16[384,512]{1,0:T(8,128)(2,1)}, bf16[384,512]{1,0:T(8,128)(2,1)S(1)}, u32[]{:S(2)}, u32[]{:S(2)}) collective-permute-start(bf16[384,512]{1,0:T(8,128)(2,1)} %pad_maximum_fusion.17), channel_id=1, source_target_pairs={{0,2},{1,3},{2,0},{3,1},{4,6},{5,7},{6,4},{7,5},{8,10},{9,11},{10,... | collective-permute-start | bytes 1179656 | tf_op jit(solution)/shard_map/ppermute | solution.py:454
  875.1 35.6 %collective-permute-start.28 = (bf16[384,512]{1,0:T(8,128)(2,1)}, bf16[384,512]{1,0:T(8,128)(2,1)S(1)}, u32[]{:S(2)}, u32[]{:S(2)}) collective-permute-start(bf16[384,512]{1,0:T(8,128)(2,1)} %pad_maximum_fusion.18), channel_id=1, source_target_pairs={{0,3},{1,0},{2,1},{3,2},{4,7},{5,4},{6,5},{7,6},{8,11},{9,8},{10,9... | collective-permute-start | bytes 1179656 | tf_op jit(solution)/shard_map/ppermute | solution.py:454
  886.1 43.7 %copy-start.93 = (bf16[384,512]{1,0:T(8,128)(2,1)}, bf16[384,512]{1,0:T(8,128)(2,1)S(1)}, u32[]{:S(2)}) copy-start(bf16[384,512]{1,0:T(8,128)(2,1)S(1)} %collective-permute-done.26) | copy-start | bytes 1179652
  932.6 31.2 %collective-permute-start.30 = (bf16[1536,384]{1,0:T(8,128)(2,1)S(1)}, bf16[1536,384]{1,0:T(8,128)(2,1)S(1)}, u32[]{:S(2)}, u32[]{:S(2)}) collective-permute-start(bf16[1536,384]{1,0:T(8,128)(2,1)S(1)} %get-tuple-element.343), channel_id=1, source_target_pairs={{0,8},{8,0},{1,9},{9,1},{2,10},{10,2},{3,11},{11,3},{4,12},{12,4},... | collective-permute-start | bytes 3538952 | tf_op jit(solution)/shard_map/ppermute | solution.py:454
  936.9 28.9 %collective-permute-start.31 = (bf16[1536,384]{1,0:T(8,128)(2,1)S(1)}, bf16[1536,384]{1,0:T(8,128)(2,1)S(1)}, u32[]{:S(2)}, u32[]{:S(2)}) collective-permute-start(bf16[1536,384]{1,0:T(8,128)(2,1)S(1)} %get-tuple-element.345), channel_id=1, source_target_pairs={{0,16},{16,0},{1,17},{17,1},{2,18},{18,2},{3,19},{19,3},{4,20},{20... | collective-permute-start | bytes 3538952 | tf_op jit(solution)/shard_map/ppermute | solution.py:454
  938.8 62.9 %collective-permute-start.35 = (bf16[3072,384]{1,0:T(8,128)(2,1)}, bf16[3072,384]{1,0:T(8,128)(2,1)}, u32[]{:S(2)}, u32[]{:S(2)}) collective-permute-start(bf16[3072,384]{1,0:T(8,128)(2,1)} %get-tuple-element.368), channel_id=1, source_target_pairs={{0,16},{16,0},{1,17},{17,1},{2,18},{18,2},{3,19},{19,3},{4,20},{20... | collective-permute-start | bytes 7077896 | tf_op jit(solution)/shard_map/ppermute | solution.py:454
  938.9 62.8 %collective-permute-start.36 = (bf16[3072,384]{1,0:T(8,128)(2,1)}, bf16[3072,384]{1,0:T(8,128)(2,1)}, u32[]{:S(2)}, u32[]{:S(2)}) collective-permute-start(bf16[3072,384]{1,0:T(8,128)(2,1)} %get-tuple-element.370), channel_id=1, source_target_pairs={{0,8},{8,0},{1,9},{9,1},{2,10},{10,2},{3,11},{11,3},{4,12},{12,4},... | collective-permute-start | bytes 7077896 | tf_op jit(solution)/shard_map/ppermute | solution.py:454
  970.2 31.5 %copy-start.15 = (bf16[3072,384]{1,0:T(8,128)(2,1)S(1)}, bf16[3072,384]{1,0:T(8,128)(2,1)}, u32[]{:S(2)}) copy-start(bf16[3072,384]{1,0:T(8,128)(2,1)} %copy-done.14) | copy-start | bytes 7077892
  970.2 10.9 collective-permute-start.32
  970.2 28.3 %collective-permute-start.33 = (bf16[384,768]{1,0:T(8,128)(2,1)}, bf16[384,768]{1,0:T(8,128)(2,1)}, u32[]{:S(2)}, u32[]{:S(2)}) collective-permute-start(bf16[384,768]{1,0:T(8,128)(2,1)} %pad_maximum_fusion.9), channel_id=1, source_target_pairs={{0,2},{1,3},{2,0},{3,1},{4,6},{5,7},{6,4},{7,5},{8,10},{9,11},{10,... | collective-permute-start | bytes 1769480 | tf_op jit(solution)/shard_map/ppermute | solution.py:454
  970.2 28.3 %collective-permute-start.34 = (bf16[384,768]{1,0:T(8,128)(2,1)}, bf16[384,768]{1,0:T(8,128)(2,1)}, u32[]{:S(2)}, u32[]{:S(2)}) collective-permute-start(bf16[384,768]{1,0:T(8,128)(2,1)} %pad_maximum_fusion.10), channel_id=1, source_target_pairs={{0,3},{1,0},{2,1},{3,2},{4,7},{5,4},{6,5},{7,6},{8,11},{9,8},{10,9... | collective-permute-start | bytes 1769480 | tf_op jit(solution)/shard_map/ppermute | solution.py:454
  1010.6 18.7 %collective-permute-start.37 = (bf16[1536,384]{1,0:T(8,128)(2,1)}, bf16[1536,384]{1,0:T(8,128)(2,1)}, u32[]{:S(2)}, u32[]{:S(2)}) collective-permute-start(bf16[1536,384]{1,0:T(8,128)(2,1)} %get-tuple-element.380), channel_id=1, source_target_pairs={{0,8},{8,0},{1,9},{9,1},{2,10},{10,2},{3,11},{11,3},{4,12},{12,4},... | collective-permute-start | bytes 3538952 | tf_op jit(solution)/shard_map/ppermute | solution.py:454
  1013.2 17.0 %collective-permute-start.38 = (bf16[1536,384]{1,0:T(8,128)(2,1)}, bf16[1536,384]{1,0:T(8,128)(2,1)}, u32[]{:S(2)}, u32[]{:S(2)}) collective-permute-start(bf16[1536,384]{1,0:T(8,128)(2,1)} %get-tuple-element.382), channel_id=1, source_target_pairs={{0,16},{16,0},{1,17},{17,1},{2,18},{18,2},{3,19},{19,3},{4,20},{20... | collective-permute-start | bytes 3538952 | tf_op jit(solution)/shard_map/ppermute | solution.py:454
  1014.7 4.4 collective-permute-start.39
  1019.9 5.6 collective-permute-start.40
  1037.3 4.6 collective-permute-start.44
  1038.1 16.0 %collective-permute-start.41 = (bf16[384,768]{1,0:T(8,128)(2,1)}, bf16[384,768]{1,0:T(8,128)(2,1)}, u32[]{:S(2)}, u32[]{:S(2)}) collective-permute-start(bf16[384,768]{1,0:T(8,128)(2,1)} %pad_maximum_fusion.12), channel_id=1, source_target_pairs={{0,1},{1,2},{2,3},{3,0},{4,5},{5,6},{6,7},{7,4},{8,9},{9,10},{10,1... | collective-permute-start | bytes 1769480 | tf_op jit(solution)/shard_map/ppermute | solution.py:454
  1038.1 46.1 %collective-permute-start.42 = (bf16[384,768]{1,0:T(8,128)(2,1)}, bf16[384,768]{1,0:T(8,128)(2,1)}, u32[]{:S(2)}, u32[]{:S(2)}) collective-permute-start(bf16[384,768]{1,0:T(8,128)(2,1)} %pad_maximum_fusion.13), channel_id=1, source_target_pairs={{0,2},{1,3},{2,0},{3,1},{4,6},{5,7},{6,4},{7,5},{8,10},{9,11},{10,... | collective-permute-start | bytes 1769480 | tf_op jit(solution)/shard_map/ppermute | solution.py:454
  1040.1 44.1 %collective-permute-start.43 = (bf16[384,768]{1,0:T(8,128)(2,1)}, bf16[384,768]{1,0:T(8,128)(2,1)}, u32[]{:S(2)}, u32[]{:S(2)}) collective-permute-start(bf16[384,768]{1,0:T(8,128)(2,1)} %pad_maximum_fusion.14), channel_id=1, source_target_pairs={{0,3},{1,0},{2,1},{3,2},{4,7},{5,4},{6,5},{7,6},{8,11},{9,8},{10,9... | collective-permute-start | bytes 1769480 | tf_op jit(solution)/shard_map/ppermute | solution.py:454
  1042.5 4.4 collective-permute-start.45
  (113 other events, 818.3 us)
Sparse Core Ops, SparseCore 0:
  11.4 213.9 all-gather.2
  228.2 234.1 all-gather.4
  707.9 227.0 reduce-scatter.1

commit v13 on v12

--- a/solution.py
+++ b/solution.py
@@ -899,71 +899,68 @@
     )(place_of(tile), own, other, sides[0], sides[0], sides[1], sides[1])
 
 
-def attention_fill_body(chunks, owners, place_ref, *refs):
+def attention_fill_body(chunks, owners, tiles, place_ref, *refs):
     own_ref, other_ref, side_ref, other_side_ref = refs[:4]
     outs = refs[4 + (len(refs) - 6) // 2 : -2]
     stage_ref, sems = refs[-2:]
     step = pl.program_id(0)
-    slot = step % 2
     start, wait = place_copies(chunks, stage_ref, sems, split_places(outs, chunks), INNER)
 
-    def put():
-        product = jnp.dot(
-            own_ref[...].T, side_ref[:, : CUTS[-1]], preferred_element_type=jnp.float32
-        ) + jnp.dot(
-            other_ref[...].T, other_side_ref[:, : CUTS[-1]], preferred_element_type=jnp.float32
-        )
-        stage_ref[slot, :, : CUTS[-1]] = product.astype(jnp.bfloat16)
-        stage_ref[slot, :, CUTS[-1] :] = jnp.zeros((INNER, PADDED - CUTS[-1]), jnp.bfloat16)
-        start(spots_of(0, place_ref), 0, step, step, slot)
-
-    @pl.when(place_ref[2] < owners)
-    def _():
-        @pl.when(step >= 2)
-        def _():
-            wait(slot)
-
-        put()
-
-        @pl.when(step == pl.num_programs(0) - 1)
-        def _():
-            wait(0)
-            wait(1)
-
-
-def attention_fill(chunks, arrays, own, other, sides):
+    def mine(tile):
+        return place_ref[2] == (0 if owners == 1 else tile // 2)
+
+    for at, tile in enumerate(tiles):
+
+        @pl.when((step == at) & mine(tile))
+        def _(at=at, row=tile % (4 // owners)):
+            product = jnp.dot(
+                own_ref[...].T, side_ref[:, : CUTS[-1]], preferred_element_type=jnp.float32
+            ) + jnp.dot(
+                other_ref[...].T, other_side_ref[:, : CUTS[-1]], preferred_element_type=jnp.float32
+            )
+            stage_ref[at, :, : CUTS[-1]] = product.astype(jnp.bfloat16)
+            stage_ref[at, :, CUTS[-1] :] = jnp.zeros((INNER, PADDED - CUTS[-1]), jnp.bfloat16)
+            start(spots_of(0, place_ref), 0, row, row, at)
+
+    for at, tile in enumerate(tiles):
+
+        @pl.when((step == len(tiles) - 1) & mine(tile))
+        def _(at=at):
+            wait(at)
+
+
+def attention_fill(chunks, arrays, own, other, sides, tiles):
     tokens = own.shape[0]
     unit_rows = unit_tiles(TILE) * TILE
     owners = 4 * INNER // unit_rows
-    steps = unit_rows // INNER
-
-    def column(i, place_ref):
-        return 0, jnp.minimum(place_ref[2], owners - 1) * steps + i
-
-    def half(i, place_ref):
-        return jnp.where(column(i, place_ref)[1] < 3, 0, 1), 0
+
+    def half(i, *_):
+        picked = 1 if tiles[0] == 3 else 0
+        for at, tile in enumerate(tiles[1:], 1):
+            picked = jnp.where(i >= at, 1 if tile == 3 else 0, picked)
+        return picked, 0
 
     anywhere = pl.BlockSpec(memory_space=pl.ANY)
     return pl.pallas_call(
-        functools.partial(attention_fill_body, chunks, owners),
+        functools.partial(attention_fill_body, chunks, owners, tiles),
         grid_spec=pltpu.PrefetchScalarGridSpec(
             num_scalar_prefetch=1,
-            grid=(steps,),
-            in_specs=[pl.BlockSpec((tokens, INNER), column)] * 2
+            grid=(len(tiles),),
+            in_specs=[pl.BlockSpec((tokens, INNER), lambda i, *_: (0, i))] * 2
             + [pl.BlockSpec((tokens, PADDED), half)] * 2
             + [anywhere] * len(arrays),
             out_specs=[anywhere] * len(arrays),
             scratch_shapes=[
-                pltpu.VMEM((2, INNER, PADDED), jnp.bfloat16),
-                pltpu.SemaphoreType.DMA((2, 5)),
+                pltpu.VMEM((len(tiles), INNER, PADDED), jnp.bfloat16),
+                pltpu.SemaphoreType.DMA((len(tiles), 5)),
             ],
         ),
         out_shape=[jax.ShapeDtypeStruct(array.shape, array.dtype) for array in arrays],
         input_output_aliases={5 + k: k for k in range(len(arrays))},
         compiler_params=pltpu.CompilerParams(vmem_limit_bytes=32 << 20),
         cost_estimate=pl.CostEstimate(
-            flops=4 * unit_rows * tokens * CUTS[-1],
-            bytes_accessed=4 * unit_rows * tokens + 2 * unit_rows * PADDED,
+            flops=4 * len(tiles) * INNER * tokens * CUTS[-1],
+            bytes_accessed=4 * len(tiles) * INNER * (tokens + PADDED),
             transcendentals=0,
         ),
         name="attention_fill",
@@ -1109,6 +1106,8 @@
     moving = start_back(grad_shared, tokens)
     chunks = 2 if before is None else 4
     arrays = weight_grads(chunks, own, other, sides)
+    early = jnp.concatenate([grad_query, attended], axis=1)
+    arrays = attention_fill(chunks, arrays, early, shift(early, "c", 1), late_sides, (0, 3))
     arrays, moving = lax.optimization_barrier((arrays, moving))
     if before is not None:
         arrays, moving = before.start((arrays, moving), (0, 1))
@@ -1117,8 +1116,8 @@
     grad_input_low = jnp.concatenate(
         [grad_query, grad_own[:, : 2 * INNER].astype(jnp.bfloat16)], axis=1
     )
-    late = jnp.concatenate([grad_input_low, attended], axis=1)
-    arrays = attention_fill(chunks, arrays, late, shift(late, "c", 1), late_sides)
+    late = grad_input_low[:, INNER:]
+    arrays = attention_fill(chunks, arrays, late, shift(late, "c", 1), late_sides, (1, 2))
     scatter = Scatter()
     along_y, along_x, rest = split_places(arrays, chunks)
     for chunk in range(chunks):

time: 1110 us -> 1150 us (1.036)
  waiting for transfers between devices: 596 us -> 628 us
  local copies, waits for them, and re-layouts: 64 us -> 79 us
    ppermute x29 -> x31, waiting for transfers between devices: 149 us -> 175 us  [shift(): lax.ppermute(value, axis, [(i, (i + amount) % count) for i in range(count)])]
    ppermute x29 -> x31, starting transfers between devices: 26.6 us -> 48.9 us  [shift(): lax.ppermute(value, axis, [(i, (i + amount) % count) for i in range(count)])]
    ppermute x4, starting transfers between devices: 21.6 us -> 5.24 us  [far_pair(): got = lax.ppermute(sent, 'z', pairs)]
    unnamed x271 -> x289, local copies, waits for them, and re-layouts: 44.4 us -> 53.4 us
  transfers between devices with their start and end apart: 49 -> 51, of which waited for: 26 -> 25; matrix products, arithmetic and copies ran while one was open for 11% -> 11% of each run, Pallas kernels for 15% -> 14%
where the time goes in v13:
time: 1150 us; the launch traced here: 1140 us
  waiting for transfers between devices  628 us (55%)
  Pallas kernels  228 us (20%)
  starting transfers between devices  79.3 us (7%)
  local copies, waits for them, and re-layouts  79 us (7%)
  other arithmetic  76.9 us (7%)
  matrix products  36.4 us (3%)
  between operations  15.9 us (1%)
    all_gather x2, waiting for transfers between devices, fetch_rows(): return lax.all_gather(local_rows, DEVICES, axis=0, tiled=True)  336 us
    ppermute x31, waiting for transfers between devices, shift(): lax.ppermute(value, axis, [(i, (i + amount) % count) for i in range(count)])  175 us
    ppermute x4, waiting for transfers between devices, far_pair(): got = lax.ppermute(sent, 'z', pairs)  94 us
    pallas_call x2, Pallas kernels, ffn_forward(): pl.pallas_call(ffn_forward_body, grid_spec=pltpu.PrefetchScalarGridSpec(n...  56.4 us
    unnamed x289, local copies, waits for them, and re-layouts  53.4 us
    pallas_call x2, Pallas kernels, ffn_backward(): pl.pallas_call(ffn_backward_body, grid_spec=pltpu.PrefetchScalarGridSpec(...  53.1 us
    ppermute x31, starting transfers between devices, shift(): lax.ppermute(value, axis, [(i, (i + amount) % count) for i in range(count)])  48.9 us
    pallas_call x2, Pallas kernels, weight_grads(): pl.pallas_call(functools.partial(weight_grads_body, chunks, tile), grid_s...  48.8 us
  transfers between devices with their start and end apart: 51, of which 25 were waited for; matrix products, arithmetic and copies ran while one was open for 11% of the time, Pallas kernels for 14%

profile of v13, /device:TPU:24, one launch (start us, length us, event | category | flops | bytes accessed | tf_op | source)
XLA Modules:
  0.0 1144.2 jit_solution(14058042415796629034)
XLA Ops:
  7.2 2.5 copy.134
  12.0 2.4 copy.133
  18.0 207.4 %all-gather.3.cloned.1.call-done.refs_2_.refs_3_.refs_4_.refs_5_ = bf16[12288,1472]{1,0:T(8,128)(2,1)} async-done(((bf16[384,1472]{1,0:T(8,128)(2,1)}), bf16[12288,1472]{1,0:T(8,128)(2,1)}) %all-gather.3.cloned.1.call-update) | async-done | bytes 36175888 | tf_op jit(solution)/shard_map/all_gather | solution.py:1033
  225.4 4.7 fusion.33
  233.3 6.0 collective-permute-start.2
  240.2 4.7 bias_tiles.1.refs_4_.refs_6_
  244.9 3.6 copy.139
  248.5 23.5 %collective-permute-done = bf16[288,768]{1,0:T(8,128)(2,1)S(1)} collective-permute-done((bf16[288,768]{1,0:T(8,128)(2,1)S(1)}, bf16[288,768]{1,0:T(8,128)(2,1)S(1)}, u32[]{:S(2)}, u32[]{:S(2)}) %collective-permute-start) | collective-permute-done | bytes 442400 | tf_op jit(solution)/shard_map/ppermute | solution.py:468
  272.1 15.6 %collective-permute-done.1 = bf16[512,768]{1,0:T(8,128)(2,1)} collective-permute-done((bf16[512,768]{1,0:T(8,128)(2,1)}, bf16[512,768]{1,0:T(8,128)(2,1)}, u32[]{:S(2)}, u32[]{:S(2)}) %collective-permute-start.1) | collective-permute-done | bytes 786464 | tf_op jit(solution)/shard_map/ppermute | solution.py:460
  290.6 5.8 attend_forward.2
  296.5 2.8 multiply_reduce_fusion.10
  300.9 28.2 %ffn_forward.2 = (f32[512,1472]{1,0:T(8,128)}, f32[512,3584]{1,0:T(8,128)}, f32[512,3584]{1,0:T(8,128)}, bf16[6144,512]{1,0:T(8,128)(2,1)}, bf16[6144,512]{1,0:T(8,128)(2,1)}) custom-call(s32[2]{0:T(128)S(1)} %pad_add_fusion.core_ref, bf16[512,1472]{1,0:T(8,128)(2,1)S(1)} %multiply_convert_fusion.2.refs_0_, f32[512,1472]{1,0:T(8,128)} %copy-done.58, ...), custom_call_target="tpu_custom_call" | custom-call | flops 16206790656 | bytes 50003968 | tf_op jit(solution)/shard_map/ffn_forward/pallas_call | solution.py:654
  329.1 2.6 multiply_reduce_fusion.9
  334.1 128.3 %all-gather.5.cloned.1.call-done.refs_2_.refs_3_.refs_4_.refs_5_ = bf16[12288,1472]{1,0:T(8,128)(2,1)} async-done(((bf16[384,1472]{1,0:T(8,128)(2,1)}), bf16[12288,1472]{1,0:T(8,128)(2,1)}) %all-gather.5.cloned.1.call-update) | async-done | bytes 36175888 | tf_op jit(solution)/shard_map/all_gather | solution.py:1033
  462.4 4.2 fusion.36
  469.0 5.0 collective-permute-start.5
  475.3 39.9 %collective-permute-done.3 = bf16[288,896]{1,0:T(8,128)(2,1)S(1)} collective-permute-done((bf16[288,896]{1,0:T(8,128)(2,1)S(1)}, bf16[288,896]{1,0:T(8,128)(2,1)S(1)}, u32[]{:S(2)}, u32[]{:S(2)}) %collective-permute-start.3) | collective-permute-done | bytes 516128 | tf_op jit(solution)/shard_map/ppermute | solution.py:468
  516.7 5.8 attend_forward.3
  522.5 2.8 multiply_reduce_fusion.7
  526.9 28.2 %ffn_forward.3 = (f32[512,1472]{1,0:T(8,128)}, f32[512,3584]{1,0:T(8,128)}, f32[512,3584]{1,0:T(8,128)}, bf16[6144,512]{1,0:T(8,128)(2,1)}, bf16[6144,512]{1,0:T(8,128)(2,1)}) custom-call(s32[2]{0:T(128)S(1)} %pad_add_fusion.core_ref, bf16[512,1472]{1,0:T(8,128)(2,1)S(1)} %multiply_convert_fusion.refs_0_, f32[512,1472]{1,0:T(8,128)} %copy-done.60, ...), custom_call_target="tpu_custom_call" | custom-call | flops 16206790656 | bytes 50003968 | tf_op jit(solution)/shard_map/ffn_forward/pallas_call | solution.py:654
  555.1 26.1 %ffn_backward.2 = (f32[512,1472]{1,0:T(8,128)}, bf16[6144,512]{1,0:T(8,128)(2,1)}, bf16[6144,512]{1,0:T(8,128)(2,1)}) custom-call(s32[2]{0:T(128)S(1)} %pad_add_fusion.core_ref, bf16[512,1472]{1,0:T(8,128)(2,1)S(1)} %bitcast_convert_fusion.refs_0_, f32[512,3584]{1,0:T(8,128)} %get-tuple-element.223.refs_1_, ...), custom_call_target="tpu_custom_call", output_to_operand_aliasing={{1}: (7, {}), {2}: (8, {})} | custom-call | flops 16206790656 | bytes 53673984 | tf_op jit(solution)/shard_map/ffn_backward/pallas_call | solution.py:719
  581.2 4.2 collective-permute-start.8
  593.6 2.5 fusion.51
  597.7 2.9 convolution_convert_fusion.1.refs_1_
  600.6 16.8 %attend_backward.2 = (bf16[512,384]{1,0:T(8,128)(2,1)S(1)}, bf16[2304,896]{1,0:T(8,128)(2,1)}, f32[3,32,256]{2,1,0:T(8,128)S(1)}) custom-call(s32[4]{0:T(128)S(1)} %copy-done.43, s32[4]{0:T(128)S(1)} %get-tuple-element.570.high_ref, bf16[512,384]{1,0:T(8,128)(2,1)S(1)} %copy-done.31, bf16[512,384]{1,0:T(8,128)(2,1)S(1)} %convolution_convert_fusion.1.refs_1_, ...), custom_call_target="tpu_custom_call" | custom-call | flops 4529848320 | bytes 12582912 | tf_op jit(solution)/shard_map/attend_backward/pallas_call | solution.py:361
  617.6 8.7 collective-permute-start.6
  626.3 3.3 fusion.52
  629.7 5.2 collective-permute-start.10
  639.5 23.8 %weight_grads.2 = (bf16[3072,256]{1,0:T(8,128)(2,1)S(1)}, bf16[3072,256]{1,0:T(8,128)(2,1)S(1)}, bf16[3072,256]{1,0:T(8,128)(2,1)S(1)}, bf16[3072,256]{1,0:T(8,128)(2,1)S(1)}, bf16[6144,1024]{1,0:T(8,128)(2,1)}) custom-call(s32[6]{0:T(128)S(1)} %copy-done.45, bf16[6144,512]{1,0:T(8,128)(2,1)} %get-tuple-element.233.refs_0_, ...), custom_call_target="tpu_custom_call" | custom-call | flops 18522046464 | bytes 31457280 | tf_op jit(solution)/shard_map/weight_grads/pallas_call | solution.py:879
  670.1 4.7 attention_fill.4
  674.8 7.4 collective-permute-done.12
  686.7 4.7 attention_fill.5
  697.5 4.0 collective-permute-start.14
  704.0 7.5 multiply_reduce_fusion.2
  711.6 2.7 fusion.49
  714.3 27.0 %ffn_backward.3 = (f32[512,1472]{1,0:T(8,128)}, bf16[6144,512]{1,0:T(8,128)(2,1)}, bf16[6144,512]{1,0:T(8,128)(2,1)}) custom-call(s32[2]{0:T(128)S(1)} %pad_add_fusion.core_ref, bf16[512,1472]{1,0:T(8,128)(2,1)S(1)} %get-tuple-element.498.refs_0_, f32[512,3584]{1,0:T(8,128)} %get-tuple-element.268.refs_1_, ...), custom_call_target="tpu_custom_call", output_to_operand_aliasing={{1}: (7, {}), {2}: (8, {})} | custom-call | flops 16206790656 | bytes 53673984 | tf_op jit(solution)/shard_map/ffn_backward/pallas_call | solution.py:719
  741.3 2.5 collective-permute-done.14
  750.4 3.7 fusion.14.refs_2_.refs_3_
  759.7 2.5 fusion.48
  762.6 3.5 convolution_convert_fusion.refs_1_
  766.2 16.1 %attend_backward.3 = (bf16[512,384]{1,0:T(8,128)(2,1)S(1)}, bf16[2304,768]{1,0:T(8,128)(2,1)}, f32[3,32,256]{2,1,0:T(8,128)S(1)}) custom-call(s32[4]{0:T(128)S(1)} %copy-done.44, s32[4]{0:T(128)S(1)} %get-tuple-element.570.high_ref, bf16[512,384]{1,0:T(8,128)(2,1)S(1)} %copy-done.35, bf16[512,384]{1,0:T(8,128)(2,1)S(1)} %convolution_convert_fusion.refs_1_, ...), custom_call_target="tpu_custom_call" | custom-call | flops 4529848320 | bytes 12582912 | tf_op jit(solution)/shard_map/attend_backward/pallas_call | solution.py:361
  788.4 8.0 collective-permute-start.18
  802.0 2.3 collective-permute-start.24
  804.3 25.0 %weight_grads.3 = (bf16[3072,384]{1,0:T(8,128)(2,1)}, bf16[3072,384]{1,0:T(8,128)(2,1)}, bf16[3072,384]{1,0:T(8,128)(2,1)S(1)}, bf16[3072,384]{1,0:T(8,128)(2,1)...) custom-call(s32[6]{0:T(128)S(1)} %copy-done.46, ...), custom_call_target="tpu_custom_call" | custom-call | flops 18522046464 | bytes 31457280 | tf_op jit(solution)/shard_map/weight_grads/pallas_call | solution.py:879
  834.7 5.8 attention_fill.6
  840.5 23.1 %collective-permute-done.24 = bf16[288,768]{1,0:T(8,128)(2,1)S(1)} collective-permute-done((bf16[288,768]{1,0:T(8,128)(2,1)}, bf16[288,768]{1,0:T(8,128)(2,1)S(1)}, u32[]{:S(2)}, u32[]{:S(2)}) %collective-permute-start.24) | collective-permute-done | bytes 442400 | tf_op jit(solution)/shard_map/ppermute | solution.py:468
  867.6 5.8 attention_fill.7
  884.1 8.0 fusion.24
  897.8 13.2 %collective-permute-done.28 = bf16[384,512]{1,0:T(8,128)(2,1)S(1)} collective-permute-done((bf16[384,512]{1,0:T(8,128)(2,1)S(1)}, bf16[384,512]{1,0:T(8,128)(2,1)S(1)}, u32[]{:S(2)}, u32[]{:S(2)}) %collective-permute-start.28) | collective-permute-done | bytes 393248 | tf_op jit(solution)/shard_map/ppermute | solution.py:454
  911.0 32.7 %collective-permute-done.29 = bf16[384,512]{1,0:T(8,128)(2,1)S(1)} collective-permute-done((bf16[384,512]{1,0:T(8,128)(2,1)S(1)}, bf16[384,512]{1,0:T(8,128)(2,1)S(1)}, u32[]{:S(2)}, u32[]{:S(2)}) %collective-permute-start.29) | collective-permute-done | bytes 393248 | tf_op jit(solution)/shard_map/ppermute | solution.py:454
  944.5 3.0 add_convert_fusion.2
  947.8 2.3 add_convert_fusion.3
  954.5 24.8 %collective-permute-done.32 = bf16[1536,384]{1,0:T(8,128)(2,1)S(1)} collective-permute-done((bf16[1536,384]{1,0:T(8,128)(2,1)S(1)}, bf16[1536,384]{1,0:T(8,128)(2,1)S(1)}, u32[]{:S(2)}, u32[]{:S(2)}) %collective-permute-start.32) | collective-permute-done | bytes 1179680 | tf_op jit(solution)/shard_map/ppermute | solution.py:454
  984.4 4.7 collective-permute-start.35
  991.1 3.5 copy.148
  994.6 4.8 collective-permute-done.34
  999.4 39.3 %collective-permute-done.35 = bf16[384,768]{1,0:T(8,128)(2,1)S(1)} collective-permute-done((bf16[384,768]{1,0:T(8,128)(2,1)}, bf16[384,768]{1,0:T(8,128)(2,1)S(1)}, u32[]{:S(2)}, u32[]{:S(2)}) %collective-permute-start.35) | collective-permute-done | bytes 589856 | tf_op jit(solution)/shard_map/ppermute | solution.py:454
  1038.8 2.5 add_convert_fusion
  1043.8 2.4 add_convert_fusion.1
  1050.6 2.3 copy.149
  1056.5 4.1 collective-permute-done.42
  1060.6 12.9 %collective-permute-done.39 = bf16[1536,384]{1,0:T(8,128)(2,1)} collective-permute-done((bf16[1536,384]{1,0:T(8,128)(2,1)}, bf16[1536,384]{1,0:T(8,128)(2,1)}, u32[]{:S(2)}, u32[]{:S(2)}) %collective-permute-start.39) | collective-permute-done | bytes 1179680 | tf_op jit(solution)/shard_map/ppermute | solution.py:454
  1091.7 4.6 collective-permute-done.43
  1096.4 35.0 %collective-permute-done.44 = bf16[384,768]{1,0:T(8,128)(2,1)} collective-permute-done((bf16[384,768]{1,0:T(8,128)(2,1)}, bf16[384,768]{1,0:T(8,128)(2,1)}, u32[]{:S(2)}, u32[]{:S(2)}) %collective-permute-start.44) | collective-permute-done | bytes 589856 | tf_op jit(solution)/shard_map/ppermute | solution.py:454
  (486 shorter events, 154.6 us)
Async XLA Ops:
  7.2 218.2 %all-gather.3.cloned.1.call-start = ((), (), s32[]{:S(2)}) async-start(), calls=%async_computation.1 | async-start | bytes 38928384 | tf_op jit(solution)/shard_map/all_gather | solution.py:1033
  9.7 452.7 %all-gather.5.cloned.1.call-start = ((), (), s32[]{:S(2)}) async-start(), calls=%async_computation.2 | async-start | bytes 38928384 | tf_op jit(solution)/shard_map/all_gather | solution.py:1033
  11.9 1026.9 %reduce-scatter.2.cloned.1.call-start = ((), (), s32[]{:S(2)}) async-start(), calls=%async_computation.3 | async-start | bytes 13369344 | tf_op jit(solution)/shard_map/reduce_scatter | solution.py:1132
  15.7 284.2 %copy-start.103 = (f32[1472]{0:T(1024)}, f32[1472]{0:T(1024)S(1)}, u32[]{:S(2)}) copy-start(f32[1472]{0:T(1024)S(1)} %get-tuple-element.489) | copy-start | bytes 17668
  16.6 213.6 %copy-start.123 = (f32[512]{0:T(512)}, f32[512]{0:T(512)S(1)}, u32[]{:S(2)}) copy-start(f32[512]{0:T(512)S(1)} %get-tuple-element.557) | copy-start | bytes 6148
  18.0 221.4 %copy-start.133 = (f32[32,6]{0,1:T(8,128)S(1)}, f32[32,6]{0,1:T(8,128)}, u32[]{:S(2)}) copy-start(f32[32,6]{0,1:T(8,128)} %param.13) | copy-start | bytes 2308
  231.1 40.9 %collective-permute-start = (bf16[288,768]{1,0:T(8,128)(2,1)S(1)}, bf16[288,768]{1,0:T(8,128)(2,1)S(1)}, u32[]{:S(2)}, u32[]{:S(2)}) collective-permute-start(bf16[288,768]{1,0:T(8,128)(2,1)S(1)} %slice_select_fusion.1), channel_id=1, source_target_pairs={{0,2},{1,3},{2,0},{3,1},{4,6},{5,7},{6,4},{7,5},{8,10},{9,11},{10,... | collective-permute-start | bytes 1327112 | tf_op jit(solution)/shard_map/ppermute | solution.py:468
  231.8 55.9 %collective-permute-start.1 = (bf16[512,768]{1,0:T(8,128)(2,1)}, bf16[512,768]{1,0:T(8,128)(2,1)}, u32[]{:S(2)}, u32[]{:S(2)}) collective-permute-start(bf16[512,768]{1,0:T(8,128)(2,1)} %slice.177), channel_id=1, source_target_pairs={{0,1},{1,2},{2,3},{4,5},{5,6},{6,7},{8,9},{9,10},{10,11},{12,13},{... | collective-permute-start | bytes 2359304 | tf_op jit(solution)/shard_map/ppermute | solution.py:460
  233.3 282.6 %copy-start.42 = (s32[4]{0:T(128)}, s32[4]{0:T(128)S(1)}, u32[]{:S(2)}) copy-start(s32[4]{0:T(128)S(1)} %get-tuple-element.571.low_ref) | copy-start | bytes 52
  233.3 55.6 %collective-permute-start.2 = (bf16[512,768]{1,0:T(8,128)(2,1)}, bf16[512,768]{1,0:T(8,128)(2,1)}, u32[]{:S(2)}, u32[]{:S(2)}) collective-permute-start(bf16[512,768]{1,0:T(8,128)(2,1)} %slice.177), channel_id=1, source_target_pairs={{1,0},{2,1},{3,2},{5,4},{6,5},{7,6},{9,8},{10,9},{11,10},{13,12},{... | collective-permute-start | bytes 2359304 | tf_op jit(solution)/shard_map/ppermute | solution.py:460
  248.5 42.1 %copy-start.34 = (bf16[512,384]{1,0:T(8,128)(2,1)}, bf16[512,384]{1,0:T(8,128)(2,1)S(1)}, u32[]{:S(2)}) copy-start(bf16[512,384]{1,0:T(8,128)(2,1)S(1)} %slice.174.refs_0_) | copy-start | bytes 1179652
  299.9 29.2 %copy-start.115 = (f32[512]{0:T(512)}, f32[512]{0:T(512)S(1)}, u32[]{:S(2)}) copy-start(f32[512]{0:T(512)S(1)} %get-tuple-element.559) | copy-start | bytes 6148
  300.9 32.0 %copy-start.111 = (f32[1472]{0:T(1024)S(1)}, f32[1472]{0:T(1024)}, u32[]{:S(2)}) copy-start(f32[1472]{0:T(1024)} %param.12) | copy-start | bytes 17668
  334.1 132.6 %copy-start.75 = (bf16[512,1472]{1,0:T(8,128)(2,1)}, bf16[512,1472]{1,0:T(8,128)(2,1)S(1)}, u32[]{:S(2)}) copy-start(bf16[512,1472]{1,0:T(8,128)(2,1)S(1)} %get-tuple-element.511) | copy-start | bytes 4521988
  467.7 47.7 %collective-permute-start.4 = (bf16[512,896]{1,0:T(8,128)(2,1)S(1)}, bf16[512,896]{1,0:T(8,128)(2,1)S(1)}, u32[]{:S(2)}, u32[]{:S(2)}) collective-permute-start(bf16[512,896]{1,0:T(8,128)(2,1)S(1)} %pad_maximum_fusion.2), channel_id=1, source_target_pairs={{0,1},{1,2},{2,3},{4,5},{5,6},{6,7},{8,9},{9,10},{10,11},{12,13},{... | collective-permute-start | bytes 2752520 | tf_op jit(solution)/shard_map/ppermute | solution.py:460
  469.0 46.7 %collective-permute-start.5 = (bf16[512,896]{1,0:T(8,128)(2,1)S(1)}, bf16[512,896]{1,0:T(8,128)(2,1)S(1)}, u32[]{:S(2)}, u32[]{:S(2)}) collective-permute-start(bf16[512,896]{1,0:T(8,128)(2,1)S(1)} %pad_maximum_fusion.2), channel_id=1, source_target_pairs={{1,0},{2,1},{3,2},{5,4},{6,5},{7,6},{9,8},{10,9},{11,10},{13,12},{... | collective-permute-start | bytes 2752520 | tf_op jit(solution)/shard_map/ppermute | solution.py:460
  474.1 41.2 %collective-permute-start.3 = (bf16[288,896]{1,0:T(8,128)(2,1)S(1)}, bf16[288,896]{1,0:T(8,128)(2,1)S(1)}, u32[]{:S(2)}, u32[]{:S(2)}) collective-permute-start(bf16[288,896]{1,0:T(8,128)(2,1)S(1)} %fusion.44), channel_id=1, source_target_pairs={{0,2},{1,3},{2,0},{3,1},{4,6},{5,7},{6,4},{7,5},{8,10},{9,11},{10,... | collective-permute-start | bytes 1548296 | tf_op jit(solution)/shard_map/ppermute | solution.py:468
  475.3 40.6 %copy-start.30 = (bf16[512,384]{1,0:T(8,128)(2,1)}, bf16[512,384]{1,0:T(8,128)(2,1)S(1)}, u32[]{:S(2)}) copy-start(bf16[512,384]{1,0:T(8,128)(2,1)S(1)} %slice.180.refs_0_) | copy-start | bytes 1179652
  581.2 57.1 %collective-permute-start.8 = (bf16[6144,512]{1,0:T(8,128)(2,1)}, bf16[6144,512]{1,0:T(8,128)(2,1)}, u32[]{:S(2)}, u32[]{:S(2)}) collective-permute-start(bf16[6144,512]{1,0:T(8,128)(2,1)} %get-tuple-element.234), channel_id=1, source_target_pairs={{0,4},{4,0},{1,5},{5,1},{2,6},{6,2},{3,7},{7,3},{8,12},{12,8},{9,1... | collective-permute-start | bytes 18874376 | tf_op jit(solution)/shard_map/ppermute | solution.py:454
  589.8 47.1 %collective-permute-start.9 = (bf16[1024,1536]{1,0:T(8,128)(2,1)S(1)}, bf16[1024,1536]{1,0:T(8,128)(2,1)}, u32[]{:S(2)}, u32[]{:S(2)}) collective-permute-start(bf16[1024,1536]{1,0:T(8,128)(2,1)S(1)} %fusion.12.refs_2_.refs_3_), channel_id=1, source_target_pairs={{0,4},{4,0},{1,5},{5,1},{2,6},{6,2},{3,7},{7,3},{8,12},{12,8},{9,1... | collective-permute-start | bytes 9437192 | tf_op jit(solution)/shard_map/ppermute | solution.py:454
  597.6 66.7 %collective-permute-start.7 = (bf16[1024,1536]{1,0:T(8,128)(2,1)S(1)}, bf16[1024,1536]{1,0:T(8,128)(2,1)S(1)}, u32[]{:S(2)}, u32[]{:S(2)}) collective-permute-start(bf16[1024,1536]{1,0:T(8,128)(2,1)S(1)} %fusion.11.refs_2_), channel_id=1, source_target_pairs={{0,4},{4,0},{1,5},{5,1},{2,6},{6,2},{3,7},{7,3},{8,12},{12,8},{9,1... | collective-permute-start | bytes 9437192 | tf_op jit(solution)/shard_map/ppermute | solution.py:454
  617.6 45.8 %collective-permute-start.6 = (bf16[512,768]{1,0:T(8,128)(2,1)S(1)}, bf16[512,768]{1,0:T(8,128)(2,1)S(1)}, u32[]{:S(2)}, u32[]{:S(2)}) collective-permute-start(bf16[512,768]{1,0:T(8,128)(2,1)S(1)} %constant_dynamic-update-slice_fusion.6.refs_0_), channel_id=1, source_target_pairs={{0,4},{4,0},{1,5},{5,1},{2,6},{6,2},{3,7},{7,3},{8,12},{12,8},{9,1... | collective-permute-start | bytes 2359304 | tf_op jit(solution)/shard_map/ppermute | solution.py:454
  629.7 52.5 %collective-permute-start.10 = (bf16[512,896]{1,0:T(8,128)(2,1)}, bf16[512,896]{1,0:T(8,128)(2,1)}, u32[]{:S(2)}, u32[]{:S(2)}) collective-permute-start(bf16[512,896]{1,0:T(8,128)(2,1)} %get-tuple-element.505), channel_id=1, source_target_pairs={{1,0},{2,1},{3,2},{5,4},{6,5},{7,6},{9,8},{10,9},{11,10},{13,12},{... | collective-permute-start | bytes 2752520 | tf_op jit(solution)/shard_map/ppermute | solution.py:460
  637.0 45.3 %collective-permute-start.11 = (bf16[512,896]{1,0:T(8,128)(2,1)}, bf16[512,896]{1,0:T(8,128)(2,1)}, u32[]{:S(2)}, u32[]{:S(2)}) collective-permute-start(bf16[512,896]{1,0:T(8,128)(2,1)} %get-tuple-element.504), channel_id=1, source_target_pairs={{0,1},{1,2},{2,3},{4,5},{5,6},{6,7},{8,9},{9,10},{10,11},{12,13},{... | collective-permute-start | bytes 2752520 | tf_op jit(solution)/shard_map/ppermute | solution.py:460
  638.3 44.0 %collective-permute-start.12 = (bf16[288,896]{1,0:T(8,128)(2,1)}, bf16[288,896]{1,0:T(8,128)(2,1)S(1)}, u32[]{:S(2)}, u32[]{:S(2)}) collective-permute-start(bf16[288,896]{1,0:T(8,128)(2,1)} %slice_select_fusion), channel_id=1, source_target_pairs={{0,2},{1,3},{2,0},{3,1},{4,6},{5,7},{6,4},{7,5},{8,10},{9,11},{10,... | collective-permute-start | bytes 1548296 | tf_op jit(solution)/shard_map/ppermute | solution.py:468
  684.4 2.4 collective-permute-start.13
  697.5 46.3 %collective-permute-start.14 = (bf16[3072,256]{1,0:T(8,128)(2,1)}, bf16[3072,256]{1,0:T(8,128)(2,1)S(1)}, u32[]{:S(2)}, u32[]{:S(2)}) collective-permute-start(bf16[3072,256]{1,0:T(8,128)(2,1)} %copy-done.22), channel_id=1, source_target_pairs={{0,16},{16,0},{1,17},{17,1},{2,18},{18,2},{3,19},{19,3},{4,20},{20... | collective-permute-start | bytes 4718600 | tf_op jit(solution)/shard_map/ppermute | solution.py:454
  701.5 43.9 %collective-permute-start.15 = (bf16[3072,256]{1,0:T(8,128)(2,1)}, bf16[3072,256]{1,0:T(8,128)(2,1)}, u32[]{:S(2)}, u32[]{:S(2)}) collective-permute-start(bf16[3072,256]{1,0:T(8,128)(2,1)} %copy-done.23), channel_id=1, source_target_pairs={{0,8},{8,0},{1,9},{9,1},{2,10},{10,2},{3,11},{11,3},{4,12},{12,4},... | collective-permute-start | bytes 4718600 | tf_op jit(solution)/shard_map/ppermute | solution.py:454
  714.3 31.1 %copy-start.15 = (bf16[3072,256]{1,0:T(8,128)(2,1)S(1)}, bf16[3072,256]{1,0:T(8,128)(2,1)}, u32[]{:S(2)}) copy-start(bf16[3072,256]{1,0:T(8,128)(2,1)} %copy-done.14) | copy-start | bytes 4718596
  750.4 51.6 %collective-permute-start.20 = (bf16[6144,512]{1,0:T(8,128)(2,1)}, bf16[6144,512]{1,0:T(8,128)(2,1)}, u32[]{:S(2)}, u32[]{:S(2)}) collective-permute-start(bf16[6144,512]{1,0:T(8,128)(2,1)} %get-tuple-element.305), channel_id=1, source_target_pairs={{0,4},{4,0},{1,5},{5,1},{2,6},{6,2},{3,7},{7,3},{8,12},{12,8},{9,1... | collective-permute-start | bytes 18874376 | tf_op jit(solution)/shard_map/ppermute | solution.py:454
  754.1 46.6 %collective-permute-start.21 = (bf16[1024,1536]{1,0:T(8,128)(2,1)}, bf16[1024,1536]{1,0:T(8,128)(2,1)}, u32[]{:S(2)}, u32[]{:S(2)}) collective-permute-start(bf16[1024,1536]{1,0:T(8,128)(2,1)} %fusion.14.refs_2_.refs_3_), channel_id=1, source_target_pairs={{0,4},{4,0},{1,5},{5,1},{2,6},{6,2},{3,7},{7,3},{8,12},{12,8},{9,1... | collective-permute-start | bytes 9437192 | tf_op jit(solution)/shard_map/ppermute | solution.py:454
  754.5 27.8 %collective-permute-start.16 = (bf16[1536,256]{1,0:T(8,128)(2,1)}, bf16[1536,256]{1,0:T(8,128)(2,1)}, u32[]{:S(2)}, u32[]{:S(2)}) collective-permute-start(bf16[1536,256]{1,0:T(8,128)(2,1)} %get-tuple-element.284), channel_id=1, source_target_pairs={{0,8},{8,0},{1,9},{9,1},{2,10},{10,2},{3,11},{11,3},{4,12},{12,4},... | collective-permute-start | bytes 2359304 | tf_op jit(solution)/shard_map/ppermute | solution.py:454
  756.4 25.9 %collective-permute-start.17 = (bf16[1536,256]{1,0:T(8,128)(2,1)}, bf16[1536,256]{1,0:T(8,128)(2,1)S(1)}, u32[]{:S(2)}, u32[]{:S(2)}) collective-permute-start(bf16[1536,256]{1,0:T(8,128)(2,1)} %get-tuple-element.286), channel_id=1, source_target_pairs={{0,16},{16,0},{1,17},{17,1},{2,18},{18,2},{3,19},{19,3},{4,20},{20... | collective-permute-start | bytes 2359304 | tf_op jit(solution)/shard_map/ppermute | solution.py:454
  762.6 66.7 %collective-permute-start.19 = (bf16[1024,1536]{1,0:T(8,128)(2,1)S(1)}, bf16[1024,1536]{1,0:T(8,128)(2,1)S(1)}, u32[]{:S(2)}, u32[]{:S(2)}) collective-permute-start(bf16[1024,1536]{1,0:T(8,128)(2,1)S(1)} %fusion.13.refs_2_), channel_id=1, source_target_pairs={{0,4},{4,0},{1,5},{5,1},{2,6},{6,2},{3,7},{7,3},{8,12},{12,8},{9,1... | collective-permute-start | bytes 9437192 | tf_op jit(solution)/shard_map/ppermute | solution.py:454
  788.4 40.9 %collective-permute-start.18 = (bf16[512,768]{1,0:T(8,128)(2,1)S(1)}, bf16[512,768]{1,0:T(8,128)(2,1)S(1)}, u32[]{:S(2)}, u32[]{:S(2)}) collective-permute-start(bf16[512,768]{1,0:T(8,128)(2,1)S(1)} %constant_dynamic-update-slice_fusion.8.refs_0_), channel_id=1, source_target_pairs={{0,4},{4,0},{1,5},{5,1},{2,6},{6,2},{3,7},{7,3},{8,12},{12,8},{9,1... | collective-permute-start | bytes 2359304 | tf_op jit(solution)/shard_map/ppermute | solution.py:454
  797.7 65.9 %collective-permute-start.22 = (bf16[512,768]{1,0:T(8,128)(2,1)}, bf16[512,768]{1,0:T(8,128)(2,1)}, u32[]{:S(2)}, u32[]{:S(2)}) collective-permute-start(bf16[512,768]{1,0:T(8,128)(2,1)} %get-tuple-element.508), channel_id=1, source_target_pairs={{1,0},{2,1},{3,2},{5,4},{6,5},{7,6},{9,8},{10,9},{11,10},{13,12},{... | collective-permute-start | bytes 2359304 | tf_op jit(solution)/shard_map/ppermute | solution.py:460
  800.7 62.9 %collective-permute-start.23 = (bf16[512,768]{1,0:T(8,128)(2,1)}, bf16[512,768]{1,0:T(8,128)(2,1)S(1)}, u32[]{:S(2)}, u32[]{:S(2)}) collective-permute-start(bf16[512,768]{1,0:T(8,128)(2,1)} %get-tuple-element.507), channel_id=1, source_target_pairs={{0,1},{1,2},{2,3},{4,5},{5,6},{6,7},{8,9},{9,10},{10,11},{12,13},{... | collective-permute-start | bytes 2359304 | tf_op jit(solution)/shard_map/ppermute | solution.py:460
  802.0 61.6 %collective-permute-start.24 = (bf16[288,768]{1,0:T(8,128)(2,1)}, bf16[288,768]{1,0:T(8,128)(2,1)S(1)}, u32[]{:S(2)}, u32[]{:S(2)}) collective-permute-start(bf16[288,768]{1,0:T(8,128)(2,1)} %slice_select_fusion.2), channel_id=1, source_target_pairs={{0,2},{1,3},{2,0},{3,1},{4,6},{5,7},{6,4},{7,5},{8,10},{9,11},{10,... | collective-permute-start | bytes 1327112 | tf_op jit(solution)/shard_map/ppermute | solution.py:468
  865.2 2.4 collective-permute-start.25
  877.7 66.0 %collective-permute-start.26 = (bf16[3072,384]{1,0:T(8,128)(2,1)}, bf16[3072,384]{1,0:T(8,128)(2,1)}, u32[]{:S(2)}, u32[]{:S(2)}) collective-permute-start(bf16[3072,384]{1,0:T(8,128)(2,1)} %get-tuple-element.353), channel_id=1, source_target_pairs={{0,16},{16,0},{1,17},{17,1},{2,18},{18,2},{3,19},{19,3},{4,20},{20... | collective-permute-start | bytes 7077896 | tf_op jit(solution)/shard_map/ppermute | solution.py:454
  879.2 65.3 %collective-permute-start.27 = (bf16[3072,384]{1,0:T(8,128)(2,1)}, bf16[3072,384]{1,0:T(8,128)(2,1)}, u32[]{:S(2)}, u32[]{:S(2)}) collective-permute-start(bf16[3072,384]{1,0:T(8,128)(2,1)} %get-tuple-element.355), channel_id=1, source_target_pairs={{0,8},{8,0},{1,9},{9,1},{2,10},{10,2},{3,11},{11,3},{4,12},{12,4},... | collective-permute-start | bytes 7077896 | tf_op jit(solution)/shard_map/ppermute | solution.py:454
  894.1 1.4 collective-permute-start.31
  894.1 16.9 %collective-permute-start.28 = (bf16[384,512]{1,0:T(8,128)(2,1)S(1)}, bf16[384,512]{1,0:T(8,128)(2,1)S(1)}, u32[]{:S(2)}, u32[]{:S(2)}) collective-permute-start(bf16[384,512]{1,0:T(8,128)(2,1)S(1)} %copy-done.102), channel_id=1, source_target_pairs={{0,1},{1,2},{2,3},{3,0},{4,5},{5,6},{6,7},{7,4},{8,9},{9,10},{10,1... | collective-permute-start | bytes 1179656 | tf_op jit(solution)/shard_map/ppermute | solution.py:454
  894.1 49.5 %collective-permute-start.29 = (bf16[384,512]{1,0:T(8,128)(2,1)S(1)}, bf16[384,512]{1,0:T(8,128)(2,1)S(1)}, u32[]{:S(2)}, u32[]{:S(2)}) collective-permute-start(bf16[384,512]{1,0:T(8,128)(2,1)S(1)} %copy-done.101), channel_id=1, source_target_pairs={{0,2},{1,3},{2,0},{3,1},{4,6},{5,7},{6,4},{7,5},{8,10},{9,11},{10,... | collective-permute-start | bytes 1179656 | tf_op jit(solution)/shard_map/ppermute | solution.py:454
  895.5 48.1 %collective-permute-start.30 = (bf16[384,512]{1,0:T(8,128)(2,1)S(1)}, bf16[384,512]{1,0:T(8,128)(2,1)S(1)}, u32[]{:S(2)}, u32[]{:S(2)}) collective-permute-start(bf16[384,512]{1,0:T(8,128)(2,1)S(1)} %copy-done.100), channel_id=1, source_target_pairs={{0,3},{1,0},{2,1},{3,2},{4,7},{5,4},{6,5},{7,6},{8,11},{9,8},{10,9... | collective-permute-start | bytes 1179656 | tf_op jit(solution)/shard_map/ppermute | solution.py:454
  911.0 32.7 %copy-start.97 = (bf16[384,512]{1,0:T(8,128)(2,1)}, bf16[384,512]{1,0:T(8,128)(2,1)S(1)}, u32[]{:S(2)}) copy-start(bf16[384,512]{1,0:T(8,128)(2,1)S(1)} %collective-permute-done.28) | copy-start | bytes 1179652
  950.3 29.0 %collective-permute-start.32 = (bf16[1536,384]{1,0:T(8,128)(2,1)S(1)}, bf16[1536,384]{1,0:T(8,128)(2,1)S(1)}, u32[]{:S(2)}, u32[]{:S(2)}) collective-permute-start(bf16[1536,384]{1,0:T(8,128)(2,1)S(1)} %get-tuple-element.369), channel_id=1, source_target_pairs={{0,8},{8,0},{1,9},{9,1},{2,10},{10,2},{3,11},{11,3},{4,12},{12,4},... | collective-permute-start | bytes 3538952 | tf_op jit(solution)/shard_map/ppermute | solution.py:454
  951.1 28.9 %collective-permute-start.33 = (bf16[1536,384]{1,0:T(8,128)(2,1)S(1)}, bf16[1536,384]{1,0:T(8,128)(2,1)S(1)}, u32[]{:S(2)}, u32[]{:S(2)}) collective-permute-start(bf16[1536,384]{1,0:T(8,128)(2,1)S(1)} %get-tuple-element.371), channel_id=1, source_target_pairs={{0,16},{16,0},{1,17},{17,1},{2,18},{18,2},{3,19},{19,3},{4,20},{20... | collective-permute-start | bytes 3538952 | tf_op jit(solution)/shard_map/ppermute | solution.py:454
  951.7 87.1 %collective-permute-start.37 = (bf16[3072,384]{1,0:T(8,128)(2,1)}, bf16[3072,384]{1,0:T(8,128)(2,1)}, u32[]{:S(2)}, u32[]{:S(2)}) collective-permute-start(bf16[3072,384]{1,0:T(8,128)(2,1)} %get-tuple-element.394), channel_id=1, source_target_pairs={{0,16},{16,0},{1,17},{17,1},{2,18},{18,2},{3,19},{19,3},{4,20},{20... | collective-permute-start | bytes 7077896 | tf_op jit(solution)/shard_map/ppermute | solution.py:454
  953.1 85.6 %collective-permute-start.38 = (bf16[3072,384]{1,0:T(8,128)(2,1)}, bf16[3072,384]{1,0:T(8,128)(2,1)}, u32[]{:S(2)}, u32[]{:S(2)}) collective-permute-start(bf16[3072,384]{1,0:T(8,128)(2,1)} %get-tuple-element.396), channel_id=1, source_target_pairs={{0,8},{8,0},{1,9},{9,1},{2,10},{10,2},{3,11},{11,3},{4,12},{12,4},... | collective-permute-start | bytes 7077896 | tf_op jit(solution)/shard_map/ppermute | solution.py:454
  984.4 54.4 %copy-start.6 = (bf16[3072,384]{1,0:T(8,128)(2,1)S(1)}, bf16[3072,384]{1,0:T(8,128)(2,1)}, u32[]{:S(2)}) copy-start(bf16[3072,384]{1,0:T(8,128)(2,1)} %copy-done.5) | copy-start | bytes 7077892
  984.4 15.0 %collective-permute-start.34 = (bf16[384,768]{1,0:T(8,128)(2,1)}, bf16[384,768]{1,0:T(8,128)(2,1)S(1)}, u32[]{:S(2)}, u32[]{:S(2)}) collective-permute-start(bf16[384,768]{1,0:T(8,128)(2,1)} %pad_maximum_fusion.6), channel_id=1, source_target_pairs={{0,1},{1,2},{2,3},{3,0},{4,5},{5,6},{6,7},{7,4},{8,9},{9,10},{10,1... | collective-permute-start | bytes 1769480 | tf_op jit(solution)/shard_map/ppermute | solution.py:454
  984.4 54.3 %collective-permute-start.35 = (bf16[384,768]{1,0:T(8,128)(2,1)}, bf16[384,768]{1,0:T(8,128)(2,1)S(1)}, u32[]{:S(2)}, u32[]{:S(2)}) collective-permute-start(bf16[384,768]{1,0:T(8,128)(2,1)} %pad_maximum_fusion.7), channel_id=1, source_target_pairs={{0,2},{1,3},{2,0},{3,1},{4,6},{5,7},{6,4},{7,5},{8,10},{9,11},{10,... | collective-permute-start | bytes 1769480 | tf_op jit(solution)/shard_map/ppermute | solution.py:454
  989.1 49.6 %collective-permute-start.36 = (bf16[384,768]{1,0:T(8,128)(2,1)}, bf16[384,768]{1,0:T(8,128)(2,1)}, u32[]{:S(2)}, u32[]{:S(2)}) collective-permute-start(bf16[384,768]{1,0:T(8,128)(2,1)} %pad_maximum_fusion.8), channel_id=1, source_target_pairs={{0,3},{1,0},{2,1},{3,2},{4,7},{5,4},{6,5},{7,6},{8,11},{9,8},{10,9... | collective-permute-start | bytes 1769480 | tf_op jit(solution)/shard_map/ppermute | solution.py:454
  999.4 41.8 %copy-start.93 = (bf16[384,768]{1,0:T(8,128)(2,1)}, bf16[384,768]{1,0:T(8,128)(2,1)S(1)}, u32[]{:S(2)}) copy-start(bf16[384,768]{1,0:T(8,128)(2,1)S(1)} %collective-permute-done.34) | copy-start | bytes 1769476
  1047.9 25.6 %collective-permute-start.39 = (bf16[1536,384]{1,0:T(8,128)(2,1)}, bf16[1536,384]{1,0:T(8,128)(2,1)}, u32[]{:S(2)}, u32[]{:S(2)}) collective-permute-start(bf16[1536,384]{1,0:T(8,128)(2,1)} %get-tuple-element.406), channel_id=1, source_target_pairs={{0,8},{8,0},{1,9},{9,1},{2,10},{10,2},{3,11},{11,3},{4,12},{12,4},... | collective-permute-start | bytes 3538952 | tf_op jit(solution)/shard_map/ppermute | solution.py:454
  1049.3 25.0 %collective-permute-start.40 = (bf16[1536,384]{1,0:T(8,128)(2,1)}, bf16[1536,384]{1,0:T(8,128)(2,1)}, u32[]{:S(2)}, u32[]{:S(2)}) collective-permute-start(bf16[1536,384]{1,0:T(8,128)(2,1)} %get-tuple-element.408), channel_id=1, source_target_pairs={{0,16},{16,0},{1,17},{17,1},{2,18},{18,2},{3,19},{19,3},{4,20},{20... | collective-permute-start | bytes 3538952 | tf_op jit(solution)/shard_map/ppermute | solution.py:454
  1049.8 4.4 collective-permute-start.41
  1055.0 5.6 collective-permute-start.42
  1081.4 4.5 collective-permute-start.46
  1082.3 14.1 %collective-permute-start.43 = (bf16[384,768]{1,0:T(8,128)(2,1)}, bf16[384,768]{1,0:T(8,128)(2,1)}, u32[]{:S(2)}, u32[]{:S(2)}) collective-permute-start(bf16[384,768]{1,0:T(8,128)(2,1)} %pad_maximum_fusion.10), channel_id=1, source_target_pairs={{0,1},{1,2},{2,3},{3,0},{4,5},{5,6},{6,7},{7,4},{8,9},{9,10},{10,1... | collective-permute-start | bytes 1769480 | tf_op jit(solution)/shard_map/ppermute | solution.py:454
  1082.3 49.1 %collective-permute-start.44 = (bf16[384,768]{1,0:T(8,128)(2,1)}, bf16[384,768]{1,0:T(8,128)(2,1)}, u32[]{:S(2)}, u32[]{:S(2)}) collective-permute-start(bf16[384,768]{1,0:T(8,128)(2,1)} %pad_maximum_fusion.11), channel_id=1, source_target_pairs={{0,2},{1,3},{2,0},{3,1},{4,6},{5,7},{6,4},{7,5},{8,10},{9,11},{10,... | collective-permute-start | bytes 1769480 | tf_op jit(solution)/shard_map/ppermute | solution.py:454
  1082.3 49.1 %collective-permute-start.45 = (bf16[384,768]{1,0:T(8,128)(2,1)}, bf16[384,768]{1,0:T(8,128)(2,1)}, u32[]{:S(2)}, u32[]{:S(2)}) collective-permute-start(bf16[384,768]{1,0:T(8,128)(2,1)} %pad_maximum_fusion.12), channel_id=1, source_target_pairs={{0,3},{1,0},{2,1},{3,2},{4,7},{5,4},{6,5},{7,6},{8,11},{9,8},{10,9... | collective-permute-start | bytes 1769480 | tf_op jit(solution)/shard_map/ppermute | solution.py:454
  1086.5 4.4 collective-permute-start.47
  (122 other events, 800.6 us)
Sparse Core Ops, SparseCore 0:
  11.4 213.9 all-gather.2
  228.2 234.1 all-gather.4
  695.0 251.6 reduce-scatter.1

commit v14 on v12

--- a/solution.py
+++ b/solution.py
@@ -597,15 +597,21 @@
     return put, wait
 
 
-def ffn_forward_body(core_ref, *refs):
-    normed_ref, middle_ref, gelu_ref, linear_ref, down_ref = refs[:5]
-    result_ref, gelu_factor_ref, linear_factor_ref, kept_ref, sent_ref, stage_ref, sems = refs[5:]
+def ffn_forward_body(whole_layer, core_ref, *refs):
+    normed_ref, gelu_ref, linear_ref = refs[:3]
+    if whole_layer:
+        middle_ref, down_ref, result_ref = refs[3:6]
+    else:
+        hidden_ref = refs[3]
+    gelu_factor_ref, linear_factor_ref, kept_ref, sent_ref, stage_ref, sems = refs[-6:]
     step = pl.program_id(0)
     put, wait = turned_rows(core_ref, kept_ref, sent_ref, stage_ref, sems)
 
-    @pl.when(step == 0)
-    def _():
-        result_ref[...] = middle_ref[...]
+    if whole_layer:
+
+        @pl.when(step == 0)
+        def _():
+            result_ref[...] = middle_ref[...]
 
     @pl.when(step >= 2)
     def _():
@@ -617,7 +623,10 @@
     linear_factor_ref[...] = active
     hidden = (active * linear).astype(jnp.bfloat16)
     put(0, 2, step, hidden.T)
-    result_ref[...] += times_plain(hidden, down_ref[...])
+    if whole_layer:
+        result_ref[...] += times_plain(hidden, down_ref[...])
+    else:
+        hidden_ref[...] = hidden
 
     @pl.when(step == pl.num_programs(0) - 1)
     def _():
@@ -651,17 +660,24 @@
     hidden = pl.BlockSpec((tokens, FORWARD_TILE), lambda i, *_: (0, i))
     side = resident((tokens, width))
     anywhere = pl.BlockSpec(memory_space=pl.ANY)
+    operands = [normed, gathered, gathered]
+    in_specs = [side, hidden_weight(0, width), hidden_weight(1, width)]
+    first_spec, first_shape = hidden, jax.ShapeDtypeStruct((tokens, FF), jnp.bfloat16)
+    if middle is not None:
+        operands += [middle, gathered]
+        in_specs += [side, hidden_weight(2, width)]
+        first_spec, first_shape = side, jax.ShapeDtypeStruct((tokens, width), jnp.float32)
     return pl.pallas_call(
-        ffn_forward_body,
+        functools.partial(ffn_forward_body, middle is not None),
         grid_spec=pltpu.PrefetchScalarGridSpec(
             num_scalar_prefetch=1,
             grid=(FF // FORWARD_TILE,),
-            in_specs=[side, side] + [hidden_weight(kind, width) for kind in range(3)],
-            out_specs=[side, hidden, hidden, anywhere, anywhere],
+            in_specs=in_specs,
+            out_specs=[first_spec, hidden, hidden, anywhere, anywhere],
             scratch_shapes=turned_scratch(1, tokens),
         ),
         out_shape=[
-            jax.ShapeDtypeStruct((tokens, width), jnp.float32),
+            first_shape,
             jax.ShapeDtypeStruct((tokens, FF), jnp.float32),
             jax.ShapeDtypeStruct((tokens, FF), jnp.float32),
             jax.ShapeDtypeStruct((half, tokens), jnp.bfloat16),
@@ -674,7 +690,7 @@
             transcendentals=tokens * FF,
         ),
         name="ffn_forward",
-    )(core_units(), normed, middle, gathered, gathered, gathered)
+    )(core_units(), *operands)
 
 
 def ffn_backward_body(core_ref, *refs):
@@ -1049,7 +1065,8 @@
     middle = stream + times_plain(attended, gathered[3 * INNER : 4 * INNER])
     normed_two, inverse_two = rms_forward(middle, gain_two)
     normed_two_low = normed_two.astype(jnp.bfloat16)
-    result, *factors = ffn_forward(normed_two_low, middle, gathered)
+    last = gate_low is not None
+    result, *factors = ffn_forward(normed_two_low, None if last else middle, gathered)
     kept = (
         stream,
         inverse_one,
@@ -1154,7 +1171,7 @@
     gate_mask = gate_scale * sigmoid_value
     gate_low = gate_mask.astype(jnp.bfloat16)
     gathered_four = fetch_rows(layer4_rows)
-    after_four, kept_four = layer_forward(
+    hidden_four, kept_four = layer_forward(
         after_three, gathered_four, norm_gains[2], norm_gains[3], gate_low, context
     )
     grad_three_out, table_four, grad_gate, gain_four_one, gain_four_two, before, rest = (
@@ -1188,7 +1205,9 @@
     small = before.settle(small, (0, 1))
     small = scatter.step(small, 0, 1)
     small = scatter.start(small, 2, 3)
-    small = scatter.step(small, 0, 1)
+    small, hidden_four = tied(small, hidden_four)
+    after_four = kept_four[8] + times_plain(hidden_four, gathered_four[4 * INNER + 2 * FF :])
+    small, after_four = scatter.step((small, after_four), 0, 1)
     small, rest = scatter.settle((small, rest), (0, 1))
     small = scatter.step(small, 2, 3)
     for bit in range(1, lax.axis_size("z")):

time: 1110 us -> 1110 us (level)
  Pallas kernels: 239 us -> 226 us
    unnamed x271 -> x293, local copies, waits for them, and re-layouts: 44.4 us -> 54.8 us
    dot_general x4 -> x5, matrix products: 19.6 us -> 29.7 us  [times_plain(): return jnp.dot(left_side, weight, preferred_element_type=jnp.float32)]
  transfers between devices with their start and end apart: 49 -> 49, of which waited for: 26 -> 22; matrix products, arithmetic and copies ran while one was open for 11% -> 12% of each run, Pallas kernels for 15% -> 15%
where the time goes in v14:
time: 1110 us; the launch traced here: 1100 us
  waiting for transfers between devices  599 us (54%)
  Pallas kernels  226 us (20%)
  other arithmetic  75.2 us (7%)
  local copies, waits for them, and re-layouts  72.3 us (7%)
  starting transfers between devices  68.1 us (6%)
  matrix products  44.6 us (4%)
  between operations  16 us (1%)
    all_gather x2, waiting for transfers between devices, fetch_rows(): return lax.all_gather(local_rows, DEVICES, axis=0, tiled=True)  333 us
    ppermute x29, waiting for transfers between devices, shift(): lax.ppermute(value, axis, [(i, (i + amount) % count) for i in range(count)])  158 us
    ppermute x4, waiting for transfers between devices, far_pair(): got = lax.ppermute(sent, 'z', pairs)  90.5 us
    unnamed x293, local copies, waits for them, and re-layouts  54.8 us
    pallas_call x2, Pallas kernels, ffn_backward(): pl.pallas_call(ffn_backward_body, grid_spec=pltpu.PrefetchScalarGridSpec(...  53.6 us
    pallas_call x2, Pallas kernels, ffn_forward(): pl.pallas_call(functools.partial(ffn_forward_body, middle is not None), g...  50.3 us
    pallas_call x2, Pallas kernels, weight_grads(): pl.pallas_call(functools.partial(weight_grads_body, chunks, tile), grid_s...  47.3 us
    pallas_call x2, Pallas kernels, attend_backward(): pl.pallas_call(functools.partial(backward_body, width > 2 * INNER), grid_...  36.5 us
  transfers between devices with their start and end apart: 49, of which 22 were waited for; matrix products, arithmetic and copies ran while one was open for 12% of the time, Pallas kernels for 15%

profile of v14, /device:TPU:24, one launch (start us, length us, event | category | flops | bytes accessed | tf_op | source)
XLA Modules:
  0.0 1101.4 jit_solution(6831492078062601504)
XLA Ops:
  7.2 2.5 copy.126
  12.0 3.6 copy.125
  16.6 2.2 fusion.20
  19.8 205.6 %all-gather.3.cloned.1.call-done.refs_1_.refs_2_.refs_4_.refs_3_.refs_5_ = bf16[12288,1472]{1,0:T(8,128)(2,1)} async-done(((bf16[384,1472]{1,0:T(8,128)(2,1)}), bf16[12288,1472]{1,0:T(8,128)(2,1)}) %all-gather.3.cloned.1.call-update) | async-done | bytes 36175888 | tf_op jit(solution)/shard_map/all_gather | solution.py:1052
  225.4 4.2 fusion.38
  232.9 6.4 collective-permute-start.2
  240.0 4.7 bias_tiles.1.refs_4_.refs_6_
  244.7 3.6 copy.130
  248.4 23.2 %collective-permute-done = bf16[288,768]{1,0:T(8,128)(2,1)S(1)} collective-permute-done((bf16[288,768]{1,0:T(8,128)(2,1)S(1)}, bf16[288,768]{1,0:T(8,128)(2,1)S(1)}, u32[]{:S(2)}, u32[]{:S(2)}) %collective-permute-start) | collective-permute-done | bytes 442400 | tf_op jit(solution)/shard_map/ppermute | solution.py:468
  271.7 15.6 %collective-permute-done.1 = bf16[512,768]{1,0:T(8,128)(2,1)} collective-permute-done((bf16[512,768]{1,0:T(8,128)(2,1)}, bf16[512,768]{1,0:T(8,128)(2,1)}, u32[]{:S(2)}, u32[]{:S(2)}) %collective-permute-start.1) | collective-permute-done | bytes 786464 | tf_op jit(solution)/shard_map/ppermute | solution.py:460
  290.2 6.8 attend_forward.2
  297.1 2.7 multiply_reduce_fusion.10
  301.5 28.2 %ffn_forward.2 = (f32[512,1472]{1,0:T(8,128)}, f32[512,3584]{1,0:T(8,128)}, f32[512,3584]{1,0:T(8,128)}, bf16[6144,512]{1,0:T(8,128)(2,1)}, bf16[6144,512]{1,0:T(8,128)(2,1)}) custom-call(s32[2]{0:T(128)S(1)} %pad_add_fusion.core_ref, bf16[512,1472]{1,0:T(8,128)(2,1)S(1)} %multiply_convert_fusion.2.refs_0_, ...), custom_call_target="tpu_custom_call" | custom-call | flops 16206790656 | bytes 50003968 | tf_op jit(solution)/shard_map/ffn_forward/pallas_call | solution.py:670
  329.7 2.4 multiply_reduce_fusion.9
  334.5 127.7 %all-gather.5.cloned.1.call-done.refs_1_.refs_2_.refs_3_.refs_4_.refs_5_ = bf16[12288,1472]{1,0:T(8,128)(2,1)} async-done(((bf16[384,1472]{1,0:T(8,128)(2,1)}), bf16[12288,1472]{1,0:T(8,128)(2,1)}) %all-gather.5.cloned.1.call-update) | async-done | bytes 36175888 | tf_op jit(solution)/shard_map/all_gather | solution.py:1052
  462.2 4.2 fusion.41
  469.4 4.6 collective-permute-start.5
  475.3 40.3 %collective-permute-done.3 = bf16[288,896]{1,0:T(8,128)(2,1)S(1)} collective-permute-done((bf16[288,896]{1,0:T(8,128)(2,1)S(1)}, bf16[288,896]{1,0:T(8,128)(2,1)S(1)}, u32[]{:S(2)}, u32[]{:S(2)}) %collective-permute-start.3) | collective-permute-done | bytes 516128 | tf_op jit(solution)/shard_map/ppermute | solution.py:468
  517.0 7.0 attend_forward.3
  524.1 2.8 multiply_reduce_fusion.7
  528.9 22.2 %ffn_forward.3 = (bf16[512,3584]{1,0:T(8,128)(2,1)}, f32[512,3584]{1,0:T(8,128)}, f32[512,3584]{1,0:T(8,128)}, bf16[6144,512]{1,0:T(8,128)(2,1)}, bf16[6144,512]{1,0:T(8,128)(2,1)}) custom-call(s32[2]{0:T(128)S(1)} %pad_add_fusion.core_ref, bf16[512,1472]{1,0:T(8,128)(2,1)S(1)} %multiply_convert_fusion.refs_0_, ...), custom_call_target="tpu_custom_call" | custom-call | flops 16206790656 | bytes 50003968 | tf_op jit(solution)/shard_map/ffn_forward/pallas_call | solution.py:670
  551.1 26.1 %ffn_backward.2 = (f32[512,1472]{1,0:T(8,128)}, bf16[6144,512]{1,0:T(8,128)(2,1)}, bf16[6144,512]{1,0:T(8,128)(2,1)}) custom-call(s32[2]{0:T(128)S(1)} %pad_add_fusion.core_ref, bf16[512,1472]{1,0:T(8,128)(2,1)S(1)} %bitcast_convert_fusion.refs_0_, f32[512,3584]{1,0:T(8,128)} %get-tuple-element.213.refs_1_, ...), custom_call_target="tpu_custom_call", output_to_operand_aliasing={{1}: (7, {}), {2}: (8, {})} | custom-call | flops 16206790656 | bytes 53673984 | tf_op jit(solution)/shard_map/ffn_backward/pallas_call | solution.py:735
  582.4 2.3 multiply_reduce_fusion.1
  584.7 2.6 fusion.56
  587.3 2.9 convolution_convert_fusion.1.refs_1_
  590.2 18.7 %attend_backward.2 = (bf16[512,384]{1,0:T(8,128)(2,1)S(1)}, bf16[2304,896]{1,0:T(8,128)(2,1)}, f32[3,32,256]{2,1,0:T(8,128)S(1)}) custom-call(s32[4]{0:T(128)S(1)} %get-tuple-element.553.low_ref, s32[4]{0:T(128)S(1)} %get-tuple-element.552.high_ref, bf16[512,384]{1,0:T(8,128)(2,1)S(1)} %copy-done.32, bf16[512,384]{1,0:T(8,128)(2,1)S(1)} %convolution_convert_fusion.1.refs_1_, ...), custom_call_target="tpu_custom_call" | custom-call | flops 4529848320 | bytes 12582912 | tf_op jit(solution)/shard_map/attend_backward/pallas_call | solution.py:361
  611.1 11.1 %collective-permute-start.8 = (bf16[512,896]{1,0:T(8,128)(2,1)S(1)}, bf16[512,896]{1,0:T(8,128)(2,1)S(1)}, u32[]{:S(2)}, u32[]{:S(2)}) collective-permute-start(bf16[512,896]{1,0:T(8,128)(2,1)S(1)} %get-tuple-element.487), channel_id=1, source_target_pairs={{1,0},{2,1},{3,2},{5,4},{6,5},{7,6},{9,8},{10,9},{11,10},{13,12},{... | collective-permute-start | bytes 2752520 | tf_op jit(solution)/shard_map/ppermute | solution.py:460
  625.0 4.0 collective-permute-start.10
  631.8 22.6 %weight_grads.2 = (bf16[3072,256]{1,0:T(8,128)(2,1)S(1)}, bf16[3072,256]{1,0:T(8,128)(2,1)S(1)}, bf16[3072,256]{1,0:T(8,128)(2,1)S(1)}, bf16[3072,256]{1,0:T(8,128)(2,1)S(1)}, bf16[6144,1024]{1,0:T(8,128)(2,1)}) custom-call(s32[6]{0:T(128)S(1)} %copy-done.46, bf16[6144,512]{1,0:T(8,128)(2,1)} %get-tuple-element.223.refs_0_, ...), custom_call_target="tpu_custom_call" | custom-call | flops 18522046464 | bytes 31457280 | tf_op jit(solution)/shard_map/weight_grads/pallas_call | solution.py:895
  655.6 14.8 %collective-permute-done.10 = bf16[288,896]{1,0:T(8,128)(2,1)S(1)} collective-permute-done((bf16[288,896]{1,0:T(8,128)(2,1)S(1)}, bf16[288,896]{1,0:T(8,128)(2,1)S(1)}, u32[]{:S(2)}, u32[]{:S(2)}) %collective-permute-start.10) | collective-permute-done | bytes 516128 | tf_op jit(solution)/shard_map/ppermute | solution.py:468
  675.4 2.5 pad_maximum_fusion.5
  682.8 10.4 attention_fill.2
  697.9 2.3 collective-permute-start.13
  702.9 6.6 multiply_reduce_fusion.2
  709.6 2.7 fusion.54
  712.3 27.5 %ffn_backward.3 = (f32[512,1472]{1,0:T(8,128)}, bf16[6144,512]{1,0:T(8,128)(2,1)}, bf16[6144,512]{1,0:T(8,128)(2,1)}) custom-call(s32[2]{0:T(128)S(1)} %pad_add_fusion.core_ref, bf16[512,1472]{1,0:T(8,128)(2,1)S(1)} %get-tuple-element.482.refs_0_, f32[512,3584]{1,0:T(8,128)} %get-tuple-element.253.refs_1_, ...), custom_call_target="tpu_custom_call", output_to_operand_aliasing={{1}: (7, {}), {2}: (8, {})} | custom-call | flops 16206790656 | bytes 53673984 | tf_op jit(solution)/shard_map/ffn_backward/pallas_call | solution.py:735
  756.3 2.5 fusion.53
  759.4 3.5 convolution_convert_fusion.refs_1_
  763.0 17.8 %attend_backward.3 = (bf16[512,384]{1,0:T(8,128)(2,1)S(1)}, bf16[2304,768]{1,0:T(8,128)(2,1)}, f32[3,32,256]{2,1,0:T(8,128)S(1)}) custom-call(s32[4]{0:T(128)S(1)} %get-tuple-element.553.low_ref, s32[4]{0:T(128)S(1)} %get-tuple-element.552.high_ref, bf16[512,384]{1,0:T(8,128)(2,1)S(1)} %copy-done.35, bf16[512,384]{1,0:T(8,128)(2,1)S(1)} %convolution_convert_fusion.refs_1_, ...), custom_call_target="tpu_custom_call" | custom-call | flops 4529848320 | bytes 12582912 | tf_op jit(solution)/shard_map/attend_backward/pallas_call | solution.py:361
  788.7 9.9 collective-permute-start.21
  798.6 24.6 %weight_grads.3 = (bf16[3072,384]{1,0:T(8,128)(2,1)}, bf16[3072,384]{1,0:T(8,128)(2,1)}, bf16[3072,384]{1,0:T(8,128)(2,1)S(1)}, bf16[3072,384]{1,0:T(8,128)(2,1)...) custom-call(s32[6]{0:T(128)S(1)} %copy-done.47, ...), custom_call_target="tpu_custom_call" | custom-call | flops 18522046464 | bytes 31457280 | tf_op jit(solution)/shard_map/weight_grads/pallas_call | solution.py:895
  823.3 12.2 %collective-permute-done.21 = bf16[288,768]{1,0:T(8,128)(2,1)S(1)} collective-permute-done((bf16[288,768]{1,0:T(8,128)(2,1)S(1)}, bf16[288,768]{1,0:T(8,128)(2,1)S(1)}, u32[]{:S(2)}, u32[]{:S(2)}) %collective-permute-start.21) | collective-permute-done | bytes 442400 | tf_op jit(solution)/shard_map/ppermute | solution.py:468
  839.6 9.5 attention_fill.3
  857.4 7.6 fusion.29
  867.9 11.6 %collective-permute-done.26 = bf16[384,512]{1,0:T(8,128)(2,1)S(1)} collective-permute-done((bf16[384,512]{1,0:T(8,128)(2,1)S(1)}, bf16[384,512]{1,0:T(8,128)(2,1)S(1)}, u32[]{:S(2)}, u32[]{:S(2)}) %collective-permute-start.26) | collective-permute-done | bytes 393248 | tf_op jit(solution)/shard_map/ppermute | solution.py:454
  879.5 25.4 %collective-permute-done.27 = bf16[384,512]{1,0:T(8,128)(2,1)S(1)} collective-permute-done((bf16[384,512]{1,0:T(8,128)(2,1)S(1)}, bf16[384,512]{1,0:T(8,128)(2,1)S(1)}, u32[]{:S(2)}, u32[]{:S(2)}) %collective-permute-start.27) | collective-permute-done | bytes 393248 | tf_op jit(solution)/shard_map/ppermute | solution.py:454
  905.0 15.1 %collective-permute-done.24 = bf16[3072,384]{1,0:T(8,128)(2,1)} collective-permute-done((bf16[3072,384]{1,0:T(8,128)(2,1)}, bf16[3072,384]{1,0:T(8,128)(2,1)}, u32[]{:S(2)}, u32[]{:S(2)}) %collective-permute-start.24) | collective-permute-done | bytes 2359328 | tf_op jit(solution)/shard_map/ppermute | solution.py:454
  920.1 3.0 add_convert_fusion.2
  924.9 2.4 add_convert_fusion.3
  931.7 10.0 fusion.10
  941.7 14.9 %collective-permute-done.30 = bf16[1536,384]{1,0:T(8,128)(2,1)S(1)} collective-permute-done((bf16[1536,384]{1,0:T(8,128)(2,1)S(1)}, bf16[1536,384]{1,0:T(8,128)(2,1)S(1)}, u32[]{:S(2)}, u32[]{:S(2)}) %collective-permute-start.30) | collective-permute-done | bytes 1179680 | tf_op jit(solution)/shard_map/ppermute | solution.py:454
  959.9 7.9 collective-permute-done.32
  967.8 27.3 %collective-permute-done.33 = bf16[384,768]{1,0:T(8,128)(2,1)S(1)} collective-permute-done((bf16[384,768]{1,0:T(8,128)(2,1)S(1)}, bf16[384,768]{1,0:T(8,128)(2,1)S(1)}, u32[]{:S(2)}, u32[]{:S(2)}) %collective-permute-start.33) | collective-permute-done | bytes 589856 | tf_op jit(solution)/shard_map/ppermute | solution.py:454
  996.5 3.0 add_convert_fusion
  1001.6 2.4 add_convert_fusion.1
  1006.9 2.5 fusion.28
  1009.4 3.5 copy.142
  1013.1 2.3 add_add_fusion.2
  1015.4 3.5 copy.141
  1018.9 11.8 %collective-permute-done.37 = bf16[1536,384]{1,0:T(8,128)(2,1)} collective-permute-done((bf16[1536,384]{1,0:T(8,128)(2,1)}, bf16[1536,384]{1,0:T(8,128)(2,1)}, u32[]{:S(2)}, u32[]{:S(2)}) %collective-permute-start.37) | collective-permute-done | bytes 1179680 | tf_op jit(solution)/shard_map/ppermute | solution.py:454
  1045.1 3.1 copy.144
  1048.1 5.5 collective-permute-done.41
  1053.7 32.5 %collective-permute-done.42 = bf16[384,768]{1,0:T(8,128)(2,1)} collective-permute-done((bf16[384,768]{1,0:T(8,128)(2,1)}, bf16[384,768]{1,0:T(8,128)(2,1)}, u32[]{:S(2)}, u32[]{:S(2)}) %collective-permute-start.42) | collective-permute-done | bytes 589856 | tf_op jit(solution)/shard_map/ppermute | solution.py:454
  1090.9 3.0 copy.143
  (486 shorter events, 129.4 us)
Async XLA Ops:
  7.2 218.2 %all-gather.3.cloned.1.call-start = ((), (), s32[]{:S(2)}) async-start(), calls=%async_computation.1 | async-start | bytes 38928384 | tf_op jit(solution)/shard_map/all_gather | solution.py:1052
  9.7 452.5 %all-gather.5.cloned.1.call-start = ((), (), s32[]{:S(2)}) async-start(), calls=%async_computation.2 | async-start | bytes 38928384 | tf_op jit(solution)/shard_map/all_gather | solution.py:1052
  11.8 983.2 %reduce-scatter.2.cloned.1.call-start = ((), (), s32[]{:S(2)}) async-start(), calls=%async_computation.3 | async-start | bytes 13369344 | tf_op jit(solution)/shard_map/reduce_scatter | solution.py:1150
  16.6 283.8 %copy-start.106 = (f32[1472]{0:T(1024)}, f32[1472]{0:T(1024)S(1)}, u32[]{:S(2)}) copy-start(f32[1472]{0:T(1024)S(1)} %get-tuple-element.471) | copy-start | bytes 17668
  19.4 210.2 %copy-start.126 = (f32[512]{0:T(512)}, f32[512]{0:T(512)S(1)}, u32[]{:S(2)}) copy-start(f32[512]{0:T(512)S(1)} %get-tuple-element.539) | copy-start | bytes 6148
  19.8 209.9 %copy-start.76 = (bf16[512,1472]{1,0:T(8,128)(2,1)}, bf16[512,1472]{1,0:T(8,128)(2,1)S(1)}, u32[]{:S(2)}) copy-start(bf16[512,1472]{1,0:T(8,128)(2,1)S(1)} %fusion.22) | copy-start | bytes 4521988
  19.8 219.6 %copy-start.136 = (f32[32,6]{0,1:T(8,128)S(1)}, f32[32,6]{0,1:T(8,128)}, u32[]{:S(2)}) copy-start(f32[32,6]{0,1:T(8,128)} %param.13) | copy-start | bytes 2308
  230.7 40.9 %collective-permute-start = (bf16[288,768]{1,0:T(8,128)(2,1)S(1)}, bf16[288,768]{1,0:T(8,128)(2,1)S(1)}, u32[]{:S(2)}, u32[]{:S(2)}) collective-permute-start(bf16[288,768]{1,0:T(8,128)(2,1)S(1)} %slice_select_fusion.1), channel_id=1, source_target_pairs={{0,2},{1,3},{2,0},{3,1},{4,6},{5,7},{6,4},{7,5},{8,10},{9,11},{10,... | collective-permute-start | bytes 1327112 | tf_op jit(solution)/shard_map/ppermute | solution.py:468
  231.3 55.9 %collective-permute-start.1 = (bf16[512,768]{1,0:T(8,128)(2,1)}, bf16[512,768]{1,0:T(8,128)(2,1)}, u32[]{:S(2)}, u32[]{:S(2)}) collective-permute-start(bf16[512,768]{1,0:T(8,128)(2,1)} %slice.181), channel_id=1, source_target_pairs={{0,1},{1,2},{2,3},{4,5},{5,6},{6,7},{8,9},{9,10},{10,11},{12,13},{... | collective-permute-start | bytes 2359304 | tf_op jit(solution)/shard_map/ppermute | solution.py:460
  232.9 55.6 %collective-permute-start.2 = (bf16[512,768]{1,0:T(8,128)(2,1)}, bf16[512,768]{1,0:T(8,128)(2,1)}, u32[]{:S(2)}, u32[]{:S(2)}) collective-permute-start(bf16[512,768]{1,0:T(8,128)(2,1)} %slice.181), channel_id=1, source_target_pairs={{1,0},{2,1},{3,2},{5,4},{6,5},{7,6},{9,8},{10,9},{11,10},{13,12},{... | collective-permute-start | bytes 2359304 | tf_op jit(solution)/shard_map/ppermute | solution.py:460
  248.4 41.8 %copy-start.34 = (bf16[512,384]{1,0:T(8,128)(2,1)}, bf16[512,384]{1,0:T(8,128)(2,1)S(1)}, u32[]{:S(2)}) copy-start(bf16[512,384]{1,0:T(8,128)(2,1)S(1)} %slice.178.refs_0_) | copy-start | bytes 1179652
  300.4 29.2 %copy-start.118 = (f32[512]{0:T(512)}, f32[512]{0:T(512)S(1)}, u32[]{:S(2)}) copy-start(f32[512]{0:T(512)S(1)} %get-tuple-element.541) | copy-start | bytes 6148
  301.5 28.2 %copy-start.1 = (bf16[512,1472]{1,0:T(8,128)(2,1)}, bf16[512,1472]{1,0:T(8,128)(2,1)S(1)}, u32[]{:S(2)}) copy-start(bf16[512,1472]{1,0:T(8,128)(2,1)S(1)} %multiply_convert_fusion.2.refs_0_) | copy-start | bytes 4521988
  301.5 31.8 %copy-start.114 = (f32[1472]{0:T(1024)S(1)}, f32[1472]{0:T(1024)}, u32[]{:S(2)}) copy-start(f32[1472]{0:T(1024)} %param.12) | copy-start | bytes 17668
  334.5 131.9 %copy-start.78 = (bf16[512,1472]{1,0:T(8,128)(2,1)}, bf16[512,1472]{1,0:T(8,128)(2,1)S(1)}, u32[]{:S(2)}) copy-start(bf16[512,1472]{1,0:T(8,128)(2,1)S(1)} %get-tuple-element.493) | copy-start | bytes 4521988
  468.1 47.7 %collective-permute-start.4 = (bf16[512,896]{1,0:T(8,128)(2,1)S(1)}, bf16[512,896]{1,0:T(8,128)(2,1)S(1)}, u32[]{:S(2)}, u32[]{:S(2)}) collective-permute-start(bf16[512,896]{1,0:T(8,128)(2,1)S(1)} %pad_maximum_fusion.2), channel_id=1, source_target_pairs={{0,1},{1,2},{2,3},{4,5},{5,6},{6,7},{8,9},{9,10},{10,11},{12,13},{... | collective-permute-start | bytes 2752520 | tf_op jit(solution)/shard_map/ppermute | solution.py:460
  469.4 46.7 %collective-permute-start.5 = (bf16[512,896]{1,0:T(8,128)(2,1)S(1)}, bf16[512,896]{1,0:T(8,128)(2,1)S(1)}, u32[]{:S(2)}, u32[]{:S(2)}) collective-permute-start(bf16[512,896]{1,0:T(8,128)(2,1)S(1)} %pad_maximum_fusion.2), channel_id=1, source_target_pairs={{1,0},{2,1},{3,2},{5,4},{6,5},{7,6},{9,8},{10,9},{11,10},{13,12},{... | collective-permute-start | bytes 2752520 | tf_op jit(solution)/shard_map/ppermute | solution.py:460
  474.0 41.6 %collective-permute-start.3 = (bf16[288,896]{1,0:T(8,128)(2,1)S(1)}, bf16[288,896]{1,0:T(8,128)(2,1)S(1)}, u32[]{:S(2)}, u32[]{:S(2)}) collective-permute-start(bf16[288,896]{1,0:T(8,128)(2,1)S(1)} %fusion.49), channel_id=1, source_target_pairs={{0,2},{1,3},{2,0},{3,1},{4,6},{5,7},{6,4},{7,5},{8,10},{9,11},{10,... | collective-permute-start | bytes 1548296 | tf_op jit(solution)/shard_map/ppermute | solution.py:468
  475.3 41.0 %copy-start.31 = (bf16[512,384]{1,0:T(8,128)(2,1)}, bf16[512,384]{1,0:T(8,128)(2,1)S(1)}, u32[]{:S(2)}) copy-start(bf16[512,384]{1,0:T(8,128)(2,1)S(1)} %slice.184.refs_0_) | copy-start | bytes 1179652
  577.1 54.6 %collective-permute-start.6 = (bf16[6144,512]{1,0:T(8,128)(2,1)}, bf16[6144,512]{1,0:T(8,128)(2,1)}, u32[]{:S(2)}, u32[]{:S(2)}) collective-permute-start(bf16[6144,512]{1,0:T(8,128)(2,1)} %get-tuple-element.224), channel_id=1, source_target_pairs={{0,4},{4,0},{1,5},{5,1},{2,6},{6,2},{3,7},{7,3},{8,12},{12,8},{9,1... | collective-permute-start | bytes 18874376 | tf_op jit(solution)/shard_map/ppermute | solution.py:454
  580.9 50.0 %collective-permute-start.7 = (bf16[1024,1536]{1,0:T(8,128)(2,1)S(1)}, bf16[1024,1536]{1,0:T(8,128)(2,1)S(1)}, u32[]{:S(2)}, u32[]{:S(2)}) collective-permute-start(bf16[1024,1536]{1,0:T(8,128)(2,1)S(1)} %fusion.16.refs_2_.refs_3_), channel_id=1, source_target_pairs={{0,4},{4,0},{1,5},{5,1},{2,6},{6,2},{3,7},{7,3},{8,12},{12,8},{9,1... | collective-permute-start | bytes 9437192 | tf_op jit(solution)/shard_map/ppermute | solution.py:454
  608.9 62.2 %copy-start.33 = (bf16[512,384]{1,0:T(8,128)(2,1)}, bf16[512,384]{1,0:T(8,128)(2,1)S(1)}, u32[]{:S(2)}) copy-start(bf16[512,384]{1,0:T(8,128)(2,1)S(1)} %get-tuple-element.220) | copy-start | bytes 1179652
  611.1 59.3 %collective-permute-start.8 = (bf16[512,896]{1,0:T(8,128)(2,1)S(1)}, bf16[512,896]{1,0:T(8,128)(2,1)S(1)}, u32[]{:S(2)}, u32[]{:S(2)}) collective-permute-start(bf16[512,896]{1,0:T(8,128)(2,1)S(1)} %get-tuple-element.487), channel_id=1, source_target_pairs={{1,0},{2,1},{3,2},{5,4},{6,5},{7,6},{9,8},{10,9},{11,10},{13,12},{... | collective-permute-start | bytes 2752520 | tf_op jit(solution)/shard_map/ppermute | solution.py:460
  622.2 48.2 %collective-permute-start.9 = (bf16[512,896]{1,0:T(8,128)(2,1)S(1)}, bf16[512,896]{1,0:T(8,128)(2,1)S(1)}, u32[]{:S(2)}, u32[]{:S(2)}) collective-permute-start(bf16[512,896]{1,0:T(8,128)(2,1)S(1)} %get-tuple-element.486), channel_id=1, source_target_pairs={{0,1},{1,2},{2,3},{4,5},{5,6},{6,7},{8,9},{9,10},{10,11},{12,13},{... | collective-permute-start | bytes 2752520 | tf_op jit(solution)/shard_map/ppermute | solution.py:460
  625.0 45.4 %collective-permute-start.10 = (bf16[288,896]{1,0:T(8,128)(2,1)S(1)}, bf16[288,896]{1,0:T(8,128)(2,1)S(1)}, u32[]{:S(2)}, u32[]{:S(2)}) collective-permute-start(bf16[288,896]{1,0:T(8,128)(2,1)S(1)} %slice_select_fusion), channel_id=1, source_target_pairs={{0,2},{1,3},{2,0},{3,1},{4,6},{5,7},{6,4},{7,5},{8,10},{9,11},{10,... | collective-permute-start | bytes 1548296 | tf_op jit(solution)/shard_map/ppermute | solution.py:468
  630.9 46.9 %collective-permute-start.12 = (bf16[1024,1536]{1,0:T(8,128)(2,1)}, bf16[1024,1536]{1,0:T(8,128)(2,1)}, u32[]{:S(2)}, u32[]{:S(2)}) collective-permute-start(bf16[1024,1536]{1,0:T(8,128)(2,1)} %fusion.17.refs_2_), channel_id=1, source_target_pairs={{0,4},{4,0},{1,5},{5,1},{2,6},{6,2},{3,7},{7,3},{8,12},{12,8},{9,1... | collective-permute-start | bytes 9437192 | tf_op jit(solution)/shard_map/ppermute | solution.py:454
  672.4 5.4 collective-permute-start.11
  697.9 43.3 %collective-permute-start.13 = (bf16[3072,256]{1,0:T(8,128)(2,1)}, bf16[3072,256]{1,0:T(8,128)(2,1)}, u32[]{:S(2)}, u32[]{:S(2)}) collective-permute-start(bf16[3072,256]{1,0:T(8,128)(2,1)} %copy-done.38), channel_id=1, source_target_pairs={{0,16},{16,0},{1,17},{17,1},{2,18},{18,2},{3,19},{19,3},{4,20},{20... | collective-permute-start | bytes 4718600 | tf_op jit(solution)/shard_map/ppermute | solution.py:454
  700.2 42.5 %collective-permute-start.14 = (bf16[3072,256]{1,0:T(8,128)(2,1)}, bf16[3072,256]{1,0:T(8,128)(2,1)}, u32[]{:S(2)}, u32[]{:S(2)}) collective-permute-start(bf16[3072,256]{1,0:T(8,128)(2,1)} %copy-done.41), channel_id=1, source_target_pairs={{0,8},{8,0},{1,9},{9,1},{2,10},{10,2},{3,11},{11,3},{4,12},{12,4},... | collective-permute-start | bytes 4718600 | tf_op jit(solution)/shard_map/ppermute | solution.py:454
  712.3 30.3 %copy-start.24 = (bf16[3072,256]{1,0:T(8,128)(2,1)S(1)}, bf16[3072,256]{1,0:T(8,128)(2,1)}, u32[]{:S(2)}) copy-start(bf16[3072,256]{1,0:T(8,128)(2,1)} %copy-done.23) | copy-start | bytes 4718596
  749.3 49.3 %collective-permute-start.17 = (bf16[6144,512]{1,0:T(8,128)(2,1)}, bf16[6144,512]{1,0:T(8,128)(2,1)}, u32[]{:S(2)}, u32[]{:S(2)}) collective-permute-start(bf16[6144,512]{1,0:T(8,128)(2,1)} %get-tuple-element.290), channel_id=1, source_target_pairs={{0,4},{4,0},{1,5},{5,1},{2,6},{6,2},{3,7},{7,3},{8,12},{12,8},{9,1... | collective-permute-start | bytes 18874376 | tf_op jit(solution)/shard_map/ppermute | solution.py:454
  751.2 37.5 %collective-permute-start.18 = (bf16[1024,1536]{1,0:T(8,128)(2,1)S(1)}, bf16[1024,1536]{1,0:T(8,128)(2,1)}, u32[]{:S(2)}, u32[]{:S(2)}) collective-permute-start(bf16[1024,1536]{1,0:T(8,128)(2,1)S(1)} %fusion.18.refs_2_.refs_3_), channel_id=1, source_target_pairs={{0,4},{4,0},{1,5},{5,1},{2,6},{6,2},{3,7},{7,3},{8,12},{12,8},{9,1... | collective-permute-start | bytes 9437192 | tf_op jit(solution)/shard_map/ppermute | solution.py:454
  751.8 29.0 %collective-permute-start.15 = (bf16[1536,256]{1,0:T(8,128)(2,1)}, bf16[1536,256]{1,0:T(8,128)(2,1)}, u32[]{:S(2)}, u32[]{:S(2)}) collective-permute-start(bf16[1536,256]{1,0:T(8,128)(2,1)} %get-tuple-element.268), channel_id=1, source_target_pairs={{0,8},{8,0},{1,9},{9,1},{2,10},{10,2},{3,11},{11,3},{4,12},{12,4},... | collective-permute-start | bytes 2359304 | tf_op jit(solution)/shard_map/ppermute | solution.py:454
  753.5 27.3 %collective-permute-start.16 = (bf16[1536,256]{1,0:T(8,128)(2,1)}, bf16[1536,256]{1,0:T(8,128)(2,1)S(1)}, u32[]{:S(2)}, u32[]{:S(2)}) collective-permute-start(bf16[1536,256]{1,0:T(8,128)(2,1)} %get-tuple-element.270), channel_id=1, source_target_pairs={{0,16},{16,0},{1,17},{17,1},{2,18},{18,2},{3,19},{19,3},{4,20},{20... | collective-permute-start | bytes 2359304 | tf_op jit(solution)/shard_map/ppermute | solution.py:454
  759.2 78.3 %collective-permute-start.23 = (bf16[1024,1536]{1,0:T(8,128)(2,1)S(1)}, bf16[1024,1536]{1,0:T(8,128)(2,1)}, u32[]{:S(2)}, u32[]{:S(2)}) collective-permute-start(bf16[1024,1536]{1,0:T(8,128)(2,1)S(1)} %fusion.19.refs_2_), channel_id=1, source_target_pairs={{0,4},{4,0},{1,5},{5,1},{2,6},{6,2},{3,7},{7,3},{8,12},{12,8},{9,1... | collective-permute-start | bytes 9437192 | tf_op jit(solution)/shard_map/ppermute | solution.py:454
  786.0 49.5 %collective-permute-start.19 = (bf16[512,768]{1,0:T(8,128)(2,1)S(1)}, bf16[512,768]{1,0:T(8,128)(2,1)S(1)}, u32[]{:S(2)}, u32[]{:S(2)}) collective-permute-start(bf16[512,768]{1,0:T(8,128)(2,1)S(1)} %get-tuple-element.490), channel_id=1, source_target_pairs={{1,0},{2,1},{3,2},{5,4},{6,5},{7,6},{9,8},{10,9},{11,10},{13,12},{... | collective-permute-start | bytes 2359304 | tf_op jit(solution)/shard_map/ppermute | solution.py:460
  787.4 48.1 %collective-permute-start.20 = (bf16[512,768]{1,0:T(8,128)(2,1)S(1)}, bf16[512,768]{1,0:T(8,128)(2,1)S(1)}, u32[]{:S(2)}, u32[]{:S(2)}) collective-permute-start(bf16[512,768]{1,0:T(8,128)(2,1)S(1)} %get-tuple-element.489), channel_id=1, source_target_pairs={{0,1},{1,2},{2,3},{4,5},{5,6},{6,7},{8,9},{9,10},{10,11},{12,13},{... | collective-permute-start | bytes 2359304 | tf_op jit(solution)/shard_map/ppermute | solution.py:460
  788.7 46.7 %collective-permute-start.21 = (bf16[288,768]{1,0:T(8,128)(2,1)S(1)}, bf16[288,768]{1,0:T(8,128)(2,1)S(1)}, u32[]{:S(2)}, u32[]{:S(2)}) collective-permute-start(bf16[288,768]{1,0:T(8,128)(2,1)S(1)} %slice_select_fusion.2), channel_id=1, source_target_pairs={{0,2},{1,3},{2,0},{3,1},{4,6},{5,7},{6,4},{7,5},{8,10},{9,11},{10,... | collective-permute-start | bytes 1327112 | tf_op jit(solution)/shard_map/ppermute | solution.py:468
  836.1 3.5 collective-permute-start.22
  854.9 65.2 %collective-permute-start.24 = (bf16[3072,384]{1,0:T(8,128)(2,1)}, bf16[3072,384]{1,0:T(8,128)(2,1)}, u32[]{:S(2)}, u32[]{:S(2)}) collective-permute-start(bf16[3072,384]{1,0:T(8,128)(2,1)} %get-tuple-element.329), channel_id=1, source_target_pairs={{0,16},{16,0},{1,17},{17,1},{2,18},{18,2},{3,19},{19,3},{4,20},{20... | collective-permute-start | bytes 7077896 | tf_op jit(solution)/shard_map/ppermute | solution.py:454
  855.0 65.2 %collective-permute-start.25 = (bf16[3072,384]{1,0:T(8,128)(2,1)}, bf16[3072,384]{1,0:T(8,128)(2,1)}, u32[]{:S(2)}, u32[]{:S(2)}) collective-permute-start(bf16[3072,384]{1,0:T(8,128)(2,1)} %get-tuple-element.331), channel_id=1, source_target_pairs={{0,8},{8,0},{1,9},{9,1},{2,10},{10,2},{3,11},{11,3},{4,12},{12,4},... | collective-permute-start | bytes 7077896 | tf_op jit(solution)/shard_map/ppermute | solution.py:454
  865.1 1.3 collective-permute-start.29
  865.2 14.4 %collective-permute-start.26 = (bf16[384,512]{1,0:T(8,128)(2,1)S(1)}, bf16[384,512]{1,0:T(8,128)(2,1)S(1)}, u32[]{:S(2)}, u32[]{:S(2)}) collective-permute-start(bf16[384,512]{1,0:T(8,128)(2,1)S(1)} %copy-done.104), channel_id=1, source_target_pairs={{0,1},{1,2},{2,3},{3,0},{4,5},{5,6},{6,7},{7,4},{8,9},{9,10},{10,1... | collective-permute-start | bytes 1179656 | tf_op jit(solution)/shard_map/ppermute | solution.py:454
  865.2 39.7 %collective-permute-start.27 = (bf16[384,512]{1,0:T(8,128)(2,1)S(1)}, bf16[384,512]{1,0:T(8,128)(2,1)S(1)}, u32[]{:S(2)}, u32[]{:S(2)}) collective-permute-start(bf16[384,512]{1,0:T(8,128)(2,1)S(1)} %copy-done.103), channel_id=1, source_target_pairs={{0,2},{1,3},{2,0},{3,1},{4,6},{5,7},{6,4},{7,5},{8,10},{9,11},{10,... | collective-permute-start | bytes 1179656 | tf_op jit(solution)/shard_map/ppermute | solution.py:454
  866.4 38.6 %collective-permute-start.28 = (bf16[384,512]{1,0:T(8,128)(2,1)S(1)}, bf16[384,512]{1,0:T(8,128)(2,1)S(1)}, u32[]{:S(2)}, u32[]{:S(2)}) collective-permute-start(bf16[384,512]{1,0:T(8,128)(2,1)S(1)} %copy-done.102), channel_id=1, source_target_pairs={{0,3},{1,0},{2,1},{3,2},{4,7},{5,4},{6,5},{7,6},{8,11},{9,8},{10,9... | collective-permute-start | bytes 1179656 | tf_op jit(solution)/shard_map/ppermute | solution.py:454
  879.5 43.6 %copy-start.99 = (bf16[384,512]{1,0:T(8,128)(2,1)}, bf16[384,512]{1,0:T(8,128)(2,1)S(1)}, u32[]{:S(2)}) copy-start(bf16[384,512]{1,0:T(8,128)(2,1)S(1)} %collective-permute-done.26) | copy-start | bytes 1179652
  927.6 29.0 %collective-permute-start.30 = (bf16[1536,384]{1,0:T(8,128)(2,1)S(1)}, bf16[1536,384]{1,0:T(8,128)(2,1)S(1)}, u32[]{:S(2)}, u32[]{:S(2)}) collective-permute-start(bf16[1536,384]{1,0:T(8,128)(2,1)S(1)} %get-tuple-element.346), channel_id=1, source_target_pairs={{0,8},{8,0},{1,9},{9,1},{2,10},{10,2},{3,11},{11,3},{4,12},{12,4},... | collective-permute-start | bytes 3538952 | tf_op jit(solution)/shard_map/ppermute | solution.py:454
  927.7 29.0 %collective-permute-start.31 = (bf16[1536,384]{1,0:T(8,128)(2,1)S(1)}, bf16[1536,384]{1,0:T(8,128)(2,1)S(1)}, u32[]{:S(2)}, u32[]{:S(2)}) collective-permute-start(bf16[1536,384]{1,0:T(8,128)(2,1)S(1)} %get-tuple-element.348), channel_id=1, source_target_pairs={{0,16},{16,0},{1,17},{17,1},{2,18},{18,2},{3,19},{19,3},{4,20},{20... | collective-permute-start | bytes 3538952 | tf_op jit(solution)/shard_map/ppermute | solution.py:454
  927.7 68.8 %collective-permute-start.35 = (bf16[3072,384]{1,0:T(8,128)(2,1)}, bf16[3072,384]{1,0:T(8,128)(2,1)}, u32[]{:S(2)}, u32[]{:S(2)}) collective-permute-start(bf16[3072,384]{1,0:T(8,128)(2,1)} %get-tuple-element.376), channel_id=1, source_target_pairs={{0,16},{16,0},{1,17},{17,1},{2,18},{18,2},{3,19},{19,3},{4,20},{20... | collective-permute-start | bytes 7077896 | tf_op jit(solution)/shard_map/ppermute | solution.py:454
  929.7 66.8 %collective-permute-start.36 = (bf16[3072,384]{1,0:T(8,128)(2,1)}, bf16[3072,384]{1,0:T(8,128)(2,1)}, u32[]{:S(2)}, u32[]{:S(2)}) collective-permute-start(bf16[3072,384]{1,0:T(8,128)(2,1)} %get-tuple-element.378), channel_id=1, source_target_pairs={{0,8},{8,0},{1,9},{9,1},{2,10},{10,2},{3,11},{11,3},{4,12},{12,4},... | collective-permute-start | bytes 7077896 | tf_op jit(solution)/shard_map/ppermute | solution.py:454
  957.8 9.9 collective-permute-start.32
  957.9 37.2 %collective-permute-start.33 = (bf16[384,768]{1,0:T(8,128)(2,1)S(1)}, bf16[384,768]{1,0:T(8,128)(2,1)S(1)}, u32[]{:S(2)}, u32[]{:S(2)}) collective-permute-start(bf16[384,768]{1,0:T(8,128)(2,1)S(1)} %pad_maximum_fusion.9), channel_id=1, source_target_pairs={{0,2},{1,3},{2,0},{3,1},{4,6},{5,7},{6,4},{7,5},{8,10},{9,11},{10,... | collective-permute-start | bytes 1769480 | tf_op jit(solution)/shard_map/ppermute | solution.py:454
  958.0 37.1 %collective-permute-start.34 = (bf16[384,768]{1,0:T(8,128)(2,1)S(1)}, bf16[384,768]{1,0:T(8,128)(2,1)}, u32[]{:S(2)}, u32[]{:S(2)}) collective-permute-start(bf16[384,768]{1,0:T(8,128)(2,1)S(1)} %pad_maximum_fusion.10), channel_id=1, source_target_pairs={{0,3},{1,0},{2,1},{3,2},{4,7},{5,4},{6,5},{7,6},{8,11},{9,8},{10,9... | collective-permute-start | bytes 1769480 | tf_op jit(solution)/shard_map/ppermute | solution.py:454
  967.8 31.7 %copy-start.95 = (bf16[384,768]{1,0:T(8,128)(2,1)}, bf16[384,768]{1,0:T(8,128)(2,1)S(1)}, u32[]{:S(2)}) copy-start(bf16[384,768]{1,0:T(8,128)(2,1)S(1)} %collective-permute-done.32) | copy-start | bytes 1769476
  1005.3 25.4 %collective-permute-start.37 = (bf16[1536,384]{1,0:T(8,128)(2,1)}, bf16[1536,384]{1,0:T(8,128)(2,1)}, u32[]{:S(2)}, u32[]{:S(2)}) collective-permute-start(bf16[1536,384]{1,0:T(8,128)(2,1)} %get-tuple-element.388), channel_id=1, source_target_pairs={{0,8},{8,0},{1,9},{9,1},{2,10},{10,2},{3,11},{11,3},{4,12},{12,4},... | collective-permute-start | bytes 3538952 | tf_op jit(solution)/shard_map/ppermute | solution.py:454
  1006.6 24.1 %collective-permute-start.38 = (bf16[1536,384]{1,0:T(8,128)(2,1)}, bf16[1536,384]{1,0:T(8,128)(2,1)}, u32[]{:S(2)}, u32[]{:S(2)}) collective-permute-start(bf16[1536,384]{1,0:T(8,128)(2,1)} %get-tuple-element.390), channel_id=1, source_target_pairs={{0,16},{16,0},{1,17},{17,1},{2,18},{18,2},{3,19},{19,3},{4,20},{20... | collective-permute-start | bytes 3538952 | tf_op jit(solution)/shard_map/ppermute | solution.py:454
  1006.9 6.0 collective-permute-start.39
  1012.9 6.0 collective-permute-start.40
  1037.7 5.4 collective-permute-start.44
  1039.4 14.2 %collective-permute-start.41 = (bf16[384,768]{1,0:T(8,128)(2,1)}, bf16[384,768]{1,0:T(8,128)(2,1)}, u32[]{:S(2)}, u32[]{:S(2)}) collective-permute-start(bf16[384,768]{1,0:T(8,128)(2,1)} %pad_maximum_fusion.12), channel_id=1, source_target_pairs={{0,1},{1,2},{2,3},{3,0},{4,5},{5,6},{6,7},{7,4},{8,9},{9,10},{10,1... | collective-permute-start | bytes 1769480 | tf_op jit(solution)/shard_map/ppermute | solution.py:454
  1039.4 46.7 %collective-permute-start.42 = (bf16[384,768]{1,0:T(8,128)(2,1)}, bf16[384,768]{1,0:T(8,128)(2,1)}, u32[]{:S(2)}, u32[]{:S(2)}) collective-permute-start(bf16[384,768]{1,0:T(8,128)(2,1)} %pad_maximum_fusion.13), channel_id=1, source_target_pairs={{0,2},{1,3},{2,0},{3,1},{4,6},{5,7},{6,4},{7,5},{8,10},{9,11},{10,... | collective-permute-start | bytes 1769480 | tf_op jit(solution)/shard_map/ppermute | solution.py:454
  1039.5 46.7 %collective-permute-start.43 = (bf16[384,768]{1,0:T(8,128)(2,1)}, bf16[384,768]{1,0:T(8,128)(2,1)}, u32[]{:S(2)}, u32[]{:S(2)}) collective-permute-start(bf16[384,768]{1,0:T(8,128)(2,1)} %pad_maximum_fusion.14), channel_id=1, source_target_pairs={{0,3},{1,0},{2,1},{3,2},{4,7},{5,4},{6,5},{7,6},{8,11},{9,8},{10,9... | collective-permute-start | bytes 1769480 | tf_op jit(solution)/shard_map/ppermute | solution.py:454
  1043.1 5.0 collective-permute-start.45
  1045.1 42.4 %copy-start.89 = (bf16[384,768]{1,0:T(8,128)(2,1)S(1)}, bf16[384,768]{1,0:T(8,128)(2,1)}, u32[]{:S(2)}) copy-start(bf16[384,768]{1,0:T(8,128)(2,1)} %pad_maximum_fusion.11) | copy-start | bytes 1769476
  (124 other events, 785.4 us)
Sparse Core Ops, SparseCore 0:
  11.4 213.9 all-gather.2
  228.2 233.9 all-gather.4
  701.9 228.3 reduce-scatter.1

commit v15 on v14

--- a/solution.py
+++ b/solution.py
@@ -1055,9 +1055,8 @@
 def layer_forward(stream, gathered, gain_one, gain_two, gate_low, context):
     normed, inverse_one = rms_forward(stream, gain_one)
     normed_low = normed.astype(jnp.bfloat16)
-    projected = times_rows(normed_low, gathered[: 3 * INNER]).astype(jnp.bfloat16)
-    queries = projected[:, :INNER]
-    parts = [projected[:, INNER:]]
+    parts = [times_rows(normed_low, gathered[INNER : 3 * INNER]).astype(jnp.bfloat16)]
+    queries = times_rows(normed_low, gathered[:INNER]).astype(jnp.bfloat16)
     if gate_low is not None:
         parts.append(jnp.broadcast_to(gate_low[:, None], (stream.shape[0], BLOCK)))
     shared = with_neighbours(jnp.concatenate(parts, axis=1))

time: 1110 us -> 1100 us (level)
  Pallas kernels: 226 us -> 249 us
  local copies, waits for them, and re-layouts: 72.3 us -> 60.8 us
    pallas_call x2, Pallas kernels: 36.5 us -> 50.2 us  [attend_backward(): pl.pallas_call(functools.partial(backward_body, width > 2 * INNER), grid_...]
    ppermute x29, starting transfers between devices: 21.3 us -> 34.5 us  [shift(): lax.ppermute(value, axis, [(i, (i + amount) % count) for i in range(count)])]
    unnamed x293 -> x281, local copies, waits for them, and re-layouts: 54.8 us -> 41.6 us
    ppermute x4, waiting for transfers between devices: 90.5 us -> 78.1 us  [far_pair(): got = lax.ppermute(sent, 'z', pairs)]
  transfers between devices with their start and end apart: 49 -> 49, of which waited for: 22 -> 24; matrix products, arithmetic and copies ran while one was open for 12% -> 12% of each run, Pallas kernels for 15% -> 16%
where the time goes in v15:
time: 1100 us
  waiting for transfers between devices  590 us (54%)
  Pallas kernels  249 us (23%)
  other arithmetic  75.8 us (7%)
  starting transfers between devices  61.5 us (6%)
  local copies, waits for them, and re-layouts  60.8 us (6%)
  matrix products  47.4 us (4%)
  between operations  16 us (1%)
    all_gather x2, waiting for transfers between devices, fetch_rows(): return lax.all_gather(local_rows, DEVICES, axis=0, tiled=True)  327 us
    ppermute x29, waiting for transfers between devices, shift(): lax.ppermute(value, axis, [(i, (i + amount) % count) for i in range(count)])  160 us
    ppermute x4, waiting for transfers between devices, far_pair(): got = lax.ppermute(sent, 'z', pairs)  78.1 us
    pallas_call x2, Pallas kernels, ffn_backward(): pl.pallas_call(ffn_backward_body, grid_spec=pltpu.PrefetchScalarGridSpec(...  53.5 us
    pallas_call x2, Pallas kernels, ffn_forward(): pl.pallas_call(functools.partial(ffn_forward_body, middle is not None), g...  50.4 us
    pallas_call x2, Pallas kernels, attend_backward(): pl.pallas_call(functools.partial(backward_body, width > 2 * INNER), grid_...  50.2 us
    pallas_call x2, Pallas kernels, weight_grads(): pl.pallas_call(functools.partial(weight_grads_body, chunks, tile), grid_s...  47.3 us
    unnamed x281, local copies, waits for them, and re-layouts  41.6 us
  transfers between devices with their start and end apart: 49, of which 24 were waited for; matrix products, arithmetic and copies ran while one was open for 12% of the time, Pallas kernels for 16%

profile of v15, /device:TPU:24, one launch (start us, length us, event | category | flops | bytes accessed | tf_op | source)
XLA Modules:
  0.0 1099.6 jit_solution(13070328189376651606)
XLA Ops:
  7.2 2.5 copy.126
  12.0 2.4 copy.125
  18.4 207.0 %all-gather.3.cloned.1.call-done.refs_1_.refs_2_.refs_4_.refs_3_.refs_5_ = bf16[12288,1472]{1,0:T(8,128)(2,1)} async-done(((bf16[384,1472]{1,0:T(8,128)(2,1)}), bf16[12288,1472]{1,0:T(8,128)(2,1)}) %all-gather.3.cloned.1.call-update) | async-done | bytes 36175888 | tf_op jit(solution)/shard_map/all_gather | solution.py:1052
  225.4 3.6 fusion.38
  230.4 4.7 bias_tiles.1.refs_4_.refs_6_
  235.2 3.8 copy.130
  240.3 5.8 collective-permute-start.2
  246.1 2.3 convolution_convert_fusion.3.refs_0_
  248.4 20.6 %collective-permute-done = bf16[288,768]{1,0:T(8,128)(2,1)} collective-permute-done((bf16[288,768]{1,0:T(8,128)(2,1)S(1)}, bf16[288,768]{1,0:T(8,128)(2,1)}, u32[]{:S(2)}, u32[]{:S(2)}) %collective-permute-start) | collective-permute-done | bytes 442400 | tf_op jit(solution)/shard_map/ppermute | solution.py:468
  270.1 20.7 %collective-permute-done.1 = bf16[512,768]{1,0:T(8,128)(2,1)S(1)} collective-permute-done((bf16[512,768]{1,0:T(8,128)(2,1)S(1)}, bf16[512,768]{1,0:T(8,128)(2,1)S(1)}, u32[]{:S(2)}, u32[]{:S(2)}) %collective-permute-start.1) | collective-permute-done | bytes 786464 | tf_op jit(solution)/shard_map/ppermute | solution.py:460
  291.5 10.8 attend_forward.2
  302.4 2.8 multiply_reduce_fusion.10
  306.8 28.3 %ffn_forward.2 = (f32[512,1472]{1,0:T(8,128)}, f32[512,3584]{1,0:T(8,128)}, f32[512,3584]{1,0:T(8,128)}, bf16[6144,512]{1,0:T(8,128)(2,1)}, bf16[6144,512]{1,0:T(8,128)(2,1)}) custom-call(s32[2]{0:T(128)S(1)} %pad_add_fusion.core_ref, bf16[512,1472]{1,0:T(8,128)(2,1)S(1)} %multiply_convert_fusion.2.refs_0_, ...), custom_call_target="tpu_custom_call" | custom-call | flops 16206790656 | bytes 50003968 | tf_op jit(solution)/shard_map/ffn_forward/pallas_call | solution.py:670
  335.2 2.3 multiply_reduce_fusion.9
  340.5 119.9 %all-gather.5.cloned.1.call-done.refs_1_.refs_2_.refs_3_.refs_4_.refs_5_ = bf16[12288,1472]{1,0:T(8,128)(2,1)} async-done(((bf16[384,1472]{1,0:T(8,128)(2,1)}), bf16[12288,1472]{1,0:T(8,128)(2,1)}) %all-gather.5.cloned.1.call-update) | async-done | bytes 36175888 | tf_op jit(solution)/shard_map/all_gather | solution.py:1052
  460.4 3.1 fusion.41
  465.5 3.7 collective-permute-start.3
  471.0 2.3 convolution_convert_fusion.2.refs_0_
  473.3 38.4 %collective-permute-done.3 = bf16[288,896]{1,0:T(8,128)(2,1)S(1)} collective-permute-done((bf16[288,896]{1,0:T(8,128)(2,1)S(1)}, bf16[288,896]{1,0:T(8,128)(2,1)S(1)}, u32[]{:S(2)}, u32[]{:S(2)}) %collective-permute-start.3) | collective-permute-done | bytes 516128 | tf_op jit(solution)/shard_map/ppermute | solution.py:468
  513.2 11.0 attend_forward.3
  524.2 2.8 multiply_reduce_fusion.7
  528.0 22.1 %ffn_forward.3 = (bf16[512,3584]{1,0:T(8,128)(2,1)}, f32[512,3584]{1,0:T(8,128)}, f32[512,3584]{1,0:T(8,128)}, bf16[6144,512]{1,0:T(8,128)(2,1)}, bf16[6144,512]{1,0:T(8,128)(2,1)}) custom-call(s32[2]{0:T(128)S(1)} %pad_add_fusion.core_ref, bf16[512,1472]{1,0:T(8,128)(2,1)S(1)} %multiply_convert_fusion.refs_0_, ...), custom_call_target="tpu_custom_call" | custom-call | flops 16206790656 | bytes 50003968 | tf_op jit(solution)/shard_map/ffn_forward/pallas_call | solution.py:670
  550.1 26.0 %ffn_backward.2 = (f32[512,1472]{1,0:T(8,128)}, bf16[6144,512]{1,0:T(8,128)(2,1)}, bf16[6144,512]{1,0:T(8,128)(2,1)}) custom-call(s32[2]{0:T(128)S(1)} %pad_add_fusion.core_ref, bf16[512,1472]{1,0:T(8,128)(2,1)S(1)} %bitcast_convert_fusion.refs_0_, f32[512,3584]{1,0:T(8,128)} %get-tuple-element.213.refs_1_, ...), custom_call_target="tpu_custom_call", output_to_operand_aliasing={{1}: (7, {}), {2}: (8, {})} | custom-call | flops 16206790656 | bytes 53673984 | tf_op jit(solution)/shard_map/ffn_backward/pallas_call | solution.py:735
  583.8 2.5 fusion.58
  586.3 2.9 convolution_convert_fusion.1.refs_1_
  589.2 25.6 %attend_backward.2 = (bf16[512,384]{1,0:T(8,128)(2,1)S(1)}, bf16[2304,896]{1,0:T(8,128)(2,1)}, f32[3,32,256]{2,1,0:T(8,128)S(1)}) custom-call(s32[4]{0:T(128)S(1)} %get-tuple-element.553.low_ref, s32[4]{0:T(128)S(1)} %get-tuple-element.552.high_ref, bf16[512,384]{1,0:T(8,128)(2,1)S(1)} %copy-done.38, bf16[512,384]{1,0:T(8,128)(2,1)S(1)} %convolution_convert_fusion.1.refs_1_, ...), custom_call_target="tpu_custom_call" | custom-call | flops 4529848320 | bytes 12582912 | tf_op jit(solution)/shard_map/attend_backward/pallas_call | solution.py:361
  617.0 2.5 collective-permute-start.8
  627.3 22.5 %weight_grads.2 = (bf16[3072,256]{1,0:T(8,128)(2,1)S(1)}, bf16[3072,256]{1,0:T(8,128)(2,1)S(1)}, bf16[3072,256]{1,0:T(8,128)(2,1)S(1)}, bf16[3072,256]{1,0:T(8,128)(2,1)S(1)}, bf16[6144,1024]{1,0:T(8,128)(2,1)}) custom-call(s32[6]{0:T(128)S(1)} %copy-done.45, bf16[6144,512]{1,0:T(8,128)(2,1)} %get-tuple-element.223.refs_0_, ...), custom_call_target="tpu_custom_call" | custom-call | flops 18522046464 | bytes 31457280 | tf_op jit(solution)/shard_map/weight_grads/pallas_call | solution.py:895
  649.9 15.9 %collective-permute-done.10 = bf16[288,896]{1,0:T(8,128)(2,1)S(1)} collective-permute-done((bf16[288,896]{1,0:T(8,128)(2,1)S(1)}, bf16[288,896]{1,0:T(8,128)(2,1)S(1)}, u32[]{:S(2)}, u32[]{:S(2)}) %collective-permute-start.10) | collective-permute-done | bytes 516128 | tf_op jit(solution)/shard_map/ppermute | solution.py:468
  671.0 2.5 pad_maximum_fusion.5
  678.4 10.4 attention_fill.2
  695.5 6.6 multiply_reduce_fusion.2
  702.2 2.7 fusion.56
  704.9 27.4 %ffn_backward.3 = (f32[512,1472]{1,0:T(8,128)}, bf16[6144,512]{1,0:T(8,128)(2,1)}, bf16[6144,512]{1,0:T(8,128)(2,1)}) custom-call(s32[2]{0:T(128)S(1)} %pad_add_fusion.core_ref, bf16[512,1472]{1,0:T(8,128)(2,1)S(1)} %get-tuple-element.482.refs_0_, f32[512,3584]{1,0:T(8,128)} %get-tuple-element.253.refs_1_, ...), custom_call_target="tpu_custom_call", output_to_operand_aliasing={{1}: (7, {}), {2}: (8, {})} | custom-call | flops 16206790656 | bytes 53673984 | tf_op jit(solution)/shard_map/ffn_backward/pallas_call | solution.py:735
  732.4 3.7 collective-permute-done.13
  749.6 2.5 fusion.55
  752.9 3.6 convolution_convert_fusion.refs_1_
  756.5 24.6 %attend_backward.3 = (bf16[512,384]{1,0:T(8,128)(2,1)S(1)}, bf16[2304,768]{1,0:T(8,128)(2,1)}, f32[3,32,256]{2,1,0:T(8,128)S(1)}) custom-call(s32[4]{0:T(128)S(1)} %get-tuple-element.553.low_ref, s32[4]{0:T(128)S(1)} %get-tuple-element.552.high_ref, bf16[512,384]{1,0:T(8,128)(2,1)S(1)} %copy-done.40, bf16[512,384]{1,0:T(8,128)(2,1)S(1)} %convolution_convert_fusion.refs_1_, ...), custom_call_target="tpu_custom_call" | custom-call | flops 4529848320 | bytes 12582912 | tf_op jit(solution)/shard_map/attend_backward/pallas_call | solution.py:361
  789.2 24.8 %weight_grads.3 = (bf16[3072,384]{1,0:T(8,128)(2,1)}, bf16[3072,384]{1,0:T(8,128)(2,1)}, bf16[3072,384]{1,0:T(8,128)(2,1)S(1)}, bf16[3072,384]{1,0:T(8,128)(2,1)...) custom-call(s32[6]{0:T(128)S(1)} %copy-done.46, ...), custom_call_target="tpu_custom_call" | custom-call | flops 18522046464 | bytes 31457280 | tf_op jit(solution)/shard_map/weight_grads/pallas_call | solution.py:895
  814.0 3.2 collective-permute-done.21
  819.3 5.7 collective-permute-start.22
  828.0 10.2 attention_fill.3
  843.2 5.8 collective-permute-start.25
  849.8 7.5 fusion.33
  861.4 10.6 collective-permute-done.26
  872.0 25.4 %collective-permute-done.27 = bf16[384,512]{1,0:T(8,128)(2,1)S(1)} collective-permute-done((bf16[384,512]{1,0:T(8,128)(2,1)}, bf16[384,512]{1,0:T(8,128)(2,1)S(1)}, u32[]{:S(2)}, u32[]{:S(2)}) %collective-permute-start.27) | collective-permute-done | bytes 393248 | tf_op jit(solution)/shard_map/ppermute | solution.py:454
  897.4 6.5 collective-permute-done.24
  903.9 3.0 add_convert_fusion.2
  907.2 2.4 add_convert_fusion.3
  909.9 2.9 collective-permute-start.30
  912.8 2.5 collective-permute-start.31
  915.5 10.1 fusion.14
  925.6 14.2 %collective-permute-done.30 = bf16[1536,384]{1,0:T(8,128)(2,1)S(1)} collective-permute-done((bf16[1536,384]{1,0:T(8,128)(2,1)S(1)}, bf16[1536,384]{1,0:T(8,128)(2,1)S(1)}, u32[]{:S(2)}, u32[]{:S(2)}) %collective-permute-start.30) | collective-permute-done | bytes 1179680 | tf_op jit(solution)/shard_map/ppermute | solution.py:454
  939.7 2.5 collective-permute-done.31
  946.3 11.8 %collective-permute-done.32 = bf16[384,768]{1,0:T(8,128)(2,1)S(1)} collective-permute-done((bf16[384,768]{1,0:T(8,128)(2,1)S(1)}, bf16[384,768]{1,0:T(8,128)(2,1)S(1)}, u32[]{:S(2)}, u32[]{:S(2)}) %collective-permute-start.32) | collective-permute-done | bytes 589856 | tf_op jit(solution)/shard_map/ppermute | solution.py:454
  958.0 31.9 %collective-permute-done.33 = bf16[384,768]{1,0:T(8,128)(2,1)} collective-permute-done((bf16[384,768]{1,0:T(8,128)(2,1)S(1)}, bf16[384,768]{1,0:T(8,128)(2,1)}, u32[]{:S(2)}, u32[]{:S(2)}) %collective-permute-start.33) | collective-permute-done | bytes 589856 | tf_op jit(solution)/shard_map/ppermute | solution.py:454
  989.9 2.3 add_convert_fusion
  994.7 2.4 add_convert_fusion.1
  1001.1 2.3 copy.142
  1006.5 2.3 add_add_fusion.2
  1008.8 3.6 copy.141
  1012.4 9.4 collective-permute-done.37
  1031.1 5.3 collective-permute-start.42
  1046.9 39.8 %collective-permute-done.42 = bf16[384,768]{1,0:T(8,128)(2,1)} collective-permute-done((bf16[384,768]{1,0:T(8,128)(2,1)}, bf16[384,768]{1,0:T(8,128)(2,1)}, u32[]{:S(2)}, u32[]{:S(2)}) %collective-permute-start.42) | collective-permute-done | bytes 589856 | tf_op jit(solution)/shard_map/ppermute | solution.py:454
  (472 shorter events, 132.5 us)
Async XLA Ops:
  7.2 218.2 %all-gather.3.cloned.1.call-start = ((), (), s32[]{:S(2)}) async-start(), calls=%async_computation.1 | async-start | bytes 38928384 | tf_op jit(solution)/shard_map/all_gather | solution.py:1052
  9.7 450.7 %all-gather.5.cloned.1.call-start = ((), (), s32[]{:S(2)}) async-start(), calls=%async_computation.2 | async-start | bytes 38928384 | tf_op jit(solution)/shard_map/all_gather | solution.py:1052
  11.9 978.1 %reduce-scatter.2.cloned.1.call-start = ((), (), s32[]{:S(2)}) async-start(), calls=%async_computation.3 | async-start | bytes 13369344 | tf_op jit(solution)/shard_map/reduce_scatter | solution.py:1149
  16.0 289.8 %copy-start.100 = (f32[1472]{0:T(1024)}, f32[1472]{0:T(1024)S(1)}, u32[]{:S(2)}) copy-start(f32[1472]{0:T(1024)S(1)} %get-tuple-element.471) | copy-start | bytes 17668
  16.9 208.5 %copy-start.120 = (f32[512]{0:T(512)}, f32[512]{0:T(512)S(1)}, u32[]{:S(2)}) copy-start(f32[512]{0:T(512)S(1)} %get-tuple-element.539) | copy-start | bytes 6148
  18.4 211.4 %copy-start.130 = (f32[32,6]{0,1:T(8,128)S(1)}, f32[32,6]{0,1:T(8,128)}, u32[]{:S(2)}) copy-start(f32[32,6]{0,1:T(8,128)} %param.13) | copy-start | bytes 2308
  229.0 40.0 %collective-permute-start = (bf16[288,768]{1,0:T(8,128)(2,1)S(1)}, bf16[288,768]{1,0:T(8,128)(2,1)}, u32[]{:S(2)}, u32[]{:S(2)}) collective-permute-start(bf16[288,768]{1,0:T(8,128)(2,1)S(1)} %slice_select_fusion.1), channel_id=1, source_target_pairs={{0,2},{1,3},{2,0},{3,1},{4,6},{5,7},{6,4},{7,5},{8,10},{9,11},{10,... | collective-permute-start | bytes 1327112 | tf_op jit(solution)/shard_map/ppermute | solution.py:468
  239.0 51.9 %collective-permute-start.1 = (bf16[512,768]{1,0:T(8,128)(2,1)S(1)}, bf16[512,768]{1,0:T(8,128)(2,1)S(1)}, u32[]{:S(2)}, u32[]{:S(2)}) collective-permute-start(bf16[512,768]{1,0:T(8,128)(2,1)S(1)} %fusion.38), channel_id=1, source_target_pairs={{0,1},{1,2},{2,3},{4,5},{5,6},{6,7},{8,9},{9,10},{10,11},{12,13},{... | collective-permute-start | bytes 2359304 | tf_op jit(solution)/shard_map/ppermute | solution.py:460
  240.3 50.7 %collective-permute-start.2 = (bf16[512,768]{1,0:T(8,128)(2,1)S(1)}, bf16[512,768]{1,0:T(8,128)(2,1)S(1)}, u32[]{:S(2)}, u32[]{:S(2)}) collective-permute-start(bf16[512,768]{1,0:T(8,128)(2,1)S(1)} %fusion.38), channel_id=1, source_target_pairs={{1,0},{2,1},{3,2},{5,4},{6,5},{7,6},{9,8},{10,9},{11,10},{13,12},{... | collective-permute-start | bytes 2359304 | tf_op jit(solution)/shard_map/ppermute | solution.py:460
  248.4 43.1 %copy-start.39 = (bf16[512,384]{1,0:T(8,128)(2,1)}, bf16[512,384]{1,0:T(8,128)(2,1)S(1)}, u32[]{:S(2)}) copy-start(bf16[512,384]{1,0:T(8,128)(2,1)S(1)} %convolution_convert_fusion.3.refs_0_) | copy-start | bytes 1179652
  305.8 29.3 %copy-start.112 = (f32[512]{0:T(512)}, f32[512]{0:T(512)S(1)}, u32[]{:S(2)}) copy-start(f32[512]{0:T(512)S(1)} %get-tuple-element.541) | copy-start | bytes 6148
  306.8 31.3 %copy-start.108 = (f32[1472]{0:T(1024)S(1)}, f32[1472]{0:T(1024)}, u32[]{:S(2)}) copy-start(f32[1472]{0:T(1024)} %param.12) | copy-start | bytes 17668
  338.7 124.8 %copy-start.77 = (bf16[512,1472]{1,0:T(8,128)(2,1)}, bf16[512,1472]{1,0:T(8,128)(2,1)S(1)}, u32[]{:S(2)}) copy-start(bf16[512,1472]{1,0:T(8,128)(2,1)S(1)} %get-tuple-element.493) | copy-start | bytes 4521988
  463.9 48.0 %collective-permute-start.4 = (bf16[512,896]{1,0:T(8,128)(2,1)S(1)}, bf16[512,896]{1,0:T(8,128)(2,1)S(1)}, u32[]{:S(2)}, u32[]{:S(2)}) collective-permute-start(bf16[512,896]{1,0:T(8,128)(2,1)S(1)} %pad_maximum_fusion.2), channel_id=1, source_target_pairs={{0,1},{1,2},{2,3},{4,5},{5,6},{6,7},{8,9},{9,10},{10,11},{12,13},{... | collective-permute-start | bytes 2752520 | tf_op jit(solution)/shard_map/ppermute | solution.py:460
  465.5 46.2 %collective-permute-start.3 = (bf16[288,896]{1,0:T(8,128)(2,1)S(1)}, bf16[288,896]{1,0:T(8,128)(2,1)S(1)}, u32[]{:S(2)}, u32[]{:S(2)}) collective-permute-start(bf16[288,896]{1,0:T(8,128)(2,1)S(1)} %fusion.51), channel_id=1, source_target_pairs={{0,2},{1,3},{2,0},{3,1},{4,6},{5,7},{6,4},{7,5},{8,10},{9,11},{10,... | collective-permute-start | bytes 1548296 | tf_op jit(solution)/shard_map/ppermute | solution.py:468
  469.4 42.8 %collective-permute-start.5 = (bf16[512,896]{1,0:T(8,128)(2,1)S(1)}, bf16[512,896]{1,0:T(8,128)(2,1)S(1)}, u32[]{:S(2)}, u32[]{:S(2)}) collective-permute-start(bf16[512,896]{1,0:T(8,128)(2,1)S(1)} %pad_maximum_fusion.2), channel_id=1, source_target_pairs={{1,0},{2,1},{3,2},{5,4},{6,5},{7,6},{9,8},{10,9},{11,10},{13,12},{... | collective-permute-start | bytes 2752520 | tf_op jit(solution)/shard_map/ppermute | solution.py:460
  473.3 39.1 %copy-start.37 = (bf16[512,384]{1,0:T(8,128)(2,1)}, bf16[512,384]{1,0:T(8,128)(2,1)S(1)}, u32[]{:S(2)}) copy-start(bf16[512,384]{1,0:T(8,128)(2,1)S(1)} %convolution_convert_fusion.2.refs_0_) | copy-start | bytes 1179652
  576.2 51.1 %collective-permute-start.6 = (bf16[6144,512]{1,0:T(8,128)(2,1)}, bf16[6144,512]{1,0:T(8,128)(2,1)}, u32[]{:S(2)}, u32[]{:S(2)}) collective-permute-start(bf16[6144,512]{1,0:T(8,128)(2,1)} %get-tuple-element.224), channel_id=1, source_target_pairs={{0,4},{4,0},{1,5},{5,1},{2,6},{6,2},{3,7},{7,3},{8,12},{12,8},{9,1... | collective-permute-start | bytes 18874376 | tf_op jit(solution)/shard_map/ppermute | solution.py:454
  580.0 46.4 %collective-permute-start.7 = (bf16[1024,1536]{1,0:T(8,128)(2,1)S(1)}, bf16[1024,1536]{1,0:T(8,128)(2,1)S(1)}, u32[]{:S(2)}, u32[]{:S(2)}) collective-permute-start(bf16[1024,1536]{1,0:T(8,128)(2,1)S(1)} %fusion.20.refs_2_.refs_3_), channel_id=1, source_target_pairs={{0,4},{4,0},{1,5},{5,1},{2,6},{6,2},{3,7},{7,3},{8,12},{12,8},{9,1... | collective-permute-start | bytes 9437192 | tf_op jit(solution)/shard_map/ppermute | solution.py:454
  586.3 28.6 %copy-start.80 = (bf16[512,1472]{1,0:T(8,128)(2,1)}, bf16[512,1472]{1,0:T(8,128)(2,1)S(1)}, u32[]{:S(2)}) copy-start(bf16[512,1472]{1,0:T(8,128)(2,1)S(1)} %get-tuple-element.484) | copy-start | bytes 4521988
  614.8 51.6 %copy-start.30 = (bf16[512,384]{1,0:T(8,128)(2,1)}, bf16[512,384]{1,0:T(8,128)(2,1)S(1)}, u32[]{:S(2)}) copy-start(bf16[512,384]{1,0:T(8,128)(2,1)S(1)} %get-tuple-element.220) | copy-start | bytes 1179652
  617.0 48.7 %collective-permute-start.8 = (bf16[512,896]{1,0:T(8,128)(2,1)S(1)}, bf16[512,896]{1,0:T(8,128)(2,1)S(1)}, u32[]{:S(2)}, u32[]{:S(2)}) collective-permute-start(bf16[512,896]{1,0:T(8,128)(2,1)S(1)} %get-tuple-element.487), channel_id=1, source_target_pairs={{1,0},{2,1},{3,2},{5,4},{6,5},{7,6},{9,8},{10,9},{11,10},{13,12},{... | collective-permute-start | bytes 2752520 | tf_op jit(solution)/shard_map/ppermute | solution.py:460
  619.6 46.2 %collective-permute-start.9 = (bf16[512,896]{1,0:T(8,128)(2,1)S(1)}, bf16[512,896]{1,0:T(8,128)(2,1)S(1)}, u32[]{:S(2)}, u32[]{:S(2)}) collective-permute-start(bf16[512,896]{1,0:T(8,128)(2,1)S(1)} %get-tuple-element.486), channel_id=1, source_target_pairs={{0,1},{1,2},{2,3},{4,5},{5,6},{6,7},{8,9},{9,10},{10,11},{12,13},{... | collective-permute-start | bytes 2752520 | tf_op jit(solution)/shard_map/ppermute | solution.py:460
  622.3 43.4 %collective-permute-start.10 = (bf16[288,896]{1,0:T(8,128)(2,1)S(1)}, bf16[288,896]{1,0:T(8,128)(2,1)S(1)}, u32[]{:S(2)}, u32[]{:S(2)}) collective-permute-start(bf16[288,896]{1,0:T(8,128)(2,1)S(1)} %slice_select_fusion), channel_id=1, source_target_pairs={{0,2},{1,3},{2,0},{3,1},{4,6},{5,7},{6,4},{7,5},{8,10},{9,11},{10,... | collective-permute-start | bytes 1548296 | tf_op jit(solution)/shard_map/ppermute | solution.py:468
  626.4 47.1 %collective-permute-start.12 = (bf16[1024,1536]{1,0:T(8,128)(2,1)}, bf16[1024,1536]{1,0:T(8,128)(2,1)}, u32[]{:S(2)}, u32[]{:S(2)}) collective-permute-start(bf16[1024,1536]{1,0:T(8,128)(2,1)} %fusion.21.refs_2_), channel_id=1, source_target_pairs={{0,4},{4,0},{1,5},{5,1},{2,6},{6,2},{3,7},{7,3},{8,12},{12,8},{9,1... | collective-permute-start | bytes 9437192 | tf_op jit(solution)/shard_map/ppermute | solution.py:454
  667.9 5.6 collective-permute-start.11
  693.4 42.7 %collective-permute-start.13 = (bf16[3072,256]{1,0:T(8,128)(2,1)}, bf16[3072,256]{1,0:T(8,128)(2,1)}, u32[]{:S(2)}, u32[]{:S(2)}) collective-permute-start(bf16[3072,256]{1,0:T(8,128)(2,1)} %copy-done.33), channel_id=1, source_target_pairs={{0,16},{16,0},{1,17},{17,1},{2,18},{18,2},{3,19},{19,3},{4,20},{20... | collective-permute-start | bytes 4718600 | tf_op jit(solution)/shard_map/ppermute | solution.py:454
  693.5 42.7 %collective-permute-start.14 = (bf16[3072,256]{1,0:T(8,128)(2,1)}, bf16[3072,256]{1,0:T(8,128)(2,1)}, u32[]{:S(2)}, u32[]{:S(2)}) collective-permute-start(bf16[3072,256]{1,0:T(8,128)(2,1)} %copy-done.36), channel_id=1, source_target_pairs={{0,8},{8,0},{1,9},{9,1},{2,10},{10,2},{3,11},{11,3},{4,12},{12,4},... | collective-permute-start | bytes 4718600 | tf_op jit(solution)/shard_map/ppermute | solution.py:454
  704.9 31.3 %copy-start.23 = (bf16[3072,256]{1,0:T(8,128)(2,1)S(1)}, bf16[3072,256]{1,0:T(8,128)(2,1)}, u32[]{:S(2)}) copy-start(bf16[3072,256]{1,0:T(8,128)(2,1)} %copy-done.22) | copy-start | bytes 4718596
  742.7 46.5 %collective-permute-start.17 = (bf16[6144,512]{1,0:T(8,128)(2,1)}, bf16[6144,512]{1,0:T(8,128)(2,1)}, u32[]{:S(2)}, u32[]{:S(2)}) collective-permute-start(bf16[6144,512]{1,0:T(8,128)(2,1)} %get-tuple-element.290), channel_id=1, source_target_pairs={{0,4},{4,0},{1,5},{5,1},{2,6},{6,2},{3,7},{7,3},{8,12},{12,8},{9,1... | collective-permute-start | bytes 18874376 | tf_op jit(solution)/shard_map/ppermute | solution.py:454
  744.8 44.3 %collective-permute-start.18 = (bf16[1024,1536]{1,0:T(8,128)(2,1)S(1)}, bf16[1024,1536]{1,0:T(8,128)(2,1)}, u32[]{:S(2)}, u32[]{:S(2)}) collective-permute-start(bf16[1024,1536]{1,0:T(8,128)(2,1)S(1)} %fusion.22.refs_2_.refs_3_), channel_id=1, source_target_pairs={{0,4},{4,0},{1,5},{5,1},{2,6},{6,2},{3,7},{7,3},{8,12},{12,8},{9,1... | collective-permute-start | bytes 9437192 | tf_op jit(solution)/shard_map/ppermute | solution.py:454
  745.2 35.9 %collective-permute-start.15 = (bf16[1536,256]{1,0:T(8,128)(2,1)}, bf16[1536,256]{1,0:T(8,128)(2,1)}, u32[]{:S(2)}, u32[]{:S(2)}) collective-permute-start(bf16[1536,256]{1,0:T(8,128)(2,1)} %get-tuple-element.268), channel_id=1, source_target_pairs={{0,8},{8,0},{1,9},{9,1},{2,10},{10,2},{3,11},{11,3},{4,12},{12,4},... | collective-permute-start | bytes 2359304 | tf_op jit(solution)/shard_map/ppermute | solution.py:454
  745.5 35.6 %collective-permute-start.16 = (bf16[1536,256]{1,0:T(8,128)(2,1)}, bf16[1536,256]{1,0:T(8,128)(2,1)S(1)}, u32[]{:S(2)}, u32[]{:S(2)}) collective-permute-start(bf16[1536,256]{1,0:T(8,128)(2,1)} %get-tuple-element.270), channel_id=1, source_target_pairs={{0,16},{16,0},{1,17},{17,1},{2,18},{18,2},{3,19},{19,3},{4,20},{20... | collective-permute-start | bytes 2359304 | tf_op jit(solution)/shard_map/ppermute | solution.py:454
  752.5 28.6 %copy-start.68 = (bf16[1024,1536]{1,0:T(8,128)(2,1)}, bf16[1024,1536]{1,0:T(8,128)(2,1)S(1)}, u32[]{:S(2)}) copy-start(bf16[1024,1536]{1,0:T(8,128)(2,1)S(1)} %fusion.23.refs_2_) | copy-start | bytes 9437188
  752.5 73.6 %collective-permute-start.23 = (bf16[1024,1536]{1,0:T(8,128)(2,1)S(1)}, bf16[1024,1536]{1,0:T(8,128)(2,1)}, u32[]{:S(2)}, u32[]{:S(2)}) collective-permute-start(bf16[1024,1536]{1,0:T(8,128)(2,1)S(1)} %fusion.23.refs_2_), channel_id=1, source_target_pairs={{0,4},{4,0},{1,5},{5,1},{2,6},{6,2},{3,7},{7,3},{8,12},{12,8},{9,1... | collective-permute-start | bytes 9437192 | tf_op jit(solution)/shard_map/ppermute | solution.py:454
  785.5 31.7 %collective-permute-start.19 = (bf16[512,768]{1,0:T(8,128)(2,1)S(1)}, bf16[512,768]{1,0:T(8,128)(2,1)}, u32[]{:S(2)}, u32[]{:S(2)}) collective-permute-start(bf16[512,768]{1,0:T(8,128)(2,1)S(1)} %get-tuple-element.490), channel_id=1, source_target_pairs={{1,0},{2,1},{3,2},{5,4},{6,5},{7,6},{9,8},{10,9},{11,10},{13,12},{... | collective-permute-start | bytes 2359304 | tf_op jit(solution)/shard_map/ppermute | solution.py:460
  787.7 29.5 %collective-permute-start.20 = (bf16[512,768]{1,0:T(8,128)(2,1)S(1)}, bf16[512,768]{1,0:T(8,128)(2,1)}, u32[]{:S(2)}, u32[]{:S(2)}) collective-permute-start(bf16[512,768]{1,0:T(8,128)(2,1)S(1)} %get-tuple-element.489), channel_id=1, source_target_pairs={{0,1},{1,2},{2,3},{4,5},{5,6},{6,7},{8,9},{9,10},{10,11},{12,13},{... | collective-permute-start | bytes 2359304 | tf_op jit(solution)/shard_map/ppermute | solution.py:460
  789.1 28.1 %collective-permute-start.21 = (bf16[288,768]{1,0:T(8,128)(2,1)S(1)}, bf16[288,768]{1,0:T(8,128)(2,1)S(1)}, u32[]{:S(2)}, u32[]{:S(2)}) collective-permute-start(bf16[288,768]{1,0:T(8,128)(2,1)S(1)} %slice_select_fusion.2), channel_id=1, source_target_pairs={{0,2},{1,3},{2,0},{3,1},{4,6},{5,7},{6,4},{7,5},{8,10},{9,11},{10,... | collective-permute-start | bytes 1327112 | tf_op jit(solution)/shard_map/ppermute | solution.py:468
  819.3 8.7 collective-permute-start.22
  842.5 61.4 %collective-permute-start.24 = (bf16[3072,384]{1,0:T(8,128)(2,1)}, bf16[3072,384]{1,0:T(8,128)(2,1)}, u32[]{:S(2)}, u32[]{:S(2)}) collective-permute-start(bf16[3072,384]{1,0:T(8,128)(2,1)} %get-tuple-element.329), channel_id=1, source_target_pairs={{0,16},{16,0},{1,17},{17,1},{2,18},{18,2},{3,19},{19,3},{4,20},{20... | collective-permute-start | bytes 7077896 | tf_op jit(solution)/shard_map/ppermute | solution.py:454
  843.2 60.8 %collective-permute-start.25 = (bf16[3072,384]{1,0:T(8,128)(2,1)}, bf16[3072,384]{1,0:T(8,128)(2,1)}, u32[]{:S(2)}, u32[]{:S(2)}) collective-permute-start(bf16[3072,384]{1,0:T(8,128)(2,1)} %get-tuple-element.331), channel_id=1, source_target_pairs={{0,8},{8,0},{1,9},{9,1},{2,10},{10,2},{3,11},{11,3},{4,12},{12,4},... | collective-permute-start | bytes 7077896 | tf_op jit(solution)/shard_map/ppermute | solution.py:454
  858.0 1.4 collective-permute-start.29
  858.0 14.0 %collective-permute-start.26 = (bf16[384,512]{1,0:T(8,128)(2,1)}, bf16[384,512]{1,0:T(8,128)(2,1)S(1)}, u32[]{:S(2)}, u32[]{:S(2)}) collective-permute-start(bf16[384,512]{1,0:T(8,128)(2,1)} %pad_maximum_fusion.16), channel_id=1, source_target_pairs={{0,1},{1,2},{2,3},{3,0},{4,5},{5,6},{6,7},{7,4},{8,9},{9,10},{10,1... | collective-permute-start | bytes 1179656 | tf_op jit(solution)/shard_map/ppermute | solution.py:454
  858.0 39.5 %collective-permute-start.27 = (bf16[384,512]{1,0:T(8,128)(2,1)}, bf16[384,512]{1,0:T(8,128)(2,1)S(1)}, u32[]{:S(2)}, u32[]{:S(2)}) collective-permute-start(bf16[384,512]{1,0:T(8,128)(2,1)} %pad_maximum_fusion.17), channel_id=1, source_target_pairs={{0,2},{1,3},{2,0},{3,1},{4,6},{5,7},{6,4},{7,5},{8,10},{9,11},{10,... | collective-permute-start | bytes 1179656 | tf_op jit(solution)/shard_map/ppermute | solution.py:454
  859.4 38.0 %collective-permute-start.28 = (bf16[384,512]{1,0:T(8,128)(2,1)}, bf16[384,512]{1,0:T(8,128)(2,1)S(1)}, u32[]{:S(2)}, u32[]{:S(2)}) collective-permute-start(bf16[384,512]{1,0:T(8,128)(2,1)} %pad_maximum_fusion.18), channel_id=1, source_target_pairs={{0,3},{1,0},{2,1},{3,2},{4,7},{5,4},{6,5},{7,6},{8,11},{9,8},{10,9... | collective-permute-start | bytes 1179656 | tf_op jit(solution)/shard_map/ppermute | solution.py:454
  872.0 34.9 %copy-start.97 = (bf16[384,512]{1,0:T(8,128)(2,1)}, bf16[384,512]{1,0:T(8,128)(2,1)S(1)}, u32[]{:S(2)}) copy-start(bf16[384,512]{1,0:T(8,128)(2,1)S(1)} %collective-permute-done.26) | copy-start | bytes 1179652
  909.9 29.8 %collective-permute-start.30 = (bf16[1536,384]{1,0:T(8,128)(2,1)S(1)}, bf16[1536,384]{1,0:T(8,128)(2,1)S(1)}, u32[]{:S(2)}, u32[]{:S(2)}) collective-permute-start(bf16[1536,384]{1,0:T(8,128)(2,1)S(1)} %get-tuple-element.346), channel_id=1, source_target_pairs={{0,8},{8,0},{1,9},{9,1},{2,10},{10,2},{3,11},{11,3},{4,12},{12,4},... | collective-permute-start | bytes 3538952 | tf_op jit(solution)/shard_map/ppermute | solution.py:454
  912.8 29.4 %collective-permute-start.31 = (bf16[1536,384]{1,0:T(8,128)(2,1)S(1)}, bf16[1536,384]{1,0:T(8,128)(2,1)S(1)}, u32[]{:S(2)}, u32[]{:S(2)}) collective-permute-start(bf16[1536,384]{1,0:T(8,128)(2,1)S(1)} %get-tuple-element.348), channel_id=1, source_target_pairs={{0,16},{16,0},{1,17},{17,1},{2,18},{18,2},{3,19},{19,3},{4,20},{20... | collective-permute-start | bytes 3538952 | tf_op jit(solution)/shard_map/ppermute | solution.py:454
  915.3 74.6 %collective-permute-start.35 = (bf16[3072,384]{1,0:T(8,128)(2,1)}, bf16[3072,384]{1,0:T(8,128)(2,1)}, u32[]{:S(2)}, u32[]{:S(2)}) collective-permute-start(bf16[3072,384]{1,0:T(8,128)(2,1)} %get-tuple-element.376), channel_id=1, source_target_pairs={{0,16},{16,0},{1,17},{17,1},{2,18},{18,2},{3,19},{19,3},{4,20},{20... | collective-permute-start | bytes 7077896 | tf_op jit(solution)/shard_map/ppermute | solution.py:454
  915.4 74.6 %collective-permute-start.36 = (bf16[3072,384]{1,0:T(8,128)(2,1)}, bf16[3072,384]{1,0:T(8,128)(2,1)}, u32[]{:S(2)}, u32[]{:S(2)}) collective-permute-start(bf16[3072,384]{1,0:T(8,128)(2,1)} %get-tuple-element.378), channel_id=1, source_target_pairs={{0,8},{8,0},{1,9},{9,1},{2,10},{10,2},{3,11},{11,3},{4,12},{12,4},... | collective-permute-start | bytes 7077896 | tf_op jit(solution)/shard_map/ppermute | solution.py:454
  943.0 46.9 %copy-start.15 = (bf16[3072,384]{1,0:T(8,128)(2,1)S(1)}, bf16[3072,384]{1,0:T(8,128)(2,1)}, u32[]{:S(2)}) copy-start(bf16[3072,384]{1,0:T(8,128)(2,1)} %copy-done.14) | copy-start | bytes 7077892
  944.2 13.8 %collective-permute-start.32 = (bf16[384,768]{1,0:T(8,128)(2,1)S(1)}, bf16[384,768]{1,0:T(8,128)(2,1)S(1)}, u32[]{:S(2)}, u32[]{:S(2)}) collective-permute-start(bf16[384,768]{1,0:T(8,128)(2,1)S(1)} %pad_maximum_fusion.8), channel_id=1, source_target_pairs={{0,1},{1,2},{2,3},{3,0},{4,5},{5,6},{6,7},{7,4},{8,9},{9,10},{10,1... | collective-permute-start | bytes 1769480 | tf_op jit(solution)/shard_map/ppermute | solution.py:454
  944.2 45.7 %collective-permute-start.33 = (bf16[384,768]{1,0:T(8,128)(2,1)S(1)}, bf16[384,768]{1,0:T(8,128)(2,1)}, u32[]{:S(2)}, u32[]{:S(2)}) collective-permute-start(bf16[384,768]{1,0:T(8,128)(2,1)S(1)} %pad_maximum_fusion.9), channel_id=1, source_target_pairs={{0,2},{1,3},{2,0},{3,1},{4,6},{5,7},{6,4},{7,5},{8,10},{9,11},{10,... | collective-permute-start | bytes 1769480 | tf_op jit(solution)/shard_map/ppermute | solution.py:454
  944.4 45.5 %collective-permute-start.34 = (bf16[384,768]{1,0:T(8,128)(2,1)S(1)}, bf16[384,768]{1,0:T(8,128)(2,1)}, u32[]{:S(2)}, u32[]{:S(2)}) collective-permute-start(bf16[384,768]{1,0:T(8,128)(2,1)S(1)} %pad_maximum_fusion.10), channel_id=1, source_target_pairs={{0,3},{1,0},{2,1},{3,2},{4,7},{5,4},{6,5},{7,6},{8,11},{9,8},{10,9... | collective-permute-start | bytes 1769480 | tf_op jit(solution)/shard_map/ppermute | solution.py:454
  958.0 34.2 %copy-start.95 = (bf16[384,768]{1,0:T(8,128)(2,1)}, bf16[384,768]{1,0:T(8,128)(2,1)S(1)}, u32[]{:S(2)}) copy-start(bf16[384,768]{1,0:T(8,128)(2,1)S(1)} %collective-permute-done.32) | copy-start | bytes 1769476
  998.8 22.9 %collective-permute-start.37 = (bf16[1536,384]{1,0:T(8,128)(2,1)}, bf16[1536,384]{1,0:T(8,128)(2,1)}, u32[]{:S(2)}, u32[]{:S(2)}) collective-permute-start(bf16[1536,384]{1,0:T(8,128)(2,1)} %get-tuple-element.388), channel_id=1, source_target_pairs={{0,8},{8,0},{1,9},{9,1},{2,10},{10,2},{3,11},{11,3},{4,12},{12,4},... | collective-permute-start | bytes 3538952 | tf_op jit(solution)/shard_map/ppermute | solution.py:454
  1000.3 22.9 %collective-permute-start.38 = (bf16[1536,384]{1,0:T(8,128)(2,1)}, bf16[1536,384]{1,0:T(8,128)(2,1)}, u32[]{:S(2)}, u32[]{:S(2)}) collective-permute-start(bf16[1536,384]{1,0:T(8,128)(2,1)} %get-tuple-element.390), channel_id=1, source_target_pairs={{0,16},{16,0},{1,17},{17,1},{2,18},{18,2},{3,19},{19,3},{4,20},{20... | collective-permute-start | bytes 3538952 | tf_op jit(solution)/shard_map/ppermute | solution.py:454
  1000.3 4.4 collective-permute-start.39
  1005.5 6.9 collective-permute-start.40
  1030.2 10.0 collective-permute-start.44
  1030.5 16.4 %collective-permute-start.41 = (bf16[384,768]{1,0:T(8,128)(2,1)}, bf16[384,768]{1,0:T(8,128)(2,1)}, u32[]{:S(2)}, u32[]{:S(2)}) collective-permute-start(bf16[384,768]{1,0:T(8,128)(2,1)} %pad_maximum_fusion.12), channel_id=1, source_target_pairs={{0,1},{1,2},{2,3},{3,0},{4,5},{5,6},{6,7},{7,4},{8,9},{9,10},{10,1... | collective-permute-start | bytes 1769480 | tf_op jit(solution)/shard_map/ppermute | solution.py:454
  1031.1 55.6 %collective-permute-start.42 = (bf16[384,768]{1,0:T(8,128)(2,1)}, bf16[384,768]{1,0:T(8,128)(2,1)}, u32[]{:S(2)}, u32[]{:S(2)}) collective-permute-start(bf16[384,768]{1,0:T(8,128)(2,1)} %pad_maximum_fusion.13), channel_id=1, source_target_pairs={{0,2},{1,3},{2,0},{3,1},{4,6},{5,7},{6,4},{7,5},{8,10},{9,11},{10,... | collective-permute-start | bytes 1769480 | tf_op jit(solution)/shard_map/ppermute | solution.py:454
  1036.4 50.3 %collective-permute-start.43 = (bf16[384,768]{1,0:T(8,128)(2,1)}, bf16[384,768]{1,0:T(8,128)(2,1)}, u32[]{:S(2)}, u32[]{:S(2)}) collective-permute-start(bf16[384,768]{1,0:T(8,128)(2,1)} %pad_maximum_fusion.14), channel_id=1, source_target_pairs={{0,3},{1,0},{2,1},{3,2},{4,7},{5,4},{6,5},{7,6},{8,11},{9,8},{10,9... | collective-permute-start | bytes 1769480 | tf_op jit(solution)/shard_map/ppermute | solution.py:454
  1040.8 4.4 collective-permute-start.45
  (118 other events, 860.2 us)
Sparse Core Ops, SparseCore 0:
  11.4 213.9 all-gather.2
  228.8 231.5 all-gather.4
  693.8 228.7 reduce-scatter.1
